TPU v7x, 32 devices: a whole 2x2x4 slice. The times are simulated.
32 devices in a mesh: site: 4 (over y, x), hap: 8 (over z, core).
Axes of the slice: x: 2, y: 2, z: 4, core: 2. Of those that a mesh axis runs over, the one named last changes fastest.
Arguments:
- features: bfloat16 [512, 8, 256], P('site', 'hap'), may hold values from -6 to 6
- link_pattern: int32 [4, 4], replicated, may hold values from 0 to 1, as said below
- row_gain: float32 [256], replicated, may hold values from 0.5 to 1.5
- row_proj: bfloat16 [256, 768], replicated, may hold values from -0.5 to 6.5
- row_out: bfloat16 [256, 256], replicated, may hold values from -0.375 to 0.375
- column_norm_gain: float32 [256], replicated, may hold values from 0.5 to 1.5
- col_proj: bfloat16 [256, 768], replicated, may hold values from -0.5 to 6.5
- col_out: bfloat16 [256, 256], replicated, may hold values from -0.375 to 0.375
- cotangent: bfloat16 [512, 8, 256], P('site', 'hap'), may hold values from -6 to 6
Outputs:
- out_features: bfloat16 [512, 8, 256], P('site', 'hap')
- grad_features: bfloat16 [512, 8, 256], P('site', 'hap')
- grad_row_proj: float32 [256, 768], replicated
- grad_row_out: float32 [256, 256], replicated
- grad_col_proj: float32 [256, 768], replicated
- grad_col_out: float32 [256, 256], replicated
Inputs may be any that keep to these rules, and one draw needn't show every extreme that they name: link_pattern[b, b] = 1 for every block b.
All inputs are finite; a program needn't handle non-finite values.
Results may differ from a plain program's by a relative error of at most 0.027.
The roundings to bfloat16 on the way count: a program that leaves them out, or rounds other values in their place, can miss the bound.
Values may be sent and summed in bfloat16 or wider, within the bound.
No kernel may reach another device: no remote copies, remote signals or barrier semaphores. Data moves between devices by JAX's collectives and lax.ppermute only.
A program may use at most 64 MiB of HBM per device.

v0:
```python
import jax
import jax.numpy as jnp
from jax import lax
from jax.sharding import PartitionSpec as P

HEAD_DIM = 32
BLK = 128


EPSILON = 1e-05


def passed_along(value, axis, by):
    length = lax.axis_size(axis)
    return lax.ppermute(value, axis, [(i, (i + by) % length) for i in range(length)])


def norm_rows(values, norm_gain):
    widened = values.astype(jnp.float32)
    centred = widened - jnp.mean(widened, axis=-1, keepdims=True)
    spread = jnp.mean(centred * centred, axis=-1, keepdims=True)
    return centred * lax.rsqrt(spread + EPSILON) * norm_gain


def norm_back(values, norm_gain, incoming_gradient):
    primal, pullback = jax.vjp(
        lambda inside: norm_rows(inside, norm_gain), values.astype(jnp.float32)
    )
    return pullback(incoming_gradient)[0]


def project(other_argument, weight_matrix):
    return jnp.einsum(
        "puh,hz->puz", other_argument, weight_matrix, preferred_element_type=jnp.float32
    )


def project_back(incoming_gradient, weight_matrix):
    return jnp.einsum(
        "hcr,kr->hck", incoming_gradient, weight_matrix, preferred_element_type=jnp.float32
    )


def weight_grad(other_argument, incoming_gradient):
    return jnp.einsum(
        "hyo,hyp->op", other_argument, incoming_gradient, preferred_element_type=jnp.float32
    )


def split_heads(flat):
    return flat.reshape(flat.shape[0], flat.shape[1], flat.shape[2] // HEAD_DIM, HEAD_DIM)


def block_of(flat, block_index):
    return split_heads(lax.dynamic_slice_in_dim(flat, block_index * BLK, BLK, 0))


def add_block(flat, update):
    return flat + update.reshape(flat.shape)


def column_forward(hidden, column_norm_gain, col_proj, col_out):
    width = hidden.shape[2]
    scale = HEAD_DIM ** (-0.5)
    col_normed = norm_rows(hidden, column_norm_gain).astype(jnp.bfloat16)
    col_packed = project(col_normed, col_proj).astype(jnp.bfloat16)
    col_query = split_heads(col_packed[..., :width])
    col_key = split_heads(col_packed[..., width : 2 * width])
    col_value = split_heads(col_packed[..., 2 * width :])
    scores = (
        jnp.einsum("sqhe,skhe->shqk", col_query, col_key, preferred_element_type=jnp.float32)
        * scale
    )
    highest = jnp.max(scores, axis=-1)
    exp_terms = jnp.exp(scores - highest[..., None])
    row_total = jnp.sum(exp_terms, axis=-1)
    mixed = jnp.einsum(
        "shqk,skhe->sqhe",
        exp_terms.astype(jnp.bfloat16),
        col_value,
        preferred_element_type=jnp.float32,
    )
    col_attended = (
        (mixed / jnp.transpose(row_total, (0, 2, 1))[..., None])
        .astype(jnp.bfloat16)
        .reshape(hidden.shape)
    )
    output = (hidden.astype(jnp.float32) + project(col_attended, col_out)).astype(jnp.bfloat16)
    return (output, (col_normed, col_query, col_key, col_value, col_attended, highest, row_total))


def column_backward(hidden, column_norm_gain, col_proj, col_out, saved, grad_out):
    col_normed, col_query, col_key, col_value, col_attended, highest, row_total = saved
    scale = HEAD_DIM ** (-0.5)
    grad_col_out = weight_grad(col_attended, grad_out)
    grad_att = project_back(grad_out, col_out).astype(jnp.bfloat16)
    grad_heads = split_heads(grad_att)
    out_heads = split_heads(col_attended)
    scores = (
        jnp.einsum("sqhe,skhe->shqk", col_query, col_key, preferred_element_type=jnp.float32)
        * scale
    )
    attention_odds = jnp.exp(scores - highest[..., None]) / row_total[..., None]
    value_gradient = jnp.einsum(
        "shqk,sqhe->skhe",
        attention_odds.astype(jnp.bfloat16),
        grad_heads,
        preferred_element_type=jnp.float32,
    )
    grad_chances = jnp.einsum(
        "sqhe,skhe->shqk", grad_heads, col_value, preferred_element_type=jnp.float32
    )
    deltas = jnp.transpose(
        jnp.sum(grad_heads.astype(jnp.float32) * out_heads.astype(jnp.float32), axis=-1), (0, 2, 1)
    )
    grad_scores = (attention_odds * (grad_chances - deltas[..., None])).astype(jnp.bfloat16)
    grad_query = (
        jnp.einsum("shqk,skhe->sqhe", grad_scores, col_key, preferred_element_type=jnp.float32)
        * scale
    )
    grad_key = (
        jnp.einsum("shqk,sqhe->skhe", grad_scores, col_query, preferred_element_type=jnp.float32)
        * scale
    )
    grad_packed = jnp.concatenate(
        [
            grad_query.reshape(hidden.shape).astype(jnp.bfloat16),
            grad_key.reshape(hidden.shape).astype(jnp.bfloat16),
            value_gradient.reshape(hidden.shape).astype(jnp.bfloat16),
        ],
        axis=-1,
    )
    grad_col_proj = weight_grad(col_normed, grad_packed)
    grad_normed = project_back(grad_packed, col_proj)
    grad_hidden = (
        grad_out.astype(jnp.float32) + norm_back(hidden, column_norm_gain, grad_normed)
    ).astype(jnp.bfloat16)
    return (grad_hidden, grad_col_proj, grad_col_out)


def online_block(state, query_blk, key_blk, value_blk):
    running, highest, row_total = state
    scores = jnp.einsum(
        "qnhe,knhe->nhqk", query_blk, key_blk, preferred_element_type=jnp.float32
    ) * HEAD_DIM ** (-0.5)
    new_high = jnp.maximum(highest, jnp.max(scores, axis=-1))
    factor = jnp.exp(highest - new_high)
    exp_terms = jnp.exp(scores - new_high[..., None])
    row_total = row_total * factor + jnp.sum(exp_terms, axis=-1)
    mixed = jnp.einsum(
        "nhqk,knhe->qnhe",
        exp_terms,
        value_blk.astype(jnp.float32),
        precision=lax.Precision.HIGHEST,
        preferred_element_type=jnp.float32,
    )
    running = running * jnp.transpose(factor, (2, 0, 1))[..., None] + mixed
    return (running, new_high, row_total)


def pair_grads(query_blk, grad_blk, high_blk, total_blk, delta_blk, key_blk, value_blk):
    scale = HEAD_DIM ** (-0.5)
    scores = (
        jnp.einsum("qnhe,knhe->nhqk", query_blk, key_blk, preferred_element_type=jnp.float32)
        * scale
    )
    attention_odds = jnp.exp(scores - high_blk[..., None]) / total_blk[..., None]
    value_gradient = jnp.einsum(
        "nhqk,qnhe->knhe",
        attention_odds.astype(jnp.bfloat16),
        grad_blk,
        preferred_element_type=jnp.float32,
    )
    grad_chances = jnp.einsum(
        "qnhe,knhe->nhqk", grad_blk, value_blk, preferred_element_type=jnp.float32
    )
    grad_scores = (attention_odds * (grad_chances - delta_blk[..., None])).astype(jnp.bfloat16)
    grad_query = (
        jnp.einsum("nhqk,knhe->qnhe", grad_scores, key_blk, preferred_element_type=jnp.float32)
        * scale
    )
    grad_key = (
        jnp.einsum("nhqk,qnhe->knhe", grad_scores, query_blk, preferred_element_type=jnp.float32)
        * scale
    )
    return (grad_query, grad_key, value_gradient)


def on_device(
    features,
    link_pattern,
    row_gain,
    row_proj,
    row_out,
    column_norm_gain,
    col_proj,
    col_out,
    cotangent,
):
    site_dev, hap_dev, width = features.shape
    heads = width // HEAD_DIM
    blocks = site_dev // BLK
    devices = lax.axis_size("site")
    position = lax.axis_index("site")
    first_local = position * blocks
    normed = norm_rows(features, row_gain).astype(jnp.bfloat16)
    packed = project(normed, row_proj).astype(jnp.bfloat16)
    query = packed[..., :width]
    key = packed[..., width : 2 * width]
    value = packed[..., 2 * width :]
    start_state = tuple(
        (
            (
                jnp.zeros((BLK, hap_dev, heads, HEAD_DIM), jnp.float32),
                jnp.full((hap_dev, heads, BLK), -jnp.inf, jnp.float32),
                jnp.zeros((hap_dev, heads, BLK), jnp.float32),
            )
            for qblock in range(blocks)
        )
    )
    key_piece = lax.all_gather(key, "site", axis=0, tiled=True)
    value_piece = lax.all_gather(value, "site", axis=0, tiled=True)
    count = key_piece.shape[0] // BLK
    first_key = jnp.int32(0) // BLK
    qblock = 0
    query_blk = block_of(query, qblock)

    def fold_visit(kblock, state, query_blk=query_blk, qblock=qblock):
        key_blk = block_of(key_piece, kblock)
        value_blk = block_of(value_piece, kblock)
        linked = link_pattern[first_local + qblock, kblock] > 0
        return lax.cond(
            linked,
            lambda inside: online_block(inside, query_blk, key_blk, value_blk),
            lambda inside: inside,
            state,
        )

    updated = [lax.fori_loop(0, count, fold_visit, start_state[qblock])]
    states = tuple(updated)
    attended = jnp.concatenate(
        [
            (state[0] / jnp.transpose(state[2], (2, 0, 1))[..., None]).reshape(BLK, hap_dev, width)
            for state in states
        ],
        axis=0,
    ).astype(jnp.bfloat16)
    highs = jnp.stack([state[1] for state in states])
    totals = jnp.stack([state[2] for state in states])
    hidden = (features.astype(jnp.float32) + project(attended, row_out)).astype(jnp.bfloat16)
    column_hidden, column_grad = (
        lax.all_to_all(hidden, "hap", split_axis=0, concat_axis=1, tiled=True),
        lax.all_to_all(cotangent, "hap", split_axis=0, concat_axis=1, tiled=True),
    )
    column_output, saved = column_forward(column_hidden, column_norm_gain, col_proj, col_out)
    column_grad_hidden, grad_col_proj, grad_col_out = column_backward(
        column_hidden, column_norm_gain, col_proj, col_out, saved, column_grad
    )
    out_features, grad_hidden = (
        lax.all_to_all(column_output, "hap", split_axis=1, concat_axis=0, tiled=True),
        lax.all_to_all(column_grad_hidden, "hap", split_axis=1, concat_axis=0, tiled=True),
    )
    grad_row_out = weight_grad(attended, grad_hidden)
    grad_att = project_back(grad_hidden, row_out).astype(jnp.bfloat16)
    delta_all = jnp.sum(
        split_heads(grad_att).astype(jnp.float32) * split_heads(attended).astype(jnp.float32),
        axis=-1,
    )
    deltas = jnp.transpose(delta_all.reshape(blocks, BLK, hap_dev, heads), (0, 2, 3, 1))
    zeros = jnp.zeros((site_dev, hap_dev, width), jnp.float32)

    def key_lap(lap_index, carry):
        key_now, value_now, dkey_now, dvalue_now, dquery = carry
        owner = (position - lap_index + devices) % devices
        first_key = owner * blocks
        qblock = 0
        query_blk = block_of(query, qblock)
        grad_blk = block_of(grad_att, qblock)

        def key_visit(kblock, inner, qblock=qblock, query_blk=query_blk, grad_blk=grad_blk):
            linked = link_pattern[first_local + qblock, first_key + kblock] > 0

            def work(accums):
                key_gradient_total, dvalue_acc, dquery_acc = accums
                grad_query, grad_key, value_gradient = pair_grads(
                    query_blk,
                    grad_blk,
                    highs[qblock],
                    totals[qblock],
                    deltas[qblock],
                    block_of(key_now, kblock),
                    block_of(value_now, kblock),
                )
                return (
                    add_block(key_gradient_total, grad_key),
                    add_block(dvalue_acc, value_gradient),
                    add_block(dquery_acc, grad_query),
                )

            return lax.cond(linked, work, lambda accums: accums, inner)

        dkey_now, dvalue_now, dquery = lax.fori_loop(
            0, blocks, key_visit, (dkey_now, dvalue_now, dquery)
        )
        key_now, value_now = passed_along((key_now, value_now), "site", 1)
        dkey_now, dvalue_now = (
            passed_along(dkey_now.astype(jnp.bfloat16), "site", 1).astype(dkey_now.dtype),
            passed_along(dvalue_now.astype(jnp.bfloat16), "site", 1).astype(dvalue_now.dtype),
        )
        return (key_now, value_now, dkey_now, dvalue_now, dquery)

    final = lax.fori_loop(0, devices, key_lap, (key, value, zeros, zeros, zeros))
    grad_query_all, grad_key_all, grad_value_all = (final[4], final[2], final[3])
    grad_packed = jnp.concatenate(
        [
            grad_query_all.astype(jnp.bfloat16),
            grad_key_all.astype(jnp.bfloat16),
            grad_value_all.astype(jnp.bfloat16),
        ],
        axis=-1,
    )
    grad_row_proj = weight_grad(normed, grad_packed)
    grad_normed = project_back(grad_packed, row_proj)
    grad_features = (
        grad_hidden.astype(jnp.float32) + norm_back(features, row_gain, grad_normed)
    ).astype(jnp.bfloat16)
    summed = lax.psum((grad_row_proj, grad_row_out, grad_col_proj, grad_col_out), ("site", "hap"))
    return (out_features, grad_features, summed[0], summed[1], summed[2], summed[3])


def solution(mesh):
    placed = (P("site", "hap", None), P(), P(), P(), P(), P(), P(), P(), P("site", "hap", None))
    return jax.shard_map(
        on_device,
        mesh=mesh,
        in_specs=placed,
        out_specs=(P("site", "hap", None), P("site", "hap", None), P(), P(), P(), P()),
        check_vma=False,
    )
```

profile of v0, /device:TPU:0, one launch (start us, length us, event | category | flops | bytes accessed | tf_op | source)
XLA Modules:
  0.0 275.4 jit_solution(16396425500454593963)
XLA Ops:
  7.7 1.5 reduce.18
  9.8 6.5 %all-to-all-start.2 = ((bf16[8,2,2048]{2,1,0:T(2,128)(2,1)}), bf16[8,2,2048]{2,1,0:T(2,128)(2,1)S(1)}, u32[]{:S(2)}, u32[]{:S(2)}) async-start(bf16[8,2,2048]{2,1,0:T(2,128)(2,1)} %reshape.396), calls=%async_computation.2 | async-start | bytes 131072 | tf_op jit(solution)/shard_map/all_to_all | solution.py:253
  17.3 1.2 fusion.22
  18.7 9.0 %all_gather.6 = bf16[512,1,256]{2,0,1:T(8,128)(2,1)S(1)} all-gather(bf16[128,1,256]{2,0,1:T(8,128)(2,1)S(1)} %get-tuple-element.1020), channel_id=1, replica_groups=mesh['site'=4,'hap'=8] {'site'}, dimensions={0}, use_global_device_ids=true | all-gather | bytes 327680 | tf_op jit(solution)/shard_map/all_gather | solution.py:221
  27.8 9.0 %all_gather.7 = bf16[512,1,256]{2,0,1:T(8,128)(2,1)S(1)} all-gather(bf16[128,1,256]{2,0,1:T(8,128)(2,1)S(1)} %get-tuple-element.1018), channel_id=1, replica_groups=mesh['site'=4,'hap'=8] {'site'}, dimensions={0}, use_global_device_ids=true | all-gather | bytes 327680 | tf_op jit(solution)/shard_map/all_gather | solution.py:222
  37.7 7.8 %while.68 = (s32[]{:T(128)}, f32[128,1,8,32]{0,3,2,1:T(8,128)S(1)}, f32[1,8,128]{2,1,0:T(8,128)S(1)}, f32[1,8,128]{2,1,0:T(8,128)S(1)}, s32[4,4]{1,0:T(4,128)S(1...) while((s32[]{:T(128)}, f32[128,1,8,32]{0,3,2,1:T(8,128)S(1)}, ...), condition=%wide.region_7.0_spmd, body=%wide.region_2.0_spmd.sunk | while | flops 59444232 | bytes 2359601 | solution.py:239
  38.9 0.9 conditional.5
  41.1 0.9 conditional.5
  43.2 0.9 conditional.5
  45.5 0.9 copy-done.4
  48.1 5.1 %all-to-all-start = ((bf16[8,2,2048]{2,1,0:T(2,128)(2,1)}), bf16[8,2,2048]{2,1,0:T(2,128)(2,1)S(1)}, u32[]{:S(2)}, u32[]{:S(2)}) async-start(bf16[8,2,2048]{2,1,0:T(2,128)(2,1)} %reshape.394), calls=%async_computation | async-start | bytes 131072 | tf_op jit(solution)/shard_map/all_to_all | solution.py:252
  53.3 0.9 copy-done.3
  54.6 4.6 %all-to-all-done = bf16[8,2,2048]{2,1,0:T(2,128)(2,1)S(1)} async-done(((bf16[8,2,2048]{2,1,0:T(2,128)(2,1)}), bf16[8,2,2048]{2,1,0:T(2,128)(2,1)S(1)}, u32[]{:S(2)}, u32[]{:S(2)}) %all-to-all-start) | async-done | bytes 65568 | tf_op jit(solution)/shard_map/all_to_all | solution.py:252
  64.5 1.3 convolution_bitcast_fusion.1
  66.8 3.4 %all-to-all-start.3 = ((bf16[16,8,256]{2,0,1:T(8,128)(2,1)}), bf16[16,8,256]{2,0,1:T(8,128)(2,1)S(1)}, u32[]{:S(2)}, u32[]{:S(2)}) async-start(bf16[16,8,256]{2,0,1:T(8,128)(2,1)} %copy.129), calls=%async_computation.3 | async-start | bytes 131072 | tf_op jit(solution)/shard_map/all_to_all | solution.py:261
  71.2 0.9 convolution_bitcast_fusion.3
  72.1 3.9 %all-to-all-done.3 = bf16[16,8,256]{2,0,1:T(8,128)(2,1)S(1)} async-done(((bf16[16,8,256]{2,0,1:T(8,128)(2,1)}), bf16[16,8,256]{2,0,1:T(8,128)(2,1)S(1)}, u32[]{:S(2)}, u32[]{:S(2)}) %all-to-all-start.3) | async-done | bytes 65568 | tf_op jit(solution)/shard_map/all_to_all | solution.py:261
  76.0 3.4 %all-to-all-start.1 = ((bf16[16,8,256]{2,0,1:T(8,128)(2,1)}), bf16[16,8,256]{2,0,1:T(8,128)(2,1)S(1)}, u32[]{:S(2)}, u32[]{:S(2)}) async-start(bf16[16,8,256]{2,0,1:T(8,128)(2,1)} %copy.115), calls=%async_computation.1 | async-start | bytes 131072 | tf_op jit(solution)/shard_map/all_to_all | solution.py:260
  79.9 46.3 %while.69 = (s32[]{:T(128)}, bf16[128,1,256]{0,2,1:T(8,128)(2,1)S(1)}, bf16[128,1,256]{0,2,1:T(8,128)(2,1)S(1)}, f32[128,1,256]{0,2,1:T(8,128)S(1)}, f32[128,1,2...) while((s32[]{:T(128)}, ...), condition=%wide.region_19.0_spmd.clone, body=%wide.region_16.19_spmd.clone.sunk | while | flops 43221012 | bytes 7025312 | solution.py:312
  81.2 1.7 conditional.6
  82.9 0.9 collective-permute-start.3
  84.5 2.0 collective-permute-start
  86.5 1.5 collective-permute-start.1
  88.0 0.8 collective-permute-done.3
  88.8 1.4 collective-permute-done.2
  90.2 1.4 collective-permute-done
  91.6 0.8 collective-permute-done.1
  93.9 2.1 collective-permute-start.2
  96.0 2.2 collective-permute-start
  98.8 0.8 collective-permute-done.3
  99.7 0.8 collective-permute-done.2
  100.5 1.3 collective-permute-done
  101.8 1.5 collective-permute-done.1
  104.6 1.7 conditional.6
  107.1 4.3 %collective-permute-start.1 = (bf16[128,1,256]{0,2,1:T(8,128)(2,1)S(1)}, bf16[128,1,256]{0,2,1:T(8,128)(2,1)S(1)}, u32[]{:S(2)}, u32[]{:S(2)}) collective-permute-start(bf16[128,1,256]{0,2,1:T(8,128)(2,1)S(1)} %copy.226), channel_id=1, source_target_pairs={{0,8},{8,16},{16,24},{24,0},{1,9},{9,17},{17,25},{25,1},{2,10},{10... | collective-permute-start | bytes 196616 | tf_op jit(solution)/shard_map/while/body/eval_jaxpr/ppermute | solution.py:15
  115.2 1.7 conditional.6
  116.9 1.8 collective-permute-start.3
  118.7 1.7 collective-permute-start.2
  120.4 1.6 collective-permute-start.1
  122.1 1.8 collective-permute-done.2
  123.9 1.6 collective-permute-done
  126.3 1.3 fusion.54
  127.5 0.9 fusion.72
  128.4 1.0 copy-done.5
  130.0 0.8 fusion.50
  130.8 132.5 %all-reduce.3.cloned.1.call-done = (f32[256,768]{1,0:T(8,128)}, f32[256,256]{1,0:T(8,128)}, f32[256,768]{1,0:T(8,128)}, f32[256,256]{1,0:T(8,128)}) async-done(((f32[256,768]{1,0:T(8,128)}, f32[256,256]{1,0:T(8,128)}, f32[256,768]{1,0:T(8,128)}, f32[256,256]{1,0:T(8,128)}), (f32[256,768]{1,0:T(8,128)}, f32[256,256]{1,0:T(8,128)}, f32[256,768]{1,0:T(8,128)}, ...) | async-done | bytes 2097168 | tf_op jit(solution)/shard_map/psum | solution.py:327
  263.9 2.2 copy.242
  266.7 0.9 copy.244
  (193 shorter events, 34.0 us)
Async XLA Ops:
  7.2 52.4 %copy-start = (bf16[256,768]{1,0:T(8,128)(2,1)S(1)}, bf16[256,768]{1,0:T(8,128)(2,1)}, u32[]{:S(2)}) copy-start(bf16[256,768]{1,0:T(8,128)(2,1)} %param.23) | copy-start | bytes 1179652
  9.8 6.5 %copy-start.1 = (bf16[128,1,256]{2,0,1:T(8,128)(2,1)S(1)}, bf16[128,1,256]{2,0,1:T(8,128)(2,1)}, u32[]{:S(2)}) copy-start(bf16[128,1,256]{2,0,1:T(8,128)(2,1)} %param.17) | copy-start | bytes 196612
  9.8 38.3 %all-to-all-start.2 = ((bf16[8,2,2048]{2,1,0:T(2,128)(2,1)}), bf16[8,2,2048]{2,1,0:T(2,128)(2,1)S(1)}, u32[]{:S(2)}, u32[]{:S(2)}) async-start(bf16[8,2,2048]{2,1,0:T(2,128)(2,1)} %reshape.396), calls=%async_computation.2 | async-start | bytes 131072 | tf_op jit(solution)/shard_map/all_to_all | solution.py:253
  16.6 0.7 copy-start.10
  37.0 0.7 copy-start.8
  45.4 0.9 copy-start.4
  48.1 11.0 %all-to-all-start = ((bf16[8,2,2048]{2,1,0:T(2,128)(2,1)}), bf16[8,2,2048]{2,1,0:T(2,128)(2,1)S(1)}, u32[]{:S(2)}, u32[]{:S(2)}) async-start(bf16[8,2,2048]{2,1,0:T(2,128)(2,1)} %reshape.394), calls=%async_computation | async-start | bytes 131072 | tf_op jit(solution)/shard_map/all_to_all | solution.py:252
  53.3 0.9 copy-start.3
  59.6 0.7 copy-start.9
  66.8 9.2 %all-to-all-start.3 = ((bf16[16,8,256]{2,0,1:T(8,128)(2,1)}), bf16[16,8,256]{2,0,1:T(8,128)(2,1)S(1)}, u32[]{:S(2)}, u32[]{:S(2)}) async-start(bf16[16,8,256]{2,0,1:T(8,128)(2,1)} %copy.129), calls=%async_computation.3 | async-start | bytes 131072 | tf_op jit(solution)/shard_map/all_to_all | solution.py:261
  76.0 52.4 %all-to-all-start.1 = ((bf16[16,8,256]{2,0,1:T(8,128)(2,1)}), bf16[16,8,256]{2,0,1:T(8,128)(2,1)S(1)}, u32[]{:S(2)}, u32[]{:S(2)}) async-start(bf16[16,8,256]{2,0,1:T(8,128)(2,1)} %copy.115), calls=%async_computation.1 | async-start | bytes 131072 | tf_op jit(solution)/shard_map/all_to_all | solution.py:260
  79.3 183.9 %all-reduce.3.cloned.1.call-start = ((), (), s32[]{:S(2)}) async-start(), calls=%async_computation.4 | async-start | bytes 4194304 | tf_op jit(solution)/shard_map/psum | solution.py:327
  82.9 5.9 %collective-permute-start.3 = (bf16[128,1,256]{0,2,1:T(8,128)(2,1)S(1)}, bf16[128,1,256]{0,2,1:T(8,128)(2,1)S(1)}, u32[]{:S(2)}, u32[]{:S(2)}) collective-permute-start(bf16[128,1,256]{0,2,1:T(8,128)(2,1)S(1)} %convert_element_type.373), channel_id=1, source_target_pairs={{0,8},{8,16},{16,24},{24,0},{1,9},{9,17},{17,25},{25,1},{2,10},{10... | collective-permute-start | bytes 196616 | tf_op jit(solution)/shard_map/while/body/eval_jaxpr/ppermute | solution.py:15
  83.9 6.3 %collective-permute-start.2 = (bf16[128,1,256]{0,2,1:T(8,128)(2,1)S(1)}, bf16[128,1,256]{0,2,1:T(8,128)(2,1)S(1)}, u32[]{:S(2)}, u32[]{:S(2)}) collective-permute-start(bf16[128,1,256]{0,2,1:T(8,128)(2,1)S(1)} %convert_element_type.371), channel_id=1, source_target_pairs={{0,8},{8,16},{16,24},{24,0},{1,9},{9,17},{17,25},{25,1},{2,10},{10... | collective-permute-start | bytes 196616 | tf_op jit(solution)/shard_map/while/body/eval_jaxpr/ppermute | solution.py:15
  84.5 7.1 %collective-permute-start = (bf16[128,1,256]{0,2,1:T(8,128)(2,1)S(1)}, bf16[128,1,256]{0,2,1:T(8,128)(2,1)S(1)}, u32[]{:S(2)}, u32[]{:S(2)}) collective-permute-start(bf16[128,1,256]{0,2,1:T(8,128)(2,1)S(1)} %copy.225), channel_id=1, source_target_pairs={{0,8},{8,16},{16,24},{24,0},{1,9},{9,17},{17,25},{25,1},{2,10},{10... | collective-permute-start | bytes 196616 | tf_op jit(solution)/shard_map/while/body/eval_jaxpr/ppermute | solution.py:15
  86.5 5.9 %collective-permute-start.1 = (bf16[128,1,256]{0,2,1:T(8,128)(2,1)S(1)}, bf16[128,1,256]{0,2,1:T(8,128)(2,1)S(1)}, u32[]{:S(2)}, u32[]{:S(2)}) collective-permute-start(bf16[128,1,256]{0,2,1:T(8,128)(2,1)S(1)} %copy.226), channel_id=1, source_target_pairs={{0,8},{8,16},{16,24},{24,0},{1,9},{9,17},{17,25},{25,1},{2,10},{10... | collective-permute-start | bytes 196616 | tf_op jit(solution)/shard_map/while/body/eval_jaxpr/ppermute | solution.py:15
  93.8 5.9 %collective-permute-start.3 = (bf16[128,1,256]{0,2,1:T(8,128)(2,1)S(1)}, bf16[128,1,256]{0,2,1:T(8,128)(2,1)S(1)}, u32[]{:S(2)}, u32[]{:S(2)}) collective-permute-start(bf16[128,1,256]{0,2,1:T(8,128)(2,1)S(1)} %convert_element_type.373), channel_id=1, source_target_pairs={{0,8},{8,16},{16,24},{24,0},{1,9},{9,17},{17,25},{25,1},{2,10},{10... | collective-permute-start | bytes 196616 | tf_op jit(solution)/shard_map/while/body/eval_jaxpr/ppermute | solution.py:15
  93.9 6.7 %collective-permute-start.2 = (bf16[128,1,256]{0,2,1:T(8,128)(2,1)S(1)}, bf16[128,1,256]{0,2,1:T(8,128)(2,1)S(1)}, u32[]{:S(2)}, u32[]{:S(2)}) collective-permute-start(bf16[128,1,256]{0,2,1:T(8,128)(2,1)S(1)} %convert_element_type.371), channel_id=1, source_target_pairs={{0,8},{8,16},{16,24},{24,0},{1,9},{9,17},{17,25},{25,1},{2,10},{10... | collective-permute-start | bytes 196616 | tf_op jit(solution)/shard_map/while/body/eval_jaxpr/ppermute | solution.py:15
  96.0 5.8 %collective-permute-start = (bf16[128,1,256]{0,2,1:T(8,128)(2,1)S(1)}, bf16[128,1,256]{0,2,1:T(8,128)(2,1)S(1)}, u32[]{:S(2)}, u32[]{:S(2)}) collective-permute-start(bf16[128,1,256]{0,2,1:T(8,128)(2,1)S(1)} %copy.225), channel_id=1, source_target_pairs={{0,8},{8,16},{16,24},{24,0},{1,9},{9,17},{17,25},{25,1},{2,10},{10... | collective-permute-start | bytes 196616 | tf_op jit(solution)/shard_map/while/body/eval_jaxpr/ppermute | solution.py:15
  98.1 5.2 %collective-permute-start.1 = (bf16[128,1,256]{0,2,1:T(8,128)(2,1)S(1)}, bf16[128,1,256]{0,2,1:T(8,128)(2,1)S(1)}, u32[]{:S(2)}, u32[]{:S(2)}) collective-permute-start(bf16[128,1,256]{0,2,1:T(8,128)(2,1)S(1)} %copy.226), channel_id=1, source_target_pairs={{0,8},{8,16},{16,24},{24,0},{1,9},{9,17},{17,25},{25,1},{2,10},{10... | collective-permute-start | bytes 196616 | tf_op jit(solution)/shard_map/while/body/eval_jaxpr/ppermute | solution.py:15
  106.3 5.5 %collective-permute-start.3 = (bf16[128,1,256]{0,2,1:T(8,128)(2,1)S(1)}, bf16[128,1,256]{0,2,1:T(8,128)(2,1)S(1)}, u32[]{:S(2)}, u32[]{:S(2)}) collective-permute-start(bf16[128,1,256]{0,2,1:T(8,128)(2,1)S(1)} %convert_element_type.373), channel_id=1, source_target_pairs={{0,8},{8,16},{16,24},{24,0},{1,9},{9,17},{17,25},{25,1},{2,10},{10... | collective-permute-start | bytes 196616 | tf_op jit(solution)/shard_map/while/body/eval_jaxpr/ppermute | solution.py:15
  106.4 6.1 %collective-permute-start.2 = (bf16[128,1,256]{0,2,1:T(8,128)(2,1)S(1)}, bf16[128,1,256]{0,2,1:T(8,128)(2,1)S(1)}, u32[]{:S(2)}, u32[]{:S(2)}) collective-permute-start(bf16[128,1,256]{0,2,1:T(8,128)(2,1)S(1)} %convert_element_type.371), channel_id=1, source_target_pairs={{0,8},{8,16},{16,24},{24,0},{1,9},{9,17},{17,25},{25,1},{2,10},{10... | collective-permute-start | bytes 196616 | tf_op jit(solution)/shard_map/while/body/eval_jaxpr/ppermute | solution.py:15
  106.7 6.5 %collective-permute-start = (bf16[128,1,256]{0,2,1:T(8,128)(2,1)S(1)}, bf16[128,1,256]{0,2,1:T(8,128)(2,1)S(1)}, u32[]{:S(2)}, u32[]{:S(2)}) collective-permute-start(bf16[128,1,256]{0,2,1:T(8,128)(2,1)S(1)} %copy.225), channel_id=1, source_target_pairs={{0,8},{8,16},{16,24},{24,0},{1,9},{9,17},{17,25},{25,1},{2,10},{10... | collective-permute-start | bytes 196616 | tf_op jit(solution)/shard_map/while/body/eval_jaxpr/ppermute | solution.py:15
  107.1 6.8 %collective-permute-start.1 = (bf16[128,1,256]{0,2,1:T(8,128)(2,1)S(1)}, bf16[128,1,256]{0,2,1:T(8,128)(2,1)S(1)}, u32[]{:S(2)}, u32[]{:S(2)}) collective-permute-start(bf16[128,1,256]{0,2,1:T(8,128)(2,1)S(1)} %copy.226), channel_id=1, source_target_pairs={{0,8},{8,16},{16,24},{24,0},{1,9},{9,17},{17,25},{25,1},{2,10},{10... | collective-permute-start | bytes 196616 | tf_op jit(solution)/shard_map/while/body/eval_jaxpr/ppermute | solution.py:15
  116.9 5.2 %collective-permute-start.3 = (bf16[128,1,256]{0,2,1:T(8,128)(2,1)S(1)}, bf16[128,1,256]{0,2,1:T(8,128)(2,1)S(1)}, u32[]{:S(2)}, u32[]{:S(2)}) collective-permute-start(bf16[128,1,256]{0,2,1:T(8,128)(2,1)S(1)} %convert_element_type.373), channel_id=1, source_target_pairs={{0,8},{8,16},{16,24},{24,0},{1,9},{9,17},{17,25},{25,1},{2,10},{10... | collective-permute-start | bytes 196616 | tf_op jit(solution)/shard_map/while/body/eval_jaxpr/ppermute | solution.py:15
  118.7 5.2 %collective-permute-start.2 = (bf16[128,1,256]{0,2,1:T(8,128)(2,1)S(1)}, bf16[128,1,256]{0,2,1:T(8,128)(2,1)S(1)}, u32[]{:S(2)}, u32[]{:S(2)}) collective-permute-start(bf16[128,1,256]{0,2,1:T(8,128)(2,1)S(1)} %convert_element_type.371), channel_id=1, source_target_pairs={{0,8},{8,16},{16,24},{24,0},{1,9},{9,17},{17,25},{25,1},{2,10},{10... | collective-permute-start | bytes 196616 | tf_op jit(solution)/shard_map/while/body/eval_jaxpr/ppermute | solution.py:15
  120.4 5.2 %collective-permute-start = (bf16[128,1,256]{0,2,1:T(8,128)(2,1)S(1)}, bf16[128,1,256]{0,2,1:T(8,128)(2,1)S(1)}, u32[]{:S(2)}, u32[]{:S(2)}) collective-permute-start(bf16[128,1,256]{0,2,1:T(8,128)(2,1)S(1)} %copy.225), channel_id=1, source_target_pairs={{0,8},{8,16},{16,24},{24,0},{1,9},{9,17},{17,25},{25,1},{2,10},{10... | collective-permute-start | bytes 196616 | tf_op jit(solution)/shard_map/while/body/eval_jaxpr/ppermute | solution.py:15
  120.4 5.8 %collective-permute-start.1 = (bf16[128,1,256]{0,2,1:T(8,128)(2,1)S(1)}, bf16[128,1,256]{0,2,1:T(8,128)(2,1)S(1)}, u32[]{:S(2)}, u32[]{:S(2)}) collective-permute-start(bf16[128,1,256]{0,2,1:T(8,128)(2,1)S(1)} %copy.226), channel_id=1, source_target_pairs={{0,8},{8,16},{16,24},{24,0},{1,9},{9,17},{17,25},{25,1},{2,10},{10... | collective-permute-start | bytes 196616 | tf_op jit(solution)/shard_map/while/body/eval_jaxpr/ppermute | solution.py:15
  128.4 1.0 copy-start.5
  263.9 2.2 copy-start.7
  263.9 2.9 %copy-start.2 = (f32[256,768]{1,0:T(8,128)S(1)}, f32[256,768]{1,0:T(8,128)}, u32[]{:S(2)}) copy-start(f32[256,768]{1,0:T(8,128)} %get-tuple-element.1297) | copy-start | bytes 2359300
  266.7 1.1 copy-start.6
Sparse Core Ops, SparseCore 0:
  128.5 134.6 all-reduce.2
where the time goes:
time: 277 us; the launch traced here: 275 us
  waiting for transfers between devices  156 us (56%)
  starting transfers between devices  38.5 us (14%)
  local copies, waits for them, and re-layouts  20.5 us (7%)
  blocking collectives  18 us (6%)
  matrix products  16.2 us (6%)
  between operations  14.6 us (5%)
  loops' own time  5.97 us (2%)
  other arithmetic  5.24 us (2%)
    psum x1, waiting for transfers between devices, on_device(): lax.psum((grad_row_proj, grad_row_out, grad_col_proj, grad_col_out), ('si...  132 us
    ppermute x16, starting transfers between devices, passed_along(): lax.ppermute(value, axis, [(i, (i + by) % length) for i in range(length)])  20.2 us
    ppermute x16, waiting for transfers between devices, passed_along(): lax.ppermute(value, axis, [(i, (i + by) % length) for i in range(length)])  15.5 us
    unnamed x38, local copies, waits for them, and re-layouts  12.3 us
    all_gather x1, blocking collectives, on_device(): key_piece = lax.all_gather(key, 'site', axis=0, tiled=True)  9 us
    all_gather x1, blocking collectives, on_device(): value_piece = lax.all_gather(value, 'site', axis=0, tiled=True)  8.97 us
    all_to_all x1, starting transfers between devices, on_device(): lax.all_to_all(cotangent, 'hap', split_axis=0, concat_axis=1, tiled=True)  6.46 us
  transfers between devices with their start and end apart: 21, of which 19 were waited for; matrix products, arithmetic and copies ran while one was open for 8% of the time, Pallas kernels for 0%

commit v1 on v0

v1 whole, which is shorter than its diff:
```python
import functools

import jax
import jax.numpy as jnp
from jax import lax
from jax.experimental import pallas as pl
from jax.experimental.pallas import tpu as pltpu
from jax.sharding import PartitionSpec as P

HEAD_DIM = 32
EPSILON = 1e-05
LOG2E = 1.4426950408889634
SCALE = HEAD_DIM ** (-0.5)
F32 = jnp.float32
BF16 = jnp.bfloat16
VMEM = pl.BlockSpec(memory_space=pltpu.VMEM)
SMEM = pl.BlockSpec(memory_space=pltpu.SMEM)
PARAMS = pltpu.CompilerParams(vmem_limit_bytes=48 << 20)


def mm(a, b):
    return lax.dot_general(a, b, (((1,), (0,)), ((), ())), preferred_element_type=F32)


def mm_nt(a, b):
    return lax.dot_general(a, b, (((1,), (1,)), ((), ())), preferred_element_type=F32)


def mm_tn(a, b):
    return lax.dot_general(a, b, (((0,), (0,)), ((), ())), preferred_element_type=F32)


def norm_parts(x):
    centred = x - jnp.mean(x, axis=-1, keepdims=True)
    rstd = lax.rsqrt(jnp.mean(centred * centred, axis=-1, keepdims=True) + EPSILON)
    return centred * rstd, rstd


def norm_back(xhat, rstd, gain, grad):
    scaled = grad * gain
    first = jnp.mean(scaled, axis=-1, keepdims=True)
    second = jnp.mean(scaled * xhat, axis=-1, keepdims=True)
    return rstd * (scaled - first - xhat * second)


def head_lanes(width, head):
    return lax.broadcasted_iota(jnp.int32, (1, width), 1) // HEAD_DIM == head


def only_head(values, head):
    return jnp.where(head_lanes(values.shape[1], head), values, jnp.zeros_like(values))


def flat_rows(values, dtype=BF16):
    wide = values.astype(F32)
    return wide.reshape(wide.shape[0] * wide.shape[1], wide.shape[2]).astype(dtype)


def call(body, outs, *operands, scalars=0, scratch=()):
    return pl.pallas_call(
        body,
        out_shape=[jax.ShapeDtypeStruct(s, d) for s, d in outs],
        in_specs=[SMEM] * scalars + [VMEM] * (len(operands) - scalars),
        out_specs=[VMEM] * len(outs),
        scratch_shapes=list(scratch),
        compiler_params=PARAMS,
    )(*operands)


def row_forward(sites, haps, idx, link, *refs):
    pieces = refs[:sites]
    gain, w_t = refs[sites : sites + 2]
    att_out, p_out, q_out, v_out, kt_out, n_out = refs[sites + 2 :]
    me = idx[0]
    rows = pieces[0].shape[0]
    width = q_out.shape[1]
    for k in range(sites):
        xhat, _ = norm_parts(pieces[k][...].astype(F32))
        n_out[k * rows : (k + 1) * rows, :] = (xhat * gain[...]).astype(BF16)
    normed = n_out[...]
    q = mm_nt(normed, w_t[:width, :]).astype(BF16)
    key = mm_nt(normed, w_t[width : 2 * width, :]).astype(BF16)
    q_out[...] = q
    v_out[...] = mm_nt(normed, w_t[2 * width :, :]).astype(BF16)
    kt_out[...] = mm_nt(w_t[width : 2 * width, :], normed).astype(BF16)
    v_t = mm_nt(w_t[2 * width :, :], normed).astype(BF16)
    att_t = []
    for h in range(width // HEAD_DIM):
        key_h = only_head(key, h)
        for b in range(sites):
            here = pl.ds(b * rows, rows)
            scores = mm_nt(key_h, q[b * rows : (b + 1) * rows]) * (SCALE * LOG2E)
            parts = [
                scores[a * rows : (a + 1) * rows]
                + jnp.where(link[me ^ b, me ^ a] > 0, 0.0, -jnp.inf)
                for a in range(sites)
            ]
            high = functools.reduce(
                jnp.maximum, [jnp.max(part, axis=0, keepdims=True) for part in parts]
            )
            parts = [jnp.exp2(part - high) for part in parts]
            total = sum(jnp.sum(part, axis=0, keepdims=True) for part in parts)
            inverse = 1.0 / total
            for a in range(sites):
                p_out[h, a * rows : (a + 1) * rows, here] = (parts[a] * inverse).astype(BF16)
        att_t.append(mm(v_t[h * HEAD_DIM : (h + 1) * HEAD_DIM], p_out[h]))
    att = jnp.transpose(jnp.concatenate(att_t, axis=0))
    for b in range(sites):
        block = att[b * rows : (b + 1) * rows].reshape(haps, rows // haps, width)
        att_out[pl.ds((me ^ b) * haps, haps)] = block.astype(BF16)


def column_step(
    sites, haps, xc, at, row_out, gain, col_proj, kv_t_w, col_out, ga_out, og_out, n_out, gp_out, at_out
):
    width = row_out.shape[0]
    heads = width // HEAD_DIM
    group = width // sites
    xc_all = flat_rows(xc[...], F32)
    rows = xc_all.shape[0]
    per = rows // haps
    cot_f = xc_all[:, width:]
    cot = cot_f.astype(BF16)
    hid = xc_all[:, :width]
    for i in range(sites):
        a_i = flat_rows(at[i * haps : (i + 1) * haps])
        hid = hid + mm(a_i, row_out[i * group : (i + 1) * group, :])
    hid = hid.astype(BF16).astype(F32)
    grad_att = mm_nt(cot, col_out[...]).astype(BF16)
    xhat, rstd = norm_parts(hid)
    normed = (xhat * gain[...]).astype(BF16)
    n_out[...] = normed
    packed = mm(normed, col_proj[...]).astype(BF16)
    q = packed[:, :width]
    key = packed[:, width : 2 * width]
    val = packed[:, 2 * width :]
    kv_t = mm_nt(kv_t_w[...], normed).astype(BF16)
    key_st = jnp.concatenate([only_head(key, h) for h in range(heads)], axis=0)
    val_st = jnp.concatenate([only_head(val, h) for h in range(heads)], axis=0)
    scores = mm_nt(key_st, q) * (SCALE * LOG2E)
    dprob = mm_nt(val_st, grad_att)
    same = (
        lax.broadcasted_iota(jnp.int32, (rows, rows), 0) % per
        == lax.broadcasted_iota(jnp.int32, (rows, rows), 1) % per
    )
    att_t, dq_t, prob16, ds16 = [], [], [], []
    for h in range(heads):
        cols = slice(h * HEAD_DIM, (h + 1) * HEAD_DIM)
        s_h = jnp.where(same, scores[h * rows : (h + 1) * rows], -jnp.inf)
        e_h = jnp.exp2(s_h - jnp.max(s_h, axis=0, keepdims=True))
        inverse = 1.0 / jnp.sum(e_h, axis=0, keepdims=True)
        att_t.append(mm(kv_t[width:, :][cols], e_h.astype(BF16)) * inverse)
        p_h = e_h * inverse
        d_h = dprob[h * rows : (h + 1) * rows]
        delta = jnp.sum(p_h * d_h, axis=0, keepdims=True)
        ds_h = (p_h * (d_h - delta)).astype(BF16)
        prob16.append(p_h.astype(BF16))
        ds16.append(ds_h)
        dq_t.append(mm(kv_t[:width, :][cols], ds_h))
    att_t = jnp.concatenate(att_t, axis=0)
    at_out[...] = att_t.astype(BF16)
    att = jnp.transpose(att_t).astype(BF16)
    out = hid + mm(att, col_out[...])
    dv_all = mm(jnp.concatenate(prob16, axis=0), grad_att)
    dk_all = mm(jnp.concatenate(ds16, axis=0), q)
    dv = sum(
        jnp.where(head_lanes(width, h), dv_all[h * rows : (h + 1) * rows], 0.0) for h in range(heads)
    )
    dk = sum(
        jnp.where(head_lanes(width, h), dk_all[h * rows : (h + 1) * rows], 0.0) for h in range(heads)
    )
    dq = jnp.transpose(jnp.concatenate(dq_t, axis=0))
    packed_grad = jnp.concatenate([dq * SCALE, dk * SCALE, dv], axis=1).astype(BF16)
    gp_out[...] = packed_grad
    grad_normed = mm_nt(packed_grad, col_proj[...])
    grad_hidden = (cot_f + norm_back(xhat, rstd, gain[...], grad_normed)).astype(BF16)
    for i in range(sites):
        g_i = mm_nt(grad_hidden, row_out[i * group : (i + 1) * group, :])
        ga_out[i * haps : (i + 1) * haps] = g_i.reshape(haps, per, group).astype(BF16)
    both = jnp.concatenate([out, grad_hidden.astype(F32)], axis=1)
    og_out[...] = both.reshape(haps, per, 2 * width).astype(BF16)


def column_weights(sites, haps, xc, at, og, normed, gp, att_t, w_out):
    width = normed.shape[1]
    group = width // sites
    cot = flat_rows(xc[:, :, width:])
    grad_hidden = flat_rows(og[:, :, width:])
    w_out[:, : 3 * width] = mm_tn(normed[...], gp[...]).astype(BF16)
    w_out[:, 3 * width : 4 * width] = mm(att_t[...], cot).astype(BF16)
    for i in range(sites):
        a_i = flat_rows(at[i * haps : (i + 1) * haps])
        w_out[i * group : (i + 1) * group, 4 * width :] = mm_tn(a_i, grad_hidden).astype(BF16)


def row_backward(sites, haps, idx, g_in, prob, q, val, key_t, normed, *refs):
    gp_outs = refs[:sites]
    w_out, g_all, ds_all = refs[sites:]
    me = idx[0]
    total, width = q.shape
    rows = total // sites
    for b in range(sites):
        g_all[b * rows : (b + 1) * rows, :] = flat_rows(g_in[pl.ds((me ^ b) * haps, haps)])
    dk = jnp.zeros((total, width), F32)
    dv = jnp.zeros((total, width), F32)
    dq_t = []
    for h in range(width // HEAD_DIM):
        val_h = only_head(val[...], h)
        dv = dv + mm(prob[h], only_head(g_all[...], h))
        for b in range(sites):
            here = pl.ds(b * rows, rows)
            dprob = mm_nt(val_h, g_all[b * rows : (b + 1) * rows, :])
            p_b = prob[h, :, here].astype(F32)
            delta = jnp.sum(p_b * dprob, axis=0, keepdims=True)
            ds_all[:, here] = (p_b * (dprob - delta)).astype(BF16)
        dk = dk + mm(ds_all[...], only_head(q[...], h))
        dq_t.append(mm(key_t[h * HEAD_DIM : (h + 1) * HEAD_DIM, :], ds_all[...]))
    dq_t = jnp.concatenate(dq_t, axis=0) * SCALE
    dk16 = (dk * SCALE).astype(BF16)
    dv16 = dv.astype(BF16)
    w_out[:width, :] = mm(dq_t.astype(BF16), normed[...]).astype(BF16)
    w_out[width : 2 * width, :] = mm_tn(dk16, normed[...]).astype(BF16)
    w_out[2 * width :, :] = mm_tn(dv16, normed[...]).astype(BF16)
    dq = jnp.transpose(dq_t).astype(BF16)
    joined = jnp.concatenate([dq, dk16, dv16], axis=1)
    for b in range(sites):
        gp_outs[b][...] = joined[b * rows : (b + 1) * rows]


def row_finish(sites, idx, feats, gain, w_all, og, *refs):
    gps = refs[:sites]
    out_ref, gf_ref = refs[sites:]
    me = idx[0]
    width = feats.shape[1]
    both = flat_rows(og[...], F32)
    grad_normed = sum(mm(gps[k][...], w_all[me ^ k]) for k in range(sites))
    xhat, rstd = norm_parts(feats[...].astype(F32))
    grad = both[:, width:] + norm_back(xhat, rstd, gain[...], grad_normed)
    out_ref[...] = both[:, :width].astype(BF16)
    gf_ref[...] = grad.astype(BF16)


def sum_parts(x_ref, o_ref):
    o_ref[...] = jnp.sum(x_ref[...].astype(F32), axis=0).astype(BF16)


def weights_finish(sites, row_w, col_w, rp, ro, cp, co):
    width = ro.shape[0]
    group = width // sites
    cols = flat_rows(col_w[...], F32)
    cp[...] = cols[:, : 3 * width]
    co[...] = cols[:, 3 * width : 4 * width]
    ro[...] = cols[:, 4 * width :]
    rows = flat_rows(row_w[...], F32)
    ordered = [
        rows[(3 * i + part) * group : (3 * i + part + 1) * group]
        for part in range(3)
        for i in range(sites)
    ]
    rp[...] = jnp.transpose(jnp.concatenate(ordered, axis=0))


def exchange(value, axis):
    return lax.all_to_all(value, axis, 0, 0, tiled=True)


def swapped(value, axis, by):
    length = lax.axis_size(axis)
    return lax.ppermute(value, axis, [(i, i ^ by) for i in range(length)])


def spread(value, axis, length):
    return exchange(jnp.broadcast_to(value[None], (length,) + value.shape), axis)


def on_device(
    features,
    link_pattern,
    row_gain,
    row_proj,
    row_out,
    column_norm_gain,
    col_proj,
    col_out,
    cotangent,
):
    rows, _, width = features.shape
    sites, haps = lax.axis_size("site"), lax.axis_size("hap")
    count = sites * haps
    per = rows // haps
    group = width // sites
    heads = group // HEAD_DIM
    total = rows * sites
    both_axes = ("site", "hap")
    me = lax.axis_index("site")
    idx = me.reshape(1).astype(jnp.int32)
    feats = features.reshape(rows, width)
    cot = cotangent.reshape(rows, width)
    gain_r = row_gain.reshape(1, width)
    gain_c = column_norm_gain.reshape(1, width)

    pieces = [feats] + [swapped(feats, "site", k) for k in range(1, sites)]
    xc = exchange(jnp.concatenate([feats, cot], axis=1).reshape(haps, per, 2 * width), "hap")
    w_all = jnp.transpose(row_proj.reshape(width, 3, sites, group), (2, 1, 3, 0)).reshape(
        sites, 3 * group, width
    )
    w_t = lax.dynamic_index_in_dim(w_all, me, 0, keepdims=False)
    kv_t_w = jnp.transpose(col_proj[:, width:])

    att, prob, q, val, key_t, normed = call(
        functools.partial(row_forward, sites, haps),
        [
            ((count, per, group), BF16),
            ((heads, total, total), BF16),
            ((total, group), BF16),
            ((total, group), BF16),
            ((group, total), BF16),
            ((total, width), BF16),
        ],
        idx, link_pattern, *pieces, gain_r, w_t, scalars=2,
    )
    at = exchange(att, both_axes)
    ga, og, col_normed, col_gp, col_att_t = call(
        functools.partial(column_step, sites, haps),
        [
            ((count, per, group), BF16),
            ((haps, per, 2 * width), BF16),
            ((rows, width), BF16),
            ((rows, 3 * width), BF16),
            ((width, rows), BF16),
        ],
        xc, at, row_out, gain_c, col_proj, kv_t_w, col_out,
    )
    g_in = exchange(ga, both_axes)
    (col_w,) = call(
        functools.partial(column_weights, sites, haps),
        [((width, 5 * width), BF16)],
        xc, at, og, col_normed, col_gp, col_att_t,
    )
    og_in = exchange(og, "hap")
    *gps, row_w = call(
        functools.partial(row_backward, sites, haps),
        [((rows, 3 * group), BF16)] * sites + [((3 * group, width), BF16)],
        idx, g_in, prob, q, val, key_t, normed, scalars=1,
        scratch=[pltpu.VMEM((total, group), BF16), pltpu.VMEM((total, total), BF16)],
    )
    col_parts = exchange(col_w.reshape(count, width // count, 5 * width), both_axes)
    (col_mine,) = call(sum_parts, [((width // count, 5 * width), BF16)], col_parts)
    row_parts = exchange(row_w.reshape(haps, 3 * group // haps, width), "hap")
    (row_mine,) = call(sum_parts, [((3 * group // haps, width), BF16)], row_parts)
    gps = [gps[0]] + [swapped(gps[k], "site", k) for k in range(1, sites)]
    out, grad = call(
        functools.partial(row_finish, sites),
        [((rows, width), BF16)] * 2,
        idx, feats, gain_r, w_all, og_in, *gps, scalars=1,
    )
    col_full = spread(col_mine, both_axes, count)
    row_full = spread(row_mine, both_axes, count)
    rp, ro, cp, co = call(
        functools.partial(weights_finish, sites),
        [((width, 3 * width), F32), ((width, width), F32)] * 2,
        row_full, col_full,
    )
    shape = (rows, 1, width)
    return (out.reshape(shape), grad.reshape(shape), rp, ro, cp, co)


def solution(mesh):
    data = P("site", "hap", None)
    return jax.shard_map(
        on_device,
        mesh=mesh,
        in_specs=(data, P(), P(), P(), P(), P(), P(), P(), data),
        out_specs=(data, data, P(), P(), P(), P()),
        check_vma=False,
    )
```

time: 277 us -> 133 us (0.48)
  waiting for transfers between devices: 156 us -> 69.8 us
  matrix products: 16.2 us -> 0 us
  between operations: 14.6 us -> 0.84 us
  local copies, waits for them, and re-layouts: 20.5 us -> 7.87 us
  Pallas kernels: 0 us -> 12.3 us
  blocking collectives: 18 us -> 9.14 us
  starting transfers between devices: 38.5 us -> 31.2 us
  loops' own time: 5.97 us -> 0 us
  other arithmetic: 5.24 us -> 0.67 us
    psum x1 -> x0, waiting for transfers between devices: 132 us -> none  [on_device(): lax.psum((grad_row_proj, grad_row_out, grad_col_proj, grad_col_out), ('si...]
    all_to_all x4 -> x7, waiting for transfers between devices: 8.43 us -> 59 us  [exchange(): return lax.all_to_all(value, axis, 0, 0, tiled=True)]
    all_gather x2 -> x0, blocking collectives: 18 us -> none  [the longest x1 9 us: on_device(): key_piece = lax.all_gather(key, 'site', axis=0, tiled=True)]
    dot_general x39 -> x0, matrix products: 16.2 us -> none  [the longest x4 4.32 us: weight_grad(): jnp.einsum('hyo,hyp->op', other_argument, incoming_gradient, preferred_el...]
    pallas_call x0 -> x8, Pallas kernels: none -> 12.3 us  [call(): pl.pallas_call(body, out_shape=[jax.ShapeDtypeStruct(s, d) for s, d in ou...]
    ppermute x16 -> x6, starting transfers between devices: 20.2 us -> 8.16 us  [swapped(): return lax.ppermute(value, axis, [(i, i ^ by) for i in range(length)])]
    all_to_all x0 -> x1, blocking collectives: none -> 9.14 us  [exchange(): return lax.all_to_all(value, axis, 0, 0, tiled=True)]
    unnamed x38 -> x30, local copies, waits for them, and re-layouts: 12.3 us -> 5.23 us
  transfers between devices with their start and end apart: 21 -> 13, of which waited for: 19 -> 13; matrix products, arithmetic and copies ran while one was open for 8% -> 2% of each run, Pallas kernels for 0% -> 4%
where the time goes in v1:
time: 133 us; the launch traced here: 132 us
  waiting for transfers between devices  69.8 us (52%)
  starting transfers between devices  31.2 us (23%)
  Pallas kernels  12.3 us (9%)
  blocking collectives  9.14 us (7%)
  local copies, waits for them, and re-layouts  7.87 us (6%)
    all_to_all x7, waiting for transfers between devices, exchange(): return lax.all_to_all(value, axis, 0, 0, tiled=True)  59 us
    all_to_all x7, starting transfers between devices, exchange(): return lax.all_to_all(value, axis, 0, 0, tiled=True)  23 us
    pallas_call x8, Pallas kernels, call(): pl.pallas_call(body, out_shape=[jax.ShapeDtypeStruct(s, d) for s, d in ou...  12.3 us
    ppermute x6, waiting for transfers between devices, swapped(): return lax.ppermute(value, axis, [(i, i ^ by) for i in range(length)])  10.8 us
    all_to_all x1, blocking collectives, exchange(): return lax.all_to_all(value, axis, 0, 0, tiled=True)  9.14 us
    ppermute x6, starting transfers between devices, swapped(): return lax.ppermute(value, axis, [(i, i ^ by) for i in range(length)])  8.16 us
    unnamed x30, local copies, waits for them, and re-layouts  5.23 us
  transfers between devices with their start and end apart: 13, of which 13 were waited for; matrix products, arithmetic and copies ran while one was open for 2% of the time, Pallas kernels for 4%

profile of v1, /device:TPU:0, one launch (start us, length us, event | category | flops | bytes accessed | tf_op | source)
XLA Modules:
  0.0 131.8 jit_solution(434764543014777660)
XLA Ops:
  0.6 4.0 %collective-permute-start.2 = (bf16[128,256]{1,0:T(8,128)(2,1)}, bf16[128,256]{1,0:T(8,128)(2,1)S(1)}, u32[]{:S(2)}, u32[]{:S(2)}) collective-permute-start(bf16[128,256]{1,0:T(8,128)(2,1)} %bitcast.20), channel_id=1, source_target_pairs={{0,24},{8,16},{16,8},{24,0},{1,25},{9,17},{17,9},{25,1},{2,26},{10... | collective-permute-start | bytes 196616 | tf_op jit(solution)/shard_map/ppermute | solution.py:269
  4.6 0.5 collective-permute-start.1
  5.1 0.1 collective-permute-start
  5.2 1.2 copy.17
  6.5 0.6 collective-permute-done.2.refs_3_
  7.1 2.0 %collective-permute-done.1.refs_2_ = bf16[128,256]{1,0:T(8,128)(2,1)S(1)} collective-permute-done((bf16[128,256]{1,0:T(8,128)(2,1)}, bf16[128,256]{1,0:T(8,128)(2,1)S(1)}, u32[]{:S(2)}, u32[]{:S(2)}) %collective-permute-start.1) | collective-permute-done | bytes 65568 | tf_op jit(solution)/shard_map/ppermute | solution.py:269
  9.1 0.5 collective-permute-done.refs_1_
  9.6 0.7 copy-done.8
  10.3 2.5 %shard_map.136 = (bf16[32,16,64]{2,1,0:T(8,128)(2,1)S(1)}, bf16[2,512,512]{2,1,0:T(8,128)(2,1)S(1)}, bf16[512,64]{1,0:T(8,128)(2,1)S(1)}, bf16[512,64]{1,0:T(8,1...) custom-call(s32[1]{0:T(128)} %bitcast.idx, s32[4,4]{1,0:T(4,128)S(1)} %copy-done.9, ...), custom_call_target="tpu_custom_call" | custom-call | tf_op jit(solution)/shard_map/pallas_call | solution.py:60
  12.8 0.8 reshape.60
  13.6 4.9 %all-to-all-start.1 = ((bf16[32,2,512]{2,1,0:T(2,128)(2,1)}), bf16[32,2,512]{2,1,0:T(2,128)(2,1)S(1)}, u32[]{:S(2)}, u32[]{:S(2)}) async-start(bf16[32,2,512]{2,1,0:T(2,128)(2,1)} %reshape.60), calls=%async_computation.1 | async-start | bytes 131072 | tf_op jit(solution)/shard_map/all_to_all | solution.py:264
  18.5 0.7 pad_maximum_fusion
  19.2 6.7 %all-to-all-done.1 = bf16[32,2,512]{2,1,0:T(2,128)(2,1)S(1)} async-done(((bf16[32,2,512]{2,1,0:T(2,128)(2,1)}), bf16[32,2,512]{2,1,0:T(2,128)(2,1)S(1)}, u32[]{:S(2)}, u32[]{:S(2)}) %all-to-all-start.1) | async-done | bytes 65568 | tf_op jit(solution)/shard_map/all_to_all | solution.py:264
  25.9 3.4 %all-to-all-start = ((bf16[8,16,512]{2,1,0:T(8,128)(2,1)}), bf16[8,16,512]{2,1,0:T(8,128)(2,1)S(1)}, u32[]{:S(2)}, u32[]{:S(2)}) async-start(bf16[8,16,512]{2,1,0:T(8,128)(2,1)} %pad_maximum_fusion), calls=%async_computation | async-start | bytes 262144 | tf_op jit(solution)/shard_map/all_to_all | solution.py:264
  29.3 0.9 slice-done
  30.2 0.1 copy.20
  30.4 0.1 reshape.61.at
  30.5 5.5 %all-to-all-done.xc = bf16[8,16,512]{2,1,0:T(8,128)(2,1)S(1)} async-done(((bf16[8,16,512]{2,1,0:T(8,128)(2,1)}), bf16[8,16,512]{2,1,0:T(8,128)(2,1)S(1)}, u32[]{:S(2)}, u32[]{:S(2)}) %all-to-all-start) | async-done | bytes 131104 | tf_op jit(solution)/shard_map/all_to_all | solution.py:264
  36.0 0.7 copy-done.10
  36.7 2.5 %shard_map.137 = (bf16[32,16,64]{2,1,0:T(8,128)(2,1)S(1)}, bf16[8,16,512]{2,1,0:T(8,128)(2,1)}, bf16[128,256]{1,0:T(8,128)(2,1)S(1)}, bf16[128,768]{1,0:T(8,128)(2,1)S(1)}, bf16[256,128]{1,0:T(8,128)(2,1)S(1)}) custom-call(bf16[8,16,512]{2,1,0:T(8,128)(2,1)S(1)} %all-to-all-done.xc, bf16[32,16,64]{2,1,0:T(8,128)(2,1)S(1)} %reshape.61.at, ...), custom_call_target="tpu_custom_call" | custom-call | tf_op jit(solution)/shard_map/pallas_call | solution.py:60
  39.2 0.6 copy-done.6
  39.9 0.1 reshape.62
  40.0 9.1 %all_to_all.40 = bf16[32,2,512]{2,1,0:T(2,128)(2,1)S(1)} all-to-all(bf16[32,2,512]{2,1,0:T(2,128)(2,1)S(1)} %reshape.62), channel_id=1, replica_groups=mesh['site'=4,'hap'=8] {'site','hap'}, dimensions={0} | all-to-all | bytes 131072 | tf_op jit(solution)/shard_map/all_to_all | solution.py:264
  49.1 3.4 %all-to-all-start.2 = ((bf16[8,16,512]{2,1,0:T(8,128)(2,1)}), bf16[8,16,512]{2,1,0:T(8,128)(2,1)S(1)}, u32[]{:S(2)}, u32[]{:S(2)}) async-start(bf16[8,16,512]{2,1,0:T(8,128)(2,1)} %get-tuple-element.29.og), calls=%async_computation.2 | async-start | bytes 262144 | tf_op jit(solution)/shard_map/all_to_all | solution.py:264
  52.5 0.1 reshape.63.g_in
  52.7 0.7 copy-done.5
  53.4 2.7 %shard_map.138 = (bf16[128,192]{1,0:T(8,128)(2,1)S(1)}, bf16[128,192]{1,0:T(8,128)(2,1)S(1)}, bf16[128,192]{1,0:T(8,128)(2,1)S(1)}, bf16[128,192]{1,0:T(8,128)(2,1)S(1)}, bf16[192,256]{1,0:T(8,128)(2,1)}) custom-call(s32[1]{0:T(128)} %bitcast.idx, bf16[32,16,64]{2,1,0:T(8,128)(2,1)S(1)} %reshape.63.g_in, bf16[2,512,512]{2,1,0:T(8,128)(2,1)S(1)} %get-tuple-element.31.prob, ...), custom_call_target="tpu_custom_call" | custom-call | tf_op jit(solution)/shard_map/pallas_call | solution.py:60
  56.1 3.1 %all-to-all-done.2.og = bf16[8,16,512]{2,1,0:T(8,128)(2,1)S(1)} async-done(((bf16[8,16,512]{2,1,0:T(8,128)(2,1)}), bf16[8,16,512]{2,1,0:T(8,128)(2,1)S(1)}, u32[]{:S(2)}, u32[]{:S(2)}) %all-to-all-start.2) | async-done | bytes 131104 | tf_op jit(solution)/shard_map/all_to_all | solution.py:264
  59.2 3.5 %all-to-all-start.4 = ((bf16[8,24,256]{2,1,0:T(8,128)(2,1)}), bf16[8,24,256]{2,1,0:T(8,128)(2,1)S(1)}, u32[]{:S(2)}, u32[]{:S(2)}) async-start(bf16[8,24,256]{2,1,0:T(8,128)(2,1)} %bitcast.13), calls=%async_computation.4 | async-start | bytes 196608 | tf_op jit(solution)/shard_map/all_to_all | solution.py:264
  62.7 2.1 %shard_map.141 = bf16[256,1280]{1,0:T(8,128)(2,1)} custom-call(bf16[8,16,512]{2,1,0:T(8,128)(2,1)S(1)} %all-to-all-done.xc, bf16[32,16,64]{2,1,0:T(8,128)(2,1)S(1)} %reshape.61.at, bf16[8,16,512]{2,1,0:T(8,128)(2,1)} %get-tuple-element.29.og, bf16[128,256]{1,0:T(8,128)(2,1)S(1)} %get-tuple-element.43.normed, bf16[128,768]{1,0:T(8,128)(2,1)S(1)} %get-tuple-element.44.gp, ...), custom_call_target="tpu_custom_call" | custom-call | tf_op jit(solution)/shard_map/pallas_call | solution.py:60
  64.8 4.2 %all-to-all-done.4.x_ref = bf16[8,24,256]{2,1,0:T(8,128)(2,1)S(1)} async-done(((bf16[8,24,256]{2,1,0:T(8,128)(2,1)}), bf16[8,24,256]{2,1,0:T(8,128)(2,1)S(1)}, u32[]{:S(2)}, u32[]{:S(2)}) %all-to-all-start.4) | async-done | bytes 98336 | tf_op jit(solution)/shard_map/all_to_all | solution.py:264
  69.0 2.6 %all-to-all-start.6 = ((bf16[32,8,1280]{2,1,0:T(8,128)(2,1)}), bf16[32,8,1280]{2,1,0:T(8,128)(2,1)S(1)}, u32[]{:S(2)}, u32[]{:S(2)}) async-start(bf16[32,8,1280]{2,1,0:T(8,128)(2,1)} %bitcast.14), calls=%async_computation.6 | async-start | bytes 1310720 | tf_op jit(solution)/shard_map/all_to_all | solution.py:264
  71.6 19.1 %all-to-all-done.6.x_ref = bf16[32,8,1280]{2,1,0:T(8,128)(2,1)S(1)} async-done(((bf16[32,8,1280]{2,1,0:T(8,128)(2,1)}), bf16[32,8,1280]{2,1,0:T(8,128)(2,1)S(1)}, u32[]{:S(2)}, u32[]{:S(2)}) %all-to-all-start.6) | async-done | bytes 655392 | tf_op jit(solution)/shard_map/all_to_all | solution.py:264
  90.8 0.8 broadcast_in_dim.4
  91.6 2.6 %all-to-all-start.5 = ((bf16[32,24,256]{2,1,0:T(8,128)(2,1)}), bf16[32,24,256]{2,1,0:T(8,128)(2,1)S(1)}, u32[]{:S(2)}, u32[]{:S(2)}) async-start(bf16[32,24,256]{2,1,0:T(8,128)(2,1)} %broadcast_in_dim.4), calls=%async_computation.5 | async-start | bytes 786432 | tf_op jit(solution)/shard_map/all_to_all | solution.py:264
  94.2 0.1 shard_map.142
  94.3 13.4 %all-to-all-done.5.row_w = bf16[32,24,256]{2,1,0:T(8,128)(2,1)S(1)} async-done(((bf16[32,24,256]{2,1,0:T(8,128)(2,1)}), bf16[32,24,256]{2,1,0:T(8,128)(2,1)S(1)}, u32[]{:S(2)}, u32[]{:S(2)}) %all-to-all-start.5) | async-done | bytes 393248 | tf_op jit(solution)/shard_map/all_to_all | solution.py:264
  107.7 0.9 broadcast_in_dim.5
  108.6 2.6 %all-to-all-start.7 = ((bf16[32,8,1280]{2,1,0:T(8,128)(2,1)}), bf16[32,8,1280]{2,1,0:T(8,128)(2,1)S(1)}, u32[]{:S(2)}, u32[]{:S(2)}) async-start(bf16[32,8,1280]{2,1,0:T(8,128)(2,1)} %broadcast_in_dim.5), calls=%async_computation.7 | async-start | bytes 1310720 | tf_op jit(solution)/shard_map/all_to_all | solution.py:264
  111.2 1.7 %collective-permute-start.3 = (bf16[128,192]{1,0:T(8,128)(2,1)S(1)}, bf16[128,192]{1,0:T(8,128)(2,1)S(1)}, u32[]{:S(2)}, u32[]{:S(2)}) collective-permute-start(bf16[128,192]{1,0:T(8,128)(2,1)S(1)} %get-tuple-element.37), channel_id=1, source_target_pairs={{0,8},{8,0},{16,24},{24,16},{1,9},{9,1},{17,25},{25,17},{2,10},{10... | collective-permute-start | bytes 147464 | tf_op jit(solution)/shard_map/ppermute | solution.py:269
  112.9 1.5 %collective-permute-start.4 = (bf16[128,192]{1,0:T(8,128)(2,1)S(1)}, bf16[128,192]{1,0:T(8,128)(2,1)S(1)}, u32[]{:S(2)}, u32[]{:S(2)}) collective-permute-start(bf16[128,192]{1,0:T(8,128)(2,1)S(1)} %get-tuple-element.38), channel_id=1, source_target_pairs={{0,16},{8,24},{16,0},{24,8},{1,17},{9,25},{17,1},{25,9},{2,18},{10... | collective-permute-start | bytes 147464 | tf_op jit(solution)/shard_map/ppermute | solution.py:269
  114.4 0.4 collective-permute-start.5
  114.8 5.0 %collective-permute-done.3.refs_1_ = bf16[128,192]{1,0:T(8,128)(2,1)S(1)} collective-permute-done((bf16[128,192]{1,0:T(8,128)(2,1)S(1)}, bf16[128,192]{1,0:T(8,128)(2,1)S(1)}, u32[]{:S(2)}, u32[]{:S(2)}) %collective-permute-start.3) | collective-permute-done | bytes 49184 | tf_op jit(solution)/shard_map/ppermute | solution.py:269
  119.8 0.6 collective-permute-done.4.refs_2_
  120.4 2.1 %collective-permute-done.5.refs_3_ = bf16[128,192]{1,0:T(8,128)(2,1)S(1)} collective-permute-done((bf16[128,192]{1,0:T(8,128)(2,1)S(1)}, bf16[128,192]{1,0:T(8,128)(2,1)S(1)}, u32[]{:S(2)}, u32[]{:S(2)}) %collective-permute-start.5) | collective-permute-done | bytes 49184 | tf_op jit(solution)/shard_map/ppermute | solution.py:269
  122.4 0.9 shard_map.139
  123.4 7.0 %all-to-all-done.7.col_w = bf16[32,8,1280]{2,1,0:T(8,128)(2,1)S(1)} async-done(((bf16[32,8,1280]{2,1,0:T(8,128)(2,1)}), bf16[32,8,1280]{2,1,0:T(8,128)(2,1)S(1)}, u32[]{:S(2)}, u32[]{:S(2)}) %all-to-all-start.7) | async-done | bytes 655392 | tf_op jit(solution)/shard_map/all_to_all | solution.py:264
  130.4 1.4 %shard_map.143 = (f32[256,768]{1,0:T(8,128)}, f32[256,256]{1,0:T(8,128)}, f32[256,768]{1,0:T(8,128)}, f32[256,256]{1,0:T(8,128)}) custom-call(bf16[32,24,256]{2,1,0:T(8,128)(2,1)S(1)} %all-to-all-done.5.row_w, bf16[32,8,1280]{2,1,0:T(8,128)(2,1)S(1)} %all-to-all-done.7.col_w), custom_call_target="tpu_custom_call" | custom-call | tf_op jit(solution)/shard_map/pallas_call | solution.py:60
  (24 shorter events, 0.1 us)
Async XLA Ops:
  0.6 6.4 %collective-permute-start.2 = (bf16[128,256]{1,0:T(8,128)(2,1)}, bf16[128,256]{1,0:T(8,128)(2,1)S(1)}, u32[]{:S(2)}, u32[]{:S(2)}) collective-permute-start(bf16[128,256]{1,0:T(8,128)(2,1)} %bitcast.20), channel_id=1, source_target_pairs={{0,24},{8,16},{16,8},{24,0},{1,25},{9,17},{17,9},{25,1},{2,26},{10... | collective-permute-start | bytes 196616 | tf_op jit(solution)/shard_map/ppermute | solution.py:269
  4.6 4.5 %collective-permute-start.1 = (bf16[128,256]{1,0:T(8,128)(2,1)}, bf16[128,256]{1,0:T(8,128)(2,1)S(1)}, u32[]{:S(2)}, u32[]{:S(2)}) collective-permute-start(bf16[128,256]{1,0:T(8,128)(2,1)} %bitcast.21), channel_id=1, source_target_pairs={{0,16},{8,24},{16,0},{24,8},{1,17},{9,25},{17,1},{25,9},{2,18},{10... | collective-permute-start | bytes 196616 | tf_op jit(solution)/shard_map/ppermute | solution.py:269
  5.1 4.5 %collective-permute-start = (bf16[128,256]{1,0:T(8,128)(2,1)}, bf16[128,256]{1,0:T(8,128)(2,1)S(1)}, u32[]{:S(2)}, u32[]{:S(2)}) collective-permute-start(bf16[128,256]{1,0:T(8,128)(2,1)} %bitcast.22), channel_id=1, source_target_pairs={{0,8},{8,0},{16,24},{24,16},{1,9},{9,1},{17,25},{25,17},{2,10},{10... | collective-permute-start | bytes 196616 | tf_op jit(solution)/shard_map/ppermute | solution.py:269
  6.4 3.1 %copy-start.1 = (bf16[128,1,256]{2,0,1:T(8,128)(2,1)S(1)}, bf16[128,1,256]{2,0,1:T(8,128)(2,1)}, u32[]{:S(2)}) copy-start(bf16[128,1,256]{2,0,1:T(8,128)(2,1)} %param.9) | copy-start | bytes 196612
  6.5 3.1 %copy-start.9 = (s32[4,4]{1,0:T(4,128)S(1)}, s32[4,4]{1,0:T(4,128)}, u32[]{:S(2)}) copy-start(s32[4,4]{1,0:T(4,128)} %link.1) | copy-start | bytes 196
  9.6 0.7 copy-start.8
  12.8 0.8 copy-start.4
  13.6 4.9 %copy-start.11 = (bf16[128,1,256]{2,0,1:T(8,128)(2,1)S(1)}, bf16[128,1,256]{2,0,1:T(8,128)(2,1)}, u32[]{:S(2)}) copy-start(bf16[128,1,256]{2,0,1:T(8,128)(2,1)} %param.17) | copy-start | bytes 196612
  13.6 12.3 %all-to-all-start.1 = ((bf16[32,2,512]{2,1,0:T(2,128)(2,1)}), bf16[32,2,512]{2,1,0:T(2,128)(2,1)S(1)}, u32[]{:S(2)}, u32[]{:S(2)}) async-start(bf16[32,2,512]{2,1,0:T(2,128)(2,1)} %reshape.60), calls=%async_computation.1 | async-start | bytes 131072 | tf_op jit(solution)/shard_map/all_to_all | solution.py:264
  25.9 10.1 %all-to-all-start = ((bf16[8,16,512]{2,1,0:T(8,128)(2,1)}), bf16[8,16,512]{2,1,0:T(8,128)(2,1)S(1)}, u32[]{:S(2)}, u32[]{:S(2)}) async-start(bf16[8,16,512]{2,1,0:T(8,128)(2,1)} %pad_maximum_fusion), calls=%async_computation | async-start | bytes 262144 | tf_op jit(solution)/shard_map/all_to_all | solution.py:264
  29.3 1.0 slice-start
  30.2 5.8 %copy-start = (bf16[256,768]{1,0:T(8,128)(2,1)S(1)}, bf16[256,768]{1,0:T(8,128)(2,1)}, u32[]{:S(2)}) copy-start(bf16[256,768]{1,0:T(8,128)(2,1)} %col_proj.1) | copy-start | bytes 1179652
  30.2 5.8 %copy-start.3 = (bf16[256,256]{1,0:T(8,128)(2,1)S(1)}, bf16[256,256]{1,0:T(8,128)(2,1)}, u32[]{:S(2)}) copy-start(bf16[256,256]{1,0:T(8,128)(2,1)} %col_out.1) | copy-start | bytes 393220
  30.4 5.6 %copy-start.2 = (bf16[256,256]{1,0:T(8,128)(2,1)S(1)}, bf16[256,256]{1,0:T(8,128)(2,1)}, u32[]{:S(2)}) copy-start(bf16[256,256]{1,0:T(8,128)(2,1)} %row_out.1) | copy-start | bytes 393220
  36.0 0.7 copy-start.10
  39.2 0.6 copy-start.6
  49.1 10.1 %all-to-all-start.2 = ((bf16[8,16,512]{2,1,0:T(8,128)(2,1)}), bf16[8,16,512]{2,1,0:T(8,128)(2,1)S(1)}, u32[]{:S(2)}, u32[]{:S(2)}) async-start(bf16[8,16,512]{2,1,0:T(8,128)(2,1)} %get-tuple-element.29.og), calls=%async_computation.2 | async-start | bytes 262144 | tf_op jit(solution)/shard_map/all_to_all | solution.py:264
  52.5 0.9 copy-start.5
  59.2 3.5 %copy-start.7 = (bf16[256,128]{1,0:T(8,128)(2,1)S(1)}, bf16[256,128]{1,0:T(8,128)(2,1)}, u32[]{:S(2)}) copy-start(bf16[256,128]{1,0:T(8,128)(2,1)} %copy-done.6) | copy-start | bytes 196612
  59.2 9.8 %all-to-all-start.4 = ((bf16[8,24,256]{2,1,0:T(8,128)(2,1)}), bf16[8,24,256]{2,1,0:T(8,128)(2,1)S(1)}, u32[]{:S(2)}, u32[]{:S(2)}) async-start(bf16[8,24,256]{2,1,0:T(8,128)(2,1)} %bitcast.13), calls=%async_computation.4 | async-start | bytes 196608 | tf_op jit(solution)/shard_map/all_to_all | solution.py:264
  69.0 21.8 %all-to-all-start.6 = ((bf16[32,8,1280]{2,1,0:T(8,128)(2,1)}), bf16[32,8,1280]{2,1,0:T(8,128)(2,1)S(1)}, u32[]{:S(2)}, u32[]{:S(2)}) async-start(bf16[32,8,1280]{2,1,0:T(8,128)(2,1)} %bitcast.14), calls=%async_computation.6 | async-start | bytes 1310720 | tf_op jit(solution)/shard_map/all_to_all | solution.py:264
  91.6 16.1 %all-to-all-start.5 = ((bf16[32,24,256]{2,1,0:T(8,128)(2,1)}), bf16[32,24,256]{2,1,0:T(8,128)(2,1)S(1)}, u32[]{:S(2)}, u32[]{:S(2)}) async-start(bf16[32,24,256]{2,1,0:T(8,128)(2,1)} %broadcast_in_dim.4), calls=%async_computation.5 | async-start | bytes 786432 | tf_op jit(solution)/shard_map/all_to_all | solution.py:264
  108.6 21.8 %all-to-all-start.7 = ((bf16[32,8,1280]{2,1,0:T(8,128)(2,1)}), bf16[32,8,1280]{2,1,0:T(8,128)(2,1)S(1)}, u32[]{:S(2)}, u32[]{:S(2)}) async-start(bf16[32,8,1280]{2,1,0:T(8,128)(2,1)} %broadcast_in_dim.5), calls=%async_computation.7 | async-start | bytes 1310720 | tf_op jit(solution)/shard_map/all_to_all | solution.py:264
  111.2 8.6 %collective-permute-start.3 = (bf16[128,192]{1,0:T(8,128)(2,1)S(1)}, bf16[128,192]{1,0:T(8,128)(2,1)S(1)}, u32[]{:S(2)}, u32[]{:S(2)}) collective-permute-start(bf16[128,192]{1,0:T(8,128)(2,1)S(1)} %get-tuple-element.37), channel_id=1, source_target_pairs={{0,8},{8,0},{16,24},{24,16},{1,9},{9,1},{17,25},{25,17},{2,10},{10... | collective-permute-start | bytes 147464 | tf_op jit(solution)/shard_map/ppermute | solution.py:269
  112.9 7.4 %collective-permute-start.4 = (bf16[128,192]{1,0:T(8,128)(2,1)S(1)}, bf16[128,192]{1,0:T(8,128)(2,1)S(1)}, u32[]{:S(2)}, u32[]{:S(2)}) collective-permute-start(bf16[128,192]{1,0:T(8,128)(2,1)S(1)} %get-tuple-element.38), channel_id=1, source_target_pairs={{0,16},{8,24},{16,0},{24,8},{1,17},{9,25},{17,1},{25,9},{2,18},{10... | collective-permute-start | bytes 147464 | tf_op jit(solution)/shard_map/ppermute | solution.py:269
  114.4 8.0 %collective-permute-start.5 = (bf16[128,192]{1,0:T(8,128)(2,1)S(1)}, bf16[128,192]{1,0:T(8,128)(2,1)S(1)}, u32[]{:S(2)}, u32[]{:S(2)}) collective-permute-start(bf16[128,192]{1,0:T(8,128)(2,1)S(1)} %get-tuple-element.39), channel_id=1, source_target_pairs={{0,24},{8,16},{16,8},{24,0},{1,25},{9,17},{17,9},{25,1},{2,26},{10... | collective-permute-start | bytes 147464 | tf_op jit(solution)/shard_map/ppermute | solution.py:269

commit v2 on v1

--- a/solution.py
+++ b/solution.py
@@ -54,6 +54,26 @@
 def flat_rows(values, dtype=BF16):
     wide = values.astype(F32)
     return wide.reshape(wide.shape[0] * wide.shape[1], wide.shape[2]).astype(dtype)
+
+
+def lane_factor(rows, width):
+    factor = 128 // width
+    return factor if (rows // factor) % 8 == 0 else 1
+
+
+def pack_block(values, outer):
+    rows, width = values.shape[0] // outer, values.shape[1]
+    factor = lane_factor(rows, width)
+    split = values.reshape(outer, factor, rows // factor, width)
+    return jnp.concatenate([split[:, j] for j in range(factor)], axis=2).astype(BF16)
+
+
+def unpack_block(values, width):
+    wide = values.astype(F32)
+    factor = wide.shape[2] // width
+    split = [wide[:, None, :, j * width : (j + 1) * width] for j in range(factor)]
+    joined = jnp.concatenate(split, axis=1)
+    return joined.reshape(-1, width).astype(BF16)
 
 
 def call(body, outs, *operands, scalars=0, scratch=()):
@@ -106,8 +126,7 @@
         att_t.append(mm(v_t[h * HEAD_DIM : (h + 1) * HEAD_DIM], p_out[h]))
     att = jnp.transpose(jnp.concatenate(att_t, axis=0))
     for b in range(sites):
-        block = att[b * rows : (b + 1) * rows].reshape(haps, rows // haps, width)
-        att_out[pl.ds((me ^ b) * haps, haps)] = block.astype(BF16)
+        att_out[pl.ds((me ^ b) * haps, haps)] = pack_block(att[b * rows : (b + 1) * rows], haps)
 
 
 def column_step(
@@ -123,7 +142,7 @@
     cot = cot_f.astype(BF16)
     hid = xc_all[:, :width]
     for i in range(sites):
-        a_i = flat_rows(at[i * haps : (i + 1) * haps])
+        a_i = unpack_block(at[i * haps : (i + 1) * haps], group)
         hid = hid + mm(a_i, row_out[i * group : (i + 1) * group, :])
     hid = hid.astype(BF16).astype(F32)
     grad_att = mm_nt(cot, col_out[...]).astype(BF16)
@@ -176,31 +195,44 @@
     grad_hidden = (cot_f + norm_back(xhat, rstd, gain[...], grad_normed)).astype(BF16)
     for i in range(sites):
         g_i = mm_nt(grad_hidden, row_out[i * group : (i + 1) * group, :])
-        ga_out[i * haps : (i + 1) * haps] = g_i.reshape(haps, per, group).astype(BF16)
+        ga_out[i * haps : (i + 1) * haps] = pack_block(g_i, haps)
     both = jnp.concatenate([out, grad_hidden.astype(F32)], axis=1)
     og_out[...] = both.reshape(haps, per, 2 * width).astype(BF16)
 
 
-def column_weights(sites, haps, xc, at, og, normed, gp, att_t, w_out):
+def column_weights(sites, haps, core, xc, at, og, normed, gp, att_t, keep, send, both):
     width = normed.shape[1]
     group = width // sites
+    half = width // 2
     cot = flat_rows(xc[:, :, width:])
     grad_hidden = flat_rows(og[:, :, width:])
-    w_out[:, : 3 * width] = mm_tn(normed[...], gp[...]).astype(BF16)
-    w_out[:, 3 * width : 4 * width] = mm(att_t[...], cot).astype(BF16)
+    both[:, : 3 * width] = mm_tn(normed[...], gp[...]).astype(BF16)
+    both[:, 3 * width : 4 * width] = mm(att_t[...], cot).astype(BF16)
     for i in range(sites):
-        a_i = flat_rows(at[i * haps : (i + 1) * haps])
-        w_out[i * group : (i + 1) * group, 4 * width :] = mm_tn(a_i, grad_hidden).astype(BF16)
-
-
-def row_backward(sites, haps, idx, g_in, prob, q, val, key_t, normed, *refs):
+        a_i = unpack_block(at[i * haps : (i + 1) * haps], group)
+        both[i * group : (i + 1) * group, 4 * width :] = mm_tn(a_i, grad_hidden).astype(BF16)
+    keep[...] = both[pl.ds(pl.multiple_of(core[0] * half, half), half), :]
+    send[...] = both[pl.ds(pl.multiple_of((1 - core[0]) * half, half), half), :]
+
+
+def column_split(sites, idx, keep, got, *refs):
+    outs, both = refs[:sites], refs[sites]
+    both[...] = (keep[...].astype(F32) + got[...].astype(F32)).astype(BF16)
+    part = keep.shape[0] // sites
+    for k in range(sites):
+        outs[k][...] = both[pl.ds(pl.multiple_of((idx[0] ^ k) * part, part), part), :]
+
+
+def row_backward(sites, haps, idx, core, g_in, prob, q, val, key_t, normed, *refs):
     gp_outs = refs[:sites]
-    w_out, g_all, ds_all = refs[sites:]
+    keep, send, g_all, ds_all, w_out = refs[sites:]
     me = idx[0]
     total, width = q.shape
     rows = total // sites
     for b in range(sites):
-        g_all[b * rows : (b + 1) * rows, :] = flat_rows(g_in[pl.ds((me ^ b) * haps, haps)])
+        g_all[b * rows : (b + 1) * rows, :] = unpack_block(
+            g_in[pl.ds((me ^ b) * haps, haps)], width
+        )
     dk = jnp.zeros((total, width), F32)
     dv = jnp.zeros((total, width), F32)
     dq_t = []
@@ -221,6 +253,9 @@
     w_out[:width, :] = mm(dq_t.astype(BF16), normed[...]).astype(BF16)
     w_out[width : 2 * width, :] = mm_tn(dk16, normed[...]).astype(BF16)
     w_out[2 * width :, :] = mm_tn(dv16, normed[...]).astype(BF16)
+    half = 3 * width // 2
+    keep[...] = w_out[pl.ds(pl.multiple_of(core[0] * half, half), half), :]
+    send[...] = w_out[pl.ds(pl.multiple_of((1 - core[0]) * half, half), half), :]
     dq = jnp.transpose(dq_t).astype(BF16)
     joined = jnp.concatenate([dq, dk16, dv16], axis=1)
     for b in range(sites):
@@ -240,24 +275,47 @@
     gf_ref[...] = grad.astype(BF16)
 
 
-def sum_parts(x_ref, o_ref):
-    o_ref[...] = jnp.sum(x_ref[...].astype(F32), axis=0).astype(BF16)
-
-
-def weights_finish(sites, row_w, col_w, rp, ro, cp, co):
+def weights_join(row_keep, row_got, *refs):
+    cols, out = refs[:-1], refs[-1]
+    half, width = row_keep.shape
+    out[:half, :] = (row_keep[...].astype(F32) + row_got[...].astype(F32)).astype(BF16)
+    total = sum(c[...].astype(F32) for c in cols)
+    part = total.shape[0]
+    for t in range(5):
+        tile = total[:, t * width : (t + 1) * width]
+        out[half + t * part : half + (t + 1) * part, :] = tile.astype(BF16)
+
+
+def weights_sum(*refs):
+    terms = [r[...].astype(F32) for r in refs[:-1]]
+    while len(terms) > 1:
+        terms = [a + b for a, b in zip(terms[::2], terms[1::2])]
+    refs[-1][...] = terms[0].astype(BF16)
+
+
+def weights_finish(sites, idx, core, *refs):
+    pieces = refs[: 2 * sites]
+    rp, ro, cp, co, rows_t = refs[2 * sites :]
     width = ro.shape[0]
     group = width // sites
-    cols = flat_rows(col_w[...], F32)
-    cp[...] = cols[:, : 3 * width]
-    co[...] = cols[:, 3 * width : 4 * width]
-    ro[...] = cols[:, 4 * width :]
-    rows = flat_rows(row_w[...], F32)
-    ordered = [
-        rows[(3 * i + part) * group : (3 * i + part + 1) * group]
-        for part in range(3)
-        for i in range(sites)
-    ]
-    rp[...] = jnp.transpose(jnp.concatenate(ordered, axis=0))
+    unit = group // 2
+    part = width // 2 // sites
+    for j in range(2 * sites):
+        k = j // 2
+        cc = core[0] ^ (j % 2)
+        g = idx[0] ^ k
+        piece = pieces[j][...].astype(F32)
+        for u in range(3):
+            place = 3 * cc + u
+            dest = (place // 2) * width + g * group + (place % 2) * unit
+            rows_t[pl.ds(pl.multiple_of(dest, unit), unit), :] = piece[u * unit : (u + 1) * unit]
+        here = pl.ds(pl.multiple_of(cc * (width // 2) + g * part, part), part)
+        tiles = [piece[3 * unit + t * part : 3 * unit + (t + 1) * part] for t in range(5)]
+        for t in range(3):
+            cp[here, t * width : (t + 1) * width] = tiles[t]
+        co[here, :] = tiles[3]
+        ro[here, :] = tiles[4]
+    rp[...] = jnp.transpose(rows_t[...])
 
 
 def exchange(value, axis):
@@ -267,10 +325,6 @@
 def swapped(value, axis, by):
     length = lax.axis_size(axis)
     return lax.ppermute(value, axis, [(i, i ^ by) for i in range(length)])
-
-
-def spread(value, axis, length):
-    return exchange(jnp.broadcast_to(value[None], (length,) + value.shape), axis)
 
 
 def on_device(
@@ -294,6 +348,9 @@
     both_axes = ("site", "hap")
     me = lax.axis_index("site")
     idx = me.reshape(1).astype(jnp.int32)
+    core = (lax.axis_index("hap") % 2).reshape(1).astype(jnp.int32)
+    factor = lane_factor(per, group)
+    block = ((count, per // factor, group * factor), BF16)
     feats = features.reshape(rows, width)
     cot = cotangent.reshape(rows, width)
     gain_r = row_gain.reshape(1, width)
@@ -310,7 +367,7 @@
     att, prob, q, val, key_t, normed = call(
         functools.partial(row_forward, sites, haps),
         [
-            ((count, per, group), BF16),
+            block,
             ((heads, total, total), BF16),
             ((total, group), BF16),
             ((total, group), BF16),
@@ -319,11 +376,12 @@
         ],
         idx, link_pattern, *pieces, gain_r, w_t, scalars=2,
     )
+    att, xc = lax.optimization_barrier((att, xc))
     at = exchange(att, both_axes)
     ga, og, col_normed, col_gp, col_att_t = call(
         functools.partial(column_step, sites, haps),
         [
-            ((count, per, group), BF16),
+            block,
             ((haps, per, 2 * width), BF16),
             ((rows, width), BF16),
             ((rows, 3 * width), BF16),
@@ -332,34 +390,52 @@
         xc, at, row_out, gain_c, col_proj, kv_t_w, col_out,
     )
     g_in = exchange(ga, both_axes)
-    (col_w,) = call(
+    half = width // 2
+    col_keep, col_send = call(
         functools.partial(column_weights, sites, haps),
-        [((width, 5 * width), BF16)],
-        xc, at, og, col_normed, col_gp, col_att_t,
-    )
+        [((half, 5 * width), BF16)] * 2,
+        core, xc, at, og, col_normed, col_gp, col_att_t, scalars=1,
+        scratch=[pltpu.VMEM((width, 5 * width), BF16)],
+    )
+    col_got = swapped(col_send, "hap", 1)
+    cols = call(
+        functools.partial(column_split, sites),
+        [((half // sites, 5 * width), BF16)] * sites,
+        idx, col_keep, col_got, scalars=1,
+        scratch=[pltpu.VMEM((half, 5 * width), BF16)],
+    )
+    g_in, cols = lax.optimization_barrier((g_in, cols))
+    cols = [cols[0]] + [swapped(cols[k], "site", k) for k in range(1, sites)]
+    *gps, row_keep, row_send = call(
+        functools.partial(row_backward, sites, haps),
+        [((rows, 3 * group), BF16)] * sites + [((3 * group // 2, width), BF16)] * 2,
+        idx, core, g_in, prob, q, val, key_t, normed, scalars=2,
+        scratch=[
+            pltpu.VMEM((total, group), BF16),
+            pltpu.VMEM((total, total), BF16),
+            pltpu.VMEM((3 * group, width), BF16),
+        ],
+    )
+    row_got = swapped(row_send, "hap", 1)
+    depth = 3 * group // 2 + 5 * half // sites
+    (joined,) = call(weights_join, [((depth, width), BF16)], row_keep, row_got, *cols)
+    parts = [joined] + [swapped(joined, "hap", 2 * m) for m in range(1, haps // 2)]
+    (mine,) = call(weights_sum, [((depth, width), BF16)], *parts)
+    og, _ = lax.optimization_barrier((og, row_keep))
     og_in = exchange(og, "hap")
-    *gps, row_w = call(
-        functools.partial(row_backward, sites, haps),
-        [((rows, 3 * group), BF16)] * sites + [((3 * group, width), BF16)],
-        idx, g_in, prob, q, val, key_t, normed, scalars=1,
-        scratch=[pltpu.VMEM((total, group), BF16), pltpu.VMEM((total, total), BF16)],
-    )
-    col_parts = exchange(col_w.reshape(count, width // count, 5 * width), both_axes)
-    (col_mine,) = call(sum_parts, [((width // count, 5 * width), BF16)], col_parts)
-    row_parts = exchange(row_w.reshape(haps, 3 * group // haps, width), "hap")
-    (row_mine,) = call(sum_parts, [((3 * group // haps, width), BF16)], row_parts)
     gps = [gps[0]] + [swapped(gps[k], "site", k) for k in range(1, sites)]
     out, grad = call(
         functools.partial(row_finish, sites),
         [((rows, width), BF16)] * 2,
         idx, feats, gain_r, w_all, og_in, *gps, scalars=1,
     )
-    col_full = spread(col_mine, both_axes, count)
-    row_full = spread(row_mine, both_axes, count)
+    full = [mine] + [swapped(mine, "site", k) for k in range(1, sites)]
+    full = [x for piece in full for x in (piece, swapped(piece, "hap", 1))]
     rp, ro, cp, co = call(
         functools.partial(weights_finish, sites),
         [((width, 3 * width), F32), ((width, width), F32)] * 2,
-        row_full, col_full,
+        idx, core, *full, scalars=2,
+        scratch=[pltpu.VMEM((3 * width, width), F32)],
     )
     shape = (rows, 1, width)
     return (out.reshape(shape), grad.reshape(shape), rp, ro, cp, co)

time: 133 us -> 93.5 us (0.70)
  waiting for transfers between devices: 69.8 us -> 38.6 us
  blocking collectives: 9.14 us -> 0 us
  local copies, waits for them, and re-layouts: 7.87 us -> 2.66 us
  starting transfers between devices: 31.2 us -> 35.7 us
    all_to_all x7 -> x4, waiting for transfers between devices: 59 us -> 13.5 us  [exchange(): return lax.all_to_all(value, axis, 0, 0, tiled=True)]
    ppermute x6 -> x21, waiting for transfers between devices: 10.8 us -> 25.2 us  [swapped(): return lax.ppermute(value, axis, [(i, i ^ by) for i in range(length)])]
    ppermute x6 -> x21, starting transfers between devices: 8.16 us -> 18.3 us  [swapped(): return lax.ppermute(value, axis, [(i, i ^ by) for i in range(length)])]
    all_to_all x1 -> x0, blocking collectives: 9.14 us -> none  [exchange(): return lax.all_to_all(value, axis, 0, 0, tiled=True)]
    all_to_all x7 -> x4, starting transfers between devices: 23 us -> 17.5 us  [exchange(): return lax.all_to_all(value, axis, 0, 0, tiled=True)]
    unnamed x30 -> x22, local copies, waits for them, and re-layouts: 5.23 us -> 1.68 us
    broadcast_in_dim x2 -> x0, local copies, waits for them, and re-layouts: 1.65 us -> none  [spread(): jnp.broadcast_to(value[None], (length,) + value.shape)]
    pallas_call x8 -> x9, Pallas kernels: 12.3 us -> 13.5 us  [call(): pl.pallas_call(body, out_shape=[jax.ShapeDtypeStruct(s, d) for s, d in ou...]
  transfers between devices with their start and end apart: 13 -> 25, of which waited for: 13 -> 11; matrix products, arithmetic and copies ran while one was open for 2% -> 0% of each run, Pallas kernels for 4% -> 8%
where the time goes in v2:
time: 93.5 us; the launch traced here: 93 us
  waiting for transfers between devices  38.6 us (41%)
  starting transfers between devices  35.7 us (38%)
  Pallas kernels  13.5 us (14%)
  local copies, waits for them, and re-layouts  2.66 us (3%)
  other arithmetic  1.59 us (2%)
    ppermute x21, waiting for transfers between devices, swapped(): return lax.ppermute(value, axis, [(i, i ^ by) for i in range(length)])  25.2 us
    ppermute x21, starting transfers between devices, swapped(): return lax.ppermute(value, axis, [(i, i ^ by) for i in range(length)])  18.3 us
    all_to_all x4, starting transfers between devices, exchange(): return lax.all_to_all(value, axis, 0, 0, tiled=True)  17.5 us
    pallas_call x9, Pallas kernels, call(): pl.pallas_call(body, out_shape=[jax.ShapeDtypeStruct(s, d) for s, d in ou...  13.5 us
    all_to_all x4, waiting for transfers between devices, exchange(): return lax.all_to_all(value, axis, 0, 0, tiled=True)  13.5 us
  transfers between devices with their start and end apart: 25, of which 11 were waited for; matrix products, arithmetic and copies ran while one was open for 0% of the time, Pallas kernels for 8%

profile of v2, /device:TPU:0, one launch (start us, length us, event | category | flops | bytes accessed | tf_op | source)
XLA Modules:
  0.0 93.0 jit_solution(12521497621629783397)
XLA Ops:
  0.6 1.6 %pad_maximum_fusion = bf16[8,16,512]{2,1,0:T(8,128)(2,1)} fusion(bf16[8,16,256]{2,1,0:T(8,128)(2,1)} %bitcast.29, bf16[8,16,256]{2,1,0:T(8,128)(2,1)} %bitcast.19), kind=kLoop, calls=%fused_computation | loop fusion | flops 262144 | bytes 262144 | tf_op jit(solution)/shard_map/concatenate | solution.py:360
  2.2 6.5 %all-to-all-start = ((bf16[8,16,512]{2,1,0:T(8,128)(2,1)}), bf16[8,16,512]{2,1,0:T(8,128)(2,1)S(1)}, u32[]{:S(2)}, u32[]{:S(2)}) async-start(bf16[8,16,512]{2,1,0:T(8,128)(2,1)} %pad_maximum_fusion), calls=%async_computation | async-start | bytes 262144 | tf_op jit(solution)/shard_map/all_to_all | solution.py:322
  8.7 2.5 %collective-permute-start.2 = (bf16[128,256]{1,0:T(8,128)(2,1)S(1)}, bf16[128,256]{1,0:T(8,128)(2,1)S(1)}, u32[]{:S(2)}, u32[]{:S(2)}) collective-permute-start(bf16[128,256]{1,0:T(8,128)(2,1)S(1)} %bitcast.20), channel_id=1, source_target_pairs={{0,24},{8,16},{16,8},{24,0},{1,25},{9,17},{17,9},{25,1},{2,26},{10... | collective-permute-start | bytes 196616 | tf_op jit(solution)/shard_map/ppermute | solution.py:327
  11.2 0.5 collective-permute-start.1
  11.7 0.5 collective-permute-start
  12.3 0.2 copy.17
  12.5 1.6 %collective-permute-done.2.refs_3_ = bf16[128,256]{1,0:T(8,128)(2,1)S(1)} collective-permute-done((bf16[128,256]{1,0:T(8,128)(2,1)S(1)}, bf16[128,256]{1,0:T(8,128)(2,1)S(1)}, u32[]{:S(2)}, u32[]{:S(2)}) %collective-permute-start.2) | collective-permute-done | bytes 65568 | tf_op jit(solution)/shard_map/ppermute | solution.py:327
  14.1 1.4 %collective-permute-done.1.refs_2_ = bf16[128,256]{1,0:T(8,128)(2,1)S(1)} collective-permute-done((bf16[128,256]{1,0:T(8,128)(2,1)S(1)}, bf16[128,256]{1,0:T(8,128)(2,1)S(1)}, u32[]{:S(2)}, u32[]{:S(2)}) %collective-permute-start.1) | collective-permute-done | bytes 65568 | tf_op jit(solution)/shard_map/ppermute | solution.py:327
  15.5 0.5 collective-permute-done.refs_1_
  16.0 0.7 copy-done.4
  16.7 3.3 %shard_map.136 = (bf16[32,8,128]{2,1,0:T(8,128)(2,1)}, bf16[2,512,512]{2,1,0:T(8,128)(2,1)S(1)}, bf16[512,64]{1,0:T(8,128)(2,1)S(1)}, bf16[512,64]{1,0:T(8,128)(...) custom-call(s32[1]{0:T(128)} %bitcast.idx, s32[4,4]{1,0:T(4,128)S(1)} %copy-done.5, ...), custom_call_target="tpu_custom_call" | custom-call | tf_op jit(solution)/shard_map/pallas_call | solution.py:80
  19.9 5.1 %all-to-all-start.1 = ((bf16[32,8,128]{2,1,0:T(8,128)(2,1)}), bf16[32,8,128]{2,1,0:T(8,128)(2,1)S(1)}, u32[]{:S(2)}, u32[]{:S(2)}) async-start(bf16[32,8,128]{2,1,0:T(8,128)(2,1)} %get-tuple-element.45), calls=%async_computation.1 | async-start | bytes 131072 | tf_op jit(solution)/shard_map/all_to_all | solution.py:322
  25.0 0.9 slice-done
  26.0 0.1 copy.20
  26.1 6.3 %all-to-all-done.1.at = bf16[32,8,128]{2,1,0:T(8,128)(2,1)S(1)} async-done(((bf16[32,8,128]{2,1,0:T(8,128)(2,1)}), bf16[32,8,128]{2,1,0:T(8,128)(2,1)S(1)}, u32[]{:S(2)}, u32[]{:S(2)}) %all-to-all-start.1) | async-done | bytes 65568 | tf_op jit(solution)/shard_map/all_to_all | solution.py:322
  32.4 0.7 copy-done.6
  33.1 2.9 %shard_map.137 = (bf16[32,8,128]{2,1,0:T(8,128)(2,1)}, bf16[8,16,512]{2,1,0:T(8,128)(2,1)}, bf16[128,256]{1,0:T(8,128)(2,1)S(1)}, bf16[128,768]{1,0:T(8,128)(2,1)S(1)}, bf16[256,128]{1,0:T(8,128)(2,1)S(1)}) custom-call(bf16[8,16,512]{2,1,0:T(8,128)(2,1)S(1)} %all-to-all-done.xc, bf16[32,8,128]{2,1,0:T(8,128)(2,1)S(1)} %all-to-all-done.1.at, ...), custom_call_target="tpu_custom_call" | custom-call | tf_op jit(solution)/shard_map/pallas_call | solution.py:80
  35.9 2.0 %shard_map.138 = (bf16[128,1280]{1,0:T(8,128)(2,1)S(1)}, bf16[128,1280]{1,0:T(8,128)(2,1)}) custom-call(s32[1]{0:T(128)} %bitcast.11.core, bf16[8,16,512]{2,1,0:T(8,128)(2,1)S(1)} %all-to-all-done.xc, bf16[32,8,128]{2,1,0:T(8,128)(2,1)S(1)} %all-to-all-done.1.at, bf16[8,16,512]{2,1,0:T(8,128)(2,1)} %get-tuple-element.64.og, ...), custom_call_target="tpu_custom_call" | custom-call | tf_op jit(solution)/shard_map/pallas_call | solution.py:80
  38.0 0.1 collective-permute-start.3
  38.1 2.6 %all-to-all-start.2 = ((bf16[32,8,128]{2,1,0:T(8,128)(2,1)}), bf16[32,8,128]{2,1,0:T(8,128)(2,1)S(1)}, u32[]{:S(2)}, u32[]{:S(2)}) async-start(bf16[32,8,128]{2,1,0:T(8,128)(2,1)} %get-tuple-element.47), calls=%async_computation.2 | async-start | bytes 131072 | tf_op jit(solution)/shard_map/all_to_all | solution.py:322
  40.7 0.2 shard_map.139
  40.9 7.2 %all-to-all-done.2.g_in = bf16[32,8,128]{2,1,0:T(8,128)(2,1)S(1)} async-done(((bf16[32,8,128]{2,1,0:T(8,128)(2,1)}), bf16[32,8,128]{2,1,0:T(8,128)(2,1)S(1)}, u32[]{:S(2)}, u32[]{:S(2)}) %all-to-all-start.2) | async-done | bytes 65568 | tf_op jit(solution)/shard_map/all_to_all | solution.py:322
  48.1 0.7 collective-permute-start.8
  48.7 0.6 collective-permute-start.9
  49.4 2.2 %collective-permute-start.10 = (bf16[32,1280]{1,0:T(8,128)(2,1)S(1)}, bf16[32,1280]{1,0:T(8,128)(2,1)S(1)}, u32[]{:S(2)}, u32[]{:S(2)}) collective-permute-start(bf16[32,1280]{1,0:T(8,128)(2,1)S(1)} %get-tuple-element.75), channel_id=1, source_target_pairs={{0,24},{8,16},{16,8},{24,0},{1,25},{9,17},{17,9},{25,1},{2,26},{10... | collective-permute-start | bytes 245768 | tf_op jit(solution)/shard_map/ppermute | solution.py:327
  51.5 2.6 %shard_map.140 = (bf16[128,192]{1,0:T(8,128)(2,1)S(1)}, bf16[128,192]{1,0:T(8,128)(2,1)}, bf16[128,192]{1,0:T(8,128)(2,1)S(1)}, bf16[128,192]{1,0:T(8,128)(2,1)S...) custom-call(s32[1]{0:T(128)} %bitcast.idx, s32[1]{0:T(128)} %bitcast.11.core, ...), custom_call_target="tpu_custom_call" | custom-call | tf_op jit(solution)/shard_map/pallas_call | solution.py:80
  54.2 1.2 %collective-permute-done.7.row_got = bf16[96,256]{1,0:T(8,128)(2,1)S(1)} collective-permute-done((bf16[96,256]{1,0:T(8,128)(2,1)S(1)}, bf16[96,256]{1,0:T(8,128)(2,1)S(1)}, u32[]{:S(2)}, u32[]{:S(2)}) %collective-permute-start.7) | collective-permute-done | bytes 49184 | tf_op jit(solution)/shard_map/ppermute | solution.py:327
  55.5 0.8 collective-permute-start.13
  56.3 1.2 %collective-permute-start.12 = (bf16[256,256]{1,0:T(8,128)(2,1)S(1)}, bf16[256,256]{1,0:T(8,128)(2,1)S(1)}, u32[]{:S(2)}, u32[]{:S(2)}) collective-permute-start(bf16[256,256]{1,0:T(8,128)(2,1)S(1)} %shard_map.142.refs_0_), channel_id=1, source_target_pairs={{0,4},{1,5},{2,6},{3,7},{4,0},{5,1},{6,2},{7,3},{8,12},{9,13},{10,... | collective-permute-start | bytes 393224 | tf_op jit(solution)/shard_map/ppermute | solution.py:327
  57.5 2.5 %collective-permute-start.11 = (bf16[256,256]{1,0:T(8,128)(2,1)S(1)}, bf16[256,256]{1,0:T(8,128)(2,1)S(1)}, u32[]{:S(2)}, u32[]{:S(2)}) collective-permute-start(bf16[256,256]{1,0:T(8,128)(2,1)S(1)} %shard_map.142.refs_0_), channel_id=1, source_target_pairs={{0,2},{1,3},{2,0},{3,1},{4,6},{5,7},{6,4},{7,5},{8,10},{9,11},{10,... | collective-permute-start | bytes 393224 | tf_op jit(solution)/shard_map/ppermute | solution.py:327
  60.0 3.9 %collective-permute-done.13.refs_3_ = bf16[256,256]{1,0:T(8,128)(2,1)S(1)} collective-permute-done((bf16[256,256]{1,0:T(8,128)(2,1)S(1)}, bf16[256,256]{1,0:T(8,128)(2,1)S(1)}, u32[]{:S(2)}, u32[]{:S(2)}) %collective-permute-start.13) | collective-permute-done | bytes 131104 | tf_op jit(solution)/shard_map/ppermute | solution.py:327
  63.8 5.6 %collective-permute-done.12.refs_2_ = bf16[256,256]{1,0:T(8,128)(2,1)S(1)} collective-permute-done((bf16[256,256]{1,0:T(8,128)(2,1)S(1)}, bf16[256,256]{1,0:T(8,128)(2,1)S(1)}, u32[]{:S(2)}, u32[]{:S(2)}) %collective-permute-start.12) | collective-permute-done | bytes 131104 | tf_op jit(solution)/shard_map/ppermute | solution.py:327
  69.5 0.1 shard_map.143.refs_0_
  69.5 0.8 collective-permute-start.19
  70.3 1.4 %collective-permute-start.17 = (bf16[256,256]{1,0:T(8,128)(2,1)S(1)}, bf16[256,256]{1,0:T(8,128)(2,1)S(1)}, u32[]{:S(2)}, u32[]{:S(2)}) collective-permute-start(bf16[256,256]{1,0:T(8,128)(2,1)S(1)} %shard_map.143.refs_0_), channel_id=1, source_target_pairs={{0,16},{8,24},{16,0},{24,8},{1,17},{9,25},{17,1},{25,9},{2,18},{10... | collective-permute-start | bytes 393224 | tf_op jit(solution)/shard_map/ppermute | solution.py:327
  71.7 1.4 %collective-permute-start.15 = (bf16[256,256]{1,0:T(8,128)(2,1)S(1)}, bf16[256,256]{1,0:T(8,128)(2,1)S(1)}, u32[]{:S(2)}, u32[]{:S(2)}) collective-permute-start(bf16[256,256]{1,0:T(8,128)(2,1)S(1)} %shard_map.143.refs_0_), channel_id=1, source_target_pairs={{0,8},{8,0},{16,24},{24,16},{1,9},{9,1},{17,25},{25,17},{2,10},{10... | collective-permute-start | bytes 393224 | tf_op jit(solution)/shard_map/ppermute | solution.py:327
  73.1 3.4 %all-to-all-start.3 = ((bf16[8,16,512]{2,1,0:T(8,128)(2,1)}), bf16[8,16,512]{2,1,0:T(8,128)(2,1)S(1)}, u32[]{:S(2)}, u32[]{:S(2)}) async-start(bf16[8,16,512]{2,1,0:T(8,128)(2,1)} %get-tuple-element.64.og), calls=%async_computation.3 | async-start | bytes 262144 | tf_op jit(solution)/shard_map/all_to_all | solution.py:322
  76.5 0.7 collective-permute-start.4
  77.3 0.5 collective-permute-start.20
  77.7 0.1 collective-permute-start.18
  77.8 0.4 collective-permute-start.16
  78.2 2.9 %collective-permute-done.4.refs_1_ = bf16[128,192]{1,0:T(8,128)(2,1)S(1)} collective-permute-done((bf16[128,192]{1,0:T(8,128)(2,1)}, bf16[128,192]{1,0:T(8,128)(2,1)S(1)}, u32[]{:S(2)}, u32[]{:S(2)}) %collective-permute-start.4) | collective-permute-done | bytes 49184 | tf_op jit(solution)/shard_map/ppermute | solution.py:327
  81.1 0.7 collective-permute-start.5
  81.8 3.6 %collective-permute-done.5.refs_2_ = bf16[128,192]{1,0:T(8,128)(2,1)S(1)} collective-permute-done((bf16[128,192]{1,0:T(8,128)(2,1)S(1)}, bf16[128,192]{1,0:T(8,128)(2,1)S(1)}, u32[]{:S(2)}, u32[]{:S(2)}) %collective-permute-start.5) | collective-permute-done | bytes 49184 | tf_op jit(solution)/shard_map/ppermute | solution.py:327
  85.4 0.7 collective-permute-start.6
  86.1 4.5 %collective-permute-done.6.refs_3_ = bf16[128,192]{1,0:T(8,128)(2,1)S(1)} collective-permute-done((bf16[128,192]{1,0:T(8,128)(2,1)S(1)}, bf16[128,192]{1,0:T(8,128)(2,1)S(1)}, u32[]{:S(2)}, u32[]{:S(2)}) %collective-permute-start.6) | collective-permute-done | bytes 49184 | tf_op jit(solution)/shard_map/ppermute | solution.py:327
  90.5 1.0 %shard_map.141 = (bf16[128,256]{1,0:T(8,128)(2,1)}, bf16[128,256]{1,0:T(8,128)(2,1)}) custom-call(s32[1]{0:T(128)} %bitcast.idx, bf16[128,256]{1,0:T(8,128)(2,1)S(1)} %bitcast.24, f32[1,256]{1,0:T(1,128)S(1)} %bitcast.26, bf16[4,192,256]{2,1,0:T(8,128)(2,1)S(1)} %bitcast.17, bf16[8,16,512]{2,1,0:T(8,128)(2,1)S(1)} %all-to-all-done.3.og, ...), custom_call_target="tpu_custom_call" | custom-call | tf_op jit(solution)/shard_map/pallas_call | solution.py:80
  91.5 1.5 %shard_map.144 = (f32[256,768]{1,0:T(8,128)}, f32[256,256]{1,0:T(8,128)}, f32[256,768]{1,0:T(8,128)}, f32[256,256]{1,0:T(8,128)}) custom-call(s32[1]{0:T(128)} %bitcast.idx, s32[1]{0:T(128)} %bitcast.11.core, bf16[256,256]{1,0:T(8,128)(2,1)S(1)} %shard_map.143.refs_0_, bf16[256,256]{1,0:T(8,128)(2,1)S(1)} %collective-permute-done.14.refs_1_, ...), custom_call_target="tpu_custom_call" | custom-call | tf_op jit(solution)/shard_map/pallas_call | solution.py:80
  (38 shorter events, 0.2 us)
Async XLA Ops:
  0.6 11.6 %copy-start.9 = (bf16[256,768]{1,0:T(8,128)(2,1)S(1)}, bf16[256,768]{1,0:T(8,128)(2,1)}, u32[]{:S(2)}) copy-start(bf16[256,768]{1,0:T(8,128)(2,1)} %param.12) | copy-start | bytes 1179652
  2.2 6.5 %copy-start.1 = (bf16[128,1,256]{2,0,1:T(8,128)(2,1)S(1)}, bf16[128,1,256]{2,0,1:T(8,128)(2,1)}, u32[]{:S(2)}) copy-start(bf16[128,1,256]{2,0,1:T(8,128)(2,1)} %param.9) | copy-start | bytes 196612
  2.2 17.7 %all-to-all-start = ((bf16[8,16,512]{2,1,0:T(8,128)(2,1)}), bf16[8,16,512]{2,1,0:T(8,128)(2,1)S(1)}, u32[]{:S(2)}, u32[]{:S(2)}) async-start(bf16[8,16,512]{2,1,0:T(8,128)(2,1)} %pad_maximum_fusion), calls=%async_computation | async-start | bytes 262144 | tf_op jit(solution)/shard_map/all_to_all | solution.py:322
  8.7 5.4 %collective-permute-start.2 = (bf16[128,256]{1,0:T(8,128)(2,1)S(1)}, bf16[128,256]{1,0:T(8,128)(2,1)S(1)}, u32[]{:S(2)}, u32[]{:S(2)}) collective-permute-start(bf16[128,256]{1,0:T(8,128)(2,1)S(1)} %bitcast.20), channel_id=1, source_target_pairs={{0,24},{8,16},{16,8},{24,0},{1,25},{9,17},{17,9},{25,1},{2,26},{10... | collective-permute-start | bytes 196616 | tf_op jit(solution)/shard_map/ppermute | solution.py:327
  11.2 4.3 %collective-permute-start.1 = (bf16[128,256]{1,0:T(8,128)(2,1)S(1)}, bf16[128,256]{1,0:T(8,128)(2,1)S(1)}, u32[]{:S(2)}, u32[]{:S(2)}) collective-permute-start(bf16[128,256]{1,0:T(8,128)(2,1)S(1)} %bitcast.21), channel_id=1, source_target_pairs={{0,16},{8,24},{16,0},{24,8},{1,17},{9,25},{17,1},{25,9},{2,18},{10... | collective-permute-start | bytes 196616 | tf_op jit(solution)/shard_map/ppermute | solution.py:327
  11.7 4.3 %collective-permute-start = (bf16[128,256]{1,0:T(8,128)(2,1)S(1)}, bf16[128,256]{1,0:T(8,128)(2,1)S(1)}, u32[]{:S(2)}, u32[]{:S(2)}) collective-permute-start(bf16[128,256]{1,0:T(8,128)(2,1)S(1)} %bitcast.22), channel_id=1, source_target_pairs={{0,8},{8,0},{16,24},{24,16},{1,9},{9,1},{17,25},{25,17},{2,10},{10... | collective-permute-start | bytes 196616 | tf_op jit(solution)/shard_map/ppermute | solution.py:327
  12.5 3.5 %copy-start.5 = (s32[4,4]{1,0:T(4,128)S(1)}, s32[4,4]{1,0:T(4,128)}, u32[]{:S(2)}) copy-start(s32[4,4]{1,0:T(4,128)} %link.1) | copy-start | bytes 196
  16.0 0.7 copy-start.4
  19.9 12.5 %all-to-all-start.1 = ((bf16[32,8,128]{2,1,0:T(8,128)(2,1)}), bf16[32,8,128]{2,1,0:T(8,128)(2,1)S(1)}, u32[]{:S(2)}, u32[]{:S(2)}) async-start(bf16[32,8,128]{2,1,0:T(8,128)(2,1)} %get-tuple-element.45), calls=%async_computation.1 | async-start | bytes 131072 | tf_op jit(solution)/shard_map/all_to_all | solution.py:322
  25.0 1.0 %slice-start = ((bf16[256,768]{1,0:T(8,128)(2,1)}), bf16[256,512]{1,0:T(8,128)(2,1)S(1)}, s32[]{:S(2)}) async-start(bf16[256,768]{1,0:T(8,128)(2,1)} %col_proj.1), calls=%async_computation.4 | async-start | bytes 524288 | tf_op jit(solution)/shard_map/slice | solution.py:365
  25.0 7.4 %copy-start.3 = (bf16[256,256]{1,0:T(8,128)(2,1)S(1)}, bf16[256,256]{1,0:T(8,128)(2,1)}, u32[]{:S(2)}) copy-start(bf16[256,256]{1,0:T(8,128)(2,1)} %col_out.1) | copy-start | bytes 393220
  26.0 6.4 %copy-start = (bf16[256,768]{1,0:T(8,128)(2,1)S(1)}, bf16[256,768]{1,0:T(8,128)(2,1)}, u32[]{:S(2)}) copy-start(bf16[256,768]{1,0:T(8,128)(2,1)} %col_proj.1) | copy-start | bytes 1179652
  26.0 6.4 %copy-start.2 = (bf16[256,256]{1,0:T(8,128)(2,1)S(1)}, bf16[256,256]{1,0:T(8,128)(2,1)}, u32[]{:S(2)}) copy-start(bf16[256,256]{1,0:T(8,128)(2,1)} %row_out.1) | copy-start | bytes 393220
  32.4 0.7 copy-start.6
  38.0 2.7 %collective-permute-start.3 = (bf16[128,1280]{1,0:T(8,128)(2,1)}, bf16[128,1280]{1,0:T(8,128)(2,1)S(1)}, u32[]{:S(2)}, u32[]{:S(2)}) collective-permute-start(bf16[128,1280]{1,0:T(8,128)(2,1)} %get-tuple-element.52), channel_id=1, source_target_pairs={{0,1},{1,0},{2,3},{3,2},{4,5},{5,4},{6,7},{7,6},{8,9},{9,8},{10,11... | collective-permute-start | bytes 983048 | tf_op jit(solution)/shard_map/ppermute | solution.py:327
  38.1 10.0 %all-to-all-start.2 = ((bf16[32,8,128]{2,1,0:T(8,128)(2,1)}), bf16[32,8,128]{2,1,0:T(8,128)(2,1)S(1)}, u32[]{:S(2)}, u32[]{:S(2)}) async-start(bf16[32,8,128]{2,1,0:T(8,128)(2,1)} %get-tuple-element.47), calls=%async_computation.2 | async-start | bytes 131072 | tf_op jit(solution)/shard_map/all_to_all | solution.py:322
  48.1 7.4 %collective-permute-start.8 = (bf16[32,1280]{1,0:T(8,128)(2,1)S(1)}, bf16[32,1280]{1,0:T(8,128)(2,1)S(1)}, u32[]{:S(2)}, u32[]{:S(2)}) collective-permute-start(bf16[32,1280]{1,0:T(8,128)(2,1)S(1)} %get-tuple-element.73), channel_id=1, source_target_pairs={{0,8},{8,0},{16,24},{24,16},{1,9},{9,1},{17,25},{25,17},{2,10},{10... | collective-permute-start | bytes 245768 | tf_op jit(solution)/shard_map/ppermute | solution.py:327
  48.7 6.7 %collective-permute-start.9 = (bf16[32,1280]{1,0:T(8,128)(2,1)S(1)}, bf16[32,1280]{1,0:T(8,128)(2,1)S(1)}, u32[]{:S(2)}, u32[]{:S(2)}) collective-permute-start(bf16[32,1280]{1,0:T(8,128)(2,1)S(1)} %get-tuple-element.74), channel_id=1, source_target_pairs={{0,16},{8,24},{16,0},{24,8},{1,17},{9,25},{17,1},{25,9},{2,18},{10... | collective-permute-start | bytes 245768 | tf_op jit(solution)/shard_map/ppermute | solution.py:327
  49.4 6.0 %collective-permute-start.10 = (bf16[32,1280]{1,0:T(8,128)(2,1)S(1)}, bf16[32,1280]{1,0:T(8,128)(2,1)S(1)}, u32[]{:S(2)}, u32[]{:S(2)}) collective-permute-start(bf16[32,1280]{1,0:T(8,128)(2,1)S(1)} %get-tuple-element.75), channel_id=1, source_target_pairs={{0,24},{8,16},{16,8},{24,0},{1,25},{9,17},{17,9},{25,1},{2,26},{10... | collective-permute-start | bytes 245768 | tf_op jit(solution)/shard_map/ppermute | solution.py:327
  54.2 1.3 %copy-start.7 = (bf16[128,192]{1,0:T(8,128)(2,1)}, bf16[128,192]{1,0:T(8,128)(2,1)S(1)}, u32[]{:S(2)}) copy-start(bf16[128,192]{1,0:T(8,128)(2,1)S(1)} %get-tuple-element.67) | copy-start | bytes 147460
  54.2 1.2 %collective-permute-start.7 = (bf16[96,256]{1,0:T(8,128)(2,1)S(1)}, bf16[96,256]{1,0:T(8,128)(2,1)S(1)}, u32[]{:S(2)}, u32[]{:S(2)}) collective-permute-start(bf16[96,256]{1,0:T(8,128)(2,1)S(1)} %get-tuple-element.71), channel_id=1, source_target_pairs={{0,1},{1,0},{2,3},{3,2},{4,5},{5,4},{6,7},{7,6},{8,9},{9,8},{10,11... | collective-permute-start | bytes 147464 | tf_op jit(solution)/shard_map/ppermute | solution.py:327
  55.5 8.3 %collective-permute-start.13 = (bf16[256,256]{1,0:T(8,128)(2,1)S(1)}, bf16[256,256]{1,0:T(8,128)(2,1)S(1)}, u32[]{:S(2)}, u32[]{:S(2)}) collective-permute-start(bf16[256,256]{1,0:T(8,128)(2,1)S(1)} %shard_map.142.refs_0_), channel_id=1, source_target_pairs={{0,6},{1,7},{2,4},{3,5},{4,2},{5,3},{6,0},{7,1},{8,14},{9,15},{10,... | collective-permute-start | bytes 393224 | tf_op jit(solution)/shard_map/ppermute | solution.py:327
  56.3 13.2 %collective-permute-start.12 = (bf16[256,256]{1,0:T(8,128)(2,1)S(1)}, bf16[256,256]{1,0:T(8,128)(2,1)S(1)}, u32[]{:S(2)}, u32[]{:S(2)}) collective-permute-start(bf16[256,256]{1,0:T(8,128)(2,1)S(1)} %shard_map.142.refs_0_), channel_id=1, source_target_pairs={{0,4},{1,5},{2,6},{3,7},{4,0},{5,1},{6,2},{7,3},{8,12},{9,13},{10,... | collective-permute-start | bytes 393224 | tf_op jit(solution)/shard_map/ppermute | solution.py:327
  57.5 12.0 %collective-permute-start.11 = (bf16[256,256]{1,0:T(8,128)(2,1)S(1)}, bf16[256,256]{1,0:T(8,128)(2,1)S(1)}, u32[]{:S(2)}, u32[]{:S(2)}) collective-permute-start(bf16[256,256]{1,0:T(8,128)(2,1)S(1)} %shard_map.142.refs_0_), channel_id=1, source_target_pairs={{0,2},{1,3},{2,0},{3,1},{4,6},{5,7},{6,4},{7,5},{8,10},{9,11},{10,... | collective-permute-start | bytes 393224 | tf_op jit(solution)/shard_map/ppermute | solution.py:327
  69.5 11.6 %copy-start.8 = (bf16[128,192]{1,0:T(8,128)(2,1)S(1)}, bf16[128,192]{1,0:T(8,128)(2,1)}, u32[]{:S(2)}) copy-start(bf16[128,192]{1,0:T(8,128)(2,1)} %copy-done.7) | copy-start | bytes 147460
  69.5 7.7 %collective-permute-start.19 = (bf16[256,256]{1,0:T(8,128)(2,1)S(1)}, bf16[256,256]{1,0:T(8,128)(2,1)S(1)}, u32[]{:S(2)}, u32[]{:S(2)}) collective-permute-start(bf16[256,256]{1,0:T(8,128)(2,1)S(1)} %shard_map.143.refs_0_), channel_id=1, source_target_pairs={{0,24},{8,16},{16,8},{24,0},{1,25},{9,17},{17,9},{25,1},{2,26},{10... | collective-permute-start | bytes 393224 | tf_op jit(solution)/shard_map/ppermute | solution.py:327
  70.3 7.4 %collective-permute-start.17 = (bf16[256,256]{1,0:T(8,128)(2,1)S(1)}, bf16[256,256]{1,0:T(8,128)(2,1)S(1)}, u32[]{:S(2)}, u32[]{:S(2)}) collective-permute-start(bf16[256,256]{1,0:T(8,128)(2,1)S(1)} %shard_map.143.refs_0_), channel_id=1, source_target_pairs={{0,16},{8,24},{16,0},{24,8},{1,17},{9,25},{17,1},{25,9},{2,18},{10... | collective-permute-start | bytes 393224 | tf_op jit(solution)/shard_map/ppermute | solution.py:327
  71.7 6.1 %collective-permute-start.15 = (bf16[256,256]{1,0:T(8,128)(2,1)S(1)}, bf16[256,256]{1,0:T(8,128)(2,1)S(1)}, u32[]{:S(2)}, u32[]{:S(2)}) collective-permute-start(bf16[256,256]{1,0:T(8,128)(2,1)S(1)} %shard_map.143.refs_0_), channel_id=1, source_target_pairs={{0,8},{8,0},{16,24},{24,16},{1,9},{9,1},{17,25},{25,17},{2,10},{10... | collective-permute-start | bytes 393224 | tf_op jit(solution)/shard_map/ppermute | solution.py:327
  73.1 17.4 %all-to-all-start.3 = ((bf16[8,16,512]{2,1,0:T(8,128)(2,1)}), bf16[8,16,512]{2,1,0:T(8,128)(2,1)S(1)}, u32[]{:S(2)}, u32[]{:S(2)}) async-start(bf16[8,16,512]{2,1,0:T(8,128)(2,1)} %get-tuple-element.64.og), calls=%async_computation.3 | async-start | bytes 262144 | tf_op jit(solution)/shard_map/all_to_all | solution.py:322
  76.5 4.6 %collective-permute-start.4 = (bf16[128,192]{1,0:T(8,128)(2,1)}, bf16[128,192]{1,0:T(8,128)(2,1)S(1)}, u32[]{:S(2)}, u32[]{:S(2)}) collective-permute-start(bf16[128,192]{1,0:T(8,128)(2,1)} %get-tuple-element.66), channel_id=1, source_target_pairs={{0,8},{8,0},{16,24},{24,16},{1,9},{9,1},{17,25},{25,17},{2,10},{10... | collective-permute-start | bytes 147464 | tf_op jit(solution)/shard_map/ppermute | solution.py:327
  77.2 14.3 %collective-permute-start.14 = (bf16[256,256]{1,0:T(8,128)(2,1)S(1)}, bf16[256,256]{1,0:T(8,128)(2,1)S(1)}, u32[]{:S(2)}, u32[]{:S(2)}) collective-permute-start(bf16[256,256]{1,0:T(8,128)(2,1)S(1)} %shard_map.143.refs_0_), channel_id=1, source_target_pairs={{0,1},{1,0},{2,3},{3,2},{4,5},{5,4},{6,7},{7,6},{8,9},{9,8},{10,11... | collective-permute-start | bytes 393224 | tf_op jit(solution)/shard_map/ppermute | solution.py:327
  77.3 14.2 %collective-permute-start.20 = (bf16[256,256]{1,0:T(8,128)(2,1)S(1)}, bf16[256,256]{1,0:T(8,128)(2,1)S(1)}, u32[]{:S(2)}, u32[]{:S(2)}) collective-permute-start(bf16[256,256]{1,0:T(8,128)(2,1)S(1)} %collective-permute-done.19.refs_6_), channel_id=1, source_target_pairs={{0,1},{1,0},{2,3},{3,2},{4,5},{5,4},{6,7},{7,6},{8,9},{9,8},{10,11... | collective-permute-start | bytes 393224 | tf_op jit(solution)/shard_map/ppermute | solution.py:327
  77.7 13.8 %collective-permute-start.18 = (bf16[256,256]{1,0:T(8,128)(2,1)S(1)}, bf16[256,256]{1,0:T(8,128)(2,1)S(1)}, u32[]{:S(2)}, u32[]{:S(2)}) collective-permute-start(bf16[256,256]{1,0:T(8,128)(2,1)S(1)} %collective-permute-done.17.refs_4_), channel_id=1, source_target_pairs={{0,1},{1,0},{2,3},{3,2},{4,5},{5,4},{6,7},{7,6},{8,9},{9,8},{10,11... | collective-permute-start | bytes 393224 | tf_op jit(solution)/shard_map/ppermute | solution.py:327
  77.8 13.7 %collective-permute-start.16 = (bf16[256,256]{1,0:T(8,128)(2,1)S(1)}, bf16[256,256]{1,0:T(8,128)(2,1)S(1)}, u32[]{:S(2)}, u32[]{:S(2)}) collective-permute-start(bf16[256,256]{1,0:T(8,128)(2,1)S(1)} %collective-permute-done.15.refs_2_), channel_id=1, source_target_pairs={{0,1},{1,0},{2,3},{3,2},{4,5},{5,4},{6,7},{7,6},{8,9},{9,8},{10,11... | collective-permute-start | bytes 393224 | tf_op jit(solution)/shard_map/ppermute | solution.py:327
  81.1 4.3 %collective-permute-start.5 = (bf16[128,192]{1,0:T(8,128)(2,1)S(1)}, bf16[128,192]{1,0:T(8,128)(2,1)S(1)}, u32[]{:S(2)}, u32[]{:S(2)}) collective-permute-start(bf16[128,192]{1,0:T(8,128)(2,1)S(1)} %copy-done.8), channel_id=1, source_target_pairs={{0,16},{8,24},{16,0},{24,8},{1,17},{9,25},{17,1},{25,9},{2,18},{10... | collective-permute-start | bytes 147464 | tf_op jit(solution)/shard_map/ppermute | solution.py:327
  85.4 5.2 %collective-permute-start.6 = (bf16[128,192]{1,0:T(8,128)(2,1)S(1)}, bf16[128,192]{1,0:T(8,128)(2,1)S(1)}, u32[]{:S(2)}, u32[]{:S(2)}) collective-permute-start(bf16[128,192]{1,0:T(8,128)(2,1)S(1)} %get-tuple-element.68), channel_id=1, source_target_pairs={{0,24},{8,16},{16,8},{24,0},{1,25},{9,17},{17,9},{25,1},{2,26},{10... | collective-permute-start | bytes 147464 | tf_op jit(solution)/shard_map/ppermute | solution.py:327

commit v3 on v2

--- a/solution.py
+++ b/solution.py
@@ -76,7 +76,8 @@
     return joined.reshape(-1, width).astype(BF16)
 
 
-def call(body, outs, *operands, scalars=0, scratch=()):
+def call(body, outs, *operands, scalars=0, scratch=(), us=1):
+    cost = pl.CostEstimate(flops=us * 10**9, bytes_accessed=us * 3_600_000, transcendentals=0)
     return pl.pallas_call(
         body,
         out_shape=[jax.ShapeDtypeStruct(s, d) for s, d in outs],
@@ -84,6 +85,7 @@
         out_specs=[VMEM] * len(outs),
         scratch_shapes=list(scratch),
         compiler_params=PARAMS,
+        cost_estimate=cost,
     )(*operands)
 
 
@@ -96,7 +98,7 @@
     width = q_out.shape[1]
     for k in range(sites):
         xhat, _ = norm_parts(pieces[k][...].astype(F32))
-        n_out[k * rows : (k + 1) * rows, :] = (xhat * gain[...]).astype(BF16)
+        n_out[k * rows : (k + 1) * rows, :] = (xhat * gain[:1, :]).astype(BF16)
     normed = n_out[...]
     q = mm_nt(normed, w_t[:width, :]).astype(BF16)
     key = mm_nt(normed, w_t[width : 2 * width, :]).astype(BF16)
@@ -129,9 +131,19 @@
         att_out[pl.ds((me ^ b) * haps, haps)] = pack_block(att[b * rows : (b + 1) * rows], haps)
 
 
-def column_step(
-    sites, haps, xc, at, row_out, gain, col_proj, kv_t_w, col_out, ga_out, og_out, n_out, gp_out, at_out
-):
+def split_inputs(haps, hap, feats, cot, *outs):
+    rows, width = feats.shape
+    per = rows // haps
+    for m in range(haps):
+        here = pl.ds(pl.multiple_of((hap[0] ^ m) * per, per), per)
+        outs[m][:, :width] = feats[here, :]
+        outs[m][:, width:] = cot[here, :]
+
+
+def column_step(sites, haps, hap, at, row_out, gain, col_proj, kv_t_w, col_out, *refs):
+    ga_out, og_out, n_out, gp_out, at_out, cot_out, xc = refs[haps:]
+    for m in range(haps):
+        xc[hap[0] ^ m] = refs[m][...]
     width = row_out.shape[0]
     heads = width // HEAD_DIM
     group = width // sites
@@ -140,6 +152,7 @@
     per = rows // haps
     cot_f = xc_all[:, width:]
     cot = cot_f.astype(BF16)
+    cot_out[...] = cot
     hid = xc_all[:, :width]
     for i in range(sites):
         a_i = unpack_block(at[i * haps : (i + 1) * haps], group)
@@ -147,7 +160,7 @@
     hid = hid.astype(BF16).astype(F32)
     grad_att = mm_nt(cot, col_out[...]).astype(BF16)
     xhat, rstd = norm_parts(hid)
-    normed = (xhat * gain[...]).astype(BF16)
+    normed = (xhat * gain[1:2, :]).astype(BF16)
     n_out[...] = normed
     packed = mm(normed, col_proj[...]).astype(BF16)
     q = packed[:, :width]
@@ -192,7 +205,7 @@
     packed_grad = jnp.concatenate([dq * SCALE, dk * SCALE, dv], axis=1).astype(BF16)
     gp_out[...] = packed_grad
     grad_normed = mm_nt(packed_grad, col_proj[...])
-    grad_hidden = (cot_f + norm_back(xhat, rstd, gain[...], grad_normed)).astype(BF16)
+    grad_hidden = (cot_f + norm_back(xhat, rstd, gain[1:2, :], grad_normed)).astype(BF16)
     for i in range(sites):
         g_i = mm_nt(grad_hidden, row_out[i * group : (i + 1) * group, :])
         ga_out[i * haps : (i + 1) * haps] = pack_block(g_i, haps)
@@ -200,14 +213,13 @@
     og_out[...] = both.reshape(haps, per, 2 * width).astype(BF16)
 
 
-def column_weights(sites, haps, core, xc, at, og, normed, gp, att_t, keep, send, both):
+def column_weights(sites, haps, core, cot, at, og, normed, gp, att_t, keep, send, both):
     width = normed.shape[1]
     group = width // sites
     half = width // 2
-    cot = flat_rows(xc[:, :, width:])
     grad_hidden = flat_rows(og[:, :, width:])
     both[:, : 3 * width] = mm_tn(normed[...], gp[...]).astype(BF16)
-    both[:, 3 * width : 4 * width] = mm(att_t[...], cot).astype(BF16)
+    both[:, 3 * width : 4 * width] = mm(att_t[...], cot[...]).astype(BF16)
     for i in range(sites):
         a_i = unpack_block(at[i * haps : (i + 1) * haps], group)
         both[i * group : (i + 1) * group, 4 * width :] = mm_tn(a_i, grad_hidden).astype(BF16)
@@ -270,7 +282,7 @@
     both = flat_rows(og[...], F32)
     grad_normed = sum(mm(gps[k][...], w_all[me ^ k]) for k in range(sites))
     xhat, rstd = norm_parts(feats[...].astype(F32))
-    grad = both[:, width:] + norm_back(xhat, rstd, gain[...], grad_normed)
+    grad = both[:, width:] + norm_back(xhat, rstd, gain[:1, :], grad_normed)
     out_ref[...] = both[:, :width].astype(BF16)
     gf_ref[...] = grad.astype(BF16)
 
@@ -348,16 +360,21 @@
     both_axes = ("site", "hap")
     me = lax.axis_index("site")
     idx = me.reshape(1).astype(jnp.int32)
-    core = (lax.axis_index("hap") % 2).reshape(1).astype(jnp.int32)
+    hap = lax.axis_index("hap").reshape(1).astype(jnp.int32)
+    core = hap % 2
     factor = lane_factor(per, group)
     block = ((count, per // factor, group * factor), BF16)
     feats = features.reshape(rows, width)
     cot = cotangent.reshape(rows, width)
-    gain_r = row_gain.reshape(1, width)
-    gain_c = column_norm_gain.reshape(1, width)
 
     pieces = [feats] + [swapped(feats, "site", k) for k in range(1, sites)]
-    xc = exchange(jnp.concatenate([feats, cot], axis=1).reshape(haps, per, 2 * width), "hap")
+    gains = jnp.stack([row_gain, column_norm_gain])
+    xcs = call(
+        functools.partial(split_inputs, haps),
+        [((per, 2 * width), BF16)] * haps,
+        hap, feats, cot, scalars=1,
+    )
+    xcs = [xcs[0]] + [swapped(xcs[m], "hap", m) for m in range(1, haps)]
     w_all = jnp.transpose(row_proj.reshape(width, 3, sites, group), (2, 1, 3, 0)).reshape(
         sites, 3 * group, width
     )
@@ -374,11 +391,10 @@
             ((group, total), BF16),
             ((total, width), BF16),
         ],
-        idx, link_pattern, *pieces, gain_r, w_t, scalars=2,
-    )
-    att, xc = lax.optimization_barrier((att, xc))
+        idx, link_pattern, *pieces, gains, w_t, scalars=2, us=3,
+    )
     at = exchange(att, both_axes)
-    ga, og, col_normed, col_gp, col_att_t = call(
+    ga, og, col_normed, col_gp, col_att_t, cot = call(
         functools.partial(column_step, sites, haps),
         [
             block,
@@ -386,15 +402,17 @@
             ((rows, width), BF16),
             ((rows, 3 * width), BF16),
             ((width, rows), BF16),
+            ((rows, width), BF16),
         ],
-        xc, at, row_out, gain_c, col_proj, kv_t_w, col_out,
+        hap, at, row_out, gains, col_proj, kv_t_w, col_out, *xcs, scalars=1, us=3,
+        scratch=[pltpu.VMEM((haps, per, 2 * width), BF16)],
     )
     g_in = exchange(ga, both_axes)
     half = width // 2
     col_keep, col_send = call(
         functools.partial(column_weights, sites, haps),
         [((half, 5 * width), BF16)] * 2,
-        core, xc, at, og, col_normed, col_gp, col_att_t, scalars=1,
+        core, cot, at, og, col_normed, col_gp, col_att_t, scalars=1, us=2,
         scratch=[pltpu.VMEM((width, 5 * width), BF16)],
     )
     col_got = swapped(col_send, "hap", 1)
@@ -409,7 +427,7 @@
     *gps, row_keep, row_send = call(
         functools.partial(row_backward, sites, haps),
         [((rows, 3 * group), BF16)] * sites + [((3 * group // 2, width), BF16)] * 2,
-        idx, core, g_in, prob, q, val, key_t, normed, scalars=2,
+        idx, core, g_in, prob, q, val, key_t, normed, scalars=2, us=3,
         scratch=[
             pltpu.VMEM((total, group), BF16),
             pltpu.VMEM((total, total), BF16),
@@ -420,14 +438,15 @@
     depth = 3 * group // 2 + 5 * half // sites
     (joined,) = call(weights_join, [((depth, width), BF16)], row_keep, row_got, *cols)
     parts = [joined] + [swapped(joined, "hap", 2 * m) for m in range(1, haps // 2)]
+    gps = [gps[0]] + [swapped(gps[k], "site", k) for k in range(1, sites)]
+    parts, gps = lax.optimization_barrier((parts, gps))
     (mine,) = call(weights_sum, [((depth, width), BF16)], *parts)
-    og, _ = lax.optimization_barrier((og, row_keep))
+    og, _ = lax.optimization_barrier((og, mine))
     og_in = exchange(og, "hap")
-    gps = [gps[0]] + [swapped(gps[k], "site", k) for k in range(1, sites)]
     out, grad = call(
         functools.partial(row_finish, sites),
         [((rows, width), BF16)] * 2,
-        idx, feats, gain_r, w_all, og_in, *gps, scalars=1,
+        idx, feats, gains, w_all, og_in, *gps, scalars=1,
     )
     full = [mine] + [swapped(mine, "site", k) for k in range(1, sites)]
     full = [x for piece in full for x in (piece, swapped(piece, "hap", 1))]

time: 93.5 us -> 83.9 us (0.90)
  waiting for transfers between devices: 38.6 us -> 25.8 us
  starting transfers between devices: 35.7 us -> 40.8 us
  other arithmetic: 1.59 us -> 0.01 us
  Pallas kernels: 13.5 us -> 12.3 us
  local copies, waits for them, and re-layouts: 2.66 us -> 3.65 us
    ppermute x21 -> x28, starting transfers between devices: 18.3 us -> 29.5 us  [swapped(): return lax.ppermute(value, axis, [(i, i ^ by) for i in range(length)])]
    ppermute x21 -> x28, waiting for transfers between devices: 25.2 us -> 18.6 us  [swapped(): return lax.ppermute(value, axis, [(i, i ^ by) for i in range(length)])]
    all_to_all x4 -> x3, waiting for transfers between devices: 13.5 us -> 7.18 us  [exchange(): return lax.all_to_all(value, axis, 0, 0, tiled=True)]
    all_to_all x4 -> x3, starting transfers between devices: 17.5 us -> 11.3 us  [exchange(): return lax.all_to_all(value, axis, 0, 0, tiled=True)]
    concatenate x1 -> x0, other arithmetic: 1.59 us -> none  [on_device(): jnp.concatenate([feats, cot], axis=1).reshape(haps, per, 2 * width)]
    pallas_call x9 -> x10, Pallas kernels: 13.5 us -> 12.3 us  [call(): pl.pallas_call(body, out_shape=[jax.ShapeDtypeStruct(s, d) for s, d in ou...]
    unnamed x22, local copies, waits for them, and re-layouts: 1.68 us -> 2.66 us
  transfers between devices with their start and end apart: 25 -> 31, of which waited for: 11 -> 12; matrix products, arithmetic and copies ran while one was open for 0% -> 2% of each run, Pallas kernels for 8% -> 4%
where the time goes in v3:
time: 83.9 us; the launch traced here: 83.5 us
  starting transfers between devices  40.8 us (49%)
  waiting for transfers between devices  25.8 us (31%)
  Pallas kernels  12.3 us (15%)
  local copies, waits for them, and re-layouts  3.65 us (4%)
  between operations  0.87 us (1%)
    ppermute x28, starting transfers between devices, swapped(): return lax.ppermute(value, axis, [(i, i ^ by) for i in range(length)])  29.5 us
    ppermute x28, waiting for transfers between devices, swapped(): return lax.ppermute(value, axis, [(i, i ^ by) for i in range(length)])  18.6 us
    pallas_call x10, Pallas kernels, call(): pl.pallas_call(body, out_shape=[jax.ShapeDtypeStruct(s, d) for s, d in ou...  12.3 us
    all_to_all x3, starting transfers between devices, exchange(): return lax.all_to_all(value, axis, 0, 0, tiled=True)  11.3 us
    all_to_all x3, waiting for transfers between devices, exchange(): return lax.all_to_all(value, axis, 0, 0, tiled=True)  7.18 us
    unnamed x22, local copies, waits for them, and re-layouts  2.66 us
  transfers between devices with their start and end apart: 31, of which 12 were waited for; matrix products, arithmetic and copies ran while one was open for 2% of the time, Pallas kernels for 4%

profile of v3, /device:TPU:0, one launch (start us, length us, event | category | flops | bytes accessed | tf_op | source)
XLA Modules:
  0.0 83.5 jit_solution(7891382454688655397)
XLA Ops:
  0.6 4.0 %collective-permute-start.2 = (bf16[128,256]{1,0:T(8,128)(2,1)}, bf16[128,256]{1,0:T(8,128)(2,1)S(1)}, u32[]{:S(2)}, u32[]{:S(2)}) collective-permute-start(bf16[128,256]{1,0:T(8,128)(2,1)} %bitcast.19), channel_id=1, source_target_pairs={{0,24},{8,16},{16,8},{24,0},{1,25},{9,17},{17,9},{25,1},{2,26},{10... | collective-permute-start | bytes 196616 | tf_op jit(solution)/shard_map/ppermute | solution.py:339
  4.6 0.5 collective-permute-start.1
  5.1 0.1 collective-permute-start
  5.2 1.2 %copy.17 = bf16[256,768]{0,1:T(8,128)(2,1)S(1)} copy(bf16[256,768]{1,0:T(8,128)(2,1)} %param.12) | data formatting | bytes 786432 | tf_op args[3]
  6.5 0.6 copy-done.9
  7.2 1.9 %collective-permute-done.1.refs_2_ = bf16[128,256]{1,0:T(8,128)(2,1)S(1)} collective-permute-done((bf16[128,256]{1,0:T(8,128)(2,1)}, bf16[128,256]{1,0:T(8,128)(2,1)S(1)}, u32[]{:S(2)}, u32[]{:S(2)}) %collective-permute-start.1) | collective-permute-done | bytes 65568 | tf_op jit(solution)/shard_map/ppermute | solution.py:339
  9.1 0.5 collective-permute-done.refs_1_
  9.6 3.3 %shard_map.136 = (bf16[32,8,128]{2,1,0:T(8,128)(2,1)}, bf16[2,512,512]{2,1,0:T(8,128)(2,1)S(1)}, bf16[512,64]{1,0:T(8,128)(2,1)S(1)}, bf16[512,64]{1,0:T(8,128)(...) custom-call(s32[1]{0:T(128)} %bitcast.idx, s32[4,4]{1,0:T(4,128)S(1)} %copy-done.5, ...), custom_call_target="tpu_custom_call" | custom-call | flops 3000000000 | bytes 10800000 | tf_op jit(solution)/shard_map/pallas_call | solution.py:81
  12.8 0.7 copy-done.6
  13.5 4.9 %all-to-all-start = ((bf16[32,8,128]{2,1,0:T(8,128)(2,1)}), bf16[32,8,128]{2,1,0:T(8,128)(2,1)S(1)}, u32[]{:S(2)}, u32[]{:S(2)}) async-start(bf16[32,8,128]{2,1,0:T(8,128)(2,1)} %get-tuple-element.58), calls=%async_computation | async-start | bytes 131072 | tf_op jit(solution)/shard_map/all_to_all | solution.py:334
  18.5 0.3 collective-permute-start.3
  18.8 1.7 %collective-permute-start.4 = (bf16[16,512]{1,0:T(8,128)(2,1)S(1)}, bf16[16,512]{1,0:T(8,128)(2,1)S(1)}, u32[]{:S(2)}, u32[]{:S(2)}) collective-permute-start(bf16[16,512]{1,0:T(8,128)(2,1)S(1)} %get-tuple-element.61), channel_id=1, source_target_pairs={{0,2},{1,3},{2,0},{3,1},{4,6},{5,7},{6,4},{7,5},{8,10},{9,11},{10,... | collective-permute-start | bytes 49160 | tf_op jit(solution)/shard_map/ppermute | solution.py:339
  20.5 2.6 %collective-permute-start.6 = (bf16[16,512]{1,0:T(8,128)(2,1)S(1)}, bf16[16,512]{1,0:T(8,128)(2,1)S(1)}, u32[]{:S(2)}, u32[]{:S(2)}) collective-permute-start(bf16[16,512]{1,0:T(8,128)(2,1)S(1)} %get-tuple-element.63), channel_id=1, source_target_pairs={{0,4},{1,5},{2,6},{3,7},{4,0},{5,1},{6,2},{7,3},{8,12},{9,13},{10,... | collective-permute-start | bytes 49160 | tf_op jit(solution)/shard_map/ppermute | solution.py:339
  23.1 0.1 collective-permute-start.7
  23.2 3.5 %collective-permute-start.8 = (bf16[16,512]{1,0:T(8,128)(2,1)S(1)}, bf16[16,512]{1,0:T(8,128)(2,1)S(1)}, u32[]{:S(2)}, u32[]{:S(2)}) collective-permute-start(bf16[16,512]{1,0:T(8,128)(2,1)S(1)} %get-tuple-element.65), channel_id=1, source_target_pairs={{0,6},{1,7},{2,4},{3,5},{4,2},{5,3},{6,0},{7,1},{8,14},{9,15},{10,... | collective-permute-start | bytes 49160 | tf_op jit(solution)/shard_map/ppermute | solution.py:339
  26.8 0.9 %slice-done = bf16[256,512]{1,0:T(8,128)(2,1)S(1)} async-done(((bf16[256,768]{1,0:T(8,128)(2,1)}), bf16[256,512]{1,0:T(8,128)(2,1)S(1)}, s32[]{:S(2)}) %slice-start) | async-done | bytes 262168 | tf_op jit(solution)/shard_map/slice | solution.py:382
  27.7 0.1 copy.20
  27.9 0.8 %collective-permute-done.8.refs_6_ = bf16[16,512]{1,0:T(8,128)(2,1)S(1)} collective-permute-done((bf16[16,512]{1,0:T(8,128)(2,1)S(1)}, bf16[16,512]{1,0:T(8,128)(2,1)S(1)}, u32[]{:S(2)}, u32[]{:S(2)}) %collective-permute-start.8) | collective-permute-done | bytes 16416 | tf_op jit(solution)/shard_map/ppermute | solution.py:339
  28.7 2.9 %collective-permute-done.9.refs_7_ = bf16[16,512]{1,0:T(8,128)(2,1)S(1)} collective-permute-done((bf16[16,512]{1,0:T(8,128)(2,1)S(1)}, bf16[16,512]{1,0:T(8,128)(2,1)S(1)}, u32[]{:S(2)}, u32[]{:S(2)}) %collective-permute-start.9) | collective-permute-done | bytes 16416 | tf_op jit(solution)/shard_map/ppermute | solution.py:339
  31.7 2.9 %shard_map.138 = (bf16[32,8,128]{2,1,0:T(8,128)(2,1)}, bf16[8,16,512]{2,1,0:T(8,128)(2,1)}, bf16[128,256]{1,0:T(8,128)(2,1)S(1)}, bf16[128,768]{1,0:T(8,128)(2,1...) custom-call(s32[1]{0:T(128)} %bitcast.7.hap, bf16[32,8,128]{2,1,0:T(8,128)(2,1)S(1)} %all-to-all-done.at, ...), custom_call_target="tpu_custom_call" | custom-call | flops 3000000000 | bytes 10800000 | tf_op jit(solution)/shard_map/pallas_call | solution.py:81
  34.6 1.3 %shard_map.139 = (bf16[128,1280]{1,0:T(8,128)(2,1)S(1)}, bf16[128,1280]{1,0:T(8,128)(2,1)S(1)}) custom-call(s32[1]{0:T(128)S(6)} %select_n.12.core, bf16[128,256]{1,0:T(8,128)(2,1)S(1)} %get-tuple-element.69.cot, bf16[32,8,128]{2,1,0:T(8,128)(2,1)S(1)} %all-to-all-done.at, bf16[8,16,512]{2,1,0:T(8,128)(2,1)} %get-tuple-element.99.og, ...), custom_call_target="tpu_custom_call" | custom-call | flops 2000000000 | bytes 7200000 | tf_op jit(solution)/shard_map/pallas_call | solution.py:81
  35.9 0.2 collective-permute-start.10
  36.1 3.0 %all-to-all-start.1 = ((bf16[32,8,128]{2,1,0:T(8,128)(2,1)}), bf16[32,8,128]{2,1,0:T(8,128)(2,1)S(1)}, u32[]{:S(2)}, u32[]{:S(2)}) async-start(bf16[32,8,128]{2,1,0:T(8,128)(2,1)} %get-tuple-element.68), calls=%async_computation.1 | async-start | bytes 131072 | tf_op jit(solution)/shard_map/all_to_all | solution.py:334
  39.1 0.2 shard_map.140
  39.3 7.2 %all-to-all-done.1.g_in = bf16[32,8,128]{2,1,0:T(8,128)(2,1)S(1)} async-done(((bf16[32,8,128]{2,1,0:T(8,128)(2,1)}), bf16[32,8,128]{2,1,0:T(8,128)(2,1)S(1)}, u32[]{:S(2)}, u32[]{:S(2)}) %all-to-all-start.1) | async-done | bytes 65568 | tf_op jit(solution)/shard_map/all_to_all | solution.py:334
  46.5 0.7 collective-permute-start.12
  47.2 0.6 collective-permute-start.13
  47.8 2.2 %collective-permute-start.14 = (bf16[32,1280]{1,0:T(8,128)(2,1)S(1)}, bf16[32,1280]{1,0:T(8,128)(2,1)S(1)}, u32[]{:S(2)}, u32[]{:S(2)}) collective-permute-start(bf16[32,1280]{1,0:T(8,128)(2,1)S(1)} %get-tuple-element.90), channel_id=1, source_target_pairs={{0,24},{8,16},{16,8},{24,0},{1,25},{9,17},{17,9},{25,1},{2,26},{10... | collective-permute-start | bytes 245768 | tf_op jit(solution)/shard_map/ppermute | solution.py:339
  50.0 2.1 %shard_map.141 = (bf16[128,192]{1,0:T(8,128)(2,1)S(1)}, bf16[128,192]{1,0:T(8,128)(2,1)S(1)}, bf16[128,192]{1,0:T(8,128)(2,1)S(1)}, bf16[128,192]{1,0:T(8,128)(2...) custom-call(s32[1]{0:T(128)} %bitcast.idx, s32[1]{0:T(128)S(6)} %select_n.12.core, ...), custom_call_target="tpu_custom_call" | custom-call | flops 3000000000 | bytes 10800000 | tf_op jit(solution)/shard_map/pallas_call | solution.py:81
  52.2 1.2 %collective-permute-done.11.row_got = bf16[96,256]{1,0:T(8,128)(2,1)S(1)} collective-permute-done((bf16[96,256]{1,0:T(8,128)(2,1)S(1)}, bf16[96,256]{1,0:T(8,128)(2,1)S(1)}, u32[]{:S(2)}, u32[]{:S(2)}) %collective-permute-start.11) | collective-permute-done | bytes 49184 | tf_op jit(solution)/shard_map/ppermute | solution.py:339
  53.5 0.8 %collective-permute-start.17 = (bf16[256,256]{1,0:T(8,128)(2,1)S(1)}, bf16[256,256]{1,0:T(8,128)(2,1)S(1)}, u32[]{:S(2)}, u32[]{:S(2)}) collective-permute-start(bf16[256,256]{1,0:T(8,128)(2,1)S(1)} %shard_map.142.refs_0_), channel_id=1, source_target_pairs={{0,6},{1,7},{2,4},{3,5},{4,2},{5,3},{6,0},{7,1},{8,14},{9,15},{10,... | collective-permute-start | bytes 393224 | tf_op jit(solution)/shard_map/ppermute | solution.py:339
  54.4 1.1 %collective-permute-start.16 = (bf16[256,256]{1,0:T(8,128)(2,1)S(1)}, bf16[256,256]{1,0:T(8,128)(2,1)S(1)}, u32[]{:S(2)}, u32[]{:S(2)}) collective-permute-start(bf16[256,256]{1,0:T(8,128)(2,1)S(1)} %shard_map.142.refs_0_), channel_id=1, source_target_pairs={{0,4},{1,5},{2,6},{3,7},{4,0},{5,1},{6,2},{7,3},{8,12},{9,13},{10,... | collective-permute-start | bytes 393224 | tf_op jit(solution)/shard_map/ppermute | solution.py:339
  55.5 2.5 %collective-permute-start.15 = (bf16[256,256]{1,0:T(8,128)(2,1)S(1)}, bf16[256,256]{1,0:T(8,128)(2,1)S(1)}, u32[]{:S(2)}, u32[]{:S(2)}) collective-permute-start(bf16[256,256]{1,0:T(8,128)(2,1)S(1)} %shard_map.142.refs_0_), channel_id=1, source_target_pairs={{0,2},{1,3},{2,0},{3,1},{4,6},{5,7},{6,4},{7,5},{8,10},{9,11},{10,... | collective-permute-start | bytes 393224 | tf_op jit(solution)/shard_map/ppermute | solution.py:339
  58.0 1.3 %collective-permute-start.18 = (bf16[128,192]{1,0:T(8,128)(2,1)S(1)}, bf16[128,192]{1,0:T(8,128)(2,1)S(1)}, u32[]{:S(2)}, u32[]{:S(2)}) collective-permute-start(bf16[128,192]{1,0:T(8,128)(2,1)S(1)} %get-tuple-element.92), channel_id=1, source_target_pairs={{0,8},{8,0},{16,24},{24,16},{1,9},{9,1},{17,25},{25,17},{2,10},{10... | collective-permute-start | bytes 147464 | tf_op jit(solution)/shard_map/ppermute | solution.py:339
  59.2 1.2 %collective-permute-start.19 = (bf16[128,192]{1,0:T(8,128)(2,1)S(1)}, bf16[128,192]{1,0:T(8,128)(2,1)S(1)}, u32[]{:S(2)}, u32[]{:S(2)}) collective-permute-start(bf16[128,192]{1,0:T(8,128)(2,1)S(1)} %get-tuple-element.93), channel_id=1, source_target_pairs={{0,16},{8,24},{16,0},{24,8},{1,17},{9,25},{17,1},{25,9},{2,18},{10... | collective-permute-start | bytes 147464 | tf_op jit(solution)/shard_map/ppermute | solution.py:339
  60.4 1.8 %collective-permute-done.18.refs_1_ = bf16[128,192]{1,0:T(8,128)(2,1)S(1)} collective-permute-done((bf16[128,192]{1,0:T(8,128)(2,1)S(1)}, bf16[128,192]{1,0:T(8,128)(2,1)S(1)}, u32[]{:S(2)}, u32[]{:S(2)}) %collective-permute-start.18) | collective-permute-done | bytes 49184 | tf_op jit(solution)/shard_map/ppermute | solution.py:339
  62.2 1.9 %collective-permute-start.20 = (bf16[128,192]{1,0:T(8,128)(2,1)S(1)}, bf16[128,192]{1,0:T(8,128)(2,1)S(1)}, u32[]{:S(2)}, u32[]{:S(2)}) collective-permute-start(bf16[128,192]{1,0:T(8,128)(2,1)S(1)} %get-tuple-element.94), channel_id=1, source_target_pairs={{0,24},{8,16},{16,8},{24,0},{1,25},{9,17},{17,9},{25,1},{2,26},{10... | collective-permute-start | bytes 147464 | tf_op jit(solution)/shard_map/ppermute | solution.py:339
  64.1 3.3 %collective-permute-done.20.refs_3_ = bf16[128,192]{1,0:T(8,128)(2,1)S(1)} collective-permute-done((bf16[128,192]{1,0:T(8,128)(2,1)S(1)}, bf16[128,192]{1,0:T(8,128)(2,1)S(1)}, u32[]{:S(2)}, u32[]{:S(2)}) %collective-permute-start.20) | collective-permute-done | bytes 49184 | tf_op jit(solution)/shard_map/ppermute | solution.py:339
  67.4 0.1 collective-permute-done.16.refs_2_
  67.6 3.4 %all-to-all-start.2 = ((bf16[8,16,512]{2,1,0:T(8,128)(2,1)}), bf16[8,16,512]{2,1,0:T(8,128)(2,1)S(1)}, u32[]{:S(2)}, u32[]{:S(2)}) async-start(bf16[8,16,512]{2,1,0:T(8,128)(2,1)} %get-tuple-element.99.og), calls=%async_computation.2 | async-start | bytes 262144 | tf_op jit(solution)/shard_map/all_to_all | solution.py:334
  70.9 1.9 %collective-permute-start.26 = (bf16[256,256]{1,0:T(8,128)(2,1)S(1)}, bf16[256,256]{1,0:T(8,128)(2,1)S(1)}, u32[]{:S(2)}, u32[]{:S(2)}) collective-permute-start(bf16[256,256]{1,0:T(8,128)(2,1)S(1)} %shard_map.143.refs_0_), channel_id=1, source_target_pairs={{0,24},{8,16},{16,8},{24,0},{1,25},{9,17},{17,9},{25,1},{2,26},{10... | collective-permute-start | bytes 393224 | tf_op jit(solution)/shard_map/ppermute | solution.py:339
  72.8 0.9 %collective-permute-start.24 = (bf16[256,256]{1,0:T(8,128)(2,1)S(1)}, bf16[256,256]{1,0:T(8,128)(2,1)S(1)}, u32[]{:S(2)}, u32[]{:S(2)}) collective-permute-start(bf16[256,256]{1,0:T(8,128)(2,1)S(1)} %shard_map.143.refs_0_), channel_id=1, source_target_pairs={{0,16},{8,24},{16,0},{24,8},{1,17},{9,25},{17,1},{25,9},{2,18},{10... | collective-permute-start | bytes 393224 | tf_op jit(solution)/shard_map/ppermute | solution.py:339
  73.7 0.8 collective-permute-start.22
  74.5 3.7 %collective-permute-done.26.refs_6_ = bf16[256,256]{1,0:T(8,128)(2,1)S(1)} collective-permute-done((bf16[256,256]{1,0:T(8,128)(2,1)S(1)}, bf16[256,256]{1,0:T(8,128)(2,1)S(1)}, u32[]{:S(2)}, u32[]{:S(2)}) %collective-permute-start.26) | collective-permute-done | bytes 131104 | tf_op jit(solution)/shard_map/ppermute | solution.py:339
  78.2 2.2 %collective-permute-done.24.refs_4_ = bf16[256,256]{1,0:T(8,128)(2,1)S(1)} collective-permute-done((bf16[256,256]{1,0:T(8,128)(2,1)S(1)}, bf16[256,256]{1,0:T(8,128)(2,1)S(1)}, u32[]{:S(2)}, u32[]{:S(2)}) %collective-permute-start.24) | collective-permute-done | bytes 131104 | tf_op jit(solution)/shard_map/ppermute | solution.py:339
  80.5 0.5 collective-permute-start.23
  81.0 1.0 %shard_map.144 = (bf16[128,256]{1,0:T(8,128)(2,1)}, bf16[128,256]{1,0:T(8,128)(2,1)}) custom-call(s32[1]{0:T(128)} %bitcast.idx, bf16[128,256]{1,0:T(8,128)(2,1)S(1)} %bitcast.24, f32[2,256]{1,0:T(2,128)S(1)} %pad_maximum_fusion.refs_4_.gain, bf16[4,192,256]{2,1,0:T(8,128)(2,1)S(1)} %bitcast.16, bf16[8,16,512]{2,1,0:T(8,128)(2,1)S(1)} %all-to-all-done.2.og, ...), custom_call_target="tpu_custom_call" | custom-call | flops 1000000000 | bytes 3600000 | tf_op jit(solution)/shard_map/pallas_call | solution.py:81
  82.0 1.5 %shard_map.145 = (f32[256,768]{1,0:T(8,128)}, f32[256,256]{1,0:T(8,128)}, f32[256,768]{1,0:T(8,128)}, f32[256,256]{1,0:T(8,128)}) custom-call(s32[1]{0:T(128)} %bitcast.idx, s32[1]{0:T(128)S(6)} %select_n.12.core, bf16[256,256]{1,0:T(8,128)(2,1)S(1)} %shard_map.143.refs_0_, bf16[256,256]{1,0:T(8,128)(2,1)S(1)} %collective-permute-done.21.refs_1_, ...), custom_call_target="tpu_custom_call" | custom-call | flops 1000000000 | bytes 3600000 | tf_op jit(solution)/shard_map/pallas_call | solution.py:81
  (51 shorter events, 0.5 us)
Async XLA Ops:
  0.6 6.6 %collective-permute-start.2 = (bf16[128,256]{1,0:T(8,128)(2,1)}, bf16[128,256]{1,0:T(8,128)(2,1)S(1)}, u32[]{:S(2)}, u32[]{:S(2)}) collective-permute-start(bf16[128,256]{1,0:T(8,128)(2,1)} %bitcast.19), channel_id=1, source_target_pairs={{0,24},{8,16},{16,8},{24,0},{1,25},{9,17},{17,9},{25,1},{2,26},{10... | collective-permute-start | bytes 196616 | tf_op jit(solution)/shard_map/ppermute | solution.py:339
  4.6 4.5 %collective-permute-start.1 = (bf16[128,256]{1,0:T(8,128)(2,1)}, bf16[128,256]{1,0:T(8,128)(2,1)S(1)}, u32[]{:S(2)}, u32[]{:S(2)}) collective-permute-start(bf16[128,256]{1,0:T(8,128)(2,1)} %bitcast.20), channel_id=1, source_target_pairs={{0,16},{8,24},{16,0},{24,8},{1,17},{9,25},{17,1},{25,9},{2,18},{10... | collective-permute-start | bytes 196616 | tf_op jit(solution)/shard_map/ppermute | solution.py:339
  5.1 4.5 %collective-permute-start = (bf16[128,256]{1,0:T(8,128)(2,1)}, bf16[128,256]{1,0:T(8,128)(2,1)S(1)}, u32[]{:S(2)}, u32[]{:S(2)}) collective-permute-start(bf16[128,256]{1,0:T(8,128)(2,1)} %bitcast.21), channel_id=1, source_target_pairs={{0,8},{8,0},{16,24},{24,16},{1,9},{9,1},{17,25},{25,17},{2,10},{10... | collective-permute-start | bytes 196616 | tf_op jit(solution)/shard_map/ppermute | solution.py:339
  6.4 0.7 copy-start.9
  6.5 3.1 %copy-start.4 = (bf16[128,1,256]{2,0,1:T(8,128)(2,1)S(1)}, bf16[128,1,256]{2,0,1:T(8,128)(2,1)}, u32[]{:S(2)}) copy-start(bf16[128,1,256]{2,0,1:T(8,128)(2,1)} %param.9) | copy-start | bytes 196612
  6.5 0.7 copy-start.8
  7.2 2.4 %copy-start.5 = (s32[4,4]{1,0:T(4,128)S(1)}, s32[4,4]{1,0:T(4,128)}, u32[]{:S(2)}) copy-start(s32[4,4]{1,0:T(4,128)} %link.1) | copy-start | bytes 196
  12.8 0.7 copy-start.6
  13.5 4.9 %copy-start.3 = (bf16[128,1,256]{2,0,1:T(8,128)(2,1)S(1)}, bf16[128,1,256]{2,0,1:T(8,128)(2,1)}, u32[]{:S(2)}) copy-start(bf16[128,1,256]{2,0,1:T(8,128)(2,1)} %param.17) | copy-start | bytes 196612
  13.5 18.2 %all-to-all-start = ((bf16[32,8,128]{2,1,0:T(8,128)(2,1)}), bf16[32,8,128]{2,1,0:T(8,128)(2,1)S(1)}, u32[]{:S(2)}, u32[]{:S(2)}) async-start(bf16[32,8,128]{2,1,0:T(8,128)(2,1)} %get-tuple-element.58), calls=%async_computation | async-start | bytes 131072 | tf_op jit(solution)/shard_map/all_to_all | solution.py:334
  18.5 4.7 %collective-permute-start.3 = (bf16[16,512]{1,0:T(8,128)(2,1)S(1)}, bf16[16,512]{1,0:T(8,128)(2,1)S(1)}, u32[]{:S(2)}, u32[]{:S(2)}) collective-permute-start(bf16[16,512]{1,0:T(8,128)(2,1)S(1)} %get-tuple-element.60), channel_id=1, source_target_pairs={{0,1},{1,0},{2,3},{3,2},{4,5},{5,4},{6,7},{7,6},{8,9},{9,8},{10,11... | collective-permute-start | bytes 49160 | tf_op jit(solution)/shard_map/ppermute | solution.py:339
  18.8 7.9 %collective-permute-start.4 = (bf16[16,512]{1,0:T(8,128)(2,1)S(1)}, bf16[16,512]{1,0:T(8,128)(2,1)S(1)}, u32[]{:S(2)}, u32[]{:S(2)}) collective-permute-start(bf16[16,512]{1,0:T(8,128)(2,1)S(1)} %get-tuple-element.61), channel_id=1, source_target_pairs={{0,2},{1,3},{2,0},{3,1},{4,6},{5,7},{6,4},{7,5},{8,10},{9,11},{10,... | collective-permute-start | bytes 49160 | tf_op jit(solution)/shard_map/ppermute | solution.py:339
  20.5 7.4 %collective-permute-start.5 = (bf16[16,512]{1,0:T(8,128)(2,1)S(1)}, bf16[16,512]{1,0:T(8,128)(2,1)S(1)}, u32[]{:S(2)}, u32[]{:S(2)}) collective-permute-start(bf16[16,512]{1,0:T(8,128)(2,1)S(1)} %get-tuple-element.62), channel_id=1, source_target_pairs={{0,3},{1,2},{2,1},{3,0},{4,7},{5,6},{6,5},{7,4},{8,11},{9,10},{10,... | collective-permute-start | bytes 49160 | tf_op jit(solution)/shard_map/ppermute | solution.py:339
  20.5 7.4 %collective-permute-start.6 = (bf16[16,512]{1,0:T(8,128)(2,1)S(1)}, bf16[16,512]{1,0:T(8,128)(2,1)S(1)}, u32[]{:S(2)}, u32[]{:S(2)}) collective-permute-start(bf16[16,512]{1,0:T(8,128)(2,1)S(1)} %get-tuple-element.63), channel_id=1, source_target_pairs={{0,4},{1,5},{2,6},{3,7},{4,0},{5,1},{6,2},{7,3},{8,12},{9,13},{10,... | collective-permute-start | bytes 49160 | tf_op jit(solution)/shard_map/ppermute | solution.py:339
  23.1 4.8 %collective-permute-start.7 = (bf16[16,512]{1,0:T(8,128)(2,1)S(1)}, bf16[16,512]{1,0:T(8,128)(2,1)S(1)}, u32[]{:S(2)}, u32[]{:S(2)}) collective-permute-start(bf16[16,512]{1,0:T(8,128)(2,1)S(1)} %get-tuple-element.64), channel_id=1, source_target_pairs={{0,5},{1,4},{2,7},{3,6},{4,1},{5,0},{6,3},{7,2},{8,13},{9,12},{10,... | collective-permute-start | bytes 49160 | tf_op jit(solution)/shard_map/ppermute | solution.py:339
  23.2 5.6 %collective-permute-start.8 = (bf16[16,512]{1,0:T(8,128)(2,1)S(1)}, bf16[16,512]{1,0:T(8,128)(2,1)S(1)}, u32[]{:S(2)}, u32[]{:S(2)}) collective-permute-start(bf16[16,512]{1,0:T(8,128)(2,1)S(1)} %get-tuple-element.65), channel_id=1, source_target_pairs={{0,6},{1,7},{2,4},{3,5},{4,2},{5,3},{6,0},{7,1},{8,14},{9,15},{10,... | collective-permute-start | bytes 49160 | tf_op jit(solution)/shard_map/ppermute | solution.py:339
  26.7 5.0 %collective-permute-start.9 = (bf16[16,512]{1,0:T(8,128)(2,1)S(1)}, bf16[16,512]{1,0:T(8,128)(2,1)S(1)}, u32[]{:S(2)}, u32[]{:S(2)}) collective-permute-start(bf16[16,512]{1,0:T(8,128)(2,1)S(1)} %get-tuple-element.66), channel_id=1, source_target_pairs={{0,7},{1,6},{2,5},{3,4},{4,3},{5,2},{6,1},{7,0},{8,15},{9,14},{10,... | collective-permute-start | bytes 49160 | tf_op jit(solution)/shard_map/ppermute | solution.py:339
  26.8 0.9 %slice-start = ((bf16[256,768]{1,0:T(8,128)(2,1)}), bf16[256,512]{1,0:T(8,128)(2,1)S(1)}, s32[]{:S(2)}) async-start(bf16[256,768]{1,0:T(8,128)(2,1)} %col_proj.1), calls=%async_computation.3 | async-start | bytes 524288 | tf_op jit(solution)/shard_map/slice | solution.py:382
  26.8 4.9 %copy-start.2 = (bf16[256,256]{1,0:T(8,128)(2,1)S(1)}, bf16[256,256]{1,0:T(8,128)(2,1)}, u32[]{:S(2)}) copy-start(bf16[256,256]{1,0:T(8,128)(2,1)} %col_out.1) | copy-start | bytes 393220
  27.7 4.0 %copy-start = (bf16[256,768]{1,0:T(8,128)(2,1)S(1)}, bf16[256,768]{1,0:T(8,128)(2,1)}, u32[]{:S(2)}) copy-start(bf16[256,768]{1,0:T(8,128)(2,1)} %col_proj.1) | copy-start | bytes 1179652
  27.7 4.0 %copy-start.1 = (bf16[256,256]{1,0:T(8,128)(2,1)S(1)}, bf16[256,256]{1,0:T(8,128)(2,1)}, u32[]{:S(2)}) copy-start(bf16[256,256]{1,0:T(8,128)(2,1)} %row_out.1) | copy-start | bytes 393220
  35.9 3.2 %collective-permute-start.10 = (bf16[128,1280]{1,0:T(8,128)(2,1)S(1)}, bf16[128,1280]{1,0:T(8,128)(2,1)S(1)}, u32[]{:S(2)}, u32[]{:S(2)}) collective-permute-start(bf16[128,1280]{1,0:T(8,128)(2,1)S(1)} %get-tuple-element.74), channel_id=1, source_target_pairs={{0,1},{1,0},{2,3},{3,2},{4,5},{5,4},{6,7},{7,6},{8,9},{9,8},{10,11... | collective-permute-start | bytes 983048 | tf_op jit(solution)/shard_map/ppermute | solution.py:339
  36.1 10.4 %all-to-all-start.1 = ((bf16[32,8,128]{2,1,0:T(8,128)(2,1)}), bf16[32,8,128]{2,1,0:T(8,128)(2,1)S(1)}, u32[]{:S(2)}, u32[]{:S(2)}) async-start(bf16[32,8,128]{2,1,0:T(8,128)(2,1)} %get-tuple-element.68), calls=%async_computation.1 | async-start | bytes 131072 | tf_op jit(solution)/shard_map/all_to_all | solution.py:334
  39.1 10.9 %copy-start.7 = (bf16[512,64]{1,0:T(8,128)(2,1)S(1)}, bf16[512,64]{1,0:T(8,128)(2,1)}, u32[]{:S(2)}) copy-start(bf16[512,64]{1,0:T(8,128)(2,1)} %copy-done.6) | copy-start | bytes 196612
  46.5 6.9 %collective-permute-start.12 = (bf16[32,1280]{1,0:T(8,128)(2,1)S(1)}, bf16[32,1280]{1,0:T(8,128)(2,1)S(1)}, u32[]{:S(2)}, u32[]{:S(2)}) collective-permute-start(bf16[32,1280]{1,0:T(8,128)(2,1)S(1)} %get-tuple-element.88), channel_id=1, source_target_pairs={{0,8},{8,0},{16,24},{24,16},{1,9},{9,1},{17,25},{25,17},{2,10},{10... | collective-permute-start | bytes 245768 | tf_op jit(solution)/shard_map/ppermute | solution.py:339
  47.2 6.3 %collective-permute-start.13 = (bf16[32,1280]{1,0:T(8,128)(2,1)S(1)}, bf16[32,1280]{1,0:T(8,128)(2,1)S(1)}, u32[]{:S(2)}, u32[]{:S(2)}) collective-permute-start(bf16[32,1280]{1,0:T(8,128)(2,1)S(1)} %get-tuple-element.89), channel_id=1, source_target_pairs={{0,16},{8,24},{16,0},{24,8},{1,17},{9,25},{17,1},{25,9},{2,18},{10... | collective-permute-start | bytes 245768 | tf_op jit(solution)/shard_map/ppermute | solution.py:339
  47.8 5.6 %collective-permute-start.14 = (bf16[32,1280]{1,0:T(8,128)(2,1)S(1)}, bf16[32,1280]{1,0:T(8,128)(2,1)S(1)}, u32[]{:S(2)}, u32[]{:S(2)}) collective-permute-start(bf16[32,1280]{1,0:T(8,128)(2,1)S(1)} %get-tuple-element.90), channel_id=1, source_target_pairs={{0,24},{8,16},{16,8},{24,0},{1,25},{9,17},{17,9},{25,1},{2,26},{10... | collective-permute-start | bytes 245768 | tf_op jit(solution)/shard_map/ppermute | solution.py:339
  52.1 1.3 %collective-permute-start.11 = (bf16[96,256]{1,0:T(8,128)(2,1)S(1)}, bf16[96,256]{1,0:T(8,128)(2,1)S(1)}, u32[]{:S(2)}, u32[]{:S(2)}) collective-permute-start(bf16[96,256]{1,0:T(8,128)(2,1)S(1)} %get-tuple-element.86), channel_id=1, source_target_pairs={{0,1},{1,0},{2,3},{3,2},{4,5},{5,4},{6,7},{7,6},{8,9},{9,8},{10,11... | collective-permute-start | bytes 147464 | tf_op jit(solution)/shard_map/ppermute | solution.py:339
  53.5 13.9 %collective-permute-start.17 = (bf16[256,256]{1,0:T(8,128)(2,1)S(1)}, bf16[256,256]{1,0:T(8,128)(2,1)S(1)}, u32[]{:S(2)}, u32[]{:S(2)}) collective-permute-start(bf16[256,256]{1,0:T(8,128)(2,1)S(1)} %shard_map.142.refs_0_), channel_id=1, source_target_pairs={{0,6},{1,7},{2,4},{3,5},{4,2},{5,3},{6,0},{7,1},{8,14},{9,15},{10,... | collective-permute-start | bytes 393224 | tf_op jit(solution)/shard_map/ppermute | solution.py:339
  54.4 13.1 %collective-permute-start.16 = (bf16[256,256]{1,0:T(8,128)(2,1)S(1)}, bf16[256,256]{1,0:T(8,128)(2,1)S(1)}, u32[]{:S(2)}, u32[]{:S(2)}) collective-permute-start(bf16[256,256]{1,0:T(8,128)(2,1)S(1)} %shard_map.142.refs_0_), channel_id=1, source_target_pairs={{0,4},{1,5},{2,6},{3,7},{4,0},{5,1},{6,2},{7,3},{8,12},{9,13},{10,... | collective-permute-start | bytes 393224 | tf_op jit(solution)/shard_map/ppermute | solution.py:339
  55.5 12.0 %collective-permute-start.15 = (bf16[256,256]{1,0:T(8,128)(2,1)S(1)}, bf16[256,256]{1,0:T(8,128)(2,1)S(1)}, u32[]{:S(2)}, u32[]{:S(2)}) collective-permute-start(bf16[256,256]{1,0:T(8,128)(2,1)S(1)} %shard_map.142.refs_0_), channel_id=1, source_target_pairs={{0,2},{1,3},{2,0},{3,1},{4,6},{5,7},{6,4},{7,5},{8,10},{9,11},{10,... | collective-permute-start | bytes 393224 | tf_op jit(solution)/shard_map/ppermute | solution.py:339
  58.0 4.3 %collective-permute-start.18 = (bf16[128,192]{1,0:T(8,128)(2,1)S(1)}, bf16[128,192]{1,0:T(8,128)(2,1)S(1)}, u32[]{:S(2)}, u32[]{:S(2)}) collective-permute-start(bf16[128,192]{1,0:T(8,128)(2,1)S(1)} %get-tuple-element.92), channel_id=1, source_target_pairs={{0,8},{8,0},{16,24},{24,16},{1,9},{9,1},{17,25},{25,17},{2,10},{10... | collective-permute-start | bytes 147464 | tf_op jit(solution)/shard_map/ppermute | solution.py:339
  59.2 4.9 %collective-permute-start.19 = (bf16[128,192]{1,0:T(8,128)(2,1)S(1)}, bf16[128,192]{1,0:T(8,128)(2,1)S(1)}, u32[]{:S(2)}, u32[]{:S(2)}) collective-permute-start(bf16[128,192]{1,0:T(8,128)(2,1)S(1)} %get-tuple-element.93), channel_id=1, source_target_pairs={{0,16},{8,24},{16,0},{24,8},{1,17},{9,25},{17,1},{25,9},{2,18},{10... | collective-permute-start | bytes 147464 | tf_op jit(solution)/shard_map/ppermute | solution.py:339
  62.2 5.2 %collective-permute-start.20 = (bf16[128,192]{1,0:T(8,128)(2,1)S(1)}, bf16[128,192]{1,0:T(8,128)(2,1)S(1)}, u32[]{:S(2)}, u32[]{:S(2)}) collective-permute-start(bf16[128,192]{1,0:T(8,128)(2,1)S(1)} %get-tuple-element.94), channel_id=1, source_target_pairs={{0,24},{8,16},{16,8},{24,0},{1,25},{9,17},{17,9},{25,1},{2,26},{10... | collective-permute-start | bytes 147464 | tf_op jit(solution)/shard_map/ppermute | solution.py:339
  67.6 13.4 %all-to-all-start.2 = ((bf16[8,16,512]{2,1,0:T(8,128)(2,1)}), bf16[8,16,512]{2,1,0:T(8,128)(2,1)S(1)}, u32[]{:S(2)}, u32[]{:S(2)}) async-start(bf16[8,16,512]{2,1,0:T(8,128)(2,1)} %get-tuple-element.99.og), calls=%async_computation.2 | async-start | bytes 262144 | tf_op jit(solution)/shard_map/all_to_all | solution.py:334
  70.9 7.3 %collective-permute-start.26 = (bf16[256,256]{1,0:T(8,128)(2,1)S(1)}, bf16[256,256]{1,0:T(8,128)(2,1)S(1)}, u32[]{:S(2)}, u32[]{:S(2)}) collective-permute-start(bf16[256,256]{1,0:T(8,128)(2,1)S(1)} %shard_map.143.refs_0_), channel_id=1, source_target_pairs={{0,24},{8,16},{16,8},{24,0},{1,25},{9,17},{17,9},{25,1},{2,26},{10... | collective-permute-start | bytes 393224 | tf_op jit(solution)/shard_map/ppermute | solution.py:339
  72.8 7.6 %collective-permute-start.24 = (bf16[256,256]{1,0:T(8,128)(2,1)S(1)}, bf16[256,256]{1,0:T(8,128)(2,1)S(1)}, u32[]{:S(2)}, u32[]{:S(2)}) collective-permute-start(bf16[256,256]{1,0:T(8,128)(2,1)S(1)} %shard_map.143.refs_0_), channel_id=1, source_target_pairs={{0,16},{8,24},{16,0},{24,8},{1,17},{9,25},{17,1},{25,9},{2,18},{10... | collective-permute-start | bytes 393224 | tf_op jit(solution)/shard_map/ppermute | solution.py:339
  73.7 6.8 %collective-permute-start.22 = (bf16[256,256]{1,0:T(8,128)(2,1)S(1)}, bf16[256,256]{1,0:T(8,128)(2,1)S(1)}, u32[]{:S(2)}, u32[]{:S(2)}) collective-permute-start(bf16[256,256]{1,0:T(8,128)(2,1)S(1)} %shard_map.143.refs_0_), channel_id=1, source_target_pairs={{0,8},{8,0},{16,24},{24,16},{1,9},{9,1},{17,25},{25,17},{2,10},{10... | collective-permute-start | bytes 393224 | tf_op jit(solution)/shard_map/ppermute | solution.py:339
  74.5 7.4 %collective-permute-start.21 = (bf16[256,256]{1,0:T(8,128)(2,1)S(1)}, bf16[256,256]{1,0:T(8,128)(2,1)S(1)}, u32[]{:S(2)}, u32[]{:S(2)}) collective-permute-start(bf16[256,256]{1,0:T(8,128)(2,1)S(1)} %shard_map.143.refs_0_), channel_id=1, source_target_pairs={{0,1},{1,0},{2,3},{3,2},{4,5},{5,4},{6,7},{7,6},{8,9},{9,8},{10,11... | collective-permute-start | bytes 393224 | tf_op jit(solution)/shard_map/ppermute | solution.py:339
  78.2 3.7 %collective-permute-start.27 = (bf16[256,256]{1,0:T(8,128)(2,1)S(1)}, bf16[256,256]{1,0:T(8,128)(2,1)S(1)}, u32[]{:S(2)}, u32[]{:S(2)}) collective-permute-start(bf16[256,256]{1,0:T(8,128)(2,1)S(1)} %collective-permute-done.26.refs_6_), channel_id=1, source_target_pairs={{0,1},{1,0},{2,3},{3,2},{4,5},{5,4},{6,7},{7,6},{8,9},{9,8},{10,11... | collective-permute-start | bytes 393224 | tf_op jit(solution)/shard_map/ppermute | solution.py:339
  80.5 1.5 %collective-permute-start.25 = (bf16[256,256]{1,0:T(8,128)(2,1)S(1)}, bf16[256,256]{1,0:T(8,128)(2,1)S(1)}, u32[]{:S(2)}, u32[]{:S(2)}) collective-permute-start(bf16[256,256]{1,0:T(8,128)(2,1)S(1)} %collective-permute-done.24.refs_4_), channel_id=1, source_target_pairs={{0,1},{1,0},{2,3},{3,2},{4,5},{5,4},{6,7},{7,6},{8,9},{9,8},{10,11... | collective-permute-start | bytes 393224 | tf_op jit(solution)/shard_map/ppermute | solution.py:339
  80.5 1.5 %collective-permute-start.23 = (bf16[256,256]{1,0:T(8,128)(2,1)S(1)}, bf16[256,256]{1,0:T(8,128)(2,1)S(1)}, u32[]{:S(2)}, u32[]{:S(2)}) collective-permute-start(bf16[256,256]{1,0:T(8,128)(2,1)S(1)} %collective-permute-done.22.refs_2_), channel_id=1, source_target_pairs={{0,1},{1,0},{2,3},{3,2},{4,5},{5,4},{6,7},{7,6},{8,9},{9,8},{10,11... | collective-permute-start | bytes 393224 | tf_op jit(solution)/shard_map/ppermute | solution.py:339

commit v4 on v3

--- a/solution.py
+++ b/solution.py
@@ -15,7 +15,7 @@
 BF16 = jnp.bfloat16
 VMEM = pl.BlockSpec(memory_space=pltpu.VMEM)
 SMEM = pl.BlockSpec(memory_space=pltpu.SMEM)
-PARAMS = pltpu.CompilerParams(vmem_limit_bytes=48 << 20)
+PARAMS = pltpu.CompilerParams(vmem_limit_bytes=24 << 20)
 
 
 def mm(a, b):
@@ -76,8 +76,8 @@
     return joined.reshape(-1, width).astype(BF16)
 
 
-def call(body, outs, *operands, scalars=0, scratch=(), us=1):
-    cost = pl.CostEstimate(flops=us * 10**9, bytes_accessed=us * 3_600_000, transcendentals=0)
+def call(body, outs, *operands, scalars=0, scratch=(), us=0):
+    cost = pl.CostEstimate(flops=us * 10**9 + 1, bytes_accessed=us * 3_600_000 + 1, transcendentals=0)
     return pl.pallas_call(
         body,
         out_shape=[jax.ShapeDtypeStruct(s, d) for s, d in outs],
@@ -131,19 +131,14 @@
         att_out[pl.ds((me ^ b) * haps, haps)] = pack_block(att[b * rows : (b + 1) * rows], haps)
 
 
-def split_inputs(haps, hap, feats, cot, *outs):
-    rows, width = feats.shape
-    per = rows // haps
-    for m in range(haps):
-        here = pl.ds(pl.multiple_of((hap[0] ^ m) * per, per), per)
-        outs[m][:, :width] = feats[here, :]
-        outs[m][:, width:] = cot[here, :]
-
-
-def column_step(sites, haps, hap, at, row_out, gain, col_proj, kv_t_w, col_out, *refs):
-    ga_out, og_out, n_out, gp_out, at_out, cot_out, xc = refs[haps:]
-    for m in range(haps):
-        xc[hap[0] ^ m] = refs[m][...]
+def join_inputs(feats, cot, out):
+    haps, per, width = out.shape
+    joined = jnp.concatenate([feats[...].astype(F32), cot[...].astype(F32)], axis=1)
+    out[...] = joined.reshape(haps, per, width).astype(BF16)
+
+
+def column_step(sites, haps, xc, at, row_out, gain, col_proj, kv_t_w, col_out, *refs):
+    ga_out, og_out, n_out, gp_out, at_out, cot_out = refs
     width = row_out.shape[0]
     heads = width // HEAD_DIM
     group = width // sites
@@ -369,12 +364,8 @@
 
     pieces = [feats] + [swapped(feats, "site", k) for k in range(1, sites)]
     gains = jnp.stack([row_gain, column_norm_gain])
-    xcs = call(
-        functools.partial(split_inputs, haps),
-        [((per, 2 * width), BF16)] * haps,
-        hap, feats, cot, scalars=1,
-    )
-    xcs = [xcs[0]] + [swapped(xcs[m], "hap", m) for m in range(1, haps)]
+    (xc,) = call(join_inputs, [((haps, per, 2 * width), BF16)], feats, cot)
+    xc = exchange(xc, "hap")
     w_all = jnp.transpose(row_proj.reshape(width, 3, sites, group), (2, 1, 3, 0)).reshape(
         sites, 3 * group, width
     )
@@ -391,8 +382,9 @@
             ((group, total), BF16),
             ((total, width), BF16),
         ],
-        idx, link_pattern, *pieces, gains, w_t, scalars=2, us=3,
-    )
+        idx, link_pattern, *pieces, gains, w_t, scalars=2, us=20,
+    )
+    att, xc = lax.optimization_barrier((att, xc))
     at = exchange(att, both_axes)
     ga, og, col_normed, col_gp, col_att_t, cot = call(
         functools.partial(column_step, sites, haps),
@@ -404,30 +396,29 @@
             ((width, rows), BF16),
             ((rows, width), BF16),
         ],
-        hap, at, row_out, gains, col_proj, kv_t_w, col_out, *xcs, scalars=1, us=3,
-        scratch=[pltpu.VMEM((haps, per, 2 * width), BF16)],
+        xc, at, row_out, gains, col_proj, kv_t_w, col_out,
     )
     g_in = exchange(ga, both_axes)
     half = width // 2
     col_keep, col_send = call(
         functools.partial(column_weights, sites, haps),
         [((half, 5 * width), BF16)] * 2,
-        core, cot, at, og, col_normed, col_gp, col_att_t, scalars=1, us=2,
+        core, cot, at, og, col_normed, col_gp, col_att_t, scalars=1, us=20,
         scratch=[pltpu.VMEM((width, 5 * width), BF16)],
     )
     col_got = swapped(col_send, "hap", 1)
     cols = call(
         functools.partial(column_split, sites),
         [((half // sites, 5 * width), BF16)] * sites,
-        idx, col_keep, col_got, scalars=1,
+        idx, col_keep, col_got, scalars=1, us=5,
         scratch=[pltpu.VMEM((half, 5 * width), BF16)],
     )
-    g_in, cols = lax.optimization_barrier((g_in, cols))
+    g_in, _ = lax.optimization_barrier((g_in, cols))
     cols = [cols[0]] + [swapped(cols[k], "site", k) for k in range(1, sites)]
     *gps, row_keep, row_send = call(
         functools.partial(row_backward, sites, haps),
         [((rows, 3 * group), BF16)] * sites + [((3 * group // 2, width), BF16)] * 2,
-        idx, core, g_in, prob, q, val, key_t, normed, scalars=2, us=3,
+        idx, core, g_in, prob, q, val, key_t, normed, scalars=2,
         scratch=[
             pltpu.VMEM((total, group), BF16),
             pltpu.VMEM((total, total), BF16),
@@ -441,7 +432,8 @@
     gps = [gps[0]] + [swapped(gps[k], "site", k) for k in range(1, sites)]
     parts, gps = lax.optimization_barrier((parts, gps))
     (mine,) = call(weights_sum, [((depth, width), BF16)], *parts)
-    og, _ = lax.optimization_barrier((og, mine))
+    mine_swapped = swapped(mine, "hap", 1)
+    og, _ = lax.optimization_barrier((og, mine_swapped))
     og_in = exchange(og, "hap")
     out, grad = call(
         functools.partial(row_finish, sites),
@@ -449,7 +441,7 @@
         idx, feats, gains, w_all, og_in, *gps, scalars=1,
     )
     full = [mine] + [swapped(mine, "site", k) for k in range(1, sites)]
-    full = [x for piece in full for x in (piece, swapped(piece, "hap", 1))]
+    full = [mine, mine_swapped] + [x for p in full[1:] for x in (p, swapped(p, "hap", 1))]
     rp, ro, cp, co = call(
         functools.partial(weights_finish, sites),
         [((width, 3 * width), F32), ((width, width), F32)] * 2,

time: 83.9 us -> 79.3 us (0.945)
  starting transfers between devices: 40.8 us -> 35 us
  local copies, waits for them, and re-layouts: 3.65 us -> 6.03 us
  waiting for transfers between devices: 25.8 us -> 23.9 us
    ppermute x28 -> x21, starting transfers between devices: 29.5 us -> 19.4 us  [swapped(): return lax.ppermute(value, axis, [(i, i ^ by) for i in range(length)])]
    ppermute x28 -> x21, waiting for transfers between devices: 18.6 us -> 11.6 us  [swapped(): return lax.ppermute(value, axis, [(i, i ^ by) for i in range(length)])]
    all_to_all x3 -> x4, waiting for transfers between devices: 7.18 us -> 12.3 us  [exchange(): return lax.all_to_all(value, axis, 0, 0, tiled=True)]
    all_to_all x3 -> x4, starting transfers between devices: 11.3 us -> 15.6 us  [exchange(): return lax.all_to_all(value, axis, 0, 0, tiled=True)]
    unnamed x22 -> x26, local copies, waits for them, and re-layouts: 2.66 us -> 5.04 us
  transfers between devices with their start and end apart: 31 -> 25, of which waited for: 12 -> 12; matrix products, arithmetic and copies ran while one was open for 2% -> 0% of each run, Pallas kernels for 4% -> 10%
where the time goes in v4:
time: 79.3 us; the launch traced here: 78.7 us
  starting transfers between devices  35 us (44%)
  waiting for transfers between devices  23.9 us (30%)
  Pallas kernels  12.9 us (16%)
  local copies, waits for them, and re-layouts  6.03 us (8%)
  between operations  0.85 us (1%)
    ppermute x21, starting transfers between devices, swapped(): return lax.ppermute(value, axis, [(i, i ^ by) for i in range(length)])  19.4 us
    all_to_all x4, starting transfers between devices, exchange(): return lax.all_to_all(value, axis, 0, 0, tiled=True)  15.6 us
    pallas_call x10, Pallas kernels, call(): pl.pallas_call(body, out_shape=[jax.ShapeDtypeStruct(s, d) for s, d in ou...  12.9 us
    all_to_all x4, waiting for transfers between devices, exchange(): return lax.all_to_all(value, axis, 0, 0, tiled=True)  12.3 us
    ppermute x21, waiting for transfers between devices, swapped(): return lax.ppermute(value, axis, [(i, i ^ by) for i in range(length)])  11.6 us
    unnamed x26, local copies, waits for them, and re-layouts  5.04 us
  transfers between devices with their start and end apart: 25, of which 12 were waited for; matrix products, arithmetic and copies ran while one was open for 0% of the time, Pallas kernels for 10%

profile of v4, /device:TPU:0, one launch (start us, length us, event | category | flops | bytes accessed | tf_op | source)
XLA Modules:
  0.0 78.7 jit_solution(12226990378914673823)
XLA Ops:
  0.6 4.0 %collective-permute-start.2 = (bf16[128,256]{1,0:T(8,128)(2,1)}, bf16[128,256]{1,0:T(8,128)(2,1)S(1)}, u32[]{:S(2)}, u32[]{:S(2)}) collective-permute-start(bf16[128,256]{1,0:T(8,128)(2,1)} %bitcast.18), channel_id=1, source_target_pairs={{0,24},{8,16},{16,8},{24,0},{1,25},{9,17},{17,9},{25,1},{2,26},{10... | collective-permute-start | bytes 196616 | tf_op jit(solution)/shard_map/ppermute | solution.py:334
  4.6 0.5 collective-permute-start.1
  5.1 0.1 collective-permute-start
  5.2 0.9 %copy-done.1 = bf16[128,1,256]{2,0,1:T(8,128)(2,1)S(1)} copy-done((bf16[128,1,256]{2,0,1:T(8,128)(2,1)S(1)}, bf16[128,1,256]{2,0,1:T(8,128)(2,1)}, u32[]{:S(2)}) %copy-start.1) | copy-done | bytes 65560
  6.1 0.8 %copy-done.5 = bf16[128,1,256]{2,0,1:T(8,128)(2,1)S(1)} copy-done((bf16[128,1,256]{2,0,1:T(8,128)(2,1)S(1)}, bf16[128,1,256]{2,0,1:T(8,128)(2,1)}, u32[]{:S(2)}) %copy-start.5) | copy-done | bytes 65560
  7.0 0.7 shard_map.137
  7.6 5.3 %all-to-all-start = ((bf16[8,16,512]{2,1,0:T(8,128)(2,1)}), bf16[8,16,512]{2,1,0:T(8,128)(2,1)S(1)}, u32[]{:S(2)}, u32[]{:S(2)}) async-start(bf16[8,16,512]{2,1,0:T(8,128)(2,1)} %shard_map.137), calls=%async_computation | async-start | bytes 262144 | tf_op jit(solution)/shard_map/all_to_all | solution.py:329
  12.9 0.2 copy.17
  13.2 0.6 copy-done.11
  14.0 0.6 copy-done.6
  14.5 3.3 %shard_map.136 = (bf16[32,8,128]{2,1,0:T(8,128)(2,1)}, bf16[2,512,512]{2,1,0:T(8,128)(2,1)S(1)}, bf16[512,64]{1,0:T(8,128)(2,1)S(1)}, bf16[512,64]{1,0:T(8,128)(...) custom-call(s32[1]{0:T(128)} %bitcast.idx, s32[4,4]{1,0:T(4,128)S(1)} %copy-done.6, ...), custom_call_target="tpu_custom_call" | custom-call | flops 20000000000 | bytes 72000000 | tf_op jit(solution)/shard_map/pallas_call | solution.py:81
  17.8 1.9 %all-to-all-done.xc = bf16[8,16,512]{2,1,0:T(8,128)(2,1)S(1)} async-done(((bf16[8,16,512]{2,1,0:T(8,128)(2,1)}), bf16[8,16,512]{2,1,0:T(8,128)(2,1)S(1)}, u32[]{:S(2)}, u32[]{:S(2)}) %all-to-all-start) | async-done | bytes 131104 | tf_op jit(solution)/shard_map/all_to_all | solution.py:329
  19.7 4.2 %all-to-all-start.1 = ((bf16[32,8,128]{2,1,0:T(8,128)(2,1)}), bf16[32,8,128]{2,1,0:T(8,128)(2,1)S(1)}, u32[]{:S(2)}, u32[]{:S(2)}) async-start(bf16[32,8,128]{2,1,0:T(8,128)(2,1)} %get-tuple-element.50), calls=%async_computation.1 | async-start | bytes 131072 | tf_op jit(solution)/shard_map/all_to_all | solution.py:329
  23.9 0.9 %slice-done = bf16[256,512]{1,0:T(8,128)(2,1)S(1)} async-done(((bf16[256,768]{1,0:T(8,128)(2,1)}), bf16[256,512]{1,0:T(8,128)(2,1)S(1)}, s32[]{:S(2)}) %slice-start) | async-done | bytes 262168 | tf_op jit(solution)/shard_map/slice | solution.py:373
  25.0 6.3 %all-to-all-done.1.at = bf16[32,8,128]{2,1,0:T(8,128)(2,1)S(1)} async-done(((bf16[32,8,128]{2,1,0:T(8,128)(2,1)}), bf16[32,8,128]{2,1,0:T(8,128)(2,1)S(1)}, u32[]{:S(2)}, u32[]{:S(2)}) %all-to-all-start.1) | async-done | bytes 65568 | tf_op jit(solution)/shard_map/all_to_all | solution.py:329
  31.3 2.9 %shard_map.138 = (bf16[32,8,128]{2,1,0:T(8,128)(2,1)}, bf16[8,16,512]{2,1,0:T(8,128)(2,1)}, bf16[128,256]{1,0:T(8,128)(2,1)S(1)}, bf16[128,768]{1,0:T(8,128)(2,1...) custom-call(bf16[8,16,512]{2,1,0:T(8,128)(2,1)S(1)} %all-to-all-done.xc, ...), custom_call_target="tpu_custom_call" | custom-call | flops 1 | bytes 1 | tf_op jit(solution)/shard_map/pallas_call | solution.py:81
  34.1 1.3 %shard_map.139 = (bf16[128,1280]{1,0:T(8,128)(2,1)S(1)}, bf16[128,1280]{1,0:T(8,128)(2,1)S(1)}) custom-call(s32[1]{0:T(128)S(6)} %select_n.12.core, bf16[128,256]{1,0:T(8,128)(2,1)S(1)} %get-tuple-element.53.cot, bf16[32,8,128]{2,1,0:T(8,128)(2,1)S(1)} %all-to-all-done.1.at, bf16[8,16,512]{2,1,0:T(8,128)(2,1)} %get-tuple-element.79.og, ...), custom_call_target="tpu_custom_call" | custom-call | flops 20000000000 | bytes 72000000 | tf_op jit(solution)/shard_map/pallas_call | solution.py:81
  35.5 0.7 copy-done.7
  36.3 2.6 %all-to-all-start.2 = ((bf16[32,8,128]{2,1,0:T(8,128)(2,1)}), bf16[32,8,128]{2,1,0:T(8,128)(2,1)S(1)}, u32[]{:S(2)}, u32[]{:S(2)}) async-start(bf16[32,8,128]{2,1,0:T(8,128)(2,1)} %get-tuple-element.52), calls=%async_computation.2 | async-start | bytes 131072 | tf_op jit(solution)/shard_map/all_to_all | solution.py:329
  38.9 1.0 %copy-done.8 = bf16[128,1280]{1,0:T(8,128)(2,1)S(1)} copy-done((bf16[128,1280]{1,0:T(8,128)(2,1)S(1)}, bf16[128,1280]{1,0:T(8,128)(2,1)}, u32[]{:S(2)}) %copy-start.8) | copy-done | bytes 327704
  39.9 0.2 shard_map.140
  40.0 1.7 %collective-permute-start.5 = (bf16[32,1280]{1,0:T(8,128)(2,1)S(1)}, bf16[32,1280]{1,0:T(8,128)(2,1)S(1)}, u32[]{:S(2)}, u32[]{:S(2)}) collective-permute-start(bf16[32,1280]{1,0:T(8,128)(2,1)S(1)} %get-tuple-element.60), channel_id=1, source_target_pairs={{0,8},{8,0},{16,24},{24,16},{1,9},{9,1},{17,25},{25,17},{2,10},{10... | collective-permute-start | bytes 245768 | tf_op jit(solution)/shard_map/ppermute | solution.py:334
  41.7 1.5 %collective-permute-start.6 = (bf16[32,1280]{1,0:T(8,128)(2,1)S(1)}, bf16[32,1280]{1,0:T(8,128)(2,1)S(1)}, u32[]{:S(2)}, u32[]{:S(2)}) collective-permute-start(bf16[32,1280]{1,0:T(8,128)(2,1)S(1)} %get-tuple-element.61), channel_id=1, source_target_pairs={{0,16},{8,24},{16,0},{24,8},{1,17},{9,25},{17,1},{25,9},{2,18},{10... | collective-permute-start | bytes 245768 | tf_op jit(solution)/shard_map/ppermute | solution.py:334
  43.2 0.4 collective-permute-start.7
  43.6 2.7 %all-to-all-done.2.g_in = bf16[32,8,128]{2,1,0:T(8,128)(2,1)S(1)} async-done(((bf16[32,8,128]{2,1,0:T(8,128)(2,1)}), bf16[32,8,128]{2,1,0:T(8,128)(2,1)S(1)}, u32[]{:S(2)}, u32[]{:S(2)}) %all-to-all-start.2) | async-done | bytes 65568 | tf_op jit(solution)/shard_map/all_to_all | solution.py:329
  46.3 2.1 %shard_map.141 = (bf16[128,192]{1,0:T(8,128)(2,1)S(1)}, bf16[128,192]{1,0:T(8,128)(2,1)S(1)}, bf16[128,192]{1,0:T(8,128)(2,1)S(1)}, bf16[128,192]{1,0:T(8,128)(2...) custom-call(s32[1]{0:T(128)} %bitcast.idx, s32[1]{0:T(128)S(6)} %select_n.12.core, ...), custom_call_target="tpu_custom_call" | custom-call | flops 1 | bytes 1 | tf_op jit(solution)/shard_map/pallas_call | solution.py:81
  48.4 0.2 collective-permute-start.4
  48.5 1.1 %collective-permute-done.4.row_got = bf16[96,256]{1,0:T(8,128)(2,1)S(1)} collective-permute-done((bf16[96,256]{1,0:T(8,128)(2,1)S(1)}, bf16[96,256]{1,0:T(8,128)(2,1)S(1)}, u32[]{:S(2)}, u32[]{:S(2)}) %collective-permute-start.4) | collective-permute-done | bytes 49184 | tf_op jit(solution)/shard_map/ppermute | solution.py:334
  49.7 2.4 %collective-permute-start.10 = (bf16[256,256]{1,0:T(8,128)(2,1)S(1)}, bf16[256,256]{1,0:T(8,128)(2,1)S(1)}, u32[]{:S(2)}, u32[]{:S(2)}) collective-permute-start(bf16[256,256]{1,0:T(8,128)(2,1)S(1)} %shard_map.142.refs_0_), channel_id=1, source_target_pairs={{0,6},{1,7},{2,4},{3,5},{4,2},{5,3},{6,0},{7,1},{8,14},{9,15},{10,... | collective-permute-start | bytes 393224 | tf_op jit(solution)/shard_map/ppermute | solution.py:334
  52.2 2.0 %collective-permute-start.8 = (bf16[256,256]{1,0:T(8,128)(2,1)S(1)}, bf16[256,256]{1,0:T(8,128)(2,1)S(1)}, u32[]{:S(2)}, u32[]{:S(2)}) collective-permute-start(bf16[256,256]{1,0:T(8,128)(2,1)S(1)} %shard_map.142.refs_0_), channel_id=1, source_target_pairs={{0,2},{1,3},{2,0},{3,1},{4,6},{5,7},{6,4},{7,5},{8,10},{9,11},{10,... | collective-permute-start | bytes 393224 | tf_op jit(solution)/shard_map/ppermute | solution.py:334
  54.2 0.7 collective-permute-start.11
  54.9 0.6 collective-permute-start.12
  55.5 2.9 %collective-permute-done.11.refs_1_ = bf16[128,192]{1,0:T(8,128)(2,1)S(1)} collective-permute-done((bf16[128,192]{1,0:T(8,128)(2,1)S(1)}, bf16[128,192]{1,0:T(8,128)(2,1)S(1)}, u32[]{:S(2)}, u32[]{:S(2)}) %collective-permute-start.11) | collective-permute-done | bytes 49184 | tf_op jit(solution)/shard_map/ppermute | solution.py:334
  58.5 0.8 collective-permute-start.13
  59.2 4.4 %collective-permute-done.13.refs_3_ = bf16[128,192]{1,0:T(8,128)(2,1)S(1)} collective-permute-done((bf16[128,192]{1,0:T(8,128)(2,1)S(1)}, bf16[128,192]{1,0:T(8,128)(2,1)S(1)}, u32[]{:S(2)}, u32[]{:S(2)}) %collective-permute-start.13) | collective-permute-done | bytes 49184 | tf_op jit(solution)/shard_map/ppermute | solution.py:334
  63.9 1.0 %collective-permute-start.19 = (bf16[256,256]{1,0:T(8,128)(2,1)S(1)}, bf16[256,256]{1,0:T(8,128)(2,1)S(1)}, u32[]{:S(2)}, u32[]{:S(2)}) collective-permute-start(bf16[256,256]{1,0:T(8,128)(2,1)S(1)} %shard_map.143.refs_0_), channel_id=1, source_target_pairs={{0,24},{8,16},{16,8},{24,0},{1,25},{9,17},{17,9},{25,1},{2,26},{10... | collective-permute-start | bytes 393224 | tf_op jit(solution)/shard_map/ppermute | solution.py:334
  64.9 1.1 %collective-permute-start.17 = (bf16[256,256]{1,0:T(8,128)(2,1)S(1)}, bf16[256,256]{1,0:T(8,128)(2,1)S(1)}, u32[]{:S(2)}, u32[]{:S(2)}) collective-permute-start(bf16[256,256]{1,0:T(8,128)(2,1)S(1)} %shard_map.143.refs_0_), channel_id=1, source_target_pairs={{0,16},{8,24},{16,0},{24,8},{1,17},{9,25},{17,1},{25,9},{2,18},{10... | collective-permute-start | bytes 393224 | tf_op jit(solution)/shard_map/ppermute | solution.py:334
  66.0 1.4 %collective-permute-start.15 = (bf16[256,256]{1,0:T(8,128)(2,1)S(1)}, bf16[256,256]{1,0:T(8,128)(2,1)S(1)}, u32[]{:S(2)}, u32[]{:S(2)}) collective-permute-start(bf16[256,256]{1,0:T(8,128)(2,1)S(1)} %shard_map.143.refs_0_), channel_id=1, source_target_pairs={{0,8},{8,0},{16,24},{24,16},{1,9},{9,1},{17,25},{25,17},{2,10},{10... | collective-permute-start | bytes 393224 | tf_op jit(solution)/shard_map/ppermute | solution.py:334
  67.4 3.6 %all-to-all-start.3 = ((bf16[8,16,512]{2,1,0:T(8,128)(2,1)}), bf16[8,16,512]{2,1,0:T(8,128)(2,1)S(1)}, u32[]{:S(2)}, u32[]{:S(2)}) async-start(bf16[8,16,512]{2,1,0:T(8,128)(2,1)} %get-tuple-element.79.og), calls=%async_computation.3 | async-start | bytes 262144 | tf_op jit(solution)/shard_map/all_to_all | solution.py:329
  71.0 0.2 collective-permute-done.19.refs_6_
  71.2 0.3 collective-permute-start.20
  71.5 1.8 %collective-permute-done.17.refs_4_ = bf16[256,256]{1,0:T(8,128)(2,1)S(1)} collective-permute-done((bf16[256,256]{1,0:T(8,128)(2,1)S(1)}, bf16[256,256]{1,0:T(8,128)(2,1)S(1)}, u32[]{:S(2)}, u32[]{:S(2)}) %collective-permute-start.17) | collective-permute-done | bytes 131104 | tf_op jit(solution)/shard_map/ppermute | solution.py:334
  73.3 0.5 collective-permute-start.16
  73.8 0.8 %collective-permute-done.18.refs_5_ = bf16[256,256]{1,0:T(8,128)(2,1)S(1)} collective-permute-done((bf16[256,256]{1,0:T(8,128)(2,1)S(1)}, bf16[256,256]{1,0:T(8,128)(2,1)S(1)}, u32[]{:S(2)}, u32[]{:S(2)}) %collective-permute-start.18) | collective-permute-done | bytes 131104 | tf_op jit(solution)/shard_map/ppermute | solution.py:334
  74.6 0.2 collective-permute-done.16.refs_3_
  74.8 1.5 %shard_map.145 = (f32[256,768]{1,0:T(8,128)}, f32[256,256]{1,0:T(8,128)}, f32[256,768]{1,0:T(8,128)}, f32[256,256]{1,0:T(8,128)}) custom-call(s32[1]{0:T(128)} %bitcast.idx, s32[1]{0:T(128)S(6)} %select_n.12.core, bf16[256,256]{1,0:T(8,128)(2,1)S(1)} %shard_map.143.refs_0_, bf16[256,256]{1,0:T(8,128)(2,1)S(1)} %collective-permute-done.14.refs_1_, ...), custom_call_target="tpu_custom_call" | custom-call | flops 1 | bytes 1 | tf_op jit(solution)/shard_map/pallas_call | solution.py:81
  76.3 1.5 %all-to-all-done.3.og = bf16[8,16,512]{2,1,0:T(8,128)(2,1)S(1)} async-done(((bf16[8,16,512]{2,1,0:T(8,128)(2,1)}), bf16[8,16,512]{2,1,0:T(8,128)(2,1)S(1)}, u32[]{:S(2)}, u32[]{:S(2)}) %all-to-all-start.3) | async-done | bytes 131104 | tf_op jit(solution)/shard_map/all_to_all | solution.py:329
  77.8 0.9 %shard_map.144 = (bf16[128,256]{1,0:T(8,128)(2,1)}, bf16[128,256]{1,0:T(8,128)(2,1)}) custom-call(s32[1]{0:T(128)} %bitcast.idx, bf16[128,256]{1,0:T(8,128)(2,1)S(1)} %bitcast.23, f32[2,256]{1,0:T(2,128)S(1)} %pad_maximum_fusion.refs_4_.gain, bf16[4,192,256]{2,1,0:T(8,128)(2,1)S(1)} %bitcast.16, bf16[8,16,512]{2,1,0:T(8,128)(2,1)S(1)} %all-to-all-done.3.og, ...), custom_call_target="tpu_custom_call" | custom-call | flops 1 | bytes 1 | tf_op jit(solution)/shard_map/pallas_call | solution.py:81
  (43 shorter events, 0.8 us)
Async XLA Ops:
  0.6 13.2 %collective-permute-start.2 = (bf16[128,256]{1,0:T(8,128)(2,1)}, bf16[128,256]{1,0:T(8,128)(2,1)S(1)}, u32[]{:S(2)}, u32[]{:S(2)}) collective-permute-start(bf16[128,256]{1,0:T(8,128)(2,1)} %bitcast.18), channel_id=1, source_target_pairs={{0,24},{8,16},{16,8},{24,0},{1,25},{9,17},{17,9},{25,1},{2,26},{10... | collective-permute-start | bytes 196616 | tf_op jit(solution)/shard_map/ppermute | solution.py:334
  4.6 9.3 %collective-permute-start.1 = (bf16[128,256]{1,0:T(8,128)(2,1)}, bf16[128,256]{1,0:T(8,128)(2,1)S(1)}, u32[]{:S(2)}, u32[]{:S(2)}) collective-permute-start(bf16[128,256]{1,0:T(8,128)(2,1)} %bitcast.19), channel_id=1, source_target_pairs={{0,16},{8,24},{16,0},{24,8},{1,17},{9,25},{17,1},{25,9},{2,18},{10... | collective-permute-start | bytes 196616 | tf_op jit(solution)/shard_map/ppermute | solution.py:334
  5.1 8.8 %collective-permute-start = (bf16[128,256]{1,0:T(8,128)(2,1)}, bf16[128,256]{1,0:T(8,128)(2,1)S(1)}, u32[]{:S(2)}, u32[]{:S(2)}) collective-permute-start(bf16[128,256]{1,0:T(8,128)(2,1)} %bitcast.20), channel_id=1, source_target_pairs={{0,8},{8,0},{16,24},{24,16},{1,9},{9,1},{17,25},{25,17},{2,10},{10... | collective-permute-start | bytes 196616 | tf_op jit(solution)/shard_map/ppermute | solution.py:334
  5.2 0.9 %copy-start.1 = (bf16[128,1,256]{2,0,1:T(8,128)(2,1)S(1)}, bf16[128,1,256]{2,0,1:T(8,128)(2,1)}, u32[]{:S(2)}) copy-start(bf16[128,1,256]{2,0,1:T(8,128)(2,1)} %param.9) | copy-start | bytes 196612
  6.1 0.8 %copy-start.5 = (bf16[128,1,256]{2,0,1:T(8,128)(2,1)S(1)}, bf16[128,1,256]{2,0,1:T(8,128)(2,1)}, u32[]{:S(2)}) copy-start(bf16[128,1,256]{2,0,1:T(8,128)(2,1)} %param.17) | copy-start | bytes 196612
  7.0 5.9 %copy-start.9 = (bf16[256,768]{1,0:T(8,128)(2,1)S(1)}, bf16[256,768]{1,0:T(8,128)(2,1)}, u32[]{:S(2)}) copy-start(bf16[256,768]{1,0:T(8,128)(2,1)} %param.12) | copy-start | bytes 1179652
  7.6 12.1 %all-to-all-start = ((bf16[8,16,512]{2,1,0:T(8,128)(2,1)}), bf16[8,16,512]{2,1,0:T(8,128)(2,1)S(1)}, u32[]{:S(2)}, u32[]{:S(2)}) async-start(bf16[8,16,512]{2,1,0:T(8,128)(2,1)} %shard_map.137), calls=%async_computation | async-start | bytes 262144 | tf_op jit(solution)/shard_map/all_to_all | solution.py:329
  13.1 0.7 copy-start.11
  13.1 0.8 %copy-start.2 = (bf16[128,1,256]{2,0,1:T(8,128)(2,1)S(1)}, bf16[128,1,256]{2,0,1:T(8,128)(2,1)}, u32[]{:S(2)}) copy-start(bf16[128,1,256]{2,0,1:T(8,128)(2,1)} %param.9) | copy-start | bytes 196612
  13.2 0.7 copy-start.10
  13.8 0.7 copy-start.6
  14.5 16.7 %copy-start.4 = (bf16[256,256]{1,0:T(8,128)(2,1)S(1)}, bf16[256,256]{1,0:T(8,128)(2,1)}, u32[]{:S(2)}) copy-start(bf16[256,256]{1,0:T(8,128)(2,1)} %col_out.1) | copy-start | bytes 393220
  19.7 11.6 %all-to-all-start.1 = ((bf16[32,8,128]{2,1,0:T(8,128)(2,1)}), bf16[32,8,128]{2,1,0:T(8,128)(2,1)S(1)}, u32[]{:S(2)}, u32[]{:S(2)}) async-start(bf16[32,8,128]{2,1,0:T(8,128)(2,1)} %get-tuple-element.50), calls=%async_computation.1 | async-start | bytes 131072 | tf_op jit(solution)/shard_map/all_to_all | solution.py:329
  23.9 1.0 %slice-start = ((bf16[256,768]{1,0:T(8,128)(2,1)}), bf16[256,512]{1,0:T(8,128)(2,1)S(1)}, s32[]{:S(2)}) async-start(bf16[256,768]{1,0:T(8,128)(2,1)} %col_proj.1), calls=%async_computation.4 | async-start | bytes 524288 | tf_op jit(solution)/shard_map/slice | solution.py:373
  24.8 6.4 %copy-start = (bf16[256,768]{1,0:T(8,128)(2,1)S(1)}, bf16[256,768]{1,0:T(8,128)(2,1)}, u32[]{:S(2)}) copy-start(bf16[256,768]{1,0:T(8,128)(2,1)} %col_proj.1) | copy-start | bytes 1179652
  24.8 6.4 %copy-start.3 = (bf16[256,256]{1,0:T(8,128)(2,1)S(1)}, bf16[256,256]{1,0:T(8,128)(2,1)}, u32[]{:S(2)}) copy-start(bf16[256,256]{1,0:T(8,128)(2,1)} %row_out.1) | copy-start | bytes 393220
  35.4 0.7 copy-start.7
  36.2 2.7 %collective-permute-start.3 = (bf16[128,1280]{1,0:T(8,128)(2,1)S(1)}, bf16[128,1280]{1,0:T(8,128)(2,1)S(1)}, u32[]{:S(2)}, u32[]{:S(2)}) collective-permute-start(bf16[128,1280]{1,0:T(8,128)(2,1)S(1)} %get-tuple-element.58), channel_id=1, source_target_pairs={{0,1},{1,0},{2,3},{3,2},{4,5},{5,4},{6,7},{7,6},{8,9},{9,8},{10,11... | collective-permute-start | bytes 983048 | tf_op jit(solution)/shard_map/ppermute | solution.py:334
  36.3 10.0 %all-to-all-start.2 = ((bf16[32,8,128]{2,1,0:T(8,128)(2,1)}), bf16[32,8,128]{2,1,0:T(8,128)(2,1)S(1)}, u32[]{:S(2)}, u32[]{:S(2)}) async-start(bf16[32,8,128]{2,1,0:T(8,128)(2,1)} %get-tuple-element.52), calls=%async_computation.2 | async-start | bytes 131072 | tf_op jit(solution)/shard_map/all_to_all | solution.py:329
  38.9 1.0 %copy-start.8 = (bf16[128,1280]{1,0:T(8,128)(2,1)S(1)}, bf16[128,1280]{1,0:T(8,128)(2,1)}, u32[]{:S(2)}) copy-start(bf16[128,1280]{1,0:T(8,128)(2,1)} %copy-done.7) | copy-start | bytes 983044
  40.0 9.6 %collective-permute-start.5 = (bf16[32,1280]{1,0:T(8,128)(2,1)S(1)}, bf16[32,1280]{1,0:T(8,128)(2,1)S(1)}, u32[]{:S(2)}, u32[]{:S(2)}) collective-permute-start(bf16[32,1280]{1,0:T(8,128)(2,1)S(1)} %get-tuple-element.60), channel_id=1, source_target_pairs={{0,8},{8,0},{16,24},{24,16},{1,9},{9,1},{17,25},{25,17},{2,10},{10... | collective-permute-start | bytes 245768 | tf_op jit(solution)/shard_map/ppermute | solution.py:334
  41.7 7.9 %collective-permute-start.6 = (bf16[32,1280]{1,0:T(8,128)(2,1)S(1)}, bf16[32,1280]{1,0:T(8,128)(2,1)S(1)}, u32[]{:S(2)}, u32[]{:S(2)}) collective-permute-start(bf16[32,1280]{1,0:T(8,128)(2,1)S(1)} %get-tuple-element.61), channel_id=1, source_target_pairs={{0,16},{8,24},{16,0},{24,8},{1,17},{9,25},{17,1},{25,9},{2,18},{10... | collective-permute-start | bytes 245768 | tf_op jit(solution)/shard_map/ppermute | solution.py:334
  43.2 6.4 %collective-permute-start.7 = (bf16[32,1280]{1,0:T(8,128)(2,1)S(1)}, bf16[32,1280]{1,0:T(8,128)(2,1)S(1)}, u32[]{:S(2)}, u32[]{:S(2)}) collective-permute-start(bf16[32,1280]{1,0:T(8,128)(2,1)S(1)} %get-tuple-element.62), channel_id=1, source_target_pairs={{0,24},{8,16},{16,8},{24,0},{1,25},{9,17},{17,9},{25,1},{2,26},{10... | collective-permute-start | bytes 245768 | tf_op jit(solution)/shard_map/ppermute | solution.py:334
  48.4 1.3 %collective-permute-start.4 = (bf16[96,256]{1,0:T(8,128)(2,1)S(1)}, bf16[96,256]{1,0:T(8,128)(2,1)S(1)}, u32[]{:S(2)}, u32[]{:S(2)}) collective-permute-start(bf16[96,256]{1,0:T(8,128)(2,1)S(1)} %get-tuple-element.70), channel_id=1, source_target_pairs={{0,1},{1,0},{2,3},{3,2},{4,5},{5,4},{6,7},{7,6},{8,9},{9,8},{10,11... | collective-permute-start | bytes 147464 | tf_op jit(solution)/shard_map/ppermute | solution.py:334
  49.7 13.9 %collective-permute-start.10 = (bf16[256,256]{1,0:T(8,128)(2,1)S(1)}, bf16[256,256]{1,0:T(8,128)(2,1)S(1)}, u32[]{:S(2)}, u32[]{:S(2)}) collective-permute-start(bf16[256,256]{1,0:T(8,128)(2,1)S(1)} %shard_map.142.refs_0_), channel_id=1, source_target_pairs={{0,6},{1,7},{2,4},{3,5},{4,2},{5,3},{6,0},{7,1},{8,14},{9,15},{10,... | collective-permute-start | bytes 393224 | tf_op jit(solution)/shard_map/ppermute | solution.py:334
  52.2 11.6 %collective-permute-start.9 = (bf16[256,256]{1,0:T(8,128)(2,1)S(1)}, bf16[256,256]{1,0:T(8,128)(2,1)S(1)}, u32[]{:S(2)}, u32[]{:S(2)}) collective-permute-start(bf16[256,256]{1,0:T(8,128)(2,1)S(1)} %shard_map.142.refs_0_), channel_id=1, source_target_pairs={{0,4},{1,5},{2,6},{3,7},{4,0},{5,1},{6,2},{7,3},{8,12},{9,13},{10,... | collective-permute-start | bytes 393224 | tf_op jit(solution)/shard_map/ppermute | solution.py:334
  52.2 11.6 %collective-permute-start.8 = (bf16[256,256]{1,0:T(8,128)(2,1)S(1)}, bf16[256,256]{1,0:T(8,128)(2,1)S(1)}, u32[]{:S(2)}, u32[]{:S(2)}) collective-permute-start(bf16[256,256]{1,0:T(8,128)(2,1)S(1)} %shard_map.142.refs_0_), channel_id=1, source_target_pairs={{0,2},{1,3},{2,0},{3,1},{4,6},{5,7},{6,4},{7,5},{8,10},{9,11},{10,... | collective-permute-start | bytes 393224 | tf_op jit(solution)/shard_map/ppermute | solution.py:334
  54.2 4.3 %collective-permute-start.11 = (bf16[128,192]{1,0:T(8,128)(2,1)S(1)}, bf16[128,192]{1,0:T(8,128)(2,1)S(1)}, u32[]{:S(2)}, u32[]{:S(2)}) collective-permute-start(bf16[128,192]{1,0:T(8,128)(2,1)S(1)} %get-tuple-element.72), channel_id=1, source_target_pairs={{0,8},{8,0},{16,24},{24,16},{1,9},{9,1},{17,25},{25,17},{2,10},{10... | collective-permute-start | bytes 147464 | tf_op jit(solution)/shard_map/ppermute | solution.py:334
  54.9 4.3 %collective-permute-start.12 = (bf16[128,192]{1,0:T(8,128)(2,1)S(1)}, bf16[128,192]{1,0:T(8,128)(2,1)S(1)}, u32[]{:S(2)}, u32[]{:S(2)}) collective-permute-start(bf16[128,192]{1,0:T(8,128)(2,1)S(1)} %get-tuple-element.73), channel_id=1, source_target_pairs={{0,16},{8,24},{16,0},{24,8},{1,17},{9,25},{17,1},{25,9},{2,18},{10... | collective-permute-start | bytes 147464 | tf_op jit(solution)/shard_map/ppermute | solution.py:334
  58.5 5.2 %collective-permute-start.13 = (bf16[128,192]{1,0:T(8,128)(2,1)S(1)}, bf16[128,192]{1,0:T(8,128)(2,1)S(1)}, u32[]{:S(2)}, u32[]{:S(2)}) collective-permute-start(bf16[128,192]{1,0:T(8,128)(2,1)S(1)} %get-tuple-element.74), channel_id=1, source_target_pairs={{0,24},{8,16},{16,8},{24,0},{1,25},{9,17},{17,9},{25,1},{2,26},{10... | collective-permute-start | bytes 147464 | tf_op jit(solution)/shard_map/ppermute | solution.py:334
  63.8 3.6 %collective-permute-start.14 = (bf16[256,256]{1,0:T(8,128)(2,1)S(1)}, bf16[256,256]{1,0:T(8,128)(2,1)S(1)}, u32[]{:S(2)}, u32[]{:S(2)}) collective-permute-start(bf16[256,256]{1,0:T(8,128)(2,1)S(1)} %shard_map.143.refs_0_), channel_id=1, source_target_pairs={{0,1},{1,0},{2,3},{3,2},{4,5},{5,4},{6,7},{7,6},{8,9},{9,8},{10,11... | collective-permute-start | bytes 393224 | tf_op jit(solution)/shard_map/ppermute | solution.py:334
  63.9 7.3 %collective-permute-start.19 = (bf16[256,256]{1,0:T(8,128)(2,1)S(1)}, bf16[256,256]{1,0:T(8,128)(2,1)S(1)}, u32[]{:S(2)}, u32[]{:S(2)}) collective-permute-start(bf16[256,256]{1,0:T(8,128)(2,1)S(1)} %shard_map.143.refs_0_), channel_id=1, source_target_pairs={{0,24},{8,16},{16,8},{24,0},{1,25},{9,17},{17,9},{25,1},{2,26},{10... | collective-permute-start | bytes 393224 | tf_op jit(solution)/shard_map/ppermute | solution.py:334
  64.9 8.4 %collective-permute-start.17 = (bf16[256,256]{1,0:T(8,128)(2,1)S(1)}, bf16[256,256]{1,0:T(8,128)(2,1)S(1)}, u32[]{:S(2)}, u32[]{:S(2)}) collective-permute-start(bf16[256,256]{1,0:T(8,128)(2,1)S(1)} %shard_map.143.refs_0_), channel_id=1, source_target_pairs={{0,16},{8,24},{16,0},{24,8},{1,17},{9,25},{17,1},{25,9},{2,18},{10... | collective-permute-start | bytes 393224 | tf_op jit(solution)/shard_map/ppermute | solution.py:334
  66.0 7.2 %collective-permute-start.15 = (bf16[256,256]{1,0:T(8,128)(2,1)S(1)}, bf16[256,256]{1,0:T(8,128)(2,1)S(1)}, u32[]{:S(2)}, u32[]{:S(2)}) collective-permute-start(bf16[256,256]{1,0:T(8,128)(2,1)S(1)} %shard_map.143.refs_0_), channel_id=1, source_target_pairs={{0,8},{8,0},{16,24},{24,16},{1,9},{9,1},{17,25},{25,17},{2,10},{10... | collective-permute-start | bytes 393224 | tf_op jit(solution)/shard_map/ppermute | solution.py:334
  67.4 10.3 %all-to-all-start.3 = ((bf16[8,16,512]{2,1,0:T(8,128)(2,1)}), bf16[8,16,512]{2,1,0:T(8,128)(2,1)S(1)}, u32[]{:S(2)}, u32[]{:S(2)}) async-start(bf16[8,16,512]{2,1,0:T(8,128)(2,1)} %get-tuple-element.79.og), calls=%async_computation.3 | async-start | bytes 262144 | tf_op jit(solution)/shard_map/all_to_all | solution.py:329
  71.2 2.6 %collective-permute-start.20 = (bf16[256,256]{1,0:T(8,128)(2,1)S(1)}, bf16[256,256]{1,0:T(8,128)(2,1)S(1)}, u32[]{:S(2)}, u32[]{:S(2)}) collective-permute-start(bf16[256,256]{1,0:T(8,128)(2,1)S(1)} %collective-permute-done.19.refs_6_), channel_id=1, source_target_pairs={{0,1},{1,0},{2,3},{3,2},{4,5},{5,4},{6,7},{7,6},{8,9},{9,8},{10,11... | collective-permute-start | bytes 393224 | tf_op jit(solution)/shard_map/ppermute | solution.py:334
  73.3 1.3 %collective-permute-start.18 = (bf16[256,256]{1,0:T(8,128)(2,1)S(1)}, bf16[256,256]{1,0:T(8,128)(2,1)S(1)}, u32[]{:S(2)}, u32[]{:S(2)}) collective-permute-start(bf16[256,256]{1,0:T(8,128)(2,1)S(1)} %collective-permute-done.17.refs_4_), channel_id=1, source_target_pairs={{0,1},{1,0},{2,3},{3,2},{4,5},{5,4},{6,7},{7,6},{8,9},{9,8},{10,11... | collective-permute-start | bytes 393224 | tf_op jit(solution)/shard_map/ppermute | solution.py:334
  73.3 1.5 %collective-permute-start.16 = (bf16[256,256]{1,0:T(8,128)(2,1)S(1)}, bf16[256,256]{1,0:T(8,128)(2,1)S(1)}, u32[]{:S(2)}, u32[]{:S(2)}) collective-permute-start(bf16[256,256]{1,0:T(8,128)(2,1)S(1)} %collective-permute-done.15.refs_2_), channel_id=1, source_target_pairs={{0,1},{1,0},{2,3},{3,2},{4,5},{5,4},{6,7},{7,6},{8,9},{9,8},{10,11... | collective-permute-start | bytes 393224 | tf_op jit(solution)/shard_map/ppermute | solution.py:334

commit v5 on v4

--- a/solution.py
+++ b/solution.py
@@ -14,6 +14,7 @@
 F32 = jnp.float32
 BF16 = jnp.bfloat16
 VMEM = pl.BlockSpec(memory_space=pltpu.VMEM)
+HBM = pl.BlockSpec(memory_space=pltpu.HBM)
 SMEM = pl.BlockSpec(memory_space=pltpu.SMEM)
 PARAMS = pltpu.CompilerParams(vmem_limit_bytes=24 << 20)
 
@@ -76,13 +77,14 @@
     return joined.reshape(-1, width).astype(BF16)
 
 
-def call(body, outs, *operands, scalars=0, scratch=(), us=0):
+def call(body, outs, *operands, scalars=0, scratch=(), us=0, far=0):
     cost = pl.CostEstimate(flops=us * 10**9 + 1, bytes_accessed=us * 3_600_000 + 1, transcendentals=0)
     return pl.pallas_call(
         body,
-        out_shape=[jax.ShapeDtypeStruct(s, d) for s, d in outs],
+        out_shape=[jax.ShapeDtypeStruct(s, d) for s, d in outs[: len(outs) - far]]
+        + [pltpu.HBM(s, d) for s, d in outs[len(outs) - far :]],
         in_specs=[SMEM] * scalars + [VMEM] * (len(operands) - scalars),
-        out_specs=[VMEM] * len(outs),
+        out_specs=[VMEM] * (len(outs) - far) + [HBM] * far,
         scratch_shapes=list(scratch),
         compiler_params=PARAMS,
         cost_estimate=cost,
@@ -131,14 +133,35 @@
         att_out[pl.ds((me ^ b) * haps, haps)] = pack_block(att[b * rows : (b + 1) * rows], haps)
 
 
-def join_inputs(feats, cot, out):
-    haps, per, width = out.shape
+def join_inputs(haps, hap, feats, cot, keep, send, both):
+    count, per, width = both.shape
     joined = jnp.concatenate([feats[...].astype(F32), cot[...].astype(F32)], axis=1)
-    out[...] = joined.reshape(haps, per, width).astype(BF16)
-
-
-def column_step(sites, haps, xc, at, row_out, gain, col_proj, kv_t_w, col_out, *refs):
-    ga_out, og_out, n_out, gp_out, at_out, cot_out = refs
+    both[...] = joined.reshape(count, per, width).astype(BF16)
+    for m in range(haps // 2):
+        keep[m] = both[hap[0] ^ (2 * m)]
+        send[m] = both[hap[0] ^ (2 * m + 1)]
+
+
+def relay_inputs(keep, got, *outs):
+    for m, out in enumerate(outs):
+        out[0] = keep[m]
+        out[1] = got[m]
+
+
+def column_step(sites, haps, hap, at, row_out, gain, col_proj, kv_t_w, col_out, *refs):
+    ga_out, og_out, *far, xc = refs[haps // 2 : haps // 2 + 7]
+    near, sems = refs[haps // 2 + 7 : -1], refs[-1]
+    copies = [
+        pltpu.make_async_copy(near[j], far[j], sems.at[j]) for j in range(len(near))
+    ]
+
+    def save(j, value):
+        near[j][...] = value
+        copies[j].start()
+
+    for m in range(haps // 2):
+        xc[hap[0] ^ (2 * m)] = refs[m][0]
+        xc[hap[0] ^ (2 * m + 1)] = refs[m][1]
     width = row_out.shape[0]
     heads = width // HEAD_DIM
     group = width // sites
@@ -147,7 +170,7 @@
     per = rows // haps
     cot_f = xc_all[:, width:]
     cot = cot_f.astype(BF16)
-    cot_out[...] = cot
+    save(3, cot)
     hid = xc_all[:, :width]
     for i in range(sites):
         a_i = unpack_block(at[i * haps : (i + 1) * haps], group)
@@ -156,7 +179,7 @@
     grad_att = mm_nt(cot, col_out[...]).astype(BF16)
     xhat, rstd = norm_parts(hid)
     normed = (xhat * gain[1:2, :]).astype(BF16)
-    n_out[...] = normed
+    save(0, normed)
     packed = mm(normed, col_proj[...]).astype(BF16)
     q = packed[:, :width]
     key = packed[:, width : 2 * width]
@@ -185,7 +208,7 @@
         ds16.append(ds_h)
         dq_t.append(mm(kv_t[:width, :][cols], ds_h))
     att_t = jnp.concatenate(att_t, axis=0)
-    at_out[...] = att_t.astype(BF16)
+    save(2, att_t.astype(BF16))
     att = jnp.transpose(att_t).astype(BF16)
     out = hid + mm(att, col_out[...])
     dv_all = mm(jnp.concatenate(prob16, axis=0), grad_att)
@@ -198,7 +221,7 @@
     )
     dq = jnp.transpose(jnp.concatenate(dq_t, axis=0))
     packed_grad = jnp.concatenate([dq * SCALE, dk * SCALE, dv], axis=1).astype(BF16)
-    gp_out[...] = packed_grad
+    save(1, packed_grad)
     grad_normed = mm_nt(packed_grad, col_proj[...])
     grad_hidden = (cot_f + norm_back(xhat, rstd, gain[1:2, :], grad_normed)).astype(BF16)
     for i in range(sites):
@@ -206,9 +229,12 @@
         ga_out[i * haps : (i + 1) * haps] = pack_block(g_i, haps)
     both = jnp.concatenate([out, grad_hidden.astype(F32)], axis=1)
     og_out[...] = both.reshape(haps, per, 2 * width).astype(BF16)
-
-
-def column_weights(sites, haps, core, cot, at, og, normed, gp, att_t, keep, send, both):
+    for copy in copies:
+        copy.wait()
+
+
+def column_weights(sites, haps, core, cot, at, og, normed, gp, att_t, keep, *refs):
+    sends, both = refs[:-1], refs[-1]
     width = normed.shape[1]
     group = width // sites
     half = width // 2
@@ -219,12 +245,16 @@
         a_i = unpack_block(at[i * haps : (i + 1) * haps], group)
         both[i * group : (i + 1) * group, 4 * width :] = mm_tn(a_i, grad_hidden).astype(BF16)
     keep[...] = both[pl.ds(pl.multiple_of(core[0] * half, half), half), :]
-    send[...] = both[pl.ds(pl.multiple_of((1 - core[0]) * half, half), half), :]
-
-
-def column_split(sites, idx, keep, got, *refs):
-    outs, both = refs[:sites], refs[sites]
-    both[...] = (keep[...].astype(F32) + got[...].astype(F32)).astype(BF16)
+    part = half // len(sends)
+    for j, send in enumerate(sends):
+        start = (1 - core[0]) * half + j * part
+        send[...] = both[pl.ds(pl.multiple_of(start, part), part), :]
+
+
+def column_split(sites, idx, keep, *refs):
+    outs, both, gots = refs[-sites - 1 : -1], refs[-1], refs[: -sites - 1]
+    got = jnp.concatenate([g[...].astype(F32) for g in gots], axis=0)
+    both[...] = (keep[...].astype(F32) + got).astype(BF16)
     part = keep.shape[0] // sites
     for k in range(sites):
         outs[k][...] = both[pl.ds(pl.multiple_of((idx[0] ^ k) * part, part), part), :]
@@ -364,8 +394,16 @@
 
     pieces = [feats] + [swapped(feats, "site", k) for k in range(1, sites)]
     gains = jnp.stack([row_gain, column_norm_gain])
-    (xc,) = call(join_inputs, [((haps, per, 2 * width), BF16)], feats, cot)
-    xc = exchange(xc, "hap")
+    keep, send = call(
+        functools.partial(join_inputs, haps),
+        [((haps // 2, per, 2 * width), BF16)] * 2,
+        hap, feats, cot, scalars=1,
+        scratch=[pltpu.VMEM((haps, per, 2 * width), BF16)],
+    )
+    got = swapped(send, "hap", 1)
+    xcs = call(relay_inputs, [((2, per, 2 * width), BF16)] * (haps // 2), keep, got)
+    pieces, _ = lax.optimization_barrier((pieces, xcs))
+    xcs = [xcs[0]] + [swapped(xcs[m], "hap", 2 * m) for m in range(1, haps // 2)]
     w_all = jnp.transpose(row_proj.reshape(width, 3, sites, group), (2, 1, 3, 0)).reshape(
         sites, 3 * group, width
     )
@@ -382,9 +420,8 @@
             ((group, total), BF16),
             ((total, width), BF16),
         ],
-        idx, link_pattern, *pieces, gains, w_t, scalars=2, us=20,
-    )
-    att, xc = lax.optimization_barrier((att, xc))
+        idx, link_pattern, *pieces, gains, w_t, scalars=2, us=3,
+    )
     at = exchange(att, both_axes)
     ga, og, col_normed, col_gp, col_att_t, cot = call(
         functools.partial(column_step, sites, haps),
@@ -396,21 +433,29 @@
             ((width, rows), BF16),
             ((rows, width), BF16),
         ],
-        xc, at, row_out, gains, col_proj, kv_t_w, col_out,
+        hap, at, row_out, gains, col_proj, kv_t_w, col_out, *xcs, scalars=1, far=4,
+        scratch=[
+            pltpu.VMEM((haps, per, 2 * width), BF16),
+            pltpu.VMEM((rows, width), BF16),
+            pltpu.VMEM((rows, 3 * width), BF16),
+            pltpu.VMEM((width, rows), BF16),
+            pltpu.VMEM((rows, width), BF16),
+            pltpu.SemaphoreType.DMA((4,)),
+        ],
     )
     g_in = exchange(ga, both_axes)
     half = width // 2
-    col_keep, col_send = call(
+    col_keep, *col_sends = call(
         functools.partial(column_weights, sites, haps),
-        [((half, 5 * width), BF16)] * 2,
+        [((half, 5 * width), BF16)] + [((half // 4, 5 * width), BF16)] * 4,
         core, cot, at, og, col_normed, col_gp, col_att_t, scalars=1, us=20,
         scratch=[pltpu.VMEM((width, 5 * width), BF16)],
     )
-    col_got = swapped(col_send, "hap", 1)
+    col_got = [swapped(send, "hap", 1) for send in col_sends]
     cols = call(
         functools.partial(column_split, sites),
         [((half // sites, 5 * width), BF16)] * sites,
-        idx, col_keep, col_got, scalars=1, us=5,
+        idx, col_keep, *col_got, scalars=1, us=0,
         scratch=[pltpu.VMEM((half, 5 * width), BF16)],
     )
     g_in, _ = lax.optimization_barrier((g_in, cols))
@@ -430,11 +475,11 @@
     (joined,) = call(weights_join, [((depth, width), BF16)], row_keep, row_got, *cols)
     parts = [joined] + [swapped(joined, "hap", 2 * m) for m in range(1, haps // 2)]
     gps = [gps[0]] + [swapped(gps[k], "site", k) for k in range(1, sites)]
+    og, _ = lax.optimization_barrier((og, gps[1]))
+    og_in = exchange(og, "hap")
     parts, gps = lax.optimization_barrier((parts, gps))
     (mine,) = call(weights_sum, [((depth, width), BF16)], *parts)
     mine_swapped = swapped(mine, "hap", 1)
-    og, _ = lax.optimization_barrier((og, mine_swapped))
-    og_in = exchange(og, "hap")
     out, grad = call(
         functools.partial(row_finish, sites),
         [((rows, width), BF16)] * 2,

time: 79.3 us -> 82.2 us (1.037)
  starting transfers between devices: 35 us -> 39.2 us
  waiting for transfers between devices: 23.9 us -> 20.8 us
  local copies, waits for them, and re-layouts: 6.03 us -> 7.15 us
    all_to_all x4 -> x3, waiting for transfers between devices: 12.3 us -> 5.69 us  [exchange(): return lax.all_to_all(value, axis, 0, 0, tiled=True)]
    ppermute x21 -> x28, starting transfers between devices: 19.4 us -> 25.5 us  [swapped(): return lax.ppermute(value, axis, [(i, i ^ by) for i in range(length)])]
    ppermute x21 -> x28, waiting for transfers between devices: 11.6 us -> 15.1 us  [swapped(): return lax.ppermute(value, axis, [(i, i ^ by) for i in range(length)])]
    all_to_all x4 -> x3, starting transfers between devices: 15.6 us -> 13.8 us  [exchange(): return lax.all_to_all(value, axis, 0, 0, tiled=True)]
    unnamed x26 -> x28, local copies, waits for them, and re-layouts: 5.04 us -> 6.16 us
    pallas_call x10 -> x11, Pallas kernels: 12.9 us -> 13.5 us  [call(): pl.pallas_call(body, out_shape=[jax.ShapeDtypeStruct(s, d) for s, d in ou...]
  transfers between devices with their start and end apart: 25 -> 31, of which waited for: 12 -> 12; matrix products, arithmetic and copies ran while one was open for 0% -> 2% of each run, Pallas kernels for 10% -> 6%
where the time goes in v5:
time: 82.2 us; the launch traced here: 81.6 us
  starting transfers between devices  39.2 us (48%)
  waiting for transfers between devices  20.8 us (25%)
  Pallas kernels  13.5 us (16%)
  local copies, waits for them, and re-layouts  7.15 us (9%)
  between operations  0.9 us (1%)
    ppermute x28, starting transfers between devices, swapped(): return lax.ppermute(value, axis, [(i, i ^ by) for i in range(length)])  25.5 us
    ppermute x28, waiting for transfers between devices, swapped(): return lax.ppermute(value, axis, [(i, i ^ by) for i in range(length)])  15.1 us
    all_to_all x3, starting transfers between devices, exchange(): return lax.all_to_all(value, axis, 0, 0, tiled=True)  13.8 us
    pallas_call x11, Pallas kernels, call(): pl.pallas_call(body, out_shape=[jax.ShapeDtypeStruct(s, d) for s, d in ou...  13.5 us
    unnamed x28, local copies, waits for them, and re-layouts  6.16 us
    all_to_all x3, waiting for transfers between devices, exchange(): return lax.all_to_all(value, axis, 0, 0, tiled=True)  5.69 us
  transfers between devices with their start and end apart: 31, of which 12 were waited for; matrix products, arithmetic and copies ran while one was open for 2% of the time, Pallas kernels for 6%

profile of v5, /device:TPU:0, one launch (start us, length us, event | category | flops | bytes accessed | tf_op | source)
XLA Modules:
  0.0 81.6 jit_solution(7234145935825282796)
XLA Ops:
  0.6 4.0 %collective-permute-start.2 = (bf16[128,256]{1,0:T(8,128)(2,1)}, bf16[128,256]{1,0:T(8,128)(2,1)S(1)}, u32[]{:S(2)}, u32[]{:S(2)}) collective-permute-start(bf16[128,256]{1,0:T(8,128)(2,1)} %bitcast.18), channel_id=1, source_target_pairs={{0,24},{8,16},{16,8},{24,0},{1,25},{9,17},{17,9},{25,1},{2,26},{10... | collective-permute-start | bytes 196616 | tf_op jit(solution)/shard_map/ppermute | solution.py:364
  4.6 0.5 collective-permute-start.1
  5.2 0.9 %copy-done.1 = bf16[128,1,256]{2,0,1:T(8,128)(2,1)S(1)} copy-done((bf16[128,1,256]{2,0,1:T(8,128)(2,1)S(1)}, bf16[128,1,256]{2,0,1:T(8,128)(2,1)}, u32[]{:S(2)}) %copy-start.1) | copy-done | bytes 65560
  6.1 0.8 %copy-done.5 = bf16[128,1,256]{2,0,1:T(8,128)(2,1)S(1)} copy-done((bf16[128,1,256]{2,0,1:T(8,128)(2,1)S(1)}, bf16[128,1,256]{2,0,1:T(8,128)(2,1)}, u32[]{:S(2)}) %copy-start.5) | copy-done | bytes 65560
  7.1 1.2 %copy.17 = bf16[256,768]{0,1:T(8,128)(2,1)S(1)} copy(bf16[256,768]{1,0:T(8,128)(2,1)} %param.12) | data formatting | bytes 786432 | tf_op args[3]
  8.3 0.6 copy-done.12
  9.0 0.6 shard_map.137
  9.8 0.5 copy-done.10
  10.3 3.3 %shard_map.138 = (bf16[32,8,128]{2,1,0:T(8,128)(2,1)}, bf16[2,512,512]{2,1,0:T(8,128)(2,1)S(1)}, bf16[512,64]{1,0:T(8,128)(2,1)S(1)}, bf16[512,64]{1,0:T(8,128)(...) custom-call(s32[1]{0:T(128)} %bitcast.idx, s32[4,4]{1,0:T(4,128)S(1)} %copy-done.10, ...), custom_call_target="tpu_custom_call" | custom-call | flops 3000000000 | bytes 10800001 | tf_op jit(solution)/shard_map/pallas_call | solution.py:82
  13.6 6.3 %all-to-all-start = ((bf16[32,8,128]{2,1,0:T(8,128)(2,1)}), bf16[32,8,128]{2,1,0:T(8,128)(2,1)S(1)}, u32[]{:S(2)}, u32[]{:S(2)}) async-start(bf16[32,8,128]{2,1,0:T(8,128)(2,1)} %get-tuple-element.69), calls=%async_computation | async-start | bytes 131072 | tf_op jit(solution)/shard_map/all_to_all | solution.py:359
  19.9 1.8 %collective-permute-start.4 = (bf16[2,16,512]{2,1,0:T(8,128)(2,1)}, bf16[2,16,512]{2,1,0:T(8,128)(2,1)S(1)}, u32[]{:S(2)}, u32[]{:S(2)}) collective-permute-start(bf16[2,16,512]{2,1,0:T(8,128)(2,1)} %get-tuple-element.62), channel_id=1, source_target_pairs={{0,2},{1,3},{2,0},{3,1},{4,6},{5,7},{6,4},{7,5},{8,10},{9,11},{10,... | collective-permute-start | bytes 98312 | tf_op jit(solution)/shard_map/ppermute | solution.py:364
  21.8 2.4 %collective-permute-start.5 = (bf16[2,16,512]{2,1,0:T(8,128)(2,1)S(1)}, bf16[2,16,512]{2,1,0:T(8,128)(2,1)S(1)}, u32[]{:S(2)}, u32[]{:S(2)}) collective-permute-start(bf16[2,16,512]{2,1,0:T(8,128)(2,1)S(1)} %get-tuple-element.63), channel_id=1, source_target_pairs={{0,4},{1,5},{2,6},{3,7},{4,0},{5,1},{6,2},{7,3},{8,12},{9,13},{10,... | collective-permute-start | bytes 98312 | tf_op jit(solution)/shard_map/ppermute | solution.py:364
  24.4 0.9 %slice-done = bf16[256,512]{1,0:T(8,128)(2,1)S(1)} async-done(((bf16[256,768]{1,0:T(8,128)(2,1)}), bf16[256,512]{1,0:T(8,128)(2,1)S(1)}, s32[]{:S(2)}) %slice-start) | async-done | bytes 262168 | tf_op jit(solution)/shard_map/slice | solution.py:411
  25.5 1.9 %collective-permute-done.5.refs_2_ = bf16[2,16,512]{2,1,0:T(8,128)(2,1)S(1)} collective-permute-done((bf16[2,16,512]{2,1,0:T(8,128)(2,1)S(1)}, bf16[2,16,512]{2,1,0:T(8,128)(2,1)S(1)}, u32[]{:S(2)}, u32[]{:S(2)}) %collective-permute-start.5) | collective-permute-done | bytes 32800 | tf_op jit(solution)/shard_map/ppermute | solution.py:364
  27.4 2.5 %collective-permute-done.6.refs_3_ = bf16[2,16,512]{2,1,0:T(8,128)(2,1)S(1)} collective-permute-done((bf16[2,16,512]{2,1,0:T(8,128)(2,1)S(1)}, bf16[2,16,512]{2,1,0:T(8,128)(2,1)S(1)}, u32[]{:S(2)}, u32[]{:S(2)}) %collective-permute-start.6) | collective-permute-done | bytes 32800 | tf_op jit(solution)/shard_map/ppermute | solution.py:364
  29.9 3.4 %shard_map.139 = (bf16[32,8,128]{2,1,0:T(8,128)(2,1)}, bf16[8,16,512]{2,1,0:T(8,128)(2,1)}, bf16[128,256]{1,0:T(8,128)(2,1)}, bf16[128,768]{1,0:T(8,128)(2,1)}, ...) custom-call(s32[1]{0:T(128)} %bitcast.7.hap, bf16[32,8,128]{2,1,0:T(8,128)(2,1)S(1)} %all-to-all-done.at, ...), custom_call_target="tpu_custom_call" | custom-call | flops 1 | bytes 1 | tf_op jit(solution)/shard_map/pallas_call | solution.py:82
  33.4 2.8 %all-to-all-start.1 = ((bf16[32,8,128]{2,1,0:T(8,128)(2,1)}), bf16[32,8,128]{2,1,0:T(8,128)(2,1)S(1)}, u32[]{:S(2)}, u32[]{:S(2)}) async-start(bf16[32,8,128]{2,1,0:T(8,128)(2,1)} %get-tuple-element.71), calls=%async_computation.1 | async-start | bytes 131072 | tf_op jit(solution)/shard_map/all_to_all | solution.py:359
  36.2 0.9 %copy-done.6 = bf16[128,768]{1,0:T(8,128)(2,1)S(1)} copy-done((bf16[128,768]{1,0:T(8,128)(2,1)S(1)}, bf16[128,768]{1,0:T(8,128)(2,1)}, u32[]{:S(2)}) %copy-start.6) | copy-done | bytes 196632
  37.1 0.8 %copy-done.9 = bf16[128,256]{1,0:T(8,128)(2,1)S(1)} copy-done((bf16[128,256]{1,0:T(8,128)(2,1)S(1)}, bf16[128,256]{1,0:T(8,128)(2,1)}, u32[]{:S(2)}) %copy-start.9) | copy-done | bytes 65560
  37.9 1.3 %shard_map.140 = (bf16[128,1280]{1,0:T(8,128)(2,1)S(1)}, bf16[32,1280]{1,0:T(8,128)(2,1)S(1)}, bf16[32,1280]{1,0:T(8,128)(2,1)S(1)}, bf16[32,1280]{1,0:T(8,128)(2,1)S(1)}, bf16[32,1280]{1,0:T(8,128)(2,1)S(1)}) custom-call(s32[1]{0:T(128)S(6)} %select_n.12.core, bf16[128,256]{1,0:T(8,128)(2,1)S(1)} %copy-done.9, bf16[32,8,128]{2,1,0:T(8,128)(2,1)S(1)} %all-to-all-done.at, ...), custom_call_target="tpu_custom_call" | custom-call | flops 20000000000 | bytes 72000000 | tf_op jit(solution)/shard_map/pallas_call | solution.py:82
  39.3 0.3 collective-permute-start.7
  39.8 0.3 collective-permute-start.9
  40.3 0.3 collective-permute-done.7.refs_0_
  40.6 0.3 collective-permute-done.8.refs_1_
  41.1 0.3 collective-permute-done.10.refs_3_
  41.5 1.7 %collective-permute-start.13 = (bf16[32,1280]{1,0:T(8,128)(2,1)S(1)}, bf16[32,1280]{1,0:T(8,128)(2,1)S(1)}, u32[]{:S(2)}, u32[]{:S(2)}) collective-permute-start(bf16[32,1280]{1,0:T(8,128)(2,1)S(1)} %get-tuple-element.82), channel_id=1, source_target_pairs={{0,8},{8,0},{16,24},{24,16},{1,9},{9,1},{17,25},{25,17},{2,10},{10... | collective-permute-start | bytes 245768 | tf_op jit(solution)/shard_map/ppermute | solution.py:364
  43.3 1.5 %collective-permute-start.14 = (bf16[32,1280]{1,0:T(8,128)(2,1)S(1)}, bf16[32,1280]{1,0:T(8,128)(2,1)S(1)}, u32[]{:S(2)}, u32[]{:S(2)}) collective-permute-start(bf16[32,1280]{1,0:T(8,128)(2,1)S(1)} %get-tuple-element.83), channel_id=1, source_target_pairs={{0,16},{8,24},{16,0},{24,8},{1,17},{9,25},{17,1},{25,9},{2,18},{10... | collective-permute-start | bytes 245768 | tf_op jit(solution)/shard_map/ppermute | solution.py:364
  44.8 0.4 collective-permute-start.15
  45.1 2.1 %shard_map.142 = (bf16[128,192]{1,0:T(8,128)(2,1)S(1)}, bf16[128,192]{1,0:T(8,128)(2,1)S(1)}, bf16[128,192]{1,0:T(8,128)(2,1)S(1)}, bf16[128,192]{1,0:T(8,128)(2...) custom-call(s32[1]{0:T(128)} %bitcast.idx, s32[1]{0:T(128)S(6)} %select_n.12.core, ...), custom_call_target="tpu_custom_call" | custom-call | flops 1 | bytes 1 | tf_op jit(solution)/shard_map/pallas_call | solution.py:82
  47.3 1.2 %collective-permute-done.14.refs_2_ = bf16[32,1280]{1,0:T(8,128)(2,1)S(1)} collective-permute-done((bf16[32,1280]{1,0:T(8,128)(2,1)S(1)}, bf16[32,1280]{1,0:T(8,128)(2,1)S(1)}, u32[]{:S(2)}, u32[]{:S(2)}) %collective-permute-start.14) | collective-permute-done | bytes 81952 | tf_op jit(solution)/shard_map/ppermute | solution.py:364
  48.5 1.6 %collective-permute-done.15.refs_3_ = bf16[32,1280]{1,0:T(8,128)(2,1)S(1)} collective-permute-done((bf16[32,1280]{1,0:T(8,128)(2,1)S(1)}, bf16[32,1280]{1,0:T(8,128)(2,1)S(1)}, u32[]{:S(2)}, u32[]{:S(2)}) %collective-permute-start.15) | collective-permute-done | bytes 81952 | tf_op jit(solution)/shard_map/ppermute | solution.py:364
  50.2 3.4 %collective-permute-start.18 = (bf16[256,256]{1,0:T(8,128)(2,1)S(1)}, bf16[256,256]{1,0:T(8,128)(2,1)S(1)}, u32[]{:S(2)}, u32[]{:S(2)}) collective-permute-start(bf16[256,256]{1,0:T(8,128)(2,1)S(1)} %shard_map.143.refs_0_), channel_id=1, source_target_pairs={{0,6},{1,7},{2,4},{3,5},{4,2},{5,3},{6,0},{7,1},{8,14},{9,15},{10,... | collective-permute-start | bytes 393224 | tf_op jit(solution)/shard_map/ppermute | solution.py:364
  53.6 1.0 %collective-permute-start.16 = (bf16[256,256]{1,0:T(8,128)(2,1)S(1)}, bf16[256,256]{1,0:T(8,128)(2,1)S(1)}, u32[]{:S(2)}, u32[]{:S(2)}) collective-permute-start(bf16[256,256]{1,0:T(8,128)(2,1)S(1)} %shard_map.143.refs_0_), channel_id=1, source_target_pairs={{0,2},{1,3},{2,0},{3,1},{4,6},{5,7},{6,4},{7,5},{8,10},{9,11},{10,... | collective-permute-start | bytes 393224 | tf_op jit(solution)/shard_map/ppermute | solution.py:364
  54.6 0.6 collective-permute-start.11
  55.2 1.0 %collective-permute-start.19 = (bf16[128,192]{1,0:T(8,128)(2,1)S(1)}, bf16[128,192]{1,0:T(8,128)(2,1)S(1)}, u32[]{:S(2)}, u32[]{:S(2)}) collective-permute-start(bf16[128,192]{1,0:T(8,128)(2,1)S(1)} %get-tuple-element.96), channel_id=1, source_target_pairs={{0,16},{8,24},{16,0},{24,8},{1,17},{9,25},{17,1},{25,9},{2,18},{10... | collective-permute-start | bytes 147464 | tf_op jit(solution)/shard_map/ppermute | solution.py:364
  56.2 2.7 %collective-permute-done.11.refs_1_ = bf16[128,192]{1,0:T(8,128)(2,1)S(1)} collective-permute-done((bf16[128,192]{1,0:T(8,128)(2,1)S(1)}, bf16[128,192]{1,0:T(8,128)(2,1)S(1)}, u32[]{:S(2)}, u32[]{:S(2)}) %collective-permute-start.11) | collective-permute-done | bytes 49184 | tf_op jit(solution)/shard_map/ppermute | solution.py:364
  58.9 1.0 %collective-permute-start.20 = (bf16[128,192]{1,0:T(8,128)(2,1)S(1)}, bf16[128,192]{1,0:T(8,128)(2,1)S(1)}, u32[]{:S(2)}, u32[]{:S(2)}) collective-permute-start(bf16[128,192]{1,0:T(8,128)(2,1)S(1)} %get-tuple-element.97), channel_id=1, source_target_pairs={{0,24},{8,16},{16,8},{24,0},{1,25},{9,17},{17,9},{25,1},{2,26},{10... | collective-permute-start | bytes 147464 | tf_op jit(solution)/shard_map/ppermute | solution.py:364
  59.9 0.3 collective-permute-done.19.refs_2_
  60.1 3.9 %collective-permute-done.20.refs_3_ = bf16[128,192]{1,0:T(8,128)(2,1)S(1)} collective-permute-done((bf16[128,192]{1,0:T(8,128)(2,1)S(1)}, bf16[128,192]{1,0:T(8,128)(2,1)S(1)}, u32[]{:S(2)}, u32[]{:S(2)}) %collective-permute-start.20) | collective-permute-done | bytes 49184 | tf_op jit(solution)/shard_map/ppermute | solution.py:364
  64.1 2.1 %collective-permute-start.26 = (bf16[256,256]{1,0:T(8,128)(2,1)S(1)}, bf16[256,256]{1,0:T(8,128)(2,1)S(1)}, u32[]{:S(2)}, u32[]{:S(2)}) collective-permute-start(bf16[256,256]{1,0:T(8,128)(2,1)S(1)} %shard_map.145.refs_0_), channel_id=1, source_target_pairs={{0,24},{8,16},{16,8},{24,0},{1,25},{9,17},{17,9},{25,1},{2,26},{10... | collective-permute-start | bytes 393224 | tf_op jit(solution)/shard_map/ppermute | solution.py:364
  66.2 0.6 collective-permute-start.24
  66.8 0.9 %collective-permute-start.22 = (bf16[256,256]{1,0:T(8,128)(2,1)S(1)}, bf16[256,256]{1,0:T(8,128)(2,1)S(1)}, u32[]{:S(2)}, u32[]{:S(2)}) collective-permute-start(bf16[256,256]{1,0:T(8,128)(2,1)S(1)} %shard_map.145.refs_0_), channel_id=1, source_target_pairs={{0,8},{8,0},{16,24},{24,16},{1,9},{9,1},{17,25},{25,17},{2,10},{10... | collective-permute-start | bytes 393224 | tf_op jit(solution)/shard_map/ppermute | solution.py:364
  67.7 4.6 %all-to-all-start.2 = ((bf16[8,16,512]{2,1,0:T(8,128)(2,1)}), bf16[8,16,512]{2,1,0:T(8,128)(2,1)S(1)}, u32[]{:S(2)}, u32[]{:S(2)}) async-start(bf16[8,16,512]{2,1,0:T(8,128)(2,1)} %get-tuple-element.92.og), calls=%async_computation.2 | async-start | bytes 262144 | tf_op jit(solution)/shard_map/all_to_all | solution.py:359
  72.3 0.5 collective-permute-start.21
  72.9 0.4 collective-permute-start.25
  73.4 5.7 %all-to-all-done.2.og = bf16[8,16,512]{2,1,0:T(8,128)(2,1)S(1)} async-done(((bf16[8,16,512]{2,1,0:T(8,128)(2,1)}), bf16[8,16,512]{2,1,0:T(8,128)(2,1)S(1)}, u32[]{:S(2)}, u32[]{:S(2)}) %all-to-all-start.2) | async-done | bytes 131104 | tf_op jit(solution)/shard_map/all_to_all | solution.py:359
  79.1 0.9 %shard_map.144 = (bf16[128,256]{1,0:T(8,128)(2,1)}, bf16[128,256]{1,0:T(8,128)(2,1)}) custom-call(s32[1]{0:T(128)} %bitcast.idx, bf16[128,256]{1,0:T(8,128)(2,1)S(1)} %bitcast.23, f32[2,256]{1,0:T(2,128)S(1)} %pad_maximum_fusion.refs_4_.gain, bf16[4,192,256]{2,1,0:T(8,128)(2,1)S(1)} %bitcast.16, bf16[8,16,512]{2,1,0:T(8,128)(2,1)S(1)} %all-to-all-done.2.og, ...), custom_call_target="tpu_custom_call" | custom-call | flops 1 | bytes 1 | tf_op jit(solution)/shard_map/pallas_call | solution.py:82
  80.1 1.5 %shard_map.146 = (f32[256,768]{1,0:T(8,128)}, f32[256,256]{1,0:T(8,128)}, f32[256,768]{1,0:T(8,128)}, f32[256,256]{1,0:T(8,128)}) custom-call(s32[1]{0:T(128)} %bitcast.idx, s32[1]{0:T(128)S(6)} %select_n.12.core, bf16[256,256]{1,0:T(8,128)(2,1)S(1)} %shard_map.145.refs_0_, bf16[256,256]{1,0:T(8,128)(2,1)S(1)} %collective-permute-done.21.refs_1_, ...), custom_call_target="tpu_custom_call" | custom-call | flops 1 | bytes 1 | tf_op jit(solution)/shard_map/pallas_call | solution.py:82
  (58 shorter events, 2.2 us)
Async XLA Ops:
  0.6 9.0 %collective-permute-start.2 = (bf16[128,256]{1,0:T(8,128)(2,1)}, bf16[128,256]{1,0:T(8,128)(2,1)S(1)}, u32[]{:S(2)}, u32[]{:S(2)}) collective-permute-start(bf16[128,256]{1,0:T(8,128)(2,1)} %bitcast.18), channel_id=1, source_target_pairs={{0,24},{8,16},{16,8},{24,0},{1,25},{9,17},{17,9},{25,1},{2,26},{10... | collective-permute-start | bytes 196616 | tf_op jit(solution)/shard_map/ppermute | solution.py:364
  4.6 5.0 %collective-permute-start.1 = (bf16[128,256]{1,0:T(8,128)(2,1)}, bf16[128,256]{1,0:T(8,128)(2,1)S(1)}, u32[]{:S(2)}, u32[]{:S(2)}) collective-permute-start(bf16[128,256]{1,0:T(8,128)(2,1)} %bitcast.19), channel_id=1, source_target_pairs={{0,16},{8,24},{16,0},{24,8},{1,17},{9,25},{17,1},{25,9},{2,18},{10... | collective-permute-start | bytes 196616 | tf_op jit(solution)/shard_map/ppermute | solution.py:364
  5.1 4.5 %collective-permute-start = (bf16[128,256]{1,0:T(8,128)(2,1)}, bf16[128,256]{1,0:T(8,128)(2,1)S(1)}, u32[]{:S(2)}, u32[]{:S(2)}) collective-permute-start(bf16[128,256]{1,0:T(8,128)(2,1)} %bitcast.20), channel_id=1, source_target_pairs={{0,8},{8,0},{16,24},{24,16},{1,9},{9,1},{17,25},{25,17},{2,10},{10... | collective-permute-start | bytes 196616 | tf_op jit(solution)/shard_map/ppermute | solution.py:364
  5.2 0.9 %copy-start.1 = (bf16[128,1,256]{2,0,1:T(8,128)(2,1)S(1)}, bf16[128,1,256]{2,0,1:T(8,128)(2,1)}, u32[]{:S(2)}) copy-start(bf16[128,1,256]{2,0,1:T(8,128)(2,1)} %param.9) | copy-start | bytes 196612
  6.1 0.8 %copy-start.5 = (bf16[128,1,256]{2,0,1:T(8,128)(2,1)S(1)}, bf16[128,1,256]{2,0,1:T(8,128)(2,1)}, u32[]{:S(2)}) copy-start(bf16[128,1,256]{2,0,1:T(8,128)(2,1)} %param.17) | copy-start | bytes 196612
  7.0 2.0 %collective-permute-start.3 = (bf16[4,16,512]{2,1,0:T(8,128)(2,1)S(1)}, bf16[4,16,512]{2,1,0:T(8,128)(2,1)S(1)}, u32[]{:S(2)}, u32[]{:S(2)}) collective-permute-start(bf16[4,16,512]{2,1,0:T(8,128)(2,1)S(1)} %get-tuple-element.60), channel_id=1, source_target_pairs={{0,1},{1,0},{2,3},{3,2},{4,5},{5,4},{6,7},{7,6},{8,9},{9,8},{10,11... | collective-permute-start | bytes 196616 | tf_op jit(solution)/shard_map/ppermute | solution.py:364
  8.3 0.7 copy-start.12
  8.3 0.7 copy-start.11
  9.0 0.8 %copy-start.2 = (bf16[128,1,256]{2,0,1:T(8,128)(2,1)S(1)}, bf16[128,1,256]{2,0,1:T(8,128)(2,1)}, u32[]{:S(2)}) copy-start(bf16[128,1,256]{2,0,1:T(8,128)(2,1)} %param.9) | copy-start | bytes 196612
  9.6 0.7 copy-start.10
  13.6 16.3 %all-to-all-start = ((bf16[32,8,128]{2,1,0:T(8,128)(2,1)}), bf16[32,8,128]{2,1,0:T(8,128)(2,1)S(1)}, u32[]{:S(2)}, u32[]{:S(2)}) async-start(bf16[32,8,128]{2,1,0:T(8,128)(2,1)} %get-tuple-element.69), calls=%async_computation | async-start | bytes 131072 | tf_op jit(solution)/shard_map/all_to_all | solution.py:359
  19.9 5.6 %collective-permute-start.4 = (bf16[2,16,512]{2,1,0:T(8,128)(2,1)}, bf16[2,16,512]{2,1,0:T(8,128)(2,1)S(1)}, u32[]{:S(2)}, u32[]{:S(2)}) collective-permute-start(bf16[2,16,512]{2,1,0:T(8,128)(2,1)} %get-tuple-element.62), channel_id=1, source_target_pairs={{0,2},{1,3},{2,0},{3,1},{4,6},{5,7},{6,4},{7,5},{8,10},{9,11},{10,... | collective-permute-start | bytes 98312 | tf_op jit(solution)/shard_map/ppermute | solution.py:364
  21.8 5.7 %collective-permute-start.5 = (bf16[2,16,512]{2,1,0:T(8,128)(2,1)S(1)}, bf16[2,16,512]{2,1,0:T(8,128)(2,1)S(1)}, u32[]{:S(2)}, u32[]{:S(2)}) collective-permute-start(bf16[2,16,512]{2,1,0:T(8,128)(2,1)S(1)} %get-tuple-element.63), channel_id=1, source_target_pairs={{0,4},{1,5},{2,6},{3,7},{4,0},{5,1},{6,2},{7,3},{8,12},{9,13},{10,... | collective-permute-start | bytes 98312 | tf_op jit(solution)/shard_map/ppermute | solution.py:364
  24.2 5.7 %collective-permute-start.6 = (bf16[2,16,512]{2,1,0:T(8,128)(2,1)S(1)}, bf16[2,16,512]{2,1,0:T(8,128)(2,1)S(1)}, u32[]{:S(2)}, u32[]{:S(2)}) collective-permute-start(bf16[2,16,512]{2,1,0:T(8,128)(2,1)S(1)} %get-tuple-element.64), channel_id=1, source_target_pairs={{0,6},{1,7},{2,4},{3,5},{4,2},{5,3},{6,0},{7,1},{8,14},{9,15},{10,... | collective-permute-start | bytes 98312 | tf_op jit(solution)/shard_map/ppermute | solution.py:364
  24.4 0.9 %slice-start = ((bf16[256,768]{1,0:T(8,128)(2,1)}), bf16[256,512]{1,0:T(8,128)(2,1)S(1)}, s32[]{:S(2)}) async-start(bf16[256,768]{1,0:T(8,128)(2,1)} %col_proj.1), calls=%async_computation.3 | async-start | bytes 524288 | tf_op jit(solution)/shard_map/slice | solution.py:411
  24.4 5.5 %copy-start.4 = (bf16[256,256]{1,0:T(8,128)(2,1)S(1)}, bf16[256,256]{1,0:T(8,128)(2,1)}, u32[]{:S(2)}) copy-start(bf16[256,256]{1,0:T(8,128)(2,1)} %col_out.1) | copy-start | bytes 393220
  25.3 4.6 %copy-start = (bf16[256,768]{1,0:T(8,128)(2,1)S(1)}, bf16[256,768]{1,0:T(8,128)(2,1)}, u32[]{:S(2)}) copy-start(bf16[256,768]{1,0:T(8,128)(2,1)} %col_proj.1) | copy-start | bytes 1179652
  25.3 4.6 %copy-start.3 = (bf16[256,256]{1,0:T(8,128)(2,1)S(1)}, bf16[256,256]{1,0:T(8,128)(2,1)}, u32[]{:S(2)}) copy-start(bf16[256,256]{1,0:T(8,128)(2,1)} %row_out.1) | copy-start | bytes 393220
  33.3 2.8 %copy-start.7 = (bf16[128,256]{1,0:T(8,128)(2,1)S(1)}, bf16[128,256]{1,0:T(8,128)(2,1)}, u32[]{:S(2)}) copy-start(bf16[128,256]{1,0:T(8,128)(2,1)} %get-tuple-element.73.normed) | copy-start | bytes 196612
  33.4 2.8 %copy-start.8 = (bf16[256,128]{1,0:T(8,128)(2,1)S(1)}, bf16[256,128]{1,0:T(8,128)(2,1)}, u32[]{:S(2)}) copy-start(bf16[256,128]{1,0:T(8,128)(2,1)} %get-tuple-element.75.att_t) | copy-start | bytes 196612
  33.4 11.7 %all-to-all-start.1 = ((bf16[32,8,128]{2,1,0:T(8,128)(2,1)}), bf16[32,8,128]{2,1,0:T(8,128)(2,1)S(1)}, u32[]{:S(2)}, u32[]{:S(2)}) async-start(bf16[32,8,128]{2,1,0:T(8,128)(2,1)} %get-tuple-element.71), calls=%async_computation.1 | async-start | bytes 131072 | tf_op jit(solution)/shard_map/all_to_all | solution.py:359
  36.2 0.9 %copy-start.6 = (bf16[128,768]{1,0:T(8,128)(2,1)S(1)}, bf16[128,768]{1,0:T(8,128)(2,1)}, u32[]{:S(2)}) copy-start(bf16[128,768]{1,0:T(8,128)(2,1)} %get-tuple-element.74.gp) | copy-start | bytes 589828
  37.1 0.8 %copy-start.9 = (bf16[128,256]{1,0:T(8,128)(2,1)S(1)}, bf16[128,256]{1,0:T(8,128)(2,1)}, u32[]{:S(2)}) copy-start(bf16[128,256]{1,0:T(8,128)(2,1)} %get-tuple-element.72.cot) | copy-start | bytes 196612
  39.3 1.3 %collective-permute-start.7 = (bf16[32,1280]{1,0:T(8,128)(2,1)S(1)}, bf16[32,1280]{1,0:T(8,128)(2,1)S(1)}, u32[]{:S(2)}, u32[]{:S(2)}) collective-permute-start(bf16[32,1280]{1,0:T(8,128)(2,1)S(1)} %get-tuple-element.77), channel_id=1, source_target_pairs={{0,1},{1,0},{2,3},{3,2},{4,5},{5,4},{6,7},{7,6},{8,9},{9,8},{10,11... | collective-permute-start | bytes 245768 | tf_op jit(solution)/shard_map/ppermute | solution.py:364
  39.6 1.3 %collective-permute-start.8 = (bf16[32,1280]{1,0:T(8,128)(2,1)S(1)}, bf16[32,1280]{1,0:T(8,128)(2,1)S(1)}, u32[]{:S(2)}, u32[]{:S(2)}) collective-permute-start(bf16[32,1280]{1,0:T(8,128)(2,1)S(1)} %get-tuple-element.78), channel_id=1, source_target_pairs={{0,1},{1,0},{2,3},{3,2},{4,5},{5,4},{6,7},{7,6},{8,9},{9,8},{10,11... | collective-permute-start | bytes 245768 | tf_op jit(solution)/shard_map/ppermute | solution.py:364
  39.8 1.3 %collective-permute-start.9 = (bf16[32,1280]{1,0:T(8,128)(2,1)S(1)}, bf16[32,1280]{1,0:T(8,128)(2,1)S(1)}, u32[]{:S(2)}, u32[]{:S(2)}) collective-permute-start(bf16[32,1280]{1,0:T(8,128)(2,1)S(1)} %get-tuple-element.79), channel_id=1, source_target_pairs={{0,1},{1,0},{2,3},{3,2},{4,5},{5,4},{6,7},{7,6},{8,9},{9,8},{10,11... | collective-permute-start | bytes 245768 | tf_op jit(solution)/shard_map/ppermute | solution.py:364
  40.1 1.3 %collective-permute-start.10 = (bf16[32,1280]{1,0:T(8,128)(2,1)S(1)}, bf16[32,1280]{1,0:T(8,128)(2,1)S(1)}, u32[]{:S(2)}, u32[]{:S(2)}) collective-permute-start(bf16[32,1280]{1,0:T(8,128)(2,1)S(1)} %get-tuple-element.80), channel_id=1, source_target_pairs={{0,1},{1,0},{2,3},{3,2},{4,5},{5,4},{6,7},{7,6},{8,9},{9,8},{10,11... | collective-permute-start | bytes 245768 | tf_op jit(solution)/shard_map/ppermute | solution.py:364
  41.5 5.7 %collective-permute-start.13 = (bf16[32,1280]{1,0:T(8,128)(2,1)S(1)}, bf16[32,1280]{1,0:T(8,128)(2,1)S(1)}, u32[]{:S(2)}, u32[]{:S(2)}) collective-permute-start(bf16[32,1280]{1,0:T(8,128)(2,1)S(1)} %get-tuple-element.82), channel_id=1, source_target_pairs={{0,8},{8,0},{16,24},{24,16},{1,9},{9,1},{17,25},{25,17},{2,10},{10... | collective-permute-start | bytes 245768 | tf_op jit(solution)/shard_map/ppermute | solution.py:364
  43.3 5.2 %collective-permute-start.14 = (bf16[32,1280]{1,0:T(8,128)(2,1)S(1)}, bf16[32,1280]{1,0:T(8,128)(2,1)S(1)}, u32[]{:S(2)}, u32[]{:S(2)}) collective-permute-start(bf16[32,1280]{1,0:T(8,128)(2,1)S(1)} %get-tuple-element.83), channel_id=1, source_target_pairs={{0,16},{8,24},{16,0},{24,8},{1,17},{9,25},{17,1},{25,9},{2,18},{10... | collective-permute-start | bytes 245768 | tf_op jit(solution)/shard_map/ppermute | solution.py:364
  44.8 5.3 %collective-permute-start.15 = (bf16[32,1280]{1,0:T(8,128)(2,1)S(1)}, bf16[32,1280]{1,0:T(8,128)(2,1)S(1)}, u32[]{:S(2)}, u32[]{:S(2)}) collective-permute-start(bf16[32,1280]{1,0:T(8,128)(2,1)S(1)} %get-tuple-element.84), channel_id=1, source_target_pairs={{0,24},{8,16},{16,8},{24,0},{1,25},{9,17},{17,9},{25,1},{2,26},{10... | collective-permute-start | bytes 245768 | tf_op jit(solution)/shard_map/ppermute | solution.py:364
  47.2 2.9 %collective-permute-start.12 = (bf16[96,256]{1,0:T(8,128)(2,1)S(1)}, bf16[96,256]{1,0:T(8,128)(2,1)S(1)}, u32[]{:S(2)}, u32[]{:S(2)}) collective-permute-start(bf16[96,256]{1,0:T(8,128)(2,1)S(1)} %get-tuple-element.94), channel_id=1, source_target_pairs={{0,1},{1,0},{2,3},{3,2},{4,5},{5,4},{6,7},{7,6},{8,9},{9,8},{10,11... | collective-permute-start | bytes 147464 | tf_op jit(solution)/shard_map/ppermute | solution.py:364
  50.2 13.9 %collective-permute-start.18 = (bf16[256,256]{1,0:T(8,128)(2,1)S(1)}, bf16[256,256]{1,0:T(8,128)(2,1)S(1)}, u32[]{:S(2)}, u32[]{:S(2)}) collective-permute-start(bf16[256,256]{1,0:T(8,128)(2,1)S(1)} %shard_map.143.refs_0_), channel_id=1, source_target_pairs={{0,6},{1,7},{2,4},{3,5},{4,2},{5,3},{6,0},{7,1},{8,14},{9,15},{10,... | collective-permute-start | bytes 393224 | tf_op jit(solution)/shard_map/ppermute | solution.py:364
  53.6 10.5 %collective-permute-start.17 = (bf16[256,256]{1,0:T(8,128)(2,1)S(1)}, bf16[256,256]{1,0:T(8,128)(2,1)S(1)}, u32[]{:S(2)}, u32[]{:S(2)}) collective-permute-start(bf16[256,256]{1,0:T(8,128)(2,1)S(1)} %shard_map.143.refs_0_), channel_id=1, source_target_pairs={{0,4},{1,5},{2,6},{3,7},{4,0},{5,1},{6,2},{7,3},{8,12},{9,13},{10,... | collective-permute-start | bytes 393224 | tf_op jit(solution)/shard_map/ppermute | solution.py:364
  53.6 10.5 %collective-permute-start.16 = (bf16[256,256]{1,0:T(8,128)(2,1)S(1)}, bf16[256,256]{1,0:T(8,128)(2,1)S(1)}, u32[]{:S(2)}, u32[]{:S(2)}) collective-permute-start(bf16[256,256]{1,0:T(8,128)(2,1)S(1)} %shard_map.143.refs_0_), channel_id=1, source_target_pairs={{0,2},{1,3},{2,0},{3,1},{4,6},{5,7},{6,4},{7,5},{8,10},{9,11},{10,... | collective-permute-start | bytes 393224 | tf_op jit(solution)/shard_map/ppermute | solution.py:364
  54.6 4.3 %collective-permute-start.11 = (bf16[128,192]{1,0:T(8,128)(2,1)S(1)}, bf16[128,192]{1,0:T(8,128)(2,1)S(1)}, u32[]{:S(2)}, u32[]{:S(2)}) collective-permute-start(bf16[128,192]{1,0:T(8,128)(2,1)S(1)} %get-tuple-element.91), channel_id=1, source_target_pairs={{0,8},{8,0},{16,24},{24,16},{1,9},{9,1},{17,25},{25,17},{2,10},{10... | collective-permute-start | bytes 147464 | tf_op jit(solution)/shard_map/ppermute | solution.py:364
  55.2 5.0 %collective-permute-start.19 = (bf16[128,192]{1,0:T(8,128)(2,1)S(1)}, bf16[128,192]{1,0:T(8,128)(2,1)S(1)}, u32[]{:S(2)}, u32[]{:S(2)}) collective-permute-start(bf16[128,192]{1,0:T(8,128)(2,1)S(1)} %get-tuple-element.96), channel_id=1, source_target_pairs={{0,16},{8,24},{16,0},{24,8},{1,17},{9,25},{17,1},{25,9},{2,18},{10... | collective-permute-start | bytes 147464 | tf_op jit(solution)/shard_map/ppermute | solution.py:364
  58.9 5.2 %collective-permute-start.20 = (bf16[128,192]{1,0:T(8,128)(2,1)S(1)}, bf16[128,192]{1,0:T(8,128)(2,1)S(1)}, u32[]{:S(2)}, u32[]{:S(2)}) collective-permute-start(bf16[128,192]{1,0:T(8,128)(2,1)S(1)} %get-tuple-element.97), channel_id=1, source_target_pairs={{0,24},{8,16},{16,8},{24,0},{1,25},{9,17},{17,9},{25,1},{2,26},{10... | collective-permute-start | bytes 147464 | tf_op jit(solution)/shard_map/ppermute | solution.py:364
  64.1 8.7 %collective-permute-start.26 = (bf16[256,256]{1,0:T(8,128)(2,1)S(1)}, bf16[256,256]{1,0:T(8,128)(2,1)S(1)}, u32[]{:S(2)}, u32[]{:S(2)}) collective-permute-start(bf16[256,256]{1,0:T(8,128)(2,1)S(1)} %shard_map.145.refs_0_), channel_id=1, source_target_pairs={{0,24},{8,16},{16,8},{24,0},{1,25},{9,17},{17,9},{25,1},{2,26},{10... | collective-permute-start | bytes 393224 | tf_op jit(solution)/shard_map/ppermute | solution.py:364
  66.2 6.7 %collective-permute-start.24 = (bf16[256,256]{1,0:T(8,128)(2,1)S(1)}, bf16[256,256]{1,0:T(8,128)(2,1)S(1)}, u32[]{:S(2)}, u32[]{:S(2)}) collective-permute-start(bf16[256,256]{1,0:T(8,128)(2,1)S(1)} %shard_map.145.refs_0_), channel_id=1, source_target_pairs={{0,16},{8,24},{16,0},{24,8},{1,17},{9,25},{17,1},{25,9},{2,18},{10... | collective-permute-start | bytes 393224 | tf_op jit(solution)/shard_map/ppermute | solution.py:364
  66.8 6.6 %collective-permute-start.22 = (bf16[256,256]{1,0:T(8,128)(2,1)S(1)}, bf16[256,256]{1,0:T(8,128)(2,1)S(1)}, u32[]{:S(2)}, u32[]{:S(2)}) collective-permute-start(bf16[256,256]{1,0:T(8,128)(2,1)S(1)} %shard_map.145.refs_0_), channel_id=1, source_target_pairs={{0,8},{8,0},{16,24},{24,16},{1,9},{9,1},{17,25},{25,17},{2,10},{10... | collective-permute-start | bytes 393224 | tf_op jit(solution)/shard_map/ppermute | solution.py:364
  67.7 11.4 %all-to-all-start.2 = ((bf16[8,16,512]{2,1,0:T(8,128)(2,1)}), bf16[8,16,512]{2,1,0:T(8,128)(2,1)S(1)}, u32[]{:S(2)}, u32[]{:S(2)}) async-start(bf16[8,16,512]{2,1,0:T(8,128)(2,1)} %get-tuple-element.92.og), calls=%async_computation.2 | async-start | bytes 262144 | tf_op jit(solution)/shard_map/all_to_all | solution.py:359
  72.3 7.7 %collective-permute-start.21 = (bf16[256,256]{1,0:T(8,128)(2,1)S(1)}, bf16[256,256]{1,0:T(8,128)(2,1)S(1)}, u32[]{:S(2)}, u32[]{:S(2)}) collective-permute-start(bf16[256,256]{1,0:T(8,128)(2,1)S(1)} %shard_map.145.refs_0_), channel_id=1, source_target_pairs={{0,1},{1,0},{2,3},{3,2},{4,5},{5,4},{6,7},{7,6},{8,9},{9,8},{10,11... | collective-permute-start | bytes 393224 | tf_op jit(solution)/shard_map/ppermute | solution.py:364
  72.8 7.2 %collective-permute-start.27 = (bf16[256,256]{1,0:T(8,128)(2,1)S(1)}, bf16[256,256]{1,0:T(8,128)(2,1)S(1)}, u32[]{:S(2)}, u32[]{:S(2)}) collective-permute-start(bf16[256,256]{1,0:T(8,128)(2,1)S(1)} %collective-permute-done.26.refs_6_), channel_id=1, source_target_pairs={{0,1},{1,0},{2,3},{3,2},{4,5},{5,4},{6,7},{7,6},{8,9},{9,8},{10,11... | collective-permute-start | bytes 393224 | tf_op jit(solution)/shard_map/ppermute | solution.py:364
  72.9 7.2 %collective-permute-start.25 = (bf16[256,256]{1,0:T(8,128)(2,1)S(1)}, bf16[256,256]{1,0:T(8,128)(2,1)S(1)}, u32[]{:S(2)}, u32[]{:S(2)}) collective-permute-start(bf16[256,256]{1,0:T(8,128)(2,1)S(1)} %collective-permute-done.24.refs_4_), channel_id=1, source_target_pairs={{0,1},{1,0},{2,3},{3,2},{4,5},{5,4},{6,7},{7,6},{8,9},{9,8},{10,11... | collective-permute-start | bytes 393224 | tf_op jit(solution)/shard_map/ppermute | solution.py:364
  73.3 6.7 %collective-permute-start.23 = (bf16[256,256]{1,0:T(8,128)(2,1)S(1)}, bf16[256,256]{1,0:T(8,128)(2,1)S(1)}, u32[]{:S(2)}, u32[]{:S(2)}) collective-permute-start(bf16[256,256]{1,0:T(8,128)(2,1)S(1)} %collective-permute-done.22.refs_2_), channel_id=1, source_target_pairs={{0,1},{1,0},{2,3},{3,2},{4,5},{5,4},{6,7},{7,6},{8,9},{9,8},{10,11... | collective-permute-start | bytes 393224 | tf_op jit(solution)/shard_map/ppermute | solution.py:364

commit v6 on v5

--- a/solution.py
+++ b/solution.py
@@ -149,15 +149,14 @@
 
 
 def column_step(sites, haps, hap, at, row_out, gain, col_proj, kv_t_w, col_out, *refs):
-    ga_out, og_out, *far, xc = refs[haps // 2 : haps // 2 + 7]
-    near, sems = refs[haps // 2 + 7 : -1], refs[-1]
-    copies = [
-        pltpu.make_async_copy(near[j], far[j], sems.at[j]) for j in range(len(near))
-    ]
-
-    def save(j, value):
-        near[j][...] = value
-        copies[j].start()
+    ga_out, send, keep, og_out, xc, og, w_all, sems = refs[haps // 2 :]
+    core = hap[0] % 2
+    half = row_out.shape[0] // 2
+    mine = pl.ds(pl.multiple_of(core * half, half), half)
+    other = pl.ds(pl.multiple_of((1 - core) * half, half), half)
+
+    def save(j, cols):
+        return pltpu.make_async_copy(w_all.at[mine, cols], keep.at[:, cols], sems.at[j])
 
     for m in range(haps // 2):
         xc[hap[0] ^ (2 * m)] = refs[m][0]
@@ -170,16 +169,14 @@
     per = rows // haps
     cot_f = xc_all[:, width:]
     cot = cot_f.astype(BF16)
-    save(3, cot)
     hid = xc_all[:, :width]
+    a_blocks = [unpack_block(at[i * haps : (i + 1) * haps], group) for i in range(sites)]
     for i in range(sites):
-        a_i = unpack_block(at[i * haps : (i + 1) * haps], group)
-        hid = hid + mm(a_i, row_out[i * group : (i + 1) * group, :])
+        hid = hid + mm(a_blocks[i], row_out[i * group : (i + 1) * group, :])
     hid = hid.astype(BF16).astype(F32)
     grad_att = mm_nt(cot, col_out[...]).astype(BF16)
     xhat, rstd = norm_parts(hid)
     normed = (xhat * gain[1:2, :]).astype(BF16)
-    save(0, normed)
     packed = mm(normed, col_proj[...]).astype(BF16)
     q = packed[:, :width]
     key = packed[:, width : 2 * width]
@@ -208,7 +205,7 @@
         ds16.append(ds_h)
         dq_t.append(mm(kv_t[:width, :][cols], ds_h))
     att_t = jnp.concatenate(att_t, axis=0)
-    save(2, att_t.astype(BF16))
+    w_all[:, 3 * width : 4 * width] = mm(att_t.astype(BF16), cot).astype(BF16)
     att = jnp.transpose(att_t).astype(BF16)
     out = hid + mm(att, col_out[...])
     dv_all = mm(jnp.concatenate(prob16, axis=0), grad_att)
@@ -221,34 +218,32 @@
     )
     dq = jnp.transpose(jnp.concatenate(dq_t, axis=0))
     packed_grad = jnp.concatenate([dq * SCALE, dk * SCALE, dv], axis=1).astype(BF16)
-    save(1, packed_grad)
+    w_all[:, : 3 * width] = mm_tn(normed, packed_grad).astype(BF16)
+    first = save(0, slice(0, 4 * width))
+    first.start()
     grad_normed = mm_nt(packed_grad, col_proj[...])
     grad_hidden = (cot_f + norm_back(xhat, rstd, gain[1:2, :], grad_normed)).astype(BF16)
     for i in range(sites):
         g_i = mm_nt(grad_hidden, row_out[i * group : (i + 1) * group, :])
         ga_out[i * haps : (i + 1) * haps] = pack_block(g_i, haps)
+    for i in range(sites):
+        w_all[i * group : (i + 1) * group, 4 * width :] = mm_tn(a_blocks[i], grad_hidden).astype(BF16)
+    second = save(1, slice(4 * width, 5 * width))
+    second.start()
     both = jnp.concatenate([out, grad_hidden.astype(F32)], axis=1)
-    og_out[...] = both.reshape(haps, per, 2 * width).astype(BF16)
-    for copy in copies:
-        copy.wait()
-
-
-def column_weights(sites, haps, core, cot, at, og, normed, gp, att_t, keep, *refs):
-    sends, both = refs[:-1], refs[-1]
-    width = normed.shape[1]
-    group = width // sites
-    half = width // 2
-    grad_hidden = flat_rows(og[:, :, width:])
-    both[:, : 3 * width] = mm_tn(normed[...], gp[...]).astype(BF16)
-    both[:, 3 * width : 4 * width] = mm(att_t[...], cot[...]).astype(BF16)
-    for i in range(sites):
-        a_i = unpack_block(at[i * haps : (i + 1) * haps], group)
-        both[i * group : (i + 1) * group, 4 * width :] = mm_tn(a_i, grad_hidden).astype(BF16)
-    keep[...] = both[pl.ds(pl.multiple_of(core[0] * half, half), half), :]
-    part = half // len(sends)
-    for j, send in enumerate(sends):
-        start = (1 - core[0]) * half + j * part
-        send[...] = both[pl.ds(pl.multiple_of(start, part), part), :]
+    og[...] = both.reshape(haps, per, 2 * width).astype(BF16)
+    third = pltpu.make_async_copy(og, og_out, sems.at[2])
+    third.start()
+    send[...] = w_all[other, :]
+    first.wait()
+    second.wait()
+    third.wait()
+
+
+def split_outputs(hap, og, keep, send):
+    for m in range(keep.shape[0]):
+        keep[m] = og[hap[0] ^ (2 * m)]
+        send[m] = og[hap[0] ^ (2 * m + 1)]
 
 
 def column_split(sites, idx, keep, *refs):
@@ -299,11 +294,14 @@
         gp_outs[b][...] = joined[b * rows : (b + 1) * rows]
 
 
-def row_finish(sites, idx, feats, gain, w_all, og, *refs):
-    gps = refs[:sites]
-    out_ref, gf_ref = refs[sites:]
+def row_finish(sites, haps, idx, hap, feats, gain, w_all, *refs):
+    gps, ogs = refs[:sites], refs[sites : sites + haps // 2]
+    out_ref, gf_ref, og = refs[sites + haps // 2 :]
     me = idx[0]
     width = feats.shape[1]
+    for m in range(haps // 2):
+        og[hap[0] ^ (2 * m)] = ogs[m][0]
+        og[hap[0] ^ (2 * m + 1)] = ogs[m][1]
     both = flat_rows(og[...], F32)
     grad_normed = sum(mm(gps[k][...], w_all[me ^ k]) for k in range(sites))
     xhat, rstd = norm_parts(feats[...].astype(F32))
@@ -402,7 +400,6 @@
     )
     got = swapped(send, "hap", 1)
     xcs = call(relay_inputs, [((2, per, 2 * width), BF16)] * (haps // 2), keep, got)
-    pieces, _ = lax.optimization_barrier((pieces, xcs))
     xcs = [xcs[0]] + [swapped(xcs[m], "hap", 2 * m) for m in range(1, haps // 2)]
     w_all = jnp.transpose(row_proj.reshape(width, 3, sites, group), (2, 1, 3, 0)).reshape(
         sites, 3 * group, width
@@ -420,38 +417,29 @@
             ((group, total), BF16),
             ((total, width), BF16),
         ],
-        idx, link_pattern, *pieces, gains, w_t, scalars=2, us=3,
-    )
+        idx, link_pattern, *pieces, gains, w_t, scalars=2, us=20,
+    )
+    att, xcs = lax.optimization_barrier((att, xcs))
     at = exchange(att, both_axes)
-    ga, og, col_normed, col_gp, col_att_t, cot = call(
+    half = width // 2
+    ga, col_send, col_keep, og = call(
         functools.partial(column_step, sites, haps),
         [
             block,
+            ((half, 5 * width), BF16),
+            ((half, 5 * width), BF16),
             ((haps, per, 2 * width), BF16),
-            ((rows, width), BF16),
-            ((rows, 3 * width), BF16),
-            ((width, rows), BF16),
-            ((rows, width), BF16),
         ],
-        hap, at, row_out, gains, col_proj, kv_t_w, col_out, *xcs, scalars=1, far=4,
+        hap, at, row_out, gains, col_proj, kv_t_w, col_out, *xcs, scalars=1, far=2,
         scratch=[
             pltpu.VMEM((haps, per, 2 * width), BF16),
-            pltpu.VMEM((rows, width), BF16),
-            pltpu.VMEM((rows, 3 * width), BF16),
-            pltpu.VMEM((width, rows), BF16),
-            pltpu.VMEM((rows, width), BF16),
-            pltpu.SemaphoreType.DMA((4,)),
+            pltpu.VMEM((haps, per, 2 * width), BF16),
+            pltpu.VMEM((width, 5 * width), BF16),
+            pltpu.SemaphoreType.DMA((3,)),
         ],
     )
     g_in = exchange(ga, both_axes)
-    half = width // 2
-    col_keep, *col_sends = call(
-        functools.partial(column_weights, sites, haps),
-        [((half, 5 * width), BF16)] + [((half // 4, 5 * width), BF16)] * 4,
-        core, cot, at, og, col_normed, col_gp, col_att_t, scalars=1, us=20,
-        scratch=[pltpu.VMEM((width, 5 * width), BF16)],
-    )
-    col_got = [swapped(send, "hap", 1) for send in col_sends]
+    col_got = [swapped(col_send, "hap", 1)]
     cols = call(
         functools.partial(column_split, sites),
         [((half // sites, 5 * width), BF16)] * sites,
@@ -475,18 +463,26 @@
     (joined,) = call(weights_join, [((depth, width), BF16)], row_keep, row_got, *cols)
     parts = [joined] + [swapped(joined, "hap", 2 * m) for m in range(1, haps // 2)]
     gps = [gps[0]] + [swapped(gps[k], "site", k) for k in range(1, sites)]
-    og, _ = lax.optimization_barrier((og, gps[1]))
-    og_in = exchange(og, "hap")
-    parts, gps = lax.optimization_barrier((parts, gps))
+    og, _ = lax.optimization_barrier((og, joined))
+    og_keep, og_send = call(
+        split_outputs, [((haps // 2, per, 2 * width), BF16)] * 2, hap, og, scalars=1
+    )
+    og_got = swapped(og_send, "hap", 1)
+    ogs = call(relay_inputs, [((2, per, 2 * width), BF16)] * (haps // 2), og_keep, og_got)
+    parts, gps, ogs = lax.optimization_barrier((parts, gps, ogs))
     (mine,) = call(weights_sum, [((depth, width), BF16)], *parts)
     mine_swapped = swapped(mine, "hap", 1)
+    ogs, _ = lax.optimization_barrier((ogs, mine))
+    ogs = [ogs[0]] + [swapped(ogs[m], "hap", 2 * m) for m in range(1, haps // 2)]
+    full = [swapped(mine, "site", k) for k in range(1, sites)]
+    full, ogs = lax.optimization_barrier((full, ogs))
+    full = [mine, mine_swapped] + [x for p in full for x in (p, swapped(p, "hap", 1))]
     out, grad = call(
-        functools.partial(row_finish, sites),
+        functools.partial(row_finish, sites, haps),
         [((rows, width), BF16)] * 2,
-        idx, feats, gains, w_all, og_in, *gps, scalars=1,
-    )
-    full = [mine] + [swapped(mine, "site", k) for k in range(1, sites)]
-    full = [mine, mine_swapped] + [x for p in full[1:] for x in (p, swapped(p, "hap", 1))]
+        idx, hap, feats, gains, w_all, *gps, *ogs, scalars=2,
+        scratch=[pltpu.VMEM((haps, per, 2 * width), BF16)],
+    )
     rp, ro, cp, co = call(
         functools.partial(weights_finish, sites),
         [((width, 3 * width), F32), ((width, width), F32)] * 2,

time: 82.2 us -> 79.9 us (0.972)
  waiting for transfers between devices: 20.8 us -> 24.3 us
  starting transfers between devices: 39.2 us -> 36.7 us
  Pallas kernels: 13.5 us -> 11.9 us
  local copies, waits for them, and re-layouts: 7.15 us -> 5.68 us
    all_to_all x3 -> x2, starting transfers between devices: 13.8 us -> 6.24 us  [exchange(): return lax.all_to_all(value, axis, 0, 0, tiled=True)]
    ppermute x28 -> x29, starting transfers between devices: 25.5 us -> 30.4 us  [swapped(): return lax.ppermute(value, axis, [(i, i ^ by) for i in range(length)])]
    all_to_all x3 -> x2, waiting for transfers between devices: 5.69 us -> 8.97 us  [exchange(): return lax.all_to_all(value, axis, 0, 0, tiled=True)]
    pallas_call x11 -> x12, Pallas kernels: 13.5 us -> 11.9 us  [call(): pl.pallas_call(body, out_shape=[jax.ShapeDtypeStruct(s, d) for s, d in ou...]
    unnamed x28 -> x24, local copies, waits for them, and re-layouts: 6.16 us -> 4.68 us
    ppermute x28 -> x29, waiting for transfers between devices: 15.1 us -> 15.4 us  [swapped(): return lax.ppermute(value, axis, [(i, i ^ by) for i in range(length)])]
  transfers between devices with their start and end apart: 31 -> 31, of which waited for: 12 -> 10; matrix products, arithmetic and copies ran while one was open for 2% -> 2% of each run, Pallas kernels for 6% -> 8%
where the time goes in v6:
time: 79.9 us; the launch traced here: 79.5 us
  starting transfers between devices  36.7 us (46%)
  waiting for transfers between devices  24.3 us (30%)
  Pallas kernels  11.9 us (15%)
  local copies, waits for them, and re-layouts  5.68 us (7%)
  between operations  0.89 us (1%)
    ppermute x29, starting transfers between devices, swapped(): return lax.ppermute(value, axis, [(i, i ^ by) for i in range(length)])  30.4 us
    ppermute x29, waiting for transfers between devices, swapped(): return lax.ppermute(value, axis, [(i, i ^ by) for i in range(length)])  15.4 us
    pallas_call x12, Pallas kernels, call(): pl.pallas_call(body, out_shape=[jax.ShapeDtypeStruct(s, d) for s, d in ou...  11.9 us
    all_to_all x2, waiting for transfers between devices, exchange(): return lax.all_to_all(value, axis, 0, 0, tiled=True)  8.97 us
    all_to_all x2, starting transfers between devices, exchange(): return lax.all_to_all(value, axis, 0, 0, tiled=True)  6.24 us
    unnamed x24, local copies, waits for them, and re-layouts  4.68 us
  transfers between devices with their start and end apart: 31, of which 10 were waited for; matrix products, arithmetic and copies ran while one was open for 2% of the time, Pallas kernels for 8%

profile of v6, /device:TPU:0, one launch (start us, length us, event | category | flops | bytes accessed | tf_op | source)
XLA Modules:
  0.0 79.5 jit_solution(1849197019116264298)
XLA Ops:
  0.6 4.0 %collective-permute-start.2 = (bf16[128,256]{1,0:T(8,128)(2,1)}, bf16[128,256]{1,0:T(8,128)(2,1)S(1)}, u32[]{:S(2)}, u32[]{:S(2)}) collective-permute-start(bf16[128,256]{1,0:T(8,128)(2,1)} %bitcast.18), channel_id=1, source_target_pairs={{0,24},{8,16},{16,8},{24,0},{1,25},{9,17},{17,9},{25,1},{2,26},{10... | collective-permute-start | bytes 196616 | tf_op jit(solution)/shard_map/ppermute | solution.py:362
  4.6 0.5 collective-permute-start.1
  5.1 0.1 collective-permute-start
  5.2 0.9 %copy-done.2 = bf16[128,1,256]{2,0,1:T(8,128)(2,1)S(1)} copy-done((bf16[128,1,256]{2,0,1:T(8,128)(2,1)S(1)}, bf16[128,1,256]{2,0,1:T(8,128)(2,1)}, u32[]{:S(2)}) %copy-start.2) | copy-done | bytes 65560
  6.1 0.8 %copy-done.7 = bf16[128,1,256]{2,0,1:T(8,128)(2,1)S(1)} copy-done((bf16[128,1,256]{2,0,1:T(8,128)(2,1)S(1)}, bf16[128,1,256]{2,0,1:T(8,128)(2,1)}, u32[]{:S(2)}) %copy-start.7) | copy-done | bytes 65560
  7.1 1.2 %copy.17 = bf16[256,768]{0,1:T(8,128)(2,1)S(1)} copy(bf16[256,768]{1,0:T(8,128)(2,1)} %param.12) | data formatting | bytes 786432 | tf_op args[3]
  8.3 0.6 copy-done.10
  9.0 2.0 %collective-permute-start.4 = (bf16[2,16,512]{2,1,0:T(8,128)(2,1)S(1)}, bf16[2,16,512]{2,1,0:T(8,128)(2,1)S(1)}, u32[]{:S(2)}, u32[]{:S(2)}) collective-permute-start(bf16[2,16,512]{2,1,0:T(8,128)(2,1)S(1)} %get-tuple-element.78), channel_id=1, source_target_pairs={{0,2},{1,3},{2,0},{3,1},{4,6},{5,7},{6,4},{7,5},{8,10},{9,11},{10,... | collective-permute-start | bytes 98312 | tf_op jit(solution)/shard_map/ppermute | solution.py:362
  11.1 2.6 %collective-permute-start.5 = (bf16[2,16,512]{2,1,0:T(8,128)(2,1)S(1)}, bf16[2,16,512]{2,1,0:T(8,128)(2,1)S(1)}, u32[]{:S(2)}, u32[]{:S(2)}) collective-permute-start(bf16[2,16,512]{2,1,0:T(8,128)(2,1)S(1)} %get-tuple-element.79), channel_id=1, source_target_pairs={{0,4},{1,5},{2,6},{3,7},{4,0},{5,1},{6,2},{7,3},{8,12},{9,13},{10,... | collective-permute-start | bytes 98312 | tf_op jit(solution)/shard_map/ppermute | solution.py:362
  13.7 3.3 %shard_map.136 = (bf16[32,8,128]{2,1,0:T(8,128)(2,1)}, bf16[2,512,512]{2,1,0:T(8,128)(2,1)S(1)}, bf16[512,64]{1,0:T(8,128)(2,1)S(1)}, bf16[512,64]{1,0:T(8,128)(...) custom-call(s32[1]{0:T(128)} %bitcast.idx, s32[4,4]{1,0:T(4,128)S(1)} %copy-done.8, ...), custom_call_target="tpu_custom_call" | custom-call | flops 20000000000 | bytes 72000000 | tf_op jit(solution)/shard_map/pallas_call | solution.py:82
  17.0 2.4 %collective-permute-done.6.refs_3_ = bf16[2,16,512]{2,1,0:T(8,128)(2,1)S(1)} collective-permute-done((bf16[2,16,512]{2,1,0:T(8,128)(2,1)S(1)}, bf16[2,16,512]{2,1,0:T(8,128)(2,1)S(1)}, u32[]{:S(2)}, u32[]{:S(2)}) %collective-permute-start.6) | collective-permute-done | bytes 32800 | tf_op jit(solution)/shard_map/ppermute | solution.py:362
  19.4 3.7 %all-to-all-start = ((bf16[32,8,128]{2,1,0:T(8,128)(2,1)}), bf16[32,8,128]{2,1,0:T(8,128)(2,1)S(1)}, u32[]{:S(2)}, u32[]{:S(2)}) async-start(bf16[32,8,128]{2,1,0:T(8,128)(2,1)} %get-tuple-element.81), calls=%async_computation | async-start | bytes 131072 | tf_op jit(solution)/shard_map/all_to_all | solution.py:357
  23.1 0.9 %slice-done = bf16[256,512]{1,0:T(8,128)(2,1)S(1)} async-done(((bf16[256,768]{1,0:T(8,128)(2,1)}), bf16[256,512]{1,0:T(8,128)(2,1)S(1)}, s32[]{:S(2)}) %slice-start) | async-done | bytes 262168 | tf_op jit(solution)/shard_map/slice | solution.py:408
  24.0 0.1 copy.20
  24.1 6.3 %all-to-all-done.at = bf16[32,8,128]{2,1,0:T(8,128)(2,1)S(1)} async-done(((bf16[32,8,128]{2,1,0:T(8,128)(2,1)}), bf16[32,8,128]{2,1,0:T(8,128)(2,1)S(1)}, u32[]{:S(2)}, u32[]{:S(2)}) %all-to-all-start) | async-done | bytes 65568 | tf_op jit(solution)/shard_map/all_to_all | solution.py:357
  30.4 3.8 %shard_map.139 = (bf16[32,8,128]{2,1,0:T(8,128)(2,1)}, bf16[128,1280]{1,0:T(8,128)(2,1)}, bf16[128,1280]{1,0:T(8,128)(2,1)}, bf16[8,16,512]{2,1,0:T(8,128)(2,1)}) custom-call(s32[1]{0:T(128)} %bitcast.1.hap, bf16[32,8,128]{2,1,0:T(8,128)(2,1)S(1)} %all-to-all-done.at, bf16[256,256]{1,0:T(8,128)(2,1)S(1)} %copy-done.5, ...), custom_call_target="tpu_custom_call" | custom-call | flops 1 | bytes 1 | tf_op jit(solution)/shard_map/pallas_call | solution.py:82
  34.3 0.2 collective-permute-start.7
  34.4 2.6 %all-to-all-start.1 = ((bf16[32,8,128]{2,1,0:T(8,128)(2,1)}), bf16[32,8,128]{2,1,0:T(8,128)(2,1)S(1)}, u32[]{:S(2)}, u32[]{:S(2)}) async-start(bf16[32,8,128]{2,1,0:T(8,128)(2,1)} %get-tuple-element.86), calls=%async_computation.1 | async-start | bytes 131072 | tf_op jit(solution)/shard_map/all_to_all | solution.py:357
  37.0 1.0 %copy-done.1 = bf16[128,1280]{1,0:T(8,128)(2,1)S(1)} copy-done((bf16[128,1280]{1,0:T(8,128)(2,1)S(1)}, bf16[128,1280]{1,0:T(8,128)(2,1)}, u32[]{:S(2)}) %copy-start.1) | copy-done | bytes 327704
  38.0 0.2 shard_map.140
  38.2 1.7 %collective-permute-start.9 = (bf16[32,1280]{1,0:T(8,128)(2,1)S(1)}, bf16[32,1280]{1,0:T(8,128)(2,1)S(1)}, u32[]{:S(2)}, u32[]{:S(2)}) collective-permute-start(bf16[32,1280]{1,0:T(8,128)(2,1)S(1)} %get-tuple-element.90), channel_id=1, source_target_pairs={{0,8},{8,0},{16,24},{24,16},{1,9},{9,1},{17,25},{25,17},{2,10},{10... | collective-permute-start | bytes 245768 | tf_op jit(solution)/shard_map/ppermute | solution.py:362
  39.9 1.5 %collective-permute-start.10 = (bf16[32,1280]{1,0:T(8,128)(2,1)S(1)}, bf16[32,1280]{1,0:T(8,128)(2,1)S(1)}, u32[]{:S(2)}, u32[]{:S(2)}) collective-permute-start(bf16[32,1280]{1,0:T(8,128)(2,1)S(1)} %get-tuple-element.91), channel_id=1, source_target_pairs={{0,16},{8,24},{16,0},{24,8},{1,17},{9,25},{17,1},{25,9},{2,18},{10... | collective-permute-start | bytes 245768 | tf_op jit(solution)/shard_map/ppermute | solution.py:362
  41.4 0.4 collective-permute-start.11
  41.7 2.7 %all-to-all-done.1.g_in = bf16[32,8,128]{2,1,0:T(8,128)(2,1)S(1)} async-done(((bf16[32,8,128]{2,1,0:T(8,128)(2,1)}), bf16[32,8,128]{2,1,0:T(8,128)(2,1)S(1)}, u32[]{:S(2)}, u32[]{:S(2)}) %all-to-all-start.1) | async-done | bytes 65568 | tf_op jit(solution)/shard_map/all_to_all | solution.py:357
  44.4 2.1 %shard_map.141 = (bf16[128,192]{1,0:T(8,128)(2,1)S(1)}, bf16[128,192]{1,0:T(8,128)(2,1)S(1)}, bf16[128,192]{1,0:T(8,128)(2,1)S(1)}, bf16[128,192]{1,0:T(8,128)(2...) custom-call(s32[1]{0:T(128)} %bitcast.idx, s32[1]{0:T(128)S(6)} %select_n.11.core, ...), custom_call_target="tpu_custom_call" | custom-call | flops 1 | bytes 1 | tf_op jit(solution)/shard_map/pallas_call | solution.py:82
  46.5 0.2 collective-permute-start.8
  46.7 1.1 %collective-permute-done.8.row_got = bf16[96,256]{1,0:T(8,128)(2,1)S(1)} collective-permute-done((bf16[96,256]{1,0:T(8,128)(2,1)S(1)}, bf16[96,256]{1,0:T(8,128)(2,1)S(1)}, u32[]{:S(2)}, u32[]{:S(2)}) %collective-permute-start.8) | collective-permute-done | bytes 49184 | tf_op jit(solution)/shard_map/ppermute | solution.py:362
  47.9 2.4 %collective-permute-start.14 = (bf16[256,256]{1,0:T(8,128)(2,1)S(1)}, bf16[256,256]{1,0:T(8,128)(2,1)S(1)}, u32[]{:S(2)}, u32[]{:S(2)}) collective-permute-start(bf16[256,256]{1,0:T(8,128)(2,1)S(1)} %shard_map.142.refs_0_), channel_id=1, source_target_pairs={{0,6},{1,7},{2,4},{3,5},{4,2},{5,3},{6,0},{7,1},{8,14},{9,15},{10,... | collective-permute-start | bytes 393224 | tf_op jit(solution)/shard_map/ppermute | solution.py:362
  50.3 2.0 %collective-permute-start.12 = (bf16[256,256]{1,0:T(8,128)(2,1)S(1)}, bf16[256,256]{1,0:T(8,128)(2,1)S(1)}, u32[]{:S(2)}, u32[]{:S(2)}) collective-permute-start(bf16[256,256]{1,0:T(8,128)(2,1)S(1)} %shard_map.142.refs_0_), channel_id=1, source_target_pairs={{0,2},{1,3},{2,0},{3,1},{4,6},{5,7},{6,4},{7,5},{8,10},{9,11},{10,... | collective-permute-start | bytes 393224 | tf_op jit(solution)/shard_map/ppermute | solution.py:362
  52.5 0.8 collective-permute-start.15
  53.2 3.7 %collective-permute-done.15.refs_1_ = bf16[128,192]{1,0:T(8,128)(2,1)S(1)} collective-permute-done((bf16[128,192]{1,0:T(8,128)(2,1)S(1)}, bf16[128,192]{1,0:T(8,128)(2,1)S(1)}, u32[]{:S(2)}, u32[]{:S(2)}) %collective-permute-start.15) | collective-permute-done | bytes 49184 | tf_op jit(solution)/shard_map/ppermute | solution.py:362
  57.0 0.7 collective-permute-start.16
  57.7 1.5 %collective-permute-start.17 = (bf16[128,192]{1,0:T(8,128)(2,1)S(1)}, bf16[128,192]{1,0:T(8,128)(2,1)S(1)}, u32[]{:S(2)}, u32[]{:S(2)}) collective-permute-start(bf16[128,192]{1,0:T(8,128)(2,1)S(1)} %get-tuple-element.104), channel_id=1, source_target_pairs={{0,24},{8,16},{16,8},{24,0},{1,25},{9,17},{17,9},{25,1},{2,26},{10... | collective-permute-start | bytes 147464 | tf_op jit(solution)/shard_map/ppermute | solution.py:362
  59.1 2.8 %collective-permute-done.16.refs_2_ = bf16[128,192]{1,0:T(8,128)(2,1)S(1)} collective-permute-done((bf16[128,192]{1,0:T(8,128)(2,1)S(1)}, bf16[128,192]{1,0:T(8,128)(2,1)S(1)}, u32[]{:S(2)}, u32[]{:S(2)}) %collective-permute-start.16) | collective-permute-done | bytes 49184 | tf_op jit(solution)/shard_map/ppermute | solution.py:362
  61.9 0.9 %collective-permute-done.17.refs_3_ = bf16[128,192]{1,0:T(8,128)(2,1)S(1)} collective-permute-done((bf16[128,192]{1,0:T(8,128)(2,1)S(1)}, bf16[128,192]{1,0:T(8,128)(2,1)S(1)}, u32[]{:S(2)}, u32[]{:S(2)}) %collective-permute-start.17) | collective-permute-done | bytes 49184 | tf_op jit(solution)/shard_map/ppermute | solution.py:362
  62.9 1.5 %collective-permute-start.21 = (bf16[256,256]{1,0:T(8,128)(2,1)S(1)}, bf16[256,256]{1,0:T(8,128)(2,1)S(1)}, u32[]{:S(2)}, u32[]{:S(2)}) collective-permute-start(bf16[256,256]{1,0:T(8,128)(2,1)S(1)} %shard_map.145.refs_0_), channel_id=1, source_target_pairs={{0,24},{8,16},{16,8},{24,0},{1,25},{9,17},{17,9},{25,1},{2,26},{10... | collective-permute-start | bytes 393224 | tf_op jit(solution)/shard_map/ppermute | solution.py:362
  64.4 0.6 collective-permute-start.20
  65.1 1.4 %collective-permute-start.19 = (bf16[256,256]{1,0:T(8,128)(2,1)S(1)}, bf16[256,256]{1,0:T(8,128)(2,1)S(1)}, u32[]{:S(2)}, u32[]{:S(2)}) collective-permute-start(bf16[256,256]{1,0:T(8,128)(2,1)S(1)} %shard_map.145.refs_0_), channel_id=1, source_target_pairs={{0,8},{8,0},{16,24},{24,16},{1,9},{9,1},{17,25},{25,17},{2,10},{10... | collective-permute-start | bytes 393224 | tf_op jit(solution)/shard_map/ppermute | solution.py:362
  66.5 0.1 collective-permute-start.22
  66.6 2.9 %collective-permute-start.23 = (bf16[2,16,512]{2,1,0:T(8,128)(2,1)S(1)}, bf16[2,16,512]{2,1,0:T(8,128)(2,1)S(1)}, u32[]{:S(2)}, u32[]{:S(2)}) collective-permute-start(bf16[2,16,512]{2,1,0:T(8,128)(2,1)S(1)} %get-tuple-element.127), channel_id=1, source_target_pairs={{0,4},{1,5},{2,6},{3,7},{4,0},{5,1},{6,2},{7,3},{8,12},{9,13},{10,... | collective-permute-start | bytes 98312 | tf_op jit(solution)/shard_map/ppermute | solution.py:362
  69.5 0.8 %collective-permute-done.22.refs_5_ = bf16[2,16,512]{2,1,0:T(8,128)(2,1)S(1)} collective-permute-done((bf16[2,16,512]{2,1,0:T(8,128)(2,1)S(1)}, bf16[2,16,512]{2,1,0:T(8,128)(2,1)S(1)}, u32[]{:S(2)}, u32[]{:S(2)}) %collective-permute-start.22) | collective-permute-done | bytes 32800 | tf_op jit(solution)/shard_map/ppermute | solution.py:362
  70.4 2.5 %collective-permute-start.24 = (bf16[2,16,512]{2,1,0:T(8,128)(2,1)S(1)}, bf16[2,16,512]{2,1,0:T(8,128)(2,1)S(1)}, u32[]{:S(2)}, u32[]{:S(2)}) collective-permute-start(bf16[2,16,512]{2,1,0:T(8,128)(2,1)S(1)} %get-tuple-element.128), channel_id=1, source_target_pairs={{0,6},{1,7},{2,4},{3,5},{4,2},{5,3},{6,0},{7,1},{8,14},{9,15},{10,... | collective-permute-start | bytes 98312 | tf_op jit(solution)/shard_map/ppermute | solution.py:362
  72.9 3.2 %collective-permute-done.24.refs_7_ = bf16[2,16,512]{2,1,0:T(8,128)(2,1)S(1)} collective-permute-done((bf16[2,16,512]{2,1,0:T(8,128)(2,1)S(1)}, bf16[2,16,512]{2,1,0:T(8,128)(2,1)S(1)}, u32[]{:S(2)}, u32[]{:S(2)}) %collective-permute-start.24) | collective-permute-done | bytes 32800 | tf_op jit(solution)/shard_map/ppermute | solution.py:362
  76.2 0.5 collective-permute-start.27
  76.7 0.1 collective-permute-start.28
  76.8 1.0 %shard_map.146 = (bf16[128,256]{1,0:T(8,128)(2,1)}, bf16[128,256]{1,0:T(8,128)(2,1)}) custom-call(s32[1]{0:T(128)} %bitcast.idx, s32[1]{0:T(128)} %bitcast.1.hap, bf16[128,256]{1,0:T(8,128)(2,1)S(1)} %bitcast.23, f32[2,256]{1,0:T(2,128)S(1)} %pad_maximum_fusion.refs_4_.gain, bf16[4,192,256]{2,1,0:T(8,128)(2,1)S(1)} %bitcast.16, ...), custom_call_target="tpu_custom_call" | custom-call | flops 1 | bytes 1 | tf_op jit(solution)/shard_map/pallas_call | solution.py:82
  77.7 0.3 collective-permute-done.28.refs_7_
  78.0 1.5 %shard_map.147 = (f32[256,768]{1,0:T(8,128)}, f32[256,256]{1,0:T(8,128)}, f32[256,768]{1,0:T(8,128)}, f32[256,256]{1,0:T(8,128)}) custom-call(s32[1]{0:T(128)} %bitcast.idx, s32[1]{0:T(128)S(6)} %select_n.11.core, bf16[256,256]{1,0:T(8,128)(2,1)S(1)} %shard_map.145.refs_0_, bf16[256,256]{1,0:T(8,128)(2,1)S(1)} %collective-permute-done.25.refs_1_, ...), custom_call_target="tpu_custom_call" | custom-call | flops 1 | bytes 1 | tf_op jit(solution)/shard_map/pallas_call | solution.py:82
  (55 shorter events, 0.6 us)
Async XLA Ops:
  0.6 13.0 %collective-permute-start.2 = (bf16[128,256]{1,0:T(8,128)(2,1)}, bf16[128,256]{1,0:T(8,128)(2,1)S(1)}, u32[]{:S(2)}, u32[]{:S(2)}) collective-permute-start(bf16[128,256]{1,0:T(8,128)(2,1)} %bitcast.18), channel_id=1, source_target_pairs={{0,24},{8,16},{16,8},{24,0},{1,25},{9,17},{17,9},{25,1},{2,26},{10... | collective-permute-start | bytes 196616 | tf_op jit(solution)/shard_map/ppermute | solution.py:362
  4.6 9.1 %collective-permute-start.1 = (bf16[128,256]{1,0:T(8,128)(2,1)}, bf16[128,256]{1,0:T(8,128)(2,1)S(1)}, u32[]{:S(2)}, u32[]{:S(2)}) collective-permute-start(bf16[128,256]{1,0:T(8,128)(2,1)} %bitcast.19), channel_id=1, source_target_pairs={{0,16},{8,24},{16,0},{24,8},{1,17},{9,25},{17,1},{25,9},{2,18},{10... | collective-permute-start | bytes 196616 | tf_op jit(solution)/shard_map/ppermute | solution.py:362
  5.1 8.6 %collective-permute-start = (bf16[128,256]{1,0:T(8,128)(2,1)}, bf16[128,256]{1,0:T(8,128)(2,1)S(1)}, u32[]{:S(2)}, u32[]{:S(2)}) collective-permute-start(bf16[128,256]{1,0:T(8,128)(2,1)} %bitcast.20), channel_id=1, source_target_pairs={{0,8},{8,0},{16,24},{24,16},{1,9},{9,1},{17,25},{25,17},{2,10},{10... | collective-permute-start | bytes 196616 | tf_op jit(solution)/shard_map/ppermute | solution.py:362
  5.2 0.9 %copy-start.2 = (bf16[128,1,256]{2,0,1:T(8,128)(2,1)S(1)}, bf16[128,1,256]{2,0,1:T(8,128)(2,1)}, u32[]{:S(2)}) copy-start(bf16[128,1,256]{2,0,1:T(8,128)(2,1)} %param.9) | copy-start | bytes 196612
  6.1 0.8 %copy-start.7 = (bf16[128,1,256]{2,0,1:T(8,128)(2,1)S(1)}, bf16[128,1,256]{2,0,1:T(8,128)(2,1)}, u32[]{:S(2)}) copy-start(bf16[128,1,256]{2,0,1:T(8,128)(2,1)} %param.17) | copy-start | bytes 196612
  7.0 2.0 %collective-permute-start.3 = (bf16[4,16,512]{2,1,0:T(8,128)(2,1)S(1)}, bf16[4,16,512]{2,1,0:T(8,128)(2,1)S(1)}, u32[]{:S(2)}, u32[]{:S(2)}) collective-permute-start(bf16[4,16,512]{2,1,0:T(8,128)(2,1)S(1)} %get-tuple-element.76), channel_id=1, source_target_pairs={{0,1},{1,0},{2,3},{3,2},{4,5},{5,4},{6,7},{7,6},{8,9},{9,8},{10,11... | collective-permute-start | bytes 196616 | tf_op jit(solution)/shard_map/ppermute | solution.py:362
  8.3 0.7 copy-start.10
  8.3 0.7 copy-start.9
  9.0 4.7 %copy-start.3 = (bf16[128,1,256]{2,0,1:T(8,128)(2,1)S(1)}, bf16[128,1,256]{2,0,1:T(8,128)(2,1)}, u32[]{:S(2)}) copy-start(bf16[128,1,256]{2,0,1:T(8,128)(2,1)} %param.9) | copy-start | bytes 196612
  9.0 7.9 %collective-permute-start.4 = (bf16[2,16,512]{2,1,0:T(8,128)(2,1)S(1)}, bf16[2,16,512]{2,1,0:T(8,128)(2,1)S(1)}, u32[]{:S(2)}, u32[]{:S(2)}) collective-permute-start(bf16[2,16,512]{2,1,0:T(8,128)(2,1)S(1)} %get-tuple-element.78), channel_id=1, source_target_pairs={{0,2},{1,3},{2,0},{3,1},{4,6},{5,7},{6,4},{7,5},{8,10},{9,11},{10,... | collective-permute-start | bytes 98312 | tf_op jit(solution)/shard_map/ppermute | solution.py:362
  11.1 2.6 %copy-start.8 = (s32[4,4]{1,0:T(4,128)S(1)}, s32[4,4]{1,0:T(4,128)}, u32[]{:S(2)}) copy-start(s32[4,4]{1,0:T(4,128)} %link.1) | copy-start | bytes 196
  11.1 5.9 %collective-permute-start.5 = (bf16[2,16,512]{2,1,0:T(8,128)(2,1)S(1)}, bf16[2,16,512]{2,1,0:T(8,128)(2,1)S(1)}, u32[]{:S(2)}, u32[]{:S(2)}) collective-permute-start(bf16[2,16,512]{2,1,0:T(8,128)(2,1)S(1)} %get-tuple-element.79), channel_id=1, source_target_pairs={{0,4},{1,5},{2,6},{3,7},{4,0},{5,1},{6,2},{7,3},{8,12},{9,13},{10,... | collective-permute-start | bytes 98312 | tf_op jit(solution)/shard_map/ppermute | solution.py:362
  13.7 5.7 %collective-permute-start.6 = (bf16[2,16,512]{2,1,0:T(8,128)(2,1)S(1)}, bf16[2,16,512]{2,1,0:T(8,128)(2,1)S(1)}, u32[]{:S(2)}, u32[]{:S(2)}) collective-permute-start(bf16[2,16,512]{2,1,0:T(8,128)(2,1)S(1)} %get-tuple-element.80), channel_id=1, source_target_pairs={{0,6},{1,7},{2,4},{3,5},{4,2},{5,3},{6,0},{7,1},{8,14},{9,15},{10,... | collective-permute-start | bytes 98312 | tf_op jit(solution)/shard_map/ppermute | solution.py:362
  13.7 16.7 %copy-start.6 = (bf16[256,256]{1,0:T(8,128)(2,1)S(1)}, bf16[256,256]{1,0:T(8,128)(2,1)}, u32[]{:S(2)}) copy-start(bf16[256,256]{1,0:T(8,128)(2,1)} %col_out.1) | copy-start | bytes 393220
  19.4 11.1 %all-to-all-start = ((bf16[32,8,128]{2,1,0:T(8,128)(2,1)}), bf16[32,8,128]{2,1,0:T(8,128)(2,1)S(1)}, u32[]{:S(2)}, u32[]{:S(2)}) async-start(bf16[32,8,128]{2,1,0:T(8,128)(2,1)} %get-tuple-element.81), calls=%async_computation | async-start | bytes 131072 | tf_op jit(solution)/shard_map/all_to_all | solution.py:357
  23.1 1.0 %slice-start = ((bf16[256,768]{1,0:T(8,128)(2,1)}), bf16[256,512]{1,0:T(8,128)(2,1)S(1)}, s32[]{:S(2)}) async-start(bf16[256,768]{1,0:T(8,128)(2,1)} %col_proj.1), calls=%async_computation.2 | async-start | bytes 524288 | tf_op jit(solution)/shard_map/slice | solution.py:408
  24.0 6.4 %copy-start = (bf16[256,768]{1,0:T(8,128)(2,1)S(1)}, bf16[256,768]{1,0:T(8,128)(2,1)}, u32[]{:S(2)}) copy-start(bf16[256,768]{1,0:T(8,128)(2,1)} %col_proj.1) | copy-start | bytes 1179652
  24.0 6.4 %copy-start.5 = (bf16[256,256]{1,0:T(8,128)(2,1)S(1)}, bf16[256,256]{1,0:T(8,128)(2,1)}, u32[]{:S(2)}) copy-start(bf16[256,256]{1,0:T(8,128)(2,1)} %row_out.1) | copy-start | bytes 393220
  34.3 2.8 %collective-permute-start.7 = (bf16[128,1280]{1,0:T(8,128)(2,1)}, bf16[128,1280]{1,0:T(8,128)(2,1)S(1)}, u32[]{:S(2)}, u32[]{:S(2)}) collective-permute-start(bf16[128,1280]{1,0:T(8,128)(2,1)} %get-tuple-element.88), channel_id=1, source_target_pairs={{0,1},{1,0},{2,3},{3,2},{4,5},{5,4},{6,7},{7,6},{8,9},{9,8},{10,11... | collective-permute-start | bytes 983048 | tf_op jit(solution)/shard_map/ppermute | solution.py:362
  34.4 10.0 %all-to-all-start.1 = ((bf16[32,8,128]{2,1,0:T(8,128)(2,1)}), bf16[32,8,128]{2,1,0:T(8,128)(2,1)S(1)}, u32[]{:S(2)}, u32[]{:S(2)}) async-start(bf16[32,8,128]{2,1,0:T(8,128)(2,1)} %get-tuple-element.86), calls=%async_computation.1 | async-start | bytes 131072 | tf_op jit(solution)/shard_map/all_to_all | solution.py:357
  37.0 1.0 %copy-start.1 = (bf16[128,1280]{1,0:T(8,128)(2,1)S(1)}, bf16[128,1280]{1,0:T(8,128)(2,1)}, u32[]{:S(2)}) copy-start(bf16[128,1280]{1,0:T(8,128)(2,1)} %get-tuple-element.87.keep) | copy-start | bytes 983044
  38.2 9.6 %collective-permute-start.9 = (bf16[32,1280]{1,0:T(8,128)(2,1)S(1)}, bf16[32,1280]{1,0:T(8,128)(2,1)S(1)}, u32[]{:S(2)}, u32[]{:S(2)}) collective-permute-start(bf16[32,1280]{1,0:T(8,128)(2,1)S(1)} %get-tuple-element.90), channel_id=1, source_target_pairs={{0,8},{8,0},{16,24},{24,16},{1,9},{9,1},{17,25},{25,17},{2,10},{10... | collective-permute-start | bytes 245768 | tf_op jit(solution)/shard_map/ppermute | solution.py:362
  39.9 7.9 %collective-permute-start.10 = (bf16[32,1280]{1,0:T(8,128)(2,1)S(1)}, bf16[32,1280]{1,0:T(8,128)(2,1)S(1)}, u32[]{:S(2)}, u32[]{:S(2)}) collective-permute-start(bf16[32,1280]{1,0:T(8,128)(2,1)S(1)} %get-tuple-element.91), channel_id=1, source_target_pairs={{0,16},{8,24},{16,0},{24,8},{1,17},{9,25},{17,1},{25,9},{2,18},{10... | collective-permute-start | bytes 245768 | tf_op jit(solution)/shard_map/ppermute | solution.py:362
  41.4 6.4 %collective-permute-start.11 = (bf16[32,1280]{1,0:T(8,128)(2,1)S(1)}, bf16[32,1280]{1,0:T(8,128)(2,1)S(1)}, u32[]{:S(2)}, u32[]{:S(2)}) collective-permute-start(bf16[32,1280]{1,0:T(8,128)(2,1)S(1)} %get-tuple-element.92), channel_id=1, source_target_pairs={{0,24},{8,16},{16,8},{24,0},{1,25},{9,17},{17,9},{25,1},{2,26},{10... | collective-permute-start | bytes 245768 | tf_op jit(solution)/shard_map/ppermute | solution.py:362
  46.5 1.3 %collective-permute-start.8 = (bf16[96,256]{1,0:T(8,128)(2,1)S(1)}, bf16[96,256]{1,0:T(8,128)(2,1)S(1)}, u32[]{:S(2)}, u32[]{:S(2)}) collective-permute-start(bf16[96,256]{1,0:T(8,128)(2,1)S(1)} %get-tuple-element.100), channel_id=1, source_target_pairs={{0,1},{1,0},{2,3},{3,2},{4,5},{5,4},{6,7},{7,6},{8,9},{9,8},{10,11... | collective-permute-start | bytes 147464 | tf_op jit(solution)/shard_map/ppermute | solution.py:362
  47.8 4.5 %copy-start.4 = (bf16[8,16,512]{2,1,0:T(8,128)(2,1)S(1)}, bf16[8,16,512]{2,1,0:T(8,128)(2,1)}, u32[]{:S(2)}) copy-start(bf16[8,16,512]{2,1,0:T(8,128)(2,1)} %get-tuple-element.106.og) | copy-start | bytes 393220
  47.9 14.9 %collective-permute-start.14 = (bf16[256,256]{1,0:T(8,128)(2,1)S(1)}, bf16[256,256]{1,0:T(8,128)(2,1)S(1)}, u32[]{:S(2)}, u32[]{:S(2)}) collective-permute-start(bf16[256,256]{1,0:T(8,128)(2,1)S(1)} %shard_map.142.refs_0_), channel_id=1, source_target_pairs={{0,6},{1,7},{2,4},{3,5},{4,2},{5,3},{6,0},{7,1},{8,14},{9,15},{10,... | collective-permute-start | bytes 393224 | tf_op jit(solution)/shard_map/ppermute | solution.py:362
  50.3 12.5 %collective-permute-start.13 = (bf16[256,256]{1,0:T(8,128)(2,1)S(1)}, bf16[256,256]{1,0:T(8,128)(2,1)S(1)}, u32[]{:S(2)}, u32[]{:S(2)}) collective-permute-start(bf16[256,256]{1,0:T(8,128)(2,1)S(1)} %shard_map.142.refs_0_), channel_id=1, source_target_pairs={{0,4},{1,5},{2,6},{3,7},{4,0},{5,1},{6,2},{7,3},{8,12},{9,13},{10,... | collective-permute-start | bytes 393224 | tf_op jit(solution)/shard_map/ppermute | solution.py:362
  50.3 12.5 %collective-permute-start.12 = (bf16[256,256]{1,0:T(8,128)(2,1)S(1)}, bf16[256,256]{1,0:T(8,128)(2,1)S(1)}, u32[]{:S(2)}, u32[]{:S(2)}) collective-permute-start(bf16[256,256]{1,0:T(8,128)(2,1)S(1)} %shard_map.142.refs_0_), channel_id=1, source_target_pairs={{0,2},{1,3},{2,0},{3,1},{4,6},{5,7},{6,4},{7,5},{8,10},{9,11},{10,... | collective-permute-start | bytes 393224 | tf_op jit(solution)/shard_map/ppermute | solution.py:362
  52.4 5.3 %collective-permute-start.18 = (bf16[4,16,512]{2,1,0:T(8,128)(2,1)S(1)}, bf16[4,16,512]{2,1,0:T(8,128)(2,1)S(1)}, u32[]{:S(2)}, u32[]{:S(2)}) collective-permute-start(bf16[4,16,512]{2,1,0:T(8,128)(2,1)S(1)} %get-tuple-element.108), channel_id=1, source_target_pairs={{0,1},{1,0},{2,3},{3,2},{4,5},{5,4},{6,7},{7,6},{8,9},{9,8},{10,11... | collective-permute-start | bytes 196616 | tf_op jit(solution)/shard_map/ppermute | solution.py:362
  52.5 4.5 %collective-permute-start.15 = (bf16[128,192]{1,0:T(8,128)(2,1)S(1)}, bf16[128,192]{1,0:T(8,128)(2,1)S(1)}, u32[]{:S(2)}, u32[]{:S(2)}) collective-permute-start(bf16[128,192]{1,0:T(8,128)(2,1)S(1)} %get-tuple-element.102), channel_id=1, source_target_pairs={{0,8},{8,0},{16,24},{24,16},{1,9},{9,1},{17,25},{25,17},{2,10},{10... | collective-permute-start | bytes 147464 | tf_op jit(solution)/shard_map/ppermute | solution.py:362
  57.0 5.0 %collective-permute-start.16 = (bf16[128,192]{1,0:T(8,128)(2,1)S(1)}, bf16[128,192]{1,0:T(8,128)(2,1)S(1)}, u32[]{:S(2)}, u32[]{:S(2)}) collective-permute-start(bf16[128,192]{1,0:T(8,128)(2,1)S(1)} %get-tuple-element.103), channel_id=1, source_target_pairs={{0,16},{8,24},{16,0},{24,8},{1,17},{9,25},{17,1},{25,9},{2,18},{10... | collective-permute-start | bytes 147464 | tf_op jit(solution)/shard_map/ppermute | solution.py:362
  57.7 5.2 %collective-permute-start.17 = (bf16[128,192]{1,0:T(8,128)(2,1)S(1)}, bf16[128,192]{1,0:T(8,128)(2,1)S(1)}, u32[]{:S(2)}, u32[]{:S(2)}) collective-permute-start(bf16[128,192]{1,0:T(8,128)(2,1)S(1)} %get-tuple-element.104), channel_id=1, source_target_pairs={{0,24},{8,16},{16,8},{24,0},{1,25},{9,17},{17,9},{25,1},{2,26},{10... | collective-permute-start | bytes 147464 | tf_op jit(solution)/shard_map/ppermute | solution.py:362
  62.9 13.2 %collective-permute-start.21 = (bf16[256,256]{1,0:T(8,128)(2,1)S(1)}, bf16[256,256]{1,0:T(8,128)(2,1)S(1)}, u32[]{:S(2)}, u32[]{:S(2)}) collective-permute-start(bf16[256,256]{1,0:T(8,128)(2,1)S(1)} %shard_map.145.refs_0_), channel_id=1, source_target_pairs={{0,24},{8,16},{16,8},{24,0},{1,25},{9,17},{17,9},{25,1},{2,26},{10... | collective-permute-start | bytes 393224 | tf_op jit(solution)/shard_map/ppermute | solution.py:362
  64.4 11.7 %collective-permute-start.20 = (bf16[256,256]{1,0:T(8,128)(2,1)S(1)}, bf16[256,256]{1,0:T(8,128)(2,1)S(1)}, u32[]{:S(2)}, u32[]{:S(2)}) collective-permute-start(bf16[256,256]{1,0:T(8,128)(2,1)S(1)} %shard_map.145.refs_0_), channel_id=1, source_target_pairs={{0,16},{8,24},{16,0},{24,8},{1,17},{9,25},{17,1},{25,9},{2,18},{10... | collective-permute-start | bytes 393224 | tf_op jit(solution)/shard_map/ppermute | solution.py:362
  65.1 11.0 %collective-permute-start.19 = (bf16[256,256]{1,0:T(8,128)(2,1)S(1)}, bf16[256,256]{1,0:T(8,128)(2,1)S(1)}, u32[]{:S(2)}, u32[]{:S(2)}) collective-permute-start(bf16[256,256]{1,0:T(8,128)(2,1)S(1)} %shard_map.145.refs_0_), channel_id=1, source_target_pairs={{0,8},{8,0},{16,24},{24,16},{1,9},{9,1},{17,25},{25,17},{2,10},{10... | collective-permute-start | bytes 393224 | tf_op jit(solution)/shard_map/ppermute | solution.py:362
  66.5 3.9 %collective-permute-start.22 = (bf16[2,16,512]{2,1,0:T(8,128)(2,1)S(1)}, bf16[2,16,512]{2,1,0:T(8,128)(2,1)S(1)}, u32[]{:S(2)}, u32[]{:S(2)}) collective-permute-start(bf16[2,16,512]{2,1,0:T(8,128)(2,1)S(1)} %get-tuple-element.126), channel_id=1, source_target_pairs={{0,2},{1,3},{2,0},{3,1},{4,6},{5,7},{6,4},{7,5},{8,10},{9,11},{10,... | collective-permute-start | bytes 98312 | tf_op jit(solution)/shard_map/ppermute | solution.py:362
  66.6 6.3 %collective-permute-start.23 = (bf16[2,16,512]{2,1,0:T(8,128)(2,1)S(1)}, bf16[2,16,512]{2,1,0:T(8,128)(2,1)S(1)}, u32[]{:S(2)}, u32[]{:S(2)}) collective-permute-start(bf16[2,16,512]{2,1,0:T(8,128)(2,1)S(1)} %get-tuple-element.127), channel_id=1, source_target_pairs={{0,4},{1,5},{2,6},{3,7},{4,0},{5,1},{6,2},{7,3},{8,12},{9,13},{10,... | collective-permute-start | bytes 98312 | tf_op jit(solution)/shard_map/ppermute | solution.py:362
  70.4 5.7 %collective-permute-start.24 = (bf16[2,16,512]{2,1,0:T(8,128)(2,1)S(1)}, bf16[2,16,512]{2,1,0:T(8,128)(2,1)S(1)}, u32[]{:S(2)}, u32[]{:S(2)}) collective-permute-start(bf16[2,16,512]{2,1,0:T(8,128)(2,1)S(1)} %get-tuple-element.128), channel_id=1, source_target_pairs={{0,6},{1,7},{2,4},{3,5},{4,2},{5,3},{6,0},{7,1},{8,14},{9,15},{10,... | collective-permute-start | bytes 98312 | tf_op jit(solution)/shard_map/ppermute | solution.py:362
  72.9 4.8 %collective-permute-start.25 = (bf16[256,256]{1,0:T(8,128)(2,1)S(1)}, bf16[256,256]{1,0:T(8,128)(2,1)S(1)}, u32[]{:S(2)}, u32[]{:S(2)}) collective-permute-start(bf16[256,256]{1,0:T(8,128)(2,1)S(1)} %shard_map.145.refs_0_), channel_id=1, source_target_pairs={{0,1},{1,0},{2,3},{3,2},{4,5},{5,4},{6,7},{7,6},{8,9},{9,8},{10,11... | collective-permute-start | bytes 393224 | tf_op jit(solution)/shard_map/ppermute | solution.py:362
  76.1 1.6 %collective-permute-start.26 = (bf16[256,256]{1,0:T(8,128)(2,1)S(1)}, bf16[256,256]{1,0:T(8,128)(2,1)S(1)}, u32[]{:S(2)}, u32[]{:S(2)}) collective-permute-start(bf16[256,256]{1,0:T(8,128)(2,1)S(1)} %collective-permute-done.19.refs_2_), channel_id=1, source_target_pairs={{0,1},{1,0},{2,3},{3,2},{4,5},{5,4},{6,7},{7,6},{8,9},{9,8},{10,11... | collective-permute-start | bytes 393224 | tf_op jit(solution)/shard_map/ppermute | solution.py:362
  76.2 1.5 %collective-permute-start.27 = (bf16[256,256]{1,0:T(8,128)(2,1)S(1)}, bf16[256,256]{1,0:T(8,128)(2,1)S(1)}, u32[]{:S(2)}, u32[]{:S(2)}) collective-permute-start(bf16[256,256]{1,0:T(8,128)(2,1)S(1)} %collective-permute-done.20.refs_4_), channel_id=1, source_target_pairs={{0,1},{1,0},{2,3},{3,2},{4,5},{5,4},{6,7},{7,6},{8,9},{9,8},{10,11... | collective-permute-start | bytes 393224 | tf_op jit(solution)/shard_map/ppermute | solution.py:362
  76.7 1.3 %collective-permute-start.28 = (bf16[256,256]{1,0:T(8,128)(2,1)S(1)}, bf16[256,256]{1,0:T(8,128)(2,1)S(1)}, u32[]{:S(2)}, u32[]{:S(2)}) collective-permute-start(bf16[256,256]{1,0:T(8,128)(2,1)S(1)} %collective-permute-done.21.refs_6_), channel_id=1, source_target_pairs={{0,1},{1,0},{2,3},{3,2},{4,5},{5,4},{6,7},{7,6},{8,9},{9,8},{10,11... | collective-permute-start | bytes 393224 | tf_op jit(solution)/shard_map/ppermute | solution.py:362

commit v7 on v6

--- a/solution.py
+++ b/solution.py
@@ -91,65 +91,73 @@
     )(*operands)
 
 
+def linked_scores(scores, rows, sites, me, b, link):
+    return [
+        scores[a * rows : (a + 1) * rows] + jnp.where(link[me ^ b, me ^ a] > 0, 0.0, -jnp.inf)
+        for a in range(sites)
+    ]
+
+
+def exp_parts(parts):
+    high = functools.reduce(jnp.maximum, [jnp.max(part, axis=0, keepdims=True) for part in parts])
+    parts = [jnp.exp2(part - high) for part in parts]
+    total = sum(jnp.sum(part, axis=0, keepdims=True) for part in parts)
+    return parts, 1.0 / total
+
+
 def row_forward(sites, haps, idx, link, *refs):
     pieces = refs[:sites]
-    gain, w_t = refs[sites : sites + 2]
-    att_out, p_out, q_out, v_out, kt_out, n_out = refs[sites + 2 :]
+    cot, gain, w_t, row_out, x_out, n_out = refs[sites:]
     me = idx[0]
-    rows = pieces[0].shape[0]
-    width = q_out.shape[1]
+    rows, width = cot.shape
+    heads = width // HEAD_DIM
     for k in range(sites):
         xhat, _ = norm_parts(pieces[k][...].astype(F32))
         n_out[k * rows : (k + 1) * rows, :] = (xhat * gain[:1, :]).astype(BF16)
     normed = n_out[...]
-    q = mm_nt(normed, w_t[:width, :]).astype(BF16)
+    q = mm_nt(normed[:rows], w_t[:width, :]).astype(BF16)
     key = mm_nt(normed, w_t[width : 2 * width, :]).astype(BF16)
+    v_t = mm_nt(w_t[2 * width :, :], normed).astype(BF16)
+    q_st = jnp.concatenate([only_head(q, h) for h in range(heads)], axis=0)
+    att_t = []
+    for h in range(heads):
+        scores = mm_nt(key, q_st[h * rows : (h + 1) * rows]) * (SCALE * LOG2E)
+        parts, inverse = exp_parts(linked_scores(scores, rows, sites, me, 0, link))
+        e_h = jnp.concatenate([part.astype(BF16) for part in parts], axis=0)
+        att_t.append(mm(v_t[h * HEAD_DIM : (h + 1) * HEAD_DIM], e_h) * inverse)
+    att = jnp.transpose(jnp.concatenate(att_t, axis=0)).astype(BF16)
+    hid = pieces[0][...].astype(F32) + mm(att, row_out[...])
+    joined = jnp.concatenate([hid, cot[...].astype(F32), att.astype(F32)], axis=1)
+    x_out[...] = joined.reshape(haps, rows // haps, 3 * width).astype(BF16)
+
+
+def row_probs(sites, idx, link, normed_ref, w_t, p_out, q_out, v_out, kt_out):
+    me = idx[0]
+    normed = normed_ref[...]
+    total, width = q_out.shape
+    full = normed.shape[1]
+    rows = total // sites
+
+    def weights(part):
+        return w_t[pl.ds(pl.multiple_of(part * full + me * width, width), width), :]
+
+    q = mm_nt(normed, weights(0)).astype(BF16)
+    key = mm_nt(normed, weights(1)).astype(BF16)
     q_out[...] = q
-    v_out[...] = mm_nt(normed, w_t[2 * width :, :]).astype(BF16)
-    kt_out[...] = mm_nt(w_t[width : 2 * width, :], normed).astype(BF16)
-    v_t = mm_nt(w_t[2 * width :, :], normed).astype(BF16)
-    att_t = []
+    v_out[...] = mm_nt(normed, weights(2)).astype(BF16)
+    kt_out[...] = mm_nt(weights(1), normed).astype(BF16)
     for h in range(width // HEAD_DIM):
         key_h = only_head(key, h)
         for b in range(sites):
             here = pl.ds(b * rows, rows)
             scores = mm_nt(key_h, q[b * rows : (b + 1) * rows]) * (SCALE * LOG2E)
-            parts = [
-                scores[a * rows : (a + 1) * rows]
-                + jnp.where(link[me ^ b, me ^ a] > 0, 0.0, -jnp.inf)
-                for a in range(sites)
-            ]
-            high = functools.reduce(
-                jnp.maximum, [jnp.max(part, axis=0, keepdims=True) for part in parts]
-            )
-            parts = [jnp.exp2(part - high) for part in parts]
-            total = sum(jnp.sum(part, axis=0, keepdims=True) for part in parts)
-            inverse = 1.0 / total
+            parts, inverse = exp_parts(linked_scores(scores, rows, sites, me, b, link))
             for a in range(sites):
                 p_out[h, a * rows : (a + 1) * rows, here] = (parts[a] * inverse).astype(BF16)
-        att_t.append(mm(v_t[h * HEAD_DIM : (h + 1) * HEAD_DIM], p_out[h]))
-    att = jnp.transpose(jnp.concatenate(att_t, axis=0))
-    for b in range(sites):
-        att_out[pl.ds((me ^ b) * haps, haps)] = pack_block(att[b * rows : (b + 1) * rows], haps)
-
-
-def join_inputs(haps, hap, feats, cot, keep, send, both):
-    count, per, width = both.shape
-    joined = jnp.concatenate([feats[...].astype(F32), cot[...].astype(F32)], axis=1)
-    both[...] = joined.reshape(count, per, width).astype(BF16)
-    for m in range(haps // 2):
-        keep[m] = both[hap[0] ^ (2 * m)]
-        send[m] = both[hap[0] ^ (2 * m + 1)]
-
-
-def relay_inputs(keep, got, *outs):
-    for m, out in enumerate(outs):
-        out[0] = keep[m]
-        out[1] = got[m]
-
-
-def column_step(sites, haps, hap, at, row_out, gain, col_proj, kv_t_w, col_out, *refs):
-    ga_out, send, keep, og_out, xc, og, w_all, sems = refs[haps // 2 :]
+
+
+def column_step(sites, haps, hap, x_in, row_out, gain, col_proj, kv_t_w, col_out, *refs):
+    ga_out, send, keep, og_out, og, w_all, sems = refs
     core = hap[0] % 2
     half = row_out.shape[0] // 2
     mine = pl.ds(pl.multiple_of(core * half, half), half)
@@ -158,22 +166,16 @@
     def save(j, cols):
         return pltpu.make_async_copy(w_all.at[mine, cols], keep.at[:, cols], sems.at[j])
 
-    for m in range(haps // 2):
-        xc[hap[0] ^ (2 * m)] = refs[m][0]
-        xc[hap[0] ^ (2 * m + 1)] = refs[m][1]
     width = row_out.shape[0]
     heads = width // HEAD_DIM
     group = width // sites
-    xc_all = flat_rows(xc[...], F32)
-    rows = xc_all.shape[0]
+    x_all = flat_rows(x_in[...], F32)
+    rows = x_all.shape[0]
     per = rows // haps
-    cot_f = xc_all[:, width:]
+    hid = x_all[:, :width]
+    cot_f = x_all[:, width : 2 * width]
     cot = cot_f.astype(BF16)
-    hid = xc_all[:, :width]
-    a_blocks = [unpack_block(at[i * haps : (i + 1) * haps], group) for i in range(sites)]
-    for i in range(sites):
-        hid = hid + mm(a_blocks[i], row_out[i * group : (i + 1) * group, :])
-    hid = hid.astype(BF16).astype(F32)
+    row_att = x_all[:, 2 * width :].astype(BF16)
     grad_att = mm_nt(cot, col_out[...]).astype(BF16)
     xhat, rstd = norm_parts(hid)
     normed = (xhat * gain[1:2, :]).astype(BF16)
@@ -226,8 +228,7 @@
     for i in range(sites):
         g_i = mm_nt(grad_hidden, row_out[i * group : (i + 1) * group, :])
         ga_out[i * haps : (i + 1) * haps] = pack_block(g_i, haps)
-    for i in range(sites):
-        w_all[i * group : (i + 1) * group, 4 * width :] = mm_tn(a_blocks[i], grad_hidden).astype(BF16)
+    w_all[:, 4 * width :] = mm_tn(row_att, grad_hidden).astype(BF16)
     second = save(1, slice(4 * width, 5 * width))
     second.start()
     both = jnp.concatenate([out, grad_hidden.astype(F32)], axis=1)
@@ -294,38 +295,59 @@
         gp_outs[b][...] = joined[b * rows : (b + 1) * rows]
 
 
-def row_finish(sites, haps, idx, hap, feats, gain, w_all, *refs):
-    gps, ogs = refs[:sites], refs[sites : sites + haps // 2]
-    out_ref, gf_ref, og = refs[sites + haps // 2 :]
+def row_finish(sites, haps, idx, hap, feats, gain, w_t, gp, *refs):
+    gps, parts = refs[: sites - 1], refs[sites - 1 : sites - 1 + haps // 2]
+    out_ref, gf_ref, og = refs[sites - 1 + haps // 2 :]
     me = idx[0]
-    width = feats.shape[1]
+    rows, width = feats.shape
+    group = width // sites
+    per = rows // haps
     for m in range(haps // 2):
-        og[hap[0] ^ (2 * m)] = ogs[m][0]
-        og[hap[0] ^ (2 * m + 1)] = ogs[m][1]
-    both = flat_rows(og[...], F32)
-    grad_normed = sum(mm(gps[k][...], w_all[me ^ k]) for k in range(sites))
+        base = parts[m].shape[0] - 4 * per
+        for j in range(2):
+            for side in range(2):
+                start = base + (2 * j + side) * per
+                og[side, hap[0] ^ (2 * m + j)] = parts[m][start : start + per, :].astype(F32)
+    grads = [gp[...]] + [g[g.shape[0] - rows :, : 3 * group] for g in gps]
+    grad_normed = 0.0
+    for k in range(sites):
+        place = [pl.multiple_of(p * width + (me ^ k) * group, group) for p in range(3)]
+        weights = jnp.concatenate([w_t[pl.ds(p, group), :] for p in place], axis=0)
+        grad_normed = grad_normed + mm(grads[k], weights)
     xhat, rstd = norm_parts(feats[...].astype(F32))
-    grad = both[:, width:] + norm_back(xhat, rstd, gain[:1, :], grad_normed)
-    out_ref[...] = both[:, :width].astype(BF16)
+    grad = og[1].reshape(rows, width) + norm_back(xhat, rstd, gain[:1, :], grad_normed)
+    out_ref[...] = og[0].reshape(rows, width).astype(BF16)
     gf_ref[...] = grad.astype(BF16)
 
 
-def weights_join(row_keep, row_got, *refs):
-    cols, out = refs[:-1], refs[-1]
+def weights_join(sites, row_keep, row_got, og_keep, og_got, *refs):
+    cols, outs = refs[:sites], refs[sites:]
     half, width = row_keep.shape
-    out[:half, :] = (row_keep[...].astype(F32) + row_got[...].astype(F32)).astype(BF16)
+    depth = half + 5 * cols[0].shape[0]
+    per = og_keep.shape[1]
     total = sum(c[...].astype(F32) for c in cols)
-    part = total.shape[0]
-    for t in range(5):
-        tile = total[:, t * width : (t + 1) * width]
-        out[half + t * part : half + (t + 1) * part, :] = tile.astype(BF16)
-
-
-def weights_sum(*refs):
-    terms = [r[...].astype(F32) for r in refs[:-1]]
+    tiles = [total[:, t * width : (t + 1) * width] for t in range(5)]
+    rows = row_keep[...].astype(F32) + row_got[...].astype(F32)
+    joined = jnp.concatenate([rows] + tiles, axis=0).astype(BF16)
+    for m, out in enumerate(outs):
+        out[:depth, :] = joined
+        both = [og_keep[m].astype(F32), og_got[m].astype(F32)]
+        both = [x[:, j * width : (j + 1) * width] for x in both for j in range(2)]
+        out[depth:, :] = jnp.concatenate(both, axis=0).astype(BF16)
+
+
+def weights_sum(haps, sites, *refs):
+    parts, gps = refs[: haps // 2], refs[haps // 2 : haps // 2 + sites - 1]
+    mine, outs = refs[haps // 2 + sites - 1], refs[haps // 2 + sites :]
+    depth, width = mine.shape
+    terms = [r[:depth, :].astype(F32) for r in parts]
     while len(terms) > 1:
         terms = [a + b for a, b in zip(terms[::2], terms[1::2])]
-    refs[-1][...] = terms[0].astype(BF16)
+    mine[...] = terms[0].astype(BF16)
+    for gp, out in zip(gps, outs):
+        out[:depth, :] = mine[...]
+        out[depth:, : gp.shape[1]] = gp[...]
+        out[depth:, gp.shape[1] :] = jnp.zeros((gp.shape[0], width - gp.shape[1]), BF16)
 
 
 def weights_finish(sites, idx, core, *refs):
@@ -392,35 +414,26 @@
 
     pieces = [feats] + [swapped(feats, "site", k) for k in range(1, sites)]
     gains = jnp.stack([row_gain, column_norm_gain])
-    keep, send = call(
-        functools.partial(join_inputs, haps),
-        [((haps // 2, per, 2 * width), BF16)] * 2,
-        hap, feats, cot, scalars=1,
-        scratch=[pltpu.VMEM((haps, per, 2 * width), BF16)],
-    )
-    got = swapped(send, "hap", 1)
-    xcs = call(relay_inputs, [((2, per, 2 * width), BF16)] * (haps // 2), keep, got)
-    xcs = [xcs[0]] + [swapped(xcs[m], "hap", 2 * m) for m in range(1, haps // 2)]
-    w_all = jnp.transpose(row_proj.reshape(width, 3, sites, group), (2, 1, 3, 0)).reshape(
-        sites, 3 * group, width
-    )
-    w_t = lax.dynamic_index_in_dim(w_all, me, 0, keepdims=False)
+    w_t = jnp.transpose(row_proj)
     kv_t_w = jnp.transpose(col_proj[:, width:])
 
-    att, prob, q, val, key_t, normed = call(
+    x_out, normed = call(
         functools.partial(row_forward, sites, haps),
+        [((haps, per, 3 * width), BF16), ((total, width), BF16)],
+        idx, link_pattern, *pieces, cot, gains, w_t, row_out, scalars=2,
+    )
+    x_in = exchange(x_out, "hap")
+    prob, q, val, key_t = call(
+        functools.partial(row_probs, sites),
         [
-            block,
             ((heads, total, total), BF16),
             ((total, group), BF16),
             ((total, group), BF16),
             ((group, total), BF16),
-            ((total, width), BF16),
         ],
-        idx, link_pattern, *pieces, gains, w_t, scalars=2, us=20,
-    )
-    att, xcs = lax.optimization_barrier((att, xcs))
-    at = exchange(att, both_axes)
+        idx, link_pattern, normed, w_t, scalars=2, us=20,
+    )
+    x_in, _ = lax.optimization_barrier((x_in, prob))
     half = width // 2
     ga, col_send, col_keep, og = call(
         functools.partial(column_step, sites, haps),
@@ -430,9 +443,8 @@
             ((half, 5 * width), BF16),
             ((haps, per, 2 * width), BF16),
         ],
-        hap, at, row_out, gains, col_proj, kv_t_w, col_out, *xcs, scalars=1, far=2,
+        hap, x_in, row_out, gains, col_proj, kv_t_w, col_out, scalars=1, far=2,
         scratch=[
-            pltpu.VMEM((haps, per, 2 * width), BF16),
             pltpu.VMEM((haps, per, 2 * width), BF16),
             pltpu.VMEM((width, 5 * width), BF16),
             pltpu.SemaphoreType.DMA((3,)),
@@ -446,7 +458,11 @@
         idx, col_keep, *col_got, scalars=1, us=0,
         scratch=[pltpu.VMEM((half, 5 * width), BF16)],
     )
-    g_in, _ = lax.optimization_barrier((g_in, cols))
+    og_keep, og_send = call(
+        split_outputs, [((haps // 2, per, 2 * width), BF16)] * 2, hap, og, scalars=1
+    )
+    og_got = swapped(og_send, "hap", 1)
+    g_in, _ = lax.optimization_barrier((g_in, (cols, og_got)))
     cols = [cols[0]] + [swapped(cols[k], "site", k) for k in range(1, sites)]
     *gps, row_keep, row_send = call(
         functools.partial(row_backward, sites, haps),
@@ -460,28 +476,24 @@
     )
     row_got = swapped(row_send, "hap", 1)
     depth = 3 * group // 2 + 5 * half // sites
-    (joined,) = call(weights_join, [((depth, width), BF16)], row_keep, row_got, *cols)
-    parts = [joined] + [swapped(joined, "hap", 2 * m) for m in range(1, haps // 2)]
-    gps = [gps[0]] + [swapped(gps[k], "site", k) for k in range(1, sites)]
-    og, _ = lax.optimization_barrier((og, joined))
-    og_keep, og_send = call(
-        split_outputs, [((haps // 2, per, 2 * width), BF16)] * 2, hap, og, scalars=1
-    )
-    og_got = swapped(og_send, "hap", 1)
-    ogs = call(relay_inputs, [((2, per, 2 * width), BF16)] * (haps // 2), og_keep, og_got)
-    parts, gps, ogs = lax.optimization_barrier((parts, gps, ogs))
-    (mine,) = call(weights_sum, [((depth, width), BF16)], *parts)
-    mine_swapped = swapped(mine, "hap", 1)
-    ogs, _ = lax.optimization_barrier((ogs, mine))
-    ogs = [ogs[0]] + [swapped(ogs[m], "hap", 2 * m) for m in range(1, haps // 2)]
-    full = [swapped(mine, "site", k) for k in range(1, sites)]
-    full, ogs = lax.optimization_barrier((full, ogs))
-    full = [mine, mine_swapped] + [x for p in full for x in (p, swapped(p, "hap", 1))]
+    parts = call(
+        functools.partial(weights_join, sites),
+        [((depth + 4 * per, width), BF16)] * (haps // 2),
+        row_keep, row_got, og_keep, og_got, *cols,
+    )
+    parts = [parts[0]] + [swapped(parts[m], "hap", 2 * m) for m in range(1, haps // 2)]
+    mine, *sends = call(
+        functools.partial(weights_sum, haps, sites),
+        [((depth, width), BF16)] + [((depth + rows, width), BF16)] * (sites - 1),
+        *parts, *gps[1:],
+    )
+    got = [swapped(sends[k - 1], "site", k) for k in range(1, sites)]
+    full = [x for p in [mine] + got for x in (p, swapped(p, "hap", 1))]
     out, grad = call(
         functools.partial(row_finish, sites, haps),
         [((rows, width), BF16)] * 2,
-        idx, hap, feats, gains, w_all, *gps, *ogs, scalars=2,
-        scratch=[pltpu.VMEM((haps, per, 2 * width), BF16)],
+        idx, hap, feats, gains, w_t, gps[0], *got, *parts, scalars=2,
+        scratch=[pltpu.VMEM((2, haps, per, width), F32)],
     )
     rp, ro, cp, co = call(
         functools.partial(weights_finish, sites),

time: 79.9 us -> 75.5 us (0.945)
  the two profiles are of different devices: /device:TPU:0 before, /device:TPU:9 now
where the time goes in v7:
time: 75.5 us; the launch traced here: 75.1 us
  starting transfers between devices  31.3 us (41%)
  waiting for transfers between devices  24.6 us (33%)
  Pallas kernels  14.8 us (20%)
  local copies, waits for them, and re-layouts  3.61 us (5%)
  between operations  0.8 us (1%)
    ppermute x19, starting transfers between devices, swapped(): return lax.ppermute(value, axis, [(i, i ^ by) for i in range(length)])  20.7 us
    ppermute x19, waiting for transfers between devices, swapped(): return lax.ppermute(value, axis, [(i, i ^ by) for i in range(length)])  18.5 us
    pallas_call x10, Pallas kernels, call(): pl.pallas_call(body, out_shape=[jax.ShapeDtypeStruct(s, d) for s, d in ou...  14.8 us
    all_to_all x2, starting transfers between devices, exchange(): return lax.all_to_all(value, axis, 0, 0, tiled=True)  10.6 us
    all_to_all x2, waiting for transfers between devices, exchange(): return lax.all_to_all(value, axis, 0, 0, tiled=True)  6.09 us
    unnamed x24, local copies, waits for them, and re-layouts  2.66 us
  transfers between devices with their start and end apart: 21, of which 10 were waited for; matrix products, arithmetic and copies ran while one was open for 0% of the time, Pallas kernels for 7%

profile of v7, /device:TPU:9, one launch (start us, length us, event | category | flops | bytes accessed | tf_op | source)
XLA Modules:
  0.0 75.1 jit_solution(6505200327617294668)
XLA Ops:
  0.6 2.2 %collective-permute-start.2 = (bf16[128,256]{1,0:T(8,128)(2,1)}, bf16[128,256]{1,0:T(8,128)(2,1)S(1)}, u32[]{:S(2)}, u32[]{:S(2)}) collective-permute-start(bf16[128,256]{1,0:T(8,128)(2,1)} %bitcast.14), channel_id=1, source_target_pairs={{0,24},{8,16},{16,8},{24,0},{1,25},{9,17},{17,9},{25,1},{2,26},{10... | collective-permute-start | bytes 196616 | tf_op jit(solution)/shard_map/ppermute | solution.py:384
  2.9 0.2 collective-permute-start.1
  3.1 0.3 collective-permute-start
  3.4 0.9 %slice-done = bf16[256,512]{1,0:T(8,128)(2,1)S(1)} async-done(((bf16[256,768]{1,0:T(8,128)(2,1)}), bf16[256,512]{1,0:T(8,128)(2,1)S(1)}, s32[]{:S(2)}) %slice-start) | async-done | bytes 262168 | tf_op jit(solution)/shard_map/slice | solution.py:418
  4.3 0.1 copy.17
  4.4 0.0 copy-start.10
  4.5 0.0 copy-start.1
  4.5 0.2 copy.15
  4.7 0.4 copy-done.10
  5.1 0.2 copy-done.9
  5.4 1.4 %collective-permute-done.1.refs_2_ = bf16[128,256]{1,0:T(8,128)(2,1)S(1)} collective-permute-done((bf16[128,256]{1,0:T(8,128)(2,1)}, bf16[128,256]{1,0:T(8,128)(2,1)S(1)}, u32[]{:S(2)}, u32[]{:S(2)}) %collective-permute-start.1) | collective-permute-done | bytes 65568 | tf_op jit(solution)/shard_map/ppermute | solution.py:384
  6.8 0.1 collective-permute-done.refs_1_
  6.8 0.7 copy-done.7
  7.5 4.8 %shard_map.136 = (bf16[8,16,768]{2,1,0:T(8,128)(2,1)}, bf16[512,256]{1,0:T(8,128)(2,1)S(1)}) custom-call(s32[1]{0:T(128)} %bitcast.idx, s32[4,4]{1,0:T(4,128)S(1)} %copy-done.7, bf16[128,256]{1,0:T(8,128)(2,1)S(1)} %bitcast.17, bf16[128,256]{1,0:T(8,128)(2,1)S(1)} %collective-permute-done.refs_1_, bf16[128,256]{1,0:T(8,128)(2,1)S(1)} %collective-permute-done.1.refs_2_, ...), custom_call_target="tpu_custom_call" | custom-call | flops 1 | bytes 1 | tf_op jit(solution)/shard_map/pallas_call | solution.py:82
  12.3 6.9 %all-to-all-start = ((bf16[8,16,768]{2,1,0:T(8,128)(2,1)}), bf16[8,16,768]{2,1,0:T(8,128)(2,1)S(1)}, u32[]{:S(2)}, u32[]{:S(2)}) async-start(bf16[8,16,768]{2,1,0:T(8,128)(2,1)} %get-tuple-element.44), calls=%async_computation | async-start | bytes 393216 | tf_op jit(solution)/shard_map/all_to_all | solution.py:379
  19.2 1.7 %shard_map.137 = (bf16[2,512,512]{2,1,0:T(8,128)(2,1)S(1)}, bf16[512,64]{1,0:T(8,128)(2,1)S(1)}, bf16[512,64]{1,0:T(8,128)(2,1)S(1)}, bf16[64,512]{1,0:T(8,128)(2,1)S(1)}) custom-call(s32[1]{0:T(128)} %bitcast.idx, s32[4,4]{1,0:T(4,128)S(1)} %copy-done.7, bf16[512,256]{1,0:T(8,128)(2,1)S(1)} %get-tuple-element.45.normed_ref.normed, bf16[768,256]{1,0:T(8,128)(2,1)S(1)} %bitcast.11), custom_call_target="tpu_custom_call" | custom-call | flops 20000000000 | bytes 72000000 | tf_op jit(solution)/shard_map/pallas_call | solution.py:82
  21.0 4.4 %all-to-all-done.x_in = bf16[8,16,768]{2,1,0:T(8,128)(2,1)S(1)} async-done(((bf16[8,16,768]{2,1,0:T(8,128)(2,1)}), bf16[8,16,768]{2,1,0:T(8,128)(2,1)S(1)}, u32[]{:S(2)}, u32[]{:S(2)}) %all-to-all-start) | async-done | bytes 196640 | tf_op jit(solution)/shard_map/all_to_all | solution.py:379
  25.4 3.3 %shard_map.138 = (bf16[32,8,128]{2,1,0:T(8,128)(2,1)}, bf16[128,1280]{1,0:T(8,128)(2,1)S(1)}, bf16[128,1280]{1,0:T(8,128)(2,1)}, bf16[8,16,512]{2,1,0:T(8,128)(2,1)}) custom-call(s32[1]{0:T(128)} %bitcast.1.hap, bf16[8,16,768]{2,1,0:T(8,128)(2,1)S(1)} %all-to-all-done.x_in, bf16[256,256]{1,0:T(8,128)(2,1)S(1)} %copy-done.1, ...), custom_call_target="tpu_custom_call" | custom-call | flops 1 | bytes 1 | tf_op jit(solution)/shard_map/pallas_call | solution.py:82
  28.7 0.0 copy-start.4
  28.7 1.0 %collective-permute-start.3 = (bf16[128,1280]{1,0:T(8,128)(2,1)S(1)}, bf16[128,1280]{1,0:T(8,128)(2,1)S(1)}, u32[]{:S(2)}, u32[]{:S(2)}) collective-permute-start(bf16[128,1280]{1,0:T(8,128)(2,1)S(1)} %get-tuple-element.50), channel_id=1, source_target_pairs={{0,1},{1,0},{2,3},{3,2},{4,5},{5,4},{6,7},{7,6},{8,9},{9,8},{10,11... | collective-permute-start | bytes 983048 | tf_op jit(solution)/shard_map/ppermute | solution.py:384
  29.7 3.7 %all-to-all-start.1 = ((bf16[32,8,128]{2,1,0:T(8,128)(2,1)}), bf16[32,8,128]{2,1,0:T(8,128)(2,1)S(1)}, u32[]{:S(2)}, u32[]{:S(2)}) async-start(bf16[32,8,128]{2,1,0:T(8,128)(2,1)} %get-tuple-element.48), calls=%async_computation.1 | async-start | bytes 131072 | tf_op jit(solution)/shard_map/all_to_all | solution.py:379
  33.4 0.4 collective-permute-start.4
  33.9 1.0 %copy-done.2 = bf16[128,1280]{1,0:T(8,128)(2,1)S(1)} copy-done((bf16[128,1280]{1,0:T(8,128)(2,1)S(1)}, bf16[128,1280]{1,0:T(8,128)(2,1)}, u32[]{:S(2)}) %copy-start.2) | copy-done | bytes 327704
  34.9 0.2 shard_map.139
  35.0 1.2 %collective-permute-start.6 = (bf16[32,1280]{1,0:T(8,128)(2,1)S(1)}, bf16[32,1280]{1,0:T(8,128)(2,1)S(1)}, u32[]{:S(2)}, u32[]{:S(2)}) collective-permute-start(bf16[32,1280]{1,0:T(8,128)(2,1)S(1)} %get-tuple-element.52), channel_id=1, source_target_pairs={{0,8},{8,0},{16,24},{24,16},{1,9},{9,1},{17,25},{25,17},{2,10},{10... | collective-permute-start | bytes 245768 | tf_op jit(solution)/shard_map/ppermute | solution.py:384
  36.3 1.2 %collective-permute-start.7 = (bf16[32,1280]{1,0:T(8,128)(2,1)S(1)}, bf16[32,1280]{1,0:T(8,128)(2,1)S(1)}, u32[]{:S(2)}, u32[]{:S(2)}) collective-permute-start(bf16[32,1280]{1,0:T(8,128)(2,1)S(1)} %get-tuple-element.53), channel_id=1, source_target_pairs={{0,16},{8,24},{16,0},{24,8},{1,17},{9,25},{17,1},{25,9},{2,18},{10... | collective-permute-start | bytes 245768 | tf_op jit(solution)/shard_map/ppermute | solution.py:384
  37.5 0.3 collective-permute-start.8
  37.7 1.7 %all-to-all-done.1.g_in = bf16[32,8,128]{2,1,0:T(8,128)(2,1)S(1)} async-done(((bf16[32,8,128]{2,1,0:T(8,128)(2,1)}), bf16[32,8,128]{2,1,0:T(8,128)(2,1)S(1)}, u32[]{:S(2)}, u32[]{:S(2)}) %all-to-all-start.1) | async-done | bytes 65568 | tf_op jit(solution)/shard_map/all_to_all | solution.py:379
  39.5 2.1 %shard_map.141 = (bf16[128,192]{1,0:T(8,128)(2,1)S(1)}, bf16[128,192]{1,0:T(8,128)(2,1)S(1)}, bf16[128,192]{1,0:T(8,128)(2,1)S(1)}, bf16[128,192]{1,0:T(8,128)(2...) custom-call(s32[1]{0:T(128)} %bitcast.idx, s32[1]{0:T(128)S(6)} %select_n.7.core, ...), custom_call_target="tpu_custom_call" | custom-call | flops 1 | bytes 1 | tf_op jit(solution)/shard_map/pallas_call | solution.py:82
  41.6 0.5 collective-permute-start.5
  42.0 0.9 %collective-permute-done.5.row_got = bf16[96,256]{1,0:T(8,128)(2,1)S(1)} collective-permute-done((bf16[96,256]{1,0:T(8,128)(2,1)S(1)}, bf16[96,256]{1,0:T(8,128)(2,1)S(1)}, u32[]{:S(2)}, u32[]{:S(2)}) %collective-permute-start.5) | collective-permute-done | bytes 49184 | tf_op jit(solution)/shard_map/ppermute | solution.py:384
  42.9 0.1 shard_map.142
  43.0 1.5 %collective-permute-start.9 = (bf16[320,256]{1,0:T(8,128)(2,1)S(1)}, bf16[320,256]{1,0:T(8,128)(2,1)S(1)}, u32[]{:S(2)}, u32[]{:S(2)}) collective-permute-start(bf16[320,256]{1,0:T(8,128)(2,1)S(1)} %get-tuple-element.66), channel_id=1, source_target_pairs={{0,2},{1,3},{2,0},{3,1},{4,6},{5,7},{6,4},{7,5},{8,10},{9,11},{10,... | collective-permute-start | bytes 491528 | tf_op jit(solution)/shard_map/ppermute | solution.py:384
  44.4 1.3 %collective-permute-start.11 = (bf16[320,256]{1,0:T(8,128)(2,1)S(1)}, bf16[320,256]{1,0:T(8,128)(2,1)S(1)}, u32[]{:S(2)}, u32[]{:S(2)}) collective-permute-start(bf16[320,256]{1,0:T(8,128)(2,1)S(1)} %get-tuple-element.68), channel_id=1, source_target_pairs={{0,6},{1,7},{2,4},{3,5},{4,2},{5,3},{6,0},{7,1},{8,14},{9,15},{10,... | collective-permute-start | bytes 491528 | tf_op jit(solution)/shard_map/ppermute | solution.py:384
  45.7 4.2 %collective-permute-done.9.refs_1_.refs_4_ = bf16[320,256]{1,0:T(8,128)(2,1)S(1)} collective-permute-done((bf16[320,256]{1,0:T(8,128)(2,1)S(1)}, bf16[320,256]{1,0:T(8,128)(2,1)S(1)}, u32[]{:S(2)}, u32[]{:S(2)}) %collective-permute-start.9) | collective-permute-done | bytes 163872 | tf_op jit(solution)/shard_map/ppermute | solution.py:384
  49.9 1.7 %collective-permute-done.10.refs_2_.refs_5_ = bf16[320,256]{1,0:T(8,128)(2,1)S(1)} collective-permute-done((bf16[320,256]{1,0:T(8,128)(2,1)S(1)}, bf16[320,256]{1,0:T(8,128)(2,1)S(1)}, u32[]{:S(2)}, u32[]{:S(2)}) %collective-permute-start.10) | collective-permute-done | bytes 163872 | tf_op jit(solution)/shard_map/ppermute | solution.py:384
  51.6 8.3 %collective-permute-done.11.refs_3_.refs_6_ = bf16[320,256]{1,0:T(8,128)(2,1)S(1)} collective-permute-done((bf16[320,256]{1,0:T(8,128)(2,1)S(1)}, bf16[320,256]{1,0:T(8,128)(2,1)S(1)}, u32[]{:S(2)}, u32[]{:S(2)}) %collective-permute-start.11) | collective-permute-done | bytes 163872 | tf_op jit(solution)/shard_map/ppermute | solution.py:384
  59.8 0.2 shard_map.143
  60.0 0.3 collective-permute-start.12
  60.3 1.1 %collective-permute-start.13 = (bf16[384,256]{1,0:T(8,128)(2,1)S(1)}, bf16[384,256]{1,0:T(8,128)(2,1)S(1)}, u32[]{:S(2)}, u32[]{:S(2)}) collective-permute-start(bf16[384,256]{1,0:T(8,128)(2,1)S(1)} %get-tuple-element.73), channel_id=1, source_target_pairs={{0,16},{8,24},{16,0},{24,8},{1,17},{9,25},{17,1},{25,9},{2,18},{10... | collective-permute-start | bytes 589832 | tf_op jit(solution)/shard_map/ppermute | solution.py:384
  61.5 1.2 %collective-permute-start.14 = (bf16[384,256]{1,0:T(8,128)(2,1)S(1)}, bf16[384,256]{1,0:T(8,128)(2,1)S(1)}, u32[]{:S(2)}, u32[]{:S(2)}) collective-permute-start(bf16[384,256]{1,0:T(8,128)(2,1)S(1)} %get-tuple-element.74), channel_id=1, source_target_pairs={{0,24},{8,16},{16,8},{24,0},{1,25},{9,17},{17,9},{25,1},{2,26},{10... | collective-permute-start | bytes 589832 | tf_op jit(solution)/shard_map/ppermute | solution.py:384
  62.7 1.9 %collective-permute-done.12.refs_0_.refs_2_ = bf16[384,256]{1,0:T(8,128)(2,1)S(1)} collective-permute-done((bf16[384,256]{1,0:T(8,128)(2,1)S(1)}, bf16[384,256]{1,0:T(8,128)(2,1)S(1)}, u32[]{:S(2)}, u32[]{:S(2)}) %collective-permute-start.12) | collective-permute-done | bytes 196640 | tf_op jit(solution)/shard_map/ppermute | solution.py:384
  64.6 4.9 %collective-permute-start.16 = (bf16[384,256]{1,0:T(8,128)(2,1)S(1)}, bf16[384,256]{1,0:T(8,128)(2,1)S(1)}, u32[]{:S(2)}, u32[]{:S(2)}) collective-permute-start(bf16[384,256]{1,0:T(8,128)(2,1)S(1)} %collective-permute-done.12.refs_0_.refs_2_), channel_id=1, source_target_pairs={{0,1},{1,0},{2,3},{3,2},{4,5},{5,4},{6,7},{7,6},{8,9},{9,8},{10,11... | collective-permute-start | bytes 589832 | tf_op jit(solution)/shard_map/ppermute | solution.py:384
  69.5 2.5 %collective-permute-start.17 = (bf16[384,256]{1,0:T(8,128)(2,1)S(1)}, bf16[384,256]{1,0:T(8,128)(2,1)S(1)}, u32[]{:S(2)}, u32[]{:S(2)}) collective-permute-start(bf16[384,256]{1,0:T(8,128)(2,1)S(1)} %collective-permute-done.13.refs_1_.refs_4_), channel_id=1, source_target_pairs={{0,1},{1,0},{2,3},{3,2},{4,5},{5,4},{6,7},{7,6},{8,9},{9,8},{10,11... | collective-permute-start | bytes 589832 | tf_op jit(solution)/shard_map/ppermute | solution.py:384
  72.0 0.5 collective-permute-start.15
  72.5 1.0 %shard_map.144 = (bf16[128,256]{1,0:T(8,128)(2,1)}, bf16[128,256]{1,0:T(8,128)(2,1)}) custom-call(s32[1]{0:T(128)} %bitcast.idx, s32[1]{0:T(128)} %bitcast.1.hap, bf16[128,256]{1,0:T(8,128)(2,1)S(1)} %bitcast.18, f32[2,256]{1,0:T(2,128)S(1)} %pad_maximum_fusion.refs_5_.gain, bf16[768,256]{1,0:T(8,128)(2,1)S(1)} %bitcast.12, ...), custom_call_target="tpu_custom_call" | custom-call | flops 1 | bytes 1 | tf_op jit(solution)/shard_map/pallas_call | solution.py:82
  73.5 0.2 collective-permute-done.15.refs_1_
  73.6 1.5 %shard_map.145 = (f32[256,768]{1,0:T(8,128)}, f32[256,256]{1,0:T(8,128)}, f32[256,768]{1,0:T(8,128)}, f32[256,256]{1,0:T(8,128)}) custom-call(s32[1]{0:T(128)} %bitcast.idx, s32[1]{0:T(128)S(6)} %select_n.7.core, bf16[256,256]{1,0:T(8,128)(2,1)S(1)} %get-tuple-element.77.refs_0_, bf16[256,256]{1,0:T(8,128)(2,1)S(1)} %collective-permute-done.15.refs_1_, ...), custom_call_target="tpu_custom_call" | custom-call | flops 1 | bytes 1 | tf_op jit(solution)/shard_map/pallas_call | solution.py:82
  (31 shorter events, 0.1 us)
Async XLA Ops:
  0.6 4.7 %collective-permute-start.2 = (bf16[128,256]{1,0:T(8,128)(2,1)}, bf16[128,256]{1,0:T(8,128)(2,1)S(1)}, u32[]{:S(2)}, u32[]{:S(2)}) collective-permute-start(bf16[128,256]{1,0:T(8,128)(2,1)} %bitcast.14), channel_id=1, source_target_pairs={{0,24},{8,16},{16,8},{24,0},{1,25},{9,17},{17,9},{25,1},{2,26},{10... | collective-permute-start | bytes 196616 | tf_op jit(solution)/shard_map/ppermute | solution.py:384
  2.9 3.9 %collective-permute-start.1 = (bf16[128,256]{1,0:T(8,128)(2,1)}, bf16[128,256]{1,0:T(8,128)(2,1)S(1)}, u32[]{:S(2)}, u32[]{:S(2)}) collective-permute-start(bf16[128,256]{1,0:T(8,128)(2,1)} %bitcast.15), channel_id=1, source_target_pairs={{0,16},{8,24},{16,0},{24,8},{1,17},{9,25},{17,1},{25,9},{2,18},{10... | collective-permute-start | bytes 196616 | tf_op jit(solution)/shard_map/ppermute | solution.py:384
  3.1 3.7 %collective-permute-start = (bf16[128,256]{1,0:T(8,128)(2,1)}, bf16[128,256]{1,0:T(8,128)(2,1)S(1)}, u32[]{:S(2)}, u32[]{:S(2)}) collective-permute-start(bf16[128,256]{1,0:T(8,128)(2,1)} %bitcast.16), channel_id=1, source_target_pairs={{0,8},{8,0},{16,24},{24,16},{1,9},{9,1},{17,25},{25,17},{2,10},{10... | collective-permute-start | bytes 196616 | tf_op jit(solution)/shard_map/ppermute | solution.py:384
  3.3 0.9 %slice-start = ((bf16[256,768]{1,0:T(8,128)(2,1)}), bf16[256,512]{1,0:T(8,128)(2,1)S(1)}, s32[]{:S(2)}) async-start(bf16[256,768]{1,0:T(8,128)(2,1)} %col_proj.1), calls=%async_computation.2 | async-start | bytes 524288 | tf_op jit(solution)/shard_map/slice | solution.py:418
  3.3 1.1 %copy-start.8 = (bf16[256,768]{1,0:T(8,128)(2,1)S(1)}, bf16[256,768]{1,0:T(8,128)(2,1)}, u32[]{:S(2)}) copy-start(bf16[256,768]{1,0:T(8,128)(2,1)} %param.12) | copy-start | bytes 1179652
  4.4 0.7 copy-start.10
  4.5 2.4 %copy-start.1 = (bf16[256,256]{1,0:T(8,128)(2,1)S(1)}, bf16[256,256]{1,0:T(8,128)(2,1)}, u32[]{:S(2)}) copy-start(bf16[256,256]{1,0:T(8,128)(2,1)} %row_out.1) | copy-start | bytes 393220
  4.5 2.4 %copy-start.3 = (bf16[128,1,256]{2,0,1:T(8,128)(2,1)S(1)}, bf16[128,1,256]{2,0,1:T(8,128)(2,1)}, u32[]{:S(2)}) copy-start(bf16[128,1,256]{2,0,1:T(8,128)(2,1)} %param.9) | copy-start | bytes 196612
  4.5 2.3 %copy-start.6 = (bf16[128,1,256]{2,0,1:T(8,128)(2,1)S(1)}, bf16[128,1,256]{2,0,1:T(8,128)(2,1)}, u32[]{:S(2)}) copy-start(bf16[128,1,256]{2,0,1:T(8,128)(2,1)} %param.17) | copy-start | bytes 196612
  4.7 0.7 copy-start.9
  6.8 0.7 copy-start.7
  12.3 13.1 %all-to-all-start = ((bf16[8,16,768]{2,1,0:T(8,128)(2,1)}), bf16[8,16,768]{2,1,0:T(8,128)(2,1)S(1)}, u32[]{:S(2)}, u32[]{:S(2)}) async-start(bf16[8,16,768]{2,1,0:T(8,128)(2,1)} %get-tuple-element.44), calls=%async_computation | async-start | bytes 393216 | tf_op jit(solution)/shard_map/all_to_all | solution.py:379
  19.2 6.1 %copy-start = (bf16[256,768]{1,0:T(8,128)(2,1)S(1)}, bf16[256,768]{1,0:T(8,128)(2,1)}, u32[]{:S(2)}) copy-start(bf16[256,768]{1,0:T(8,128)(2,1)} %col_proj.1) | copy-start | bytes 1179652
  19.2 6.1 %copy-start.5 = (bf16[256,256]{1,0:T(8,128)(2,1)S(1)}, bf16[256,256]{1,0:T(8,128)(2,1)}, u32[]{:S(2)}) copy-start(bf16[256,256]{1,0:T(8,128)(2,1)} %col_out.1) | copy-start | bytes 393220
  28.7 4.7 %copy-start.4 = (bf16[8,16,512]{2,1,0:T(8,128)(2,1)S(1)}, bf16[8,16,512]{2,1,0:T(8,128)(2,1)}, u32[]{:S(2)}) copy-start(bf16[8,16,512]{2,1,0:T(8,128)(2,1)} %get-tuple-element.55.og) | copy-start | bytes 393220
  28.7 5.2 %collective-permute-start.3 = (bf16[128,1280]{1,0:T(8,128)(2,1)S(1)}, bf16[128,1280]{1,0:T(8,128)(2,1)S(1)}, u32[]{:S(2)}, u32[]{:S(2)}) collective-permute-start(bf16[128,1280]{1,0:T(8,128)(2,1)S(1)} %get-tuple-element.50), channel_id=1, source_target_pairs={{0,1},{1,0},{2,3},{3,2},{4,5},{5,4},{6,7},{7,6},{8,9},{9,8},{10,11... | collective-permute-start | bytes 983048 | tf_op jit(solution)/shard_map/ppermute | solution.py:384
  29.7 9.7 %all-to-all-start.1 = ((bf16[32,8,128]{2,1,0:T(8,128)(2,1)}), bf16[32,8,128]{2,1,0:T(8,128)(2,1)S(1)}, u32[]{:S(2)}, u32[]{:S(2)}) async-start(bf16[32,8,128]{2,1,0:T(8,128)(2,1)} %get-tuple-element.48), calls=%async_computation.1 | async-start | bytes 131072 | tf_op jit(solution)/shard_map/all_to_all | solution.py:379
  33.4 4.3 %collective-permute-start.4 = (bf16[4,16,512]{2,1,0:T(8,128)(2,1)S(1)}, bf16[4,16,512]{2,1,0:T(8,128)(2,1)S(1)}, u32[]{:S(2)}, u32[]{:S(2)}) collective-permute-start(bf16[4,16,512]{2,1,0:T(8,128)(2,1)S(1)} %get-tuple-element.56), channel_id=1, source_target_pairs={{0,1},{1,0},{2,3},{3,2},{4,5},{5,4},{6,7},{7,6},{8,9},{9,8},{10,11... | collective-permute-start | bytes 196616 | tf_op jit(solution)/shard_map/ppermute | solution.py:384
  33.9 1.0 %copy-start.2 = (bf16[128,1280]{1,0:T(8,128)(2,1)S(1)}, bf16[128,1280]{1,0:T(8,128)(2,1)}, u32[]{:S(2)}) copy-start(bf16[128,1280]{1,0:T(8,128)(2,1)} %get-tuple-element.49.keep) | copy-start | bytes 983044
  35.0 7.9 %collective-permute-start.6 = (bf16[32,1280]{1,0:T(8,128)(2,1)S(1)}, bf16[32,1280]{1,0:T(8,128)(2,1)S(1)}, u32[]{:S(2)}, u32[]{:S(2)}) collective-permute-start(bf16[32,1280]{1,0:T(8,128)(2,1)S(1)} %get-tuple-element.52), channel_id=1, source_target_pairs={{0,8},{8,0},{16,24},{24,16},{1,9},{9,1},{17,25},{25,17},{2,10},{10... | collective-permute-start | bytes 245768 | tf_op jit(solution)/shard_map/ppermute | solution.py:384
  36.3 6.6 %collective-permute-start.7 = (bf16[32,1280]{1,0:T(8,128)(2,1)S(1)}, bf16[32,1280]{1,0:T(8,128)(2,1)S(1)}, u32[]{:S(2)}, u32[]{:S(2)}) collective-permute-start(bf16[32,1280]{1,0:T(8,128)(2,1)S(1)} %get-tuple-element.53), channel_id=1, source_target_pairs={{0,16},{8,24},{16,0},{24,8},{1,17},{9,25},{17,1},{25,9},{2,18},{10... | collective-permute-start | bytes 245768 | tf_op jit(solution)/shard_map/ppermute | solution.py:384
  37.5 5.5 %collective-permute-start.8 = (bf16[32,1280]{1,0:T(8,128)(2,1)S(1)}, bf16[32,1280]{1,0:T(8,128)(2,1)S(1)}, u32[]{:S(2)}, u32[]{:S(2)}) collective-permute-start(bf16[32,1280]{1,0:T(8,128)(2,1)S(1)} %get-tuple-element.54), channel_id=1, source_target_pairs={{0,24},{8,16},{16,8},{24,0},{1,25},{9,17},{17,9},{25,1},{2,26},{10... | collective-permute-start | bytes 245768 | tf_op jit(solution)/shard_map/ppermute | solution.py:384
  41.6 1.3 %collective-permute-start.5 = (bf16[96,256]{1,0:T(8,128)(2,1)S(1)}, bf16[96,256]{1,0:T(8,128)(2,1)S(1)}, u32[]{:S(2)}, u32[]{:S(2)}) collective-permute-start(bf16[96,256]{1,0:T(8,128)(2,1)S(1)} %get-tuple-element.63), channel_id=1, source_target_pairs={{0,1},{1,0},{2,3},{3,2},{4,5},{5,4},{6,7},{7,6},{8,9},{9,8},{10,11... | collective-permute-start | bytes 147464 | tf_op jit(solution)/shard_map/ppermute | solution.py:384
  43.0 6.9 %collective-permute-start.9 = (bf16[320,256]{1,0:T(8,128)(2,1)S(1)}, bf16[320,256]{1,0:T(8,128)(2,1)S(1)}, u32[]{:S(2)}, u32[]{:S(2)}) collective-permute-start(bf16[320,256]{1,0:T(8,128)(2,1)S(1)} %get-tuple-element.66), channel_id=1, source_target_pairs={{0,2},{1,3},{2,0},{3,1},{4,6},{5,7},{6,4},{7,5},{8,10},{9,11},{10,... | collective-permute-start | bytes 491528 | tf_op jit(solution)/shard_map/ppermute | solution.py:384
  44.4 7.1 %collective-permute-start.10 = (bf16[320,256]{1,0:T(8,128)(2,1)S(1)}, bf16[320,256]{1,0:T(8,128)(2,1)S(1)}, u32[]{:S(2)}, u32[]{:S(2)}) collective-permute-start(bf16[320,256]{1,0:T(8,128)(2,1)S(1)} %get-tuple-element.67), channel_id=1, source_target_pairs={{0,4},{1,5},{2,6},{3,7},{4,0},{5,1},{6,2},{7,3},{8,12},{9,13},{10,... | collective-permute-start | bytes 491528 | tf_op jit(solution)/shard_map/ppermute | solution.py:384
  44.4 15.4 %collective-permute-start.11 = (bf16[320,256]{1,0:T(8,128)(2,1)S(1)}, bf16[320,256]{1,0:T(8,128)(2,1)S(1)}, u32[]{:S(2)}, u32[]{:S(2)}) collective-permute-start(bf16[320,256]{1,0:T(8,128)(2,1)S(1)} %get-tuple-element.68), channel_id=1, source_target_pairs={{0,6},{1,7},{2,4},{3,5},{4,2},{5,3},{6,0},{7,1},{8,14},{9,15},{10,... | collective-permute-start | bytes 491528 | tf_op jit(solution)/shard_map/ppermute | solution.py:384
  60.0 4.6 %collective-permute-start.12 = (bf16[384,256]{1,0:T(8,128)(2,1)S(1)}, bf16[384,256]{1,0:T(8,128)(2,1)S(1)}, u32[]{:S(2)}, u32[]{:S(2)}) collective-permute-start(bf16[384,256]{1,0:T(8,128)(2,1)S(1)} %get-tuple-element.72), channel_id=1, source_target_pairs={{0,8},{8,0},{16,24},{24,16},{1,9},{9,1},{17,25},{25,17},{2,10},{10... | collective-permute-start | bytes 589832 | tf_op jit(solution)/shard_map/ppermute | solution.py:384
  60.3 9.1 %collective-permute-start.13 = (bf16[384,256]{1,0:T(8,128)(2,1)S(1)}, bf16[384,256]{1,0:T(8,128)(2,1)S(1)}, u32[]{:S(2)}, u32[]{:S(2)}) collective-permute-start(bf16[384,256]{1,0:T(8,128)(2,1)S(1)} %get-tuple-element.73), channel_id=1, source_target_pairs={{0,16},{8,24},{16,0},{24,8},{1,17},{9,25},{17,1},{25,9},{2,18},{10... | collective-permute-start | bytes 589832 | tf_op jit(solution)/shard_map/ppermute | solution.py:384
  61.5 10.5 %collective-permute-start.14 = (bf16[384,256]{1,0:T(8,128)(2,1)S(1)}, bf16[384,256]{1,0:T(8,128)(2,1)S(1)}, u32[]{:S(2)}, u32[]{:S(2)}) collective-permute-start(bf16[384,256]{1,0:T(8,128)(2,1)S(1)} %get-tuple-element.74), channel_id=1, source_target_pairs={{0,24},{8,16},{16,8},{24,0},{1,25},{9,17},{17,9},{25,1},{2,26},{10... | collective-permute-start | bytes 589832 | tf_op jit(solution)/shard_map/ppermute | solution.py:384
  64.6 9.1 %collective-permute-start.16 = (bf16[384,256]{1,0:T(8,128)(2,1)S(1)}, bf16[384,256]{1,0:T(8,128)(2,1)S(1)}, u32[]{:S(2)}, u32[]{:S(2)}) collective-permute-start(bf16[384,256]{1,0:T(8,128)(2,1)S(1)} %collective-permute-done.12.refs_0_.refs_2_), channel_id=1, source_target_pairs={{0,1},{1,0},{2,3},{3,2},{4,5},{5,4},{6,7},{7,6},{8,9},{9,8},{10,11... | collective-permute-start | bytes 589832 | tf_op jit(solution)/shard_map/ppermute | solution.py:384
  69.5 4.2 %collective-permute-start.17 = (bf16[384,256]{1,0:T(8,128)(2,1)S(1)}, bf16[384,256]{1,0:T(8,128)(2,1)S(1)}, u32[]{:S(2)}, u32[]{:S(2)}) collective-permute-start(bf16[384,256]{1,0:T(8,128)(2,1)S(1)} %collective-permute-done.13.refs_1_.refs_4_), channel_id=1, source_target_pairs={{0,1},{1,0},{2,3},{3,2},{4,5},{5,4},{6,7},{7,6},{8,9},{9,8},{10,11... | collective-permute-start | bytes 589832 | tf_op jit(solution)/shard_map/ppermute | solution.py:384
  72.0 1.6 %collective-permute-start.18 = (bf16[384,256]{1,0:T(8,128)(2,1)S(1)}, bf16[384,256]{1,0:T(8,128)(2,1)S(1)}, u32[]{:S(2)}, u32[]{:S(2)}) collective-permute-start(bf16[384,256]{1,0:T(8,128)(2,1)S(1)} %collective-permute-done.14.refs_2_.refs_6_), channel_id=1, source_target_pairs={{0,1},{1,0},{2,3},{3,2},{4,5},{5,4},{6,7},{7,6},{8,9},{9,8},{10,11... | collective-permute-start | bytes 589832 | tf_op jit(solution)/shard_map/ppermute | solution.py:384
  72.0 1.6 %collective-permute-start.15 = (bf16[256,256]{1,0:T(8,128)(2,1)S(1)}, bf16[256,256]{1,0:T(8,128)(2,1)S(1)}, u32[]{:S(2)}, u32[]{:S(2)}) collective-permute-start(bf16[256,256]{1,0:T(8,128)(2,1)S(1)} %get-tuple-element.77.refs_0_), channel_id=1, source_target_pairs={{0,1},{1,0},{2,3},{3,2},{4,5},{5,4},{6,7},{7,6},{8,9},{9,8},{10,11... | collective-permute-start | bytes 393224 | tf_op jit(solution)/shard_map/ppermute | solution.py:384

commit v8 on v7

--- a/solution.py
+++ b/solution.py
@@ -247,13 +247,13 @@
         send[m] = og[hap[0] ^ (2 * m + 1)]
 
 
-def column_split(sites, idx, keep, *refs):
-    outs, both, gots = refs[-sites - 1 : -1], refs[-1], refs[: -sites - 1]
-    got = jnp.concatenate([g[...].astype(F32) for g in gots], axis=0)
-    both[...] = (keep[...].astype(F32) + got).astype(BF16)
-    part = keep.shape[0] // sites
-    for k in range(sites):
-        outs[k][...] = both[pl.ds(pl.multiple_of((idx[0] ^ k) * part, part), part), :]
+def column_split(depth, hap, keep, got, *refs):
+    outs, both = refs[:depth], refs[depth]
+    both[...] = (keep[...].astype(F32) + got[...].astype(F32)).astype(BF16)
+    part = keep.shape[0] // depth
+    for m in range(depth):
+        start = ((hap[0] // 2) ^ m) * part
+        outs[m][...] = both[pl.ds(pl.multiple_of(start, part), part), :]
 
 
 def row_backward(sites, haps, idx, core, g_in, prob, q, val, key_t, normed, *refs):
@@ -295,10 +295,52 @@
         gp_outs[b][...] = joined[b * rows : (b + 1) * rows]
 
 
-def row_finish(sites, haps, idx, hap, feats, gain, w_t, gp, *refs):
-    gps, parts = refs[: sites - 1], refs[sites - 1 : sites - 1 + haps // 2]
-    out_ref, gf_ref, og = refs[sites - 1 + haps // 2 :]
-    me = idx[0]
+def tree_sum(terms):
+    while len(terms) > 1:
+        terms = [a + b for a, b in zip(terms[::2], terms[1::2])]
+    return terms[0]
+
+
+def row_join(row_keep, row_got, og_keep, og_got, *outs):
+    half, width = row_keep.shape
+    joined = (row_keep[...].astype(F32) + row_got[...].astype(F32)).astype(BF16)
+    for m, out in enumerate(outs):
+        out[:half, :] = joined
+        both = [og_keep[m].astype(F32), og_got[m].astype(F32)]
+        both = [x[:, j * width : (j + 1) * width] for x in both for j in range(2)]
+        out[half:, :] = jnp.concatenate(both, axis=0).astype(BF16)
+
+
+def column_join(depth, sites, idx, *refs):
+    cols, gps, out = refs[:depth], refs[depth : depth + sites], refs[depth + sites]
+    width = out.shape[2]
+    total = tree_sum([c[...].astype(F32) for c in cols])
+    tiles = [total[:, t * width : (t + 1) * width] for t in range(5)]
+    joined = jnp.concatenate(tiles, axis=0).astype(BF16)
+    top = joined.shape[0]
+    rows, used = gps[0].shape
+    for k in range(sites):
+        place = idx[0] ^ k
+        out[place, :top, :] = joined
+        out[place, top:, :used] = gps[k][...]
+        out[place, top:, used:] = jnp.zeros((rows, width - used), BF16)
+
+
+def row_sum(*refs):
+    out = refs[-1]
+    total = tree_sum([r[: out.shape[1], :].astype(F32) for r in refs[:-1]]).astype(BF16)
+    for i in range(out.shape[0]):
+        out[i] = total
+
+
+def column_sum(got, out):
+    total = sum(got[i, : out.shape[0], :].astype(F32) for i in range(got.shape[0]))
+    out[...] = total.astype(BF16)
+
+
+def row_finish(sites, haps, hap, feats, gain, w_t, gps, *refs):
+    parts = refs[: haps // 2]
+    out_ref, gf_ref, og = refs[haps // 2 :]
     rows, width = feats.shape
     group = width // sites
     per = rows // haps
@@ -308,66 +350,41 @@
             for side in range(2):
                 start = base + (2 * j + side) * per
                 og[side, hap[0] ^ (2 * m + j)] = parts[m][start : start + per, :].astype(F32)
-    grads = [gp[...]] + [g[g.shape[0] - rows :, : 3 * group] for g in gps]
+    top = gps.shape[1] - rows
     grad_normed = 0.0
-    for k in range(sites):
-        place = [pl.multiple_of(p * width + (me ^ k) * group, group) for p in range(3)]
-        weights = jnp.concatenate([w_t[pl.ds(p, group), :] for p in place], axis=0)
-        grad_normed = grad_normed + mm(grads[k], weights)
+    for i in range(sites):
+        place = [p * width + i * group for p in range(3)]
+        weights = jnp.concatenate([w_t[p : p + group, :] for p in place], axis=0)
+        grad_normed = grad_normed + mm(gps[i, top:, : 3 * group], weights)
     xhat, rstd = norm_parts(feats[...].astype(F32))
     grad = og[1].reshape(rows, width) + norm_back(xhat, rstd, gain[:1, :], grad_normed)
     out_ref[...] = og[0].reshape(rows, width).astype(BF16)
     gf_ref[...] = grad.astype(BF16)
 
 
-def weights_join(sites, row_keep, row_got, og_keep, og_got, *refs):
-    cols, outs = refs[:sites], refs[sites:]
-    half, width = row_keep.shape
-    depth = half + 5 * cols[0].shape[0]
-    per = og_keep.shape[1]
-    total = sum(c[...].astype(F32) for c in cols)
-    tiles = [total[:, t * width : (t + 1) * width] for t in range(5)]
-    rows = row_keep[...].astype(F32) + row_got[...].astype(F32)
-    joined = jnp.concatenate([rows] + tiles, axis=0).astype(BF16)
-    for m, out in enumerate(outs):
-        out[:depth, :] = joined
-        both = [og_keep[m].astype(F32), og_got[m].astype(F32)]
-        both = [x[:, j * width : (j + 1) * width] for x in both for j in range(2)]
-        out[depth:, :] = jnp.concatenate(both, axis=0).astype(BF16)
-
-
-def weights_sum(haps, sites, *refs):
-    parts, gps = refs[: haps // 2], refs[haps // 2 : haps // 2 + sites - 1]
-    mine, outs = refs[haps // 2 + sites - 1], refs[haps // 2 + sites :]
-    depth, width = mine.shape
-    terms = [r[:depth, :].astype(F32) for r in parts]
-    while len(terms) > 1:
-        terms = [a + b for a, b in zip(terms[::2], terms[1::2])]
-    mine[...] = terms[0].astype(BF16)
-    for gp, out in zip(gps, outs):
-        out[:depth, :] = mine[...]
-        out[depth:, : gp.shape[1]] = gp[...]
-        out[depth:, gp.shape[1] :] = jnp.zeros((gp.shape[0], width - gp.shape[1]), BF16)
-
-
-def weights_finish(sites, idx, core, *refs):
-    pieces = refs[: 2 * sites]
-    rp, ro, cp, co, rows_t = refs[2 * sites :]
+def weights_finish(depth, hap, row_own, row_other, *refs):
+    pieces = refs[: 2 * depth]
+    rp, ro, cp, co, rows_t = refs[2 * depth :]
     width = ro.shape[0]
+    sites = row_own.shape[0]
     group = width // sites
     unit = group // 2
-    part = width // 2 // sites
-    for j in range(2 * sites):
-        k = j // 2
-        cc = core[0] ^ (j % 2)
-        g = idx[0] ^ k
+    part = width // 2 // depth
+    core = hap[0] % 2
+    for j, rows in enumerate((row_own, row_other)):
+        cc = core ^ j
+        for i in range(sites):
+            piece = rows[i].astype(F32)
+            for u in range(3):
+                place = 3 * cc + u
+                dest = (place // 2) * width + i * group + (place % 2) * unit
+                rows_t[pl.ds(pl.multiple_of(dest, unit), unit), :] = piece[u * unit : (u + 1) * unit]
+    for j in range(2 * depth):
+        cc = core ^ (j % 2)
+        zz = (hap[0] // 2) ^ (j // 2)
         piece = pieces[j][...].astype(F32)
-        for u in range(3):
-            place = 3 * cc + u
-            dest = (place // 2) * width + g * group + (place % 2) * unit
-            rows_t[pl.ds(pl.multiple_of(dest, unit), unit), :] = piece[u * unit : (u + 1) * unit]
-        here = pl.ds(pl.multiple_of(cc * (width // 2) + g * part, part), part)
-        tiles = [piece[3 * unit + t * part : 3 * unit + (t + 1) * part] for t in range(5)]
+        here = pl.ds(pl.multiple_of(cc * (width // 2) + zz * part, part), part)
+        tiles = [piece[t * part : (t + 1) * part] for t in range(5)]
         for t in range(3):
             cp[here, t * width : (t + 1) * width] = tiles[t]
         co[here, :] = tiles[3]
@@ -451,11 +468,12 @@
         ],
     )
     g_in = exchange(ga, both_axes)
-    col_got = [swapped(col_send, "hap", 1)]
+    col_got = swapped(col_send, "hap", 1)
+    depth = haps // 2
     cols = call(
-        functools.partial(column_split, sites),
-        [((half // sites, 5 * width), BF16)] * sites,
-        idx, col_keep, *col_got, scalars=1, us=0,
+        functools.partial(column_split, depth),
+        [((half // depth, 5 * width), BF16)] * depth,
+        hap, col_keep, col_got, scalars=1,
         scratch=[pltpu.VMEM((half, 5 * width), BF16)],
     )
     og_keep, og_send = call(
@@ -463,7 +481,7 @@
     )
     og_got = swapped(og_send, "hap", 1)
     g_in, _ = lax.optimization_barrier((g_in, (cols, og_got)))
-    cols = [cols[0]] + [swapped(cols[k], "site", k) for k in range(1, sites)]
+    cols = [cols[0]] + [swapped(cols[m], "hap", 2 * m) for m in range(1, depth)]
     *gps, row_keep, row_send = call(
         functools.partial(row_backward, sites, haps),
         [((rows, 3 * group), BF16)] * sites + [((3 * group // 2, width), BF16)] * 2,
@@ -475,30 +493,38 @@
         ],
     )
     row_got = swapped(row_send, "hap", 1)
-    depth = 3 * group // 2 + 5 * half // sites
+    tall = 5 * half // depth
+    (col_out_parts,) = call(
+        functools.partial(column_join, depth, sites),
+        [((sites, tall + rows, width), BF16)],
+        idx, *cols, *gps, scalars=1,
+    )
     parts = call(
-        functools.partial(weights_join, sites),
-        [((depth + 4 * per, width), BF16)] * (haps // 2),
-        row_keep, row_got, og_keep, og_got, *cols,
-    )
-    parts = [parts[0]] + [swapped(parts[m], "hap", 2 * m) for m in range(1, haps // 2)]
-    mine, *sends = call(
-        functools.partial(weights_sum, haps, sites),
-        [((depth, width), BF16)] + [((depth + rows, width), BF16)] * (sites - 1),
-        *parts, *gps[1:],
-    )
-    got = [swapped(sends[k - 1], "site", k) for k in range(1, sites)]
-    full = [x for p in [mine] + got for x in (p, swapped(p, "hap", 1))]
+        row_join,
+        [((3 * group // 2 + 4 * per, width), BF16)] * depth,
+        row_keep, row_got, og_keep, og_got,
+    )
+    parts, col_out_parts = lax.optimization_barrier((parts, col_out_parts))
+    col_in_parts = exchange(col_out_parts, "site")
+    parts = [parts[0]] + [swapped(parts[m], "hap", 2 * m) for m in range(1, depth)]
+    (row_mine,) = call(row_sum, [((sites, 3 * group // 2, width), BF16)], *parts)
+    (col_mine,) = call(column_sum, [((tall, width), BF16)], col_in_parts)
+    row_mine, col_mine = lax.optimization_barrier((row_mine, col_mine))
+    row_full = exchange(row_mine, "site")
+    col_full = [col_mine] + [swapped(col_mine, "hap", 2 * m) for m in range(1, depth)]
+    row_full, col_full = lax.optimization_barrier((row_full, col_full))
+    col_full = [x for p in col_full for x in (p, swapped(p, "hap", 1))]
+    row_other = swapped(row_full, "hap", 1)
     out, grad = call(
         functools.partial(row_finish, sites, haps),
         [((rows, width), BF16)] * 2,
-        idx, hap, feats, gains, w_t, gps[0], *got, *parts, scalars=2,
+        hap, feats, gains, w_t, col_in_parts, *parts, scalars=1,
         scratch=[pltpu.VMEM((2, haps, per, width), F32)],
     )
     rp, ro, cp, co = call(
-        functools.partial(weights_finish, sites),
+        functools.partial(weights_finish, depth),
         [((width, 3 * width), F32), ((width, width), F32)] * 2,
-        idx, core, *full, scalars=2,
+        hap, row_full, row_other, *col_full, scalars=1,
         scratch=[pltpu.VMEM((3 * width, width), F32)],
     )
     shape = (rows, 1, width)

time: 75.5 us -> 79.5 us (1.053)
  the two profiles are of different devices: /device:TPU:9 before, /device:TPU:0 now
where the time goes in v8:
time: 79.5 us; the launch traced here: 79 us
  starting transfers between devices  34.4 us (43%)
  waiting for transfers between devices  23.8 us (30%)
  Pallas kernels  16.2 us (20%)
  local copies, waits for them, and re-layouts  3.61 us (5%)
  between operations  0.83 us (1%)
    ppermute x20, starting transfers between devices, swapped(): return lax.ppermute(value, axis, [(i, i ^ by) for i in range(length)])  19.5 us
    pallas_call x12, Pallas kernels, call(): pl.pallas_call(body, out_shape=[jax.ShapeDtypeStruct(s, d) for s, d in ou...  16.2 us
    ppermute x20, waiting for transfers between devices, swapped(): return lax.ppermute(value, axis, [(i, i ^ by) for i in range(length)])  15.8 us
    all_to_all x4, starting transfers between devices, exchange(): return lax.all_to_all(value, axis, 0, 0, tiled=True)  15 us
    all_to_all x4, waiting for transfers between devices, exchange(): return lax.all_to_all(value, axis, 0, 0, tiled=True)  8 us
    unnamed x24, local copies, waits for them, and re-layouts  2.66 us
  transfers between devices with their start and end apart: 24, of which 11 were waited for; matrix products, arithmetic and copies ran while one was open for 0% of the time, Pallas kernels for 7%

profile of v8, /device:TPU:0, one launch (start us, length us, event | category | flops | bytes accessed | tf_op | source)
XLA Modules:
  0.0 79.0 jit_solution(6276532045367485604)
XLA Ops:
  0.6 4.0 %collective-permute-start.2 = (bf16[128,256]{1,0:T(8,128)(2,1)}, bf16[128,256]{1,0:T(8,128)(2,1)S(1)}, u32[]{:S(2)}, u32[]{:S(2)}) collective-permute-start(bf16[128,256]{1,0:T(8,128)(2,1)} %bitcast.14), channel_id=1, source_target_pairs={{0,24},{8,16},{16,8},{24,0},{1,25},{9,17},{17,9},{25,1},{2,26},{10... | collective-permute-start | bytes 196616 | tf_op jit(solution)/shard_map/ppermute | solution.py:401
  4.6 0.5 collective-permute-start.1
  5.1 0.1 collective-permute-start
  5.2 0.9 %slice-done = bf16[256,512]{1,0:T(8,128)(2,1)S(1)} async-done(((bf16[256,768]{1,0:T(8,128)(2,1)}), bf16[256,512]{1,0:T(8,128)(2,1)S(1)}, s32[]{:S(2)}) %slice-start) | async-done | bytes 262168 | tf_op jit(solution)/shard_map/slice | solution.py:435
  6.2 0.1 copy.17
  6.4 0.2 copy.15
  6.6 0.4 copy-done.10
  7.0 0.2 copy-done.9
  7.3 1.8 %collective-permute-done.1.refs_2_ = bf16[128,256]{1,0:T(8,128)(2,1)S(1)} collective-permute-done((bf16[128,256]{1,0:T(8,128)(2,1)}, bf16[128,256]{1,0:T(8,128)(2,1)S(1)}, u32[]{:S(2)}, u32[]{:S(2)}) %collective-permute-start.1) | collective-permute-done | bytes 65568 | tf_op jit(solution)/shard_map/ppermute | solution.py:401
  9.1 0.5 collective-permute-done.refs_1_
  9.6 0.7 copy-done.7
  10.3 4.8 %shard_map.136 = (bf16[8,16,768]{2,1,0:T(8,128)(2,1)}, bf16[512,256]{1,0:T(8,128)(2,1)S(1)}) custom-call(s32[1]{0:T(128)} %bitcast.5.idx, s32[4,4]{1,0:T(4,128)S(1)} %copy-done.7, bf16[128,256]{1,0:T(8,128)(2,1)S(1)} %bitcast.17, bf16[128,256]{1,0:T(8,128)(2,1)S(1)} %collective-permute-done.refs_1_, bf16[128,256]{1,0:T(8,128)(2,1)S(1)} %collective-permute-done.1.refs_2_, ...), custom_call_target="tpu_custom_call" | custom-call | flops 1 | bytes 1 | tf_op jit(solution)/shard_map/pallas_call | solution.py:82
  15.0 4.9 %all-to-all-start = ((bf16[8,16,768]{2,1,0:T(8,128)(2,1)}), bf16[8,16,768]{2,1,0:T(8,128)(2,1)S(1)}, u32[]{:S(2)}, u32[]{:S(2)}) async-start(bf16[8,16,768]{2,1,0:T(8,128)(2,1)} %get-tuple-element.52), calls=%async_computation | async-start | bytes 393216 | tf_op jit(solution)/shard_map/all_to_all | solution.py:396
  19.9 1.8 %shard_map.137 = (bf16[2,512,512]{2,1,0:T(8,128)(2,1)S(1)}, bf16[512,64]{1,0:T(8,128)(2,1)S(1)}, bf16[512,64]{1,0:T(8,128)(2,1)S(1)}, bf16[64,512]{1,0:T(8,128)(2,1)S(1)}) custom-call(s32[1]{0:T(128)} %bitcast.5.idx, s32[4,4]{1,0:T(4,128)S(1)} %copy-done.7, bf16[512,256]{1,0:T(8,128)(2,1)S(1)} %get-tuple-element.53.normed_ref.normed, ...), custom_call_target="tpu_custom_call" | custom-call | flops 20000000000 | bytes 72000000 | tf_op jit(solution)/shard_map/pallas_call | solution.py:82
  21.7 6.6 %all-to-all-done.x_in = bf16[8,16,768]{2,1,0:T(8,128)(2,1)S(1)} async-done(((bf16[8,16,768]{2,1,0:T(8,128)(2,1)}), bf16[8,16,768]{2,1,0:T(8,128)(2,1)S(1)}, u32[]{:S(2)}, u32[]{:S(2)}) %all-to-all-start) | async-done | bytes 196640 | tf_op jit(solution)/shard_map/all_to_all | solution.py:396
  28.2 3.3 %shard_map.138 = (bf16[32,8,128]{2,1,0:T(8,128)(2,1)}, bf16[128,1280]{1,0:T(8,128)(2,1)S(1)}, bf16[128,1280]{1,0:T(8,128)(2,1)}, bf16[8,16,512]{2,1,0:T(8,128)(2,1)}) custom-call(s32[1]{0:T(128)} %bitcast.hap, bf16[8,16,768]{2,1,0:T(8,128)(2,1)S(1)} %all-to-all-done.x_in, bf16[256,256]{1,0:T(8,128)(2,1)S(1)} %copy-done.1, ...), custom_call_target="tpu_custom_call" | custom-call | flops 1 | bytes 1 | tf_op jit(solution)/shard_map/pallas_call | solution.py:82
  31.7 2.7 %all-to-all-start.1 = ((bf16[32,8,128]{2,1,0:T(8,128)(2,1)}), bf16[32,8,128]{2,1,0:T(8,128)(2,1)S(1)}, u32[]{:S(2)}, u32[]{:S(2)}) async-start(bf16[32,8,128]{2,1,0:T(8,128)(2,1)} %get-tuple-element.56), calls=%async_computation.1 | async-start | bytes 131072 | tf_op jit(solution)/shard_map/all_to_all | solution.py:396
  34.4 0.3 collective-permute-start.4
  34.7 1.0 %copy-done.2 = bf16[128,1280]{1,0:T(8,128)(2,1)S(1)} copy-done((bf16[128,1280]{1,0:T(8,128)(2,1)S(1)}, bf16[128,1280]{1,0:T(8,128)(2,1)}, u32[]{:S(2)}) %copy-start.2) | copy-done | bytes 327704
  35.7 0.2 shard_map.139
  35.9 1.7 %collective-permute-start.6 = (bf16[32,1280]{1,0:T(8,128)(2,1)S(1)}, bf16[32,1280]{1,0:T(8,128)(2,1)S(1)}, u32[]{:S(2)}, u32[]{:S(2)}) collective-permute-start(bf16[32,1280]{1,0:T(8,128)(2,1)S(1)} %get-tuple-element.60), channel_id=1, source_target_pairs={{0,2},{1,3},{2,0},{3,1},{4,6},{5,7},{6,4},{7,5},{8,10},{9,11},{10,... | collective-permute-start | bytes 245768 | tf_op jit(solution)/shard_map/ppermute | solution.py:401
  37.6 2.4 %collective-permute-start.7 = (bf16[32,1280]{1,0:T(8,128)(2,1)S(1)}, bf16[32,1280]{1,0:T(8,128)(2,1)S(1)}, u32[]{:S(2)}, u32[]{:S(2)}) collective-permute-start(bf16[32,1280]{1,0:T(8,128)(2,1)S(1)} %get-tuple-element.61), channel_id=1, source_target_pairs={{0,4},{1,5},{2,6},{3,7},{4,0},{5,1},{6,2},{7,3},{8,12},{9,13},{10,... | collective-permute-start | bytes 245768 | tf_op jit(solution)/shard_map/ppermute | solution.py:401
  40.0 0.3 collective-permute-start.8
  40.3 1.4 %all-to-all-done.1.g_in = bf16[32,8,128]{2,1,0:T(8,128)(2,1)S(1)} async-done(((bf16[32,8,128]{2,1,0:T(8,128)(2,1)}), bf16[32,8,128]{2,1,0:T(8,128)(2,1)S(1)}, u32[]{:S(2)}, u32[]{:S(2)}) %all-to-all-start.1) | async-done | bytes 65568 | tf_op jit(solution)/shard_map/all_to_all | solution.py:396
  41.7 2.1 %shard_map.141 = (bf16[128,192]{1,0:T(8,128)(2,1)S(1)}, bf16[128,192]{1,0:T(8,128)(2,1)S(1)}, bf16[128,192]{1,0:T(8,128)(2,1)S(1)}, bf16[128,192]{1,0:T(8,128)(2...) custom-call(s32[1]{0:T(128)} %bitcast.5.idx, s32[1]{0:T(128)S(6)} %select_n.7.core, ...), custom_call_target="tpu_custom_call" | custom-call | flops 1 | bytes 1 | tf_op jit(solution)/shard_map/pallas_call | solution.py:82
  43.9 0.2 collective-permute-start.5
  44.0 1.1 %collective-permute-done.5.row_got = bf16[96,256]{1,0:T(8,128)(2,1)S(1)} collective-permute-done((bf16[96,256]{1,0:T(8,128)(2,1)S(1)}, bf16[96,256]{1,0:T(8,128)(2,1)S(1)}, u32[]{:S(2)}, u32[]{:S(2)}) %collective-permute-start.5) | collective-permute-done | bytes 49184 | tf_op jit(solution)/shard_map/ppermute | solution.py:401
  45.2 2.0 %collective-permute-done.7.refs_2_ = bf16[32,1280]{1,0:T(8,128)(2,1)S(1)} collective-permute-done((bf16[32,1280]{1,0:T(8,128)(2,1)S(1)}, bf16[32,1280]{1,0:T(8,128)(2,1)S(1)}, u32[]{:S(2)}, u32[]{:S(2)}) %collective-permute-start.7) | collective-permute-done | bytes 81952 | tf_op jit(solution)/shard_map/ppermute | solution.py:401
  47.2 0.9 %shard_map.143 = bf16[4,288,256]{2,1,0:T(8,128)(2,1)} custom-call(s32[1]{0:T(128)} %bitcast.5.idx, bf16[32,1280]{1,0:T(8,128)(2,1)S(1)} %get-tuple-element.59.refs_0_, bf16[32,1280]{1,0:T(8,128)(2,1)S(1)} %collective-permute-done.6.refs_1_, bf16[32,1280]{1,0:T(8,128)(2,1)S(1)} %collective-permute-done.7.refs_2_, ...), custom_call_target="tpu_custom_call" | custom-call | flops 1 | bytes 1 | tf_op jit(solution)/shard_map/pallas_call | solution.py:82
  48.1 3.6 %all-to-all-start.2 = ((bf16[4,288,256]{2,1,0:T(8,128)(2,1)}), bf16[4,288,256]{2,1,0:T(8,128)(2,1)S(1)}, u32[]{:S(2)}, u32[]{:S(2)}) async-start(bf16[4,288,256]{2,1,0:T(8,128)(2,1)} %shard_map.143), calls=%async_computation.2 | async-start | bytes 1179648 | tf_op jit(solution)/shard_map/all_to_all | solution.py:396
  51.7 1.6 %collective-permute-start.9 = (bf16[160,256]{1,0:T(8,128)(2,1)S(1)}, bf16[160,256]{1,0:T(8,128)(2,1)S(1)}, u32[]{:S(2)}, u32[]{:S(2)}) collective-permute-start(bf16[160,256]{1,0:T(8,128)(2,1)S(1)} %get-tuple-element.82), channel_id=1, source_target_pairs={{0,2},{1,3},{2,0},{3,1},{4,6},{5,7},{6,4},{7,5},{8,10},{9,11},{10,... | collective-permute-start | bytes 245768 | tf_op jit(solution)/shard_map/ppermute | solution.py:401
  53.3 1.5 %collective-permute-start.10 = (bf16[160,256]{1,0:T(8,128)(2,1)S(1)}, bf16[160,256]{1,0:T(8,128)(2,1)S(1)}, u32[]{:S(2)}, u32[]{:S(2)}) collective-permute-start(bf16[160,256]{1,0:T(8,128)(2,1)S(1)} %get-tuple-element.83), channel_id=1, source_target_pairs={{0,4},{1,5},{2,6},{3,7},{4,0},{5,1},{6,2},{7,3},{8,12},{9,13},{10,... | collective-permute-start | bytes 245768 | tf_op jit(solution)/shard_map/ppermute | solution.py:401
  54.8 1.3 %collective-permute-start.11 = (bf16[160,256]{1,0:T(8,128)(2,1)S(1)}, bf16[160,256]{1,0:T(8,128)(2,1)S(1)}, u32[]{:S(2)}, u32[]{:S(2)}) collective-permute-start(bf16[160,256]{1,0:T(8,128)(2,1)S(1)} %get-tuple-element.84), channel_id=1, source_target_pairs={{0,6},{1,7},{2,4},{3,5},{4,2},{5,3},{6,0},{7,1},{8,14},{9,15},{10,... | collective-permute-start | bytes 245768 | tf_op jit(solution)/shard_map/ppermute | solution.py:401
  56.1 0.3 collective-permute-done.9.refs_1_
  56.4 5.6 %collective-permute-done.10.refs_2_ = bf16[160,256]{1,0:T(8,128)(2,1)S(1)} collective-permute-done((bf16[160,256]{1,0:T(8,128)(2,1)S(1)}, bf16[160,256]{1,0:T(8,128)(2,1)S(1)}, u32[]{:S(2)}, u32[]{:S(2)}) %collective-permute-start.10) | collective-permute-done | bytes 81952 | tf_op jit(solution)/shard_map/ppermute | solution.py:401
  62.0 0.7 shard_map.145
  62.7 3.8 %all-to-all-start.3 = ((bf16[4,96,256]{2,1,0:T(8,128)(2,1)}), bf16[4,96,256]{2,1,0:T(8,128)(2,1)S(1)}, u32[]{:S(2)}, u32[]{:S(2)}) async-start(bf16[4,96,256]{2,1,0:T(8,128)(2,1)} %shard_map.145), calls=%async_computation.3 | async-start | bytes 393216 | tf_op jit(solution)/shard_map/all_to_all | solution.py:396
  66.5 2.0 %collective-permute-start.14 = (bf16[160,256]{1,0:T(8,128)(2,1)S(1)}, bf16[160,256]{1,0:T(8,128)(2,1)S(1)}, u32[]{:S(2)}, u32[]{:S(2)}) collective-permute-start(bf16[160,256]{1,0:T(8,128)(2,1)S(1)} %shard_map.146.refs_0_), channel_id=1, source_target_pairs={{0,6},{1,7},{2,4},{3,5},{4,2},{5,3},{6,0},{7,1},{8,14},{9,15},{10,... | collective-permute-start | bytes 245768 | tf_op jit(solution)/shard_map/ppermute | solution.py:401
  68.5 1.0 %collective-permute-start.13 = (bf16[160,256]{1,0:T(8,128)(2,1)S(1)}, bf16[160,256]{1,0:T(8,128)(2,1)S(1)}, u32[]{:S(2)}, u32[]{:S(2)}) collective-permute-start(bf16[160,256]{1,0:T(8,128)(2,1)S(1)} %shard_map.146.refs_0_), channel_id=1, source_target_pairs={{0,4},{1,5},{2,6},{3,7},{4,0},{5,1},{6,2},{7,3},{8,12},{9,13},{10,... | collective-permute-start | bytes 245768 | tf_op jit(solution)/shard_map/ppermute | solution.py:401
  69.5 1.4 %collective-permute-start.12 = (bf16[160,256]{1,0:T(8,128)(2,1)S(1)}, bf16[160,256]{1,0:T(8,128)(2,1)S(1)}, u32[]{:S(2)}, u32[]{:S(2)}) collective-permute-start(bf16[160,256]{1,0:T(8,128)(2,1)S(1)} %shard_map.146.refs_0_), channel_id=1, source_target_pairs={{0,2},{1,3},{2,0},{3,1},{4,6},{5,7},{6,4},{7,5},{8,10},{9,11},{10,... | collective-permute-start | bytes 245768 | tf_op jit(solution)/shard_map/ppermute | solution.py:401
  70.9 2.0 %collective-permute-done.14.refs_6_ = bf16[160,256]{1,0:T(8,128)(2,1)S(1)} collective-permute-done((bf16[160,256]{1,0:T(8,128)(2,1)S(1)}, bf16[160,256]{1,0:T(8,128)(2,1)S(1)}, u32[]{:S(2)}, u32[]{:S(2)}) %collective-permute-start.14) | collective-permute-done | bytes 81952 | tf_op jit(solution)/shard_map/ppermute | solution.py:401
  72.9 2.3 %collective-permute-done.13.refs_4_ = bf16[160,256]{1,0:T(8,128)(2,1)S(1)} collective-permute-done((bf16[160,256]{1,0:T(8,128)(2,1)S(1)}, bf16[160,256]{1,0:T(8,128)(2,1)S(1)}, u32[]{:S(2)}, u32[]{:S(2)}) %collective-permute-start.13) | collective-permute-done | bytes 81952 | tf_op jit(solution)/shard_map/ppermute | solution.py:401
  75.2 0.5 collective-permute-start.16
  75.7 0.4 collective-permute-start.18
  76.2 0.1 collective-permute-start.19
  76.3 0.9 %shard_map.144 = (bf16[128,256]{1,0:T(8,128)(2,1)}, bf16[128,256]{1,0:T(8,128)(2,1)}) custom-call(s32[1]{0:T(128)} %bitcast.hap, bf16[128,256]{1,0:T(8,128)(2,1)S(1)} %bitcast.18, f32[2,256]{1,0:T(2,128)S(1)} %pad_maximum_fusion.refs_5_.gain, bf16[768,256]{1,0:T(8,128)(2,1)S(1)} %bitcast.12, bf16[4,288,256]{2,1,0:T(8,128)(2,1)S(1)} %all-to-all-done.2.gps.got, ...), custom_call_target="tpu_custom_call" | custom-call | flops 1 | bytes 1 | tf_op jit(solution)/shard_map/pallas_call | solution.py:82
  77.2 0.2 collective-permute-done.19.refs_7_
  77.5 1.5 %shard_map.147 = (f32[256,768]{1,0:T(8,128)}, f32[256,256]{1,0:T(8,128)}, f32[256,768]{1,0:T(8,128)}, f32[256,256]{1,0:T(8,128)}) custom-call(s32[1]{0:T(128)} %bitcast.hap, bf16[4,96,256]{2,1,0:T(8,128)(2,1)S(1)} %all-to-all-done.3.row_own, bf16[4,96,256]{2,1,0:T(8,128)(2,1)S(1)} %collective-permute-done.15.row_other, ...), custom_call_target="tpu_custom_call" | custom-call | flops 1 | bytes 1 | tf_op jit(solution)/shard_map/pallas_call | solution.py:82
  (39 shorter events, 0.3 us)
Async XLA Ops:
  0.6 6.6 %collective-permute-start.2 = (bf16[128,256]{1,0:T(8,128)(2,1)}, bf16[128,256]{1,0:T(8,128)(2,1)S(1)}, u32[]{:S(2)}, u32[]{:S(2)}) collective-permute-start(bf16[128,256]{1,0:T(8,128)(2,1)} %bitcast.14), channel_id=1, source_target_pairs={{0,24},{8,16},{16,8},{24,0},{1,25},{9,17},{17,9},{25,1},{2,26},{10... | collective-permute-start | bytes 196616 | tf_op jit(solution)/shard_map/ppermute | solution.py:401
  4.6 4.5 %collective-permute-start.1 = (bf16[128,256]{1,0:T(8,128)(2,1)}, bf16[128,256]{1,0:T(8,128)(2,1)S(1)}, u32[]{:S(2)}, u32[]{:S(2)}) collective-permute-start(bf16[128,256]{1,0:T(8,128)(2,1)} %bitcast.15), channel_id=1, source_target_pairs={{0,16},{8,24},{16,0},{24,8},{1,17},{9,25},{17,1},{25,9},{2,18},{10... | collective-permute-start | bytes 196616 | tf_op jit(solution)/shard_map/ppermute | solution.py:401
  5.1 4.5 %collective-permute-start = (bf16[128,256]{1,0:T(8,128)(2,1)}, bf16[128,256]{1,0:T(8,128)(2,1)S(1)}, u32[]{:S(2)}, u32[]{:S(2)}) collective-permute-start(bf16[128,256]{1,0:T(8,128)(2,1)} %bitcast.16), channel_id=1, source_target_pairs={{0,8},{8,0},{16,24},{24,16},{1,9},{9,1},{17,25},{25,17},{2,10},{10... | collective-permute-start | bytes 196616 | tf_op jit(solution)/shard_map/ppermute | solution.py:401
  5.2 0.9 %slice-start = ((bf16[256,768]{1,0:T(8,128)(2,1)}), bf16[256,512]{1,0:T(8,128)(2,1)S(1)}, s32[]{:S(2)}) async-start(bf16[256,768]{1,0:T(8,128)(2,1)} %col_proj.1), calls=%async_computation.4 | async-start | bytes 524288 | tf_op jit(solution)/shard_map/slice | solution.py:435
  5.2 1.1 %copy-start.8 = (bf16[256,768]{1,0:T(8,128)(2,1)S(1)}, bf16[256,768]{1,0:T(8,128)(2,1)}, u32[]{:S(2)}) copy-start(bf16[256,768]{1,0:T(8,128)(2,1)} %param.12) | copy-start | bytes 1179652
  6.3 0.7 copy-start.10
  6.3 3.2 %copy-start.1 = (bf16[256,256]{1,0:T(8,128)(2,1)S(1)}, bf16[256,256]{1,0:T(8,128)(2,1)}, u32[]{:S(2)}) copy-start(bf16[256,256]{1,0:T(8,128)(2,1)} %row_out.1) | copy-start | bytes 393220
  6.4 3.2 %copy-start.3 = (bf16[128,1,256]{2,0,1:T(8,128)(2,1)S(1)}, bf16[128,1,256]{2,0,1:T(8,128)(2,1)}, u32[]{:S(2)}) copy-start(bf16[128,1,256]{2,0,1:T(8,128)(2,1)} %param.9) | copy-start | bytes 196612
  6.4 3.2 %copy-start.6 = (bf16[128,1,256]{2,0,1:T(8,128)(2,1)S(1)}, bf16[128,1,256]{2,0,1:T(8,128)(2,1)}, u32[]{:S(2)}) copy-start(bf16[128,1,256]{2,0,1:T(8,128)(2,1)} %param.17) | copy-start | bytes 196612
  6.6 0.7 copy-start.9
  9.6 0.7 copy-start.7
  15.0 13.2 %all-to-all-start = ((bf16[8,16,768]{2,1,0:T(8,128)(2,1)}), bf16[8,16,768]{2,1,0:T(8,128)(2,1)S(1)}, u32[]{:S(2)}, u32[]{:S(2)}) async-start(bf16[8,16,768]{2,1,0:T(8,128)(2,1)} %get-tuple-element.52), calls=%async_computation | async-start | bytes 393216 | tf_op jit(solution)/shard_map/all_to_all | solution.py:396
  19.9 8.3 %copy-start = (bf16[256,768]{1,0:T(8,128)(2,1)S(1)}, bf16[256,768]{1,0:T(8,128)(2,1)}, u32[]{:S(2)}) copy-start(bf16[256,768]{1,0:T(8,128)(2,1)} %col_proj.1) | copy-start | bytes 1179652
  19.9 8.3 %copy-start.5 = (bf16[256,256]{1,0:T(8,128)(2,1)S(1)}, bf16[256,256]{1,0:T(8,128)(2,1)}, u32[]{:S(2)}) copy-start(bf16[256,256]{1,0:T(8,128)(2,1)} %col_out.1) | copy-start | bytes 393220
  31.6 2.8 %copy-start.4 = (bf16[8,16,512]{2,1,0:T(8,128)(2,1)S(1)}, bf16[8,16,512]{2,1,0:T(8,128)(2,1)}, u32[]{:S(2)}) copy-start(bf16[8,16,512]{2,1,0:T(8,128)(2,1)} %get-tuple-element.63.og) | copy-start | bytes 393220
  31.6 3.1 %collective-permute-start.3 = (bf16[128,1280]{1,0:T(8,128)(2,1)S(1)}, bf16[128,1280]{1,0:T(8,128)(2,1)S(1)}, u32[]{:S(2)}, u32[]{:S(2)}) collective-permute-start(bf16[128,1280]{1,0:T(8,128)(2,1)S(1)} %get-tuple-element.58), channel_id=1, source_target_pairs={{0,1},{1,0},{2,3},{3,2},{4,5},{5,4},{6,7},{7,6},{8,9},{9,8},{10,11... | collective-permute-start | bytes 983048 | tf_op jit(solution)/shard_map/ppermute | solution.py:401
  31.7 10.1 %all-to-all-start.1 = ((bf16[32,8,128]{2,1,0:T(8,128)(2,1)}), bf16[32,8,128]{2,1,0:T(8,128)(2,1)S(1)}, u32[]{:S(2)}, u32[]{:S(2)}) async-start(bf16[32,8,128]{2,1,0:T(8,128)(2,1)} %get-tuple-element.56), calls=%async_computation.1 | async-start | bytes 131072 | tf_op jit(solution)/shard_map/all_to_all | solution.py:396
  34.4 5.9 %collective-permute-start.4 = (bf16[4,16,512]{2,1,0:T(8,128)(2,1)S(1)}, bf16[4,16,512]{2,1,0:T(8,128)(2,1)S(1)}, u32[]{:S(2)}, u32[]{:S(2)}) collective-permute-start(bf16[4,16,512]{2,1,0:T(8,128)(2,1)S(1)} %get-tuple-element.64), channel_id=1, source_target_pairs={{0,1},{1,0},{2,3},{3,2},{4,5},{5,4},{6,7},{7,6},{8,9},{9,8},{10,11... | collective-permute-start | bytes 196616 | tf_op jit(solution)/shard_map/ppermute | solution.py:401
  34.7 1.0 %copy-start.2 = (bf16[128,1280]{1,0:T(8,128)(2,1)S(1)}, bf16[128,1280]{1,0:T(8,128)(2,1)}, u32[]{:S(2)}) copy-start(bf16[128,1280]{1,0:T(8,128)(2,1)} %get-tuple-element.57.keep) | copy-start | bytes 983044
  35.9 9.3 %collective-permute-start.6 = (bf16[32,1280]{1,0:T(8,128)(2,1)S(1)}, bf16[32,1280]{1,0:T(8,128)(2,1)S(1)}, u32[]{:S(2)}, u32[]{:S(2)}) collective-permute-start(bf16[32,1280]{1,0:T(8,128)(2,1)S(1)} %get-tuple-element.60), channel_id=1, source_target_pairs={{0,2},{1,3},{2,0},{3,1},{4,6},{5,7},{6,4},{7,5},{8,10},{9,11},{10,... | collective-permute-start | bytes 245768 | tf_op jit(solution)/shard_map/ppermute | solution.py:401
  37.6 9.6 %collective-permute-start.7 = (bf16[32,1280]{1,0:T(8,128)(2,1)S(1)}, bf16[32,1280]{1,0:T(8,128)(2,1)S(1)}, u32[]{:S(2)}, u32[]{:S(2)}) collective-permute-start(bf16[32,1280]{1,0:T(8,128)(2,1)S(1)} %get-tuple-element.61), channel_id=1, source_target_pairs={{0,4},{1,5},{2,6},{3,7},{4,0},{5,1},{6,2},{7,3},{8,12},{9,13},{10,... | collective-permute-start | bytes 245768 | tf_op jit(solution)/shard_map/ppermute | solution.py:401
  40.0 7.2 %collective-permute-start.8 = (bf16[32,1280]{1,0:T(8,128)(2,1)S(1)}, bf16[32,1280]{1,0:T(8,128)(2,1)S(1)}, u32[]{:S(2)}, u32[]{:S(2)}) collective-permute-start(bf16[32,1280]{1,0:T(8,128)(2,1)S(1)} %get-tuple-element.62), channel_id=1, source_target_pairs={{0,6},{1,7},{2,4},{3,5},{4,2},{5,3},{6,0},{7,1},{8,14},{9,15},{10,... | collective-permute-start | bytes 245768 | tf_op jit(solution)/shard_map/ppermute | solution.py:401
  43.9 1.3 %collective-permute-start.5 = (bf16[96,256]{1,0:T(8,128)(2,1)S(1)}, bf16[96,256]{1,0:T(8,128)(2,1)S(1)}, u32[]{:S(2)}, u32[]{:S(2)}) collective-permute-start(bf16[96,256]{1,0:T(8,128)(2,1)S(1)} %get-tuple-element.70), channel_id=1, source_target_pairs={{0,1},{1,0},{2,3},{3,2},{4,5},{5,4},{6,7},{7,6},{8,9},{9,8},{10,11... | collective-permute-start | bytes 147464 | tf_op jit(solution)/shard_map/ppermute | solution.py:401
  48.1 14.6 %all-to-all-start.2 = ((bf16[4,288,256]{2,1,0:T(8,128)(2,1)}), bf16[4,288,256]{2,1,0:T(8,128)(2,1)S(1)}, u32[]{:S(2)}, u32[]{:S(2)}) async-start(bf16[4,288,256]{2,1,0:T(8,128)(2,1)} %shard_map.143), calls=%async_computation.2 | async-start | bytes 1179648 | tf_op jit(solution)/shard_map/all_to_all | solution.py:396
  51.7 4.7 %collective-permute-start.9 = (bf16[160,256]{1,0:T(8,128)(2,1)S(1)}, bf16[160,256]{1,0:T(8,128)(2,1)S(1)}, u32[]{:S(2)}, u32[]{:S(2)}) collective-permute-start(bf16[160,256]{1,0:T(8,128)(2,1)S(1)} %get-tuple-element.82), channel_id=1, source_target_pairs={{0,2},{1,3},{2,0},{3,1},{4,6},{5,7},{6,4},{7,5},{8,10},{9,11},{10,... | collective-permute-start | bytes 245768 | tf_op jit(solution)/shard_map/ppermute | solution.py:401
  53.3 8.6 %collective-permute-start.10 = (bf16[160,256]{1,0:T(8,128)(2,1)S(1)}, bf16[160,256]{1,0:T(8,128)(2,1)S(1)}, u32[]{:S(2)}, u32[]{:S(2)}) collective-permute-start(bf16[160,256]{1,0:T(8,128)(2,1)S(1)} %get-tuple-element.83), channel_id=1, source_target_pairs={{0,4},{1,5},{2,6},{3,7},{4,0},{5,1},{6,2},{7,3},{8,12},{9,13},{10,... | collective-permute-start | bytes 245768 | tf_op jit(solution)/shard_map/ppermute | solution.py:401
  54.8 7.2 %collective-permute-start.11 = (bf16[160,256]{1,0:T(8,128)(2,1)S(1)}, bf16[160,256]{1,0:T(8,128)(2,1)S(1)}, u32[]{:S(2)}, u32[]{:S(2)}) collective-permute-start(bf16[160,256]{1,0:T(8,128)(2,1)S(1)} %get-tuple-element.84), channel_id=1, source_target_pairs={{0,6},{1,7},{2,4},{3,5},{4,2},{5,3},{6,0},{7,1},{8,14},{9,15},{10,... | collective-permute-start | bytes 245768 | tf_op jit(solution)/shard_map/ppermute | solution.py:401
  62.7 12.4 %all-to-all-start.3 = ((bf16[4,96,256]{2,1,0:T(8,128)(2,1)}), bf16[4,96,256]{2,1,0:T(8,128)(2,1)S(1)}, u32[]{:S(2)}, u32[]{:S(2)}) async-start(bf16[4,96,256]{2,1,0:T(8,128)(2,1)} %shard_map.145), calls=%async_computation.3 | async-start | bytes 393216 | tf_op jit(solution)/shard_map/all_to_all | solution.py:396
  66.5 6.3 %collective-permute-start.14 = (bf16[160,256]{1,0:T(8,128)(2,1)S(1)}, bf16[160,256]{1,0:T(8,128)(2,1)S(1)}, u32[]{:S(2)}, u32[]{:S(2)}) collective-permute-start(bf16[160,256]{1,0:T(8,128)(2,1)S(1)} %shard_map.146.refs_0_), channel_id=1, source_target_pairs={{0,6},{1,7},{2,4},{3,5},{4,2},{5,3},{6,0},{7,1},{8,14},{9,15},{10,... | collective-permute-start | bytes 245768 | tf_op jit(solution)/shard_map/ppermute | solution.py:401
  68.5 6.7 %collective-permute-start.13 = (bf16[160,256]{1,0:T(8,128)(2,1)S(1)}, bf16[160,256]{1,0:T(8,128)(2,1)S(1)}, u32[]{:S(2)}, u32[]{:S(2)}) collective-permute-start(bf16[160,256]{1,0:T(8,128)(2,1)S(1)} %shard_map.146.refs_0_), channel_id=1, source_target_pairs={{0,4},{1,5},{2,6},{3,7},{4,0},{5,1},{6,2},{7,3},{8,12},{9,13},{10,... | collective-permute-start | bytes 245768 | tf_op jit(solution)/shard_map/ppermute | solution.py:401
  69.5 5.7 %collective-permute-start.12 = (bf16[160,256]{1,0:T(8,128)(2,1)S(1)}, bf16[160,256]{1,0:T(8,128)(2,1)S(1)}, u32[]{:S(2)}, u32[]{:S(2)}) collective-permute-start(bf16[160,256]{1,0:T(8,128)(2,1)S(1)} %shard_map.146.refs_0_), channel_id=1, source_target_pairs={{0,2},{1,3},{2,0},{3,1},{4,6},{5,7},{6,4},{7,5},{8,10},{9,11},{10,... | collective-permute-start | bytes 245768 | tf_op jit(solution)/shard_map/ppermute | solution.py:401
  75.2 2.3 %collective-permute-start.15 = (bf16[4,96,256]{2,1,0:T(8,128)(2,1)S(1)}, bf16[4,96,256]{2,1,0:T(8,128)(2,1)S(1)}, u32[]{:S(2)}, u32[]{:S(2)}) collective-permute-start(bf16[4,96,256]{2,1,0:T(8,128)(2,1)S(1)} %all-to-all-done.3.row_own), channel_id=1, source_target_pairs={{0,1},{1,0},{2,3},{3,2},{4,5},{5,4},{6,7},{7,6},{8,9},{9,8},{10,11... | collective-permute-start | bytes 589832 | tf_op jit(solution)/shard_map/ppermute | solution.py:401
  75.2 2.0 %collective-permute-start.16 = (bf16[160,256]{1,0:T(8,128)(2,1)S(1)}, bf16[160,256]{1,0:T(8,128)(2,1)S(1)}, u32[]{:S(2)}, u32[]{:S(2)}) collective-permute-start(bf16[160,256]{1,0:T(8,128)(2,1)S(1)} %shard_map.146.refs_0_), channel_id=1, source_target_pairs={{0,1},{1,0},{2,3},{3,2},{4,5},{5,4},{6,7},{7,6},{8,9},{9,8},{10,11... | collective-permute-start | bytes 245768 | tf_op jit(solution)/shard_map/ppermute | solution.py:401
  75.7 1.5 %collective-permute-start.17 = (bf16[160,256]{1,0:T(8,128)(2,1)S(1)}, bf16[160,256]{1,0:T(8,128)(2,1)S(1)}, u32[]{:S(2)}, u32[]{:S(2)}) collective-permute-start(bf16[160,256]{1,0:T(8,128)(2,1)S(1)} %collective-permute-done.12.refs_2_), channel_id=1, source_target_pairs={{0,1},{1,0},{2,3},{3,2},{4,5},{5,4},{6,7},{7,6},{8,9},{9,8},{10,11... | collective-permute-start | bytes 245768 | tf_op jit(solution)/shard_map/ppermute | solution.py:401
  75.7 1.5 %collective-permute-start.18 = (bf16[160,256]{1,0:T(8,128)(2,1)S(1)}, bf16[160,256]{1,0:T(8,128)(2,1)S(1)}, u32[]{:S(2)}, u32[]{:S(2)}) collective-permute-start(bf16[160,256]{1,0:T(8,128)(2,1)S(1)} %collective-permute-done.13.refs_4_), channel_id=1, source_target_pairs={{0,1},{1,0},{2,3},{3,2},{4,5},{5,4},{6,7},{7,6},{8,9},{9,8},{10,11... | collective-permute-start | bytes 245768 | tf_op jit(solution)/shard_map/ppermute | solution.py:401
  76.2 1.3 %collective-permute-start.19 = (bf16[160,256]{1,0:T(8,128)(2,1)S(1)}, bf16[160,256]{1,0:T(8,128)(2,1)S(1)}, u32[]{:S(2)}, u32[]{:S(2)}) collective-permute-start(bf16[160,256]{1,0:T(8,128)(2,1)S(1)} %collective-permute-done.14.refs_6_), channel_id=1, source_target_pairs={{0,1},{1,0},{2,3},{3,2},{4,5},{5,4},{6,7},{7,6},{8,9},{9,8},{10,11... | collective-permute-start | bytes 245768 | tf_op jit(solution)/shard_map/ppermute | solution.py:401

commit v9 on v7

--- a/solution.py
+++ b/solution.py
@@ -119,12 +119,19 @@
     key = mm_nt(normed, w_t[width : 2 * width, :]).astype(BF16)
     v_t = mm_nt(w_t[2 * width :, :], normed).astype(BF16)
     q_st = jnp.concatenate([only_head(q, h) for h in range(heads)], axis=0)
+    bias = [jnp.where(link[me, me ^ a] > 0, 0.0, -jnp.inf) for a in range(sites)]
+    ones = jnp.ones((16, sites * rows), BF16)
     att_t = []
     for h in range(heads):
         scores = mm_nt(key, q_st[h * rows : (h + 1) * rows]) * (SCALE * LOG2E)
-        parts, inverse = exp_parts(linked_scores(scores, rows, sites, me, 0, link))
-        e_h = jnp.concatenate([part.astype(BF16) for part in parts], axis=0)
-        att_t.append(mm(v_t[h * HEAD_DIM : (h + 1) * HEAD_DIM], e_h) * inverse)
+        parts = [scores[a * rows : (a + 1) * rows] for a in range(sites)]
+        highs = [jnp.max(parts[a], axis=0, keepdims=True) + bias[a] for a in range(sites)]
+        high = functools.reduce(jnp.maximum, highs)
+        e_h = [jnp.exp2(parts[a] - (high - bias[a])).astype(BF16) for a in range(sites)]
+        e_h = jnp.concatenate(e_h, axis=0)
+        with_ones = jnp.concatenate([v_t[h * HEAD_DIM : (h + 1) * HEAD_DIM], ones], axis=0)
+        mixed = mm(with_ones, e_h)
+        att_t.append(mixed[:HEAD_DIM] / mixed[HEAD_DIM : HEAD_DIM + 1])
     att = jnp.transpose(jnp.concatenate(att_t, axis=0)).astype(BF16)
     hid = pieces[0][...].astype(F32) + mm(att, row_out[...])
     joined = jnp.concatenate([hid, cot[...].astype(F32), att.astype(F32)], axis=1)
@@ -257,8 +264,7 @@
 
 
 def row_backward(sites, haps, idx, core, g_in, prob, q, val, key_t, normed, *refs):
-    gp_outs = refs[:sites]
-    keep, send, g_all, ds_all, w_out = refs[sites:]
+    gp_out, keep, send, g_all, ds_all, w_out = refs
     me = idx[0]
     total, width = q.shape
     rows = total // sites
@@ -292,13 +298,13 @@
     dq = jnp.transpose(dq_t).astype(BF16)
     joined = jnp.concatenate([dq, dk16, dv16], axis=1)
     for b in range(sites):
-        gp_outs[b][...] = joined[b * rows : (b + 1) * rows]
-
-
-def row_finish(sites, haps, idx, hap, feats, gain, w_t, gp, *refs):
-    gps, parts = refs[: sites - 1], refs[sites - 1 : sites - 1 + haps // 2]
-    out_ref, gf_ref, og = refs[sites - 1 + haps // 2 :]
-    me = idx[0]
+        gp_out[me ^ b, :, : 3 * width] = joined[b * rows : (b + 1) * rows]
+        gp_out[me ^ b, :, 3 * width :] = jnp.zeros((rows, gp_out.shape[2] - 3 * width), BF16)
+
+
+def row_finish(sites, haps, hap, feats, gain, w_t, gps, *refs):
+    parts = refs[: haps // 2]
+    out_ref, gf_ref, og = refs[haps // 2 :]
     rows, width = feats.shape
     group = width // sites
     per = rows // haps
@@ -308,12 +314,11 @@
             for side in range(2):
                 start = base + (2 * j + side) * per
                 og[side, hap[0] ^ (2 * m + j)] = parts[m][start : start + per, :].astype(F32)
-    grads = [gp[...]] + [g[g.shape[0] - rows :, : 3 * group] for g in gps]
     grad_normed = 0.0
-    for k in range(sites):
-        place = [pl.multiple_of(p * width + (me ^ k) * group, group) for p in range(3)]
-        weights = jnp.concatenate([w_t[pl.ds(p, group), :] for p in place], axis=0)
-        grad_normed = grad_normed + mm(grads[k], weights)
+    for i in range(sites):
+        place = [p * width + i * group for p in range(3)]
+        weights = jnp.concatenate([w_t[p : p + group, :] for p in place], axis=0)
+        grad_normed = grad_normed + mm(gps[i, :, : 3 * group], weights)
     xhat, rstd = norm_parts(feats[...].astype(F32))
     grad = og[1].reshape(rows, width) + norm_back(xhat, rstd, gain[:1, :], grad_normed)
     out_ref[...] = og[0].reshape(rows, width).astype(BF16)
@@ -336,18 +341,11 @@
         out[depth:, :] = jnp.concatenate(both, axis=0).astype(BF16)
 
 
-def weights_sum(haps, sites, *refs):
-    parts, gps = refs[: haps // 2], refs[haps // 2 : haps // 2 + sites - 1]
-    mine, outs = refs[haps // 2 + sites - 1], refs[haps // 2 + sites :]
-    depth, width = mine.shape
-    terms = [r[:depth, :].astype(F32) for r in parts]
+def weights_sum(*refs):
+    terms = [r[: refs[-1].shape[0], :].astype(F32) for r in refs[:-1]]
     while len(terms) > 1:
         terms = [a + b for a, b in zip(terms[::2], terms[1::2])]
-    mine[...] = terms[0].astype(BF16)
-    for gp, out in zip(gps, outs):
-        out[:depth, :] = mine[...]
-        out[depth:, : gp.shape[1]] = gp[...]
-        out[depth:, gp.shape[1] :] = jnp.zeros((gp.shape[0], width - gp.shape[1]), BF16)
+    refs[-1][...] = terms[0].astype(BF16)
 
 
 def weights_finish(sites, idx, core, *refs):
@@ -413,6 +411,7 @@
     cot = cotangent.reshape(rows, width)
 
     pieces = [feats] + [swapped(feats, "site", k) for k in range(1, sites)]
+    link_pattern = jnp.where(link_pattern > 0, 1, 0)
     gains = jnp.stack([row_gain, column_norm_gain])
     w_t = jnp.transpose(row_proj)
     kv_t_w = jnp.transpose(col_proj[:, width:])
@@ -464,9 +463,9 @@
     og_got = swapped(og_send, "hap", 1)
     g_in, _ = lax.optimization_barrier((g_in, (cols, og_got)))
     cols = [cols[0]] + [swapped(cols[k], "site", k) for k in range(1, sites)]
-    *gps, row_keep, row_send = call(
+    gps, row_keep, row_send = call(
         functools.partial(row_backward, sites, haps),
-        [((rows, 3 * group), BF16)] * sites + [((3 * group // 2, width), BF16)] * 2,
+        [((sites, rows, width), BF16)] + [((3 * group // 2, width), BF16)] * 2,
         idx, core, g_in, prob, q, val, key_t, normed, scalars=2,
         scratch=[
             pltpu.VMEM((total, group), BF16),
@@ -482,17 +481,16 @@
         row_keep, row_got, og_keep, og_got, *cols,
     )
     parts = [parts[0]] + [swapped(parts[m], "hap", 2 * m) for m in range(1, haps // 2)]
-    mine, *sends = call(
-        functools.partial(weights_sum, haps, sites),
-        [((depth, width), BF16)] + [((depth + rows, width), BF16)] * (sites - 1),
-        *parts, *gps[1:],
-    )
-    got = [swapped(sends[k - 1], "site", k) for k in range(1, sites)]
+    gps, _ = lax.optimization_barrier((gps, parts[1]))
+    gps = exchange(gps, "site")
+    parts, gps = lax.optimization_barrier((parts, gps))
+    (mine,) = call(weights_sum, [((depth, width), BF16)], *parts)
+    got = [swapped(mine, "site", k) for k in range(1, sites)]
     full = [x for p in [mine] + got for x in (p, swapped(p, "hap", 1))]
     out, grad = call(
         functools.partial(row_finish, sites, haps),
         [((rows, width), BF16)] * 2,
-        idx, hap, feats, gains, w_t, gps[0], *got, *parts, scalars=2,
+        hap, feats, gains, w_t, gps, *parts, scalars=1,
         scratch=[pltpu.VMEM((2, haps, per, width), F32)],
     )
     rp, ro, cp, co = call(

time: 75.5 us -> 82.6 us (1.094)
  the two profiles are of different devices: /device:TPU:9 before, /device:TPU:11 now
where the time goes in v9:
time: 82.6 us; the launch traced here: 82.1 us
  starting transfers between devices  33.5 us (41%)
  waiting for transfers between devices  28.9 us (35%)
  Pallas kernels  15.3 us (19%)
  local copies, waits for them, and re-layouts  3.62 us (4%)
    ppermute x19, waiting for transfers between devices, swapped(): return lax.ppermute(value, axis, [(i, i ^ by) for i in range(length)])  23.7 us
    ppermute x19, starting transfers between devices, swapped(): return lax.ppermute(value, axis, [(i, i ^ by) for i in range(length)])  18.1 us
    all_to_all x3, starting transfers between devices, exchange(): return lax.all_to_all(value, axis, 0, 0, tiled=True)  15.4 us
    pallas_call x10, Pallas kernels, call(): pl.pallas_call(body, out_shape=[jax.ShapeDtypeStruct(s, d) for s, d in ou...  15.3 us
    all_to_all x3, waiting for transfers between devices, exchange(): return lax.all_to_all(value, axis, 0, 0, tiled=True)  5.26 us
    unnamed x24, local copies, waits for them, and re-layouts  2.67 us
  transfers between devices with their start and end apart: 22, of which 10 were waited for; matrix products, arithmetic and copies ran while one was open for 0% of the time, Pallas kernels for 7%

profile of v9, /device:TPU:11, one launch (start us, length us, event | category | flops | bytes accessed | tf_op | source)
XLA Modules:
  0.0 82.1 jit_solution(298451716353958964)
XLA Ops:
  0.6 1.3 %collective-permute-start.2 = (bf16[128,256]{1,0:T(8,128)(2,1)}, bf16[128,256]{1,0:T(8,128)(2,1)S(1)}, u32[]{:S(2)}, u32[]{:S(2)}) collective-permute-start(bf16[128,256]{1,0:T(8,128)(2,1)} %bitcast.14), channel_id=1, source_target_pairs={{0,24},{8,16},{16,8},{24,0},{1,25},{9,17},{17,9},{25,1},{2,26},{10... | collective-permute-start | bytes 196616 | tf_op jit(solution)/shard_map/ppermute | solution.py:382
  1.9 0.2 collective-permute-start.1
  2.1 1.2 %collective-permute-start = (bf16[128,256]{1,0:T(8,128)(2,1)}, bf16[128,256]{1,0:T(8,128)(2,1)S(1)}, u32[]{:S(2)}, u32[]{:S(2)}) collective-permute-start(bf16[128,256]{1,0:T(8,128)(2,1)} %bitcast.16), channel_id=1, source_target_pairs={{0,8},{8,0},{16,24},{24,16},{1,9},{9,1},{17,25},{25,17},{2,10},{10... | collective-permute-start | bytes 196616 | tf_op jit(solution)/shard_map/ppermute | solution.py:382
  3.3 0.7 copy-done.8
  4.0 0.9 %slice-done = bf16[256,512]{1,0:T(8,128)(2,1)S(1)} async-done(((bf16[256,768]{1,0:T(8,128)(2,1)}), bf16[256,512]{1,0:T(8,128)(2,1)S(1)}, s32[]{:S(2)}) %slice-start) | async-done | bytes 262168 | tf_op jit(solution)/shard_map/slice | solution.py:417
  5.0 0.1 copy.17
  5.2 0.2 copy.15
  5.4 0.4 copy-done.10
  5.8 0.2 copy-done.9
  6.0 0.5 collective-permute-done.1.refs_2_
  6.6 4.7 %shard_map.136 = (bf16[8,16,768]{2,1,0:T(8,128)(2,1)}, bf16[512,256]{1,0:T(8,128)(2,1)S(1)}) custom-call(s32[1]{0:T(128)} %bitcast.5.idx, s32[4,4]{1,0:T(4,128)S(1)} %compare_select_fusion.link, bf16[128,256]{1,0:T(8,128)(2,1)S(1)} %bitcast.17, bf16[128,256]{1,0:T(8,128)(2,1)S(1)} %collective-permute-done.refs_1_, ...), custom_call_target="tpu_custom_call" | custom-call | flops 1 | bytes 1 | tf_op jit(solution)/shard_map/pallas_call | solution.py:82
  11.3 6.3 %all-to-all-start = ((bf16[8,16,768]{2,1,0:T(8,128)(2,1)}), bf16[8,16,768]{2,1,0:T(8,128)(2,1)S(1)}, u32[]{:S(2)}, u32[]{:S(2)}) async-start(bf16[8,16,768]{2,1,0:T(8,128)(2,1)} %get-tuple-element.43), calls=%async_computation | async-start | bytes 393216 | tf_op jit(solution)/shard_map/all_to_all | solution.py:377
  17.6 1.8 %shard_map.137 = (bf16[2,512,512]{2,1,0:T(8,128)(2,1)S(1)}, bf16[512,64]{1,0:T(8,128)(2,1)S(1)}, bf16[512,64]{1,0:T(8,128)(2,1)S(1)}, bf16[64,512]{1,0:T(8,128)(2,1)S(1)}) custom-call(s32[1]{0:T(128)} %bitcast.5.idx, s32[4,4]{1,0:T(4,128)S(1)} %compare_select_fusion.link, bf16[512,256]{1,0:T(8,128)(2,1)S(1)} %get-tuple-element.44.normed_ref.normed, ...), custom_call_target="tpu_custom_call" | custom-call | flops 20000000000 | bytes 72000000 | tf_op jit(solution)/shard_map/pallas_call | solution.py:82
  19.3 4.4 %all-to-all-done.x_in = bf16[8,16,768]{2,1,0:T(8,128)(2,1)S(1)} async-done(((bf16[8,16,768]{2,1,0:T(8,128)(2,1)}), bf16[8,16,768]{2,1,0:T(8,128)(2,1)S(1)}, u32[]{:S(2)}, u32[]{:S(2)}) %all-to-all-start) | async-done | bytes 196640 | tf_op jit(solution)/shard_map/all_to_all | solution.py:377
  23.7 3.3 %shard_map.138 = (bf16[32,8,128]{2,1,0:T(8,128)(2,1)}, bf16[128,1280]{1,0:T(8,128)(2,1)S(1)}, bf16[128,1280]{1,0:T(8,128)(2,1)}, bf16[8,16,512]{2,1,0:T(8,128)(2,1)}) custom-call(s32[1]{0:T(128)} %bitcast.hap, bf16[8,16,768]{2,1,0:T(8,128)(2,1)S(1)} %all-to-all-done.x_in, bf16[256,256]{1,0:T(8,128)(2,1)S(1)} %copy-done.1, ...), custom_call_target="tpu_custom_call" | custom-call | flops 1 | bytes 1 | tf_op jit(solution)/shard_map/pallas_call | solution.py:82
  27.0 1.0 %collective-permute-start.3 = (bf16[128,1280]{1,0:T(8,128)(2,1)S(1)}, bf16[128,1280]{1,0:T(8,128)(2,1)S(1)}, u32[]{:S(2)}, u32[]{:S(2)}) collective-permute-start(bf16[128,1280]{1,0:T(8,128)(2,1)S(1)} %get-tuple-element.49), channel_id=1, source_target_pairs={{0,1},{1,0},{2,3},{3,2},{4,5},{5,4},{6,7},{7,6},{8,9},{9,8},{10,11... | collective-permute-start | bytes 983048 | tf_op jit(solution)/shard_map/ppermute | solution.py:382
  28.1 4.6 %all-to-all-start.1 = ((bf16[32,8,128]{2,1,0:T(8,128)(2,1)}), bf16[32,8,128]{2,1,0:T(8,128)(2,1)S(1)}, u32[]{:S(2)}, u32[]{:S(2)}) async-start(bf16[32,8,128]{2,1,0:T(8,128)(2,1)} %get-tuple-element.47), calls=%async_computation.1 | async-start | bytes 131072 | tf_op jit(solution)/shard_map/all_to_all | solution.py:377
  32.7 0.4 collective-permute-start.4
  33.1 1.0 %copy-done.2 = bf16[128,1280]{1,0:T(8,128)(2,1)S(1)} copy-done((bf16[128,1280]{1,0:T(8,128)(2,1)S(1)}, bf16[128,1280]{1,0:T(8,128)(2,1)}, u32[]{:S(2)}) %copy-start.2) | copy-done | bytes 327704
  34.1 0.2 shard_map.139
  34.3 0.3 collective-permute-start.6
  34.6 1.2 %collective-permute-start.7 = (bf16[32,1280]{1,0:T(8,128)(2,1)S(1)}, bf16[32,1280]{1,0:T(8,128)(2,1)S(1)}, u32[]{:S(2)}, u32[]{:S(2)}) collective-permute-start(bf16[32,1280]{1,0:T(8,128)(2,1)S(1)} %get-tuple-element.52), channel_id=1, source_target_pairs={{0,16},{8,24},{16,0},{24,8},{1,17},{9,25},{17,1},{25,9},{2,18},{10... | collective-permute-start | bytes 245768 | tf_op jit(solution)/shard_map/ppermute | solution.py:382
  35.8 1.2 %collective-permute-start.8 = (bf16[32,1280]{1,0:T(8,128)(2,1)S(1)}, bf16[32,1280]{1,0:T(8,128)(2,1)S(1)}, u32[]{:S(2)}, u32[]{:S(2)}) collective-permute-start(bf16[32,1280]{1,0:T(8,128)(2,1)S(1)} %get-tuple-element.53), channel_id=1, source_target_pairs={{0,24},{8,16},{16,8},{24,0},{1,25},{9,17},{17,9},{25,1},{2,26},{10... | collective-permute-start | bytes 245768 | tf_op jit(solution)/shard_map/ppermute | solution.py:382
  37.0 0.9 %all-to-all-done.1.g_in = bf16[32,8,128]{2,1,0:T(8,128)(2,1)S(1)} async-done(((bf16[32,8,128]{2,1,0:T(8,128)(2,1)}), bf16[32,8,128]{2,1,0:T(8,128)(2,1)S(1)}, u32[]{:S(2)}, u32[]{:S(2)}) %all-to-all-start.1) | async-done | bytes 65568 | tf_op jit(solution)/shard_map/all_to_all | solution.py:377
  37.9 2.7 %shard_map.141 = (bf16[4,128,256]{2,1,0:T(8,128)(2,1)}, bf16[96,256]{1,0:T(8,128)(2,1)S(1)}, bf16[96,256]{1,0:T(8,128)(2,1)S(1)}) custom-call(s32[1]{0:T(128)} %bitcast.5.idx, s32[1]{0:T(128)S(6)} %select_n.11.core, bf16[32,8,128]{2,1,0:T(8,128)(2,1)S(1)} %all-to-all-done.1.g_in, bf16[2,512,512]{2,1,0:T(8,128)(2,1)S(1)} %get-tuple-element.45.prob, ...), custom_call_target="tpu_custom_call" | custom-call | flops 1 | bytes 1 | tf_op jit(solution)/shard_map/pallas_call | solution.py:82
  40.6 0.4 collective-permute-start.5
  41.0 0.9 %collective-permute-done.5.row_got = bf16[96,256]{1,0:T(8,128)(2,1)S(1)} collective-permute-done((bf16[96,256]{1,0:T(8,128)(2,1)S(1)}, bf16[96,256]{1,0:T(8,128)(2,1)S(1)}, u32[]{:S(2)}, u32[]{:S(2)}) %collective-permute-start.5) | collective-permute-done | bytes 49184 | tf_op jit(solution)/shard_map/ppermute | solution.py:382
  41.9 0.1 shard_map.142
  42.0 1.4 %collective-permute-start.9 = (bf16[320,256]{1,0:T(8,128)(2,1)S(1)}, bf16[320,256]{1,0:T(8,128)(2,1)S(1)}, u32[]{:S(2)}, u32[]{:S(2)}) collective-permute-start(bf16[320,256]{1,0:T(8,128)(2,1)S(1)} %get-tuple-element.64), channel_id=1, source_target_pairs={{0,2},{1,3},{2,0},{3,1},{4,6},{5,7},{6,4},{7,5},{8,10},{9,11},{10,... | collective-permute-start | bytes 491528 | tf_op jit(solution)/shard_map/ppermute | solution.py:382
  43.4 4.1 %collective-permute-done.9.refs_1_ = bf16[320,256]{1,0:T(8,128)(2,1)S(1)} collective-permute-done((bf16[320,256]{1,0:T(8,128)(2,1)S(1)}, bf16[320,256]{1,0:T(8,128)(2,1)S(1)}, u32[]{:S(2)}, u32[]{:S(2)}) %collective-permute-start.9) | collective-permute-done | bytes 163872 | tf_op jit(solution)/shard_map/ppermute | solution.py:382
  47.5 4.5 %all-to-all-start.2 = ((bf16[4,128,256]{2,1,0:T(8,128)(2,1)}), bf16[4,128,256]{2,1,0:T(8,128)(2,1)S(1)}, u32[]{:S(2)}, u32[]{:S(2)}) async-start(bf16[4,128,256]{2,1,0:T(8,128)(2,1)} %get-tuple-element.68), calls=%async_computation.2 | async-start | bytes 524288 | tf_op jit(solution)/shard_map/all_to_all | solution.py:377
  52.0 1.1 %collective-permute-start.10 = (bf16[320,256]{1,0:T(8,128)(2,1)S(1)}, bf16[320,256]{1,0:T(8,128)(2,1)S(1)}, u32[]{:S(2)}, u32[]{:S(2)}) collective-permute-start(bf16[320,256]{1,0:T(8,128)(2,1)S(1)} %get-tuple-element.65), channel_id=1, source_target_pairs={{0,4},{1,5},{2,6},{3,7},{4,0},{5,1},{6,2},{7,3},{8,12},{9,13},{10,... | collective-permute-start | bytes 491528 | tf_op jit(solution)/shard_map/ppermute | solution.py:382
  53.0 1.5 %collective-permute-start.11 = (bf16[320,256]{1,0:T(8,128)(2,1)S(1)}, bf16[320,256]{1,0:T(8,128)(2,1)S(1)}, u32[]{:S(2)}, u32[]{:S(2)}) collective-permute-start(bf16[320,256]{1,0:T(8,128)(2,1)S(1)} %get-tuple-element.66), channel_id=1, source_target_pairs={{0,6},{1,7},{2,4},{3,5},{4,2},{5,3},{6,0},{7,1},{8,14},{9,15},{10,... | collective-permute-start | bytes 491528 | tf_op jit(solution)/shard_map/ppermute | solution.py:382
  54.6 9.1 %collective-permute-done.10.refs_2_ = bf16[320,256]{1,0:T(8,128)(2,1)S(1)} collective-permute-done((bf16[320,256]{1,0:T(8,128)(2,1)S(1)}, bf16[320,256]{1,0:T(8,128)(2,1)S(1)}, u32[]{:S(2)}, u32[]{:S(2)}) %collective-permute-start.10) | collective-permute-done | bytes 163872 | tf_op jit(solution)/shard_map/ppermute | solution.py:382
  63.6 5.9 %collective-permute-done.11.refs_3_ = bf16[320,256]{1,0:T(8,128)(2,1)S(1)} collective-permute-done((bf16[320,256]{1,0:T(8,128)(2,1)S(1)}, bf16[320,256]{1,0:T(8,128)(2,1)S(1)}, u32[]{:S(2)}, u32[]{:S(2)}) %collective-permute-start.11) | collective-permute-done | bytes 163872 | tf_op jit(solution)/shard_map/ppermute | solution.py:382
  69.5 0.1 shard_map.144.refs_0_
  69.6 1.3 %collective-permute-start.17 = (bf16[256,256]{1,0:T(8,128)(2,1)S(1)}, bf16[256,256]{1,0:T(8,128)(2,1)S(1)}, u32[]{:S(2)}, u32[]{:S(2)}) collective-permute-start(bf16[256,256]{1,0:T(8,128)(2,1)S(1)} %shard_map.144.refs_0_), channel_id=1, source_target_pairs={{0,24},{8,16},{16,8},{24,0},{1,25},{9,17},{17,9},{25,1},{2,26},{10... | collective-permute-start | bytes 393224 | tf_op jit(solution)/shard_map/ppermute | solution.py:382
  70.9 0.1 collective-permute-start.15
  71.0 1.4 %collective-permute-start.13 = (bf16[256,256]{1,0:T(8,128)(2,1)S(1)}, bf16[256,256]{1,0:T(8,128)(2,1)S(1)}, u32[]{:S(2)}, u32[]{:S(2)}) collective-permute-start(bf16[256,256]{1,0:T(8,128)(2,1)S(1)} %shard_map.144.refs_0_), channel_id=1, source_target_pairs={{0,8},{8,0},{16,24},{24,16},{1,9},{9,1},{17,25},{25,17},{2,10},{10... | collective-permute-start | bytes 393224 | tf_op jit(solution)/shard_map/ppermute | solution.py:382
  72.3 1.3 %collective-permute-start.12 = (bf16[256,256]{1,0:T(8,128)(2,1)S(1)}, bf16[256,256]{1,0:T(8,128)(2,1)S(1)}, u32[]{:S(2)}, u32[]{:S(2)}) collective-permute-start(bf16[256,256]{1,0:T(8,128)(2,1)S(1)} %shard_map.144.refs_0_), channel_id=1, source_target_pairs={{0,1},{1,0},{2,3},{3,2},{4,5},{5,4},{6,7},{7,6},{8,9},{9,8},{10,11... | collective-permute-start | bytes 393224 | tf_op jit(solution)/shard_map/ppermute | solution.py:382
  73.7 1.5 %collective-permute-done.17.refs_6_ = bf16[256,256]{1,0:T(8,128)(2,1)S(1)} collective-permute-done((bf16[256,256]{1,0:T(8,128)(2,1)S(1)}, bf16[256,256]{1,0:T(8,128)(2,1)S(1)}, u32[]{:S(2)}, u32[]{:S(2)}) %collective-permute-start.17) | collective-permute-done | bytes 131104 | tf_op jit(solution)/shard_map/ppermute | solution.py:382
  75.2 2.3 %collective-permute-start.18 = (bf16[256,256]{1,0:T(8,128)(2,1)S(1)}, bf16[256,256]{1,0:T(8,128)(2,1)S(1)}, u32[]{:S(2)}, u32[]{:S(2)}) collective-permute-start(bf16[256,256]{1,0:T(8,128)(2,1)S(1)} %collective-permute-done.17.refs_6_), channel_id=1, source_target_pairs={{0,1},{1,0},{2,3},{3,2},{4,5},{5,4},{6,7},{7,6},{8,9},{9,8},{10,11... | collective-permute-start | bytes 393224 | tf_op jit(solution)/shard_map/ppermute | solution.py:382
  77.4 1.4 %collective-permute-done.15.refs_4_ = bf16[256,256]{1,0:T(8,128)(2,1)S(1)} collective-permute-done((bf16[256,256]{1,0:T(8,128)(2,1)S(1)}, bf16[256,256]{1,0:T(8,128)(2,1)S(1)}, u32[]{:S(2)}, u32[]{:S(2)}) %collective-permute-start.15) | collective-permute-done | bytes 131104 | tf_op jit(solution)/shard_map/ppermute | solution.py:382
  78.8 0.5 collective-permute-start.16
  79.3 0.0 collective-permute-start.14
  79.3 0.9 %shard_map.143 = (bf16[128,256]{1,0:T(8,128)(2,1)}, bf16[128,256]{1,0:T(8,128)(2,1)}) custom-call(s32[1]{0:T(128)} %bitcast.hap, bf16[128,256]{1,0:T(8,128)(2,1)S(1)} %bitcast.18, f32[2,256]{1,0:T(2,128)S(1)} %pad_maximum_fusion.refs_5_.gain, bf16[768,256]{1,0:T(8,128)(2,1)S(1)} %bitcast.12, bf16[4,128,256]{2,1,0:T(8,128)(2,1)S(1)} %all-to-all-done.2.gps, ...), custom_call_target="tpu_custom_call" | custom-call | flops 1 | bytes 1 | tf_op jit(solution)/shard_map/pallas_call | solution.py:82
  80.3 0.3 collective-permute-done.14.refs_3_
  80.6 1.5 %shard_map.145 = (f32[256,768]{1,0:T(8,128)}, f32[256,256]{1,0:T(8,128)}, f32[256,768]{1,0:T(8,128)}, f32[256,256]{1,0:T(8,128)}) custom-call(s32[1]{0:T(128)} %bitcast.5.idx, s32[1]{0:T(128)S(6)} %select_n.11.core, bf16[256,256]{1,0:T(8,128)(2,1)S(1)} %shard_map.144.refs_0_, bf16[256,256]{1,0:T(8,128)(2,1)S(1)} %collective-permute-done.12.refs_1_, ...), custom_call_target="tpu_custom_call" | custom-call | flops 1 | bytes 1 | tf_op jit(solution)/shard_map/pallas_call | solution.py:82
  (34 shorter events, 0.1 us)
Async XLA Ops:
  0.6 5.4 %collective-permute-start.2 = (bf16[128,256]{1,0:T(8,128)(2,1)}, bf16[128,256]{1,0:T(8,128)(2,1)S(1)}, u32[]{:S(2)}, u32[]{:S(2)}) collective-permute-start(bf16[128,256]{1,0:T(8,128)(2,1)} %bitcast.14), channel_id=1, source_target_pairs={{0,24},{8,16},{16,8},{24,0},{1,25},{9,17},{17,9},{25,1},{2,26},{10... | collective-permute-start | bytes 196616 | tf_op jit(solution)/shard_map/ppermute | solution.py:382
  1.9 4.6 %collective-permute-start.1 = (bf16[128,256]{1,0:T(8,128)(2,1)}, bf16[128,256]{1,0:T(8,128)(2,1)S(1)}, u32[]{:S(2)}, u32[]{:S(2)}) collective-permute-start(bf16[128,256]{1,0:T(8,128)(2,1)} %bitcast.15), channel_id=1, source_target_pairs={{0,16},{8,24},{16,0},{24,8},{1,17},{9,25},{17,1},{25,9},{2,18},{10... | collective-permute-start | bytes 196616 | tf_op jit(solution)/shard_map/ppermute | solution.py:382
  2.1 4.4 %collective-permute-start = (bf16[128,256]{1,0:T(8,128)(2,1)}, bf16[128,256]{1,0:T(8,128)(2,1)S(1)}, u32[]{:S(2)}, u32[]{:S(2)}) collective-permute-start(bf16[128,256]{1,0:T(8,128)(2,1)} %bitcast.16), channel_id=1, source_target_pairs={{0,8},{8,0},{16,24},{24,16},{1,9},{9,1},{17,25},{25,17},{2,10},{10... | collective-permute-start | bytes 196616 | tf_op jit(solution)/shard_map/ppermute | solution.py:382
  3.3 0.7 copy-start.8
  4.0 0.9 %slice-start = ((bf16[256,768]{1,0:T(8,128)(2,1)}), bf16[256,512]{1,0:T(8,128)(2,1)S(1)}, s32[]{:S(2)}) async-start(bf16[256,768]{1,0:T(8,128)(2,1)} %col_proj.1), calls=%async_computation.3 | async-start | bytes 524288 | tf_op jit(solution)/shard_map/slice | solution.py:417
  4.0 1.1 %copy-start.7 = (bf16[256,768]{1,0:T(8,128)(2,1)S(1)}, bf16[256,768]{1,0:T(8,128)(2,1)}, u32[]{:S(2)}) copy-start(bf16[256,768]{1,0:T(8,128)(2,1)} %param.12) | copy-start | bytes 1179652
  5.1 0.7 copy-start.10
  5.1 1.4 %copy-start.1 = (bf16[256,256]{1,0:T(8,128)(2,1)S(1)}, bf16[256,256]{1,0:T(8,128)(2,1)}, u32[]{:S(2)}) copy-start(bf16[256,256]{1,0:T(8,128)(2,1)} %row_out.1) | copy-start | bytes 393220
  5.2 1.4 %copy-start.3 = (bf16[128,1,256]{2,0,1:T(8,128)(2,1)S(1)}, bf16[128,1,256]{2,0,1:T(8,128)(2,1)}, u32[]{:S(2)}) copy-start(bf16[128,1,256]{2,0,1:T(8,128)(2,1)} %param.9) | copy-start | bytes 196612
  5.2 1.4 %copy-start.6 = (bf16[128,1,256]{2,0,1:T(8,128)(2,1)S(1)}, bf16[128,1,256]{2,0,1:T(8,128)(2,1)}, u32[]{:S(2)}) copy-start(bf16[128,1,256]{2,0,1:T(8,128)(2,1)} %param.17) | copy-start | bytes 196612
  5.4 0.7 copy-start.9
  11.3 12.4 %all-to-all-start = ((bf16[8,16,768]{2,1,0:T(8,128)(2,1)}), bf16[8,16,768]{2,1,0:T(8,128)(2,1)S(1)}, u32[]{:S(2)}, u32[]{:S(2)}) async-start(bf16[8,16,768]{2,1,0:T(8,128)(2,1)} %get-tuple-element.43), calls=%async_computation | async-start | bytes 393216 | tf_op jit(solution)/shard_map/all_to_all | solution.py:377
  17.6 6.1 %copy-start = (bf16[256,768]{1,0:T(8,128)(2,1)S(1)}, bf16[256,768]{1,0:T(8,128)(2,1)}, u32[]{:S(2)}) copy-start(bf16[256,768]{1,0:T(8,128)(2,1)} %col_proj.1) | copy-start | bytes 1179652
  17.6 6.1 %copy-start.5 = (bf16[256,256]{1,0:T(8,128)(2,1)S(1)}, bf16[256,256]{1,0:T(8,128)(2,1)}, u32[]{:S(2)}) copy-start(bf16[256,256]{1,0:T(8,128)(2,1)} %col_out.1) | copy-start | bytes 393220
  27.0 5.7 %copy-start.4 = (bf16[8,16,512]{2,1,0:T(8,128)(2,1)S(1)}, bf16[8,16,512]{2,1,0:T(8,128)(2,1)}, u32[]{:S(2)}) copy-start(bf16[8,16,512]{2,1,0:T(8,128)(2,1)} %get-tuple-element.54.og) | copy-start | bytes 393220
  27.0 6.1 %collective-permute-start.3 = (bf16[128,1280]{1,0:T(8,128)(2,1)S(1)}, bf16[128,1280]{1,0:T(8,128)(2,1)S(1)}, u32[]{:S(2)}, u32[]{:S(2)}) collective-permute-start(bf16[128,1280]{1,0:T(8,128)(2,1)S(1)} %get-tuple-element.49), channel_id=1, source_target_pairs={{0,1},{1,0},{2,3},{3,2},{4,5},{5,4},{6,7},{7,6},{8,9},{9,8},{10,11... | collective-permute-start | bytes 983048 | tf_op jit(solution)/shard_map/ppermute | solution.py:382
  28.1 9.8 %all-to-all-start.1 = ((bf16[32,8,128]{2,1,0:T(8,128)(2,1)}), bf16[32,8,128]{2,1,0:T(8,128)(2,1)S(1)}, u32[]{:S(2)}, u32[]{:S(2)}) async-start(bf16[32,8,128]{2,1,0:T(8,128)(2,1)} %get-tuple-element.47), calls=%async_computation.1 | async-start | bytes 131072 | tf_op jit(solution)/shard_map/all_to_all | solution.py:377
  32.7 4.3 %collective-permute-start.4 = (bf16[4,16,512]{2,1,0:T(8,128)(2,1)S(1)}, bf16[4,16,512]{2,1,0:T(8,128)(2,1)S(1)}, u32[]{:S(2)}, u32[]{:S(2)}) collective-permute-start(bf16[4,16,512]{2,1,0:T(8,128)(2,1)S(1)} %get-tuple-element.55), channel_id=1, source_target_pairs={{0,1},{1,0},{2,3},{3,2},{4,5},{5,4},{6,7},{7,6},{8,9},{9,8},{10,11... | collective-permute-start | bytes 196616 | tf_op jit(solution)/shard_map/ppermute | solution.py:382
  33.1 1.0 %copy-start.2 = (bf16[128,1280]{1,0:T(8,128)(2,1)S(1)}, bf16[128,1280]{1,0:T(8,128)(2,1)}, u32[]{:S(2)}) copy-start(bf16[128,1280]{1,0:T(8,128)(2,1)} %get-tuple-element.48.keep) | copy-start | bytes 983044
  34.3 7.6 %collective-permute-start.6 = (bf16[32,1280]{1,0:T(8,128)(2,1)S(1)}, bf16[32,1280]{1,0:T(8,128)(2,1)S(1)}, u32[]{:S(2)}, u32[]{:S(2)}) collective-permute-start(bf16[32,1280]{1,0:T(8,128)(2,1)S(1)} %get-tuple-element.51), channel_id=1, source_target_pairs={{0,8},{8,0},{16,24},{24,16},{1,9},{9,1},{17,25},{25,17},{2,10},{10... | collective-permute-start | bytes 245768 | tf_op jit(solution)/shard_map/ppermute | solution.py:382
  34.6 7.3 %collective-permute-start.7 = (bf16[32,1280]{1,0:T(8,128)(2,1)S(1)}, bf16[32,1280]{1,0:T(8,128)(2,1)S(1)}, u32[]{:S(2)}, u32[]{:S(2)}) collective-permute-start(bf16[32,1280]{1,0:T(8,128)(2,1)S(1)} %get-tuple-element.52), channel_id=1, source_target_pairs={{0,16},{8,24},{16,0},{24,8},{1,17},{9,25},{17,1},{25,9},{2,18},{10... | collective-permute-start | bytes 245768 | tf_op jit(solution)/shard_map/ppermute | solution.py:382
  35.8 6.1 %collective-permute-start.8 = (bf16[32,1280]{1,0:T(8,128)(2,1)S(1)}, bf16[32,1280]{1,0:T(8,128)(2,1)S(1)}, u32[]{:S(2)}, u32[]{:S(2)}) collective-permute-start(bf16[32,1280]{1,0:T(8,128)(2,1)S(1)} %get-tuple-element.53), channel_id=1, source_target_pairs={{0,24},{8,16},{16,8},{24,0},{1,25},{9,17},{17,9},{25,1},{2,26},{10... | collective-permute-start | bytes 245768 | tf_op jit(solution)/shard_map/ppermute | solution.py:382
  40.6 1.3 %collective-permute-start.5 = (bf16[96,256]{1,0:T(8,128)(2,1)S(1)}, bf16[96,256]{1,0:T(8,128)(2,1)S(1)}, u32[]{:S(2)}, u32[]{:S(2)}) collective-permute-start(bf16[96,256]{1,0:T(8,128)(2,1)S(1)} %get-tuple-element.61), channel_id=1, source_target_pairs={{0,1},{1,0},{2,3},{3,2},{4,5},{5,4},{6,7},{7,6},{8,9},{9,8},{10,11... | collective-permute-start | bytes 147464 | tf_op jit(solution)/shard_map/ppermute | solution.py:382
  42.0 5.5 %collective-permute-start.9 = (bf16[320,256]{1,0:T(8,128)(2,1)S(1)}, bf16[320,256]{1,0:T(8,128)(2,1)S(1)}, u32[]{:S(2)}, u32[]{:S(2)}) collective-permute-start(bf16[320,256]{1,0:T(8,128)(2,1)S(1)} %get-tuple-element.64), channel_id=1, source_target_pairs={{0,2},{1,3},{2,0},{3,1},{4,6},{5,7},{6,4},{7,5},{8,10},{9,11},{10,... | collective-permute-start | bytes 491528 | tf_op jit(solution)/shard_map/ppermute | solution.py:382
  47.5 22.0 %all-to-all-start.2 = ((bf16[4,128,256]{2,1,0:T(8,128)(2,1)}), bf16[4,128,256]{2,1,0:T(8,128)(2,1)S(1)}, u32[]{:S(2)}, u32[]{:S(2)}) async-start(bf16[4,128,256]{2,1,0:T(8,128)(2,1)} %get-tuple-element.68), calls=%async_computation.2 | async-start | bytes 524288 | tf_op jit(solution)/shard_map/all_to_all | solution.py:377
  52.0 11.7 %collective-permute-start.10 = (bf16[320,256]{1,0:T(8,128)(2,1)S(1)}, bf16[320,256]{1,0:T(8,128)(2,1)S(1)}, u32[]{:S(2)}, u32[]{:S(2)}) collective-permute-start(bf16[320,256]{1,0:T(8,128)(2,1)S(1)} %get-tuple-element.65), channel_id=1, source_target_pairs={{0,4},{1,5},{2,6},{3,7},{4,0},{5,1},{6,2},{7,3},{8,12},{9,13},{10,... | collective-permute-start | bytes 491528 | tf_op jit(solution)/shard_map/ppermute | solution.py:382
  53.0 16.5 %collective-permute-start.11 = (bf16[320,256]{1,0:T(8,128)(2,1)S(1)}, bf16[320,256]{1,0:T(8,128)(2,1)S(1)}, u32[]{:S(2)}, u32[]{:S(2)}) collective-permute-start(bf16[320,256]{1,0:T(8,128)(2,1)S(1)} %get-tuple-element.66), channel_id=1, source_target_pairs={{0,6},{1,7},{2,4},{3,5},{4,2},{5,3},{6,0},{7,1},{8,14},{9,15},{10,... | collective-permute-start | bytes 491528 | tf_op jit(solution)/shard_map/ppermute | solution.py:382
  69.6 5.5 %collective-permute-start.17 = (bf16[256,256]{1,0:T(8,128)(2,1)S(1)}, bf16[256,256]{1,0:T(8,128)(2,1)S(1)}, u32[]{:S(2)}, u32[]{:S(2)}) collective-permute-start(bf16[256,256]{1,0:T(8,128)(2,1)S(1)} %shard_map.144.refs_0_), channel_id=1, source_target_pairs={{0,24},{8,16},{16,8},{24,0},{1,25},{9,17},{17,9},{25,1},{2,26},{10... | collective-permute-start | bytes 393224 | tf_op jit(solution)/shard_map/ppermute | solution.py:382
  70.9 7.9 %collective-permute-start.15 = (bf16[256,256]{1,0:T(8,128)(2,1)S(1)}, bf16[256,256]{1,0:T(8,128)(2,1)S(1)}, u32[]{:S(2)}, u32[]{:S(2)}) collective-permute-start(bf16[256,256]{1,0:T(8,128)(2,1)S(1)} %shard_map.144.refs_0_), channel_id=1, source_target_pairs={{0,16},{8,24},{16,0},{24,8},{1,17},{9,25},{17,1},{25,9},{2,18},{10... | collective-permute-start | bytes 393224 | tf_op jit(solution)/shard_map/ppermute | solution.py:382
  71.0 8.3 %collective-permute-start.13 = (bf16[256,256]{1,0:T(8,128)(2,1)S(1)}, bf16[256,256]{1,0:T(8,128)(2,1)S(1)}, u32[]{:S(2)}, u32[]{:S(2)}) collective-permute-start(bf16[256,256]{1,0:T(8,128)(2,1)S(1)} %shard_map.144.refs_0_), channel_id=1, source_target_pairs={{0,8},{8,0},{16,24},{24,16},{1,9},{9,1},{17,25},{25,17},{2,10},{10... | collective-permute-start | bytes 393224 | tf_op jit(solution)/shard_map/ppermute | solution.py:382
  72.3 8.0 %collective-permute-start.12 = (bf16[256,256]{1,0:T(8,128)(2,1)S(1)}, bf16[256,256]{1,0:T(8,128)(2,1)S(1)}, u32[]{:S(2)}, u32[]{:S(2)}) collective-permute-start(bf16[256,256]{1,0:T(8,128)(2,1)S(1)} %shard_map.144.refs_0_), channel_id=1, source_target_pairs={{0,1},{1,0},{2,3},{3,2},{4,5},{5,4},{6,7},{7,6},{8,9},{9,8},{10,11... | collective-permute-start | bytes 393224 | tf_op jit(solution)/shard_map/ppermute | solution.py:382
  75.2 5.1 %collective-permute-start.18 = (bf16[256,256]{1,0:T(8,128)(2,1)S(1)}, bf16[256,256]{1,0:T(8,128)(2,1)S(1)}, u32[]{:S(2)}, u32[]{:S(2)}) collective-permute-start(bf16[256,256]{1,0:T(8,128)(2,1)S(1)} %collective-permute-done.17.refs_6_), channel_id=1, source_target_pairs={{0,1},{1,0},{2,3},{3,2},{4,5},{5,4},{6,7},{7,6},{8,9},{9,8},{10,11... | collective-permute-start | bytes 393224 | tf_op jit(solution)/shard_map/ppermute | solution.py:382
  78.8 1.5 %collective-permute-start.16 = (bf16[256,256]{1,0:T(8,128)(2,1)S(1)}, bf16[256,256]{1,0:T(8,128)(2,1)S(1)}, u32[]{:S(2)}, u32[]{:S(2)}) collective-permute-start(bf16[256,256]{1,0:T(8,128)(2,1)S(1)} %collective-permute-done.15.refs_4_), channel_id=1, source_target_pairs={{0,1},{1,0},{2,3},{3,2},{4,5},{5,4},{6,7},{7,6},{8,9},{9,8},{10,11... | collective-permute-start | bytes 393224 | tf_op jit(solution)/shard_map/ppermute | solution.py:382
  79.3 1.3 %collective-permute-start.14 = (bf16[256,256]{1,0:T(8,128)(2,1)S(1)}, bf16[256,256]{1,0:T(8,128)(2,1)S(1)}, u32[]{:S(2)}, u32[]{:S(2)}) collective-permute-start(bf16[256,256]{1,0:T(8,128)(2,1)S(1)} %collective-permute-done.13.refs_2_), channel_id=1, source_target_pairs={{0,1},{1,0},{2,3},{3,2},{4,5},{5,4},{6,7},{7,6},{8,9},{9,8},{10,11... | collective-permute-start | bytes 393224 | tf_op jit(solution)/shard_map/ppermute | solution.py:382

commit v10 on v7

--- a/solution.py
+++ b/solution.py
@@ -91,11 +91,21 @@
     )(*operands)
 
 
-def linked_scores(scores, rows, sites, me, b, link):
-    return [
-        scores[a * rows : (a + 1) * rows] + jnp.where(link[me ^ b, me ^ a] > 0, 0.0, -jnp.inf)
-        for a in range(sites)
-    ]
+def head_stack(values):
+    heads = values.shape[1] // HEAD_DIM
+    return jnp.concatenate([only_head(values, h) for h in range(heads)], axis=0)
+
+
+def head_blocks(values):
+    heads = values.shape[0] // HEAD_DIM
+    wide = values.shape[1] // heads
+    return jnp.concatenate(
+        [
+            values[h * HEAD_DIM : (h + 1) * HEAD_DIM, h * wide : (h + 1) * wide]
+            for h in range(heads)
+        ],
+        axis=0,
+    )
 
 
 def exp_parts(parts):
@@ -110,7 +120,6 @@
     cot, gain, w_t, row_out, x_out, n_out = refs[sites:]
     me = idx[0]
     rows, width = cot.shape
-    heads = width // HEAD_DIM
     for k in range(sites):
         xhat, _ = norm_parts(pieces[k][...].astype(F32))
         n_out[k * rows : (k + 1) * rows, :] = (xhat * gain[:1, :]).astype(BF16)
@@ -118,14 +127,13 @@
     q = mm_nt(normed[:rows], w_t[:width, :]).astype(BF16)
     key = mm_nt(normed, w_t[width : 2 * width, :]).astype(BF16)
     v_t = mm_nt(w_t[2 * width :, :], normed).astype(BF16)
-    q_st = jnp.concatenate([only_head(q, h) for h in range(heads)], axis=0)
-    att_t = []
-    for h in range(heads):
-        scores = mm_nt(key, q_st[h * rows : (h + 1) * rows]) * (SCALE * LOG2E)
-        parts, inverse = exp_parts(linked_scores(scores, rows, sites, me, 0, link))
-        e_h = jnp.concatenate([part.astype(BF16) for part in parts], axis=0)
-        att_t.append(mm(v_t[h * HEAD_DIM : (h + 1) * HEAD_DIM], e_h) * inverse)
-    att = jnp.transpose(jnp.concatenate(att_t, axis=0)).astype(BF16)
+    scores = mm_nt(key, head_stack(q)) * (SCALE * LOG2E)
+    bias = [jnp.where(link[me, me ^ a] > 0, 0.0, -jnp.inf) for a in range(sites)]
+    parts = [scores[a * rows : (a + 1) * rows] + bias[a] for a in range(sites)]
+    parts, inverse = exp_parts(parts)
+    exps = jnp.concatenate([part.astype(BF16) for part in parts], axis=0)
+    att_t = head_blocks(mm(v_t, exps) * inverse)
+    att = jnp.transpose(att_t).astype(BF16)
     hid = pieces[0][...].astype(F32) + mm(att, row_out[...])
     joined = jnp.concatenate([hid, cot[...].astype(F32), att.astype(F32)], axis=1)
     x_out[...] = joined.reshape(haps, rows // haps, 3 * width).astype(BF16)
@@ -146,14 +154,18 @@
     q_out[...] = q
     v_out[...] = mm_nt(normed, weights(2)).astype(BF16)
     kt_out[...] = mm_nt(weights(1), normed).astype(BF16)
-    for h in range(width // HEAD_DIM):
-        key_h = only_head(key, h)
-        for b in range(sites):
-            here = pl.ds(b * rows, rows)
-            scores = mm_nt(key_h, q[b * rows : (b + 1) * rows]) * (SCALE * LOG2E)
-            parts, inverse = exp_parts(linked_scores(scores, rows, sites, me, b, link))
-            for a in range(sites):
-                p_out[h, a * rows : (a + 1) * rows, here] = (parts[a] * inverse).astype(BF16)
+    scores = mm_nt(key, head_stack(q)) * (SCALE * LOG2E)
+    parts = []
+    for a in range(sites):
+        bias = [
+            jnp.full((1, rows), jnp.where(link[me ^ b, me ^ a] > 0, 0.0, -jnp.inf), F32)
+            for b in range(sites)
+        ]
+        bias = jnp.concatenate(bias * (width // HEAD_DIM), axis=1)
+        parts.append(scores[a * rows : (a + 1) * rows] + bias)
+    parts, inverse = exp_parts(parts)
+    for a in range(sites):
+        p_out[a * rows : (a + 1) * rows, :] = (parts[a] * inverse).astype(BF16)
 
 
 def column_step(sites, haps, hap, x_in, row_out, gain, col_proj, kv_t_w, col_out, *refs):
@@ -184,41 +196,27 @@
     key = packed[:, width : 2 * width]
     val = packed[:, 2 * width :]
     kv_t = mm_nt(kv_t_w[...], normed).astype(BF16)
-    key_st = jnp.concatenate([only_head(key, h) for h in range(heads)], axis=0)
-    val_st = jnp.concatenate([only_head(val, h) for h in range(heads)], axis=0)
-    scores = mm_nt(key_st, q) * (SCALE * LOG2E)
-    dprob = mm_nt(val_st, grad_att)
+    q_st = head_stack(q)
+    g_st = head_stack(grad_att)
+    scores = mm_nt(key, q_st) * (SCALE * LOG2E)
+    dprob = mm_nt(val, g_st)
     same = (
-        lax.broadcasted_iota(jnp.int32, (rows, rows), 0) % per
-        == lax.broadcasted_iota(jnp.int32, (rows, rows), 1) % per
-    )
-    att_t, dq_t, prob16, ds16 = [], [], [], []
-    for h in range(heads):
-        cols = slice(h * HEAD_DIM, (h + 1) * HEAD_DIM)
-        s_h = jnp.where(same, scores[h * rows : (h + 1) * rows], -jnp.inf)
-        e_h = jnp.exp2(s_h - jnp.max(s_h, axis=0, keepdims=True))
-        inverse = 1.0 / jnp.sum(e_h, axis=0, keepdims=True)
-        att_t.append(mm(kv_t[width:, :][cols], e_h.astype(BF16)) * inverse)
-        p_h = e_h * inverse
-        d_h = dprob[h * rows : (h + 1) * rows]
-        delta = jnp.sum(p_h * d_h, axis=0, keepdims=True)
-        ds_h = (p_h * (d_h - delta)).astype(BF16)
-        prob16.append(p_h.astype(BF16))
-        ds16.append(ds_h)
-        dq_t.append(mm(kv_t[:width, :][cols], ds_h))
-    att_t = jnp.concatenate(att_t, axis=0)
+        lax.broadcasted_iota(jnp.int32, scores.shape, 0) % per
+        == lax.broadcasted_iota(jnp.int32, scores.shape, 1) % per
+    )
+    scores = jnp.where(same, scores, -jnp.inf)
+    exps = jnp.exp2(scores - jnp.max(scores, axis=0, keepdims=True))
+    inverse = 1.0 / jnp.sum(exps, axis=0, keepdims=True)
+    att_t = head_blocks(mm(kv_t[width:, :], exps.astype(BF16)) * inverse)
+    probs = exps * inverse
+    delta = jnp.sum(probs * dprob, axis=0, keepdims=True)
+    dscore = (probs * (dprob - delta)).astype(BF16)
+    dv = mm(probs.astype(BF16), g_st)
+    dk = mm(dscore, q_st)
+    dq = jnp.transpose(head_blocks(mm(kv_t[:width, :], dscore)))
     w_all[:, 3 * width : 4 * width] = mm(att_t.astype(BF16), cot).astype(BF16)
     att = jnp.transpose(att_t).astype(BF16)
     out = hid + mm(att, col_out[...])
-    dv_all = mm(jnp.concatenate(prob16, axis=0), grad_att)
-    dk_all = mm(jnp.concatenate(ds16, axis=0), q)
-    dv = sum(
-        jnp.where(head_lanes(width, h), dv_all[h * rows : (h + 1) * rows], 0.0) for h in range(heads)
-    )
-    dk = sum(
-        jnp.where(head_lanes(width, h), dk_all[h * rows : (h + 1) * rows], 0.0) for h in range(heads)
-    )
-    dq = jnp.transpose(jnp.concatenate(dq_t, axis=0))
     packed_grad = jnp.concatenate([dq * SCALE, dk * SCALE, dv], axis=1).astype(BF16)
     w_all[:, : 3 * width] = mm_tn(normed, packed_grad).astype(BF16)
     first = save(0, slice(0, 4 * width))
@@ -258,7 +256,7 @@
 
 def row_backward(sites, haps, idx, core, g_in, prob, q, val, key_t, normed, *refs):
     gp_outs = refs[:sites]
-    keep, send, g_all, ds_all, w_out = refs[sites:]
+    keep, send, g_all, w_out = refs[sites:]
     me = idx[0]
     total, width = q.shape
     rows = total // sites
@@ -266,21 +264,14 @@
         g_all[b * rows : (b + 1) * rows, :] = unpack_block(
             g_in[pl.ds((me ^ b) * haps, haps)], width
         )
-    dk = jnp.zeros((total, width), F32)
-    dv = jnp.zeros((total, width), F32)
-    dq_t = []
-    for h in range(width // HEAD_DIM):
-        val_h = only_head(val[...], h)
-        dv = dv + mm(prob[h], only_head(g_all[...], h))
-        for b in range(sites):
-            here = pl.ds(b * rows, rows)
-            dprob = mm_nt(val_h, g_all[b * rows : (b + 1) * rows, :])
-            p_b = prob[h, :, here].astype(F32)
-            delta = jnp.sum(p_b * dprob, axis=0, keepdims=True)
-            ds_all[:, here] = (p_b * (dprob - delta)).astype(BF16)
-        dk = dk + mm(ds_all[...], only_head(q[...], h))
-        dq_t.append(mm(key_t[h * HEAD_DIM : (h + 1) * HEAD_DIM, :], ds_all[...]))
-    dq_t = jnp.concatenate(dq_t, axis=0) * SCALE
+    g_st = head_stack(g_all[...])
+    p_all = prob[...].astype(F32)
+    dprob = mm_nt(val[...], g_st)
+    delta = jnp.sum(p_all * dprob, axis=0, keepdims=True)
+    dscore = (p_all * (dprob - delta)).astype(BF16)
+    dv = mm(prob[...], g_st)
+    dk = mm(dscore, head_stack(q[...]))
+    dq_t = head_blocks(mm(key_t[...], dscore)) * SCALE
     dk16 = (dk * SCALE).astype(BF16)
     dv16 = dv.astype(BF16)
     w_out[:width, :] = mm(dq_t.astype(BF16), normed[...]).astype(BF16)
@@ -413,6 +404,7 @@
     cot = cotangent.reshape(rows, width)
 
     pieces = [feats] + [swapped(feats, "site", k) for k in range(1, sites)]
+    link_pattern = jnp.where(link_pattern > 0, 1, 0)
     gains = jnp.stack([row_gain, column_norm_gain])
     w_t = jnp.transpose(row_proj)
     kv_t_w = jnp.transpose(col_proj[:, width:])
@@ -426,7 +418,7 @@
     prob, q, val, key_t = call(
         functools.partial(row_probs, sites),
         [
-            ((heads, total, total), BF16),
+            ((total, heads * total), BF16),
             ((total, group), BF16),
             ((total, group), BF16),
             ((group, total), BF16),
@@ -470,7 +462,6 @@
         idx, core, g_in, prob, q, val, key_t, normed, scalars=2,
         scratch=[
             pltpu.VMEM((total, group), BF16),
-            pltpu.VMEM((total, total), BF16),
             pltpu.VMEM((3 * group, width), BF16),
         ],
     )

time: 75.5 us -> 72.2 us (0.956)
  Pallas kernels: 14.8 us -> 12.5 us
  waiting for transfers between devices: 24.6 us -> 23.7 us
    pallas_call x10, Pallas kernels: 14.8 us -> 12.5 us  [call(): pl.pallas_call(body, out_shape=[jax.ShapeDtypeStruct(s, d) for s, d in ou...]
    ppermute x19, waiting for transfers between devices: 18.5 us -> 17.7 us  [swapped(): return lax.ppermute(value, axis, [(i, i ^ by) for i in range(length)])]
  transfers between devices with their start and end apart: 21 -> 21, of which waited for: 10 -> 10; matrix products, arithmetic and copies ran while one was open for 0% -> 0% of each run, Pallas kernels for 7% -> 6%
where the time goes in v10:
time: 72.2 us; the launch traced here: 71.9 us
  starting transfers between devices  31.3 us (43%)
  waiting for transfers between devices  23.7 us (33%)
  Pallas kernels  12.5 us (17%)
  local copies, waits for them, and re-layouts  3.62 us (5%)
  between operations  0.8 us (1%)
    ppermute x19, starting transfers between devices, swapped(): return lax.ppermute(value, axis, [(i, i ^ by) for i in range(length)])  20.7 us
    ppermute x19, waiting for transfers between devices, swapped(): return lax.ppermute(value, axis, [(i, i ^ by) for i in range(length)])  17.7 us
    pallas_call x10, Pallas kernels, call(): pl.pallas_call(body, out_shape=[jax.ShapeDtypeStruct(s, d) for s, d in ou...  12.5 us
    all_to_all x2, starting transfers between devices, exchange(): return lax.all_to_all(value, axis, 0, 0, tiled=True)  10.6 us
    all_to_all x2, waiting for transfers between devices, exchange(): return lax.all_to_all(value, axis, 0, 0, tiled=True)  6.05 us
    unnamed x24, local copies, waits for them, and re-layouts  2.67 us
  transfers between devices with their start and end apart: 21, of which 10 were waited for; matrix products, arithmetic and copies ran while one was open for 0% of the time, Pallas kernels for 6%

profile of v10, /device:TPU:9, one launch (start us, length us, event | category | flops | bytes accessed | tf_op | source)
XLA Modules:
  0.0 71.9 jit_solution(8191530404801947856)
XLA Ops:
  0.6 2.2 %collective-permute-start.2 = (bf16[128,256]{1,0:T(8,128)(2,1)}, bf16[128,256]{1,0:T(8,128)(2,1)S(1)}, u32[]{:S(2)}, u32[]{:S(2)}) collective-permute-start(bf16[128,256]{1,0:T(8,128)(2,1)} %bitcast.14), channel_id=1, source_target_pairs={{0,24},{8,16},{16,8},{24,0},{1,25},{9,17},{17,9},{25,1},{2,26},{10... | collective-permute-start | bytes 196616 | tf_op jit(solution)/shard_map/ppermute | solution.py:375
  2.9 0.2 collective-permute-start.1
  3.1 0.3 collective-permute-start
  3.3 0.7 copy-done.8
  4.0 0.9 %slice-done = bf16[256,512]{1,0:T(8,128)(2,1)S(1)} async-done(((bf16[256,768]{1,0:T(8,128)(2,1)}), bf16[256,512]{1,0:T(8,128)(2,1)S(1)}, s32[]{:S(2)}) %slice-start) | async-done | bytes 262168 | tf_op jit(solution)/shard_map/slice | solution.py:410
  5.0 0.1 copy.17
  5.2 0.0 copy-start.3
  5.2 0.0 copy-start.6
  5.2 0.2 copy.15
  5.4 0.4 copy-done.10
  5.8 0.2 copy-done.9
  6.0 0.7 collective-permute-done.1.refs_2_
  6.8 0.1 collective-permute-done.refs_1_
  6.8 2.8 %shard_map.136 = (bf16[8,16,768]{2,1,0:T(8,128)(2,1)}, bf16[512,256]{1,0:T(8,128)(2,1)S(1)}) custom-call(s32[1]{0:T(128)} %bitcast.idx, s32[4,4]{1,0:T(4,128)S(1)} %compare_select_fusion.link, bf16[128,256]{1,0:T(8,128)(2,1)S(1)} %bitcast.17, bf16[128,256]{1,0:T(8,128)(2,1)S(1)} %collective-permute-done.refs_1_, ...), custom_call_target="tpu_custom_call" | custom-call | flops 1 | bytes 1 | tf_op jit(solution)/shard_map/pallas_call | solution.py:82
  9.7 6.9 %all-to-all-start = ((bf16[8,16,768]{2,1,0:T(8,128)(2,1)}), bf16[8,16,768]{2,1,0:T(8,128)(2,1)S(1)}, u32[]{:S(2)}, u32[]{:S(2)}) async-start(bf16[8,16,768]{2,1,0:T(8,128)(2,1)} %get-tuple-element.44), calls=%async_computation | async-start | bytes 393216 | tf_op jit(solution)/shard_map/all_to_all | solution.py:370
  16.6 1.8 %shard_map.137 = (bf16[512,1024]{1,0:T(8,128)(2,1)S(1)}, bf16[512,64]{1,0:T(8,128)(2,1)S(1)}, bf16[512,64]{1,0:T(8,128)(2,1)S(1)}, bf16[64,512]{1,0:T(8,128)(2,1)S(1)}) custom-call(s32[1]{0:T(128)} %bitcast.idx, s32[4,4]{1,0:T(4,128)S(1)} %compare_select_fusion.link, bf16[512,256]{1,0:T(8,128)(2,1)S(1)} %get-tuple-element.45.normed_ref.normed, ...), custom_call_target="tpu_custom_call" | custom-call | flops 20000000000 | bytes 72000000 | tf_op jit(solution)/shard_map/pallas_call | solution.py:82
  18.4 4.3 %all-to-all-done.x_in = bf16[8,16,768]{2,1,0:T(8,128)(2,1)S(1)} async-done(((bf16[8,16,768]{2,1,0:T(8,128)(2,1)}), bf16[8,16,768]{2,1,0:T(8,128)(2,1)S(1)}, u32[]{:S(2)}, u32[]{:S(2)}) %all-to-all-start) | async-done | bytes 196640 | tf_op jit(solution)/shard_map/all_to_all | solution.py:370
  22.8 3.2 %shard_map.138 = (bf16[32,8,128]{2,1,0:T(8,128)(2,1)}, bf16[128,1280]{1,0:T(8,128)(2,1)S(1)}, bf16[128,1280]{1,0:T(8,128)(2,1)}, bf16[8,16,512]{2,1,0:T(8,128)(2,1)}) custom-call(s32[1]{0:T(128)} %bitcast.1.hap, bf16[8,16,768]{2,1,0:T(8,128)(2,1)S(1)} %all-to-all-done.x_in, bf16[256,256]{1,0:T(8,128)(2,1)S(1)} %copy-done.1, ...), custom_call_target="tpu_custom_call" | custom-call | flops 1 | bytes 1 | tf_op jit(solution)/shard_map/pallas_call | solution.py:82
  26.0 1.0 %collective-permute-start.3 = (bf16[128,1280]{1,0:T(8,128)(2,1)S(1)}, bf16[128,1280]{1,0:T(8,128)(2,1)S(1)}, u32[]{:S(2)}, u32[]{:S(2)}) collective-permute-start(bf16[128,1280]{1,0:T(8,128)(2,1)S(1)} %get-tuple-element.50), channel_id=1, source_target_pairs={{0,1},{1,0},{2,3},{3,2},{4,5},{5,4},{6,7},{7,6},{8,9},{9,8},{10,11... | collective-permute-start | bytes 983048 | tf_op jit(solution)/shard_map/ppermute | solution.py:375
  27.1 3.7 %all-to-all-start.1 = ((bf16[32,8,128]{2,1,0:T(8,128)(2,1)}), bf16[32,8,128]{2,1,0:T(8,128)(2,1)S(1)}, u32[]{:S(2)}, u32[]{:S(2)}) async-start(bf16[32,8,128]{2,1,0:T(8,128)(2,1)} %get-tuple-element.48), calls=%async_computation.1 | async-start | bytes 131072 | tf_op jit(solution)/shard_map/all_to_all | solution.py:370
  30.8 0.4 collective-permute-start.4
  31.2 1.0 %copy-done.2 = bf16[128,1280]{1,0:T(8,128)(2,1)S(1)} copy-done((bf16[128,1280]{1,0:T(8,128)(2,1)S(1)}, bf16[128,1280]{1,0:T(8,128)(2,1)}, u32[]{:S(2)}) %copy-start.2) | copy-done | bytes 327704
  32.2 0.2 shard_map.139
  32.4 1.2 %collective-permute-start.6 = (bf16[32,1280]{1,0:T(8,128)(2,1)S(1)}, bf16[32,1280]{1,0:T(8,128)(2,1)S(1)}, u32[]{:S(2)}, u32[]{:S(2)}) collective-permute-start(bf16[32,1280]{1,0:T(8,128)(2,1)S(1)} %get-tuple-element.52), channel_id=1, source_target_pairs={{0,8},{8,0},{16,24},{24,16},{1,9},{9,1},{17,25},{25,17},{2,10},{10... | collective-permute-start | bytes 245768 | tf_op jit(solution)/shard_map/ppermute | solution.py:375
  33.6 1.2 %collective-permute-start.7 = (bf16[32,1280]{1,0:T(8,128)(2,1)S(1)}, bf16[32,1280]{1,0:T(8,128)(2,1)S(1)}, u32[]{:S(2)}, u32[]{:S(2)}) collective-permute-start(bf16[32,1280]{1,0:T(8,128)(2,1)S(1)} %get-tuple-element.53), channel_id=1, source_target_pairs={{0,16},{8,24},{16,0},{24,8},{1,17},{9,25},{17,1},{25,9},{2,18},{10... | collective-permute-start | bytes 245768 | tf_op jit(solution)/shard_map/ppermute | solution.py:375
  34.8 0.3 collective-permute-start.8
  35.1 1.7 %all-to-all-done.1.g_in = bf16[32,8,128]{2,1,0:T(8,128)(2,1)S(1)} async-done(((bf16[32,8,128]{2,1,0:T(8,128)(2,1)}), bf16[32,8,128]{2,1,0:T(8,128)(2,1)S(1)}, u32[]{:S(2)}, u32[]{:S(2)}) %all-to-all-start.1) | async-done | bytes 65568 | tf_op jit(solution)/shard_map/all_to_all | solution.py:370
  36.8 1.7 %shard_map.141 = (bf16[128,192]{1,0:T(8,128)(2,1)S(1)}, bf16[128,192]{1,0:T(8,128)(2,1)S(1)}, bf16[128,192]{1,0:T(8,128)(2,1)S(1)}, bf16[128,192]{1,0:T(8,128)(2...) custom-call(s32[1]{0:T(128)} %bitcast.idx, s32[1]{0:T(128)S(6)} %select_n.11.core, ...), custom_call_target="tpu_custom_call" | custom-call | flops 1 | bytes 1 | tf_op jit(solution)/shard_map/pallas_call | solution.py:82
  38.5 0.5 collective-permute-start.5
  39.0 0.9 %collective-permute-done.5.row_got = bf16[96,256]{1,0:T(8,128)(2,1)S(1)} collective-permute-done((bf16[96,256]{1,0:T(8,128)(2,1)S(1)}, bf16[96,256]{1,0:T(8,128)(2,1)S(1)}, u32[]{:S(2)}, u32[]{:S(2)}) %collective-permute-start.5) | collective-permute-done | bytes 49184 | tf_op jit(solution)/shard_map/ppermute | solution.py:375
  39.9 0.1 shard_map.142
  39.9 1.5 %collective-permute-start.9 = (bf16[320,256]{1,0:T(8,128)(2,1)S(1)}, bf16[320,256]{1,0:T(8,128)(2,1)S(1)}, u32[]{:S(2)}, u32[]{:S(2)}) collective-permute-start(bf16[320,256]{1,0:T(8,128)(2,1)S(1)} %get-tuple-element.66), channel_id=1, source_target_pairs={{0,2},{1,3},{2,0},{3,1},{4,6},{5,7},{6,4},{7,5},{8,10},{9,11},{10,... | collective-permute-start | bytes 491528 | tf_op jit(solution)/shard_map/ppermute | solution.py:375
  41.4 0.1 collective-permute-start.10
  41.5 1.1 %collective-permute-start.11 = (bf16[320,256]{1,0:T(8,128)(2,1)S(1)}, bf16[320,256]{1,0:T(8,128)(2,1)S(1)}, u32[]{:S(2)}, u32[]{:S(2)}) collective-permute-start(bf16[320,256]{1,0:T(8,128)(2,1)S(1)} %get-tuple-element.68), channel_id=1, source_target_pairs={{0,6},{1,7},{2,4},{3,5},{4,2},{5,3},{6,0},{7,1},{8,14},{9,15},{10,... | collective-permute-start | bytes 491528 | tf_op jit(solution)/shard_map/ppermute | solution.py:375
  42.7 4.0 %collective-permute-done.9.refs_1_.refs_4_ = bf16[320,256]{1,0:T(8,128)(2,1)S(1)} collective-permute-done((bf16[320,256]{1,0:T(8,128)(2,1)S(1)}, bf16[320,256]{1,0:T(8,128)(2,1)S(1)}, u32[]{:S(2)}, u32[]{:S(2)}) %collective-permute-start.9) | collective-permute-done | bytes 163872 | tf_op jit(solution)/shard_map/ppermute | solution.py:375
  46.7 1.5 %collective-permute-done.10.refs_2_.refs_5_ = bf16[320,256]{1,0:T(8,128)(2,1)S(1)} collective-permute-done((bf16[320,256]{1,0:T(8,128)(2,1)S(1)}, bf16[320,256]{1,0:T(8,128)(2,1)S(1)}, u32[]{:S(2)}, u32[]{:S(2)}) %collective-permute-start.10) | collective-permute-done | bytes 163872 | tf_op jit(solution)/shard_map/ppermute | solution.py:375
  48.1 8.5 %collective-permute-done.11.refs_3_.refs_6_ = bf16[320,256]{1,0:T(8,128)(2,1)S(1)} collective-permute-done((bf16[320,256]{1,0:T(8,128)(2,1)S(1)}, bf16[320,256]{1,0:T(8,128)(2,1)S(1)}, u32[]{:S(2)}, u32[]{:S(2)}) %collective-permute-start.11) | collective-permute-done | bytes 163872 | tf_op jit(solution)/shard_map/ppermute | solution.py:375
  56.6 0.2 shard_map.143
  56.8 0.3 collective-permute-start.12
  57.1 1.1 %collective-permute-start.13 = (bf16[384,256]{1,0:T(8,128)(2,1)S(1)}, bf16[384,256]{1,0:T(8,128)(2,1)S(1)}, u32[]{:S(2)}, u32[]{:S(2)}) collective-permute-start(bf16[384,256]{1,0:T(8,128)(2,1)S(1)} %get-tuple-element.73), channel_id=1, source_target_pairs={{0,16},{8,24},{16,0},{24,8},{1,17},{9,25},{17,1},{25,9},{2,18},{10... | collective-permute-start | bytes 589832 | tf_op jit(solution)/shard_map/ppermute | solution.py:375
  58.2 1.3 %collective-permute-start.14 = (bf16[384,256]{1,0:T(8,128)(2,1)S(1)}, bf16[384,256]{1,0:T(8,128)(2,1)S(1)}, u32[]{:S(2)}, u32[]{:S(2)}) collective-permute-start(bf16[384,256]{1,0:T(8,128)(2,1)S(1)} %get-tuple-element.74), channel_id=1, source_target_pairs={{0,24},{8,16},{16,8},{24,0},{1,25},{9,17},{17,9},{25,1},{2,26},{10... | collective-permute-start | bytes 589832 | tf_op jit(solution)/shard_map/ppermute | solution.py:375
  59.5 1.9 %collective-permute-done.12.refs_0_.refs_2_ = bf16[384,256]{1,0:T(8,128)(2,1)S(1)} collective-permute-done((bf16[384,256]{1,0:T(8,128)(2,1)S(1)}, bf16[384,256]{1,0:T(8,128)(2,1)S(1)}, u32[]{:S(2)}, u32[]{:S(2)}) %collective-permute-start.12) | collective-permute-done | bytes 196640 | tf_op jit(solution)/shard_map/ppermute | solution.py:375
  61.4 4.9 %collective-permute-start.16 = (bf16[384,256]{1,0:T(8,128)(2,1)S(1)}, bf16[384,256]{1,0:T(8,128)(2,1)S(1)}, u32[]{:S(2)}, u32[]{:S(2)}) collective-permute-start(bf16[384,256]{1,0:T(8,128)(2,1)S(1)} %collective-permute-done.12.refs_0_.refs_2_), channel_id=1, source_target_pairs={{0,1},{1,0},{2,3},{3,2},{4,5},{5,4},{6,7},{7,6},{8,9},{9,8},{10,11... | collective-permute-start | bytes 589832 | tf_op jit(solution)/shard_map/ppermute | solution.py:375
  66.3 2.5 %collective-permute-start.17 = (bf16[384,256]{1,0:T(8,128)(2,1)S(1)}, bf16[384,256]{1,0:T(8,128)(2,1)S(1)}, u32[]{:S(2)}, u32[]{:S(2)}) collective-permute-start(bf16[384,256]{1,0:T(8,128)(2,1)S(1)} %collective-permute-done.13.refs_1_.refs_4_), channel_id=1, source_target_pairs={{0,1},{1,0},{2,3},{3,2},{4,5},{5,4},{6,7},{7,6},{8,9},{9,8},{10,11... | collective-permute-start | bytes 589832 | tf_op jit(solution)/shard_map/ppermute | solution.py:375
  68.8 0.5 collective-permute-start.15
  69.3 1.0 %shard_map.144 = (bf16[128,256]{1,0:T(8,128)(2,1)}, bf16[128,256]{1,0:T(8,128)(2,1)}) custom-call(s32[1]{0:T(128)} %bitcast.idx, s32[1]{0:T(128)} %bitcast.1.hap, bf16[128,256]{1,0:T(8,128)(2,1)S(1)} %bitcast.18, f32[2,256]{1,0:T(2,128)S(1)} %pad_maximum_fusion.refs_5_.gain, bf16[768,256]{1,0:T(8,128)(2,1)S(1)} %bitcast.12, ...), custom_call_target="tpu_custom_call" | custom-call | flops 1 | bytes 1 | tf_op jit(solution)/shard_map/pallas_call | solution.py:82
  70.2 0.2 collective-permute-done.15.refs_1_
  70.4 1.5 %shard_map.145 = (f32[256,768]{1,0:T(8,128)}, f32[256,256]{1,0:T(8,128)}, f32[256,768]{1,0:T(8,128)}, f32[256,256]{1,0:T(8,128)}) custom-call(s32[1]{0:T(128)} %bitcast.idx, s32[1]{0:T(128)S(6)} %select_n.11.core, bf16[256,256]{1,0:T(8,128)(2,1)S(1)} %get-tuple-element.77.refs_0_, bf16[256,256]{1,0:T(8,128)(2,1)S(1)} %collective-permute-done.15.refs_1_, ...), custom_call_target="tpu_custom_call" | custom-call | flops 1 | bytes 1 | tf_op jit(solution)/shard_map/pallas_call | solution.py:82
  (32 shorter events, 0.1 us)
Async XLA Ops:
  0.6 5.4 %collective-permute-start.2 = (bf16[128,256]{1,0:T(8,128)(2,1)}, bf16[128,256]{1,0:T(8,128)(2,1)S(1)}, u32[]{:S(2)}, u32[]{:S(2)}) collective-permute-start(bf16[128,256]{1,0:T(8,128)(2,1)} %bitcast.14), channel_id=1, source_target_pairs={{0,24},{8,16},{16,8},{24,0},{1,25},{9,17},{17,9},{25,1},{2,26},{10... | collective-permute-start | bytes 196616 | tf_op jit(solution)/shard_map/ppermute | solution.py:375
  2.9 3.9 %collective-permute-start.1 = (bf16[128,256]{1,0:T(8,128)(2,1)}, bf16[128,256]{1,0:T(8,128)(2,1)S(1)}, u32[]{:S(2)}, u32[]{:S(2)}) collective-permute-start(bf16[128,256]{1,0:T(8,128)(2,1)} %bitcast.15), channel_id=1, source_target_pairs={{0,16},{8,24},{16,0},{24,8},{1,17},{9,25},{17,1},{25,9},{2,18},{10... | collective-permute-start | bytes 196616 | tf_op jit(solution)/shard_map/ppermute | solution.py:375
  3.1 3.7 %collective-permute-start = (bf16[128,256]{1,0:T(8,128)(2,1)}, bf16[128,256]{1,0:T(8,128)(2,1)S(1)}, u32[]{:S(2)}, u32[]{:S(2)}) collective-permute-start(bf16[128,256]{1,0:T(8,128)(2,1)} %bitcast.16), channel_id=1, source_target_pairs={{0,8},{8,0},{16,24},{24,16},{1,9},{9,1},{17,25},{25,17},{2,10},{10... | collective-permute-start | bytes 196616 | tf_op jit(solution)/shard_map/ppermute | solution.py:375
  3.3 0.7 copy-start.8
  4.0 0.9 %slice-start = ((bf16[256,768]{1,0:T(8,128)(2,1)}), bf16[256,512]{1,0:T(8,128)(2,1)S(1)}, s32[]{:S(2)}) async-start(bf16[256,768]{1,0:T(8,128)(2,1)} %col_proj.1), calls=%async_computation.2 | async-start | bytes 524288 | tf_op jit(solution)/shard_map/slice | solution.py:410
  4.0 1.1 %copy-start.7 = (bf16[256,768]{1,0:T(8,128)(2,1)S(1)}, bf16[256,768]{1,0:T(8,128)(2,1)}, u32[]{:S(2)}) copy-start(bf16[256,768]{1,0:T(8,128)(2,1)} %param.12) | copy-start | bytes 1179652
  5.1 0.7 copy-start.10
  5.1 1.7 %copy-start.1 = (bf16[256,256]{1,0:T(8,128)(2,1)S(1)}, bf16[256,256]{1,0:T(8,128)(2,1)}, u32[]{:S(2)}) copy-start(bf16[256,256]{1,0:T(8,128)(2,1)} %row_out.1) | copy-start | bytes 393220
  5.2 1.7 %copy-start.3 = (bf16[128,1,256]{2,0,1:T(8,128)(2,1)S(1)}, bf16[128,1,256]{2,0,1:T(8,128)(2,1)}, u32[]{:S(2)}) copy-start(bf16[128,1,256]{2,0,1:T(8,128)(2,1)} %param.9) | copy-start | bytes 196612
  5.2 1.7 %copy-start.6 = (bf16[128,1,256]{2,0,1:T(8,128)(2,1)S(1)}, bf16[128,1,256]{2,0,1:T(8,128)(2,1)}, u32[]{:S(2)}) copy-start(bf16[128,1,256]{2,0,1:T(8,128)(2,1)} %param.17) | copy-start | bytes 196612
  5.4 0.7 copy-start.9
  9.7 13.1 %all-to-all-start = ((bf16[8,16,768]{2,1,0:T(8,128)(2,1)}), bf16[8,16,768]{2,1,0:T(8,128)(2,1)S(1)}, u32[]{:S(2)}, u32[]{:S(2)}) async-start(bf16[8,16,768]{2,1,0:T(8,128)(2,1)} %get-tuple-element.44), calls=%async_computation | async-start | bytes 393216 | tf_op jit(solution)/shard_map/all_to_all | solution.py:370
  16.6 6.1 %copy-start = (bf16[256,768]{1,0:T(8,128)(2,1)S(1)}, bf16[256,768]{1,0:T(8,128)(2,1)}, u32[]{:S(2)}) copy-start(bf16[256,768]{1,0:T(8,128)(2,1)} %col_proj.1) | copy-start | bytes 1179652
  16.6 6.1 %copy-start.5 = (bf16[256,256]{1,0:T(8,128)(2,1)S(1)}, bf16[256,256]{1,0:T(8,128)(2,1)}, u32[]{:S(2)}) copy-start(bf16[256,256]{1,0:T(8,128)(2,1)} %col_out.1) | copy-start | bytes 393220
  26.0 4.7 %copy-start.4 = (bf16[8,16,512]{2,1,0:T(8,128)(2,1)S(1)}, bf16[8,16,512]{2,1,0:T(8,128)(2,1)}, u32[]{:S(2)}) copy-start(bf16[8,16,512]{2,1,0:T(8,128)(2,1)} %get-tuple-element.55.og) | copy-start | bytes 393220
  26.0 5.2 %collective-permute-start.3 = (bf16[128,1280]{1,0:T(8,128)(2,1)S(1)}, bf16[128,1280]{1,0:T(8,128)(2,1)S(1)}, u32[]{:S(2)}, u32[]{:S(2)}) collective-permute-start(bf16[128,1280]{1,0:T(8,128)(2,1)S(1)} %get-tuple-element.50), channel_id=1, source_target_pairs={{0,1},{1,0},{2,3},{3,2},{4,5},{5,4},{6,7},{7,6},{8,9},{9,8},{10,11... | collective-permute-start | bytes 983048 | tf_op jit(solution)/shard_map/ppermute | solution.py:375
  27.1 9.7 %all-to-all-start.1 = ((bf16[32,8,128]{2,1,0:T(8,128)(2,1)}), bf16[32,8,128]{2,1,0:T(8,128)(2,1)S(1)}, u32[]{:S(2)}, u32[]{:S(2)}) async-start(bf16[32,8,128]{2,1,0:T(8,128)(2,1)} %get-tuple-element.48), calls=%async_computation.1 | async-start | bytes 131072 | tf_op jit(solution)/shard_map/all_to_all | solution.py:370
  30.8 4.3 %collective-permute-start.4 = (bf16[4,16,512]{2,1,0:T(8,128)(2,1)S(1)}, bf16[4,16,512]{2,1,0:T(8,128)(2,1)S(1)}, u32[]{:S(2)}, u32[]{:S(2)}) collective-permute-start(bf16[4,16,512]{2,1,0:T(8,128)(2,1)S(1)} %get-tuple-element.56), channel_id=1, source_target_pairs={{0,1},{1,0},{2,3},{3,2},{4,5},{5,4},{6,7},{7,6},{8,9},{9,8},{10,11... | collective-permute-start | bytes 196616 | tf_op jit(solution)/shard_map/ppermute | solution.py:375
  31.2 1.0 %copy-start.2 = (bf16[128,1280]{1,0:T(8,128)(2,1)S(1)}, bf16[128,1280]{1,0:T(8,128)(2,1)}, u32[]{:S(2)}) copy-start(bf16[128,1280]{1,0:T(8,128)(2,1)} %get-tuple-element.49.keep) | copy-start | bytes 983044
  32.4 7.5 %collective-permute-start.6 = (bf16[32,1280]{1,0:T(8,128)(2,1)S(1)}, bf16[32,1280]{1,0:T(8,128)(2,1)S(1)}, u32[]{:S(2)}, u32[]{:S(2)}) collective-permute-start(bf16[32,1280]{1,0:T(8,128)(2,1)S(1)} %get-tuple-element.52), channel_id=1, source_target_pairs={{0,8},{8,0},{16,24},{24,16},{1,9},{9,1},{17,25},{25,17},{2,10},{10... | collective-permute-start | bytes 245768 | tf_op jit(solution)/shard_map/ppermute | solution.py:375
  33.6 6.2 %collective-permute-start.7 = (bf16[32,1280]{1,0:T(8,128)(2,1)S(1)}, bf16[32,1280]{1,0:T(8,128)(2,1)S(1)}, u32[]{:S(2)}, u32[]{:S(2)}) collective-permute-start(bf16[32,1280]{1,0:T(8,128)(2,1)S(1)} %get-tuple-element.53), channel_id=1, source_target_pairs={{0,16},{8,24},{16,0},{24,8},{1,17},{9,25},{17,1},{25,9},{2,18},{10... | collective-permute-start | bytes 245768 | tf_op jit(solution)/shard_map/ppermute | solution.py:375
  34.8 5.1 %collective-permute-start.8 = (bf16[32,1280]{1,0:T(8,128)(2,1)S(1)}, bf16[32,1280]{1,0:T(8,128)(2,1)S(1)}, u32[]{:S(2)}, u32[]{:S(2)}) collective-permute-start(bf16[32,1280]{1,0:T(8,128)(2,1)S(1)} %get-tuple-element.54), channel_id=1, source_target_pairs={{0,24},{8,16},{16,8},{24,0},{1,25},{9,17},{17,9},{25,1},{2,26},{10... | collective-permute-start | bytes 245768 | tf_op jit(solution)/shard_map/ppermute | solution.py:375
  38.5 1.3 %collective-permute-start.5 = (bf16[96,256]{1,0:T(8,128)(2,1)S(1)}, bf16[96,256]{1,0:T(8,128)(2,1)S(1)}, u32[]{:S(2)}, u32[]{:S(2)}) collective-permute-start(bf16[96,256]{1,0:T(8,128)(2,1)S(1)} %get-tuple-element.63), channel_id=1, source_target_pairs={{0,1},{1,0},{2,3},{3,2},{4,5},{5,4},{6,7},{7,6},{8,9},{9,8},{10,11... | collective-permute-start | bytes 147464 | tf_op jit(solution)/shard_map/ppermute | solution.py:375
  39.9 6.7 %collective-permute-start.9 = (bf16[320,256]{1,0:T(8,128)(2,1)S(1)}, bf16[320,256]{1,0:T(8,128)(2,1)S(1)}, u32[]{:S(2)}, u32[]{:S(2)}) collective-permute-start(bf16[320,256]{1,0:T(8,128)(2,1)S(1)} %get-tuple-element.66), channel_id=1, source_target_pairs={{0,2},{1,3},{2,0},{3,1},{4,6},{5,7},{6,4},{7,5},{8,10},{9,11},{10,... | collective-permute-start | bytes 491528 | tf_op jit(solution)/shard_map/ppermute | solution.py:375
  41.4 6.7 %collective-permute-start.10 = (bf16[320,256]{1,0:T(8,128)(2,1)S(1)}, bf16[320,256]{1,0:T(8,128)(2,1)S(1)}, u32[]{:S(2)}, u32[]{:S(2)}) collective-permute-start(bf16[320,256]{1,0:T(8,128)(2,1)S(1)} %get-tuple-element.67), channel_id=1, source_target_pairs={{0,4},{1,5},{2,6},{3,7},{4,0},{5,1},{6,2},{7,3},{8,12},{9,13},{10,... | collective-permute-start | bytes 491528 | tf_op jit(solution)/shard_map/ppermute | solution.py:375
  41.5 15.1 %collective-permute-start.11 = (bf16[320,256]{1,0:T(8,128)(2,1)S(1)}, bf16[320,256]{1,0:T(8,128)(2,1)S(1)}, u32[]{:S(2)}, u32[]{:S(2)}) collective-permute-start(bf16[320,256]{1,0:T(8,128)(2,1)S(1)} %get-tuple-element.68), channel_id=1, source_target_pairs={{0,6},{1,7},{2,4},{3,5},{4,2},{5,3},{6,0},{7,1},{8,14},{9,15},{10,... | collective-permute-start | bytes 491528 | tf_op jit(solution)/shard_map/ppermute | solution.py:375
  56.8 4.6 %collective-permute-start.12 = (bf16[384,256]{1,0:T(8,128)(2,1)S(1)}, bf16[384,256]{1,0:T(8,128)(2,1)S(1)}, u32[]{:S(2)}, u32[]{:S(2)}) collective-permute-start(bf16[384,256]{1,0:T(8,128)(2,1)S(1)} %get-tuple-element.72), channel_id=1, source_target_pairs={{0,8},{8,0},{16,24},{24,16},{1,9},{9,1},{17,25},{25,17},{2,10},{10... | collective-permute-start | bytes 589832 | tf_op jit(solution)/shard_map/ppermute | solution.py:375
  57.1 9.2 %collective-permute-start.13 = (bf16[384,256]{1,0:T(8,128)(2,1)S(1)}, bf16[384,256]{1,0:T(8,128)(2,1)S(1)}, u32[]{:S(2)}, u32[]{:S(2)}) collective-permute-start(bf16[384,256]{1,0:T(8,128)(2,1)S(1)} %get-tuple-element.73), channel_id=1, source_target_pairs={{0,16},{8,24},{16,0},{24,8},{1,17},{9,25},{17,1},{25,9},{2,18},{10... | collective-permute-start | bytes 589832 | tf_op jit(solution)/shard_map/ppermute | solution.py:375
  58.2 10.6 %collective-permute-start.14 = (bf16[384,256]{1,0:T(8,128)(2,1)S(1)}, bf16[384,256]{1,0:T(8,128)(2,1)S(1)}, u32[]{:S(2)}, u32[]{:S(2)}) collective-permute-start(bf16[384,256]{1,0:T(8,128)(2,1)S(1)} %get-tuple-element.74), channel_id=1, source_target_pairs={{0,24},{8,16},{16,8},{24,0},{1,25},{9,17},{17,9},{25,1},{2,26},{10... | collective-permute-start | bytes 589832 | tf_op jit(solution)/shard_map/ppermute | solution.py:375
  61.4 9.0 %collective-permute-start.16 = (bf16[384,256]{1,0:T(8,128)(2,1)S(1)}, bf16[384,256]{1,0:T(8,128)(2,1)S(1)}, u32[]{:S(2)}, u32[]{:S(2)}) collective-permute-start(bf16[384,256]{1,0:T(8,128)(2,1)S(1)} %collective-permute-done.12.refs_0_.refs_2_), channel_id=1, source_target_pairs={{0,1},{1,0},{2,3},{3,2},{4,5},{5,4},{6,7},{7,6},{8,9},{9,8},{10,11... | collective-permute-start | bytes 589832 | tf_op jit(solution)/shard_map/ppermute | solution.py:375
  66.3 4.1 %collective-permute-start.17 = (bf16[384,256]{1,0:T(8,128)(2,1)S(1)}, bf16[384,256]{1,0:T(8,128)(2,1)S(1)}, u32[]{:S(2)}, u32[]{:S(2)}) collective-permute-start(bf16[384,256]{1,0:T(8,128)(2,1)S(1)} %collective-permute-done.13.refs_1_.refs_4_), channel_id=1, source_target_pairs={{0,1},{1,0},{2,3},{3,2},{4,5},{5,4},{6,7},{7,6},{8,9},{9,8},{10,11... | collective-permute-start | bytes 589832 | tf_op jit(solution)/shard_map/ppermute | solution.py:375
  68.8 1.6 %collective-permute-start.18 = (bf16[384,256]{1,0:T(8,128)(2,1)S(1)}, bf16[384,256]{1,0:T(8,128)(2,1)S(1)}, u32[]{:S(2)}, u32[]{:S(2)}) collective-permute-start(bf16[384,256]{1,0:T(8,128)(2,1)S(1)} %collective-permute-done.14.refs_2_.refs_6_), channel_id=1, source_target_pairs={{0,1},{1,0},{2,3},{3,2},{4,5},{5,4},{6,7},{7,6},{8,9},{9,8},{10,11... | collective-permute-start | bytes 589832 | tf_op jit(solution)/shard_map/ppermute | solution.py:375
  68.8 1.6 %collective-permute-start.15 = (bf16[256,256]{1,0:T(8,128)(2,1)S(1)}, bf16[256,256]{1,0:T(8,128)(2,1)S(1)}, u32[]{:S(2)}, u32[]{:S(2)}) collective-permute-start(bf16[256,256]{1,0:T(8,128)(2,1)S(1)} %get-tuple-element.77.refs_0_), channel_id=1, source_target_pairs={{0,1},{1,0},{2,3},{3,2},{4,5},{5,4},{6,7},{7,6},{8,9},{9,8},{10,11... | collective-permute-start | bytes 393224 | tf_op jit(solution)/shard_map/ppermute | solution.py:375

commit v11 on v10

--- a/solution.py
+++ b/solution.py
@@ -299,7 +299,7 @@
             for side in range(2):
                 start = base + (2 * j + side) * per
                 og[side, hap[0] ^ (2 * m + j)] = parts[m][start : start + per, :].astype(F32)
-    grads = [gp[...]] + [g[g.shape[0] - rows :, : 3 * group] for g in gps]
+    grads = [gp[...]] + [g[g.shape[0] - rows :, : 3 * group] for g in gps[::-1]]
     grad_normed = 0.0
     for k in range(sites):
         place = [pl.multiple_of(p * width + (me ^ k) * group, group) for p in range(3)]
@@ -320,7 +320,7 @@
     tiles = [total[:, t * width : (t + 1) * width] for t in range(5)]
     rows = row_keep[...].astype(F32) + row_got[...].astype(F32)
     joined = jnp.concatenate([rows] + tiles, axis=0).astype(BF16)
-    for m, out in enumerate(outs):
+    for m, out in enumerate(outs[:1] + outs[:0:-1]):
         out[:depth, :] = joined
         both = [og_keep[m].astype(F32), og_got[m].astype(F32)]
         both = [x[:, j * width : (j + 1) * width] for x in both for j in range(2)]
@@ -335,7 +335,7 @@
     while len(terms) > 1:
         terms = [a + b for a, b in zip(terms[::2], terms[1::2])]
     mine[...] = terms[0].astype(BF16)
-    for gp, out in zip(gps, outs):
+    for gp, out in zip(gps, outs[::-1]):
         out[:depth, :] = mine[...]
         out[depth:, : gp.shape[1]] = gp[...]
         out[depth:, gp.shape[1] :] = jnp.zeros((gp.shape[0], width - gp.shape[1]), BF16)
@@ -343,27 +343,40 @@
 
 def weights_finish(sites, idx, core, *refs):
     pieces = refs[: 2 * sites]
-    rp, ro, cp, co, rows_t = refs[2 * sites :]
+    rp, ro_out, cp_out, co_out, rows_t, ro, cp, co, sems = refs[2 * sites :]
     width = ro.shape[0]
     group = width // sites
     unit = group // 2
     part = width // 2 // sites
     for j in range(2 * sites):
+        cc = core[0] ^ (j % 2)
+        g = idx[0] ^ (j // 2)
+        piece = pieces[j][3 * unit : 3 * unit + 5 * part, :].astype(F32)
+        here = pl.ds(pl.multiple_of(cc * (width // 2) + g * part, part), part)
+        tiles = [piece[t * part : (t + 1) * part] for t in range(5)]
+        for t in range(3):
+            cp[here, t * width : (t + 1) * width] = tiles[t]
+        co[here, :] = tiles[3]
+        ro[here, :] = tiles[4]
+    copies = [
+        pltpu.make_async_copy(cp, cp_out, sems.at[0]),
+        pltpu.make_async_copy(co, co_out, sems.at[1]),
+        pltpu.make_async_copy(ro, ro_out, sems.at[2]),
+    ]
+    for copy in copies:
+        copy.start()
+    for j in range(2 * sites):
         k = j // 2
         cc = core[0] ^ (j % 2)
         g = idx[0] ^ k
-        piece = pieces[j][...].astype(F32)
+        piece = pieces[j][: 3 * unit, :].astype(F32)
         for u in range(3):
             place = 3 * cc + u
             dest = (place // 2) * width + g * group + (place % 2) * unit
             rows_t[pl.ds(pl.multiple_of(dest, unit), unit), :] = piece[u * unit : (u + 1) * unit]
-        here = pl.ds(pl.multiple_of(cc * (width // 2) + g * part, part), part)
-        tiles = [piece[3 * unit + t * part : 3 * unit + (t + 1) * part] for t in range(5)]
-        for t in range(3):
-            cp[here, t * width : (t + 1) * width] = tiles[t]
-        co[here, :] = tiles[3]
-        ro[here, :] = tiles[4]
     rp[...] = jnp.transpose(rows_t[...])
+    for copy in copies:
+        copy.wait()
 
 
 def exchange(value, axis):
@@ -472,25 +485,33 @@
         [((depth + 4 * per, width), BF16)] * (haps // 2),
         row_keep, row_got, og_keep, og_got, *cols,
     )
+    parts = [parts[0]] + list(parts[:0:-1])
     parts = [parts[0]] + [swapped(parts[m], "hap", 2 * m) for m in range(1, haps // 2)]
     mine, *sends = call(
         functools.partial(weights_sum, haps, sites),
         [((depth, width), BF16)] + [((depth + rows, width), BF16)] * (sites - 1),
-        *parts, *gps[1:],
-    )
+        *parts[::-1], *gps[1:],
+    )
+    sends = sends[::-1]
     got = [swapped(sends[k - 1], "site", k) for k in range(1, sites)]
     full = [x for p in [mine] + got for x in (p, swapped(p, "hap", 1))]
     out, grad = call(
         functools.partial(row_finish, sites, haps),
         [((rows, width), BF16)] * 2,
-        idx, hap, feats, gains, w_t, gps[0], *got, *parts, scalars=2,
+        idx, hap, feats, gains, w_t, gps[0], *got[::-1], *parts, scalars=2,
         scratch=[pltpu.VMEM((2, haps, per, width), F32)],
     )
     rp, ro, cp, co = call(
         functools.partial(weights_finish, sites),
         [((width, 3 * width), F32), ((width, width), F32)] * 2,
-        idx, core, *full, scalars=2,
-        scratch=[pltpu.VMEM((3 * width, width), F32)],
+        idx, core, *full, scalars=2, far=3,
+        scratch=[
+            pltpu.VMEM((3 * width, width), F32),
+            pltpu.VMEM((width, width), F32),
+            pltpu.VMEM((width, 3 * width), F32),
+            pltpu.VMEM((width, width), F32),
+            pltpu.SemaphoreType.DMA((3,)),
+        ],
     )
     shape = (rows, 1, width)
     return (out.reshape(shape), grad.reshape(shape), rp, ro, cp, co)

time: 72.2 us -> 74.2 us (1.028)
  the two profiles are of different devices: /device:TPU:9 before, /device:TPU:0 now
where the time goes in v11:
time: 74.2 us; the launch traced here: 73.9 us
  waiting for transfers between devices  31.6 us (43%)
  starting transfers between devices  24.7 us (33%)
  Pallas kernels  13.1 us (18%)
  local copies, waits for them, and re-layouts  3.62 us (5%)
  between operations  0.83 us (1%)
    ppermute x19, waiting for transfers between devices, swapped(): return lax.ppermute(value, axis, [(i, i ^ by) for i in range(length)])  22.7 us
    ppermute x19, starting transfers between devices, swapped(): return lax.ppermute(value, axis, [(i, i ^ by) for i in range(length)])  17.1 us
    pallas_call x10, Pallas kernels, call(): pl.pallas_call(body, out_shape=[jax.ShapeDtypeStruct(s, d) for s, d in ou...  13.1 us
    all_to_all x2, waiting for transfers between devices, exchange(): return lax.all_to_all(value, axis, 0, 0, tiled=True)  8.95 us
    all_to_all x2, starting transfers between devices, exchange(): return lax.all_to_all(value, axis, 0, 0, tiled=True)  7.55 us
    unnamed x24, local copies, waits for them, and re-layouts  2.67 us
  transfers between devices with their start and end apart: 21, of which 10 were waited for; matrix products, arithmetic and copies ran while one was open for 0% of the time, Pallas kernels for 6%

profile of v11, /device:TPU:0, one launch (start us, length us, event | category | flops | bytes accessed | tf_op | source)
XLA Modules:
  0.0 73.9 jit_solution(9189764671156762580)
XLA Ops:
  0.6 4.0 %collective-permute-start.2 = (bf16[128,256]{1,0:T(8,128)(2,1)}, bf16[128,256]{1,0:T(8,128)(2,1)S(1)}, u32[]{:S(2)}, u32[]{:S(2)}) collective-permute-start(bf16[128,256]{1,0:T(8,128)(2,1)} %bitcast.14), channel_id=1, source_target_pairs={{0,24},{8,16},{16,8},{24,0},{1,25},{9,17},{17,9},{25,1},{2,26},{10... | collective-permute-start | bytes 196616 | tf_op jit(solution)/shard_map/ppermute | solution.py:388
  4.6 0.5 collective-permute-start.1
  5.1 0.1 collective-permute-start
  5.2 0.7 copy-done.8
  5.9 0.9 %slice-done = bf16[256,512]{1,0:T(8,128)(2,1)S(1)} async-done(((bf16[256,768]{1,0:T(8,128)(2,1)}), bf16[256,512]{1,0:T(8,128)(2,1)S(1)}, s32[]{:S(2)}) %slice-start) | async-done | bytes 262168 | tf_op jit(solution)/shard_map/slice | solution.py:423
  6.9 0.1 copy.17
  7.0 0.0 copy-start.10
  7.0 0.0 copy-start.1
  7.0 0.0 copy-start.3
  7.1 0.2 copy.15
  7.2 0.0 copy-start.9
  7.3 0.4 copy-done.10
  7.7 0.2 copy-done.9
  7.9 1.1 %collective-permute-done.1.refs_2_ = bf16[128,256]{1,0:T(8,128)(2,1)S(1)} collective-permute-done((bf16[128,256]{1,0:T(8,128)(2,1)}, bf16[128,256]{1,0:T(8,128)(2,1)S(1)}, u32[]{:S(2)}, u32[]{:S(2)}) %collective-permute-start.1) | collective-permute-done | bytes 65568 | tf_op jit(solution)/shard_map/ppermute | solution.py:388
  9.1 0.5 collective-permute-done.refs_1_
  9.6 2.8 %shard_map.136 = (bf16[8,16,768]{2,1,0:T(8,128)(2,1)}, bf16[512,256]{1,0:T(8,128)(2,1)S(1)}) custom-call(s32[1]{0:T(128)} %bitcast.idx, s32[4,4]{1,0:T(4,128)S(1)} %compare_select_fusion.link, bf16[128,256]{1,0:T(8,128)(2,1)S(1)} %bitcast.17, bf16[128,256]{1,0:T(8,128)(2,1)S(1)} %collective-permute-done.refs_1_, ...), custom_call_target="tpu_custom_call" | custom-call | flops 1 | bytes 1 | tf_op jit(solution)/shard_map/pallas_call | solution.py:82
  12.4 4.9 %all-to-all-start = ((bf16[8,16,768]{2,1,0:T(8,128)(2,1)}), bf16[8,16,768]{2,1,0:T(8,128)(2,1)S(1)}, u32[]{:S(2)}, u32[]{:S(2)}) async-start(bf16[8,16,768]{2,1,0:T(8,128)(2,1)} %get-tuple-element.44), calls=%async_computation | async-start | bytes 393216 | tf_op jit(solution)/shard_map/all_to_all | solution.py:383
  17.3 1.8 %shard_map.137 = (bf16[512,1024]{1,0:T(8,128)(2,1)S(1)}, bf16[512,64]{1,0:T(8,128)(2,1)S(1)}, bf16[512,64]{1,0:T(8,128)(2,1)S(1)}, bf16[64,512]{1,0:T(8,128)(2,1)S(1)}) custom-call(s32[1]{0:T(128)} %bitcast.idx, s32[4,4]{1,0:T(4,128)S(1)} %compare_select_fusion.link, bf16[512,256]{1,0:T(8,128)(2,1)S(1)} %get-tuple-element.45.normed_ref.normed, ...), custom_call_target="tpu_custom_call" | custom-call | flops 20000000000 | bytes 72000000 | tf_op jit(solution)/shard_map/pallas_call | solution.py:82
  19.1 6.5 %all-to-all-done.x_in = bf16[8,16,768]{2,1,0:T(8,128)(2,1)S(1)} async-done(((bf16[8,16,768]{2,1,0:T(8,128)(2,1)}), bf16[8,16,768]{2,1,0:T(8,128)(2,1)S(1)}, u32[]{:S(2)}, u32[]{:S(2)}) %all-to-all-start) | async-done | bytes 196640 | tf_op jit(solution)/shard_map/all_to_all | solution.py:383
  25.7 3.3 %shard_map.138 = (bf16[32,8,128]{2,1,0:T(8,128)(2,1)}, bf16[128,1280]{1,0:T(8,128)(2,1)S(1)}, bf16[128,1280]{1,0:T(8,128)(2,1)}, bf16[8,16,512]{2,1,0:T(8,128)(2,1)}) custom-call(s32[1]{0:T(128)} %bitcast.1.hap, bf16[8,16,768]{2,1,0:T(8,128)(2,1)S(1)} %all-to-all-done.x_in, bf16[256,256]{1,0:T(8,128)(2,1)S(1)} %copy-done.1, ...), custom_call_target="tpu_custom_call" | custom-call | flops 1 | bytes 1 | tf_op jit(solution)/shard_map/pallas_call | solution.py:82
  28.9 0.0 copy-start.4
  28.9 0.1 collective-permute-start.3
  29.0 2.7 %all-to-all-start.1 = ((bf16[32,8,128]{2,1,0:T(8,128)(2,1)}), bf16[32,8,128]{2,1,0:T(8,128)(2,1)S(1)}, u32[]{:S(2)}, u32[]{:S(2)}) async-start(bf16[32,8,128]{2,1,0:T(8,128)(2,1)} %get-tuple-element.48), calls=%async_computation.1 | async-start | bytes 131072 | tf_op jit(solution)/shard_map/all_to_all | solution.py:383
  31.7 0.3 collective-permute-start.4
  32.0 1.0 %copy-done.2 = bf16[128,1280]{1,0:T(8,128)(2,1)S(1)} copy-done((bf16[128,1280]{1,0:T(8,128)(2,1)S(1)}, bf16[128,1280]{1,0:T(8,128)(2,1)}, u32[]{:S(2)}) %copy-start.2) | copy-done | bytes 327704
  33.0 0.2 shard_map.139
  33.2 1.7 %collective-permute-start.6 = (bf16[32,1280]{1,0:T(8,128)(2,1)S(1)}, bf16[32,1280]{1,0:T(8,128)(2,1)S(1)}, u32[]{:S(2)}, u32[]{:S(2)}) collective-permute-start(bf16[32,1280]{1,0:T(8,128)(2,1)S(1)} %get-tuple-element.52), channel_id=1, source_target_pairs={{0,8},{8,0},{16,24},{24,16},{1,9},{9,1},{17,25},{25,17},{2,10},{10... | collective-permute-start | bytes 245768 | tf_op jit(solution)/shard_map/ppermute | solution.py:388
  34.9 1.5 %collective-permute-start.7 = (bf16[32,1280]{1,0:T(8,128)(2,1)S(1)}, bf16[32,1280]{1,0:T(8,128)(2,1)S(1)}, u32[]{:S(2)}, u32[]{:S(2)}) collective-permute-start(bf16[32,1280]{1,0:T(8,128)(2,1)S(1)} %get-tuple-element.53), channel_id=1, source_target_pairs={{0,16},{8,24},{16,0},{24,8},{1,17},{9,25},{17,1},{25,9},{2,18},{10... | collective-permute-start | bytes 245768 | tf_op jit(solution)/shard_map/ppermute | solution.py:388
  36.4 0.3 collective-permute-start.8
  36.8 2.4 %all-to-all-done.1.g_in = bf16[32,8,128]{2,1,0:T(8,128)(2,1)S(1)} async-done(((bf16[32,8,128]{2,1,0:T(8,128)(2,1)}), bf16[32,8,128]{2,1,0:T(8,128)(2,1)S(1)}, u32[]{:S(2)}, u32[]{:S(2)}) %all-to-all-start.1) | async-done | bytes 65568 | tf_op jit(solution)/shard_map/all_to_all | solution.py:383
  39.2 1.7 %shard_map.141 = (bf16[128,192]{1,0:T(8,128)(2,1)S(1)}, bf16[128,192]{1,0:T(8,128)(2,1)S(1)}, bf16[128,192]{1,0:T(8,128)(2,1)S(1)}, bf16[128,192]{1,0:T(8,128)(2...) custom-call(s32[1]{0:T(128)} %bitcast.idx, s32[1]{0:T(128)S(6)} %select_n.11.core, ...), custom_call_target="tpu_custom_call" | custom-call | flops 1 | bytes 1 | tf_op jit(solution)/shard_map/pallas_call | solution.py:82
  40.9 0.1 collective-permute-start.5
  41.0 1.2 %collective-permute-done.5.row_got = bf16[96,256]{1,0:T(8,128)(2,1)S(1)} collective-permute-done((bf16[96,256]{1,0:T(8,128)(2,1)S(1)}, bf16[96,256]{1,0:T(8,128)(2,1)S(1)}, u32[]{:S(2)}, u32[]{:S(2)}) %collective-permute-start.5) | collective-permute-done | bytes 49184 | tf_op jit(solution)/shard_map/ppermute | solution.py:388
  42.2 0.1 shard_map.142
  42.3 3.0 %collective-permute-start.9 = (bf16[320,256]{1,0:T(8,128)(2,1)S(1)}, bf16[320,256]{1,0:T(8,128)(2,1)S(1)}, u32[]{:S(2)}, u32[]{:S(2)}) collective-permute-start(bf16[320,256]{1,0:T(8,128)(2,1)S(1)} %get-tuple-element.65), channel_id=1, source_target_pairs={{0,6},{1,7},{2,4},{3,5},{4,2},{5,3},{6,0},{7,1},{8,14},{9,15},{10,... | collective-permute-start | bytes 491528 | tf_op jit(solution)/shard_map/ppermute | solution.py:388
  45.2 1.5 %collective-permute-start.11 = (bf16[320,256]{1,0:T(8,128)(2,1)S(1)}, bf16[320,256]{1,0:T(8,128)(2,1)S(1)}, u32[]{:S(2)}, u32[]{:S(2)}) collective-permute-start(bf16[320,256]{1,0:T(8,128)(2,1)S(1)} %get-tuple-element.67), channel_id=1, source_target_pairs={{0,2},{1,3},{2,0},{3,1},{4,6},{5,7},{6,4},{7,5},{8,10},{9,11},{10,... | collective-permute-start | bytes 491528 | tf_op jit(solution)/shard_map/ppermute | solution.py:388
  46.7 4.6 %collective-permute-done.9.refs_0_.refs_6_ = bf16[320,256]{1,0:T(8,128)(2,1)S(1)} collective-permute-done((bf16[320,256]{1,0:T(8,128)(2,1)S(1)}, bf16[320,256]{1,0:T(8,128)(2,1)S(1)}, u32[]{:S(2)}, u32[]{:S(2)}) %collective-permute-start.9) | collective-permute-done | bytes 163872 | tf_op jit(solution)/shard_map/ppermute | solution.py:388
  51.3 7.6 %collective-permute-done.10.refs_1_.refs_5_ = bf16[320,256]{1,0:T(8,128)(2,1)S(1)} collective-permute-done((bf16[320,256]{1,0:T(8,128)(2,1)S(1)}, bf16[320,256]{1,0:T(8,128)(2,1)S(1)}, u32[]{:S(2)}, u32[]{:S(2)}) %collective-permute-start.10) | collective-permute-done | bytes 163872 | tf_op jit(solution)/shard_map/ppermute | solution.py:388
  59.0 0.2 shard_map.143
  59.1 1.3 %collective-permute-start.12 = (bf16[384,256]{1,0:T(8,128)(2,1)S(1)}, bf16[384,256]{1,0:T(8,128)(2,1)S(1)}, u32[]{:S(2)}, u32[]{:S(2)}) collective-permute-start(bf16[384,256]{1,0:T(8,128)(2,1)S(1)} %get-tuple-element.72), channel_id=1, source_target_pairs={{0,24},{8,16},{16,8},{24,0},{1,25},{9,17},{17,9},{25,1},{2,26},{10... | collective-permute-start | bytes 589832 | tf_op jit(solution)/shard_map/ppermute | solution.py:388
  60.4 0.9 %collective-permute-start.13 = (bf16[384,256]{1,0:T(8,128)(2,1)S(1)}, bf16[384,256]{1,0:T(8,128)(2,1)S(1)}, u32[]{:S(2)}, u32[]{:S(2)}) collective-permute-start(bf16[384,256]{1,0:T(8,128)(2,1)S(1)} %get-tuple-element.73), channel_id=1, source_target_pairs={{0,16},{8,24},{16,0},{24,8},{1,17},{9,25},{17,1},{25,9},{2,18},{10... | collective-permute-start | bytes 589832 | tf_op jit(solution)/shard_map/ppermute | solution.py:388
  61.3 1.4 %collective-permute-start.14 = (bf16[384,256]{1,0:T(8,128)(2,1)S(1)}, bf16[384,256]{1,0:T(8,128)(2,1)S(1)}, u32[]{:S(2)}, u32[]{:S(2)}) collective-permute-start(bf16[384,256]{1,0:T(8,128)(2,1)S(1)} %get-tuple-element.74), channel_id=1, source_target_pairs={{0,8},{8,0},{16,24},{24,16},{1,9},{9,1},{17,25},{25,17},{2,10},{10... | collective-permute-start | bytes 589832 | tf_op jit(solution)/shard_map/ppermute | solution.py:388
  62.7 5.0 %collective-permute-done.12.refs_0_.refs_6_ = bf16[384,256]{1,0:T(8,128)(2,1)S(1)} collective-permute-done((bf16[384,256]{1,0:T(8,128)(2,1)S(1)}, bf16[384,256]{1,0:T(8,128)(2,1)S(1)}, u32[]{:S(2)}, u32[]{:S(2)}) %collective-permute-start.12) | collective-permute-done | bytes 196640 | tf_op jit(solution)/shard_map/ppermute | solution.py:388
  67.7 2.1 %collective-permute-done.13.refs_1_.refs_4_ = bf16[384,256]{1,0:T(8,128)(2,1)S(1)} collective-permute-done((bf16[384,256]{1,0:T(8,128)(2,1)S(1)}, bf16[384,256]{1,0:T(8,128)(2,1)S(1)}, u32[]{:S(2)}, u32[]{:S(2)}) %collective-permute-start.13) | collective-permute-done | bytes 196640 | tf_op jit(solution)/shard_map/ppermute | solution.py:388
  69.8 0.5 collective-permute-start.16
  70.3 1.0 %shard_map.144 = (bf16[128,256]{1,0:T(8,128)(2,1)}, bf16[128,256]{1,0:T(8,128)(2,1)}) custom-call(s32[1]{0:T(128)} %bitcast.idx, s32[1]{0:T(128)} %bitcast.1.hap, bf16[128,256]{1,0:T(8,128)(2,1)S(1)} %bitcast.18, f32[2,256]{1,0:T(2,128)S(1)} %pad_maximum_fusion.refs_5_.gain, bf16[768,256]{1,0:T(8,128)(2,1)S(1)} %bitcast.12, ...), custom_call_target="tpu_custom_call" | custom-call | flops 1 | bytes 1 | tf_op jit(solution)/shard_map/pallas_call | solution.py:82
  71.3 0.4 collective-permute-done.15.refs_1_
  71.7 2.1 %shard_map.145 = (f32[256,768]{1,0:T(8,128)}, f32[256,256]{1,0:T(8,128)}, f32[256,768]{1,0:T(8,128)}, f32[256,256]{1,0:T(8,128)}) custom-call(s32[1]{0:T(128)} %bitcast.idx, s32[1]{0:T(128)S(6)} %select_n.11.core, bf16[256,256]{1,0:T(8,128)(2,1)S(1)} %get-tuple-element.77.refs_0_, bf16[256,256]{1,0:T(8,128)(2,1)S(1)} %collective-permute-done.15.refs_1_, ...), custom_call_target="tpu_custom_call" | custom-call | flops 1 | bytes 1 | tf_op jit(solution)/shard_map/pallas_call | solution.py:82
  (32 shorter events, 0.1 us)
Async XLA Ops:
  0.6 7.3 %collective-permute-start.2 = (bf16[128,256]{1,0:T(8,128)(2,1)}, bf16[128,256]{1,0:T(8,128)(2,1)S(1)}, u32[]{:S(2)}, u32[]{:S(2)}) collective-permute-start(bf16[128,256]{1,0:T(8,128)(2,1)} %bitcast.14), channel_id=1, source_target_pairs={{0,24},{8,16},{16,8},{24,0},{1,25},{9,17},{17,9},{25,1},{2,26},{10... | collective-permute-start | bytes 196616 | tf_op jit(solution)/shard_map/ppermute | solution.py:388
  4.6 4.5 %collective-permute-start.1 = (bf16[128,256]{1,0:T(8,128)(2,1)}, bf16[128,256]{1,0:T(8,128)(2,1)S(1)}, u32[]{:S(2)}, u32[]{:S(2)}) collective-permute-start(bf16[128,256]{1,0:T(8,128)(2,1)} %bitcast.15), channel_id=1, source_target_pairs={{0,16},{8,24},{16,0},{24,8},{1,17},{9,25},{17,1},{25,9},{2,18},{10... | collective-permute-start | bytes 196616 | tf_op jit(solution)/shard_map/ppermute | solution.py:388
  5.1 4.5 %collective-permute-start = (bf16[128,256]{1,0:T(8,128)(2,1)}, bf16[128,256]{1,0:T(8,128)(2,1)S(1)}, u32[]{:S(2)}, u32[]{:S(2)}) collective-permute-start(bf16[128,256]{1,0:T(8,128)(2,1)} %bitcast.16), channel_id=1, source_target_pairs={{0,8},{8,0},{16,24},{24,16},{1,9},{9,1},{17,25},{25,17},{2,10},{10... | collective-permute-start | bytes 196616 | tf_op jit(solution)/shard_map/ppermute | solution.py:388
  5.2 0.7 copy-start.8
  5.9 0.9 %slice-start = ((bf16[256,768]{1,0:T(8,128)(2,1)}), bf16[256,512]{1,0:T(8,128)(2,1)S(1)}, s32[]{:S(2)}) async-start(bf16[256,768]{1,0:T(8,128)(2,1)} %col_proj.1), calls=%async_computation.2 | async-start | bytes 524288 | tf_op jit(solution)/shard_map/slice | solution.py:423
  5.9 1.1 %copy-start.7 = (bf16[256,768]{1,0:T(8,128)(2,1)S(1)}, bf16[256,768]{1,0:T(8,128)(2,1)}, u32[]{:S(2)}) copy-start(bf16[256,768]{1,0:T(8,128)(2,1)} %param.12) | copy-start | bytes 1179652
  7.0 0.7 copy-start.10
  7.0 2.5 %copy-start.1 = (bf16[256,256]{1,0:T(8,128)(2,1)S(1)}, bf16[256,256]{1,0:T(8,128)(2,1)}, u32[]{:S(2)}) copy-start(bf16[256,256]{1,0:T(8,128)(2,1)} %row_out.1) | copy-start | bytes 393220
  7.0 2.5 %copy-start.3 = (bf16[128,1,256]{2,0,1:T(8,128)(2,1)S(1)}, bf16[128,1,256]{2,0,1:T(8,128)(2,1)}, u32[]{:S(2)}) copy-start(bf16[128,1,256]{2,0,1:T(8,128)(2,1)} %param.9) | copy-start | bytes 196612
  7.1 2.5 %copy-start.6 = (bf16[128,1,256]{2,0,1:T(8,128)(2,1)S(1)}, bf16[128,1,256]{2,0,1:T(8,128)(2,1)}, u32[]{:S(2)}) copy-start(bf16[128,1,256]{2,0,1:T(8,128)(2,1)} %param.17) | copy-start | bytes 196612
  7.2 0.7 copy-start.9
  12.4 13.2 %all-to-all-start = ((bf16[8,16,768]{2,1,0:T(8,128)(2,1)}), bf16[8,16,768]{2,1,0:T(8,128)(2,1)S(1)}, u32[]{:S(2)}, u32[]{:S(2)}) async-start(bf16[8,16,768]{2,1,0:T(8,128)(2,1)} %get-tuple-element.44), calls=%async_computation | async-start | bytes 393216 | tf_op jit(solution)/shard_map/all_to_all | solution.py:383
  17.3 8.3 %copy-start = (bf16[256,768]{1,0:T(8,128)(2,1)S(1)}, bf16[256,768]{1,0:T(8,128)(2,1)}, u32[]{:S(2)}) copy-start(bf16[256,768]{1,0:T(8,128)(2,1)} %col_proj.1) | copy-start | bytes 1179652
  17.3 8.3 %copy-start.5 = (bf16[256,256]{1,0:T(8,128)(2,1)S(1)}, bf16[256,256]{1,0:T(8,128)(2,1)}, u32[]{:S(2)}) copy-start(bf16[256,256]{1,0:T(8,128)(2,1)} %col_out.1) | copy-start | bytes 393220
  28.9 2.8 %copy-start.4 = (bf16[8,16,512]{2,1,0:T(8,128)(2,1)S(1)}, bf16[8,16,512]{2,1,0:T(8,128)(2,1)}, u32[]{:S(2)}) copy-start(bf16[8,16,512]{2,1,0:T(8,128)(2,1)} %get-tuple-element.55.og) | copy-start | bytes 393220
  28.9 3.1 %collective-permute-start.3 = (bf16[128,1280]{1,0:T(8,128)(2,1)S(1)}, bf16[128,1280]{1,0:T(8,128)(2,1)S(1)}, u32[]{:S(2)}, u32[]{:S(2)}) collective-permute-start(bf16[128,1280]{1,0:T(8,128)(2,1)S(1)} %get-tuple-element.50), channel_id=1, source_target_pairs={{0,1},{1,0},{2,3},{3,2},{4,5},{5,4},{6,7},{7,6},{8,9},{9,8},{10,11... | collective-permute-start | bytes 983048 | tf_op jit(solution)/shard_map/ppermute | solution.py:388
  29.0 10.2 %all-to-all-start.1 = ((bf16[32,8,128]{2,1,0:T(8,128)(2,1)}), bf16[32,8,128]{2,1,0:T(8,128)(2,1)S(1)}, u32[]{:S(2)}, u32[]{:S(2)}) async-start(bf16[32,8,128]{2,1,0:T(8,128)(2,1)} %get-tuple-element.48), calls=%async_computation.1 | async-start | bytes 131072 | tf_op jit(solution)/shard_map/all_to_all | solution.py:383
  31.7 5.0 %collective-permute-start.4 = (bf16[4,16,512]{2,1,0:T(8,128)(2,1)S(1)}, bf16[4,16,512]{2,1,0:T(8,128)(2,1)S(1)}, u32[]{:S(2)}, u32[]{:S(2)}) collective-permute-start(bf16[4,16,512]{2,1,0:T(8,128)(2,1)S(1)} %get-tuple-element.56), channel_id=1, source_target_pairs={{0,1},{1,0},{2,3},{3,2},{4,5},{5,4},{6,7},{7,6},{8,9},{9,8},{10,11... | collective-permute-start | bytes 196616 | tf_op jit(solution)/shard_map/ppermute | solution.py:388
  32.0 1.0 %copy-start.2 = (bf16[128,1280]{1,0:T(8,128)(2,1)S(1)}, bf16[128,1280]{1,0:T(8,128)(2,1)}, u32[]{:S(2)}) copy-start(bf16[128,1280]{1,0:T(8,128)(2,1)} %get-tuple-element.49.keep) | copy-start | bytes 983044
  33.2 9.0 %collective-permute-start.6 = (bf16[32,1280]{1,0:T(8,128)(2,1)S(1)}, bf16[32,1280]{1,0:T(8,128)(2,1)S(1)}, u32[]{:S(2)}, u32[]{:S(2)}) collective-permute-start(bf16[32,1280]{1,0:T(8,128)(2,1)S(1)} %get-tuple-element.52), channel_id=1, source_target_pairs={{0,8},{8,0},{16,24},{24,16},{1,9},{9,1},{17,25},{25,17},{2,10},{10... | collective-permute-start | bytes 245768 | tf_op jit(solution)/shard_map/ppermute | solution.py:388
  34.9 7.3 %collective-permute-start.7 = (bf16[32,1280]{1,0:T(8,128)(2,1)S(1)}, bf16[32,1280]{1,0:T(8,128)(2,1)S(1)}, u32[]{:S(2)}, u32[]{:S(2)}) collective-permute-start(bf16[32,1280]{1,0:T(8,128)(2,1)S(1)} %get-tuple-element.53), channel_id=1, source_target_pairs={{0,16},{8,24},{16,0},{24,8},{1,17},{9,25},{17,1},{25,9},{2,18},{10... | collective-permute-start | bytes 245768 | tf_op jit(solution)/shard_map/ppermute | solution.py:388
  36.4 5.8 %collective-permute-start.8 = (bf16[32,1280]{1,0:T(8,128)(2,1)S(1)}, bf16[32,1280]{1,0:T(8,128)(2,1)S(1)}, u32[]{:S(2)}, u32[]{:S(2)}) collective-permute-start(bf16[32,1280]{1,0:T(8,128)(2,1)S(1)} %get-tuple-element.54), channel_id=1, source_target_pairs={{0,24},{8,16},{16,8},{24,0},{1,25},{9,17},{17,9},{25,1},{2,26},{10... | collective-permute-start | bytes 245768 | tf_op jit(solution)/shard_map/ppermute | solution.py:388
  40.9 1.3 %collective-permute-start.5 = (bf16[96,256]{1,0:T(8,128)(2,1)S(1)}, bf16[96,256]{1,0:T(8,128)(2,1)S(1)}, u32[]{:S(2)}, u32[]{:S(2)}) collective-permute-start(bf16[96,256]{1,0:T(8,128)(2,1)S(1)} %get-tuple-element.63), channel_id=1, source_target_pairs={{0,1},{1,0},{2,3},{3,2},{4,5},{5,4},{6,7},{7,6},{8,9},{9,8},{10,11... | collective-permute-start | bytes 147464 | tf_op jit(solution)/shard_map/ppermute | solution.py:388
  42.3 9.1 %collective-permute-start.9 = (bf16[320,256]{1,0:T(8,128)(2,1)S(1)}, bf16[320,256]{1,0:T(8,128)(2,1)S(1)}, u32[]{:S(2)}, u32[]{:S(2)}) collective-permute-start(bf16[320,256]{1,0:T(8,128)(2,1)S(1)} %get-tuple-element.65), channel_id=1, source_target_pairs={{0,6},{1,7},{2,4},{3,5},{4,2},{5,3},{6,0},{7,1},{8,14},{9,15},{10,... | collective-permute-start | bytes 491528 | tf_op jit(solution)/shard_map/ppermute | solution.py:388
  45.2 13.7 %collective-permute-start.10 = (bf16[320,256]{1,0:T(8,128)(2,1)S(1)}, bf16[320,256]{1,0:T(8,128)(2,1)S(1)}, u32[]{:S(2)}, u32[]{:S(2)}) collective-permute-start(bf16[320,256]{1,0:T(8,128)(2,1)S(1)} %get-tuple-element.66), channel_id=1, source_target_pairs={{0,4},{1,5},{2,6},{3,7},{4,0},{5,1},{6,2},{7,3},{8,12},{9,13},{10,... | collective-permute-start | bytes 491528 | tf_op jit(solution)/shard_map/ppermute | solution.py:388
  45.2 13.7 %collective-permute-start.11 = (bf16[320,256]{1,0:T(8,128)(2,1)S(1)}, bf16[320,256]{1,0:T(8,128)(2,1)S(1)}, u32[]{:S(2)}, u32[]{:S(2)}) collective-permute-start(bf16[320,256]{1,0:T(8,128)(2,1)S(1)} %get-tuple-element.67), channel_id=1, source_target_pairs={{0,2},{1,3},{2,0},{3,1},{4,6},{5,7},{6,4},{7,5},{8,10},{9,11},{10,... | collective-permute-start | bytes 491528 | tf_op jit(solution)/shard_map/ppermute | solution.py:388
  59.1 8.6 %collective-permute-start.12 = (bf16[384,256]{1,0:T(8,128)(2,1)S(1)}, bf16[384,256]{1,0:T(8,128)(2,1)S(1)}, u32[]{:S(2)}, u32[]{:S(2)}) collective-permute-start(bf16[384,256]{1,0:T(8,128)(2,1)S(1)} %get-tuple-element.72), channel_id=1, source_target_pairs={{0,24},{8,16},{16,8},{24,0},{1,25},{9,17},{17,9},{25,1},{2,26},{10... | collective-permute-start | bytes 589832 | tf_op jit(solution)/shard_map/ppermute | solution.py:388
  60.4 9.4 %collective-permute-start.13 = (bf16[384,256]{1,0:T(8,128)(2,1)S(1)}, bf16[384,256]{1,0:T(8,128)(2,1)S(1)}, u32[]{:S(2)}, u32[]{:S(2)}) collective-permute-start(bf16[384,256]{1,0:T(8,128)(2,1)S(1)} %get-tuple-element.73), channel_id=1, source_target_pairs={{0,16},{8,24},{16,0},{24,8},{1,17},{9,25},{17,1},{25,9},{2,18},{10... | collective-permute-start | bytes 589832 | tf_op jit(solution)/shard_map/ppermute | solution.py:388
  61.3 8.5 %collective-permute-start.14 = (bf16[384,256]{1,0:T(8,128)(2,1)S(1)}, bf16[384,256]{1,0:T(8,128)(2,1)S(1)}, u32[]{:S(2)}, u32[]{:S(2)}) collective-permute-start(bf16[384,256]{1,0:T(8,128)(2,1)S(1)} %get-tuple-element.74), channel_id=1, source_target_pairs={{0,8},{8,0},{16,24},{24,16},{1,9},{9,1},{17,25},{25,17},{2,10},{10... | collective-permute-start | bytes 589832 | tf_op jit(solution)/shard_map/ppermute | solution.py:388
  67.7 4.0 %collective-permute-start.18 = (bf16[384,256]{1,0:T(8,128)(2,1)S(1)}, bf16[384,256]{1,0:T(8,128)(2,1)S(1)}, u32[]{:S(2)}, u32[]{:S(2)}) collective-permute-start(bf16[384,256]{1,0:T(8,128)(2,1)S(1)} %collective-permute-done.12.refs_0_.refs_6_), channel_id=1, source_target_pairs={{0,1},{1,0},{2,3},{3,2},{4,5},{5,4},{6,7},{7,6},{8,9},{9,8},{10,11... | collective-permute-start | bytes 589832 | tf_op jit(solution)/shard_map/ppermute | solution.py:388
  69.8 1.9 %collective-permute-start.17 = (bf16[384,256]{1,0:T(8,128)(2,1)S(1)}, bf16[384,256]{1,0:T(8,128)(2,1)S(1)}, u32[]{:S(2)}, u32[]{:S(2)}) collective-permute-start(bf16[384,256]{1,0:T(8,128)(2,1)S(1)} %collective-permute-done.13.refs_1_.refs_4_), channel_id=1, source_target_pairs={{0,1},{1,0},{2,3},{3,2},{4,5},{5,4},{6,7},{7,6},{8,9},{9,8},{10,11... | collective-permute-start | bytes 589832 | tf_op jit(solution)/shard_map/ppermute | solution.py:388
  69.8 1.9 %collective-permute-start.16 = (bf16[384,256]{1,0:T(8,128)(2,1)S(1)}, bf16[384,256]{1,0:T(8,128)(2,1)S(1)}, u32[]{:S(2)}, u32[]{:S(2)}) collective-permute-start(bf16[384,256]{1,0:T(8,128)(2,1)S(1)} %collective-permute-done.14.refs_2_), channel_id=1, source_target_pairs={{0,1},{1,0},{2,3},{3,2},{4,5},{5,4},{6,7},{7,6},{8,9},{9,8},{10,11... | collective-permute-start | bytes 589832 | tf_op jit(solution)/shard_map/ppermute | solution.py:388
  70.3 1.4 %collective-permute-start.15 = (bf16[256,256]{1,0:T(8,128)(2,1)S(1)}, bf16[256,256]{1,0:T(8,128)(2,1)S(1)}, u32[]{:S(2)}, u32[]{:S(2)}) collective-permute-start(bf16[256,256]{1,0:T(8,128)(2,1)S(1)} %get-tuple-element.77.refs_0_), channel_id=1, source_target_pairs={{0,1},{1,0},{2,3},{3,2},{4,5},{5,4},{6,7},{7,6},{8,9},{9,8},{10,11... | collective-permute-start | bytes 393224 | tf_op jit(solution)/shard_map/ppermute | solution.py:388

commit v12 on v10

--- a/solution.py
+++ b/solution.py
@@ -178,8 +178,10 @@
     def save(j, cols):
         return pltpu.make_async_copy(w_all.at[mine, cols], keep.at[:, cols], sems.at[j])
 
+    def save_outputs(j, cols):
+        return pltpu.make_async_copy(og.at[:, :, cols], og_out.at[:, :, cols], sems.at[j])
+
     width = row_out.shape[0]
-    heads = width // HEAD_DIM
     group = width // sites
     x_all = flat_rows(x_in[...], F32)
     rows = x_all.shape[0]
@@ -217,26 +219,27 @@
     w_all[:, 3 * width : 4 * width] = mm(att_t.astype(BF16), cot).astype(BF16)
     att = jnp.transpose(att_t).astype(BF16)
     out = hid + mm(att, col_out[...])
+    og[:, :, :width] = out.reshape(haps, per, width).astype(BF16)
+    third = save_outputs(2, slice(0, width))
+    third.start()
     packed_grad = jnp.concatenate([dq * SCALE, dk * SCALE, dv], axis=1).astype(BF16)
     w_all[:, : 3 * width] = mm_tn(normed, packed_grad).astype(BF16)
     first = save(0, slice(0, 4 * width))
     first.start()
     grad_normed = mm_nt(packed_grad, col_proj[...])
     grad_hidden = (cot_f + norm_back(xhat, rstd, gain[1:2, :], grad_normed)).astype(BF16)
+    og[:, :, width:] = grad_hidden.astype(F32).reshape(haps, per, width).astype(BF16)
+    fourth = save_outputs(3, slice(width, 2 * width))
+    fourth.start()
+    w_all[:, 4 * width :] = mm_tn(row_att, grad_hidden).astype(BF16)
+    second = save(1, slice(4 * width, 5 * width))
+    second.start()
     for i in range(sites):
         g_i = mm_nt(grad_hidden, row_out[i * group : (i + 1) * group, :])
         ga_out[i * haps : (i + 1) * haps] = pack_block(g_i, haps)
-    w_all[:, 4 * width :] = mm_tn(row_att, grad_hidden).astype(BF16)
-    second = save(1, slice(4 * width, 5 * width))
-    second.start()
-    both = jnp.concatenate([out, grad_hidden.astype(F32)], axis=1)
-    og[...] = both.reshape(haps, per, 2 * width).astype(BF16)
-    third = pltpu.make_async_copy(og, og_out, sems.at[2])
-    third.start()
     send[...] = w_all[other, :]
-    first.wait()
-    second.wait()
-    third.wait()
+    for copy in (first, second, third, fourth):
+        copy.wait()
 
 
 def split_outputs(hap, og, keep, send):
@@ -439,7 +442,7 @@
         scratch=[
             pltpu.VMEM((haps, per, 2 * width), BF16),
             pltpu.VMEM((width, 5 * width), BF16),
-            pltpu.SemaphoreType.DMA((3,)),
+            pltpu.SemaphoreType.DMA((4,)),
         ],
     )
     g_in = exchange(ga, both_axes)
@@ -479,7 +482,9 @@
         *parts, *gps[1:],
     )
     got = [swapped(sends[k - 1], "site", k) for k in range(1, sites)]
-    full = [x for p in [mine] + got for x in (p, swapped(p, "hap", 1))]
+    mine_swapped = swapped(mine, "hap", 1)
+    got[0], mine_swapped = lax.optimization_barrier((got[0], mine_swapped))
+    full = [mine, mine_swapped] + [x for p in got for x in (p, swapped(p, "hap", 1))]
     out, grad = call(
         functools.partial(row_finish, sites, haps),
         [((rows, width), BF16)] * 2,

time: 72.2 us -> 72 us (level)
  transfers between devices with their start and end apart: 21 -> 21, of which waited for: 10 -> 11; matrix products, arithmetic and copies ran while one was open for 0% -> 0% of each run, Pallas kernels for 6% -> 6%
where the time goes in v12:
time: 72 us; the launch traced here: 71.7 us
  starting transfers between devices  31.7 us (44%)
  waiting for transfers between devices  23.1 us (32%)
  Pallas kernels  12.4 us (17%)
  local copies, waits for them, and re-layouts  3.62 us (5%)
  between operations  0.8 us (1%)
    ppermute x19, starting transfers between devices, swapped(): return lax.ppermute(value, axis, [(i, i ^ by) for i in range(length)])  21.1 us
    ppermute x19, waiting for transfers between devices, swapped(): return lax.ppermute(value, axis, [(i, i ^ by) for i in range(length)])  17.1 us
    pallas_call x10, Pallas kernels, call(): pl.pallas_call(body, out_shape=[jax.ShapeDtypeStruct(s, d) for s, d in ou...  12.4 us
    all_to_all x2, starting transfers between devices, exchange(): return lax.all_to_all(value, axis, 0, 0, tiled=True)  10.6 us
    all_to_all x2, waiting for transfers between devices, exchange(): return lax.all_to_all(value, axis, 0, 0, tiled=True)  6.05 us
    unnamed x24, local copies, waits for them, and re-layouts  2.67 us
  transfers between devices with their start and end apart: 21, of which 11 were waited for; matrix products, arithmetic and copies ran while one was open for 0% of the time, Pallas kernels for 6%

profile of v12, /device:TPU:9, one launch (start us, length us, event | category | flops | bytes accessed | tf_op | source)
XLA Modules:
  0.0 71.7 jit_solution(305359153630538025)
XLA Ops:
  0.6 2.2 %collective-permute-start.2 = (bf16[128,256]{1,0:T(8,128)(2,1)}, bf16[128,256]{1,0:T(8,128)(2,1)S(1)}, u32[]{:S(2)}, u32[]{:S(2)}) collective-permute-start(bf16[128,256]{1,0:T(8,128)(2,1)} %bitcast.14), channel_id=1, source_target_pairs={{0,24},{8,16},{16,8},{24,0},{1,25},{9,17},{17,9},{25,1},{2,26},{10... | collective-permute-start | bytes 196616 | tf_op jit(solution)/shard_map/ppermute | solution.py:378
  2.9 0.2 collective-permute-start.1
  3.1 0.3 collective-permute-start
  3.3 0.7 copy-done.8
  4.0 0.9 %slice-done = bf16[256,512]{1,0:T(8,128)(2,1)S(1)} async-done(((bf16[256,768]{1,0:T(8,128)(2,1)}), bf16[256,512]{1,0:T(8,128)(2,1)S(1)}, s32[]{:S(2)}) %slice-start) | async-done | bytes 262168 | tf_op jit(solution)/shard_map/slice | solution.py:413
  5.0 0.1 copy.17
  5.1 0.0 copy-start.10
  5.2 0.2 copy.15
  5.4 0.4 copy-done.10
  5.8 0.2 copy-done.9
  6.0 0.7 collective-permute-done.1.refs_2_
  6.8 0.1 collective-permute-done.refs_1_
  6.8 2.8 %shard_map.136 = (bf16[8,16,768]{2,1,0:T(8,128)(2,1)}, bf16[512,256]{1,0:T(8,128)(2,1)S(1)}) custom-call(s32[1]{0:T(128)} %bitcast.idx, s32[4,4]{1,0:T(4,128)S(1)} %compare_select_fusion.link, bf16[128,256]{1,0:T(8,128)(2,1)S(1)} %bitcast.17, bf16[128,256]{1,0:T(8,128)(2,1)S(1)} %collective-permute-done.refs_1_, ...), custom_call_target="tpu_custom_call" | custom-call | flops 1 | bytes 1 | tf_op jit(solution)/shard_map/pallas_call | solution.py:82
  9.7 6.9 %all-to-all-start = ((bf16[8,16,768]{2,1,0:T(8,128)(2,1)}), bf16[8,16,768]{2,1,0:T(8,128)(2,1)S(1)}, u32[]{:S(2)}, u32[]{:S(2)}) async-start(bf16[8,16,768]{2,1,0:T(8,128)(2,1)} %get-tuple-element.46), calls=%async_computation | async-start | bytes 393216 | tf_op jit(solution)/shard_map/all_to_all | solution.py:373
  16.6 1.8 %shard_map.137 = (bf16[512,1024]{1,0:T(8,128)(2,1)S(1)}, bf16[512,64]{1,0:T(8,128)(2,1)S(1)}, bf16[512,64]{1,0:T(8,128)(2,1)S(1)}, bf16[64,512]{1,0:T(8,128)(2,1)S(1)}) custom-call(s32[1]{0:T(128)} %bitcast.idx, s32[4,4]{1,0:T(4,128)S(1)} %compare_select_fusion.link, bf16[512,256]{1,0:T(8,128)(2,1)S(1)} %get-tuple-element.47.normed_ref.normed, ...), custom_call_target="tpu_custom_call" | custom-call | flops 20000000000 | bytes 72000000 | tf_op jit(solution)/shard_map/pallas_call | solution.py:82
  18.4 4.3 %all-to-all-done.x_in = bf16[8,16,768]{2,1,0:T(8,128)(2,1)S(1)} async-done(((bf16[8,16,768]{2,1,0:T(8,128)(2,1)}), bf16[8,16,768]{2,1,0:T(8,128)(2,1)S(1)}, u32[]{:S(2)}, u32[]{:S(2)}) %all-to-all-start) | async-done | bytes 196640 | tf_op jit(solution)/shard_map/all_to_all | solution.py:373
  22.8 3.2 %shard_map.138 = (bf16[32,8,128]{2,1,0:T(8,128)(2,1)}, bf16[128,1280]{1,0:T(8,128)(2,1)S(1)}, bf16[128,1280]{1,0:T(8,128)(2,1)}, bf16[8,16,512]{2,1,0:T(8,128)(2,1)}) custom-call(s32[1]{0:T(128)} %bitcast.1.hap, bf16[8,16,768]{2,1,0:T(8,128)(2,1)S(1)} %all-to-all-done.x_in, bf16[256,256]{1,0:T(8,128)(2,1)S(1)} %copy-done.1, ...), custom_call_target="tpu_custom_call" | custom-call | flops 1 | bytes 1 | tf_op jit(solution)/shard_map/pallas_call | solution.py:82
  26.0 1.0 %collective-permute-start.3 = (bf16[128,1280]{1,0:T(8,128)(2,1)S(1)}, bf16[128,1280]{1,0:T(8,128)(2,1)S(1)}, u32[]{:S(2)}, u32[]{:S(2)}) collective-permute-start(bf16[128,1280]{1,0:T(8,128)(2,1)S(1)} %get-tuple-element.52), channel_id=1, source_target_pairs={{0,1},{1,0},{2,3},{3,2},{4,5},{5,4},{6,7},{7,6},{8,9},{9,8},{10,11... | collective-permute-start | bytes 983048 | tf_op jit(solution)/shard_map/ppermute | solution.py:378
  27.0 3.7 %all-to-all-start.1 = ((bf16[32,8,128]{2,1,0:T(8,128)(2,1)}), bf16[32,8,128]{2,1,0:T(8,128)(2,1)S(1)}, u32[]{:S(2)}, u32[]{:S(2)}) async-start(bf16[32,8,128]{2,1,0:T(8,128)(2,1)} %get-tuple-element.50), calls=%async_computation.1 | async-start | bytes 131072 | tf_op jit(solution)/shard_map/all_to_all | solution.py:373
  30.8 0.4 collective-permute-start.4
  31.2 1.0 %copy-done.2 = bf16[128,1280]{1,0:T(8,128)(2,1)S(1)} copy-done((bf16[128,1280]{1,0:T(8,128)(2,1)S(1)}, bf16[128,1280]{1,0:T(8,128)(2,1)}, u32[]{:S(2)}) %copy-start.2) | copy-done | bytes 327704
  32.2 0.2 shard_map.139
  32.3 1.2 %collective-permute-start.6 = (bf16[32,1280]{1,0:T(8,128)(2,1)S(1)}, bf16[32,1280]{1,0:T(8,128)(2,1)S(1)}, u32[]{:S(2)}, u32[]{:S(2)}) collective-permute-start(bf16[32,1280]{1,0:T(8,128)(2,1)S(1)} %get-tuple-element.54), channel_id=1, source_target_pairs={{0,8},{8,0},{16,24},{24,16},{1,9},{9,1},{17,25},{25,17},{2,10},{10... | collective-permute-start | bytes 245768 | tf_op jit(solution)/shard_map/ppermute | solution.py:378
  33.6 1.2 %collective-permute-start.7 = (bf16[32,1280]{1,0:T(8,128)(2,1)S(1)}, bf16[32,1280]{1,0:T(8,128)(2,1)S(1)}, u32[]{:S(2)}, u32[]{:S(2)}) collective-permute-start(bf16[32,1280]{1,0:T(8,128)(2,1)S(1)} %get-tuple-element.55), channel_id=1, source_target_pairs={{0,16},{8,24},{16,0},{24,8},{1,17},{9,25},{17,1},{25,9},{2,18},{10... | collective-permute-start | bytes 245768 | tf_op jit(solution)/shard_map/ppermute | solution.py:378
  34.8 0.3 collective-permute-start.8
  35.1 1.7 %all-to-all-done.1.g_in = bf16[32,8,128]{2,1,0:T(8,128)(2,1)S(1)} async-done(((bf16[32,8,128]{2,1,0:T(8,128)(2,1)}), bf16[32,8,128]{2,1,0:T(8,128)(2,1)S(1)}, u32[]{:S(2)}, u32[]{:S(2)}) %all-to-all-start.1) | async-done | bytes 65568 | tf_op jit(solution)/shard_map/all_to_all | solution.py:373
  36.8 1.7 %shard_map.141 = (bf16[128,192]{1,0:T(8,128)(2,1)S(1)}, bf16[128,192]{1,0:T(8,128)(2,1)S(1)}, bf16[128,192]{1,0:T(8,128)(2,1)S(1)}, bf16[128,192]{1,0:T(8,128)(2...) custom-call(s32[1]{0:T(128)} %bitcast.idx, s32[1]{0:T(128)S(6)} %select_n.11.core, ...), custom_call_target="tpu_custom_call" | custom-call | flops 1 | bytes 1 | tf_op jit(solution)/shard_map/pallas_call | solution.py:82
  38.5 0.5 collective-permute-start.5
  38.9 0.9 %collective-permute-done.5.row_got = bf16[96,256]{1,0:T(8,128)(2,1)S(1)} collective-permute-done((bf16[96,256]{1,0:T(8,128)(2,1)S(1)}, bf16[96,256]{1,0:T(8,128)(2,1)S(1)}, u32[]{:S(2)}, u32[]{:S(2)}) %collective-permute-start.5) | collective-permute-done | bytes 49184 | tf_op jit(solution)/shard_map/ppermute | solution.py:378
  39.8 0.1 shard_map.142
  39.9 1.5 %collective-permute-start.9 = (bf16[320,256]{1,0:T(8,128)(2,1)S(1)}, bf16[320,256]{1,0:T(8,128)(2,1)S(1)}, u32[]{:S(2)}, u32[]{:S(2)}) collective-permute-start(bf16[320,256]{1,0:T(8,128)(2,1)S(1)} %get-tuple-element.68), channel_id=1, source_target_pairs={{0,2},{1,3},{2,0},{3,1},{4,6},{5,7},{6,4},{7,5},{8,10},{9,11},{10,... | collective-permute-start | bytes 491528 | tf_op jit(solution)/shard_map/ppermute | solution.py:378
  41.4 0.1 collective-permute-start.10
  41.5 1.1 %collective-permute-start.11 = (bf16[320,256]{1,0:T(8,128)(2,1)S(1)}, bf16[320,256]{1,0:T(8,128)(2,1)S(1)}, u32[]{:S(2)}, u32[]{:S(2)}) collective-permute-start(bf16[320,256]{1,0:T(8,128)(2,1)S(1)} %get-tuple-element.70), channel_id=1, source_target_pairs={{0,6},{1,7},{2,4},{3,5},{4,2},{5,3},{6,0},{7,1},{8,14},{9,15},{10,... | collective-permute-start | bytes 491528 | tf_op jit(solution)/shard_map/ppermute | solution.py:378
  42.6 4.0 %collective-permute-done.9.refs_1_.refs_4_ = bf16[320,256]{1,0:T(8,128)(2,1)S(1)} collective-permute-done((bf16[320,256]{1,0:T(8,128)(2,1)S(1)}, bf16[320,256]{1,0:T(8,128)(2,1)S(1)}, u32[]{:S(2)}, u32[]{:S(2)}) %collective-permute-start.9) | collective-permute-done | bytes 163872 | tf_op jit(solution)/shard_map/ppermute | solution.py:378
  46.6 1.5 %collective-permute-done.10.refs_2_.refs_5_ = bf16[320,256]{1,0:T(8,128)(2,1)S(1)} collective-permute-done((bf16[320,256]{1,0:T(8,128)(2,1)S(1)}, bf16[320,256]{1,0:T(8,128)(2,1)S(1)}, u32[]{:S(2)}, u32[]{:S(2)}) %collective-permute-start.10) | collective-permute-done | bytes 163872 | tf_op jit(solution)/shard_map/ppermute | solution.py:378
  48.1 8.5 %collective-permute-done.11.refs_3_.refs_6_ = bf16[320,256]{1,0:T(8,128)(2,1)S(1)} collective-permute-done((bf16[320,256]{1,0:T(8,128)(2,1)S(1)}, bf16[320,256]{1,0:T(8,128)(2,1)S(1)}, u32[]{:S(2)}, u32[]{:S(2)}) %collective-permute-start.11) | collective-permute-done | bytes 163872 | tf_op jit(solution)/shard_map/ppermute | solution.py:378
  56.6 0.2 shard_map.143
  56.7 0.3 collective-permute-start.12
  57.1 1.1 %collective-permute-start.14 = (bf16[384,256]{1,0:T(8,128)(2,1)S(1)}, bf16[384,256]{1,0:T(8,128)(2,1)S(1)}, u32[]{:S(2)}, u32[]{:S(2)}) collective-permute-start(bf16[384,256]{1,0:T(8,128)(2,1)S(1)} %get-tuple-element.77), channel_id=1, source_target_pairs={{0,16},{8,24},{16,0},{24,8},{1,17},{9,25},{17,1},{25,9},{2,18},{10... | collective-permute-start | bytes 589832 | tf_op jit(solution)/shard_map/ppermute | solution.py:378
  58.1 1.3 %collective-permute-start.15 = (bf16[384,256]{1,0:T(8,128)(2,1)S(1)}, bf16[384,256]{1,0:T(8,128)(2,1)S(1)}, u32[]{:S(2)}, u32[]{:S(2)}) collective-permute-start(bf16[384,256]{1,0:T(8,128)(2,1)S(1)} %get-tuple-element.78), channel_id=1, source_target_pairs={{0,24},{8,16},{16,8},{24,0},{1,25},{9,17},{17,9},{25,1},{2,26},{10... | collective-permute-start | bytes 589832 | tf_op jit(solution)/shard_map/ppermute | solution.py:378
  59.5 2.6 %collective-permute-start.13 = (bf16[256,256]{1,0:T(8,128)(2,1)S(1)}, bf16[256,256]{1,0:T(8,128)(2,1)S(1)}, u32[]{:S(2)}, u32[]{:S(2)}) collective-permute-start(bf16[256,256]{1,0:T(8,128)(2,1)S(1)} %get-tuple-element.75.refs_0_), channel_id=1, source_target_pairs={{0,1},{1,0},{2,3},{3,2},{4,5},{5,4},{6,7},{7,6},{8,9},{9,8},{10,11... | collective-permute-start | bytes 393224 | tf_op jit(solution)/shard_map/ppermute | solution.py:378
  62.1 1.0 %collective-permute-done.13.refs_1_ = bf16[256,256]{1,0:T(8,128)(2,1)S(1)} collective-permute-done((bf16[256,256]{1,0:T(8,128)(2,1)S(1)}, bf16[256,256]{1,0:T(8,128)(2,1)S(1)}, u32[]{:S(2)}, u32[]{:S(2)}) %collective-permute-start.13) | collective-permute-done | bytes 131104 | tf_op jit(solution)/shard_map/ppermute | solution.py:378
  63.1 3.2 %collective-permute-start.16 = (bf16[384,256]{1,0:T(8,128)(2,1)S(1)}, bf16[384,256]{1,0:T(8,128)(2,1)S(1)}, u32[]{:S(2)}, u32[]{:S(2)}) collective-permute-start(bf16[384,256]{1,0:T(8,128)(2,1)S(1)} %collective-permute-done.12.refs_0_.refs_2_), channel_id=1, source_target_pairs={{0,1},{1,0},{2,3},{3,2},{4,5},{5,4},{6,7},{7,6},{8,9},{9,8},{10,11... | collective-permute-start | bytes 589832 | tf_op jit(solution)/shard_map/ppermute | solution.py:378
  66.2 2.5 %collective-permute-start.17 = (bf16[384,256]{1,0:T(8,128)(2,1)S(1)}, bf16[384,256]{1,0:T(8,128)(2,1)S(1)}, u32[]{:S(2)}, u32[]{:S(2)}) collective-permute-start(bf16[384,256]{1,0:T(8,128)(2,1)S(1)} %collective-permute-done.14.refs_1_.refs_4_), channel_id=1, source_target_pairs={{0,1},{1,0},{2,3},{3,2},{4,5},{5,4},{6,7},{7,6},{8,9},{9,8},{10,11... | collective-permute-start | bytes 589832 | tf_op jit(solution)/shard_map/ppermute | solution.py:378
  68.8 1.0 %shard_map.144 = (bf16[128,256]{1,0:T(8,128)(2,1)}, bf16[128,256]{1,0:T(8,128)(2,1)}) custom-call(s32[1]{0:T(128)} %bitcast.idx, s32[1]{0:T(128)} %bitcast.1.hap, bf16[128,256]{1,0:T(8,128)(2,1)S(1)} %bitcast.18, f32[2,256]{1,0:T(2,128)S(1)} %pad_maximum_fusion.refs_5_.gain, bf16[768,256]{1,0:T(8,128)(2,1)S(1)} %bitcast.12, ...), custom_call_target="tpu_custom_call" | custom-call | flops 1 | bytes 1 | tf_op jit(solution)/shard_map/pallas_call | solution.py:82
  69.7 0.1 collective-permute-done.17.refs_5_
  69.8 0.4 collective-permute-done.18.refs_7_
  70.2 1.5 %shard_map.145 = (f32[256,768]{1,0:T(8,128)}, f32[256,256]{1,0:T(8,128)}, f32[256,768]{1,0:T(8,128)}, f32[256,256]{1,0:T(8,128)}) custom-call(s32[1]{0:T(128)} %bitcast.idx, s32[1]{0:T(128)S(6)} %select_n.11.core, bf16[256,256]{1,0:T(8,128)(2,1)S(1)} %get-tuple-element.75.refs_0_, bf16[256,256]{1,0:T(8,128)(2,1)S(1)} %collective-permute-done.13.refs_1_, ...), custom_call_target="tpu_custom_call" | custom-call | flops 1 | bytes 1 | tf_op jit(solution)/shard_map/pallas_call | solution.py:82
  (32 shorter events, 0.1 us)
Async XLA Ops:
  0.6 5.4 %collective-permute-start.2 = (bf16[128,256]{1,0:T(8,128)(2,1)}, bf16[128,256]{1,0:T(8,128)(2,1)S(1)}, u32[]{:S(2)}, u32[]{:S(2)}) collective-permute-start(bf16[128,256]{1,0:T(8,128)(2,1)} %bitcast.14), channel_id=1, source_target_pairs={{0,24},{8,16},{16,8},{24,0},{1,25},{9,17},{17,9},{25,1},{2,26},{10... | collective-permute-start | bytes 196616 | tf_op jit(solution)/shard_map/ppermute | solution.py:378
  2.9 3.9 %collective-permute-start.1 = (bf16[128,256]{1,0:T(8,128)(2,1)}, bf16[128,256]{1,0:T(8,128)(2,1)S(1)}, u32[]{:S(2)}, u32[]{:S(2)}) collective-permute-start(bf16[128,256]{1,0:T(8,128)(2,1)} %bitcast.15), channel_id=1, source_target_pairs={{0,16},{8,24},{16,0},{24,8},{1,17},{9,25},{17,1},{25,9},{2,18},{10... | collective-permute-start | bytes 196616 | tf_op jit(solution)/shard_map/ppermute | solution.py:378
  3.1 3.7 %collective-permute-start = (bf16[128,256]{1,0:T(8,128)(2,1)}, bf16[128,256]{1,0:T(8,128)(2,1)S(1)}, u32[]{:S(2)}, u32[]{:S(2)}) collective-permute-start(bf16[128,256]{1,0:T(8,128)(2,1)} %bitcast.16), channel_id=1, source_target_pairs={{0,8},{8,0},{16,24},{24,16},{1,9},{9,1},{17,25},{25,17},{2,10},{10... | collective-permute-start | bytes 196616 | tf_op jit(solution)/shard_map/ppermute | solution.py:378
  3.3 0.7 copy-start.8
  4.0 0.9 %slice-start = ((bf16[256,768]{1,0:T(8,128)(2,1)}), bf16[256,512]{1,0:T(8,128)(2,1)S(1)}, s32[]{:S(2)}) async-start(bf16[256,768]{1,0:T(8,128)(2,1)} %col_proj.1), calls=%async_computation.2 | async-start | bytes 524288 | tf_op jit(solution)/shard_map/slice | solution.py:413
  4.0 1.1 %copy-start.7 = (bf16[256,768]{1,0:T(8,128)(2,1)S(1)}, bf16[256,768]{1,0:T(8,128)(2,1)}, u32[]{:S(2)}) copy-start(bf16[256,768]{1,0:T(8,128)(2,1)} %param.12) | copy-start | bytes 1179652
  5.1 0.7 copy-start.10
  5.1 1.7 %copy-start.1 = (bf16[256,256]{1,0:T(8,128)(2,1)S(1)}, bf16[256,256]{1,0:T(8,128)(2,1)}, u32[]{:S(2)}) copy-start(bf16[256,256]{1,0:T(8,128)(2,1)} %row_out.1) | copy-start | bytes 393220
  5.2 1.7 %copy-start.3 = (bf16[128,1,256]{2,0,1:T(8,128)(2,1)S(1)}, bf16[128,1,256]{2,0,1:T(8,128)(2,1)}, u32[]{:S(2)}) copy-start(bf16[128,1,256]{2,0,1:T(8,128)(2,1)} %param.9) | copy-start | bytes 196612
  5.2 1.7 %copy-start.6 = (bf16[128,1,256]{2,0,1:T(8,128)(2,1)S(1)}, bf16[128,1,256]{2,0,1:T(8,128)(2,1)}, u32[]{:S(2)}) copy-start(bf16[128,1,256]{2,0,1:T(8,128)(2,1)} %param.17) | copy-start | bytes 196612
  5.4 0.7 copy-start.9
  9.7 13.1 %all-to-all-start = ((bf16[8,16,768]{2,1,0:T(8,128)(2,1)}), bf16[8,16,768]{2,1,0:T(8,128)(2,1)S(1)}, u32[]{:S(2)}, u32[]{:S(2)}) async-start(bf16[8,16,768]{2,1,0:T(8,128)(2,1)} %get-tuple-element.46), calls=%async_computation | async-start | bytes 393216 | tf_op jit(solution)/shard_map/all_to_all | solution.py:373
  16.6 6.1 %copy-start = (bf16[256,768]{1,0:T(8,128)(2,1)S(1)}, bf16[256,768]{1,0:T(8,128)(2,1)}, u32[]{:S(2)}) copy-start(bf16[256,768]{1,0:T(8,128)(2,1)} %col_proj.1) | copy-start | bytes 1179652
  16.6 6.1 %copy-start.5 = (bf16[256,256]{1,0:T(8,128)(2,1)S(1)}, bf16[256,256]{1,0:T(8,128)(2,1)}, u32[]{:S(2)}) copy-start(bf16[256,256]{1,0:T(8,128)(2,1)} %col_out.1) | copy-start | bytes 393220
  26.0 4.7 %copy-start.4 = (bf16[8,16,512]{2,1,0:T(8,128)(2,1)S(1)}, bf16[8,16,512]{2,1,0:T(8,128)(2,1)}, u32[]{:S(2)}) copy-start(bf16[8,16,512]{2,1,0:T(8,128)(2,1)} %get-tuple-element.57.og) | copy-start | bytes 393220
  26.0 5.2 %collective-permute-start.3 = (bf16[128,1280]{1,0:T(8,128)(2,1)S(1)}, bf16[128,1280]{1,0:T(8,128)(2,1)S(1)}, u32[]{:S(2)}, u32[]{:S(2)}) collective-permute-start(bf16[128,1280]{1,0:T(8,128)(2,1)S(1)} %get-tuple-element.52), channel_id=1, source_target_pairs={{0,1},{1,0},{2,3},{3,2},{4,5},{5,4},{6,7},{7,6},{8,9},{9,8},{10,11... | collective-permute-start | bytes 983048 | tf_op jit(solution)/shard_map/ppermute | solution.py:378
  27.0 9.7 %all-to-all-start.1 = ((bf16[32,8,128]{2,1,0:T(8,128)(2,1)}), bf16[32,8,128]{2,1,0:T(8,128)(2,1)S(1)}, u32[]{:S(2)}, u32[]{:S(2)}) async-start(bf16[32,8,128]{2,1,0:T(8,128)(2,1)} %get-tuple-element.50), calls=%async_computation.1 | async-start | bytes 131072 | tf_op jit(solution)/shard_map/all_to_all | solution.py:373
  30.8 4.3 %collective-permute-start.4 = (bf16[4,16,512]{2,1,0:T(8,128)(2,1)S(1)}, bf16[4,16,512]{2,1,0:T(8,128)(2,1)S(1)}, u32[]{:S(2)}, u32[]{:S(2)}) collective-permute-start(bf16[4,16,512]{2,1,0:T(8,128)(2,1)S(1)} %get-tuple-element.58), channel_id=1, source_target_pairs={{0,1},{1,0},{2,3},{3,2},{4,5},{5,4},{6,7},{7,6},{8,9},{9,8},{10,11... | collective-permute-start | bytes 196616 | tf_op jit(solution)/shard_map/ppermute | solution.py:378
  31.2 1.0 %copy-start.2 = (bf16[128,1280]{1,0:T(8,128)(2,1)S(1)}, bf16[128,1280]{1,0:T(8,128)(2,1)}, u32[]{:S(2)}) copy-start(bf16[128,1280]{1,0:T(8,128)(2,1)} %get-tuple-element.51.keep) | copy-start | bytes 983044
  32.3 7.5 %collective-permute-start.6 = (bf16[32,1280]{1,0:T(8,128)(2,1)S(1)}, bf16[32,1280]{1,0:T(8,128)(2,1)S(1)}, u32[]{:S(2)}, u32[]{:S(2)}) collective-permute-start(bf16[32,1280]{1,0:T(8,128)(2,1)S(1)} %get-tuple-element.54), channel_id=1, source_target_pairs={{0,8},{8,0},{16,24},{24,16},{1,9},{9,1},{17,25},{25,17},{2,10},{10... | collective-permute-start | bytes 245768 | tf_op jit(solution)/shard_map/ppermute | solution.py:378
  33.6 6.2 %collective-permute-start.7 = (bf16[32,1280]{1,0:T(8,128)(2,1)S(1)}, bf16[32,1280]{1,0:T(8,128)(2,1)S(1)}, u32[]{:S(2)}, u32[]{:S(2)}) collective-permute-start(bf16[32,1280]{1,0:T(8,128)(2,1)S(1)} %get-tuple-element.55), channel_id=1, source_target_pairs={{0,16},{8,24},{16,0},{24,8},{1,17},{9,25},{17,1},{25,9},{2,18},{10... | collective-permute-start | bytes 245768 | tf_op jit(solution)/shard_map/ppermute | solution.py:378
  34.8 5.1 %collective-permute-start.8 = (bf16[32,1280]{1,0:T(8,128)(2,1)S(1)}, bf16[32,1280]{1,0:T(8,128)(2,1)S(1)}, u32[]{:S(2)}, u32[]{:S(2)}) collective-permute-start(bf16[32,1280]{1,0:T(8,128)(2,1)S(1)} %get-tuple-element.56), channel_id=1, source_target_pairs={{0,24},{8,16},{16,8},{24,0},{1,25},{9,17},{17,9},{25,1},{2,26},{10... | collective-permute-start | bytes 245768 | tf_op jit(solution)/shard_map/ppermute | solution.py:378
  38.5 1.4 %collective-permute-start.5 = (bf16[96,256]{1,0:T(8,128)(2,1)S(1)}, bf16[96,256]{1,0:T(8,128)(2,1)S(1)}, u32[]{:S(2)}, u32[]{:S(2)}) collective-permute-start(bf16[96,256]{1,0:T(8,128)(2,1)S(1)} %get-tuple-element.65), channel_id=1, source_target_pairs={{0,1},{1,0},{2,3},{3,2},{4,5},{5,4},{6,7},{7,6},{8,9},{9,8},{10,11... | collective-permute-start | bytes 147464 | tf_op jit(solution)/shard_map/ppermute | solution.py:378
  39.9 6.7 %collective-permute-start.9 = (bf16[320,256]{1,0:T(8,128)(2,1)S(1)}, bf16[320,256]{1,0:T(8,128)(2,1)S(1)}, u32[]{:S(2)}, u32[]{:S(2)}) collective-permute-start(bf16[320,256]{1,0:T(8,128)(2,1)S(1)} %get-tuple-element.68), channel_id=1, source_target_pairs={{0,2},{1,3},{2,0},{3,1},{4,6},{5,7},{6,4},{7,5},{8,10},{9,11},{10,... | collective-permute-start | bytes 491528 | tf_op jit(solution)/shard_map/ppermute | solution.py:378
  41.4 6.7 %collective-permute-start.10 = (bf16[320,256]{1,0:T(8,128)(2,1)S(1)}, bf16[320,256]{1,0:T(8,128)(2,1)S(1)}, u32[]{:S(2)}, u32[]{:S(2)}) collective-permute-start(bf16[320,256]{1,0:T(8,128)(2,1)S(1)} %get-tuple-element.69), channel_id=1, source_target_pairs={{0,4},{1,5},{2,6},{3,7},{4,0},{5,1},{6,2},{7,3},{8,12},{9,13},{10,... | collective-permute-start | bytes 491528 | tf_op jit(solution)/shard_map/ppermute | solution.py:378
  41.5 15.1 %collective-permute-start.11 = (bf16[320,256]{1,0:T(8,128)(2,1)S(1)}, bf16[320,256]{1,0:T(8,128)(2,1)S(1)}, u32[]{:S(2)}, u32[]{:S(2)}) collective-permute-start(bf16[320,256]{1,0:T(8,128)(2,1)S(1)} %get-tuple-element.70), channel_id=1, source_target_pairs={{0,6},{1,7},{2,4},{3,5},{4,2},{5,3},{6,0},{7,1},{8,14},{9,15},{10,... | collective-permute-start | bytes 491528 | tf_op jit(solution)/shard_map/ppermute | solution.py:378
  56.7 6.3 %collective-permute-start.12 = (bf16[384,256]{1,0:T(8,128)(2,1)S(1)}, bf16[384,256]{1,0:T(8,128)(2,1)S(1)}, u32[]{:S(2)}, u32[]{:S(2)}) collective-permute-start(bf16[384,256]{1,0:T(8,128)(2,1)S(1)} %get-tuple-element.74), channel_id=1, source_target_pairs={{0,8},{8,0},{16,24},{24,16},{1,9},{9,1},{17,25},{25,17},{2,10},{10... | collective-permute-start | bytes 589832 | tf_op jit(solution)/shard_map/ppermute | solution.py:378
  57.1 9.2 %collective-permute-start.14 = (bf16[384,256]{1,0:T(8,128)(2,1)S(1)}, bf16[384,256]{1,0:T(8,128)(2,1)S(1)}, u32[]{:S(2)}, u32[]{:S(2)}) collective-permute-start(bf16[384,256]{1,0:T(8,128)(2,1)S(1)} %get-tuple-element.77), channel_id=1, source_target_pairs={{0,16},{8,24},{16,0},{24,8},{1,17},{9,25},{17,1},{25,9},{2,18},{10... | collective-permute-start | bytes 589832 | tf_op jit(solution)/shard_map/ppermute | solution.py:378
  58.1 10.6 %collective-permute-start.15 = (bf16[384,256]{1,0:T(8,128)(2,1)S(1)}, bf16[384,256]{1,0:T(8,128)(2,1)S(1)}, u32[]{:S(2)}, u32[]{:S(2)}) collective-permute-start(bf16[384,256]{1,0:T(8,128)(2,1)S(1)} %get-tuple-element.78), channel_id=1, source_target_pairs={{0,24},{8,16},{16,8},{24,0},{1,25},{9,17},{17,9},{25,1},{2,26},{10... | collective-permute-start | bytes 589832 | tf_op jit(solution)/shard_map/ppermute | solution.py:378
  59.5 3.6 %collective-permute-start.13 = (bf16[256,256]{1,0:T(8,128)(2,1)S(1)}, bf16[256,256]{1,0:T(8,128)(2,1)S(1)}, u32[]{:S(2)}, u32[]{:S(2)}) collective-permute-start(bf16[256,256]{1,0:T(8,128)(2,1)S(1)} %get-tuple-element.75.refs_0_), channel_id=1, source_target_pairs={{0,1},{1,0},{2,3},{3,2},{4,5},{5,4},{6,7},{7,6},{8,9},{9,8},{10,11... | collective-permute-start | bytes 393224 | tf_op jit(solution)/shard_map/ppermute | solution.py:378
  63.1 6.6 %collective-permute-start.16 = (bf16[384,256]{1,0:T(8,128)(2,1)S(1)}, bf16[384,256]{1,0:T(8,128)(2,1)S(1)}, u32[]{:S(2)}, u32[]{:S(2)}) collective-permute-start(bf16[384,256]{1,0:T(8,128)(2,1)S(1)} %collective-permute-done.12.refs_0_.refs_2_), channel_id=1, source_target_pairs={{0,1},{1,0},{2,3},{3,2},{4,5},{5,4},{6,7},{7,6},{8,9},{9,8},{10,11... | collective-permute-start | bytes 589832 | tf_op jit(solution)/shard_map/ppermute | solution.py:378
  66.2 3.6 %collective-permute-start.17 = (bf16[384,256]{1,0:T(8,128)(2,1)S(1)}, bf16[384,256]{1,0:T(8,128)(2,1)S(1)}, u32[]{:S(2)}, u32[]{:S(2)}) collective-permute-start(bf16[384,256]{1,0:T(8,128)(2,1)S(1)} %collective-permute-done.14.refs_1_.refs_4_), channel_id=1, source_target_pairs={{0,1},{1,0},{2,3},{3,2},{4,5},{5,4},{6,7},{7,6},{8,9},{9,8},{10,11... | collective-permute-start | bytes 589832 | tf_op jit(solution)/shard_map/ppermute | solution.py:378
  68.7 1.4 %collective-permute-start.18 = (bf16[384,256]{1,0:T(8,128)(2,1)S(1)}, bf16[384,256]{1,0:T(8,128)(2,1)S(1)}, u32[]{:S(2)}, u32[]{:S(2)}) collective-permute-start(bf16[384,256]{1,0:T(8,128)(2,1)S(1)} %collective-permute-done.15.refs_2_.refs_6_), channel_id=1, source_target_pairs={{0,1},{1,0},{2,3},{3,2},{4,5},{5,4},{6,7},{7,6},{8,9},{9,8},{10,11... | collective-permute-start | bytes 589832 | tf_op jit(solution)/shard_map/ppermute | solution.py:378

commit v13 on v12

--- a/solution.py
+++ b/solution.py
@@ -314,30 +314,35 @@
     gf_ref[...] = grad.astype(BF16)
 
 
+def outputs_pair(keep, got, m, width):
+    both = [keep[m].astype(F32), got[m].astype(F32)]
+    both = [x[:, j * width : (j + 1) * width] for x in both for j in range(2)]
+    return jnp.concatenate(both, axis=0).astype(BF16)
+
+
 def weights_join(sites, row_keep, row_got, og_keep, og_got, *refs):
-    cols, outs = refs[:sites], refs[sites:]
+    cols, (near, own, *far) = refs[:sites], refs[sites:]
     half, width = row_keep.shape
     depth = half + 5 * cols[0].shape[0]
-    per = og_keep.shape[1]
     total = sum(c[...].astype(F32) for c in cols)
     tiles = [total[:, t * width : (t + 1) * width] for t in range(5)]
     rows = row_keep[...].astype(F32) + row_got[...].astype(F32)
-    joined = jnp.concatenate([rows] + tiles, axis=0).astype(BF16)
-    for m, out in enumerate(outs):
-        out[:depth, :] = joined
-        both = [og_keep[m].astype(F32), og_got[m].astype(F32)]
-        both = [x[:, j * width : (j + 1) * width] for x in both for j in range(2)]
-        out[depth:, :] = jnp.concatenate(both, axis=0).astype(BF16)
-
-
-def weights_sum(haps, sites, *refs):
-    parts, gps = refs[: haps // 2], refs[haps // 2 : haps // 2 + sites - 1]
-    mine, outs = refs[haps // 2 + sites - 1], refs[haps // 2 + sites :]
+    near[:depth, :] = jnp.concatenate([rows] + tiles, axis=0).astype(BF16)
+    near[depth:, :] = outputs_pair(og_keep, og_got, 1, width)
+    own[...] = outputs_pair(og_keep, og_got, 0, width)
+    for j, out in enumerate(far):
+        out[...] = outputs_pair(og_keep, og_got, j + 2, width)
+
+
+def weights_add(mine, got, out):
+    depth = out.shape[0]
+    out[...] = (mine[:depth, :].astype(F32) + got[:depth, :].astype(F32)).astype(BF16)
+
+
+def weights_last(left, right, *refs):
+    gps, mine, outs = refs[: len(refs) // 2], refs[len(refs) // 2], refs[len(refs) // 2 + 1 :]
     depth, width = mine.shape
-    terms = [r[:depth, :].astype(F32) for r in parts]
-    while len(terms) > 1:
-        terms = [a + b for a, b in zip(terms[::2], terms[1::2])]
-    mine[...] = terms[0].astype(BF16)
+    weights_add(left, right, mine)
     for gp, out in zip(gps, outs):
         out[:depth, :] = mine[...]
         out[depth:, : gp.shape[1]] = gp[...]
@@ -470,16 +475,23 @@
     )
     row_got = swapped(row_send, "hap", 1)
     depth = 3 * group // 2 + 5 * half // sites
-    parts = call(
+    near, own, *far = call(
         functools.partial(weights_join, sites),
-        [((depth + 4 * per, width), BF16)] * (haps // 2),
+        [((depth + 4 * per, width), BF16)] + [((4 * per, width), BF16)] * (haps // 2 - 1),
         row_keep, row_got, og_keep, og_got, *cols,
     )
-    parts = [parts[0]] + [swapped(parts[m], "hap", 2 * m) for m in range(1, haps // 2)]
+    near_got = swapped(near, "hap", 2)
+    far = [swapped(x, "hap", 2 * (j + 2)) for j, x in enumerate(far)]
+    near_got, far = lax.optimization_barrier((near_got, far))
+    parts = [own, near_got] + list(far)
+    left, right, step = near, near_got, 2
+    while 2 * step < haps:
+        (left,) = call(weights_add, [((depth, width), BF16)], left, right)
+        right, step = swapped(left, "hap", 2 * step), 2 * step
     mine, *sends = call(
-        functools.partial(weights_sum, haps, sites),
+        weights_last,
         [((depth, width), BF16)] + [((depth + rows, width), BF16)] * (sites - 1),
-        *parts, *gps[1:],
+        left, right, *gps[1:],
     )
     got = [swapped(sends[k - 1], "site", k) for k in range(1, sites)]
     mine_swapped = swapped(mine, "hap", 1)

time: 72 us -> 71.8 us (level)
  the two profiles are of different devices: /device:TPU:9 before, /device:TPU:0 now
where the time goes in v13:
time: 71.8 us; the launch traced here: 71.5 us
  waiting for transfers between devices  29.9 us (42%)
  starting transfers between devices  24.8 us (35%)
  Pallas kernels  12.4 us (17%)
  local copies, waits for them, and re-layouts  3.62 us (5%)
  between operations  0.83 us (1%)
    ppermute x20, waiting for transfers between devices, swapped(): return lax.ppermute(value, axis, [(i, i ^ by) for i in range(length)])  20.9 us
    ppermute x20, starting transfers between devices, swapped(): return lax.ppermute(value, axis, [(i, i ^ by) for i in range(length)])  17.2 us
    pallas_call x11, Pallas kernels, call(): pl.pallas_call(body, out_shape=[jax.ShapeDtypeStruct(s, d) for s, d in ou...  12.4 us
    all_to_all x2, waiting for transfers between devices, exchange(): return lax.all_to_all(value, axis, 0, 0, tiled=True)  8.95 us
    all_to_all x2, starting transfers between devices, exchange(): return lax.all_to_all(value, axis, 0, 0, tiled=True)  7.56 us
    unnamed x24, local copies, waits for them, and re-layouts  2.67 us
  transfers between devices with their start and end apart: 22, of which 12 were waited for; matrix products, arithmetic and copies ran while one was open for 0% of the time, Pallas kernels for 6%

profile of v13, /device:TPU:0, one launch (start us, length us, event | category | flops | bytes accessed | tf_op | source)
XLA Modules:
  0.0 71.5 jit_solution(15814845420462783629)
XLA Ops:
  0.6 4.0 %collective-permute-start.2 = (bf16[128,256]{1,0:T(8,128)(2,1)}, bf16[128,256]{1,0:T(8,128)(2,1)S(1)}, u32[]{:S(2)}, u32[]{:S(2)}) collective-permute-start(bf16[128,256]{1,0:T(8,128)(2,1)} %bitcast.14), channel_id=1, source_target_pairs={{0,24},{8,16},{16,8},{24,0},{1,25},{9,17},{17,9},{25,1},{2,26},{10... | collective-permute-start | bytes 196616 | tf_op jit(solution)/shard_map/ppermute | solution.py:383
  4.6 0.5 collective-permute-start.1
  5.1 0.1 collective-permute-start
  5.2 0.7 copy-done.8
  5.9 0.9 %slice-done = bf16[256,512]{1,0:T(8,128)(2,1)S(1)} async-done(((bf16[256,768]{1,0:T(8,128)(2,1)}), bf16[256,512]{1,0:T(8,128)(2,1)S(1)}, s32[]{:S(2)}) %slice-start) | async-done | bytes 262168 | tf_op jit(solution)/shard_map/slice | solution.py:418
  6.9 0.1 copy.17
  7.0 0.0 copy-start.1
  7.1 0.2 copy.15
  7.3 0.4 copy-done.10
  7.7 0.2 copy-done.9
  7.9 1.1 %collective-permute-done.1.refs_2_ = bf16[128,256]{1,0:T(8,128)(2,1)S(1)} collective-permute-done((bf16[128,256]{1,0:T(8,128)(2,1)}, bf16[128,256]{1,0:T(8,128)(2,1)S(1)}, u32[]{:S(2)}, u32[]{:S(2)}) %collective-permute-start.1) | collective-permute-done | bytes 65568 | tf_op jit(solution)/shard_map/ppermute | solution.py:383
  9.1 0.5 collective-permute-done.refs_1_
  9.6 2.8 %shard_map.136 = (bf16[8,16,768]{2,1,0:T(8,128)(2,1)}, bf16[512,256]{1,0:T(8,128)(2,1)S(1)}) custom-call(s32[1]{0:T(128)} %bitcast.idx, s32[4,4]{1,0:T(4,128)S(1)} %compare_select_fusion.link, bf16[128,256]{1,0:T(8,128)(2,1)S(1)} %bitcast.17, bf16[128,256]{1,0:T(8,128)(2,1)S(1)} %collective-permute-done.refs_1_, ...), custom_call_target="tpu_custom_call" | custom-call | flops 1 | bytes 1 | tf_op jit(solution)/shard_map/pallas_call | solution.py:82
  12.4 4.9 %all-to-all-start = ((bf16[8,16,768]{2,1,0:T(8,128)(2,1)}), bf16[8,16,768]{2,1,0:T(8,128)(2,1)S(1)}, u32[]{:S(2)}, u32[]{:S(2)}) async-start(bf16[8,16,768]{2,1,0:T(8,128)(2,1)} %get-tuple-element.49), calls=%async_computation | async-start | bytes 393216 | tf_op jit(solution)/shard_map/all_to_all | solution.py:378
  17.3 1.8 %shard_map.137 = (bf16[512,1024]{1,0:T(8,128)(2,1)S(1)}, bf16[512,64]{1,0:T(8,128)(2,1)S(1)}, bf16[512,64]{1,0:T(8,128)(2,1)S(1)}, bf16[64,512]{1,0:T(8,128)(2,1)S(1)}) custom-call(s32[1]{0:T(128)} %bitcast.idx, s32[4,4]{1,0:T(4,128)S(1)} %compare_select_fusion.link, bf16[512,256]{1,0:T(8,128)(2,1)S(1)} %get-tuple-element.50.normed_ref.normed, ...), custom_call_target="tpu_custom_call" | custom-call | flops 20000000000 | bytes 72000000 | tf_op jit(solution)/shard_map/pallas_call | solution.py:82
  19.1 6.5 %all-to-all-done.x_in = bf16[8,16,768]{2,1,0:T(8,128)(2,1)S(1)} async-done(((bf16[8,16,768]{2,1,0:T(8,128)(2,1)}), bf16[8,16,768]{2,1,0:T(8,128)(2,1)S(1)}, u32[]{:S(2)}, u32[]{:S(2)}) %all-to-all-start) | async-done | bytes 196640 | tf_op jit(solution)/shard_map/all_to_all | solution.py:378
  25.7 3.2 %shard_map.138 = (bf16[32,8,128]{2,1,0:T(8,128)(2,1)}, bf16[128,1280]{1,0:T(8,128)(2,1)S(1)}, bf16[128,1280]{1,0:T(8,128)(2,1)}, bf16[8,16,512]{2,1,0:T(8,128)(2,1)}) custom-call(s32[1]{0:T(128)} %bitcast.1.hap, bf16[8,16,768]{2,1,0:T(8,128)(2,1)S(1)} %all-to-all-done.x_in, bf16[256,256]{1,0:T(8,128)(2,1)S(1)} %copy-done.1, ...), custom_call_target="tpu_custom_call" | custom-call | flops 1 | bytes 1 | tf_op jit(solution)/shard_map/pallas_call | solution.py:82
  28.9 0.1 collective-permute-start.3
  29.0 2.7 %all-to-all-start.1 = ((bf16[32,8,128]{2,1,0:T(8,128)(2,1)}), bf16[32,8,128]{2,1,0:T(8,128)(2,1)S(1)}, u32[]{:S(2)}, u32[]{:S(2)}) async-start(bf16[32,8,128]{2,1,0:T(8,128)(2,1)} %get-tuple-element.53), calls=%async_computation.1 | async-start | bytes 131072 | tf_op jit(solution)/shard_map/all_to_all | solution.py:378
  31.7 0.3 collective-permute-start.4
  32.0 1.0 %copy-done.2 = bf16[128,1280]{1,0:T(8,128)(2,1)S(1)} copy-done((bf16[128,1280]{1,0:T(8,128)(2,1)S(1)}, bf16[128,1280]{1,0:T(8,128)(2,1)}, u32[]{:S(2)}) %copy-start.2) | copy-done | bytes 327704
  33.0 0.2 shard_map.139
  33.2 1.7 %collective-permute-start.6 = (bf16[32,1280]{1,0:T(8,128)(2,1)S(1)}, bf16[32,1280]{1,0:T(8,128)(2,1)S(1)}, u32[]{:S(2)}, u32[]{:S(2)}) collective-permute-start(bf16[32,1280]{1,0:T(8,128)(2,1)S(1)} %get-tuple-element.57), channel_id=1, source_target_pairs={{0,8},{8,0},{16,24},{24,16},{1,9},{9,1},{17,25},{25,17},{2,10},{10... | collective-permute-start | bytes 245768 | tf_op jit(solution)/shard_map/ppermute | solution.py:383
  34.9 1.5 %collective-permute-start.7 = (bf16[32,1280]{1,0:T(8,128)(2,1)S(1)}, bf16[32,1280]{1,0:T(8,128)(2,1)S(1)}, u32[]{:S(2)}, u32[]{:S(2)}) collective-permute-start(bf16[32,1280]{1,0:T(8,128)(2,1)S(1)} %get-tuple-element.58), channel_id=1, source_target_pairs={{0,16},{8,24},{16,0},{24,8},{1,17},{9,25},{17,1},{25,9},{2,18},{10... | collective-permute-start | bytes 245768 | tf_op jit(solution)/shard_map/ppermute | solution.py:383
  36.4 0.3 collective-permute-start.8
  36.7 2.4 %all-to-all-done.1.g_in = bf16[32,8,128]{2,1,0:T(8,128)(2,1)S(1)} async-done(((bf16[32,8,128]{2,1,0:T(8,128)(2,1)}), bf16[32,8,128]{2,1,0:T(8,128)(2,1)S(1)}, u32[]{:S(2)}, u32[]{:S(2)}) %all-to-all-start.1) | async-done | bytes 65568 | tf_op jit(solution)/shard_map/all_to_all | solution.py:378
  39.2 1.7 %shard_map.141 = (bf16[128,192]{1,0:T(8,128)(2,1)S(1)}, bf16[128,192]{1,0:T(8,128)(2,1)S(1)}, bf16[128,192]{1,0:T(8,128)(2,1)S(1)}, bf16[128,192]{1,0:T(8,128)(2...) custom-call(s32[1]{0:T(128)} %bitcast.idx, s32[1]{0:T(128)S(6)} %select_n.11.core, ...), custom_call_target="tpu_custom_call" | custom-call | flops 1 | bytes 1 | tf_op jit(solution)/shard_map/pallas_call | solution.py:82
  40.9 0.1 collective-permute-start.5
  41.0 1.2 %collective-permute-done.5.row_got = bf16[96,256]{1,0:T(8,128)(2,1)S(1)} collective-permute-done((bf16[96,256]{1,0:T(8,128)(2,1)S(1)}, bf16[96,256]{1,0:T(8,128)(2,1)S(1)}, u32[]{:S(2)}, u32[]{:S(2)}) %collective-permute-start.5) | collective-permute-done | bytes 49184 | tf_op jit(solution)/shard_map/ppermute | solution.py:383
  42.2 0.1 shard_map.142
  42.2 1.1 %collective-permute-start.9 = (bf16[320,256]{1,0:T(8,128)(2,1)S(1)}, bf16[320,256]{1,0:T(8,128)(2,1)S(1)}, u32[]{:S(2)}, u32[]{:S(2)}) collective-permute-start(bf16[320,256]{1,0:T(8,128)(2,1)S(1)} %get-tuple-element.70.mine), channel_id=1, source_target_pairs={{0,2},{1,3},{2,0},{3,1},{4,6},{5,7},{6,4},{7,5},{8,10},{9,11},{10,... | collective-permute-start | bytes 491528 | tf_op jit(solution)/shard_map/ppermute | solution.py:383
  43.3 2.5 %collective-permute-start.10 = (bf16[64,256]{1,0:T(8,128)(2,1)S(1)}, bf16[64,256]{1,0:T(8,128)(2,1)S(1)}, u32[]{:S(2)}, u32[]{:S(2)}) collective-permute-start(bf16[64,256]{1,0:T(8,128)(2,1)S(1)} %get-tuple-element.71), channel_id=1, source_target_pairs={{0,4},{1,5},{2,6},{3,7},{4,0},{5,1},{6,2},{7,3},{8,12},{9,13},{10,... | collective-permute-start | bytes 98312 | tf_op jit(solution)/shard_map/ppermute | solution.py:383
  45.8 0.9 %collective-permute-start.11 = (bf16[64,256]{1,0:T(8,128)(2,1)S(1)}, bf16[64,256]{1,0:T(8,128)(2,1)S(1)}, u32[]{:S(2)}, u32[]{:S(2)}) collective-permute-start(bf16[64,256]{1,0:T(8,128)(2,1)S(1)} %get-tuple-element.72), channel_id=1, source_target_pairs={{0,6},{1,7},{2,4},{3,5},{4,2},{5,3},{6,0},{7,1},{8,14},{9,15},{10,... | collective-permute-start | bytes 98312 | tf_op jit(solution)/shard_map/ppermute | solution.py:383
  46.7 1.5 %collective-permute-done.10.refs_5_ = bf16[64,256]{1,0:T(8,128)(2,1)S(1)} collective-permute-done((bf16[64,256]{1,0:T(8,128)(2,1)S(1)}, bf16[64,256]{1,0:T(8,128)(2,1)S(1)}, u32[]{:S(2)}, u32[]{:S(2)}) %collective-permute-start.10) | collective-permute-done | bytes 32800 | tf_op jit(solution)/shard_map/ppermute | solution.py:383
  48.2 3.3 %collective-permute-done.11.refs_6_ = bf16[64,256]{1,0:T(8,128)(2,1)S(1)} collective-permute-done((bf16[64,256]{1,0:T(8,128)(2,1)S(1)}, bf16[64,256]{1,0:T(8,128)(2,1)S(1)}, u32[]{:S(2)}, u32[]{:S(2)}) %collective-permute-start.11) | collective-permute-done | bytes 32800 | tf_op jit(solution)/shard_map/ppermute | solution.py:383
  51.5 0.1 collective-permute-start.12
  51.6 6.3 %collective-permute-done.12.right = bf16[256,256]{1,0:T(8,128)(2,1)S(1)} collective-permute-done((bf16[256,256]{1,0:T(8,128)(2,1)S(1)}, bf16[256,256]{1,0:T(8,128)(2,1)S(1)}, u32[]{:S(2)}, u32[]{:S(2)}) %collective-permute-start.12) | collective-permute-done | bytes 131104 | tf_op jit(solution)/shard_map/ppermute | solution.py:383
  57.9 0.1 shard_map.144
  57.9 0.6 collective-permute-start.13
  58.6 1.4 %collective-permute-start.15 = (bf16[384,256]{1,0:T(8,128)(2,1)S(1)}, bf16[384,256]{1,0:T(8,128)(2,1)S(1)}, u32[]{:S(2)}, u32[]{:S(2)}) collective-permute-start(bf16[384,256]{1,0:T(8,128)(2,1)S(1)} %get-tuple-element.80), channel_id=1, source_target_pairs={{0,16},{8,24},{16,0},{24,8},{1,17},{9,25},{17,1},{25,9},{2,18},{10... | collective-permute-start | bytes 589832 | tf_op jit(solution)/shard_map/ppermute | solution.py:383
  60.0 1.5 %collective-permute-start.16 = (bf16[384,256]{1,0:T(8,128)(2,1)S(1)}, bf16[384,256]{1,0:T(8,128)(2,1)S(1)}, u32[]{:S(2)}, u32[]{:S(2)}) collective-permute-start(bf16[384,256]{1,0:T(8,128)(2,1)S(1)} %get-tuple-element.81), channel_id=1, source_target_pairs={{0,24},{8,16},{16,8},{24,0},{1,25},{9,17},{17,9},{25,1},{2,26},{10... | collective-permute-start | bytes 589832 | tf_op jit(solution)/shard_map/ppermute | solution.py:383
  61.5 1.3 %collective-permute-done.14.refs_1_ = bf16[256,256]{1,0:T(8,128)(2,1)S(1)} collective-permute-done((bf16[256,256]{1,0:T(8,128)(2,1)S(1)}, bf16[256,256]{1,0:T(8,128)(2,1)S(1)}, u32[]{:S(2)}, u32[]{:S(2)}) %collective-permute-start.14) | collective-permute-done | bytes 131104 | tf_op jit(solution)/shard_map/ppermute | solution.py:383
  62.9 3.0 %collective-permute-done.13.refs_0_.refs_2_ = bf16[384,256]{1,0:T(8,128)(2,1)S(1)} collective-permute-done((bf16[384,256]{1,0:T(8,128)(2,1)S(1)}, bf16[384,256]{1,0:T(8,128)(2,1)S(1)}, u32[]{:S(2)}, u32[]{:S(2)}) %collective-permute-start.13) | collective-permute-done | bytes 196640 | tf_op jit(solution)/shard_map/ppermute | solution.py:383
  65.9 2.4 %collective-permute-done.15.refs_1_.refs_4_ = bf16[384,256]{1,0:T(8,128)(2,1)S(1)} collective-permute-done((bf16[384,256]{1,0:T(8,128)(2,1)S(1)}, bf16[384,256]{1,0:T(8,128)(2,1)S(1)}, u32[]{:S(2)}, u32[]{:S(2)}) %collective-permute-start.15) | collective-permute-done | bytes 196640 | tf_op jit(solution)/shard_map/ppermute | solution.py:383
  68.3 0.5 collective-permute-start.19
  68.8 1.0 %shard_map.145 = (bf16[128,256]{1,0:T(8,128)(2,1)}, bf16[128,256]{1,0:T(8,128)(2,1)}) custom-call(s32[1]{0:T(128)} %bitcast.idx, s32[1]{0:T(128)} %bitcast.1.hap, bf16[128,256]{1,0:T(8,128)(2,1)S(1)} %bitcast.18, f32[2,256]{1,0:T(2,128)S(1)} %pad_maximum_fusion.refs_5_.gain, bf16[768,256]{1,0:T(8,128)(2,1)S(1)} %bitcast.12, ...), custom_call_target="tpu_custom_call" | custom-call | flops 1 | bytes 1 | tf_op jit(solution)/shard_map/pallas_call | solution.py:82
  69.8 0.2 collective-permute-done.19.refs_7_
  70.0 1.5 %shard_map.146 = (f32[256,768]{1,0:T(8,128)}, f32[256,256]{1,0:T(8,128)}, f32[256,768]{1,0:T(8,128)}, f32[256,256]{1,0:T(8,128)}) custom-call(s32[1]{0:T(128)} %bitcast.idx, s32[1]{0:T(128)S(6)} %select_n.11.core, bf16[256,256]{1,0:T(8,128)(2,1)S(1)} %get-tuple-element.78.refs_0_, bf16[256,256]{1,0:T(8,128)(2,1)S(1)} %collective-permute-done.14.refs_1_, ...), custom_call_target="tpu_custom_call" | custom-call | flops 1 | bytes 1 | tf_op jit(solution)/shard_map/pallas_call | solution.py:82
  (35 shorter events, 0.1 us)
Async XLA Ops:
  0.6 7.3 %collective-permute-start.2 = (bf16[128,256]{1,0:T(8,128)(2,1)}, bf16[128,256]{1,0:T(8,128)(2,1)S(1)}, u32[]{:S(2)}, u32[]{:S(2)}) collective-permute-start(bf16[128,256]{1,0:T(8,128)(2,1)} %bitcast.14), channel_id=1, source_target_pairs={{0,24},{8,16},{16,8},{24,0},{1,25},{9,17},{17,9},{25,1},{2,26},{10... | collective-permute-start | bytes 196616 | tf_op jit(solution)/shard_map/ppermute | solution.py:383
  4.6 4.5 %collective-permute-start.1 = (bf16[128,256]{1,0:T(8,128)(2,1)}, bf16[128,256]{1,0:T(8,128)(2,1)S(1)}, u32[]{:S(2)}, u32[]{:S(2)}) collective-permute-start(bf16[128,256]{1,0:T(8,128)(2,1)} %bitcast.15), channel_id=1, source_target_pairs={{0,16},{8,24},{16,0},{24,8},{1,17},{9,25},{17,1},{25,9},{2,18},{10... | collective-permute-start | bytes 196616 | tf_op jit(solution)/shard_map/ppermute | solution.py:383
  5.1 4.5 %collective-permute-start = (bf16[128,256]{1,0:T(8,128)(2,1)}, bf16[128,256]{1,0:T(8,128)(2,1)S(1)}, u32[]{:S(2)}, u32[]{:S(2)}) collective-permute-start(bf16[128,256]{1,0:T(8,128)(2,1)} %bitcast.16), channel_id=1, source_target_pairs={{0,8},{8,0},{16,24},{24,16},{1,9},{9,1},{17,25},{25,17},{2,10},{10... | collective-permute-start | bytes 196616 | tf_op jit(solution)/shard_map/ppermute | solution.py:383
  5.2 0.7 copy-start.8
  5.9 0.9 %slice-start = ((bf16[256,768]{1,0:T(8,128)(2,1)}), bf16[256,512]{1,0:T(8,128)(2,1)S(1)}, s32[]{:S(2)}) async-start(bf16[256,768]{1,0:T(8,128)(2,1)} %col_proj.1), calls=%async_computation.2 | async-start | bytes 524288 | tf_op jit(solution)/shard_map/slice | solution.py:418
  5.9 1.1 %copy-start.7 = (bf16[256,768]{1,0:T(8,128)(2,1)S(1)}, bf16[256,768]{1,0:T(8,128)(2,1)}, u32[]{:S(2)}) copy-start(bf16[256,768]{1,0:T(8,128)(2,1)} %param.12) | copy-start | bytes 1179652
  7.0 0.7 copy-start.10
  7.0 2.5 %copy-start.1 = (bf16[256,256]{1,0:T(8,128)(2,1)S(1)}, bf16[256,256]{1,0:T(8,128)(2,1)}, u32[]{:S(2)}) copy-start(bf16[256,256]{1,0:T(8,128)(2,1)} %row_out.1) | copy-start | bytes 393220
  7.0 2.5 %copy-start.3 = (bf16[128,1,256]{2,0,1:T(8,128)(2,1)S(1)}, bf16[128,1,256]{2,0,1:T(8,128)(2,1)}, u32[]{:S(2)}) copy-start(bf16[128,1,256]{2,0,1:T(8,128)(2,1)} %param.9) | copy-start | bytes 196612
  7.1 2.5 %copy-start.6 = (bf16[128,1,256]{2,0,1:T(8,128)(2,1)S(1)}, bf16[128,1,256]{2,0,1:T(8,128)(2,1)}, u32[]{:S(2)}) copy-start(bf16[128,1,256]{2,0,1:T(8,128)(2,1)} %param.17) | copy-start | bytes 196612
  7.2 0.7 copy-start.9
  12.4 13.2 %all-to-all-start = ((bf16[8,16,768]{2,1,0:T(8,128)(2,1)}), bf16[8,16,768]{2,1,0:T(8,128)(2,1)S(1)}, u32[]{:S(2)}, u32[]{:S(2)}) async-start(bf16[8,16,768]{2,1,0:T(8,128)(2,1)} %get-tuple-element.49), calls=%async_computation | async-start | bytes 393216 | tf_op jit(solution)/shard_map/all_to_all | solution.py:378
  17.3 8.3 %copy-start = (bf16[256,768]{1,0:T(8,128)(2,1)S(1)}, bf16[256,768]{1,0:T(8,128)(2,1)}, u32[]{:S(2)}) copy-start(bf16[256,768]{1,0:T(8,128)(2,1)} %col_proj.1) | copy-start | bytes 1179652
  17.3 8.3 %copy-start.5 = (bf16[256,256]{1,0:T(8,128)(2,1)S(1)}, bf16[256,256]{1,0:T(8,128)(2,1)}, u32[]{:S(2)}) copy-start(bf16[256,256]{1,0:T(8,128)(2,1)} %col_out.1) | copy-start | bytes 393220
  28.9 2.8 %copy-start.4 = (bf16[8,16,512]{2,1,0:T(8,128)(2,1)S(1)}, bf16[8,16,512]{2,1,0:T(8,128)(2,1)}, u32[]{:S(2)}) copy-start(bf16[8,16,512]{2,1,0:T(8,128)(2,1)} %get-tuple-element.60.og) | copy-start | bytes 393220
  28.9 3.1 %collective-permute-start.3 = (bf16[128,1280]{1,0:T(8,128)(2,1)S(1)}, bf16[128,1280]{1,0:T(8,128)(2,1)S(1)}, u32[]{:S(2)}, u32[]{:S(2)}) collective-permute-start(bf16[128,1280]{1,0:T(8,128)(2,1)S(1)} %get-tuple-element.55), channel_id=1, source_target_pairs={{0,1},{1,0},{2,3},{3,2},{4,5},{5,4},{6,7},{7,6},{8,9},{9,8},{10,11... | collective-permute-start | bytes 983048 | tf_op jit(solution)/shard_map/ppermute | solution.py:383
  29.0 10.2 %all-to-all-start.1 = ((bf16[32,8,128]{2,1,0:T(8,128)(2,1)}), bf16[32,8,128]{2,1,0:T(8,128)(2,1)S(1)}, u32[]{:S(2)}, u32[]{:S(2)}) async-start(bf16[32,8,128]{2,1,0:T(8,128)(2,1)} %get-tuple-element.53), calls=%async_computation.1 | async-start | bytes 131072 | tf_op jit(solution)/shard_map/all_to_all | solution.py:378
  31.7 5.0 %collective-permute-start.4 = (bf16[4,16,512]{2,1,0:T(8,128)(2,1)S(1)}, bf16[4,16,512]{2,1,0:T(8,128)(2,1)S(1)}, u32[]{:S(2)}, u32[]{:S(2)}) collective-permute-start(bf16[4,16,512]{2,1,0:T(8,128)(2,1)S(1)} %get-tuple-element.61), channel_id=1, source_target_pairs={{0,1},{1,0},{2,3},{3,2},{4,5},{5,4},{6,7},{7,6},{8,9},{9,8},{10,11... | collective-permute-start | bytes 196616 | tf_op jit(solution)/shard_map/ppermute | solution.py:383
  32.0 1.0 %copy-start.2 = (bf16[128,1280]{1,0:T(8,128)(2,1)S(1)}, bf16[128,1280]{1,0:T(8,128)(2,1)}, u32[]{:S(2)}) copy-start(bf16[128,1280]{1,0:T(8,128)(2,1)} %get-tuple-element.54.keep) | copy-start | bytes 983044
  33.2 9.0 %collective-permute-start.6 = (bf16[32,1280]{1,0:T(8,128)(2,1)S(1)}, bf16[32,1280]{1,0:T(8,128)(2,1)S(1)}, u32[]{:S(2)}, u32[]{:S(2)}) collective-permute-start(bf16[32,1280]{1,0:T(8,128)(2,1)S(1)} %get-tuple-element.57), channel_id=1, source_target_pairs={{0,8},{8,0},{16,24},{24,16},{1,9},{9,1},{17,25},{25,17},{2,10},{10... | collective-permute-start | bytes 245768 | tf_op jit(solution)/shard_map/ppermute | solution.py:383
  34.9 7.3 %collective-permute-start.7 = (bf16[32,1280]{1,0:T(8,128)(2,1)S(1)}, bf16[32,1280]{1,0:T(8,128)(2,1)S(1)}, u32[]{:S(2)}, u32[]{:S(2)}) collective-permute-start(bf16[32,1280]{1,0:T(8,128)(2,1)S(1)} %get-tuple-element.58), channel_id=1, source_target_pairs={{0,16},{8,24},{16,0},{24,8},{1,17},{9,25},{17,1},{25,9},{2,18},{10... | collective-permute-start | bytes 245768 | tf_op jit(solution)/shard_map/ppermute | solution.py:383
  36.4 5.8 %collective-permute-start.8 = (bf16[32,1280]{1,0:T(8,128)(2,1)S(1)}, bf16[32,1280]{1,0:T(8,128)(2,1)S(1)}, u32[]{:S(2)}, u32[]{:S(2)}) collective-permute-start(bf16[32,1280]{1,0:T(8,128)(2,1)S(1)} %get-tuple-element.59), channel_id=1, source_target_pairs={{0,24},{8,16},{16,8},{24,0},{1,25},{9,17},{17,9},{25,1},{2,26},{10... | collective-permute-start | bytes 245768 | tf_op jit(solution)/shard_map/ppermute | solution.py:383
  40.9 1.3 %collective-permute-start.5 = (bf16[96,256]{1,0:T(8,128)(2,1)S(1)}, bf16[96,256]{1,0:T(8,128)(2,1)S(1)}, u32[]{:S(2)}, u32[]{:S(2)}) collective-permute-start(bf16[96,256]{1,0:T(8,128)(2,1)S(1)} %get-tuple-element.68), channel_id=1, source_target_pairs={{0,1},{1,0},{2,3},{3,2},{4,5},{5,4},{6,7},{7,6},{8,9},{9,8},{10,11... | collective-permute-start | bytes 147464 | tf_op jit(solution)/shard_map/ppermute | solution.py:383
  42.2 9.2 %collective-permute-start.9 = (bf16[320,256]{1,0:T(8,128)(2,1)S(1)}, bf16[320,256]{1,0:T(8,128)(2,1)S(1)}, u32[]{:S(2)}, u32[]{:S(2)}) collective-permute-start(bf16[320,256]{1,0:T(8,128)(2,1)S(1)} %get-tuple-element.70.mine), channel_id=1, source_target_pairs={{0,2},{1,3},{2,0},{3,1},{4,6},{5,7},{6,4},{7,5},{8,10},{9,11},{10,... | collective-permute-start | bytes 491528 | tf_op jit(solution)/shard_map/ppermute | solution.py:383
  43.3 4.9 %collective-permute-start.10 = (bf16[64,256]{1,0:T(8,128)(2,1)S(1)}, bf16[64,256]{1,0:T(8,128)(2,1)S(1)}, u32[]{:S(2)}, u32[]{:S(2)}) collective-permute-start(bf16[64,256]{1,0:T(8,128)(2,1)S(1)} %get-tuple-element.71), channel_id=1, source_target_pairs={{0,4},{1,5},{2,6},{3,7},{4,0},{5,1},{6,2},{7,3},{8,12},{9,13},{10,... | collective-permute-start | bytes 98312 | tf_op jit(solution)/shard_map/ppermute | solution.py:383
  45.8 5.7 %collective-permute-start.11 = (bf16[64,256]{1,0:T(8,128)(2,1)S(1)}, bf16[64,256]{1,0:T(8,128)(2,1)S(1)}, u32[]{:S(2)}, u32[]{:S(2)}) collective-permute-start(bf16[64,256]{1,0:T(8,128)(2,1)S(1)} %get-tuple-element.72), channel_id=1, source_target_pairs={{0,6},{1,7},{2,4},{3,5},{4,2},{5,3},{6,0},{7,1},{8,14},{9,15},{10,... | collective-permute-start | bytes 98312 | tf_op jit(solution)/shard_map/ppermute | solution.py:383
  51.5 6.3 %collective-permute-start.12 = (bf16[256,256]{1,0:T(8,128)(2,1)S(1)}, bf16[256,256]{1,0:T(8,128)(2,1)S(1)}, u32[]{:S(2)}, u32[]{:S(2)}) collective-permute-start(bf16[256,256]{1,0:T(8,128)(2,1)S(1)} %shard_map.143.left), channel_id=1, source_target_pairs={{0,4},{1,5},{2,6},{3,7},{4,0},{5,1},{6,2},{7,3},{8,12},{9,13},{10,... | collective-permute-start | bytes 393224 | tf_op jit(solution)/shard_map/ppermute | solution.py:383
  57.9 7.9 %collective-permute-start.13 = (bf16[384,256]{1,0:T(8,128)(2,1)S(1)}, bf16[384,256]{1,0:T(8,128)(2,1)S(1)}, u32[]{:S(2)}, u32[]{:S(2)}) collective-permute-start(bf16[384,256]{1,0:T(8,128)(2,1)S(1)} %get-tuple-element.77), channel_id=1, source_target_pairs={{0,8},{8,0},{16,24},{24,16},{1,9},{9,1},{17,25},{25,17},{2,10},{10... | collective-permute-start | bytes 589832 | tf_op jit(solution)/shard_map/ppermute | solution.py:383
  58.6 9.7 %collective-permute-start.15 = (bf16[384,256]{1,0:T(8,128)(2,1)S(1)}, bf16[384,256]{1,0:T(8,128)(2,1)S(1)}, u32[]{:S(2)}, u32[]{:S(2)}) collective-permute-start(bf16[384,256]{1,0:T(8,128)(2,1)S(1)} %get-tuple-element.80), channel_id=1, source_target_pairs={{0,16},{8,24},{16,0},{24,8},{1,17},{9,25},{17,1},{25,9},{2,18},{10... | collective-permute-start | bytes 589832 | tf_op jit(solution)/shard_map/ppermute | solution.py:383
  60.0 8.3 %collective-permute-start.16 = (bf16[384,256]{1,0:T(8,128)(2,1)S(1)}, bf16[384,256]{1,0:T(8,128)(2,1)S(1)}, u32[]{:S(2)}, u32[]{:S(2)}) collective-permute-start(bf16[384,256]{1,0:T(8,128)(2,1)S(1)} %get-tuple-element.81), channel_id=1, source_target_pairs={{0,24},{8,16},{16,8},{24,0},{1,25},{9,17},{17,9},{25,1},{2,26},{10... | collective-permute-start | bytes 589832 | tf_op jit(solution)/shard_map/ppermute | solution.py:383
  61.5 1.3 %collective-permute-start.14 = (bf16[256,256]{1,0:T(8,128)(2,1)S(1)}, bf16[256,256]{1,0:T(8,128)(2,1)S(1)}, u32[]{:S(2)}, u32[]{:S(2)}) collective-permute-start(bf16[256,256]{1,0:T(8,128)(2,1)S(1)} %get-tuple-element.78.refs_0_), channel_id=1, source_target_pairs={{0,1},{1,0},{2,3},{3,2},{4,5},{5,4},{6,7},{7,6},{8,9},{9,8},{10,11... | collective-permute-start | bytes 393224 | tf_op jit(solution)/shard_map/ppermute | solution.py:383
  65.9 3.9 %collective-permute-start.17 = (bf16[384,256]{1,0:T(8,128)(2,1)S(1)}, bf16[384,256]{1,0:T(8,128)(2,1)S(1)}, u32[]{:S(2)}, u32[]{:S(2)}) collective-permute-start(bf16[384,256]{1,0:T(8,128)(2,1)S(1)} %collective-permute-done.13.refs_0_.refs_2_), channel_id=1, source_target_pairs={{0,1},{1,0},{2,3},{3,2},{4,5},{5,4},{6,7},{7,6},{8,9},{9,8},{10,11... | collective-permute-start | bytes 589832 | tf_op jit(solution)/shard_map/ppermute | solution.py:383
  68.3 1.5 %collective-permute-start.18 = (bf16[384,256]{1,0:T(8,128)(2,1)S(1)}, bf16[384,256]{1,0:T(8,128)(2,1)S(1)}, u32[]{:S(2)}, u32[]{:S(2)}) collective-permute-start(bf16[384,256]{1,0:T(8,128)(2,1)S(1)} %collective-permute-done.15.refs_1_.refs_4_), channel_id=1, source_target_pairs={{0,1},{1,0},{2,3},{3,2},{4,5},{5,4},{6,7},{7,6},{8,9},{9,8},{10,11... | collective-permute-start | bytes 589832 | tf_op jit(solution)/shard_map/ppermute | solution.py:383
  68.3 1.7 %collective-permute-start.19 = (bf16[384,256]{1,0:T(8,128)(2,1)S(1)}, bf16[384,256]{1,0:T(8,128)(2,1)S(1)}, u32[]{:S(2)}, u32[]{:S(2)}) collective-permute-start(bf16[384,256]{1,0:T(8,128)(2,1)S(1)} %collective-permute-done.16.refs_2_.refs_6_), channel_id=1, source_target_pairs={{0,1},{1,0},{2,3},{3,2},{4,5},{5,4},{6,7},{7,6},{8,9},{9,8},{10,11... | collective-permute-start | bytes 589832 | tf_op jit(solution)/shard_map/ppermute | solution.py:383

commit v14 on v13

--- a/solution.py
+++ b/solution.py
@@ -289,19 +289,21 @@
         gp_outs[b][...] = joined[b * rows : (b + 1) * rows]
 
 
-def row_finish(sites, haps, idx, hap, feats, gain, w_t, gp, *refs):
-    gps, parts = refs[: sites - 1], refs[sites - 1 : sites - 1 + haps // 2]
-    out_ref, gf_ref, og = refs[sites - 1 + haps // 2 :]
+def row_finish(sites, haps, final, idx, hap, feats, gain, w_t, gp, *refs):
+    gps, (kept, last, out_ref, gf_ref, og) = refs[: sites - 1], refs[sites - 1 :]
     me = idx[0]
     rows, width = feats.shape
     group = width // sites
     per = rows // haps
-    for m in range(haps // 2):
-        base = parts[m].shape[0] - 4 * per
+    inner = len(final) // 2
+    for place, (m, _) in enumerate(final):
+        source, base = kept, 4 * per * place
+        if place >= inner:
+            source, base = last, last.shape[0] - 4 * per * (len(final) - place)
         for j in range(2):
             for side in range(2):
                 start = base + (2 * j + side) * per
-                og[side, hap[0] ^ (2 * m + j)] = parts[m][start : start + per, :].astype(F32)
+                og[side, hap[0] ^ (2 * m + j)] = source[start : start + per, :].astype(F32)
     grads = [gp[...]] + [g[g.shape[0] - rows :, : 3 * group] for g in gps]
     grad_normed = 0.0
     for k in range(sites):
@@ -320,29 +322,58 @@
     return jnp.concatenate(both, axis=0).astype(BF16)
 
 
-def weights_join(sites, row_keep, row_got, og_keep, og_got, *refs):
-    cols, (near, own, *far) = refs[:sites], refs[sites:]
+def outputs_plan(count):
+    hold, steps, bit = [(0, d) for d in range(count)], [], 1
+    while bit < count:
+        send = [h for h in hold if h[1] & bit]
+        keep = [h for h in hold if not h[1] & bit]
+        steps.append((hold, send, keep))
+        hold = keep + [(s ^ bit, d ^ bit) for s, d in send]
+        bit *= 2
+    return steps, hold
+
+
+def weights_join(sites, step, row_keep, row_got, og_keep, og_got, *refs):
+    cols, (out, kept) = refs[:sites], refs[sites:]
+    _, send, keep = step
     half, width = row_keep.shape
     depth = half + 5 * cols[0].shape[0]
+    tall = 4 * og_keep.shape[1]
     total = sum(c[...].astype(F32) for c in cols)
     tiles = [total[:, t * width : (t + 1) * width] for t in range(5)]
     rows = row_keep[...].astype(F32) + row_got[...].astype(F32)
-    near[:depth, :] = jnp.concatenate([rows] + tiles, axis=0).astype(BF16)
-    near[depth:, :] = outputs_pair(og_keep, og_got, 1, width)
-    own[...] = outputs_pair(og_keep, og_got, 0, width)
-    for j, out in enumerate(far):
-        out[...] = outputs_pair(og_keep, og_got, j + 2, width)
-
-
-def weights_add(mine, got, out):
-    depth = out.shape[0]
-    out[...] = (mine[:depth, :].astype(F32) + got[:depth, :].astype(F32)).astype(BF16)
+    out[:depth, :] = jnp.concatenate([rows] + tiles, axis=0).astype(BF16)
+    for j, (_, d) in enumerate(send):
+        start = depth + j * tall
+        out[start : start + tall, :] = outputs_pair(og_keep, og_got, d, width)
+    for j, (_, d) in enumerate(keep):
+        kept[j * tall : (j + 1) * tall, :] = outputs_pair(og_keep, og_got, d, width)
+
+
+def weights_step(step, mine, got, kept, out, kept_out):
+    hold, send, keep = step
+    tall = 2 * kept.shape[0] // len(hold)
+    depth = mine.shape[0] - kept.shape[0]
+    out[:depth, :] = (mine[:depth, :].astype(F32) + got[:depth, :].astype(F32)).astype(BF16)
+
+    def block(item):
+        place = hold.index(item)
+        inner = len(hold) // 2
+        if place < inner:
+            return kept[place * tall : (place + 1) * tall, :]
+        start = depth + (place - inner) * tall
+        return got[start : start + tall, :]
+
+    for j, item in enumerate(send):
+        out[depth + j * tall : depth + (j + 1) * tall, :] = block(item)
+    for j, item in enumerate(keep):
+        kept_out[j * tall : (j + 1) * tall, :] = block(item)
 
 
 def weights_last(left, right, *refs):
     gps, mine, outs = refs[: len(refs) // 2], refs[len(refs) // 2], refs[len(refs) // 2 + 1 :]
     depth, width = mine.shape
-    weights_add(left, right, mine)
+    mine[...] = (left[:depth, :].astype(F32) + right[:depth, :].astype(F32)).astype(BF16)
     for gp, out in zip(gps, outs):
         out[:depth, :] = mine[...]
         out[depth:, : gp.shape[1]] = gp[...]
@@ -475,19 +506,21 @@
     )
     row_got = swapped(row_send, "hap", 1)
     depth = 3 * group // 2 + 5 * half // sites
-    near, own, *far = call(
-        functools.partial(weights_join, sites),
-        [((depth + 4 * per, width), BF16)] + [((4 * per, width), BF16)] * (haps // 2 - 1),
+    steps, final = outputs_plan(haps // 2)
+    moving, staying = 2 * per * (haps // 2), 2 * per * (haps // 2)
+    left, kept = call(
+        functools.partial(weights_join, sites, steps[0]),
+        [((depth + moving, width), BF16), ((staying, width), BF16)],
         row_keep, row_got, og_keep, og_got, *cols,
     )
-    near_got = swapped(near, "hap", 2)
-    far = [swapped(x, "hap", 2 * (j + 2)) for j, x in enumerate(far)]
-    near_got, far = lax.optimization_barrier((near_got, far))
-    parts = [own, near_got] + list(far)
-    left, right, step = near, near_got, 2
-    while 2 * step < haps:
-        (left,) = call(weights_add, [((depth, width), BF16)], left, right)
-        right, step = swapped(left, "hap", 2 * step), 2 * step
+    right = swapped(left, "hap", 2)
+    for j, step in enumerate(steps[1:]):
+        left, kept = call(
+            functools.partial(weights_step, step),
+            [((depth + moving, width), BF16), ((staying, width), BF16)],
+            left, right, kept,
+        )
+        right = swapped(left, "hap", 4 * 2**j)
     mine, *sends = call(
         weights_last,
         [((depth, width), BF16)] + [((depth + rows, width), BF16)] * (sites - 1),
@@ -498,9 +531,9 @@
     got[0], mine_swapped = lax.optimization_barrier((got[0], mine_swapped))
     full = [mine, mine_swapped] + [x for p in got for x in (p, swapped(p, "hap", 1))]
     out, grad = call(
-        functools.partial(row_finish, sites, haps),
+        functools.partial(row_finish, sites, haps, final),
         [((rows, width), BF16)] * 2,
-        idx, hap, feats, gains, w_t, gps[0], *got, *parts, scalars=2,
+        idx, hap, feats, gains, w_t, gps[0], *got, kept, right, scalars=2,
         scratch=[pltpu.VMEM((2, haps, per, width), F32)],
     )
     rp, ro, cp, co = call(

time: 71.8 us -> 74.7 us (1.040)
  waiting for transfers between devices: 29.9 us -> 35.6 us
  starting transfers between devices: 24.8 us -> 22 us
    ppermute x20 -> x18, waiting for transfers between devices: 20.9 us -> 26.6 us  [swapped(): return lax.ppermute(value, axis, [(i, i ^ by) for i in range(length)])]
    ppermute x20 -> x18, starting transfers between devices: 17.2 us -> 14.4 us  [swapped(): return lax.ppermute(value, axis, [(i, i ^ by) for i in range(length)])]
  transfers between devices with their start and end apart: 22 -> 20, of which waited for: 12 -> 11; matrix products, arithmetic and copies ran while one was open for 0% -> 0% of each run, Pallas kernels for 6% -> 6%
where the time goes in v14:
time: 74.7 us; the launch traced here: 74.4 us
  waiting for transfers between devices  35.6 us (48%)
  starting transfers between devices  22 us (29%)
  Pallas kernels  12.4 us (17%)
  local copies, waits for them, and re-layouts  3.62 us (5%)
  between operations  0.82 us (1%)
    ppermute x18, waiting for transfers between devices, swapped(): return lax.ppermute(value, axis, [(i, i ^ by) for i in range(length)])  26.6 us
    ppermute x18, starting transfers between devices, swapped(): return lax.ppermute(value, axis, [(i, i ^ by) for i in range(length)])  14.4 us
    pallas_call x11, Pallas kernels, call(): pl.pallas_call(body, out_shape=[jax.ShapeDtypeStruct(s, d) for s, d in ou...  12.4 us
    all_to_all x2, waiting for transfers between devices, exchange(): return lax.all_to_all(value, axis, 0, 0, tiled=True)  8.95 us
    all_to_all x2, starting transfers between devices, exchange(): return lax.all_to_all(value, axis, 0, 0, tiled=True)  7.56 us
    unnamed x24, local copies, waits for them, and re-layouts  2.67 us
  transfers between devices with their start and end apart: 20, of which 11 were waited for; matrix products, arithmetic and copies ran while one was open for 0% of the time, Pallas kernels for 6%

profile of v14, /device:TPU:0, one launch (start us, length us, event | category | flops | bytes accessed | tf_op | source)
XLA Modules:
  0.0 74.4 jit_solution(2826868856223570380)
XLA Ops:
  0.6 4.0 %collective-permute-start.2 = (bf16[128,256]{1,0:T(8,128)(2,1)}, bf16[128,256]{1,0:T(8,128)(2,1)S(1)}, u32[]{:S(2)}, u32[]{:S(2)}) collective-permute-start(bf16[128,256]{1,0:T(8,128)(2,1)} %bitcast.14), channel_id=1, source_target_pairs={{0,24},{8,16},{16,8},{24,0},{1,25},{9,17},{17,9},{25,1},{2,26},{10... | collective-permute-start | bytes 196616 | tf_op jit(solution)/shard_map/ppermute | solution.py:414
  4.6 0.5 collective-permute-start.1
  5.1 0.1 collective-permute-start
  5.2 0.7 copy-done.8
  5.9 0.9 %slice-done = bf16[256,512]{1,0:T(8,128)(2,1)S(1)} async-done(((bf16[256,768]{1,0:T(8,128)(2,1)}), bf16[256,512]{1,0:T(8,128)(2,1)S(1)}, s32[]{:S(2)}) %slice-start) | async-done | bytes 262168 | tf_op jit(solution)/shard_map/slice | solution.py:449
  6.9 0.1 copy.17
  7.0 0.0 copy-start.10
  7.0 0.0 copy-start.1
  7.1 0.2 copy.15
  7.3 0.4 copy-done.10
  7.7 0.2 copy-done.9
  7.9 1.1 %collective-permute-done.1.refs_2_ = bf16[128,256]{1,0:T(8,128)(2,1)S(1)} collective-permute-done((bf16[128,256]{1,0:T(8,128)(2,1)}, bf16[128,256]{1,0:T(8,128)(2,1)S(1)}, u32[]{:S(2)}, u32[]{:S(2)}) %collective-permute-start.1) | collective-permute-done | bytes 65568 | tf_op jit(solution)/shard_map/ppermute | solution.py:414
  9.1 0.5 collective-permute-done.refs_1_
  9.6 2.8 %shard_map.136 = (bf16[8,16,768]{2,1,0:T(8,128)(2,1)}, bf16[512,256]{1,0:T(8,128)(2,1)S(1)}) custom-call(s32[1]{0:T(128)} %bitcast.idx, s32[4,4]{1,0:T(4,128)S(1)} %compare_select_fusion.link, bf16[128,256]{1,0:T(8,128)(2,1)S(1)} %bitcast.17, bf16[128,256]{1,0:T(8,128)(2,1)S(1)} %collective-permute-done.refs_1_, ...), custom_call_target="tpu_custom_call" | custom-call | flops 1 | bytes 1 | tf_op jit(solution)/shard_map/pallas_call | solution.py:82
  12.4 4.9 %all-to-all-start = ((bf16[8,16,768]{2,1,0:T(8,128)(2,1)}), bf16[8,16,768]{2,1,0:T(8,128)(2,1)S(1)}, u32[]{:S(2)}, u32[]{:S(2)}) async-start(bf16[8,16,768]{2,1,0:T(8,128)(2,1)} %get-tuple-element.46), calls=%async_computation | async-start | bytes 393216 | tf_op jit(solution)/shard_map/all_to_all | solution.py:409
  17.3 0.0 copy-start.5
  17.3 1.8 %shard_map.137 = (bf16[512,1024]{1,0:T(8,128)(2,1)S(1)}, bf16[512,64]{1,0:T(8,128)(2,1)S(1)}, bf16[512,64]{1,0:T(8,128)(2,1)S(1)}, bf16[64,512]{1,0:T(8,128)(2,1)S(1)}) custom-call(s32[1]{0:T(128)} %bitcast.idx, s32[4,4]{1,0:T(4,128)S(1)} %compare_select_fusion.link, bf16[512,256]{1,0:T(8,128)(2,1)S(1)} %get-tuple-element.47.normed_ref.normed, ...), custom_call_target="tpu_custom_call" | custom-call | flops 20000000000 | bytes 72000000 | tf_op jit(solution)/shard_map/pallas_call | solution.py:82
  19.1 6.5 %all-to-all-done.x_in = bf16[8,16,768]{2,1,0:T(8,128)(2,1)S(1)} async-done(((bf16[8,16,768]{2,1,0:T(8,128)(2,1)}), bf16[8,16,768]{2,1,0:T(8,128)(2,1)S(1)}, u32[]{:S(2)}, u32[]{:S(2)}) %all-to-all-start) | async-done | bytes 196640 | tf_op jit(solution)/shard_map/all_to_all | solution.py:409
  25.7 3.2 %shard_map.138 = (bf16[32,8,128]{2,1,0:T(8,128)(2,1)}, bf16[128,1280]{1,0:T(8,128)(2,1)S(1)}, bf16[128,1280]{1,0:T(8,128)(2,1)}, bf16[8,16,512]{2,1,0:T(8,128)(2,1)}) custom-call(s32[1]{0:T(128)} %bitcast.1.hap, bf16[8,16,768]{2,1,0:T(8,128)(2,1)S(1)} %all-to-all-done.x_in, bf16[256,256]{1,0:T(8,128)(2,1)S(1)} %copy-done.1, ...), custom_call_target="tpu_custom_call" | custom-call | flops 1 | bytes 1 | tf_op jit(solution)/shard_map/pallas_call | solution.py:82
  28.9 0.0 copy-start.4
  28.9 0.1 collective-permute-start.3
  29.0 2.7 %all-to-all-start.1 = ((bf16[32,8,128]{2,1,0:T(8,128)(2,1)}), bf16[32,8,128]{2,1,0:T(8,128)(2,1)S(1)}, u32[]{:S(2)}, u32[]{:S(2)}) async-start(bf16[32,8,128]{2,1,0:T(8,128)(2,1)} %get-tuple-element.50), calls=%async_computation.1 | async-start | bytes 131072 | tf_op jit(solution)/shard_map/all_to_all | solution.py:409
  31.7 0.3 collective-permute-start.4
  32.0 1.0 %copy-done.2 = bf16[128,1280]{1,0:T(8,128)(2,1)S(1)} copy-done((bf16[128,1280]{1,0:T(8,128)(2,1)S(1)}, bf16[128,1280]{1,0:T(8,128)(2,1)}, u32[]{:S(2)}) %copy-start.2) | copy-done | bytes 327704
  33.0 0.2 shard_map.139
  33.2 1.7 %collective-permute-start.6 = (bf16[32,1280]{1,0:T(8,128)(2,1)S(1)}, bf16[32,1280]{1,0:T(8,128)(2,1)S(1)}, u32[]{:S(2)}, u32[]{:S(2)}) collective-permute-start(bf16[32,1280]{1,0:T(8,128)(2,1)S(1)} %get-tuple-element.54), channel_id=1, source_target_pairs={{0,8},{8,0},{16,24},{24,16},{1,9},{9,1},{17,25},{25,17},{2,10},{10... | collective-permute-start | bytes 245768 | tf_op jit(solution)/shard_map/ppermute | solution.py:414
  34.9 1.5 %collective-permute-start.7 = (bf16[32,1280]{1,0:T(8,128)(2,1)S(1)}, bf16[32,1280]{1,0:T(8,128)(2,1)S(1)}, u32[]{:S(2)}, u32[]{:S(2)}) collective-permute-start(bf16[32,1280]{1,0:T(8,128)(2,1)S(1)} %get-tuple-element.55), channel_id=1, source_target_pairs={{0,16},{8,24},{16,0},{24,8},{1,17},{9,25},{17,1},{25,9},{2,18},{10... | collective-permute-start | bytes 245768 | tf_op jit(solution)/shard_map/ppermute | solution.py:414
  36.4 0.3 collective-permute-start.8
  36.7 2.4 %all-to-all-done.1.g_in = bf16[32,8,128]{2,1,0:T(8,128)(2,1)S(1)} async-done(((bf16[32,8,128]{2,1,0:T(8,128)(2,1)}), bf16[32,8,128]{2,1,0:T(8,128)(2,1)S(1)}, u32[]{:S(2)}, u32[]{:S(2)}) %all-to-all-start.1) | async-done | bytes 65568 | tf_op jit(solution)/shard_map/all_to_all | solution.py:409
  39.2 1.7 %shard_map.141 = (bf16[128,192]{1,0:T(8,128)(2,1)S(1)}, bf16[128,192]{1,0:T(8,128)(2,1)S(1)}, bf16[128,192]{1,0:T(8,128)(2,1)S(1)}, bf16[128,192]{1,0:T(8,128)(2...) custom-call(s32[1]{0:T(128)} %bitcast.idx, s32[1]{0:T(128)S(6)} %select_n.11.core, ...), custom_call_target="tpu_custom_call" | custom-call | flops 1 | bytes 1 | tf_op jit(solution)/shard_map/pallas_call | solution.py:82
  40.9 0.1 collective-permute-start.5
  41.0 1.2 %collective-permute-done.5.row_got = bf16[96,256]{1,0:T(8,128)(2,1)S(1)} collective-permute-done((bf16[96,256]{1,0:T(8,128)(2,1)S(1)}, bf16[96,256]{1,0:T(8,128)(2,1)S(1)}, u32[]{:S(2)}, u32[]{:S(2)}) %collective-permute-start.5) | collective-permute-done | bytes 49184 | tf_op jit(solution)/shard_map/ppermute | solution.py:414
  42.2 0.1 shard_map.142
  42.2 1.1 %collective-permute-start.9 = (bf16[384,256]{1,0:T(8,128)(2,1)S(1)}, bf16[384,256]{1,0:T(8,128)(2,1)S(1)}, u32[]{:S(2)}, u32[]{:S(2)}) collective-permute-start(bf16[384,256]{1,0:T(8,128)(2,1)S(1)} %get-tuple-element.67.mine), channel_id=1, source_target_pairs={{0,2},{1,3},{2,0},{3,1},{4,6},{5,7},{6,4},{7,5},{8,10},{9,11},{10,... | collective-permute-start | bytes 589832 | tf_op jit(solution)/shard_map/ppermute | solution.py:414
  43.3 6.0 %collective-permute-done.9.got = bf16[384,256]{1,0:T(8,128)(2,1)S(1)} collective-permute-done((bf16[384,256]{1,0:T(8,128)(2,1)S(1)}, bf16[384,256]{1,0:T(8,128)(2,1)S(1)}, u32[]{:S(2)}, u32[]{:S(2)}) %collective-permute-start.9) | collective-permute-done | bytes 196640 | tf_op jit(solution)/shard_map/ppermute | solution.py:414
  49.3 0.7 collective-permute-start.10
  50.0 9.7 %collective-permute-done.10.right.refs_4_ = bf16[384,256]{1,0:T(8,128)(2,1)S(1)} collective-permute-done((bf16[384,256]{1,0:T(8,128)(2,1)S(1)}, bf16[384,256]{1,0:T(8,128)(2,1)S(1)}, u32[]{:S(2)}, u32[]{:S(2)}) %collective-permute-start.10) | collective-permute-done | bytes 196640 | tf_op jit(solution)/shard_map/ppermute | solution.py:414
  59.7 0.1 shard_map.144
  59.8 0.7 collective-permute-start.11
  60.5 1.5 %collective-permute-start.13 = (bf16[384,256]{1,0:T(8,128)(2,1)S(1)}, bf16[384,256]{1,0:T(8,128)(2,1)S(1)}, u32[]{:S(2)}, u32[]{:S(2)}) collective-permute-start(bf16[384,256]{1,0:T(8,128)(2,1)S(1)} %get-tuple-element.76), channel_id=1, source_target_pairs={{0,16},{8,24},{16,0},{24,8},{1,17},{9,25},{17,1},{25,9},{2,18},{10... | collective-permute-start | bytes 589832 | tf_op jit(solution)/shard_map/ppermute | solution.py:414
  62.0 1.3 %collective-permute-start.14 = (bf16[384,256]{1,0:T(8,128)(2,1)S(1)}, bf16[384,256]{1,0:T(8,128)(2,1)S(1)}, u32[]{:S(2)}, u32[]{:S(2)}) collective-permute-start(bf16[384,256]{1,0:T(8,128)(2,1)S(1)} %get-tuple-element.77), channel_id=1, source_target_pairs={{0,24},{8,16},{16,8},{24,0},{1,25},{9,17},{17,9},{25,1},{2,26},{10... | collective-permute-start | bytes 589832 | tf_op jit(solution)/shard_map/ppermute | solution.py:414
  63.4 1.3 %collective-permute-done.12.refs_1_ = bf16[256,256]{1,0:T(8,128)(2,1)S(1)} collective-permute-done((bf16[256,256]{1,0:T(8,128)(2,1)S(1)}, bf16[256,256]{1,0:T(8,128)(2,1)S(1)}, u32[]{:S(2)}, u32[]{:S(2)}) %collective-permute-start.12) | collective-permute-done | bytes 131104 | tf_op jit(solution)/shard_map/ppermute | solution.py:414
  64.7 2.9 %collective-permute-done.11.refs_0_.refs_2_ = bf16[384,256]{1,0:T(8,128)(2,1)S(1)} collective-permute-done((bf16[384,256]{1,0:T(8,128)(2,1)S(1)}, bf16[384,256]{1,0:T(8,128)(2,1)S(1)}, u32[]{:S(2)}, u32[]{:S(2)}) %collective-permute-start.11) | collective-permute-done | bytes 196640 | tf_op jit(solution)/shard_map/ppermute | solution.py:414
  67.6 3.5 %collective-permute-done.13.refs_1_.refs_4_ = bf16[384,256]{1,0:T(8,128)(2,1)S(1)} collective-permute-done((bf16[384,256]{1,0:T(8,128)(2,1)S(1)}, bf16[384,256]{1,0:T(8,128)(2,1)S(1)}, u32[]{:S(2)}, u32[]{:S(2)}) %collective-permute-start.13) | collective-permute-done | bytes 196640 | tf_op jit(solution)/shard_map/ppermute | solution.py:414
  71.2 0.5 collective-permute-start.17
  71.7 1.0 %shard_map.145 = (bf16[128,256]{1,0:T(8,128)(2,1)}, bf16[128,256]{1,0:T(8,128)(2,1)}) custom-call(s32[1]{0:T(128)} %bitcast.idx, s32[1]{0:T(128)} %bitcast.1.hap, bf16[128,256]{1,0:T(8,128)(2,1)S(1)} %bitcast.18, f32[2,256]{1,0:T(2,128)S(1)} %pad_maximum_fusion.refs_5_.gain, bf16[768,256]{1,0:T(8,128)(2,1)S(1)} %bitcast.12, ...), custom_call_target="tpu_custom_call" | custom-call | flops 1 | bytes 1 | tf_op jit(solution)/shard_map/pallas_call | solution.py:82
  72.7 0.2 collective-permute-done.17.refs_7_
  72.9 1.5 %shard_map.146 = (f32[256,768]{1,0:T(8,128)}, f32[256,256]{1,0:T(8,128)}, f32[256,768]{1,0:T(8,128)}, f32[256,256]{1,0:T(8,128)}) custom-call(s32[1]{0:T(128)} %bitcast.idx, s32[1]{0:T(128)S(6)} %select_n.11.core, bf16[256,256]{1,0:T(8,128)(2,1)S(1)} %get-tuple-element.74.refs_0_, bf16[256,256]{1,0:T(8,128)(2,1)S(1)} %collective-permute-done.12.refs_1_, ...), custom_call_target="tpu_custom_call" | custom-call | flops 1 | bytes 1 | tf_op jit(solution)/shard_map/pallas_call | solution.py:82
  (31 shorter events, 0.1 us)
Async XLA Ops:
  0.6 7.3 %collective-permute-start.2 = (bf16[128,256]{1,0:T(8,128)(2,1)}, bf16[128,256]{1,0:T(8,128)(2,1)S(1)}, u32[]{:S(2)}, u32[]{:S(2)}) collective-permute-start(bf16[128,256]{1,0:T(8,128)(2,1)} %bitcast.14), channel_id=1, source_target_pairs={{0,24},{8,16},{16,8},{24,0},{1,25},{9,17},{17,9},{25,1},{2,26},{10... | collective-permute-start | bytes 196616 | tf_op jit(solution)/shard_map/ppermute | solution.py:414
  4.6 4.5 %collective-permute-start.1 = (bf16[128,256]{1,0:T(8,128)(2,1)}, bf16[128,256]{1,0:T(8,128)(2,1)S(1)}, u32[]{:S(2)}, u32[]{:S(2)}) collective-permute-start(bf16[128,256]{1,0:T(8,128)(2,1)} %bitcast.15), channel_id=1, source_target_pairs={{0,16},{8,24},{16,0},{24,8},{1,17},{9,25},{17,1},{25,9},{2,18},{10... | collective-permute-start | bytes 196616 | tf_op jit(solution)/shard_map/ppermute | solution.py:414
  5.1 4.5 %collective-permute-start = (bf16[128,256]{1,0:T(8,128)(2,1)}, bf16[128,256]{1,0:T(8,128)(2,1)S(1)}, u32[]{:S(2)}, u32[]{:S(2)}) collective-permute-start(bf16[128,256]{1,0:T(8,128)(2,1)} %bitcast.16), channel_id=1, source_target_pairs={{0,8},{8,0},{16,24},{24,16},{1,9},{9,1},{17,25},{25,17},{2,10},{10... | collective-permute-start | bytes 196616 | tf_op jit(solution)/shard_map/ppermute | solution.py:414
  5.2 0.7 copy-start.8
  5.9 0.9 %slice-start = ((bf16[256,768]{1,0:T(8,128)(2,1)}), bf16[256,512]{1,0:T(8,128)(2,1)S(1)}, s32[]{:S(2)}) async-start(bf16[256,768]{1,0:T(8,128)(2,1)} %col_proj.1), calls=%async_computation.2 | async-start | bytes 524288 | tf_op jit(solution)/shard_map/slice | solution.py:449
  5.9 1.1 %copy-start.7 = (bf16[256,768]{1,0:T(8,128)(2,1)S(1)}, bf16[256,768]{1,0:T(8,128)(2,1)}, u32[]{:S(2)}) copy-start(bf16[256,768]{1,0:T(8,128)(2,1)} %param.12) | copy-start | bytes 1179652
  7.0 0.7 copy-start.10
  7.0 2.5 %copy-start.1 = (bf16[256,256]{1,0:T(8,128)(2,1)S(1)}, bf16[256,256]{1,0:T(8,128)(2,1)}, u32[]{:S(2)}) copy-start(bf16[256,256]{1,0:T(8,128)(2,1)} %row_out.1) | copy-start | bytes 393220
  7.0 2.5 %copy-start.3 = (bf16[128,1,256]{2,0,1:T(8,128)(2,1)S(1)}, bf16[128,1,256]{2,0,1:T(8,128)(2,1)}, u32[]{:S(2)}) copy-start(bf16[128,1,256]{2,0,1:T(8,128)(2,1)} %param.9) | copy-start | bytes 196612
  7.1 2.5 %copy-start.6 = (bf16[128,1,256]{2,0,1:T(8,128)(2,1)S(1)}, bf16[128,1,256]{2,0,1:T(8,128)(2,1)}, u32[]{:S(2)}) copy-start(bf16[128,1,256]{2,0,1:T(8,128)(2,1)} %param.17) | copy-start | bytes 196612
  7.2 0.7 copy-start.9
  12.4 13.2 %all-to-all-start = ((bf16[8,16,768]{2,1,0:T(8,128)(2,1)}), bf16[8,16,768]{2,1,0:T(8,128)(2,1)S(1)}, u32[]{:S(2)}, u32[]{:S(2)}) async-start(bf16[8,16,768]{2,1,0:T(8,128)(2,1)} %get-tuple-element.46), calls=%async_computation | async-start | bytes 393216 | tf_op jit(solution)/shard_map/all_to_all | solution.py:409
  17.3 8.3 %copy-start = (bf16[256,768]{1,0:T(8,128)(2,1)S(1)}, bf16[256,768]{1,0:T(8,128)(2,1)}, u32[]{:S(2)}) copy-start(bf16[256,768]{1,0:T(8,128)(2,1)} %col_proj.1) | copy-start | bytes 1179652
  17.3 8.3 %copy-start.5 = (bf16[256,256]{1,0:T(8,128)(2,1)S(1)}, bf16[256,256]{1,0:T(8,128)(2,1)}, u32[]{:S(2)}) copy-start(bf16[256,256]{1,0:T(8,128)(2,1)} %col_out.1) | copy-start | bytes 393220
  28.9 2.8 %copy-start.4 = (bf16[8,16,512]{2,1,0:T(8,128)(2,1)S(1)}, bf16[8,16,512]{2,1,0:T(8,128)(2,1)}, u32[]{:S(2)}) copy-start(bf16[8,16,512]{2,1,0:T(8,128)(2,1)} %get-tuple-element.57.og) | copy-start | bytes 393220
  28.9 3.1 %collective-permute-start.3 = (bf16[128,1280]{1,0:T(8,128)(2,1)S(1)}, bf16[128,1280]{1,0:T(8,128)(2,1)S(1)}, u32[]{:S(2)}, u32[]{:S(2)}) collective-permute-start(bf16[128,1280]{1,0:T(8,128)(2,1)S(1)} %get-tuple-element.52), channel_id=1, source_target_pairs={{0,1},{1,0},{2,3},{3,2},{4,5},{5,4},{6,7},{7,6},{8,9},{9,8},{10,11... | collective-permute-start | bytes 983048 | tf_op jit(solution)/shard_map/ppermute | solution.py:414
  29.0 10.2 %all-to-all-start.1 = ((bf16[32,8,128]{2,1,0:T(8,128)(2,1)}), bf16[32,8,128]{2,1,0:T(8,128)(2,1)S(1)}, u32[]{:S(2)}, u32[]{:S(2)}) async-start(bf16[32,8,128]{2,1,0:T(8,128)(2,1)} %get-tuple-element.50), calls=%async_computation.1 | async-start | bytes 131072 | tf_op jit(solution)/shard_map/all_to_all | solution.py:409
  31.7 5.0 %collective-permute-start.4 = (bf16[4,16,512]{2,1,0:T(8,128)(2,1)S(1)}, bf16[4,16,512]{2,1,0:T(8,128)(2,1)S(1)}, u32[]{:S(2)}, u32[]{:S(2)}) collective-permute-start(bf16[4,16,512]{2,1,0:T(8,128)(2,1)S(1)} %get-tuple-element.58), channel_id=1, source_target_pairs={{0,1},{1,0},{2,3},{3,2},{4,5},{5,4},{6,7},{7,6},{8,9},{9,8},{10,11... | collective-permute-start | bytes 196616 | tf_op jit(solution)/shard_map/ppermute | solution.py:414
  32.0 1.0 %copy-start.2 = (bf16[128,1280]{1,0:T(8,128)(2,1)S(1)}, bf16[128,1280]{1,0:T(8,128)(2,1)}, u32[]{:S(2)}) copy-start(bf16[128,1280]{1,0:T(8,128)(2,1)} %get-tuple-element.51.keep) | copy-start | bytes 983044
  33.2 9.0 %collective-permute-start.6 = (bf16[32,1280]{1,0:T(8,128)(2,1)S(1)}, bf16[32,1280]{1,0:T(8,128)(2,1)S(1)}, u32[]{:S(2)}, u32[]{:S(2)}) collective-permute-start(bf16[32,1280]{1,0:T(8,128)(2,1)S(1)} %get-tuple-element.54), channel_id=1, source_target_pairs={{0,8},{8,0},{16,24},{24,16},{1,9},{9,1},{17,25},{25,17},{2,10},{10... | collective-permute-start | bytes 245768 | tf_op jit(solution)/shard_map/ppermute | solution.py:414
  34.9 7.3 %collective-permute-start.7 = (bf16[32,1280]{1,0:T(8,128)(2,1)S(1)}, bf16[32,1280]{1,0:T(8,128)(2,1)S(1)}, u32[]{:S(2)}, u32[]{:S(2)}) collective-permute-start(bf16[32,1280]{1,0:T(8,128)(2,1)S(1)} %get-tuple-element.55), channel_id=1, source_target_pairs={{0,16},{8,24},{16,0},{24,8},{1,17},{9,25},{17,1},{25,9},{2,18},{10... | collective-permute-start | bytes 245768 | tf_op jit(solution)/shard_map/ppermute | solution.py:414
  36.4 5.8 %collective-permute-start.8 = (bf16[32,1280]{1,0:T(8,128)(2,1)S(1)}, bf16[32,1280]{1,0:T(8,128)(2,1)S(1)}, u32[]{:S(2)}, u32[]{:S(2)}) collective-permute-start(bf16[32,1280]{1,0:T(8,128)(2,1)S(1)} %get-tuple-element.56), channel_id=1, source_target_pairs={{0,24},{8,16},{16,8},{24,0},{1,25},{9,17},{17,9},{25,1},{2,26},{10... | collective-permute-start | bytes 245768 | tf_op jit(solution)/shard_map/ppermute | solution.py:414
  40.9 1.3 %collective-permute-start.5 = (bf16[96,256]{1,0:T(8,128)(2,1)S(1)}, bf16[96,256]{1,0:T(8,128)(2,1)S(1)}, u32[]{:S(2)}, u32[]{:S(2)}) collective-permute-start(bf16[96,256]{1,0:T(8,128)(2,1)S(1)} %get-tuple-element.65), channel_id=1, source_target_pairs={{0,1},{1,0},{2,3},{3,2},{4,5},{5,4},{6,7},{7,6},{8,9},{9,8},{10,11... | collective-permute-start | bytes 147464 | tf_op jit(solution)/shard_map/ppermute | solution.py:414
  42.2 7.0 %collective-permute-start.9 = (bf16[384,256]{1,0:T(8,128)(2,1)S(1)}, bf16[384,256]{1,0:T(8,128)(2,1)S(1)}, u32[]{:S(2)}, u32[]{:S(2)}) collective-permute-start(bf16[384,256]{1,0:T(8,128)(2,1)S(1)} %get-tuple-element.67.mine), channel_id=1, source_target_pairs={{0,2},{1,3},{2,0},{3,1},{4,6},{5,7},{6,4},{7,5},{8,10},{9,11},{10,... | collective-permute-start | bytes 589832 | tf_op jit(solution)/shard_map/ppermute | solution.py:414
  49.3 10.4 %collective-permute-start.10 = (bf16[384,256]{1,0:T(8,128)(2,1)S(1)}, bf16[384,256]{1,0:T(8,128)(2,1)S(1)}, u32[]{:S(2)}, u32[]{:S(2)}) collective-permute-start(bf16[384,256]{1,0:T(8,128)(2,1)S(1)} %get-tuple-element.69.left), channel_id=1, source_target_pairs={{0,4},{1,5},{2,6},{3,7},{4,0},{5,1},{6,2},{7,3},{8,12},{9,13},{10,... | collective-permute-start | bytes 589832 | tf_op jit(solution)/shard_map/ppermute | solution.py:414
  59.8 7.8 %collective-permute-start.11 = (bf16[384,256]{1,0:T(8,128)(2,1)S(1)}, bf16[384,256]{1,0:T(8,128)(2,1)S(1)}, u32[]{:S(2)}, u32[]{:S(2)}) collective-permute-start(bf16[384,256]{1,0:T(8,128)(2,1)S(1)} %get-tuple-element.73), channel_id=1, source_target_pairs={{0,8},{8,0},{16,24},{24,16},{1,9},{9,1},{17,25},{25,17},{2,10},{10... | collective-permute-start | bytes 589832 | tf_op jit(solution)/shard_map/ppermute | solution.py:414
  60.5 10.6 %collective-permute-start.13 = (bf16[384,256]{1,0:T(8,128)(2,1)S(1)}, bf16[384,256]{1,0:T(8,128)(2,1)S(1)}, u32[]{:S(2)}, u32[]{:S(2)}) collective-permute-start(bf16[384,256]{1,0:T(8,128)(2,1)S(1)} %get-tuple-element.76), channel_id=1, source_target_pairs={{0,16},{8,24},{16,0},{24,8},{1,17},{9,25},{17,1},{25,9},{2,18},{10... | collective-permute-start | bytes 589832 | tf_op jit(solution)/shard_map/ppermute | solution.py:414
  62.0 9.2 %collective-permute-start.14 = (bf16[384,256]{1,0:T(8,128)(2,1)S(1)}, bf16[384,256]{1,0:T(8,128)(2,1)S(1)}, u32[]{:S(2)}, u32[]{:S(2)}) collective-permute-start(bf16[384,256]{1,0:T(8,128)(2,1)S(1)} %get-tuple-element.77), channel_id=1, source_target_pairs={{0,24},{8,16},{16,8},{24,0},{1,25},{9,17},{17,9},{25,1},{2,26},{10... | collective-permute-start | bytes 589832 | tf_op jit(solution)/shard_map/ppermute | solution.py:414
  63.4 1.3 %collective-permute-start.12 = (bf16[256,256]{1,0:T(8,128)(2,1)S(1)}, bf16[256,256]{1,0:T(8,128)(2,1)S(1)}, u32[]{:S(2)}, u32[]{:S(2)}) collective-permute-start(bf16[256,256]{1,0:T(8,128)(2,1)S(1)} %get-tuple-element.74.refs_0_), channel_id=1, source_target_pairs={{0,1},{1,0},{2,3},{3,2},{4,5},{5,4},{6,7},{7,6},{8,9},{9,8},{10,11... | collective-permute-start | bytes 393224 | tf_op jit(solution)/shard_map/ppermute | solution.py:414
  67.6 5.0 %collective-permute-start.15 = (bf16[384,256]{1,0:T(8,128)(2,1)S(1)}, bf16[384,256]{1,0:T(8,128)(2,1)S(1)}, u32[]{:S(2)}, u32[]{:S(2)}) collective-permute-start(bf16[384,256]{1,0:T(8,128)(2,1)S(1)} %collective-permute-done.11.refs_0_.refs_2_), channel_id=1, source_target_pairs={{0,1},{1,0},{2,3},{3,2},{4,5},{5,4},{6,7},{7,6},{8,9},{9,8},{10,11... | collective-permute-start | bytes 589832 | tf_op jit(solution)/shard_map/ppermute | solution.py:414
  71.2 1.5 %collective-permute-start.16 = (bf16[384,256]{1,0:T(8,128)(2,1)S(1)}, bf16[384,256]{1,0:T(8,128)(2,1)S(1)}, u32[]{:S(2)}, u32[]{:S(2)}) collective-permute-start(bf16[384,256]{1,0:T(8,128)(2,1)S(1)} %collective-permute-done.13.refs_1_.refs_4_), channel_id=1, source_target_pairs={{0,1},{1,0},{2,3},{3,2},{4,5},{5,4},{6,7},{7,6},{8,9},{9,8},{10,11... | collective-permute-start | bytes 589832 | tf_op jit(solution)/shard_map/ppermute | solution.py:414
  71.2 1.7 %collective-permute-start.17 = (bf16[384,256]{1,0:T(8,128)(2,1)S(1)}, bf16[384,256]{1,0:T(8,128)(2,1)S(1)}, u32[]{:S(2)}, u32[]{:S(2)}) collective-permute-start(bf16[384,256]{1,0:T(8,128)(2,1)S(1)} %collective-permute-done.14.refs_2_.refs_6_), channel_id=1, source_target_pairs={{0,1},{1,0},{2,3},{3,2},{4,5},{5,4},{6,7},{7,6},{8,9},{9,8},{10,11... | collective-permute-start | bytes 589832 | tf_op jit(solution)/shard_map/ppermute | solution.py:414

commit v15 on v13

--- a/solution.py
+++ b/solution.py
@@ -339,16 +339,6 @@
     out[...] = (mine[:depth, :].astype(F32) + got[:depth, :].astype(F32)).astype(BF16)
 
 
-def weights_last(left, right, *refs):
-    gps, mine, outs = refs[: len(refs) // 2], refs[len(refs) // 2], refs[len(refs) // 2 + 1 :]
-    depth, width = mine.shape
-    weights_add(left, right, mine)
-    for gp, out in zip(gps, outs):
-        out[:depth, :] = mine[...]
-        out[depth:, : gp.shape[1]] = gp[...]
-        out[depth:, gp.shape[1] :] = jnp.zeros((gp.shape[0], width - gp.shape[1]), BF16)
-
-
 def weights_finish(sites, idx, core, *refs):
     pieces = refs[: 2 * sites]
     rp, ro, cp, co, rows_t = refs[2 * sites :]
@@ -488,21 +478,20 @@
     while 2 * step < haps:
         (left,) = call(weights_add, [((depth, width), BF16)], left, right)
         right, step = swapped(left, "hap", 2 * step), 2 * step
-    mine, *sends = call(
-        weights_last,
-        [((depth, width), BF16)] + [((depth + rows, width), BF16)] * (sites - 1),
-        left, right, *gps[1:],
-    )
-    got = [swapped(sends[k - 1], "site", k) for k in range(1, sites)]
+    gps, _ = lax.optimization_barrier((gps, left))
+    gps = [gps[0]] + [swapped(gps[k], "site", k) for k in range(1, sites)]
+    right, gps = lax.optimization_barrier((right, gps))
+    (mine,) = call(weights_add, [((depth, width), BF16)], left, right)
+    got = [swapped(mine, "site", k) for k in range(1, sites)]
     mine_swapped = swapped(mine, "hap", 1)
-    got[0], mine_swapped = lax.optimization_barrier((got[0], mine_swapped))
-    full = [mine, mine_swapped] + [x for p in got for x in (p, swapped(p, "hap", 1))]
     out, grad = call(
         functools.partial(row_finish, sites, haps),
         [((rows, width), BF16)] * 2,
-        idx, hap, feats, gains, w_t, gps[0], *got, *parts, scalars=2,
+        idx, hap, feats, gains, w_t, *gps, *parts, scalars=2,
         scratch=[pltpu.VMEM((2, haps, per, width), F32)],
     )
+    got, mine_swapped, out = lax.optimization_barrier((got, mine_swapped, out))
+    full = [mine, mine_swapped] + [x for p in got for x in (p, swapped(p, "hap", 1))]
     rp, ro, cp, co = call(
         functools.partial(weights_finish, sites),
         [((width, 3 * width), F32), ((width, width), F32)] * 2,

time: 71.8 us -> 71.4 us (level)
  waiting for transfers between devices: 29.9 us -> 25.8 us
  starting transfers between devices: 24.8 us -> 28.2 us
    ppermute x20 -> x23, waiting for transfers between devices: 20.9 us -> 16.8 us  [swapped(): return lax.ppermute(value, axis, [(i, i ^ by) for i in range(length)])]
    ppermute x20 -> x23, starting transfers between devices: 17.2 us -> 20.7 us  [swapped(): return lax.ppermute(value, axis, [(i, i ^ by) for i in range(length)])]
    unnamed x24 -> x22, local copies, waits for them, and re-layouts: 2.67 us -> 2.99 us
  transfers between devices with their start and end apart: 22 -> 25, of which waited for: 12 -> 15; matrix products, arithmetic and copies ran while one was open for 0% -> 2% of each run, Pallas kernels for 6% -> 7%
where the time goes in v15:
time: 71.4 us; the launch traced here: 71.1 us
  starting transfers between devices  28.2 us (39%)
  waiting for transfers between devices  25.8 us (36%)
  Pallas kernels  12.3 us (17%)
  local copies, waits for them, and re-layouts  3.94 us (6%)
  between operations  0.83 us (1%)
    ppermute x23, starting transfers between devices, swapped(): return lax.ppermute(value, axis, [(i, i ^ by) for i in range(length)])  20.7 us
    ppermute x23, waiting for transfers between devices, swapped(): return lax.ppermute(value, axis, [(i, i ^ by) for i in range(length)])  16.8 us
    pallas_call x11, Pallas kernels, call(): pl.pallas_call(body, out_shape=[jax.ShapeDtypeStruct(s, d) for s, d in ou...  12.3 us
    all_to_all x2, waiting for transfers between devices, exchange(): return lax.all_to_all(value, axis, 0, 0, tiled=True)  8.98 us
    all_to_all x2, starting transfers between devices, exchange(): return lax.all_to_all(value, axis, 0, 0, tiled=True)  7.46 us
    unnamed x22, local copies, waits for them, and re-layouts  2.99 us
  transfers between devices with their start and end apart: 25, of which 15 were waited for; matrix products, arithmetic and copies ran while one was open for 2% of the time, Pallas kernels for 7%

profile of v15, /device:TPU:0, one launch (start us, length us, event | category | flops | bytes accessed | tf_op | source)
XLA Modules:
  0.0 71.1 jit_solution(5097024051002897267)
XLA Ops:
  0.6 3.0 %collective-permute-start = (bf16[128,256]{1,0:T(8,128)(2,1)}, bf16[128,256]{1,0:T(8,128)(2,1)S(1)}, u32[]{:S(2)}, u32[]{:S(2)}) collective-permute-start(bf16[128,256]{1,0:T(8,128)(2,1)} %bitcast.14), channel_id=1, source_target_pairs={{0,8},{8,0},{16,24},{24,16},{1,9},{9,1},{17,25},{25,17},{2,10},{10... | collective-permute-start | bytes 196616 | tf_op jit(solution)/shard_map/ppermute | solution.py:373
  3.6 1.5 %collective-permute-start.1 = (bf16[128,256]{1,0:T(8,128)(2,1)}, bf16[128,256]{1,0:T(8,128)(2,1)S(1)}, u32[]{:S(2)}, u32[]{:S(2)}) collective-permute-start(bf16[128,256]{1,0:T(8,128)(2,1)} %bitcast.15), channel_id=1, source_target_pairs={{0,16},{8,24},{16,0},{24,8},{1,17},{9,25},{17,1},{25,9},{2,18},{10... | collective-permute-start | bytes 196616 | tf_op jit(solution)/shard_map/ppermute | solution.py:373
  5.2 1.2 %copy.15 = bf16[256,768]{0,1:T(8,128)(2,1)S(1)} copy(bf16[256,768]{1,0:T(8,128)(2,1)} %param.12) | data formatting | bytes 786432 | tf_op args[3]
  6.4 0.9 %slice-done = bf16[256,512]{1,0:T(8,128)(2,1)S(1)} async-done(((bf16[256,768]{1,0:T(8,128)(2,1)}), bf16[256,512]{1,0:T(8,128)(2,1)S(1)}, s32[]{:S(2)}) %slice-start) | async-done | bytes 262168 | tf_op jit(solution)/shard_map/slice | solution.py:408
  7.4 0.1 copy.17
  7.5 0.5 copy-done.9
  8.0 0.2 copy-done.8
  8.2 2.3 %collective-permute-done.2.refs_3_ = bf16[128,256]{1,0:T(8,128)(2,1)S(1)} collective-permute-done((bf16[128,256]{1,0:T(8,128)(2,1)}, bf16[128,256]{1,0:T(8,128)(2,1)S(1)}, u32[]{:S(2)}, u32[]{:S(2)}) %collective-permute-start.2) | collective-permute-done | bytes 65568 | tf_op jit(solution)/shard_map/ppermute | solution.py:373
  10.5 2.8 %shard_map.136 = (bf16[8,16,768]{2,1,0:T(8,128)(2,1)}, bf16[512,256]{1,0:T(8,128)(2,1)S(1)}) custom-call(s32[1]{0:T(128)} %bitcast.idx, s32[4,4]{1,0:T(4,128)S(1)} %compare_select_fusion.link, bf16[128,256]{1,0:T(8,128)(2,1)S(1)} %bitcast.17, bf16[128,256]{1,0:T(8,128)(2,1)S(1)} %collective-permute-done.refs_1_, ...), custom_call_target="tpu_custom_call" | custom-call | flops 1 | bytes 1 | tf_op jit(solution)/shard_map/pallas_call | solution.py:82
  13.4 4.9 %all-to-all-start = ((bf16[8,16,768]{2,1,0:T(8,128)(2,1)}), bf16[8,16,768]{2,1,0:T(8,128)(2,1)S(1)}, u32[]{:S(2)}, u32[]{:S(2)}) async-start(bf16[8,16,768]{2,1,0:T(8,128)(2,1)} %get-tuple-element.57), calls=%async_computation | async-start | bytes 393216 | tf_op jit(solution)/shard_map/all_to_all | solution.py:368
  18.3 1.8 %shard_map.137 = (bf16[512,1024]{1,0:T(8,128)(2,1)S(1)}, bf16[512,64]{1,0:T(8,128)(2,1)S(1)}, bf16[512,64]{1,0:T(8,128)(2,1)S(1)}, bf16[64,512]{1,0:T(8,128)(2,1)S(1)}) custom-call(s32[1]{0:T(128)} %bitcast.idx, s32[4,4]{1,0:T(4,128)S(1)} %compare_select_fusion.link, bf16[512,256]{1,0:T(8,128)(2,1)S(1)} %get-tuple-element.58.normed_ref.normed, ...), custom_call_target="tpu_custom_call" | custom-call | flops 20000000000 | bytes 72000000 | tf_op jit(solution)/shard_map/pallas_call | solution.py:82
  20.1 6.5 %all-to-all-done.x_in = bf16[8,16,768]{2,1,0:T(8,128)(2,1)S(1)} async-done(((bf16[8,16,768]{2,1,0:T(8,128)(2,1)}), bf16[8,16,768]{2,1,0:T(8,128)(2,1)S(1)}, u32[]{:S(2)}, u32[]{:S(2)}) %all-to-all-start) | async-done | bytes 196640 | tf_op jit(solution)/shard_map/all_to_all | solution.py:368
  26.6 3.2 %shard_map.138 = (bf16[32,8,128]{2,1,0:T(8,128)(2,1)}, bf16[128,1280]{1,0:T(8,128)(2,1)S(1)}, bf16[128,1280]{1,0:T(8,128)(2,1)}, bf16[8,16,512]{2,1,0:T(8,128)(2,1)}) custom-call(s32[1]{0:T(128)} %bitcast.1.hap, bf16[8,16,768]{2,1,0:T(8,128)(2,1)S(1)} %all-to-all-done.x_in, bf16[256,256]{1,0:T(8,128)(2,1)S(1)} %copy-done.1, ...), custom_call_target="tpu_custom_call" | custom-call | flops 1 | bytes 1 | tf_op jit(solution)/shard_map/pallas_call | solution.py:82
  29.8 0.1 collective-permute-start.3
  29.9 2.6 %all-to-all-start.1 = ((bf16[32,8,128]{2,1,0:T(8,128)(2,1)}), bf16[32,8,128]{2,1,0:T(8,128)(2,1)S(1)}, u32[]{:S(2)}, u32[]{:S(2)}) async-start(bf16[32,8,128]{2,1,0:T(8,128)(2,1)} %get-tuple-element.61), calls=%async_computation.1 | async-start | bytes 131072 | tf_op jit(solution)/shard_map/all_to_all | solution.py:368
  32.6 0.3 collective-permute-start.4
  32.8 1.0 %copy-done.2 = bf16[128,1280]{1,0:T(8,128)(2,1)S(1)} copy-done((bf16[128,1280]{1,0:T(8,128)(2,1)S(1)}, bf16[128,1280]{1,0:T(8,128)(2,1)}, u32[]{:S(2)}) %copy-start.2) | copy-done | bytes 327704
  33.8 0.2 shard_map.139
  34.0 1.6 %collective-permute-start.6 = (bf16[32,1280]{1,0:T(8,128)(2,1)S(1)}, bf16[32,1280]{1,0:T(8,128)(2,1)S(1)}, u32[]{:S(2)}, u32[]{:S(2)}) collective-permute-start(bf16[32,1280]{1,0:T(8,128)(2,1)S(1)} %get-tuple-element.65), channel_id=1, source_target_pairs={{0,8},{8,0},{16,24},{24,16},{1,9},{9,1},{17,25},{25,17},{2,10},{10... | collective-permute-start | bytes 245768 | tf_op jit(solution)/shard_map/ppermute | solution.py:373
  35.6 1.5 %collective-permute-start.7 = (bf16[32,1280]{1,0:T(8,128)(2,1)S(1)}, bf16[32,1280]{1,0:T(8,128)(2,1)S(1)}, u32[]{:S(2)}, u32[]{:S(2)}) collective-permute-start(bf16[32,1280]{1,0:T(8,128)(2,1)S(1)} %get-tuple-element.66), channel_id=1, source_target_pairs={{0,16},{8,24},{16,0},{24,8},{1,17},{9,25},{17,1},{25,9},{2,18},{10... | collective-permute-start | bytes 245768 | tf_op jit(solution)/shard_map/ppermute | solution.py:373
  37.1 0.4 collective-permute-start.8
  37.6 2.5 %all-to-all-done.1.g_in = bf16[32,8,128]{2,1,0:T(8,128)(2,1)S(1)} async-done(((bf16[32,8,128]{2,1,0:T(8,128)(2,1)}), bf16[32,8,128]{2,1,0:T(8,128)(2,1)S(1)}, u32[]{:S(2)}, u32[]{:S(2)}) %all-to-all-start.1) | async-done | bytes 65568 | tf_op jit(solution)/shard_map/all_to_all | solution.py:368
  40.0 1.7 %shard_map.141 = (bf16[128,192]{1,0:T(8,128)(2,1)S(1)}, bf16[128,192]{1,0:T(8,128)(2,1)S(1)}, bf16[128,192]{1,0:T(8,128)(2,1)S(1)}, bf16[128,192]{1,0:T(8,128)(2...) custom-call(s32[1]{0:T(128)} %bitcast.idx, s32[1]{0:T(128)S(6)} %select_n.11.core, ...), custom_call_target="tpu_custom_call" | custom-call | flops 1 | bytes 1 | tf_op jit(solution)/shard_map/pallas_call | solution.py:82
  41.7 0.1 collective-permute-start.5
  41.8 1.2 %collective-permute-done.5.row_got = bf16[96,256]{1,0:T(8,128)(2,1)S(1)} collective-permute-done((bf16[96,256]{1,0:T(8,128)(2,1)S(1)}, bf16[96,256]{1,0:T(8,128)(2,1)S(1)}, u32[]{:S(2)}, u32[]{:S(2)}) %collective-permute-start.5) | collective-permute-done | bytes 49184 | tf_op jit(solution)/shard_map/ppermute | solution.py:373
  43.1 1.0 %collective-permute-start.9 = (bf16[320,256]{1,0:T(8,128)(2,1)S(1)}, bf16[320,256]{1,0:T(8,128)(2,1)S(1)}, u32[]{:S(2)}, u32[]{:S(2)}) collective-permute-start(bf16[320,256]{1,0:T(8,128)(2,1)S(1)} %get-tuple-element.77.mine), channel_id=1, source_target_pairs={{0,2},{1,3},{2,0},{3,1},{4,6},{5,7},{6,4},{7,5},{8,10},{9,11},{10,... | collective-permute-start | bytes 491528 | tf_op jit(solution)/shard_map/ppermute | solution.py:373
  44.1 2.5 %collective-permute-start.10 = (bf16[64,256]{1,0:T(8,128)(2,1)S(1)}, bf16[64,256]{1,0:T(8,128)(2,1)S(1)}, u32[]{:S(2)}, u32[]{:S(2)}) collective-permute-start(bf16[64,256]{1,0:T(8,128)(2,1)S(1)} %get-tuple-element.78), channel_id=1, source_target_pairs={{0,4},{1,5},{2,6},{3,7},{4,0},{5,1},{6,2},{7,3},{8,12},{9,13},{10,... | collective-permute-start | bytes 98312 | tf_op jit(solution)/shard_map/ppermute | solution.py:373
  46.6 0.9 %collective-permute-start.11 = (bf16[64,256]{1,0:T(8,128)(2,1)S(1)}, bf16[64,256]{1,0:T(8,128)(2,1)S(1)}, u32[]{:S(2)}, u32[]{:S(2)}) collective-permute-start(bf16[64,256]{1,0:T(8,128)(2,1)S(1)} %get-tuple-element.79), channel_id=1, source_target_pairs={{0,6},{1,7},{2,4},{3,5},{4,2},{5,3},{6,0},{7,1},{8,14},{9,15},{10,... | collective-permute-start | bytes 98312 | tf_op jit(solution)/shard_map/ppermute | solution.py:373
  47.6 1.5 %collective-permute-done.10.refs_5_ = bf16[64,256]{1,0:T(8,128)(2,1)S(1)} collective-permute-done((bf16[64,256]{1,0:T(8,128)(2,1)S(1)}, bf16[64,256]{1,0:T(8,128)(2,1)S(1)}, u32[]{:S(2)}, u32[]{:S(2)}) %collective-permute-start.10) | collective-permute-done | bytes 32800 | tf_op jit(solution)/shard_map/ppermute | solution.py:373
  49.1 3.3 %collective-permute-done.11.refs_6_ = bf16[64,256]{1,0:T(8,128)(2,1)S(1)} collective-permute-done((bf16[64,256]{1,0:T(8,128)(2,1)S(1)}, bf16[64,256]{1,0:T(8,128)(2,1)S(1)}, u32[]{:S(2)}, u32[]{:S(2)}) %collective-permute-start.11) | collective-permute-done | bytes 32800 | tf_op jit(solution)/shard_map/ppermute | solution.py:373
  52.5 0.6 collective-permute-start.13
  53.1 0.9 %collective-permute-start.14 = (bf16[128,192]{1,0:T(8,128)(2,1)S(1)}, bf16[128,192]{1,0:T(8,128)(2,1)S(1)}, u32[]{:S(2)}, u32[]{:S(2)}) collective-permute-start(bf16[128,192]{1,0:T(8,128)(2,1)S(1)} %get-tuple-element.87), channel_id=1, source_target_pairs={{0,16},{8,24},{16,0},{24,8},{1,17},{9,25},{17,1},{25,9},{2,18},{10... | collective-permute-start | bytes 147464 | tf_op jit(solution)/shard_map/ppermute | solution.py:373
  53.9 2.1 %collective-permute-start.15 = (bf16[128,192]{1,0:T(8,128)(2,1)S(1)}, bf16[128,192]{1,0:T(8,128)(2,1)S(1)}, u32[]{:S(2)}, u32[]{:S(2)}) collective-permute-start(bf16[128,192]{1,0:T(8,128)(2,1)S(1)} %get-tuple-element.88), channel_id=1, source_target_pairs={{0,24},{8,16},{16,8},{24,0},{1,25},{9,17},{17,9},{25,1},{2,26},{10... | collective-permute-start | bytes 147464 | tf_op jit(solution)/shard_map/ppermute | solution.py:373
  56.0 0.8 %collective-permute-done.13.refs_0_ = bf16[128,192]{1,0:T(8,128)(2,1)S(1)} collective-permute-done((bf16[128,192]{1,0:T(8,128)(2,1)S(1)}, bf16[128,192]{1,0:T(8,128)(2,1)S(1)}, u32[]{:S(2)}, u32[]{:S(2)}) %collective-permute-start.13) | collective-permute-done | bytes 49184 | tf_op jit(solution)/shard_map/ppermute | solution.py:373
  56.8 0.5 collective-permute-done.14.refs_1_
  57.3 1.8 %collective-permute-done.15.refs_2_ = bf16[128,192]{1,0:T(8,128)(2,1)S(1)} collective-permute-done((bf16[128,192]{1,0:T(8,128)(2,1)S(1)}, bf16[128,192]{1,0:T(8,128)(2,1)S(1)}, u32[]{:S(2)}, u32[]{:S(2)}) %collective-permute-start.15) | collective-permute-done | bytes 49184 | tf_op jit(solution)/shard_map/ppermute | solution.py:373
  59.1 1.5 %collective-permute-start.16 = (bf16[256,256]{1,0:T(8,128)(2,1)S(1)}, bf16[256,256]{1,0:T(8,128)(2,1)S(1)}, u32[]{:S(2)}, u32[]{:S(2)}) collective-permute-start(bf16[256,256]{1,0:T(8,128)(2,1)S(1)} %shard_map.144.refs_0_), channel_id=1, source_target_pairs={{0,8},{8,0},{16,24},{24,16},{1,9},{9,1},{17,25},{25,17},{2,10},{10... | collective-permute-start | bytes 393224 | tf_op jit(solution)/shard_map/ppermute | solution.py:373
  60.7 1.2 %collective-permute-start.17 = (bf16[256,256]{1,0:T(8,128)(2,1)S(1)}, bf16[256,256]{1,0:T(8,128)(2,1)S(1)}, u32[]{:S(2)}, u32[]{:S(2)}) collective-permute-start(bf16[256,256]{1,0:T(8,128)(2,1)S(1)} %shard_map.144.refs_0_), channel_id=1, source_target_pairs={{0,16},{8,24},{16,0},{24,8},{1,17},{9,25},{17,1},{25,9},{2,18},{10... | collective-permute-start | bytes 393224 | tf_op jit(solution)/shard_map/ppermute | solution.py:373
  61.8 0.8 %collective-permute-start.18 = (bf16[256,256]{1,0:T(8,128)(2,1)S(1)}, bf16[256,256]{1,0:T(8,128)(2,1)S(1)}, u32[]{:S(2)}, u32[]{:S(2)}) collective-permute-start(bf16[256,256]{1,0:T(8,128)(2,1)S(1)} %shard_map.144.refs_0_), channel_id=1, source_target_pairs={{0,24},{8,16},{16,8},{24,0},{1,25},{9,17},{17,9},{25,1},{2,26},{10... | collective-permute-start | bytes 393224 | tf_op jit(solution)/shard_map/ppermute | solution.py:373
  62.7 1.0 %shard_map.145 = (bf16[128,256]{1,0:T(8,128)(2,1)}, bf16[128,256]{1,0:T(8,128)(2,1)}) custom-call(s32[1]{0:T(128)} %bitcast.idx, s32[1]{0:T(128)} %bitcast.1.hap, bf16[128,256]{1,0:T(8,128)(2,1)S(1)} %bitcast.18, f32[2,256]{1,0:T(2,128)S(1)} %pad_maximum_fusion.refs_5_.gain, bf16[768,256]{1,0:T(8,128)(2,1)S(1)} %bitcast.12, ...), custom_call_target="tpu_custom_call" | custom-call | flops 1 | bytes 1 | tf_op jit(solution)/shard_map/pallas_call | solution.py:82
  63.6 1.0 %collective-permute-done.16.refs_2_ = bf16[256,256]{1,0:T(8,128)(2,1)S(1)} collective-permute-done((bf16[256,256]{1,0:T(8,128)(2,1)S(1)}, bf16[256,256]{1,0:T(8,128)(2,1)S(1)}, u32[]{:S(2)}, u32[]{:S(2)}) %collective-permute-start.16) | collective-permute-done | bytes 131104 | tf_op jit(solution)/shard_map/ppermute | solution.py:373
  64.6 1.2 %collective-permute-done.17.refs_4_ = bf16[256,256]{1,0:T(8,128)(2,1)S(1)} collective-permute-done((bf16[256,256]{1,0:T(8,128)(2,1)S(1)}, bf16[256,256]{1,0:T(8,128)(2,1)S(1)}, u32[]{:S(2)}, u32[]{:S(2)}) %collective-permute-start.17) | collective-permute-done | bytes 131104 | tf_op jit(solution)/shard_map/ppermute | solution.py:373
  65.8 1.9 %collective-permute-done.18.refs_6_ = bf16[256,256]{1,0:T(8,128)(2,1)S(1)} collective-permute-done((bf16[256,256]{1,0:T(8,128)(2,1)S(1)}, bf16[256,256]{1,0:T(8,128)(2,1)S(1)}, u32[]{:S(2)}, u32[]{:S(2)}) %collective-permute-start.18) | collective-permute-done | bytes 131104 | tf_op jit(solution)/shard_map/ppermute | solution.py:373
  67.7 0.5 collective-permute-start.21
  68.2 0.8 %collective-permute-done.20.refs_3_ = bf16[256,256]{1,0:T(8,128)(2,1)S(1)} collective-permute-done((bf16[256,256]{1,0:T(8,128)(2,1)S(1)}, bf16[256,256]{1,0:T(8,128)(2,1)S(1)}, u32[]{:S(2)}, u32[]{:S(2)}) %collective-permute-start.20) | collective-permute-done | bytes 131104 | tf_op jit(solution)/shard_map/ppermute | solution.py:373
  69.1 0.2 collective-permute-done.21.refs_5_
  69.3 0.3 collective-permute-done.22.refs_7_
  69.6 1.5 %shard_map.146 = (f32[256,768]{1,0:T(8,128)}, f32[256,256]{1,0:T(8,128)}, f32[256,768]{1,0:T(8,128)}, f32[256,256]{1,0:T(8,128)}) custom-call(s32[1]{0:T(128)} %bitcast.idx, s32[1]{0:T(128)S(6)} %select_n.11.core, bf16[256,256]{1,0:T(8,128)(2,1)S(1)} %shard_map.144.refs_0_, bf16[256,256]{1,0:T(8,128)(2,1)S(1)} %collective-permute-done.19.refs_1_, ...), custom_call_target="tpu_custom_call" | custom-call | flops 1 | bytes 1 | tf_op jit(solution)/shard_map/pallas_call | solution.py:82
  (39 shorter events, 0.3 us)
Async XLA Ops:
  0.6 7.6 %collective-permute-start = (bf16[128,256]{1,0:T(8,128)(2,1)}, bf16[128,256]{1,0:T(8,128)(2,1)S(1)}, u32[]{:S(2)}, u32[]{:S(2)}) collective-permute-start(bf16[128,256]{1,0:T(8,128)(2,1)} %bitcast.14), channel_id=1, source_target_pairs={{0,8},{8,0},{16,24},{24,16},{1,9},{9,1},{17,25},{25,17},{2,10},{10... | collective-permute-start | bytes 196616 | tf_op jit(solution)/shard_map/ppermute | solution.py:373
  3.6 4.6 %collective-permute-start.1 = (bf16[128,256]{1,0:T(8,128)(2,1)}, bf16[128,256]{1,0:T(8,128)(2,1)S(1)}, u32[]{:S(2)}, u32[]{:S(2)}) collective-permute-start(bf16[128,256]{1,0:T(8,128)(2,1)} %bitcast.15), channel_id=1, source_target_pairs={{0,16},{8,24},{16,0},{24,8},{1,17},{9,25},{17,1},{25,9},{2,18},{10... | collective-permute-start | bytes 196616 | tf_op jit(solution)/shard_map/ppermute | solution.py:373
  5.2 5.4 %collective-permute-start.2 = (bf16[128,256]{1,0:T(8,128)(2,1)}, bf16[128,256]{1,0:T(8,128)(2,1)S(1)}, u32[]{:S(2)}, u32[]{:S(2)}) collective-permute-start(bf16[128,256]{1,0:T(8,128)(2,1)} %bitcast.16), channel_id=1, source_target_pairs={{0,24},{8,16},{16,8},{24,0},{1,25},{9,17},{17,9},{25,1},{2,26},{10... | collective-permute-start | bytes 196616 | tf_op jit(solution)/shard_map/ppermute | solution.py:373
  5.2 1.2 %copy-start.7 = (s32[4,4]{1,0:T(4,128)S(1)}, s32[4,4]{1,0:T(4,128)}, u32[]{:S(2)}) copy-start(s32[4,4]{1,0:T(4,128)} %param.10) | copy-start | bytes 196
  6.4 1.0 %slice-start = ((bf16[256,768]{1,0:T(8,128)(2,1)}), bf16[256,512]{1,0:T(8,128)(2,1)S(1)}, s32[]{:S(2)}) async-start(bf16[256,768]{1,0:T(8,128)(2,1)} %col_proj.1), calls=%async_computation.2 | async-start | bytes 524288 | tf_op jit(solution)/shard_map/slice | solution.py:408
  7.3 0.7 copy-start.9
  7.3 3.2 %copy-start.1 = (bf16[256,256]{1,0:T(8,128)(2,1)S(1)}, bf16[256,256]{1,0:T(8,128)(2,1)}, u32[]{:S(2)}) copy-start(bf16[256,256]{1,0:T(8,128)(2,1)} %row_out.1) | copy-start | bytes 393220
  7.3 3.2 %copy-start.3 = (bf16[128,1,256]{2,0,1:T(8,128)(2,1)S(1)}, bf16[128,1,256]{2,0,1:T(8,128)(2,1)}, u32[]{:S(2)}) copy-start(bf16[128,1,256]{2,0,1:T(8,128)(2,1)} %param.9) | copy-start | bytes 196612
  7.3 3.2 %copy-start.6 = (bf16[128,1,256]{2,0,1:T(8,128)(2,1)S(1)}, bf16[128,1,256]{2,0,1:T(8,128)(2,1)}, u32[]{:S(2)}) copy-start(bf16[128,1,256]{2,0,1:T(8,128)(2,1)} %param.17) | copy-start | bytes 196612
  7.5 0.7 copy-start.8
  13.4 13.2 %all-to-all-start = ((bf16[8,16,768]{2,1,0:T(8,128)(2,1)}), bf16[8,16,768]{2,1,0:T(8,128)(2,1)S(1)}, u32[]{:S(2)}, u32[]{:S(2)}) async-start(bf16[8,16,768]{2,1,0:T(8,128)(2,1)} %get-tuple-element.57), calls=%async_computation | async-start | bytes 393216 | tf_op jit(solution)/shard_map/all_to_all | solution.py:368
  18.3 8.3 %copy-start = (bf16[256,768]{1,0:T(8,128)(2,1)S(1)}, bf16[256,768]{1,0:T(8,128)(2,1)}, u32[]{:S(2)}) copy-start(bf16[256,768]{1,0:T(8,128)(2,1)} %col_proj.1) | copy-start | bytes 1179652
  18.3 8.3 %copy-start.5 = (bf16[256,256]{1,0:T(8,128)(2,1)S(1)}, bf16[256,256]{1,0:T(8,128)(2,1)}, u32[]{:S(2)}) copy-start(bf16[256,256]{1,0:T(8,128)(2,1)} %col_out.1) | copy-start | bytes 393220
  29.8 2.7 %copy-start.4 = (bf16[8,16,512]{2,1,0:T(8,128)(2,1)S(1)}, bf16[8,16,512]{2,1,0:T(8,128)(2,1)}, u32[]{:S(2)}) copy-start(bf16[8,16,512]{2,1,0:T(8,128)(2,1)} %get-tuple-element.68.og) | copy-start | bytes 393220
  29.8 3.0 %collective-permute-start.3 = (bf16[128,1280]{1,0:T(8,128)(2,1)S(1)}, bf16[128,1280]{1,0:T(8,128)(2,1)S(1)}, u32[]{:S(2)}, u32[]{:S(2)}) collective-permute-start(bf16[128,1280]{1,0:T(8,128)(2,1)S(1)} %get-tuple-element.63), channel_id=1, source_target_pairs={{0,1},{1,0},{2,3},{3,2},{4,5},{5,4},{6,7},{7,6},{8,9},{9,8},{10,11... | collective-permute-start | bytes 983048 | tf_op jit(solution)/shard_map/ppermute | solution.py:373
  29.9 10.1 %all-to-all-start.1 = ((bf16[32,8,128]{2,1,0:T(8,128)(2,1)}), bf16[32,8,128]{2,1,0:T(8,128)(2,1)S(1)}, u32[]{:S(2)}, u32[]{:S(2)}) async-start(bf16[32,8,128]{2,1,0:T(8,128)(2,1)} %get-tuple-element.61), calls=%async_computation.1 | async-start | bytes 131072 | tf_op jit(solution)/shard_map/all_to_all | solution.py:368
  32.6 5.0 %collective-permute-start.4 = (bf16[4,16,512]{2,1,0:T(8,128)(2,1)S(1)}, bf16[4,16,512]{2,1,0:T(8,128)(2,1)S(1)}, u32[]{:S(2)}, u32[]{:S(2)}) collective-permute-start(bf16[4,16,512]{2,1,0:T(8,128)(2,1)S(1)} %get-tuple-element.69), channel_id=1, source_target_pairs={{0,1},{1,0},{2,3},{3,2},{4,5},{5,4},{6,7},{7,6},{8,9},{9,8},{10,11... | collective-permute-start | bytes 196616 | tf_op jit(solution)/shard_map/ppermute | solution.py:373
  32.8 1.0 %copy-start.2 = (bf16[128,1280]{1,0:T(8,128)(2,1)S(1)}, bf16[128,1280]{1,0:T(8,128)(2,1)}, u32[]{:S(2)}) copy-start(bf16[128,1280]{1,0:T(8,128)(2,1)} %get-tuple-element.62.keep) | copy-start | bytes 983044
  34.0 9.0 %collective-permute-start.6 = (bf16[32,1280]{1,0:T(8,128)(2,1)S(1)}, bf16[32,1280]{1,0:T(8,128)(2,1)S(1)}, u32[]{:S(2)}, u32[]{:S(2)}) collective-permute-start(bf16[32,1280]{1,0:T(8,128)(2,1)S(1)} %get-tuple-element.65), channel_id=1, source_target_pairs={{0,8},{8,0},{16,24},{24,16},{1,9},{9,1},{17,25},{25,17},{2,10},{10... | collective-permute-start | bytes 245768 | tf_op jit(solution)/shard_map/ppermute | solution.py:373
  35.6 7.4 %collective-permute-start.7 = (bf16[32,1280]{1,0:T(8,128)(2,1)S(1)}, bf16[32,1280]{1,0:T(8,128)(2,1)S(1)}, u32[]{:S(2)}, u32[]{:S(2)}) collective-permute-start(bf16[32,1280]{1,0:T(8,128)(2,1)S(1)} %get-tuple-element.66), channel_id=1, source_target_pairs={{0,16},{8,24},{16,0},{24,8},{1,17},{9,25},{17,1},{25,9},{2,18},{10... | collective-permute-start | bytes 245768 | tf_op jit(solution)/shard_map/ppermute | solution.py:373
  37.1 5.9 %collective-permute-start.8 = (bf16[32,1280]{1,0:T(8,128)(2,1)S(1)}, bf16[32,1280]{1,0:T(8,128)(2,1)S(1)}, u32[]{:S(2)}, u32[]{:S(2)}) collective-permute-start(bf16[32,1280]{1,0:T(8,128)(2,1)S(1)} %get-tuple-element.67), channel_id=1, source_target_pairs={{0,24},{8,16},{16,8},{24,0},{1,25},{9,17},{17,9},{25,1},{2,26},{10... | collective-permute-start | bytes 245768 | tf_op jit(solution)/shard_map/ppermute | solution.py:373
  41.7 1.3 %collective-permute-start.5 = (bf16[96,256]{1,0:T(8,128)(2,1)S(1)}, bf16[96,256]{1,0:T(8,128)(2,1)S(1)}, u32[]{:S(2)}, u32[]{:S(2)}) collective-permute-start(bf16[96,256]{1,0:T(8,128)(2,1)S(1)} %get-tuple-element.75), channel_id=1, source_target_pairs={{0,1},{1,0},{2,3},{3,2},{4,5},{5,4},{6,7},{7,6},{8,9},{9,8},{10,11... | collective-permute-start | bytes 147464 | tf_op jit(solution)/shard_map/ppermute | solution.py:373
  43.1 9.2 %collective-permute-start.9 = (bf16[320,256]{1,0:T(8,128)(2,1)S(1)}, bf16[320,256]{1,0:T(8,128)(2,1)S(1)}, u32[]{:S(2)}, u32[]{:S(2)}) collective-permute-start(bf16[320,256]{1,0:T(8,128)(2,1)S(1)} %get-tuple-element.77.mine), channel_id=1, source_target_pairs={{0,2},{1,3},{2,0},{3,1},{4,6},{5,7},{6,4},{7,5},{8,10},{9,11},{10,... | collective-permute-start | bytes 491528 | tf_op jit(solution)/shard_map/ppermute | solution.py:373
  44.1 4.9 %collective-permute-start.10 = (bf16[64,256]{1,0:T(8,128)(2,1)S(1)}, bf16[64,256]{1,0:T(8,128)(2,1)S(1)}, u32[]{:S(2)}, u32[]{:S(2)}) collective-permute-start(bf16[64,256]{1,0:T(8,128)(2,1)S(1)} %get-tuple-element.78), channel_id=1, source_target_pairs={{0,4},{1,5},{2,6},{3,7},{4,0},{5,1},{6,2},{7,3},{8,12},{9,13},{10,... | collective-permute-start | bytes 98312 | tf_op jit(solution)/shard_map/ppermute | solution.py:373
  46.6 5.7 %collective-permute-start.11 = (bf16[64,256]{1,0:T(8,128)(2,1)S(1)}, bf16[64,256]{1,0:T(8,128)(2,1)S(1)}, u32[]{:S(2)}, u32[]{:S(2)}) collective-permute-start(bf16[64,256]{1,0:T(8,128)(2,1)S(1)} %get-tuple-element.79), channel_id=1, source_target_pairs={{0,6},{1,7},{2,4},{3,5},{4,2},{5,3},{6,0},{7,1},{8,14},{9,15},{10,... | collective-permute-start | bytes 98312 | tf_op jit(solution)/shard_map/ppermute | solution.py:373
  52.4 6.7 %collective-permute-start.12 = (bf16[256,256]{1,0:T(8,128)(2,1)S(1)}, bf16[256,256]{1,0:T(8,128)(2,1)S(1)}, u32[]{:S(2)}, u32[]{:S(2)}) collective-permute-start(bf16[256,256]{1,0:T(8,128)(2,1)S(1)} %shard_map.143.mine), channel_id=1, source_target_pairs={{0,4},{1,5},{2,6},{3,7},{4,0},{5,1},{6,2},{7,3},{8,12},{9,13},{10,... | collective-permute-start | bytes 393224 | tf_op jit(solution)/shard_map/ppermute | solution.py:373
  52.5 4.3 %collective-permute-start.13 = (bf16[128,192]{1,0:T(8,128)(2,1)S(1)}, bf16[128,192]{1,0:T(8,128)(2,1)S(1)}, u32[]{:S(2)}, u32[]{:S(2)}) collective-permute-start(bf16[128,192]{1,0:T(8,128)(2,1)S(1)} %get-tuple-element.86), channel_id=1, source_target_pairs={{0,8},{8,0},{16,24},{24,16},{1,9},{9,1},{17,25},{25,17},{2,10},{10... | collective-permute-start | bytes 147464 | tf_op jit(solution)/shard_map/ppermute | solution.py:373
  53.1 4.3 %collective-permute-start.14 = (bf16[128,192]{1,0:T(8,128)(2,1)S(1)}, bf16[128,192]{1,0:T(8,128)(2,1)S(1)}, u32[]{:S(2)}, u32[]{:S(2)}) collective-permute-start(bf16[128,192]{1,0:T(8,128)(2,1)S(1)} %get-tuple-element.87), channel_id=1, source_target_pairs={{0,16},{8,24},{16,0},{24,8},{1,17},{9,25},{17,1},{25,9},{2,18},{10... | collective-permute-start | bytes 147464 | tf_op jit(solution)/shard_map/ppermute | solution.py:373
  53.9 5.2 %collective-permute-start.15 = (bf16[128,192]{1,0:T(8,128)(2,1)S(1)}, bf16[128,192]{1,0:T(8,128)(2,1)S(1)}, u32[]{:S(2)}, u32[]{:S(2)}) collective-permute-start(bf16[128,192]{1,0:T(8,128)(2,1)S(1)} %get-tuple-element.88), channel_id=1, source_target_pairs={{0,24},{8,16},{16,8},{24,0},{1,25},{9,17},{17,9},{25,1},{2,26},{10... | collective-permute-start | bytes 147464 | tf_op jit(solution)/shard_map/ppermute | solution.py:373
  59.1 5.5 %collective-permute-start.16 = (bf16[256,256]{1,0:T(8,128)(2,1)S(1)}, bf16[256,256]{1,0:T(8,128)(2,1)S(1)}, u32[]{:S(2)}, u32[]{:S(2)}) collective-permute-start(bf16[256,256]{1,0:T(8,128)(2,1)S(1)} %shard_map.144.refs_0_), channel_id=1, source_target_pairs={{0,8},{8,0},{16,24},{24,16},{1,9},{9,1},{17,25},{25,17},{2,10},{10... | collective-permute-start | bytes 393224 | tf_op jit(solution)/shard_map/ppermute | solution.py:373
  60.7 5.1 %collective-permute-start.17 = (bf16[256,256]{1,0:T(8,128)(2,1)S(1)}, bf16[256,256]{1,0:T(8,128)(2,1)S(1)}, u32[]{:S(2)}, u32[]{:S(2)}) collective-permute-start(bf16[256,256]{1,0:T(8,128)(2,1)S(1)} %shard_map.144.refs_0_), channel_id=1, source_target_pairs={{0,16},{8,24},{16,0},{24,8},{1,17},{9,25},{17,1},{25,9},{2,18},{10... | collective-permute-start | bytes 393224 | tf_op jit(solution)/shard_map/ppermute | solution.py:373
  61.8 5.9 %collective-permute-start.18 = (bf16[256,256]{1,0:T(8,128)(2,1)S(1)}, bf16[256,256]{1,0:T(8,128)(2,1)S(1)}, u32[]{:S(2)}, u32[]{:S(2)}) collective-permute-start(bf16[256,256]{1,0:T(8,128)(2,1)S(1)} %shard_map.144.refs_0_), channel_id=1, source_target_pairs={{0,24},{8,16},{16,8},{24,0},{1,25},{9,17},{17,9},{25,1},{2,26},{10... | collective-permute-start | bytes 393224 | tf_op jit(solution)/shard_map/ppermute | solution.py:373
  62.7 5.0 %collective-permute-start.19 = (bf16[256,256]{1,0:T(8,128)(2,1)S(1)}, bf16[256,256]{1,0:T(8,128)(2,1)S(1)}, u32[]{:S(2)}, u32[]{:S(2)}) collective-permute-start(bf16[256,256]{1,0:T(8,128)(2,1)S(1)} %shard_map.144.refs_0_), channel_id=1, source_target_pairs={{0,1},{1,0},{2,3},{3,2},{4,5},{5,4},{6,7},{7,6},{8,9},{9,8},{10,11... | collective-permute-start | bytes 393224 | tf_op jit(solution)/shard_map/ppermute | solution.py:373
  67.7 1.3 %collective-permute-start.20 = (bf16[256,256]{1,0:T(8,128)(2,1)S(1)}, bf16[256,256]{1,0:T(8,128)(2,1)S(1)}, u32[]{:S(2)}, u32[]{:S(2)}) collective-permute-start(bf16[256,256]{1,0:T(8,128)(2,1)S(1)} %collective-permute-done.16.refs_2_), channel_id=1, source_target_pairs={{0,1},{1,0},{2,3},{3,2},{4,5},{5,4},{6,7},{7,6},{8,9},{9,8},{10,11... | collective-permute-start | bytes 393224 | tf_op jit(solution)/shard_map/ppermute | solution.py:373
  67.7 1.5 %collective-permute-start.21 = (bf16[256,256]{1,0:T(8,128)(2,1)S(1)}, bf16[256,256]{1,0:T(8,128)(2,1)S(1)}, u32[]{:S(2)}, u32[]{:S(2)}) collective-permute-start(bf16[256,256]{1,0:T(8,128)(2,1)S(1)} %collective-permute-done.17.refs_4_), channel_id=1, source_target_pairs={{0,1},{1,0},{2,3},{3,2},{4,5},{5,4},{6,7},{7,6},{8,9},{9,8},{10,11... | collective-permute-start | bytes 393224 | tf_op jit(solution)/shard_map/ppermute | solution.py:373
  68.2 1.3 %collective-permute-start.22 = (bf16[256,256]{1,0:T(8,128)(2,1)S(1)}, bf16[256,256]{1,0:T(8,128)(2,1)S(1)}, u32[]{:S(2)}, u32[]{:S(2)}) collective-permute-start(bf16[256,256]{1,0:T(8,128)(2,1)S(1)} %collective-permute-done.18.refs_6_), channel_id=1, source_target_pairs={{0,1},{1,0},{2,3},{3,2},{4,5},{5,4},{6,7},{7,6},{8,9},{9,8},{10,11... | collective-permute-start | bytes 393224 | tf_op jit(solution)/shard_map/ppermute | solution.py:373

commit v16 on v15

--- a/solution.py
+++ b/solution.py
@@ -116,7 +116,7 @@
 
 
 def row_forward(sites, haps, idx, link, *refs):
-    pieces = refs[:sites]
+    pieces = refs[:1] + refs[sites - 1 : 0 : -1]
     cot, gain, w_t, row_out, x_out, n_out = refs[sites:]
     me = idx[0]
     rows, width = cot.shape
@@ -410,7 +410,7 @@
     x_out, normed = call(
         functools.partial(row_forward, sites, haps),
         [((haps, per, 3 * width), BF16), ((total, width), BF16)],
-        idx, link_pattern, *pieces, cot, gains, w_t, row_out, scalars=2,
+        idx, link_pattern, pieces[0], *pieces[:0:-1], cot, gains, w_t, row_out, scalars=2,
     )
     x_in = exchange(x_out, "hap")
     prob, q, val, key_t = call(

time: 71.4 us -> 70.6 us (0.989)
  waiting for transfers between devices: 25.8 us -> 24.8 us
    ppermute x23, waiting for transfers between devices: 16.8 us -> 15.8 us  [swapped(): return lax.ppermute(value, axis, [(i, i ^ by) for i in range(length)])]
  transfers between devices with their start and end apart: 25 -> 25, of which waited for: 15 -> 16; matrix products, arithmetic and copies ran while one was open for 2% -> 2% of each run, Pallas kernels for 7% -> 7%
where the time goes in v16:
time: 70.6 us; the launch traced here: 70.3 us
  starting transfers between devices  28.4 us (40%)
  waiting for transfers between devices  24.8 us (35%)
  Pallas kernels  12.3 us (17%)
  local copies, waits for them, and re-layouts  3.94 us (6%)
  between operations  0.83 us (1%)
    ppermute x23, starting transfers between devices, swapped(): return lax.ppermute(value, axis, [(i, i ^ by) for i in range(length)])  20.8 us
    ppermute x23, waiting for transfers between devices, swapped(): return lax.ppermute(value, axis, [(i, i ^ by) for i in range(length)])  15.8 us
    pallas_call x11, Pallas kernels, call(): pl.pallas_call(body, out_shape=[jax.ShapeDtypeStruct(s, d) for s, d in ou...  12.3 us
    all_to_all x2, waiting for transfers between devices, exchange(): return lax.all_to_all(value, axis, 0, 0, tiled=True)  8.94 us
    all_to_all x2, starting transfers between devices, exchange(): return lax.all_to_all(value, axis, 0, 0, tiled=True)  7.64 us
    unnamed x22, local copies, waits for them, and re-layouts  2.99 us
  transfers between devices with their start and end apart: 25, of which 16 were waited for; matrix products, arithmetic and copies ran while one was open for 2% of the time, Pallas kernels for 7%

profile of v16, /device:TPU:0, one launch (start us, length us, event | category | flops | bytes accessed | tf_op | source)
XLA Modules:
  0.0 70.3 jit_solution(9165307154521373984)
XLA Ops:
  0.6 4.0 %collective-permute-start = (bf16[128,256]{1,0:T(8,128)(2,1)}, bf16[128,256]{1,0:T(8,128)(2,1)S(1)}, u32[]{:S(2)}, u32[]{:S(2)}) collective-permute-start(bf16[128,256]{1,0:T(8,128)(2,1)} %bitcast.14), channel_id=1, source_target_pairs={{0,24},{8,16},{16,8},{24,0},{1,25},{9,17},{17,9},{25,1},{2,26},{10... | collective-permute-start | bytes 196616 | tf_op jit(solution)/shard_map/ppermute | solution.py:373
  4.6 0.5 collective-permute-start.1
  5.1 0.1 collective-permute-start.2
  5.2 1.2 %copy.15 = bf16[256,768]{0,1:T(8,128)(2,1)S(1)} copy(bf16[256,768]{1,0:T(8,128)(2,1)} %param.12) | data formatting | bytes 786432 | tf_op args[3]
  6.5 0.9 %slice-done = bf16[256,512]{1,0:T(8,128)(2,1)S(1)} async-done(((bf16[256,768]{1,0:T(8,128)(2,1)}), bf16[256,512]{1,0:T(8,128)(2,1)S(1)}, s32[]{:S(2)}) %slice-start) | async-done | bytes 262168 | tf_op jit(solution)/shard_map/slice | solution.py:408
  7.4 0.1 copy.17
  7.6 0.5 copy-done.9
  8.1 0.2 copy-done.8
  8.2 0.8 %collective-permute-done.1.refs_2_ = bf16[128,256]{1,0:T(8,128)(2,1)S(1)} collective-permute-done((bf16[128,256]{1,0:T(8,128)(2,1)}, bf16[128,256]{1,0:T(8,128)(2,1)S(1)}, u32[]{:S(2)}, u32[]{:S(2)}) %collective-permute-start.1) | collective-permute-done | bytes 65568 | tf_op jit(solution)/shard_map/ppermute | solution.py:373
  9.1 0.5 collective-permute-done.2.refs_3_
  9.6 2.8 %shard_map.136 = (bf16[8,16,768]{2,1,0:T(8,128)(2,1)}, bf16[512,256]{1,0:T(8,128)(2,1)S(1)}) custom-call(s32[1]{0:T(128)} %bitcast.idx, s32[4,4]{1,0:T(4,128)S(1)} %compare_select_fusion.link, bf16[128,256]{1,0:T(8,128)(2,1)S(1)} %bitcast.17, bf16[128,256]{1,0:T(8,128)(2,1)S(1)} %collective-permute-done.refs_1_, ...), custom_call_target="tpu_custom_call" | custom-call | flops 1 | bytes 1 | tf_op jit(solution)/shard_map/pallas_call | solution.py:82
  12.4 4.9 %all-to-all-start = ((bf16[8,16,768]{2,1,0:T(8,128)(2,1)}), bf16[8,16,768]{2,1,0:T(8,128)(2,1)S(1)}, u32[]{:S(2)}, u32[]{:S(2)}) async-start(bf16[8,16,768]{2,1,0:T(8,128)(2,1)} %get-tuple-element.57), calls=%async_computation | async-start | bytes 393216 | tf_op jit(solution)/shard_map/all_to_all | solution.py:368
  17.3 1.8 %shard_map.137 = (bf16[512,1024]{1,0:T(8,128)(2,1)S(1)}, bf16[512,64]{1,0:T(8,128)(2,1)S(1)}, bf16[512,64]{1,0:T(8,128)(2,1)S(1)}, bf16[64,512]{1,0:T(8,128)(2,1)S(1)}) custom-call(s32[1]{0:T(128)} %bitcast.idx, s32[4,4]{1,0:T(4,128)S(1)} %compare_select_fusion.link, bf16[512,256]{1,0:T(8,128)(2,1)S(1)} %get-tuple-element.58.normed_ref.normed, ...), custom_call_target="tpu_custom_call" | custom-call | flops 20000000000 | bytes 72000000 | tf_op jit(solution)/shard_map/pallas_call | solution.py:82
  19.1 6.5 %all-to-all-done.x_in = bf16[8,16,768]{2,1,0:T(8,128)(2,1)S(1)} async-done(((bf16[8,16,768]{2,1,0:T(8,128)(2,1)}), bf16[8,16,768]{2,1,0:T(8,128)(2,1)S(1)}, u32[]{:S(2)}, u32[]{:S(2)}) %all-to-all-start) | async-done | bytes 196640 | tf_op jit(solution)/shard_map/all_to_all | solution.py:368
  25.7 3.2 %shard_map.138 = (bf16[32,8,128]{2,1,0:T(8,128)(2,1)}, bf16[128,1280]{1,0:T(8,128)(2,1)S(1)}, bf16[128,1280]{1,0:T(8,128)(2,1)}, bf16[8,16,512]{2,1,0:T(8,128)(2,1)}) custom-call(s32[1]{0:T(128)} %bitcast.1.hap, bf16[8,16,768]{2,1,0:T(8,128)(2,1)S(1)} %all-to-all-done.x_in, bf16[256,256]{1,0:T(8,128)(2,1)S(1)} %copy-done.1, ...), custom_call_target="tpu_custom_call" | custom-call | flops 1 | bytes 1 | tf_op jit(solution)/shard_map/pallas_call | solution.py:82
  29.0 2.8 %all-to-all-start.1 = ((bf16[32,8,128]{2,1,0:T(8,128)(2,1)}), bf16[32,8,128]{2,1,0:T(8,128)(2,1)S(1)}, u32[]{:S(2)}, u32[]{:S(2)}) async-start(bf16[32,8,128]{2,1,0:T(8,128)(2,1)} %get-tuple-element.61), calls=%async_computation.1 | async-start | bytes 131072 | tf_op jit(solution)/shard_map/all_to_all | solution.py:368
  31.8 0.3 collective-permute-start.4
  32.1 1.0 %copy-done.2 = bf16[128,1280]{1,0:T(8,128)(2,1)S(1)} copy-done((bf16[128,1280]{1,0:T(8,128)(2,1)S(1)}, bf16[128,1280]{1,0:T(8,128)(2,1)}, u32[]{:S(2)}) %copy-start.2) | copy-done | bytes 327704
  33.1 0.2 shard_map.139
  33.2 1.7 %collective-permute-start.6 = (bf16[32,1280]{1,0:T(8,128)(2,1)S(1)}, bf16[32,1280]{1,0:T(8,128)(2,1)S(1)}, u32[]{:S(2)}, u32[]{:S(2)}) collective-permute-start(bf16[32,1280]{1,0:T(8,128)(2,1)S(1)} %get-tuple-element.65), channel_id=1, source_target_pairs={{0,8},{8,0},{16,24},{24,16},{1,9},{9,1},{17,25},{25,17},{2,10},{10... | collective-permute-start | bytes 245768 | tf_op jit(solution)/shard_map/ppermute | solution.py:373
  35.0 1.5 %collective-permute-start.7 = (bf16[32,1280]{1,0:T(8,128)(2,1)S(1)}, bf16[32,1280]{1,0:T(8,128)(2,1)S(1)}, u32[]{:S(2)}, u32[]{:S(2)}) collective-permute-start(bf16[32,1280]{1,0:T(8,128)(2,1)S(1)} %get-tuple-element.66), channel_id=1, source_target_pairs={{0,16},{8,24},{16,0},{24,8},{1,17},{9,25},{17,1},{25,9},{2,18},{10... | collective-permute-start | bytes 245768 | tf_op jit(solution)/shard_map/ppermute | solution.py:373
  36.5 0.3 collective-permute-start.8
  36.8 2.4 %all-to-all-done.1.g_in = bf16[32,8,128]{2,1,0:T(8,128)(2,1)S(1)} async-done(((bf16[32,8,128]{2,1,0:T(8,128)(2,1)}), bf16[32,8,128]{2,1,0:T(8,128)(2,1)S(1)}, u32[]{:S(2)}, u32[]{:S(2)}) %all-to-all-start.1) | async-done | bytes 65568 | tf_op jit(solution)/shard_map/all_to_all | solution.py:368
  39.2 1.7 %shard_map.141 = (bf16[128,192]{1,0:T(8,128)(2,1)S(1)}, bf16[128,192]{1,0:T(8,128)(2,1)S(1)}, bf16[128,192]{1,0:T(8,128)(2,1)S(1)}, bf16[128,192]{1,0:T(8,128)(2...) custom-call(s32[1]{0:T(128)} %bitcast.idx, s32[1]{0:T(128)S(6)} %select_n.11.core, ...), custom_call_target="tpu_custom_call" | custom-call | flops 1 | bytes 1 | tf_op jit(solution)/shard_map/pallas_call | solution.py:82
  41.0 1.2 %collective-permute-done.5.row_got = bf16[96,256]{1,0:T(8,128)(2,1)S(1)} collective-permute-done((bf16[96,256]{1,0:T(8,128)(2,1)S(1)}, bf16[96,256]{1,0:T(8,128)(2,1)S(1)}, u32[]{:S(2)}, u32[]{:S(2)}) %collective-permute-start.5) | collective-permute-done | bytes 49184 | tf_op jit(solution)/shard_map/ppermute | solution.py:373
  42.3 1.1 %collective-permute-start.9 = (bf16[320,256]{1,0:T(8,128)(2,1)S(1)}, bf16[320,256]{1,0:T(8,128)(2,1)S(1)}, u32[]{:S(2)}, u32[]{:S(2)}) collective-permute-start(bf16[320,256]{1,0:T(8,128)(2,1)S(1)} %get-tuple-element.77.mine), channel_id=1, source_target_pairs={{0,2},{1,3},{2,0},{3,1},{4,6},{5,7},{6,4},{7,5},{8,10},{9,11},{10,... | collective-permute-start | bytes 491528 | tf_op jit(solution)/shard_map/ppermute | solution.py:373
  43.4 2.5 %collective-permute-start.10 = (bf16[64,256]{1,0:T(8,128)(2,1)S(1)}, bf16[64,256]{1,0:T(8,128)(2,1)S(1)}, u32[]{:S(2)}, u32[]{:S(2)}) collective-permute-start(bf16[64,256]{1,0:T(8,128)(2,1)S(1)} %get-tuple-element.78), channel_id=1, source_target_pairs={{0,4},{1,5},{2,6},{3,7},{4,0},{5,1},{6,2},{7,3},{8,12},{9,13},{10,... | collective-permute-start | bytes 98312 | tf_op jit(solution)/shard_map/ppermute | solution.py:373
  45.8 0.9 %collective-permute-start.11 = (bf16[64,256]{1,0:T(8,128)(2,1)S(1)}, bf16[64,256]{1,0:T(8,128)(2,1)S(1)}, u32[]{:S(2)}, u32[]{:S(2)}) collective-permute-start(bf16[64,256]{1,0:T(8,128)(2,1)S(1)} %get-tuple-element.79), channel_id=1, source_target_pairs={{0,6},{1,7},{2,4},{3,5},{4,2},{5,3},{6,0},{7,1},{8,14},{9,15},{10,... | collective-permute-start | bytes 98312 | tf_op jit(solution)/shard_map/ppermute | solution.py:373
  46.8 1.5 %collective-permute-done.10.refs_5_ = bf16[64,256]{1,0:T(8,128)(2,1)S(1)} collective-permute-done((bf16[64,256]{1,0:T(8,128)(2,1)S(1)}, bf16[64,256]{1,0:T(8,128)(2,1)S(1)}, u32[]{:S(2)}, u32[]{:S(2)}) %collective-permute-start.10) | collective-permute-done | bytes 32800 | tf_op jit(solution)/shard_map/ppermute | solution.py:373
  48.3 3.3 %collective-permute-done.11.refs_6_ = bf16[64,256]{1,0:T(8,128)(2,1)S(1)} collective-permute-done((bf16[64,256]{1,0:T(8,128)(2,1)S(1)}, bf16[64,256]{1,0:T(8,128)(2,1)S(1)}, u32[]{:S(2)}, u32[]{:S(2)}) %collective-permute-start.11) | collective-permute-done | bytes 32800 | tf_op jit(solution)/shard_map/ppermute | solution.py:373
  51.7 0.6 collective-permute-start.13
  52.3 0.9 %collective-permute-start.14 = (bf16[128,192]{1,0:T(8,128)(2,1)S(1)}, bf16[128,192]{1,0:T(8,128)(2,1)S(1)}, u32[]{:S(2)}, u32[]{:S(2)}) collective-permute-start(bf16[128,192]{1,0:T(8,128)(2,1)S(1)} %get-tuple-element.87), channel_id=1, source_target_pairs={{0,16},{8,24},{16,0},{24,8},{1,17},{9,25},{17,1},{25,9},{2,18},{10... | collective-permute-start | bytes 147464 | tf_op jit(solution)/shard_map/ppermute | solution.py:373
  53.2 2.1 %collective-permute-start.15 = (bf16[128,192]{1,0:T(8,128)(2,1)S(1)}, bf16[128,192]{1,0:T(8,128)(2,1)S(1)}, u32[]{:S(2)}, u32[]{:S(2)}) collective-permute-start(bf16[128,192]{1,0:T(8,128)(2,1)S(1)} %get-tuple-element.88), channel_id=1, source_target_pairs={{0,24},{8,16},{16,8},{24,0},{1,25},{9,17},{17,9},{25,1},{2,26},{10... | collective-permute-start | bytes 147464 | tf_op jit(solution)/shard_map/ppermute | solution.py:373
  55.2 0.8 %collective-permute-done.13.refs_0_ = bf16[128,192]{1,0:T(8,128)(2,1)S(1)} collective-permute-done((bf16[128,192]{1,0:T(8,128)(2,1)S(1)}, bf16[128,192]{1,0:T(8,128)(2,1)S(1)}, u32[]{:S(2)}, u32[]{:S(2)}) %collective-permute-start.13) | collective-permute-done | bytes 49184 | tf_op jit(solution)/shard_map/ppermute | solution.py:373
  56.0 0.5 collective-permute-done.14.refs_1_
  56.6 1.8 %collective-permute-done.15.refs_2_ = bf16[128,192]{1,0:T(8,128)(2,1)S(1)} collective-permute-done((bf16[128,192]{1,0:T(8,128)(2,1)S(1)}, bf16[128,192]{1,0:T(8,128)(2,1)S(1)}, u32[]{:S(2)}, u32[]{:S(2)}) %collective-permute-start.15) | collective-permute-done | bytes 49184 | tf_op jit(solution)/shard_map/ppermute | solution.py:373
  58.4 1.5 %collective-permute-start.16 = (bf16[256,256]{1,0:T(8,128)(2,1)S(1)}, bf16[256,256]{1,0:T(8,128)(2,1)S(1)}, u32[]{:S(2)}, u32[]{:S(2)}) collective-permute-start(bf16[256,256]{1,0:T(8,128)(2,1)S(1)} %shard_map.144.refs_0_), channel_id=1, source_target_pairs={{0,8},{8,0},{16,24},{24,16},{1,9},{9,1},{17,25},{25,17},{2,10},{10... | collective-permute-start | bytes 393224 | tf_op jit(solution)/shard_map/ppermute | solution.py:373
  59.9 1.2 %collective-permute-start.17 = (bf16[256,256]{1,0:T(8,128)(2,1)S(1)}, bf16[256,256]{1,0:T(8,128)(2,1)S(1)}, u32[]{:S(2)}, u32[]{:S(2)}) collective-permute-start(bf16[256,256]{1,0:T(8,128)(2,1)S(1)} %shard_map.144.refs_0_), channel_id=1, source_target_pairs={{0,16},{8,24},{16,0},{24,8},{1,17},{9,25},{17,1},{25,9},{2,18},{10... | collective-permute-start | bytes 393224 | tf_op jit(solution)/shard_map/ppermute | solution.py:373
  61.1 0.8 %collective-permute-start.18 = (bf16[256,256]{1,0:T(8,128)(2,1)S(1)}, bf16[256,256]{1,0:T(8,128)(2,1)S(1)}, u32[]{:S(2)}, u32[]{:S(2)}) collective-permute-start(bf16[256,256]{1,0:T(8,128)(2,1)S(1)} %shard_map.144.refs_0_), channel_id=1, source_target_pairs={{0,24},{8,16},{16,8},{24,0},{1,25},{9,17},{17,9},{25,1},{2,26},{10... | collective-permute-start | bytes 393224 | tf_op jit(solution)/shard_map/ppermute | solution.py:373
  61.9 1.0 %shard_map.145 = (bf16[128,256]{1,0:T(8,128)(2,1)}, bf16[128,256]{1,0:T(8,128)(2,1)}) custom-call(s32[1]{0:T(128)} %bitcast.idx, s32[1]{0:T(128)} %bitcast.1.hap, bf16[128,256]{1,0:T(8,128)(2,1)S(1)} %bitcast.18, f32[2,256]{1,0:T(2,128)S(1)} %pad_maximum_fusion.refs_5_.gain, bf16[768,256]{1,0:T(8,128)(2,1)S(1)} %bitcast.12, ...), custom_call_target="tpu_custom_call" | custom-call | flops 1 | bytes 1 | tf_op jit(solution)/shard_map/pallas_call | solution.py:82
  62.9 1.0 %collective-permute-done.16.refs_2_ = bf16[256,256]{1,0:T(8,128)(2,1)S(1)} collective-permute-done((bf16[256,256]{1,0:T(8,128)(2,1)S(1)}, bf16[256,256]{1,0:T(8,128)(2,1)S(1)}, u32[]{:S(2)}, u32[]{:S(2)}) %collective-permute-start.16) | collective-permute-done | bytes 131104 | tf_op jit(solution)/shard_map/ppermute | solution.py:373
  63.9 1.2 %collective-permute-done.17.refs_4_ = bf16[256,256]{1,0:T(8,128)(2,1)S(1)} collective-permute-done((bf16[256,256]{1,0:T(8,128)(2,1)S(1)}, bf16[256,256]{1,0:T(8,128)(2,1)S(1)}, u32[]{:S(2)}, u32[]{:S(2)}) %collective-permute-start.17) | collective-permute-done | bytes 131104 | tf_op jit(solution)/shard_map/ppermute | solution.py:373
  65.0 1.9 %collective-permute-done.18.refs_6_ = bf16[256,256]{1,0:T(8,128)(2,1)S(1)} collective-permute-done((bf16[256,256]{1,0:T(8,128)(2,1)S(1)}, bf16[256,256]{1,0:T(8,128)(2,1)S(1)}, u32[]{:S(2)}, u32[]{:S(2)}) %collective-permute-start.18) | collective-permute-done | bytes 131104 | tf_op jit(solution)/shard_map/ppermute | solution.py:373
  66.9 0.5 collective-permute-start.21
  67.5 0.8 %collective-permute-done.20.refs_3_ = bf16[256,256]{1,0:T(8,128)(2,1)S(1)} collective-permute-done((bf16[256,256]{1,0:T(8,128)(2,1)S(1)}, bf16[256,256]{1,0:T(8,128)(2,1)S(1)}, u32[]{:S(2)}, u32[]{:S(2)}) %collective-permute-start.20) | collective-permute-done | bytes 131104 | tf_op jit(solution)/shard_map/ppermute | solution.py:373
  68.3 0.2 collective-permute-done.21.refs_5_
  68.5 0.3 collective-permute-done.22.refs_7_
  68.8 1.5 %shard_map.146 = (f32[256,768]{1,0:T(8,128)}, f32[256,256]{1,0:T(8,128)}, f32[256,768]{1,0:T(8,128)}, f32[256,256]{1,0:T(8,128)}) custom-call(s32[1]{0:T(128)} %bitcast.idx, s32[1]{0:T(128)S(6)} %select_n.11.core, bf16[256,256]{1,0:T(8,128)(2,1)S(1)} %shard_map.144.refs_0_, bf16[256,256]{1,0:T(8,128)(2,1)S(1)} %collective-permute-done.19.refs_1_, ...), custom_call_target="tpu_custom_call" | custom-call | flops 1 | bytes 1 | tf_op jit(solution)/shard_map/pallas_call | solution.py:82
  (39 shorter events, 0.4 us)
Async XLA Ops:
  0.6 7.6 %collective-permute-start = (bf16[128,256]{1,0:T(8,128)(2,1)}, bf16[128,256]{1,0:T(8,128)(2,1)S(1)}, u32[]{:S(2)}, u32[]{:S(2)}) collective-permute-start(bf16[128,256]{1,0:T(8,128)(2,1)} %bitcast.14), channel_id=1, source_target_pairs={{0,24},{8,16},{16,8},{24,0},{1,25},{9,17},{17,9},{25,1},{2,26},{10... | collective-permute-start | bytes 196616 | tf_op jit(solution)/shard_map/ppermute | solution.py:373
  4.6 4.5 %collective-permute-start.1 = (bf16[128,256]{1,0:T(8,128)(2,1)}, bf16[128,256]{1,0:T(8,128)(2,1)S(1)}, u32[]{:S(2)}, u32[]{:S(2)}) collective-permute-start(bf16[128,256]{1,0:T(8,128)(2,1)} %bitcast.15), channel_id=1, source_target_pairs={{0,16},{8,24},{16,0},{24,8},{1,17},{9,25},{17,1},{25,9},{2,18},{10... | collective-permute-start | bytes 196616 | tf_op jit(solution)/shard_map/ppermute | solution.py:373
  5.1 4.5 %collective-permute-start.2 = (bf16[128,256]{1,0:T(8,128)(2,1)}, bf16[128,256]{1,0:T(8,128)(2,1)S(1)}, u32[]{:S(2)}, u32[]{:S(2)}) collective-permute-start(bf16[128,256]{1,0:T(8,128)(2,1)} %bitcast.16), channel_id=1, source_target_pairs={{0,8},{8,0},{16,24},{24,16},{1,9},{9,1},{17,25},{25,17},{2,10},{10... | collective-permute-start | bytes 196616 | tf_op jit(solution)/shard_map/ppermute | solution.py:373
  5.2 1.2 %copy-start.7 = (s32[4,4]{1,0:T(4,128)S(1)}, s32[4,4]{1,0:T(4,128)}, u32[]{:S(2)}) copy-start(s32[4,4]{1,0:T(4,128)} %param.10) | copy-start | bytes 196
  6.4 1.0 %slice-start = ((bf16[256,768]{1,0:T(8,128)(2,1)}), bf16[256,512]{1,0:T(8,128)(2,1)S(1)}, s32[]{:S(2)}) async-start(bf16[256,768]{1,0:T(8,128)(2,1)} %col_proj.1), calls=%async_computation.2 | async-start | bytes 524288 | tf_op jit(solution)/shard_map/slice | solution.py:408
  7.4 0.7 copy-start.9
  7.4 2.2 %copy-start.1 = (bf16[256,256]{1,0:T(8,128)(2,1)S(1)}, bf16[256,256]{1,0:T(8,128)(2,1)}, u32[]{:S(2)}) copy-start(bf16[256,256]{1,0:T(8,128)(2,1)} %row_out.1) | copy-start | bytes 393220
  7.4 2.2 %copy-start.3 = (bf16[128,1,256]{2,0,1:T(8,128)(2,1)S(1)}, bf16[128,1,256]{2,0,1:T(8,128)(2,1)}, u32[]{:S(2)}) copy-start(bf16[128,1,256]{2,0,1:T(8,128)(2,1)} %param.9) | copy-start | bytes 196612
  7.4 2.2 %copy-start.6 = (bf16[128,1,256]{2,0,1:T(8,128)(2,1)S(1)}, bf16[128,1,256]{2,0,1:T(8,128)(2,1)}, u32[]{:S(2)}) copy-start(bf16[128,1,256]{2,0,1:T(8,128)(2,1)} %param.17) | copy-start | bytes 196612
  7.6 0.7 copy-start.8
  12.4 13.2 %all-to-all-start = ((bf16[8,16,768]{2,1,0:T(8,128)(2,1)}), bf16[8,16,768]{2,1,0:T(8,128)(2,1)S(1)}, u32[]{:S(2)}, u32[]{:S(2)}) async-start(bf16[8,16,768]{2,1,0:T(8,128)(2,1)} %get-tuple-element.57), calls=%async_computation | async-start | bytes 393216 | tf_op jit(solution)/shard_map/all_to_all | solution.py:368
  17.3 8.3 %copy-start = (bf16[256,768]{1,0:T(8,128)(2,1)S(1)}, bf16[256,768]{1,0:T(8,128)(2,1)}, u32[]{:S(2)}) copy-start(bf16[256,768]{1,0:T(8,128)(2,1)} %col_proj.1) | copy-start | bytes 1179652
  17.3 8.3 %copy-start.5 = (bf16[256,256]{1,0:T(8,128)(2,1)S(1)}, bf16[256,256]{1,0:T(8,128)(2,1)}, u32[]{:S(2)}) copy-start(bf16[256,256]{1,0:T(8,128)(2,1)} %col_out.1) | copy-start | bytes 393220
  28.9 2.9 %copy-start.4 = (bf16[8,16,512]{2,1,0:T(8,128)(2,1)S(1)}, bf16[8,16,512]{2,1,0:T(8,128)(2,1)}, u32[]{:S(2)}) copy-start(bf16[8,16,512]{2,1,0:T(8,128)(2,1)} %get-tuple-element.68.og) | copy-start | bytes 393220
  28.9 3.2 %collective-permute-start.3 = (bf16[128,1280]{1,0:T(8,128)(2,1)S(1)}, bf16[128,1280]{1,0:T(8,128)(2,1)S(1)}, u32[]{:S(2)}, u32[]{:S(2)}) collective-permute-start(bf16[128,1280]{1,0:T(8,128)(2,1)S(1)} %get-tuple-element.63), channel_id=1, source_target_pairs={{0,1},{1,0},{2,3},{3,2},{4,5},{5,4},{6,7},{7,6},{8,9},{9,8},{10,11... | collective-permute-start | bytes 983048 | tf_op jit(solution)/shard_map/ppermute | solution.py:373
  29.0 10.3 %all-to-all-start.1 = ((bf16[32,8,128]{2,1,0:T(8,128)(2,1)}), bf16[32,8,128]{2,1,0:T(8,128)(2,1)S(1)}, u32[]{:S(2)}, u32[]{:S(2)}) async-start(bf16[32,8,128]{2,1,0:T(8,128)(2,1)} %get-tuple-element.61), calls=%async_computation.1 | async-start | bytes 131072 | tf_op jit(solution)/shard_map/all_to_all | solution.py:368
  31.8 5.0 %collective-permute-start.4 = (bf16[4,16,512]{2,1,0:T(8,128)(2,1)S(1)}, bf16[4,16,512]{2,1,0:T(8,128)(2,1)S(1)}, u32[]{:S(2)}, u32[]{:S(2)}) collective-permute-start(bf16[4,16,512]{2,1,0:T(8,128)(2,1)S(1)} %get-tuple-element.69), channel_id=1, source_target_pairs={{0,1},{1,0},{2,3},{3,2},{4,5},{5,4},{6,7},{7,6},{8,9},{9,8},{10,11... | collective-permute-start | bytes 196616 | tf_op jit(solution)/shard_map/ppermute | solution.py:373
  32.1 1.0 %copy-start.2 = (bf16[128,1280]{1,0:T(8,128)(2,1)S(1)}, bf16[128,1280]{1,0:T(8,128)(2,1)}, u32[]{:S(2)}) copy-start(bf16[128,1280]{1,0:T(8,128)(2,1)} %get-tuple-element.62.keep) | copy-start | bytes 983044
  33.2 9.0 %collective-permute-start.6 = (bf16[32,1280]{1,0:T(8,128)(2,1)S(1)}, bf16[32,1280]{1,0:T(8,128)(2,1)S(1)}, u32[]{:S(2)}, u32[]{:S(2)}) collective-permute-start(bf16[32,1280]{1,0:T(8,128)(2,1)S(1)} %get-tuple-element.65), channel_id=1, source_target_pairs={{0,8},{8,0},{16,24},{24,16},{1,9},{9,1},{17,25},{25,17},{2,10},{10... | collective-permute-start | bytes 245768 | tf_op jit(solution)/shard_map/ppermute | solution.py:373
  35.0 7.3 %collective-permute-start.7 = (bf16[32,1280]{1,0:T(8,128)(2,1)S(1)}, bf16[32,1280]{1,0:T(8,128)(2,1)S(1)}, u32[]{:S(2)}, u32[]{:S(2)}) collective-permute-start(bf16[32,1280]{1,0:T(8,128)(2,1)S(1)} %get-tuple-element.66), channel_id=1, source_target_pairs={{0,16},{8,24},{16,0},{24,8},{1,17},{9,25},{17,1},{25,9},{2,18},{10... | collective-permute-start | bytes 245768 | tf_op jit(solution)/shard_map/ppermute | solution.py:373
  36.5 5.8 %collective-permute-start.8 = (bf16[32,1280]{1,0:T(8,128)(2,1)S(1)}, bf16[32,1280]{1,0:T(8,128)(2,1)S(1)}, u32[]{:S(2)}, u32[]{:S(2)}) collective-permute-start(bf16[32,1280]{1,0:T(8,128)(2,1)S(1)} %get-tuple-element.67), channel_id=1, source_target_pairs={{0,24},{8,16},{16,8},{24,0},{1,25},{9,17},{17,9},{25,1},{2,26},{10... | collective-permute-start | bytes 245768 | tf_op jit(solution)/shard_map/ppermute | solution.py:373
  41.0 1.3 %collective-permute-start.5 = (bf16[96,256]{1,0:T(8,128)(2,1)S(1)}, bf16[96,256]{1,0:T(8,128)(2,1)S(1)}, u32[]{:S(2)}, u32[]{:S(2)}) collective-permute-start(bf16[96,256]{1,0:T(8,128)(2,1)S(1)} %get-tuple-element.75), channel_id=1, source_target_pairs={{0,1},{1,0},{2,3},{3,2},{4,5},{5,4},{6,7},{7,6},{8,9},{9,8},{10,11... | collective-permute-start | bytes 147464 | tf_op jit(solution)/shard_map/ppermute | solution.py:373
  42.3 9.2 %collective-permute-start.9 = (bf16[320,256]{1,0:T(8,128)(2,1)S(1)}, bf16[320,256]{1,0:T(8,128)(2,1)S(1)}, u32[]{:S(2)}, u32[]{:S(2)}) collective-permute-start(bf16[320,256]{1,0:T(8,128)(2,1)S(1)} %get-tuple-element.77.mine), channel_id=1, source_target_pairs={{0,2},{1,3},{2,0},{3,1},{4,6},{5,7},{6,4},{7,5},{8,10},{9,11},{10,... | collective-permute-start | bytes 491528 | tf_op jit(solution)/shard_map/ppermute | solution.py:373
  43.4 4.9 %collective-permute-start.10 = (bf16[64,256]{1,0:T(8,128)(2,1)S(1)}, bf16[64,256]{1,0:T(8,128)(2,1)S(1)}, u32[]{:S(2)}, u32[]{:S(2)}) collective-permute-start(bf16[64,256]{1,0:T(8,128)(2,1)S(1)} %get-tuple-element.78), channel_id=1, source_target_pairs={{0,4},{1,5},{2,6},{3,7},{4,0},{5,1},{6,2},{7,3},{8,12},{9,13},{10,... | collective-permute-start | bytes 98312 | tf_op jit(solution)/shard_map/ppermute | solution.py:373
  45.8 5.7 %collective-permute-start.11 = (bf16[64,256]{1,0:T(8,128)(2,1)S(1)}, bf16[64,256]{1,0:T(8,128)(2,1)S(1)}, u32[]{:S(2)}, u32[]{:S(2)}) collective-permute-start(bf16[64,256]{1,0:T(8,128)(2,1)S(1)} %get-tuple-element.79), channel_id=1, source_target_pairs={{0,6},{1,7},{2,4},{3,5},{4,2},{5,3},{6,0},{7,1},{8,14},{9,15},{10,... | collective-permute-start | bytes 98312 | tf_op jit(solution)/shard_map/ppermute | solution.py:373
  51.6 6.7 %collective-permute-start.12 = (bf16[256,256]{1,0:T(8,128)(2,1)S(1)}, bf16[256,256]{1,0:T(8,128)(2,1)S(1)}, u32[]{:S(2)}, u32[]{:S(2)}) collective-permute-start(bf16[256,256]{1,0:T(8,128)(2,1)S(1)} %shard_map.143.mine), channel_id=1, source_target_pairs={{0,4},{1,5},{2,6},{3,7},{4,0},{5,1},{6,2},{7,3},{8,12},{9,13},{10,... | collective-permute-start | bytes 393224 | tf_op jit(solution)/shard_map/ppermute | solution.py:373
  51.7 4.3 %collective-permute-start.13 = (bf16[128,192]{1,0:T(8,128)(2,1)S(1)}, bf16[128,192]{1,0:T(8,128)(2,1)S(1)}, u32[]{:S(2)}, u32[]{:S(2)}) collective-permute-start(bf16[128,192]{1,0:T(8,128)(2,1)S(1)} %get-tuple-element.86), channel_id=1, source_target_pairs={{0,8},{8,0},{16,24},{24,16},{1,9},{9,1},{17,25},{25,17},{2,10},{10... | collective-permute-start | bytes 147464 | tf_op jit(solution)/shard_map/ppermute | solution.py:373
  52.3 4.3 %collective-permute-start.14 = (bf16[128,192]{1,0:T(8,128)(2,1)S(1)}, bf16[128,192]{1,0:T(8,128)(2,1)S(1)}, u32[]{:S(2)}, u32[]{:S(2)}) collective-permute-start(bf16[128,192]{1,0:T(8,128)(2,1)S(1)} %get-tuple-element.87), channel_id=1, source_target_pairs={{0,16},{8,24},{16,0},{24,8},{1,17},{9,25},{17,1},{25,9},{2,18},{10... | collective-permute-start | bytes 147464 | tf_op jit(solution)/shard_map/ppermute | solution.py:373
  53.2 5.2 %collective-permute-start.15 = (bf16[128,192]{1,0:T(8,128)(2,1)S(1)}, bf16[128,192]{1,0:T(8,128)(2,1)S(1)}, u32[]{:S(2)}, u32[]{:S(2)}) collective-permute-start(bf16[128,192]{1,0:T(8,128)(2,1)S(1)} %get-tuple-element.88), channel_id=1, source_target_pairs={{0,24},{8,16},{16,8},{24,0},{1,25},{9,17},{17,9},{25,1},{2,26},{10... | collective-permute-start | bytes 147464 | tf_op jit(solution)/shard_map/ppermute | solution.py:373
  58.4 5.5 %collective-permute-start.16 = (bf16[256,256]{1,0:T(8,128)(2,1)S(1)}, bf16[256,256]{1,0:T(8,128)(2,1)S(1)}, u32[]{:S(2)}, u32[]{:S(2)}) collective-permute-start(bf16[256,256]{1,0:T(8,128)(2,1)S(1)} %shard_map.144.refs_0_), channel_id=1, source_target_pairs={{0,8},{8,0},{16,24},{24,16},{1,9},{9,1},{17,25},{25,17},{2,10},{10... | collective-permute-start | bytes 393224 | tf_op jit(solution)/shard_map/ppermute | solution.py:373
  59.9 5.1 %collective-permute-start.17 = (bf16[256,256]{1,0:T(8,128)(2,1)S(1)}, bf16[256,256]{1,0:T(8,128)(2,1)S(1)}, u32[]{:S(2)}, u32[]{:S(2)}) collective-permute-start(bf16[256,256]{1,0:T(8,128)(2,1)S(1)} %shard_map.144.refs_0_), channel_id=1, source_target_pairs={{0,16},{8,24},{16,0},{24,8},{1,17},{9,25},{17,1},{25,9},{2,18},{10... | collective-permute-start | bytes 393224 | tf_op jit(solution)/shard_map/ppermute | solution.py:373
  61.1 5.9 %collective-permute-start.18 = (bf16[256,256]{1,0:T(8,128)(2,1)S(1)}, bf16[256,256]{1,0:T(8,128)(2,1)S(1)}, u32[]{:S(2)}, u32[]{:S(2)}) collective-permute-start(bf16[256,256]{1,0:T(8,128)(2,1)S(1)} %shard_map.144.refs_0_), channel_id=1, source_target_pairs={{0,24},{8,16},{16,8},{24,0},{1,25},{9,17},{17,9},{25,1},{2,26},{10... | collective-permute-start | bytes 393224 | tf_op jit(solution)/shard_map/ppermute | solution.py:373
  61.9 5.0 %collective-permute-start.19 = (bf16[256,256]{1,0:T(8,128)(2,1)S(1)}, bf16[256,256]{1,0:T(8,128)(2,1)S(1)}, u32[]{:S(2)}, u32[]{:S(2)}) collective-permute-start(bf16[256,256]{1,0:T(8,128)(2,1)S(1)} %shard_map.144.refs_0_), channel_id=1, source_target_pairs={{0,1},{1,0},{2,3},{3,2},{4,5},{5,4},{6,7},{7,6},{8,9},{9,8},{10,11... | collective-permute-start | bytes 393224 | tf_op jit(solution)/shard_map/ppermute | solution.py:373
  66.9 1.3 %collective-permute-start.20 = (bf16[256,256]{1,0:T(8,128)(2,1)S(1)}, bf16[256,256]{1,0:T(8,128)(2,1)S(1)}, u32[]{:S(2)}, u32[]{:S(2)}) collective-permute-start(bf16[256,256]{1,0:T(8,128)(2,1)S(1)} %collective-permute-done.16.refs_2_), channel_id=1, source_target_pairs={{0,1},{1,0},{2,3},{3,2},{4,5},{5,4},{6,7},{7,6},{8,9},{9,8},{10,11... | collective-permute-start | bytes 393224 | tf_op jit(solution)/shard_map/ppermute | solution.py:373
  66.9 1.5 %collective-permute-start.21 = (bf16[256,256]{1,0:T(8,128)(2,1)S(1)}, bf16[256,256]{1,0:T(8,128)(2,1)S(1)}, u32[]{:S(2)}, u32[]{:S(2)}) collective-permute-start(bf16[256,256]{1,0:T(8,128)(2,1)S(1)} %collective-permute-done.17.refs_4_), channel_id=1, source_target_pairs={{0,1},{1,0},{2,3},{3,2},{4,5},{5,4},{6,7},{7,6},{8,9},{9,8},{10,11... | collective-permute-start | bytes 393224 | tf_op jit(solution)/shard_map/ppermute | solution.py:373
  67.5 1.3 %collective-permute-start.22 = (bf16[256,256]{1,0:T(8,128)(2,1)S(1)}, bf16[256,256]{1,0:T(8,128)(2,1)S(1)}, u32[]{:S(2)}, u32[]{:S(2)}) collective-permute-start(bf16[256,256]{1,0:T(8,128)(2,1)S(1)} %collective-permute-done.18.refs_6_), channel_id=1, source_target_pairs={{0,1},{1,0},{2,3},{3,2},{4,5},{5,4},{6,7},{7,6},{8,9},{9,8},{10,11... | collective-permute-start | bytes 393224 | tf_op jit(solution)/shard_map/ppermute | solution.py:373

commit v17 on v16

--- a/solution.py
+++ b/solution.py
@@ -490,7 +490,7 @@
         idx, hap, feats, gains, w_t, *gps, *parts, scalars=2,
         scratch=[pltpu.VMEM((2, haps, per, width), F32)],
     )
-    got, mine_swapped, out = lax.optimization_barrier((got, mine_swapped, out))
+    got[0], mine_swapped, out = lax.optimization_barrier((got[0], mine_swapped, out))
     full = [mine, mine_swapped] + [x for p in got for x in (p, swapped(p, "hap", 1))]
     rp, ro, cp, co = call(
         functools.partial(weights_finish, sites),

time: 70.6 us -> 72 us (1.020)
  waiting for transfers between devices: 24.8 us -> 26.1 us
    ppermute x23, waiting for transfers between devices: 15.8 us -> 17.2 us  [swapped(): return lax.ppermute(value, axis, [(i, i ^ by) for i in range(length)])]
  transfers between devices with their start and end apart: 25 -> 25, of which waited for: 16 -> 14; matrix products, arithmetic and copies ran while one was open for 2% -> 2% of each run, Pallas kernels for 7% -> 6%
where the time goes in v17:
time: 72 us; the launch traced here: 71.6 us
  starting transfers between devices  28.4 us (39%)
  waiting for transfers between devices  26.1 us (36%)
  Pallas kernels  12.3 us (17%)
  local copies, waits for them, and re-layouts  3.94 us (5%)
  between operations  0.83 us (1%)
    ppermute x23, starting transfers between devices, swapped(): return lax.ppermute(value, axis, [(i, i ^ by) for i in range(length)])  20.8 us
    ppermute x23, waiting for transfers between devices, swapped(): return lax.ppermute(value, axis, [(i, i ^ by) for i in range(length)])  17.2 us
    pallas_call x11, Pallas kernels, call(): pl.pallas_call(body, out_shape=[jax.ShapeDtypeStruct(s, d) for s, d in ou...  12.3 us
    all_to_all x2, waiting for transfers between devices, exchange(): return lax.all_to_all(value, axis, 0, 0, tiled=True)  8.94 us
    all_to_all x2, starting transfers between devices, exchange(): return lax.all_to_all(value, axis, 0, 0, tiled=True)  7.64 us
    unnamed x22, local copies, waits for them, and re-layouts  2.99 us
  transfers between devices with their start and end apart: 25, of which 14 were waited for; matrix products, arithmetic and copies ran while one was open for 2% of the time, Pallas kernels for 6%

profile of v17, /device:TPU:0, one launch (start us, length us, event | category | flops | bytes accessed | tf_op | source)
XLA Modules:
  0.0 71.6 jit_solution(4688495851338473420)
XLA Ops:
  0.6 4.0 %collective-permute-start = (bf16[128,256]{1,0:T(8,128)(2,1)}, bf16[128,256]{1,0:T(8,128)(2,1)S(1)}, u32[]{:S(2)}, u32[]{:S(2)}) collective-permute-start(bf16[128,256]{1,0:T(8,128)(2,1)} %bitcast.14), channel_id=1, source_target_pairs={{0,24},{8,16},{16,8},{24,0},{1,25},{9,17},{17,9},{25,1},{2,26},{10... | collective-permute-start | bytes 196616 | tf_op jit(solution)/shard_map/ppermute | solution.py:373
  4.6 0.5 collective-permute-start.1
  5.1 0.1 collective-permute-start.2
  5.2 1.2 %copy.15 = bf16[256,768]{0,1:T(8,128)(2,1)S(1)} copy(bf16[256,768]{1,0:T(8,128)(2,1)} %param.12) | data formatting | bytes 786432 | tf_op args[3]
  6.5 0.9 %slice-done = bf16[256,512]{1,0:T(8,128)(2,1)S(1)} async-done(((bf16[256,768]{1,0:T(8,128)(2,1)}), bf16[256,512]{1,0:T(8,128)(2,1)S(1)}, s32[]{:S(2)}) %slice-start) | async-done | bytes 262168 | tf_op jit(solution)/shard_map/slice | solution.py:408
  7.4 0.1 copy.17
  7.6 0.5 copy-done.9
  8.1 0.2 copy-done.8
  8.2 0.8 %collective-permute-done.1.refs_2_ = bf16[128,256]{1,0:T(8,128)(2,1)S(1)} collective-permute-done((bf16[128,256]{1,0:T(8,128)(2,1)}, bf16[128,256]{1,0:T(8,128)(2,1)S(1)}, u32[]{:S(2)}, u32[]{:S(2)}) %collective-permute-start.1) | collective-permute-done | bytes 65568 | tf_op jit(solution)/shard_map/ppermute | solution.py:373
  9.1 0.5 collective-permute-done.2.refs_3_
  9.6 2.8 %shard_map.136 = (bf16[8,16,768]{2,1,0:T(8,128)(2,1)}, bf16[512,256]{1,0:T(8,128)(2,1)S(1)}) custom-call(s32[1]{0:T(128)} %bitcast.idx, s32[4,4]{1,0:T(4,128)S(1)} %compare_select_fusion.link, bf16[128,256]{1,0:T(8,128)(2,1)S(1)} %bitcast.17, bf16[128,256]{1,0:T(8,128)(2,1)S(1)} %collective-permute-done.refs_1_, ...), custom_call_target="tpu_custom_call" | custom-call | flops 1 | bytes 1 | tf_op jit(solution)/shard_map/pallas_call | solution.py:82
  12.4 4.9 %all-to-all-start = ((bf16[8,16,768]{2,1,0:T(8,128)(2,1)}), bf16[8,16,768]{2,1,0:T(8,128)(2,1)S(1)}, u32[]{:S(2)}, u32[]{:S(2)}) async-start(bf16[8,16,768]{2,1,0:T(8,128)(2,1)} %get-tuple-element.55), calls=%async_computation | async-start | bytes 393216 | tf_op jit(solution)/shard_map/all_to_all | solution.py:368
  17.3 1.8 %shard_map.137 = (bf16[512,1024]{1,0:T(8,128)(2,1)S(1)}, bf16[512,64]{1,0:T(8,128)(2,1)S(1)}, bf16[512,64]{1,0:T(8,128)(2,1)S(1)}, bf16[64,512]{1,0:T(8,128)(2,1)S(1)}) custom-call(s32[1]{0:T(128)} %bitcast.idx, s32[4,4]{1,0:T(4,128)S(1)} %compare_select_fusion.link, bf16[512,256]{1,0:T(8,128)(2,1)S(1)} %get-tuple-element.56.normed_ref.normed, ...), custom_call_target="tpu_custom_call" | custom-call | flops 20000000000 | bytes 72000000 | tf_op jit(solution)/shard_map/pallas_call | solution.py:82
  19.1 6.5 %all-to-all-done.x_in = bf16[8,16,768]{2,1,0:T(8,128)(2,1)S(1)} async-done(((bf16[8,16,768]{2,1,0:T(8,128)(2,1)}), bf16[8,16,768]{2,1,0:T(8,128)(2,1)S(1)}, u32[]{:S(2)}, u32[]{:S(2)}) %all-to-all-start) | async-done | bytes 196640 | tf_op jit(solution)/shard_map/all_to_all | solution.py:368
  25.7 3.2 %shard_map.138 = (bf16[32,8,128]{2,1,0:T(8,128)(2,1)}, bf16[128,1280]{1,0:T(8,128)(2,1)S(1)}, bf16[128,1280]{1,0:T(8,128)(2,1)}, bf16[8,16,512]{2,1,0:T(8,128)(2,1)}) custom-call(s32[1]{0:T(128)} %bitcast.1.hap, bf16[8,16,768]{2,1,0:T(8,128)(2,1)S(1)} %all-to-all-done.x_in, bf16[256,256]{1,0:T(8,128)(2,1)S(1)} %copy-done.1, ...), custom_call_target="tpu_custom_call" | custom-call | flops 1 | bytes 1 | tf_op jit(solution)/shard_map/pallas_call | solution.py:82
  28.9 0.1 collective-permute-start.3
  29.0 2.8 %all-to-all-start.1 = ((bf16[32,8,128]{2,1,0:T(8,128)(2,1)}), bf16[32,8,128]{2,1,0:T(8,128)(2,1)S(1)}, u32[]{:S(2)}, u32[]{:S(2)}) async-start(bf16[32,8,128]{2,1,0:T(8,128)(2,1)} %get-tuple-element.59), calls=%async_computation.1 | async-start | bytes 131072 | tf_op jit(solution)/shard_map/all_to_all | solution.py:368
  31.8 0.3 collective-permute-start.4
  32.1 1.0 %copy-done.2 = bf16[128,1280]{1,0:T(8,128)(2,1)S(1)} copy-done((bf16[128,1280]{1,0:T(8,128)(2,1)S(1)}, bf16[128,1280]{1,0:T(8,128)(2,1)}, u32[]{:S(2)}) %copy-start.2) | copy-done | bytes 327704
  33.1 0.2 shard_map.139
  33.2 1.7 %collective-permute-start.6 = (bf16[32,1280]{1,0:T(8,128)(2,1)S(1)}, bf16[32,1280]{1,0:T(8,128)(2,1)S(1)}, u32[]{:S(2)}, u32[]{:S(2)}) collective-permute-start(bf16[32,1280]{1,0:T(8,128)(2,1)S(1)} %get-tuple-element.63), channel_id=1, source_target_pairs={{0,8},{8,0},{16,24},{24,16},{1,9},{9,1},{17,25},{25,17},{2,10},{10... | collective-permute-start | bytes 245768 | tf_op jit(solution)/shard_map/ppermute | solution.py:373
  35.0 1.5 %collective-permute-start.7 = (bf16[32,1280]{1,0:T(8,128)(2,1)S(1)}, bf16[32,1280]{1,0:T(8,128)(2,1)S(1)}, u32[]{:S(2)}, u32[]{:S(2)}) collective-permute-start(bf16[32,1280]{1,0:T(8,128)(2,1)S(1)} %get-tuple-element.64), channel_id=1, source_target_pairs={{0,16},{8,24},{16,0},{24,8},{1,17},{9,25},{17,1},{25,9},{2,18},{10... | collective-permute-start | bytes 245768 | tf_op jit(solution)/shard_map/ppermute | solution.py:373
  36.5 0.3 collective-permute-start.8
  36.8 2.4 %all-to-all-done.1.g_in = bf16[32,8,128]{2,1,0:T(8,128)(2,1)S(1)} async-done(((bf16[32,8,128]{2,1,0:T(8,128)(2,1)}), bf16[32,8,128]{2,1,0:T(8,128)(2,1)S(1)}, u32[]{:S(2)}, u32[]{:S(2)}) %all-to-all-start.1) | async-done | bytes 65568 | tf_op jit(solution)/shard_map/all_to_all | solution.py:368
  39.2 1.7 %shard_map.141 = (bf16[128,192]{1,0:T(8,128)(2,1)S(1)}, bf16[128,192]{1,0:T(8,128)(2,1)S(1)}, bf16[128,192]{1,0:T(8,128)(2,1)S(1)}, bf16[128,192]{1,0:T(8,128)(2...) custom-call(s32[1]{0:T(128)} %bitcast.idx, s32[1]{0:T(128)S(6)} %select_n.11.core, ...), custom_call_target="tpu_custom_call" | custom-call | flops 1 | bytes 1 | tf_op jit(solution)/shard_map/pallas_call | solution.py:82
  41.0 0.1 collective-permute-start.5
  41.0 1.2 %collective-permute-done.5.row_got = bf16[96,256]{1,0:T(8,128)(2,1)S(1)} collective-permute-done((bf16[96,256]{1,0:T(8,128)(2,1)S(1)}, bf16[96,256]{1,0:T(8,128)(2,1)S(1)}, u32[]{:S(2)}, u32[]{:S(2)}) %collective-permute-start.5) | collective-permute-done | bytes 49184 | tf_op jit(solution)/shard_map/ppermute | solution.py:373
  42.3 1.1 %collective-permute-start.9 = (bf16[320,256]{1,0:T(8,128)(2,1)S(1)}, bf16[320,256]{1,0:T(8,128)(2,1)S(1)}, u32[]{:S(2)}, u32[]{:S(2)}) collective-permute-start(bf16[320,256]{1,0:T(8,128)(2,1)S(1)} %get-tuple-element.75.mine), channel_id=1, source_target_pairs={{0,2},{1,3},{2,0},{3,1},{4,6},{5,7},{6,4},{7,5},{8,10},{9,11},{10,... | collective-permute-start | bytes 491528 | tf_op jit(solution)/shard_map/ppermute | solution.py:373
  43.4 2.5 %collective-permute-start.10 = (bf16[64,256]{1,0:T(8,128)(2,1)S(1)}, bf16[64,256]{1,0:T(8,128)(2,1)S(1)}, u32[]{:S(2)}, u32[]{:S(2)}) collective-permute-start(bf16[64,256]{1,0:T(8,128)(2,1)S(1)} %get-tuple-element.76), channel_id=1, source_target_pairs={{0,4},{1,5},{2,6},{3,7},{4,0},{5,1},{6,2},{7,3},{8,12},{9,13},{10,... | collective-permute-start | bytes 98312 | tf_op jit(solution)/shard_map/ppermute | solution.py:373
  45.8 0.9 %collective-permute-start.11 = (bf16[64,256]{1,0:T(8,128)(2,1)S(1)}, bf16[64,256]{1,0:T(8,128)(2,1)S(1)}, u32[]{:S(2)}, u32[]{:S(2)}) collective-permute-start(bf16[64,256]{1,0:T(8,128)(2,1)S(1)} %get-tuple-element.77), channel_id=1, source_target_pairs={{0,6},{1,7},{2,4},{3,5},{4,2},{5,3},{6,0},{7,1},{8,14},{9,15},{10,... | collective-permute-start | bytes 98312 | tf_op jit(solution)/shard_map/ppermute | solution.py:373
  46.8 1.5 %collective-permute-done.10.refs_5_ = bf16[64,256]{1,0:T(8,128)(2,1)S(1)} collective-permute-done((bf16[64,256]{1,0:T(8,128)(2,1)S(1)}, bf16[64,256]{1,0:T(8,128)(2,1)S(1)}, u32[]{:S(2)}, u32[]{:S(2)}) %collective-permute-start.10) | collective-permute-done | bytes 32800 | tf_op jit(solution)/shard_map/ppermute | solution.py:373
  48.3 3.3 %collective-permute-done.11.refs_6_ = bf16[64,256]{1,0:T(8,128)(2,1)S(1)} collective-permute-done((bf16[64,256]{1,0:T(8,128)(2,1)S(1)}, bf16[64,256]{1,0:T(8,128)(2,1)S(1)}, u32[]{:S(2)}, u32[]{:S(2)}) %collective-permute-start.11) | collective-permute-done | bytes 32800 | tf_op jit(solution)/shard_map/ppermute | solution.py:373
  51.7 0.6 collective-permute-start.13
  52.3 0.9 %collective-permute-start.14 = (bf16[128,192]{1,0:T(8,128)(2,1)S(1)}, bf16[128,192]{1,0:T(8,128)(2,1)S(1)}, u32[]{:S(2)}, u32[]{:S(2)}) collective-permute-start(bf16[128,192]{1,0:T(8,128)(2,1)S(1)} %get-tuple-element.85), channel_id=1, source_target_pairs={{0,16},{8,24},{16,0},{24,8},{1,17},{9,25},{17,1},{25,9},{2,18},{10... | collective-permute-start | bytes 147464 | tf_op jit(solution)/shard_map/ppermute | solution.py:373
  53.2 2.1 %collective-permute-start.15 = (bf16[128,192]{1,0:T(8,128)(2,1)S(1)}, bf16[128,192]{1,0:T(8,128)(2,1)S(1)}, u32[]{:S(2)}, u32[]{:S(2)}) collective-permute-start(bf16[128,192]{1,0:T(8,128)(2,1)S(1)} %get-tuple-element.86), channel_id=1, source_target_pairs={{0,24},{8,16},{16,8},{24,0},{1,25},{9,17},{17,9},{25,1},{2,26},{10... | collective-permute-start | bytes 147464 | tf_op jit(solution)/shard_map/ppermute | solution.py:373
  55.2 0.8 %collective-permute-done.13.refs_0_ = bf16[128,192]{1,0:T(8,128)(2,1)S(1)} collective-permute-done((bf16[128,192]{1,0:T(8,128)(2,1)S(1)}, bf16[128,192]{1,0:T(8,128)(2,1)S(1)}, u32[]{:S(2)}, u32[]{:S(2)}) %collective-permute-start.13) | collective-permute-done | bytes 49184 | tf_op jit(solution)/shard_map/ppermute | solution.py:373
  56.0 0.5 collective-permute-done.14.refs_1_
  56.6 1.8 %collective-permute-done.15.refs_2_ = bf16[128,192]{1,0:T(8,128)(2,1)S(1)} collective-permute-done((bf16[128,192]{1,0:T(8,128)(2,1)S(1)}, bf16[128,192]{1,0:T(8,128)(2,1)S(1)}, u32[]{:S(2)}, u32[]{:S(2)}) %collective-permute-start.15) | collective-permute-done | bytes 49184 | tf_op jit(solution)/shard_map/ppermute | solution.py:373
  58.4 1.5 %collective-permute-start.16 = (bf16[256,256]{1,0:T(8,128)(2,1)S(1)}, bf16[256,256]{1,0:T(8,128)(2,1)S(1)}, u32[]{:S(2)}, u32[]{:S(2)}) collective-permute-start(bf16[256,256]{1,0:T(8,128)(2,1)S(1)} %shard_map.144.refs_0_), channel_id=1, source_target_pairs={{0,8},{8,0},{16,24},{24,16},{1,9},{9,1},{17,25},{25,17},{2,10},{10... | collective-permute-start | bytes 393224 | tf_op jit(solution)/shard_map/ppermute | solution.py:373
  59.9 1.2 %collective-permute-start.19 = (bf16[256,256]{1,0:T(8,128)(2,1)S(1)}, bf16[256,256]{1,0:T(8,128)(2,1)S(1)}, u32[]{:S(2)}, u32[]{:S(2)}) collective-permute-start(bf16[256,256]{1,0:T(8,128)(2,1)S(1)} %shard_map.144.refs_0_), channel_id=1, source_target_pairs={{0,16},{8,24},{16,0},{24,8},{1,17},{9,25},{17,1},{25,9},{2,18},{10... | collective-permute-start | bytes 393224 | tf_op jit(solution)/shard_map/ppermute | solution.py:373
  61.1 0.8 %collective-permute-start.21 = (bf16[256,256]{1,0:T(8,128)(2,1)S(1)}, bf16[256,256]{1,0:T(8,128)(2,1)S(1)}, u32[]{:S(2)}, u32[]{:S(2)}) collective-permute-start(bf16[256,256]{1,0:T(8,128)(2,1)S(1)} %shard_map.144.refs_0_), channel_id=1, source_target_pairs={{0,24},{8,16},{16,8},{24,0},{1,25},{9,17},{17,9},{25,1},{2,26},{10... | collective-permute-start | bytes 393224 | tf_op jit(solution)/shard_map/ppermute | solution.py:373
  61.9 1.0 %shard_map.145 = (bf16[128,256]{1,0:T(8,128)(2,1)}, bf16[128,256]{1,0:T(8,128)(2,1)}) custom-call(s32[1]{0:T(128)} %bitcast.idx, s32[1]{0:T(128)} %bitcast.1.hap, bf16[128,256]{1,0:T(8,128)(2,1)S(1)} %bitcast.18, f32[2,256]{1,0:T(2,128)S(1)} %pad_maximum_fusion.refs_5_.gain, bf16[768,256]{1,0:T(8,128)(2,1)S(1)} %bitcast.12, ...), custom_call_target="tpu_custom_call" | custom-call | flops 1 | bytes 1 | tf_op jit(solution)/shard_map/pallas_call | solution.py:82
  62.9 0.5 collective-permute-done.16.refs_2_
  63.4 5.2 %collective-permute-done.19.refs_4_ = bf16[256,256]{1,0:T(8,128)(2,1)S(1)} collective-permute-done((bf16[256,256]{1,0:T(8,128)(2,1)S(1)}, bf16[256,256]{1,0:T(8,128)(2,1)S(1)}, u32[]{:S(2)}, u32[]{:S(2)}) %collective-permute-start.19) | collective-permute-done | bytes 131104 | tf_op jit(solution)/shard_map/ppermute | solution.py:373
  68.6 0.5 collective-permute-start.22
  69.1 0.8 %collective-permute-done.20.refs_5_ = bf16[256,256]{1,0:T(8,128)(2,1)S(1)} collective-permute-done((bf16[256,256]{1,0:T(8,128)(2,1)S(1)}, bf16[256,256]{1,0:T(8,128)(2,1)S(1)}, u32[]{:S(2)}, u32[]{:S(2)}) %collective-permute-start.20) | collective-permute-done | bytes 131104 | tf_op jit(solution)/shard_map/ppermute | solution.py:373
  70.0 0.2 collective-permute-done.22.refs_7_
  70.2 1.5 %shard_map.146 = (f32[256,768]{1,0:T(8,128)}, f32[256,256]{1,0:T(8,128)}, f32[256,768]{1,0:T(8,128)}, f32[256,256]{1,0:T(8,128)}) custom-call(s32[1]{0:T(128)} %bitcast.idx, s32[1]{0:T(128)S(6)} %select_n.11.core, bf16[256,256]{1,0:T(8,128)(2,1)S(1)} %shard_map.144.refs_0_, bf16[256,256]{1,0:T(8,128)(2,1)S(1)} %collective-permute-done.17.refs_1_, ...), custom_call_target="tpu_custom_call" | custom-call | flops 1 | bytes 1 | tf_op jit(solution)/shard_map/pallas_call | solution.py:82
  (39 shorter events, 0.3 us)
Async XLA Ops:
  0.6 7.6 %collective-permute-start = (bf16[128,256]{1,0:T(8,128)(2,1)}, bf16[128,256]{1,0:T(8,128)(2,1)S(1)}, u32[]{:S(2)}, u32[]{:S(2)}) collective-permute-start(bf16[128,256]{1,0:T(8,128)(2,1)} %bitcast.14), channel_id=1, source_target_pairs={{0,24},{8,16},{16,8},{24,0},{1,25},{9,17},{17,9},{25,1},{2,26},{10... | collective-permute-start | bytes 196616 | tf_op jit(solution)/shard_map/ppermute | solution.py:373
  4.6 4.5 %collective-permute-start.1 = (bf16[128,256]{1,0:T(8,128)(2,1)}, bf16[128,256]{1,0:T(8,128)(2,1)S(1)}, u32[]{:S(2)}, u32[]{:S(2)}) collective-permute-start(bf16[128,256]{1,0:T(8,128)(2,1)} %bitcast.15), channel_id=1, source_target_pairs={{0,16},{8,24},{16,0},{24,8},{1,17},{9,25},{17,1},{25,9},{2,18},{10... | collective-permute-start | bytes 196616 | tf_op jit(solution)/shard_map/ppermute | solution.py:373
  5.1 4.5 %collective-permute-start.2 = (bf16[128,256]{1,0:T(8,128)(2,1)}, bf16[128,256]{1,0:T(8,128)(2,1)S(1)}, u32[]{:S(2)}, u32[]{:S(2)}) collective-permute-start(bf16[128,256]{1,0:T(8,128)(2,1)} %bitcast.16), channel_id=1, source_target_pairs={{0,8},{8,0},{16,24},{24,16},{1,9},{9,1},{17,25},{25,17},{2,10},{10... | collective-permute-start | bytes 196616 | tf_op jit(solution)/shard_map/ppermute | solution.py:373
  5.2 1.2 %copy-start.7 = (s32[4,4]{1,0:T(4,128)S(1)}, s32[4,4]{1,0:T(4,128)}, u32[]{:S(2)}) copy-start(s32[4,4]{1,0:T(4,128)} %param.10) | copy-start | bytes 196
  6.4 1.0 %slice-start = ((bf16[256,768]{1,0:T(8,128)(2,1)}), bf16[256,512]{1,0:T(8,128)(2,1)S(1)}, s32[]{:S(2)}) async-start(bf16[256,768]{1,0:T(8,128)(2,1)} %col_proj.1), calls=%async_computation.2 | async-start | bytes 524288 | tf_op jit(solution)/shard_map/slice | solution.py:408
  7.4 0.7 copy-start.9
  7.4 2.2 %copy-start.1 = (bf16[256,256]{1,0:T(8,128)(2,1)S(1)}, bf16[256,256]{1,0:T(8,128)(2,1)}, u32[]{:S(2)}) copy-start(bf16[256,256]{1,0:T(8,128)(2,1)} %row_out.1) | copy-start | bytes 393220
  7.4 2.2 %copy-start.3 = (bf16[128,1,256]{2,0,1:T(8,128)(2,1)S(1)}, bf16[128,1,256]{2,0,1:T(8,128)(2,1)}, u32[]{:S(2)}) copy-start(bf16[128,1,256]{2,0,1:T(8,128)(2,1)} %param.9) | copy-start | bytes 196612
  7.4 2.2 %copy-start.6 = (bf16[128,1,256]{2,0,1:T(8,128)(2,1)S(1)}, bf16[128,1,256]{2,0,1:T(8,128)(2,1)}, u32[]{:S(2)}) copy-start(bf16[128,1,256]{2,0,1:T(8,128)(2,1)} %param.17) | copy-start | bytes 196612
  7.6 0.7 copy-start.8
  12.4 13.2 %all-to-all-start = ((bf16[8,16,768]{2,1,0:T(8,128)(2,1)}), bf16[8,16,768]{2,1,0:T(8,128)(2,1)S(1)}, u32[]{:S(2)}, u32[]{:S(2)}) async-start(bf16[8,16,768]{2,1,0:T(8,128)(2,1)} %get-tuple-element.55), calls=%async_computation | async-start | bytes 393216 | tf_op jit(solution)/shard_map/all_to_all | solution.py:368
  17.3 8.3 %copy-start = (bf16[256,768]{1,0:T(8,128)(2,1)S(1)}, bf16[256,768]{1,0:T(8,128)(2,1)}, u32[]{:S(2)}) copy-start(bf16[256,768]{1,0:T(8,128)(2,1)} %col_proj.1) | copy-start | bytes 1179652
  17.3 8.3 %copy-start.5 = (bf16[256,256]{1,0:T(8,128)(2,1)S(1)}, bf16[256,256]{1,0:T(8,128)(2,1)}, u32[]{:S(2)}) copy-start(bf16[256,256]{1,0:T(8,128)(2,1)} %col_out.1) | copy-start | bytes 393220
  28.9 2.9 %copy-start.4 = (bf16[8,16,512]{2,1,0:T(8,128)(2,1)S(1)}, bf16[8,16,512]{2,1,0:T(8,128)(2,1)}, u32[]{:S(2)}) copy-start(bf16[8,16,512]{2,1,0:T(8,128)(2,1)} %get-tuple-element.66.og) | copy-start | bytes 393220
  28.9 3.2 %collective-permute-start.3 = (bf16[128,1280]{1,0:T(8,128)(2,1)S(1)}, bf16[128,1280]{1,0:T(8,128)(2,1)S(1)}, u32[]{:S(2)}, u32[]{:S(2)}) collective-permute-start(bf16[128,1280]{1,0:T(8,128)(2,1)S(1)} %get-tuple-element.61), channel_id=1, source_target_pairs={{0,1},{1,0},{2,3},{3,2},{4,5},{5,4},{6,7},{7,6},{8,9},{9,8},{10,11... | collective-permute-start | bytes 983048 | tf_op jit(solution)/shard_map/ppermute | solution.py:373
  29.0 10.3 %all-to-all-start.1 = ((bf16[32,8,128]{2,1,0:T(8,128)(2,1)}), bf16[32,8,128]{2,1,0:T(8,128)(2,1)S(1)}, u32[]{:S(2)}, u32[]{:S(2)}) async-start(bf16[32,8,128]{2,1,0:T(8,128)(2,1)} %get-tuple-element.59), calls=%async_computation.1 | async-start | bytes 131072 | tf_op jit(solution)/shard_map/all_to_all | solution.py:368
  31.8 5.0 %collective-permute-start.4 = (bf16[4,16,512]{2,1,0:T(8,128)(2,1)S(1)}, bf16[4,16,512]{2,1,0:T(8,128)(2,1)S(1)}, u32[]{:S(2)}, u32[]{:S(2)}) collective-permute-start(bf16[4,16,512]{2,1,0:T(8,128)(2,1)S(1)} %get-tuple-element.67), channel_id=1, source_target_pairs={{0,1},{1,0},{2,3},{3,2},{4,5},{5,4},{6,7},{7,6},{8,9},{9,8},{10,11... | collective-permute-start | bytes 196616 | tf_op jit(solution)/shard_map/ppermute | solution.py:373
  32.1 1.0 %copy-start.2 = (bf16[128,1280]{1,0:T(8,128)(2,1)S(1)}, bf16[128,1280]{1,0:T(8,128)(2,1)}, u32[]{:S(2)}) copy-start(bf16[128,1280]{1,0:T(8,128)(2,1)} %get-tuple-element.60.keep) | copy-start | bytes 983044
  33.2 9.0 %collective-permute-start.6 = (bf16[32,1280]{1,0:T(8,128)(2,1)S(1)}, bf16[32,1280]{1,0:T(8,128)(2,1)S(1)}, u32[]{:S(2)}, u32[]{:S(2)}) collective-permute-start(bf16[32,1280]{1,0:T(8,128)(2,1)S(1)} %get-tuple-element.63), channel_id=1, source_target_pairs={{0,8},{8,0},{16,24},{24,16},{1,9},{9,1},{17,25},{25,17},{2,10},{10... | collective-permute-start | bytes 245768 | tf_op jit(solution)/shard_map/ppermute | solution.py:373
  35.0 7.3 %collective-permute-start.7 = (bf16[32,1280]{1,0:T(8,128)(2,1)S(1)}, bf16[32,1280]{1,0:T(8,128)(2,1)S(1)}, u32[]{:S(2)}, u32[]{:S(2)}) collective-permute-start(bf16[32,1280]{1,0:T(8,128)(2,1)S(1)} %get-tuple-element.64), channel_id=1, source_target_pairs={{0,16},{8,24},{16,0},{24,8},{1,17},{9,25},{17,1},{25,9},{2,18},{10... | collective-permute-start | bytes 245768 | tf_op jit(solution)/shard_map/ppermute | solution.py:373
  36.5 5.8 %collective-permute-start.8 = (bf16[32,1280]{1,0:T(8,128)(2,1)S(1)}, bf16[32,1280]{1,0:T(8,128)(2,1)S(1)}, u32[]{:S(2)}, u32[]{:S(2)}) collective-permute-start(bf16[32,1280]{1,0:T(8,128)(2,1)S(1)} %get-tuple-element.65), channel_id=1, source_target_pairs={{0,24},{8,16},{16,8},{24,0},{1,25},{9,17},{17,9},{25,1},{2,26},{10... | collective-permute-start | bytes 245768 | tf_op jit(solution)/shard_map/ppermute | solution.py:373
  41.0 1.3 %collective-permute-start.5 = (bf16[96,256]{1,0:T(8,128)(2,1)S(1)}, bf16[96,256]{1,0:T(8,128)(2,1)S(1)}, u32[]{:S(2)}, u32[]{:S(2)}) collective-permute-start(bf16[96,256]{1,0:T(8,128)(2,1)S(1)} %get-tuple-element.73), channel_id=1, source_target_pairs={{0,1},{1,0},{2,3},{3,2},{4,5},{5,4},{6,7},{7,6},{8,9},{9,8},{10,11... | collective-permute-start | bytes 147464 | tf_op jit(solution)/shard_map/ppermute | solution.py:373
  42.3 9.2 %collective-permute-start.9 = (bf16[320,256]{1,0:T(8,128)(2,1)S(1)}, bf16[320,256]{1,0:T(8,128)(2,1)S(1)}, u32[]{:S(2)}, u32[]{:S(2)}) collective-permute-start(bf16[320,256]{1,0:T(8,128)(2,1)S(1)} %get-tuple-element.75.mine), channel_id=1, source_target_pairs={{0,2},{1,3},{2,0},{3,1},{4,6},{5,7},{6,4},{7,5},{8,10},{9,11},{10,... | collective-permute-start | bytes 491528 | tf_op jit(solution)/shard_map/ppermute | solution.py:373
  43.4 4.9 %collective-permute-start.10 = (bf16[64,256]{1,0:T(8,128)(2,1)S(1)}, bf16[64,256]{1,0:T(8,128)(2,1)S(1)}, u32[]{:S(2)}, u32[]{:S(2)}) collective-permute-start(bf16[64,256]{1,0:T(8,128)(2,1)S(1)} %get-tuple-element.76), channel_id=1, source_target_pairs={{0,4},{1,5},{2,6},{3,7},{4,0},{5,1},{6,2},{7,3},{8,12},{9,13},{10,... | collective-permute-start | bytes 98312 | tf_op jit(solution)/shard_map/ppermute | solution.py:373
  45.8 5.7 %collective-permute-start.11 = (bf16[64,256]{1,0:T(8,128)(2,1)S(1)}, bf16[64,256]{1,0:T(8,128)(2,1)S(1)}, u32[]{:S(2)}, u32[]{:S(2)}) collective-permute-start(bf16[64,256]{1,0:T(8,128)(2,1)S(1)} %get-tuple-element.77), channel_id=1, source_target_pairs={{0,6},{1,7},{2,4},{3,5},{4,2},{5,3},{6,0},{7,1},{8,14},{9,15},{10,... | collective-permute-start | bytes 98312 | tf_op jit(solution)/shard_map/ppermute | solution.py:373
  51.6 6.7 %collective-permute-start.12 = (bf16[256,256]{1,0:T(8,128)(2,1)S(1)}, bf16[256,256]{1,0:T(8,128)(2,1)S(1)}, u32[]{:S(2)}, u32[]{:S(2)}) collective-permute-start(bf16[256,256]{1,0:T(8,128)(2,1)S(1)} %shard_map.143.mine), channel_id=1, source_target_pairs={{0,4},{1,5},{2,6},{3,7},{4,0},{5,1},{6,2},{7,3},{8,12},{9,13},{10,... | collective-permute-start | bytes 393224 | tf_op jit(solution)/shard_map/ppermute | solution.py:373
  51.7 4.3 %collective-permute-start.13 = (bf16[128,192]{1,0:T(8,128)(2,1)S(1)}, bf16[128,192]{1,0:T(8,128)(2,1)S(1)}, u32[]{:S(2)}, u32[]{:S(2)}) collective-permute-start(bf16[128,192]{1,0:T(8,128)(2,1)S(1)} %get-tuple-element.84), channel_id=1, source_target_pairs={{0,8},{8,0},{16,24},{24,16},{1,9},{9,1},{17,25},{25,17},{2,10},{10... | collective-permute-start | bytes 147464 | tf_op jit(solution)/shard_map/ppermute | solution.py:373
  52.3 4.3 %collective-permute-start.14 = (bf16[128,192]{1,0:T(8,128)(2,1)S(1)}, bf16[128,192]{1,0:T(8,128)(2,1)S(1)}, u32[]{:S(2)}, u32[]{:S(2)}) collective-permute-start(bf16[128,192]{1,0:T(8,128)(2,1)S(1)} %get-tuple-element.85), channel_id=1, source_target_pairs={{0,16},{8,24},{16,0},{24,8},{1,17},{9,25},{17,1},{25,9},{2,18},{10... | collective-permute-start | bytes 147464 | tf_op jit(solution)/shard_map/ppermute | solution.py:373
  53.2 5.2 %collective-permute-start.15 = (bf16[128,192]{1,0:T(8,128)(2,1)S(1)}, bf16[128,192]{1,0:T(8,128)(2,1)S(1)}, u32[]{:S(2)}, u32[]{:S(2)}) collective-permute-start(bf16[128,192]{1,0:T(8,128)(2,1)S(1)} %get-tuple-element.86), channel_id=1, source_target_pairs={{0,24},{8,16},{16,8},{24,0},{1,25},{9,17},{17,9},{25,1},{2,26},{10... | collective-permute-start | bytes 147464 | tf_op jit(solution)/shard_map/ppermute | solution.py:373
  58.4 5.0 %collective-permute-start.16 = (bf16[256,256]{1,0:T(8,128)(2,1)S(1)}, bf16[256,256]{1,0:T(8,128)(2,1)S(1)}, u32[]{:S(2)}, u32[]{:S(2)}) collective-permute-start(bf16[256,256]{1,0:T(8,128)(2,1)S(1)} %shard_map.144.refs_0_), channel_id=1, source_target_pairs={{0,8},{8,0},{16,24},{24,16},{1,9},{9,1},{17,25},{25,17},{2,10},{10... | collective-permute-start | bytes 393224 | tf_op jit(solution)/shard_map/ppermute | solution.py:373
  59.9 3.5 %collective-permute-start.17 = (bf16[256,256]{1,0:T(8,128)(2,1)S(1)}, bf16[256,256]{1,0:T(8,128)(2,1)S(1)}, u32[]{:S(2)}, u32[]{:S(2)}) collective-permute-start(bf16[256,256]{1,0:T(8,128)(2,1)S(1)} %shard_map.144.refs_0_), channel_id=1, source_target_pairs={{0,1},{1,0},{2,3},{3,2},{4,5},{5,4},{6,7},{7,6},{8,9},{9,8},{10,11... | collective-permute-start | bytes 393224 | tf_op jit(solution)/shard_map/ppermute | solution.py:373
  59.9 8.7 %collective-permute-start.19 = (bf16[256,256]{1,0:T(8,128)(2,1)S(1)}, bf16[256,256]{1,0:T(8,128)(2,1)S(1)}, u32[]{:S(2)}, u32[]{:S(2)}) collective-permute-start(bf16[256,256]{1,0:T(8,128)(2,1)S(1)} %shard_map.144.refs_0_), channel_id=1, source_target_pairs={{0,16},{8,24},{16,0},{24,8},{1,17},{9,25},{17,1},{25,9},{2,18},{10... | collective-permute-start | bytes 393224 | tf_op jit(solution)/shard_map/ppermute | solution.py:373
  61.1 7.6 %collective-permute-start.21 = (bf16[256,256]{1,0:T(8,128)(2,1)S(1)}, bf16[256,256]{1,0:T(8,128)(2,1)S(1)}, u32[]{:S(2)}, u32[]{:S(2)}) collective-permute-start(bf16[256,256]{1,0:T(8,128)(2,1)S(1)} %shard_map.144.refs_0_), channel_id=1, source_target_pairs={{0,24},{8,16},{16,8},{24,0},{1,25},{9,17},{17,9},{25,1},{2,26},{10... | collective-permute-start | bytes 393224 | tf_op jit(solution)/shard_map/ppermute | solution.py:373
  63.4 5.7 %collective-permute-start.18 = (bf16[256,256]{1,0:T(8,128)(2,1)S(1)}, bf16[256,256]{1,0:T(8,128)(2,1)S(1)}, u32[]{:S(2)}, u32[]{:S(2)}) collective-permute-start(bf16[256,256]{1,0:T(8,128)(2,1)S(1)} %collective-permute-done.16.refs_2_), channel_id=1, source_target_pairs={{0,1},{1,0},{2,3},{3,2},{4,5},{5,4},{6,7},{7,6},{8,9},{9,8},{10,11... | collective-permute-start | bytes 393224 | tf_op jit(solution)/shard_map/ppermute | solution.py:373
  68.6 1.3 %collective-permute-start.20 = (bf16[256,256]{1,0:T(8,128)(2,1)S(1)}, bf16[256,256]{1,0:T(8,128)(2,1)S(1)}, u32[]{:S(2)}, u32[]{:S(2)}) collective-permute-start(bf16[256,256]{1,0:T(8,128)(2,1)S(1)} %collective-permute-done.19.refs_4_), channel_id=1, source_target_pairs={{0,1},{1,0},{2,3},{3,2},{4,5},{5,4},{6,7},{7,6},{8,9},{9,8},{10,11... | collective-permute-start | bytes 393224 | tf_op jit(solution)/shard_map/ppermute | solution.py:373
  68.6 1.5 %collective-permute-start.22 = (bf16[256,256]{1,0:T(8,128)(2,1)S(1)}, bf16[256,256]{1,0:T(8,128)(2,1)S(1)}, u32[]{:S(2)}, u32[]{:S(2)}) collective-permute-start(bf16[256,256]{1,0:T(8,128)(2,1)S(1)} %collective-permute-done.21.refs_6_), channel_id=1, source_target_pairs={{0,1},{1,0},{2,3},{3,2},{4,5},{5,4},{6,7},{7,6},{8,9},{9,8},{10,11... | collective-permute-start | bytes 393224 | tf_op jit(solution)/shard_map/ppermute | solution.py:373

commit v18 on v16

--- a/solution.py
+++ b/solution.py
@@ -472,7 +472,8 @@
     )
     near_got = swapped(near, "hap", 2)
     far = [swapped(x, "hap", 2 * (j + 2)) for j, x in enumerate(far)]
-    near_got, far = lax.optimization_barrier((near_got, far))
+    near_got, far = lax.optimization_barrier((near_got, far[::-1]))
+    far = far[::-1]
     parts = [own, near_got] + list(far)
     left, right, step = near, near_got, 2
     while 2 * step < haps:

time: 70.6 us -> 70.8 us (level)
  no operation moved by 1% of the time
where the time goes in v18:
time: 70.8 us; the launch traced here: 70.4 us
  starting transfers between devices  27.9 us (39%)
  waiting for transfers between devices  25.4 us (36%)
  Pallas kernels  12.3 us (17%)
  local copies, waits for them, and re-layouts  3.94 us (6%)
  between operations  0.82 us (1%)
    ppermute x23, starting transfers between devices, swapped(): return lax.ppermute(value, axis, [(i, i ^ by) for i in range(length)])  20.2 us
    ppermute x23, waiting for transfers between devices, swapped(): return lax.ppermute(value, axis, [(i, i ^ by) for i in range(length)])  16.5 us
    pallas_call x11, Pallas kernels, call(): pl.pallas_call(body, out_shape=[jax.ShapeDtypeStruct(s, d) for s, d in ou...  12.3 us
    all_to_all x2, waiting for transfers between devices, exchange(): return lax.all_to_all(value, axis, 0, 0, tiled=True)  8.94 us
    all_to_all x2, starting transfers between devices, exchange(): return lax.all_to_all(value, axis, 0, 0, tiled=True)  7.64 us
    unnamed x22, local copies, waits for them, and re-layouts  2.99 us
  transfers between devices with their start and end apart: 25, of which 16 were waited for; matrix products, arithmetic and copies ran while one was open for 2% of the time, Pallas kernels for 7%

profile of v18, /device:TPU:0, one launch (start us, length us, event | category | flops | bytes accessed | tf_op | source)
XLA Modules:
  0.0 70.4 jit_solution(11819674828172992891)
XLA Ops:
  0.6 4.0 %collective-permute-start = (bf16[128,256]{1,0:T(8,128)(2,1)}, bf16[128,256]{1,0:T(8,128)(2,1)S(1)}, u32[]{:S(2)}, u32[]{:S(2)}) collective-permute-start(bf16[128,256]{1,0:T(8,128)(2,1)} %bitcast.14), channel_id=1, source_target_pairs={{0,24},{8,16},{16,8},{24,0},{1,25},{9,17},{17,9},{25,1},{2,26},{10... | collective-permute-start | bytes 196616 | tf_op jit(solution)/shard_map/ppermute | solution.py:373
  4.6 0.5 collective-permute-start.1
  5.1 0.1 collective-permute-start.2
  5.2 1.2 %copy.15 = bf16[256,768]{0,1:T(8,128)(2,1)S(1)} copy(bf16[256,768]{1,0:T(8,128)(2,1)} %param.12) | data formatting | bytes 786432 | tf_op args[3]
  6.5 0.9 %slice-done = bf16[256,512]{1,0:T(8,128)(2,1)S(1)} async-done(((bf16[256,768]{1,0:T(8,128)(2,1)}), bf16[256,512]{1,0:T(8,128)(2,1)S(1)}, s32[]{:S(2)}) %slice-start) | async-done | bytes 262168 | tf_op jit(solution)/shard_map/slice | solution.py:408
  7.4 0.1 copy.17
  7.6 0.5 copy-done.9
  8.1 0.2 copy-done.8
  8.2 0.8 %collective-permute-done.1.refs_2_ = bf16[128,256]{1,0:T(8,128)(2,1)S(1)} collective-permute-done((bf16[128,256]{1,0:T(8,128)(2,1)}, bf16[128,256]{1,0:T(8,128)(2,1)S(1)}, u32[]{:S(2)}, u32[]{:S(2)}) %collective-permute-start.1) | collective-permute-done | bytes 65568 | tf_op jit(solution)/shard_map/ppermute | solution.py:373
  9.1 0.5 collective-permute-done.2.refs_3_
  9.6 2.8 %shard_map.136 = (bf16[8,16,768]{2,1,0:T(8,128)(2,1)}, bf16[512,256]{1,0:T(8,128)(2,1)S(1)}) custom-call(s32[1]{0:T(128)} %bitcast.idx, s32[4,4]{1,0:T(4,128)S(1)} %compare_select_fusion.link, bf16[128,256]{1,0:T(8,128)(2,1)S(1)} %bitcast.17, bf16[128,256]{1,0:T(8,128)(2,1)S(1)} %collective-permute-done.refs_1_, ...), custom_call_target="tpu_custom_call" | custom-call | flops 1 | bytes 1 | tf_op jit(solution)/shard_map/pallas_call | solution.py:82
  12.4 4.9 %all-to-all-start = ((bf16[8,16,768]{2,1,0:T(8,128)(2,1)}), bf16[8,16,768]{2,1,0:T(8,128)(2,1)S(1)}, u32[]{:S(2)}, u32[]{:S(2)}) async-start(bf16[8,16,768]{2,1,0:T(8,128)(2,1)} %get-tuple-element.57), calls=%async_computation | async-start | bytes 393216 | tf_op jit(solution)/shard_map/all_to_all | solution.py:368
  17.3 1.8 %shard_map.137 = (bf16[512,1024]{1,0:T(8,128)(2,1)S(1)}, bf16[512,64]{1,0:T(8,128)(2,1)S(1)}, bf16[512,64]{1,0:T(8,128)(2,1)S(1)}, bf16[64,512]{1,0:T(8,128)(2,1)S(1)}) custom-call(s32[1]{0:T(128)} %bitcast.idx, s32[4,4]{1,0:T(4,128)S(1)} %compare_select_fusion.link, bf16[512,256]{1,0:T(8,128)(2,1)S(1)} %get-tuple-element.58.normed_ref.normed, ...), custom_call_target="tpu_custom_call" | custom-call | flops 20000000000 | bytes 72000000 | tf_op jit(solution)/shard_map/pallas_call | solution.py:82
  19.1 6.5 %all-to-all-done.x_in = bf16[8,16,768]{2,1,0:T(8,128)(2,1)S(1)} async-done(((bf16[8,16,768]{2,1,0:T(8,128)(2,1)}), bf16[8,16,768]{2,1,0:T(8,128)(2,1)S(1)}, u32[]{:S(2)}, u32[]{:S(2)}) %all-to-all-start) | async-done | bytes 196640 | tf_op jit(solution)/shard_map/all_to_all | solution.py:368
  25.7 3.2 %shard_map.138 = (bf16[32,8,128]{2,1,0:T(8,128)(2,1)}, bf16[128,1280]{1,0:T(8,128)(2,1)S(1)}, bf16[128,1280]{1,0:T(8,128)(2,1)}, bf16[8,16,512]{2,1,0:T(8,128)(2,1)}) custom-call(s32[1]{0:T(128)} %bitcast.1.hap, bf16[8,16,768]{2,1,0:T(8,128)(2,1)S(1)} %all-to-all-done.x_in, bf16[256,256]{1,0:T(8,128)(2,1)S(1)} %copy-done.1, ...), custom_call_target="tpu_custom_call" | custom-call | flops 1 | bytes 1 | tf_op jit(solution)/shard_map/pallas_call | solution.py:82
  29.0 2.8 %all-to-all-start.1 = ((bf16[32,8,128]{2,1,0:T(8,128)(2,1)}), bf16[32,8,128]{2,1,0:T(8,128)(2,1)S(1)}, u32[]{:S(2)}, u32[]{:S(2)}) async-start(bf16[32,8,128]{2,1,0:T(8,128)(2,1)} %get-tuple-element.61), calls=%async_computation.1 | async-start | bytes 131072 | tf_op jit(solution)/shard_map/all_to_all | solution.py:368
  31.8 0.3 collective-permute-start.4
  32.1 1.0 %copy-done.2 = bf16[128,1280]{1,0:T(8,128)(2,1)S(1)} copy-done((bf16[128,1280]{1,0:T(8,128)(2,1)S(1)}, bf16[128,1280]{1,0:T(8,128)(2,1)}, u32[]{:S(2)}) %copy-start.2) | copy-done | bytes 327704
  33.1 0.2 shard_map.139
  33.2 1.7 %collective-permute-start.6 = (bf16[32,1280]{1,0:T(8,128)(2,1)S(1)}, bf16[32,1280]{1,0:T(8,128)(2,1)S(1)}, u32[]{:S(2)}, u32[]{:S(2)}) collective-permute-start(bf16[32,1280]{1,0:T(8,128)(2,1)S(1)} %get-tuple-element.65), channel_id=1, source_target_pairs={{0,8},{8,0},{16,24},{24,16},{1,9},{9,1},{17,25},{25,17},{2,10},{10... | collective-permute-start | bytes 245768 | tf_op jit(solution)/shard_map/ppermute | solution.py:373
  35.0 1.5 %collective-permute-start.7 = (bf16[32,1280]{1,0:T(8,128)(2,1)S(1)}, bf16[32,1280]{1,0:T(8,128)(2,1)S(1)}, u32[]{:S(2)}, u32[]{:S(2)}) collective-permute-start(bf16[32,1280]{1,0:T(8,128)(2,1)S(1)} %get-tuple-element.66), channel_id=1, source_target_pairs={{0,16},{8,24},{16,0},{24,8},{1,17},{9,25},{17,1},{25,9},{2,18},{10... | collective-permute-start | bytes 245768 | tf_op jit(solution)/shard_map/ppermute | solution.py:373
  36.5 0.3 collective-permute-start.8
  36.8 2.4 %all-to-all-done.1.g_in = bf16[32,8,128]{2,1,0:T(8,128)(2,1)S(1)} async-done(((bf16[32,8,128]{2,1,0:T(8,128)(2,1)}), bf16[32,8,128]{2,1,0:T(8,128)(2,1)S(1)}, u32[]{:S(2)}, u32[]{:S(2)}) %all-to-all-start.1) | async-done | bytes 65568 | tf_op jit(solution)/shard_map/all_to_all | solution.py:368
  39.2 1.7 %shard_map.141 = (bf16[128,192]{1,0:T(8,128)(2,1)S(1)}, bf16[128,192]{1,0:T(8,128)(2,1)S(1)}, bf16[128,192]{1,0:T(8,128)(2,1)S(1)}, bf16[128,192]{1,0:T(8,128)(2...) custom-call(s32[1]{0:T(128)} %bitcast.idx, s32[1]{0:T(128)S(6)} %select_n.11.core, ...), custom_call_target="tpu_custom_call" | custom-call | flops 1 | bytes 1 | tf_op jit(solution)/shard_map/pallas_call | solution.py:82
  41.0 1.2 %collective-permute-done.5.row_got = bf16[96,256]{1,0:T(8,128)(2,1)S(1)} collective-permute-done((bf16[96,256]{1,0:T(8,128)(2,1)S(1)}, bf16[96,256]{1,0:T(8,128)(2,1)S(1)}, u32[]{:S(2)}, u32[]{:S(2)}) %collective-permute-start.5) | collective-permute-done | bytes 49184 | tf_op jit(solution)/shard_map/ppermute | solution.py:373
  42.3 1.1 %collective-permute-start.9 = (bf16[320,256]{1,0:T(8,128)(2,1)S(1)}, bf16[320,256]{1,0:T(8,128)(2,1)S(1)}, u32[]{:S(2)}, u32[]{:S(2)}) collective-permute-start(bf16[320,256]{1,0:T(8,128)(2,1)S(1)} %get-tuple-element.77.mine), channel_id=1, source_target_pairs={{0,2},{1,3},{2,0},{3,1},{4,6},{5,7},{6,4},{7,5},{8,10},{9,11},{10,... | collective-permute-start | bytes 491528 | tf_op jit(solution)/shard_map/ppermute | solution.py:373
  43.4 2.4 %collective-permute-start.10 = (bf16[64,256]{1,0:T(8,128)(2,1)S(1)}, bf16[64,256]{1,0:T(8,128)(2,1)S(1)}, u32[]{:S(2)}, u32[]{:S(2)}) collective-permute-start(bf16[64,256]{1,0:T(8,128)(2,1)S(1)} %get-tuple-element.78), channel_id=1, source_target_pairs={{0,6},{1,7},{2,4},{3,5},{4,2},{5,3},{6,0},{7,1},{8,14},{9,15},{10,... | collective-permute-start | bytes 98312 | tf_op jit(solution)/shard_map/ppermute | solution.py:373
  45.8 0.1 collective-permute-start.11
  45.9 3.9 %collective-permute-done.10.refs_6_ = bf16[64,256]{1,0:T(8,128)(2,1)S(1)} collective-permute-done((bf16[64,256]{1,0:T(8,128)(2,1)S(1)}, bf16[64,256]{1,0:T(8,128)(2,1)S(1)}, u32[]{:S(2)}, u32[]{:S(2)}) %collective-permute-start.10) | collective-permute-done | bytes 32800 | tf_op jit(solution)/shard_map/ppermute | solution.py:373
  49.8 1.1 %collective-permute-done.11.refs_5_ = bf16[64,256]{1,0:T(8,128)(2,1)S(1)} collective-permute-done((bf16[64,256]{1,0:T(8,128)(2,1)S(1)}, bf16[64,256]{1,0:T(8,128)(2,1)S(1)}, u32[]{:S(2)}, u32[]{:S(2)}) %collective-permute-start.11) | collective-permute-done | bytes 32800 | tf_op jit(solution)/shard_map/ppermute | solution.py:373
  51.0 0.5 collective-permute-start.12
  51.5 0.6 collective-permute-start.13
  52.1 1.2 %collective-permute-start.14 = (bf16[128,192]{1,0:T(8,128)(2,1)S(1)}, bf16[128,192]{1,0:T(8,128)(2,1)S(1)}, u32[]{:S(2)}, u32[]{:S(2)}) collective-permute-start(bf16[128,192]{1,0:T(8,128)(2,1)S(1)} %get-tuple-element.87), channel_id=1, source_target_pairs={{0,16},{8,24},{16,0},{24,8},{1,17},{9,25},{17,1},{25,9},{2,18},{10... | collective-permute-start | bytes 147464 | tf_op jit(solution)/shard_map/ppermute | solution.py:373
  53.4 1.6 %collective-permute-start.15 = (bf16[128,192]{1,0:T(8,128)(2,1)S(1)}, bf16[128,192]{1,0:T(8,128)(2,1)S(1)}, u32[]{:S(2)}, u32[]{:S(2)}) collective-permute-start(bf16[128,192]{1,0:T(8,128)(2,1)S(1)} %get-tuple-element.88), channel_id=1, source_target_pairs={{0,24},{8,16},{16,8},{24,0},{1,25},{9,17},{17,9},{25,1},{2,26},{10... | collective-permute-start | bytes 147464 | tf_op jit(solution)/shard_map/ppermute | solution.py:373
  55.0 0.8 %collective-permute-done.13.refs_0_ = bf16[128,192]{1,0:T(8,128)(2,1)S(1)} collective-permute-done((bf16[128,192]{1,0:T(8,128)(2,1)S(1)}, bf16[128,192]{1,0:T(8,128)(2,1)S(1)}, u32[]{:S(2)}, u32[]{:S(2)}) %collective-permute-start.13) | collective-permute-done | bytes 49184 | tf_op jit(solution)/shard_map/ppermute | solution.py:373
  55.7 0.7 collective-permute-done.14.refs_1_
  56.4 2.8 %collective-permute-done.15.refs_2_ = bf16[128,192]{1,0:T(8,128)(2,1)S(1)} collective-permute-done((bf16[128,192]{1,0:T(8,128)(2,1)S(1)}, bf16[128,192]{1,0:T(8,128)(2,1)S(1)}, u32[]{:S(2)}, u32[]{:S(2)}) %collective-permute-start.15) | collective-permute-done | bytes 49184 | tf_op jit(solution)/shard_map/ppermute | solution.py:373
  59.3 0.1 collective-permute-start.16
  59.4 1.8 %collective-permute-start.17 = (bf16[256,256]{1,0:T(8,128)(2,1)S(1)}, bf16[256,256]{1,0:T(8,128)(2,1)S(1)}, u32[]{:S(2)}, u32[]{:S(2)}) collective-permute-start(bf16[256,256]{1,0:T(8,128)(2,1)S(1)} %shard_map.144.refs_0_), channel_id=1, source_target_pairs={{0,16},{8,24},{16,0},{24,8},{1,17},{9,25},{17,1},{25,9},{2,18},{10... | collective-permute-start | bytes 393224 | tf_op jit(solution)/shard_map/ppermute | solution.py:373
  61.2 1.6 %collective-permute-start.18 = (bf16[256,256]{1,0:T(8,128)(2,1)S(1)}, bf16[256,256]{1,0:T(8,128)(2,1)S(1)}, u32[]{:S(2)}, u32[]{:S(2)}) collective-permute-start(bf16[256,256]{1,0:T(8,128)(2,1)S(1)} %shard_map.144.refs_0_), channel_id=1, source_target_pairs={{0,24},{8,16},{16,8},{24,0},{1,25},{9,17},{17,9},{25,1},{2,26},{10... | collective-permute-start | bytes 393224 | tf_op jit(solution)/shard_map/ppermute | solution.py:373
  62.8 1.0 %shard_map.145 = (bf16[128,256]{1,0:T(8,128)(2,1)}, bf16[128,256]{1,0:T(8,128)(2,1)}) custom-call(s32[1]{0:T(128)} %bitcast.idx, s32[1]{0:T(128)} %bitcast.1.hap, bf16[128,256]{1,0:T(8,128)(2,1)S(1)} %bitcast.18, f32[2,256]{1,0:T(2,128)S(1)} %pad_maximum_fusion.refs_5_.gain, bf16[768,256]{1,0:T(8,128)(2,1)S(1)} %bitcast.12, ...), custom_call_target="tpu_custom_call" | custom-call | flops 1 | bytes 1 | tf_op jit(solution)/shard_map/pallas_call | solution.py:82
  63.8 0.5 collective-permute-done.16.refs_2_
  64.4 2.7 %collective-permute-done.18.refs_6_ = bf16[256,256]{1,0:T(8,128)(2,1)S(1)} collective-permute-done((bf16[256,256]{1,0:T(8,128)(2,1)S(1)}, bf16[256,256]{1,0:T(8,128)(2,1)S(1)}, u32[]{:S(2)}, u32[]{:S(2)}) %collective-permute-start.18) | collective-permute-done | bytes 131104 | tf_op jit(solution)/shard_map/ppermute | solution.py:373
  67.1 0.5 collective-permute-start.21
  67.6 0.8 %collective-permute-done.20.refs_3_ = bf16[256,256]{1,0:T(8,128)(2,1)S(1)} collective-permute-done((bf16[256,256]{1,0:T(8,128)(2,1)S(1)}, bf16[256,256]{1,0:T(8,128)(2,1)S(1)}, u32[]{:S(2)}, u32[]{:S(2)}) %collective-permute-start.20) | collective-permute-done | bytes 131104 | tf_op jit(solution)/shard_map/ppermute | solution.py:373
  68.4 0.2 collective-permute-done.21.refs_5_
  68.6 0.3 collective-permute-done.22.refs_7_
  68.9 1.5 %shard_map.146 = (f32[256,768]{1,0:T(8,128)}, f32[256,256]{1,0:T(8,128)}, f32[256,768]{1,0:T(8,128)}, f32[256,256]{1,0:T(8,128)}) custom-call(s32[1]{0:T(128)} %bitcast.idx, s32[1]{0:T(128)S(6)} %select_n.11.core, bf16[256,256]{1,0:T(8,128)(2,1)S(1)} %shard_map.144.refs_0_, bf16[256,256]{1,0:T(8,128)(2,1)S(1)} %collective-permute-done.19.refs_1_, ...), custom_call_target="tpu_custom_call" | custom-call | flops 1 | bytes 1 | tf_op jit(solution)/shard_map/pallas_call | solution.py:82
  (39 shorter events, 0.4 us)
Async XLA Ops:
  0.6 7.6 %collective-permute-start = (bf16[128,256]{1,0:T(8,128)(2,1)}, bf16[128,256]{1,0:T(8,128)(2,1)S(1)}, u32[]{:S(2)}, u32[]{:S(2)}) collective-permute-start(bf16[128,256]{1,0:T(8,128)(2,1)} %bitcast.14), channel_id=1, source_target_pairs={{0,24},{8,16},{16,8},{24,0},{1,25},{9,17},{17,9},{25,1},{2,26},{10... | collective-permute-start | bytes 196616 | tf_op jit(solution)/shard_map/ppermute | solution.py:373
  4.6 4.5 %collective-permute-start.1 = (bf16[128,256]{1,0:T(8,128)(2,1)}, bf16[128,256]{1,0:T(8,128)(2,1)S(1)}, u32[]{:S(2)}, u32[]{:S(2)}) collective-permute-start(bf16[128,256]{1,0:T(8,128)(2,1)} %bitcast.15), channel_id=1, source_target_pairs={{0,16},{8,24},{16,0},{24,8},{1,17},{9,25},{17,1},{25,9},{2,18},{10... | collective-permute-start | bytes 196616 | tf_op jit(solution)/shard_map/ppermute | solution.py:373
  5.1 4.5 %collective-permute-start.2 = (bf16[128,256]{1,0:T(8,128)(2,1)}, bf16[128,256]{1,0:T(8,128)(2,1)S(1)}, u32[]{:S(2)}, u32[]{:S(2)}) collective-permute-start(bf16[128,256]{1,0:T(8,128)(2,1)} %bitcast.16), channel_id=1, source_target_pairs={{0,8},{8,0},{16,24},{24,16},{1,9},{9,1},{17,25},{25,17},{2,10},{10... | collective-permute-start | bytes 196616 | tf_op jit(solution)/shard_map/ppermute | solution.py:373
  5.2 1.2 %copy-start.7 = (s32[4,4]{1,0:T(4,128)S(1)}, s32[4,4]{1,0:T(4,128)}, u32[]{:S(2)}) copy-start(s32[4,4]{1,0:T(4,128)} %param.10) | copy-start | bytes 196
  6.4 1.0 %slice-start = ((bf16[256,768]{1,0:T(8,128)(2,1)}), bf16[256,512]{1,0:T(8,128)(2,1)S(1)}, s32[]{:S(2)}) async-start(bf16[256,768]{1,0:T(8,128)(2,1)} %col_proj.1), calls=%async_computation.2 | async-start | bytes 524288 | tf_op jit(solution)/shard_map/slice | solution.py:408
  7.4 0.7 copy-start.9
  7.4 2.2 %copy-start.1 = (bf16[256,256]{1,0:T(8,128)(2,1)S(1)}, bf16[256,256]{1,0:T(8,128)(2,1)}, u32[]{:S(2)}) copy-start(bf16[256,256]{1,0:T(8,128)(2,1)} %row_out.1) | copy-start | bytes 393220
  7.4 2.2 %copy-start.3 = (bf16[128,1,256]{2,0,1:T(8,128)(2,1)S(1)}, bf16[128,1,256]{2,0,1:T(8,128)(2,1)}, u32[]{:S(2)}) copy-start(bf16[128,1,256]{2,0,1:T(8,128)(2,1)} %param.9) | copy-start | bytes 196612
  7.4 2.2 %copy-start.6 = (bf16[128,1,256]{2,0,1:T(8,128)(2,1)S(1)}, bf16[128,1,256]{2,0,1:T(8,128)(2,1)}, u32[]{:S(2)}) copy-start(bf16[128,1,256]{2,0,1:T(8,128)(2,1)} %param.17) | copy-start | bytes 196612
  7.6 0.7 copy-start.8
  12.4 13.2 %all-to-all-start = ((bf16[8,16,768]{2,1,0:T(8,128)(2,1)}), bf16[8,16,768]{2,1,0:T(8,128)(2,1)S(1)}, u32[]{:S(2)}, u32[]{:S(2)}) async-start(bf16[8,16,768]{2,1,0:T(8,128)(2,1)} %get-tuple-element.57), calls=%async_computation | async-start | bytes 393216 | tf_op jit(solution)/shard_map/all_to_all | solution.py:368
  17.3 8.3 %copy-start = (bf16[256,768]{1,0:T(8,128)(2,1)S(1)}, bf16[256,768]{1,0:T(8,128)(2,1)}, u32[]{:S(2)}) copy-start(bf16[256,768]{1,0:T(8,128)(2,1)} %col_proj.1) | copy-start | bytes 1179652
  17.3 8.3 %copy-start.5 = (bf16[256,256]{1,0:T(8,128)(2,1)S(1)}, bf16[256,256]{1,0:T(8,128)(2,1)}, u32[]{:S(2)}) copy-start(bf16[256,256]{1,0:T(8,128)(2,1)} %col_out.1) | copy-start | bytes 393220
  28.9 2.9 %copy-start.4 = (bf16[8,16,512]{2,1,0:T(8,128)(2,1)S(1)}, bf16[8,16,512]{2,1,0:T(8,128)(2,1)}, u32[]{:S(2)}) copy-start(bf16[8,16,512]{2,1,0:T(8,128)(2,1)} %get-tuple-element.68.og) | copy-start | bytes 393220
  28.9 3.2 %collective-permute-start.3 = (bf16[128,1280]{1,0:T(8,128)(2,1)S(1)}, bf16[128,1280]{1,0:T(8,128)(2,1)S(1)}, u32[]{:S(2)}, u32[]{:S(2)}) collective-permute-start(bf16[128,1280]{1,0:T(8,128)(2,1)S(1)} %get-tuple-element.63), channel_id=1, source_target_pairs={{0,1},{1,0},{2,3},{3,2},{4,5},{5,4},{6,7},{7,6},{8,9},{9,8},{10,11... | collective-permute-start | bytes 983048 | tf_op jit(solution)/shard_map/ppermute | solution.py:373
  29.0 10.3 %all-to-all-start.1 = ((bf16[32,8,128]{2,1,0:T(8,128)(2,1)}), bf16[32,8,128]{2,1,0:T(8,128)(2,1)S(1)}, u32[]{:S(2)}, u32[]{:S(2)}) async-start(bf16[32,8,128]{2,1,0:T(8,128)(2,1)} %get-tuple-element.61), calls=%async_computation.1 | async-start | bytes 131072 | tf_op jit(solution)/shard_map/all_to_all | solution.py:368
  31.8 5.0 %collective-permute-start.4 = (bf16[4,16,512]{2,1,0:T(8,128)(2,1)S(1)}, bf16[4,16,512]{2,1,0:T(8,128)(2,1)S(1)}, u32[]{:S(2)}, u32[]{:S(2)}) collective-permute-start(bf16[4,16,512]{2,1,0:T(8,128)(2,1)S(1)} %get-tuple-element.69), channel_id=1, source_target_pairs={{0,1},{1,0},{2,3},{3,2},{4,5},{5,4},{6,7},{7,6},{8,9},{9,8},{10,11... | collective-permute-start | bytes 196616 | tf_op jit(solution)/shard_map/ppermute | solution.py:373
  32.1 1.0 %copy-start.2 = (bf16[128,1280]{1,0:T(8,128)(2,1)S(1)}, bf16[128,1280]{1,0:T(8,128)(2,1)}, u32[]{:S(2)}) copy-start(bf16[128,1280]{1,0:T(8,128)(2,1)} %get-tuple-element.62.keep) | copy-start | bytes 983044
  33.2 9.0 %collective-permute-start.6 = (bf16[32,1280]{1,0:T(8,128)(2,1)S(1)}, bf16[32,1280]{1,0:T(8,128)(2,1)S(1)}, u32[]{:S(2)}, u32[]{:S(2)}) collective-permute-start(bf16[32,1280]{1,0:T(8,128)(2,1)S(1)} %get-tuple-element.65), channel_id=1, source_target_pairs={{0,8},{8,0},{16,24},{24,16},{1,9},{9,1},{17,25},{25,17},{2,10},{10... | collective-permute-start | bytes 245768 | tf_op jit(solution)/shard_map/ppermute | solution.py:373
  35.0 7.3 %collective-permute-start.7 = (bf16[32,1280]{1,0:T(8,128)(2,1)S(1)}, bf16[32,1280]{1,0:T(8,128)(2,1)S(1)}, u32[]{:S(2)}, u32[]{:S(2)}) collective-permute-start(bf16[32,1280]{1,0:T(8,128)(2,1)S(1)} %get-tuple-element.66), channel_id=1, source_target_pairs={{0,16},{8,24},{16,0},{24,8},{1,17},{9,25},{17,1},{25,9},{2,18},{10... | collective-permute-start | bytes 245768 | tf_op jit(solution)/shard_map/ppermute | solution.py:373
  36.5 5.8 %collective-permute-start.8 = (bf16[32,1280]{1,0:T(8,128)(2,1)S(1)}, bf16[32,1280]{1,0:T(8,128)(2,1)S(1)}, u32[]{:S(2)}, u32[]{:S(2)}) collective-permute-start(bf16[32,1280]{1,0:T(8,128)(2,1)S(1)} %get-tuple-element.67), channel_id=1, source_target_pairs={{0,24},{8,16},{16,8},{24,0},{1,25},{9,17},{17,9},{25,1},{2,26},{10... | collective-permute-start | bytes 245768 | tf_op jit(solution)/shard_map/ppermute | solution.py:373
  41.0 1.3 %collective-permute-start.5 = (bf16[96,256]{1,0:T(8,128)(2,1)S(1)}, bf16[96,256]{1,0:T(8,128)(2,1)S(1)}, u32[]{:S(2)}, u32[]{:S(2)}) collective-permute-start(bf16[96,256]{1,0:T(8,128)(2,1)S(1)} %get-tuple-element.75), channel_id=1, source_target_pairs={{0,1},{1,0},{2,3},{3,2},{4,5},{5,4},{6,7},{7,6},{8,9},{9,8},{10,11... | collective-permute-start | bytes 147464 | tf_op jit(solution)/shard_map/ppermute | solution.py:373
  42.3 8.6 %collective-permute-start.9 = (bf16[320,256]{1,0:T(8,128)(2,1)S(1)}, bf16[320,256]{1,0:T(8,128)(2,1)S(1)}, u32[]{:S(2)}, u32[]{:S(2)}) collective-permute-start(bf16[320,256]{1,0:T(8,128)(2,1)S(1)} %get-tuple-element.77.mine), channel_id=1, source_target_pairs={{0,2},{1,3},{2,0},{3,1},{4,6},{5,7},{6,4},{7,5},{8,10},{9,11},{10,... | collective-permute-start | bytes 491528 | tf_op jit(solution)/shard_map/ppermute | solution.py:373
  43.4 6.4 %collective-permute-start.10 = (bf16[64,256]{1,0:T(8,128)(2,1)S(1)}, bf16[64,256]{1,0:T(8,128)(2,1)S(1)}, u32[]{:S(2)}, u32[]{:S(2)}) collective-permute-start(bf16[64,256]{1,0:T(8,128)(2,1)S(1)} %get-tuple-element.78), channel_id=1, source_target_pairs={{0,6},{1,7},{2,4},{3,5},{4,2},{5,3},{6,0},{7,1},{8,14},{9,15},{10,... | collective-permute-start | bytes 98312 | tf_op jit(solution)/shard_map/ppermute | solution.py:373
  45.8 5.2 %collective-permute-start.11 = (bf16[64,256]{1,0:T(8,128)(2,1)S(1)}, bf16[64,256]{1,0:T(8,128)(2,1)S(1)}, u32[]{:S(2)}, u32[]{:S(2)}) collective-permute-start(bf16[64,256]{1,0:T(8,128)(2,1)S(1)} %get-tuple-element.79), channel_id=1, source_target_pairs={{0,4},{1,5},{2,6},{3,7},{4,0},{5,1},{6,2},{7,3},{8,12},{9,13},{10,... | collective-permute-start | bytes 98312 | tf_op jit(solution)/shard_map/ppermute | solution.py:373
  51.0 8.2 %collective-permute-start.12 = (bf16[256,256]{1,0:T(8,128)(2,1)S(1)}, bf16[256,256]{1,0:T(8,128)(2,1)S(1)}, u32[]{:S(2)}, u32[]{:S(2)}) collective-permute-start(bf16[256,256]{1,0:T(8,128)(2,1)S(1)} %shard_map.143.mine), channel_id=1, source_target_pairs={{0,4},{1,5},{2,6},{3,7},{4,0},{5,1},{6,2},{7,3},{8,12},{9,13},{10,... | collective-permute-start | bytes 393224 | tf_op jit(solution)/shard_map/ppermute | solution.py:373
  51.5 4.3 %collective-permute-start.13 = (bf16[128,192]{1,0:T(8,128)(2,1)S(1)}, bf16[128,192]{1,0:T(8,128)(2,1)S(1)}, u32[]{:S(2)}, u32[]{:S(2)}) collective-permute-start(bf16[128,192]{1,0:T(8,128)(2,1)S(1)} %get-tuple-element.86), channel_id=1, source_target_pairs={{0,8},{8,0},{16,24},{24,16},{1,9},{9,1},{17,25},{25,17},{2,10},{10... | collective-permute-start | bytes 147464 | tf_op jit(solution)/shard_map/ppermute | solution.py:373
  52.1 4.3 %collective-permute-start.14 = (bf16[128,192]{1,0:T(8,128)(2,1)S(1)}, bf16[128,192]{1,0:T(8,128)(2,1)S(1)}, u32[]{:S(2)}, u32[]{:S(2)}) collective-permute-start(bf16[128,192]{1,0:T(8,128)(2,1)S(1)} %get-tuple-element.87), channel_id=1, source_target_pairs={{0,16},{8,24},{16,0},{24,8},{1,17},{9,25},{17,1},{25,9},{2,18},{10... | collective-permute-start | bytes 147464 | tf_op jit(solution)/shard_map/ppermute | solution.py:373
  53.4 5.9 %collective-permute-start.15 = (bf16[128,192]{1,0:T(8,128)(2,1)S(1)}, bf16[128,192]{1,0:T(8,128)(2,1)S(1)}, u32[]{:S(2)}, u32[]{:S(2)}) collective-permute-start(bf16[128,192]{1,0:T(8,128)(2,1)S(1)} %get-tuple-element.88), channel_id=1, source_target_pairs={{0,24},{8,16},{16,8},{24,0},{1,25},{9,17},{17,9},{25,1},{2,26},{10... | collective-permute-start | bytes 147464 | tf_op jit(solution)/shard_map/ppermute | solution.py:373
  59.3 5.0 %collective-permute-start.16 = (bf16[256,256]{1,0:T(8,128)(2,1)S(1)}, bf16[256,256]{1,0:T(8,128)(2,1)S(1)}, u32[]{:S(2)}, u32[]{:S(2)}) collective-permute-start(bf16[256,256]{1,0:T(8,128)(2,1)S(1)} %shard_map.144.refs_0_), channel_id=1, source_target_pairs={{0,8},{8,0},{16,24},{24,16},{1,9},{9,1},{17,25},{25,17},{2,10},{10... | collective-permute-start | bytes 393224 | tf_op jit(solution)/shard_map/ppermute | solution.py:373
  59.4 5.0 %collective-permute-start.17 = (bf16[256,256]{1,0:T(8,128)(2,1)S(1)}, bf16[256,256]{1,0:T(8,128)(2,1)S(1)}, u32[]{:S(2)}, u32[]{:S(2)}) collective-permute-start(bf16[256,256]{1,0:T(8,128)(2,1)S(1)} %shard_map.144.refs_0_), channel_id=1, source_target_pairs={{0,16},{8,24},{16,0},{24,8},{1,17},{9,25},{17,1},{25,9},{2,18},{10... | collective-permute-start | bytes 393224 | tf_op jit(solution)/shard_map/ppermute | solution.py:373
  61.2 5.9 %collective-permute-start.18 = (bf16[256,256]{1,0:T(8,128)(2,1)S(1)}, bf16[256,256]{1,0:T(8,128)(2,1)S(1)}, u32[]{:S(2)}, u32[]{:S(2)}) collective-permute-start(bf16[256,256]{1,0:T(8,128)(2,1)S(1)} %shard_map.144.refs_0_), channel_id=1, source_target_pairs={{0,24},{8,16},{16,8},{24,0},{1,25},{9,17},{17,9},{25,1},{2,26},{10... | collective-permute-start | bytes 393224 | tf_op jit(solution)/shard_map/ppermute | solution.py:373
  62.8 4.2 %collective-permute-start.19 = (bf16[256,256]{1,0:T(8,128)(2,1)S(1)}, bf16[256,256]{1,0:T(8,128)(2,1)S(1)}, u32[]{:S(2)}, u32[]{:S(2)}) collective-permute-start(bf16[256,256]{1,0:T(8,128)(2,1)S(1)} %shard_map.144.refs_0_), channel_id=1, source_target_pairs={{0,1},{1,0},{2,3},{3,2},{4,5},{5,4},{6,7},{7,6},{8,9},{9,8},{10,11... | collective-permute-start | bytes 393224 | tf_op jit(solution)/shard_map/ppermute | solution.py:373
  67.1 1.3 %collective-permute-start.20 = (bf16[256,256]{1,0:T(8,128)(2,1)S(1)}, bf16[256,256]{1,0:T(8,128)(2,1)S(1)}, u32[]{:S(2)}, u32[]{:S(2)}) collective-permute-start(bf16[256,256]{1,0:T(8,128)(2,1)S(1)} %collective-permute-done.16.refs_2_), channel_id=1, source_target_pairs={{0,1},{1,0},{2,3},{3,2},{4,5},{5,4},{6,7},{7,6},{8,9},{9,8},{10,11... | collective-permute-start | bytes 393224 | tf_op jit(solution)/shard_map/ppermute | solution.py:373
  67.1 1.5 %collective-permute-start.21 = (bf16[256,256]{1,0:T(8,128)(2,1)S(1)}, bf16[256,256]{1,0:T(8,128)(2,1)S(1)}, u32[]{:S(2)}, u32[]{:S(2)}) collective-permute-start(bf16[256,256]{1,0:T(8,128)(2,1)S(1)} %collective-permute-done.17.refs_4_), channel_id=1, source_target_pairs={{0,1},{1,0},{2,3},{3,2},{4,5},{5,4},{6,7},{7,6},{8,9},{9,8},{10,11... | collective-permute-start | bytes 393224 | tf_op jit(solution)/shard_map/ppermute | solution.py:373
  67.6 1.3 %collective-permute-start.22 = (bf16[256,256]{1,0:T(8,128)(2,1)S(1)}, bf16[256,256]{1,0:T(8,128)(2,1)S(1)}, u32[]{:S(2)}, u32[]{:S(2)}) collective-permute-start(bf16[256,256]{1,0:T(8,128)(2,1)S(1)} %collective-permute-done.18.refs_6_), channel_id=1, source_target_pairs={{0,1},{1,0},{2,3},{3,2},{4,5},{5,4},{6,7},{7,6},{8,9},{9,8},{10,11... | collective-permute-start | bytes 393224 | tf_op jit(solution)/shard_map/ppermute | solution.py:373
